TPU v7x, 128 devices: a whole 4x4x4 slice. The times are simulated.
128 devices in a mesh: dp: 64 (over y, z_hi, x, core), mp: 2 (over z_lo).
Axes of the slice: x: 4, y: 4, z: 4 (z_hi: 2, z_lo: 2; z = z_hi * 2 + z_lo), core: 2. Of those that a mesh axis runs over, the one named last changes fastest.
Arguments:
- belief: bfloat16 [16384, 2652], P('dp'), may hold values from -6 to 6
- target_value: bfloat16 [16384, 1326], P('dp'), may hold values from -6 to 6
- counts: int32 [128], P('dp'), may hold values from 1 to 128, as said below
- w_first: bfloat16 [2652, 1536], P(None, 'mp'), may hold values from -0.125 to 0.125
- w_middle: bfloat16 [1536, 1536], P('mp'), may hold values from -0.15625 to 0.15625
- w_last: bfloat16 [1536, 1326], P(None, 'mp'), may hold values from -0.15625 to 0.15625
Outputs:
- grad_first: float32 [2652, 1536], P(None, ('mp', 'dp'))
- grad_middle: float32 [1536, 1536], P('mp', 'dp')
- grad_last: float32 [1536, 1326], P('dp', 'mp')
Inputs may be any that keep to these rules, and one draw needn't show every extreme that they name: `counts`: rows past a subgame's count in its block are padding with arbitrary values.
All inputs are finite; a program needn't handle non-finite values.
Results may differ from a plain program's by a relative error of at most 0.0089.
Values may be sent and summed in bfloat16 or wider, within the bound.
No kernel may reach another device: no remote copies, remote signals or barrier semaphores. Data moves between devices by JAX's collectives and lax.ppermute only.
A program may use at most 192 MiB of HBM per device.

v0:
```python
import jax
import jax.numpy as jnp
from jax import lax
from jax.sharding import Mesh
from jax.sharding import PartitionSpec as P

BLOCK = 128
PARAMS = 8469504
DP = ("dp_0", "dp_1", "dp_2", "dp_3")
DP_MP = ("dp_0", "dp_1", "dp_2", "dp_3", "mp")
MP_DP = ("mp", "dp_0", "dp_1", "dp_2", "dp_3")


def copy_for_each(shard, axis):
    size = lax.axis_size(axis)
    return lax.all_to_all(
        jnp.broadcast_to(shard[None], (size, *shard.shape)), axis, 0, 0, tiled=True
    )


def taken_together(shard, axis):
    return copy_for_each(shard, axis).astype(jnp.float32).sum(axis=0)


def cut_along(shard, dim, size):
    lengths = shard.shape
    blocks = shard.reshape(*lengths[:dim], size, lengths[dim] // size, *lengths[dim + 1 :])
    return jnp.moveaxis(blocks, dim, 0)


def sum_at_owner(shard, axis, dim):
    size = lax.axis_size(axis)
    blocks = lax.all_to_all(cut_along(shard, dim, size), axis, 0, 0, tiled=True)
    return jnp.sum(blocks.astype(jnp.float32), axis=0)


def one_axis_at_a_time(shard, axes):
    for axis in axes:
        shard = lax.psum(shard, axis)
    return shard


def silu_slope(pre_act):
    sigmoid_of = jax.nn.sigmoid(pre_act)
    return sigmoid_of * (1.0 + pre_act * (1.0 - sigmoid_of))


def rows_grads(belief, target_value, live_mask, w_first, w_middle, w_last):
    pre_first = jnp.dot(belief, w_first, preferred_element_type=jnp.float32)
    act_first = jax.nn.silu(pre_first).astype(jnp.bfloat16)
    partial_middle = jnp.dot(act_first, w_middle, preferred_element_type=jnp.float32)
    pre_middle = taken_together(partial_middle.astype(jnp.bfloat16), "mp").astype(jnp.float32)
    act_middle = jax.nn.silu(pre_middle).astype(jnp.bfloat16)
    predicted = jnp.dot(act_middle, w_last, preferred_element_type=jnp.float32)
    mismatch = predicted - target_value.astype(jnp.float32)
    slope_out = (jnp.clip(mismatch, -1.0, 1.0) * live_mask[:, None]).astype(jnp.bfloat16)
    raw_last = jnp.dot(act_middle.T, slope_out, preferred_element_type=jnp.float32)
    partial_back = jnp.dot(slope_out, w_last.T, preferred_element_type=jnp.float32)
    back_middle = taken_together(partial_back.astype(jnp.bfloat16), "mp").astype(jnp.float32)
    slope_middle = (back_middle * silu_slope(pre_middle)).astype(jnp.bfloat16)
    raw_middle = jnp.dot(act_first.T, slope_middle, preferred_element_type=jnp.float32)
    back_first = jnp.dot(slope_middle, w_middle.T, preferred_element_type=jnp.float32)
    slope_first = (back_first * silu_slope(pre_first)).astype(jnp.bfloat16)
    raw_first = jnp.dot(belief.T, slope_first, preferred_element_type=jnp.float32)
    return (raw_first, raw_middle, raw_last)


def per_device(belief, target_value, counts, w_first, w_middle, w_last):
    total_rows = belief.shape[0]
    own_width = w_last.shape[1]
    target_value = lax.dynamic_slice_in_dim(
        target_value, lax.axis_index("mp") * own_width, own_width, 1
    )
    live_rows = (counts[:, None] > jnp.arange(BLOCK, dtype=jnp.int32)[None, :]).reshape(total_rows)
    raw_first, raw_middle, raw_last = rows_grads(
        belief, target_value, live_rows.astype(jnp.float32), w_first, w_middle, w_last
    )
    shard_first, shard_middle = (
        sum_at_owner(raw_first.astype(jnp.bfloat16), DP, 1),
        sum_at_owner(raw_middle.astype(jnp.bfloat16), DP, 1),
    )
    shard_last = sum_at_owner(raw_last.astype(jnp.bfloat16), DP, 0)
    local_squares = (
        jnp.sum(shard_first * shard_first)
        + jnp.sum(shard_middle * shard_middle)
        + jnp.sum(shard_last * shard_last)
    )
    square_sum = one_axis_at_a_time(local_squares, DP_MP)
    norm_scale = lax.rsqrt(square_sum / PARAMS + 1e-06)
    return (shard_first * norm_scale, shard_middle * norm_scale, shard_last * norm_scale)


def solution(mesh):
    finer = Mesh(
        mesh.devices.reshape(4, 2, 4, 2, mesh.shape["mp"]), ("dp_0", "dp_1", "dp_2", "dp_3", "mp")
    )
    return jax.shard_map(
        per_device,
        mesh=finer,
        in_specs=(P(DP, None), P(DP, None), P(DP), P(None, "mp"), P("mp", None), P(None, "mp")),
        out_specs=(P(None, MP_DP), P("mp", DP), P(DP, "mp")),
        check_vma=False,
    )
```

profile of v0, /device:TPU:1, one launch (start us, length us, event | category | flops | bytes accessed | tf_op | source)
XLA Modules:
  0.0 262.4 jit_solution(7464437599135056884)
XLA Ops:
  0.6 0.0 copy-start
  0.6 4.0 %fusion.12 = f32[256,768]{1,0:T(8,128)S(1)} fusion(bf16[256,2652]{0,1:T(8,128)(2,1)} %param.6, bf16[2652,768]{1,0:T(8,128)(2,1)} %param.9), kind=kOutput, calls=%fused_computation.36 | convolution fusion | flops 1042808832 | bytes 6217728 | tf_op jit(solution)/shard_map/dot_general | solution.py:49
  4.7 0.0 copy-start.6
  4.7 0.9 copy-done.6
  5.6 0.0 copy-done
  5.6 0.8 convolution_convert_fusion.3
  6.4 1.2 broadcast_in_dim.4
  7.7 0.0 copy-start.5
  7.7 4.7 %all-to-all-start = ((bf16[2,256,1536]{2,1,0:T(8,128)(2,1)}), bf16[2,256,1536]{2,1,0:T(8,128)(2,1)}, u32[]{:S(2)}, u32[]{:S(2)}) async-start(bf16[2,256,1536]{2,1,0:T(8,128)(2,1)} %broadcast_in_dim.4), calls=%async_computation | async-start | bytes 3145728 | tf_op jit(solution)/shard_map/all_to_all | solution.py:16
  12.4 0.0 copy-done.5
  12.4 0.1 fusion.10
  12.5 0.0 copy-start.4
  12.5 20.0 %all-to-all-done = bf16[2,256,1536]{2,1,0:T(8,128)(2,1)} async-done(((bf16[2,256,1536]{2,1,0:T(8,128)(2,1)}), bf16[2,256,1536]{2,1,0:T(8,128)(2,1)}, u32[]{:S(2)}, u32[]{:S(2)}) %all-to-all-start) | async-done | bytes 1572896 | tf_op jit(solution)/shard_map/all_to_all | solution.py:16
  32.4 0.0 copy-start.3
  32.4 2.0 convert_reduce_fusion.4
  34.4 0.0 copy-done.4
  34.4 0.0 copy-done.3
  34.5 0.0 copy-start.1
  34.5 0.9 fusion.4
  35.4 0.3 copy-done.1
  35.6 0.8 convolution_convert_fusion.4
  36.4 1.3 broadcast_in_dim.5
  37.7 4.6 %all-to-all-start.1 = ((bf16[2,256,1536]{2,1,0:T(8,128)(2,1)}), bf16[2,256,1536]{2,1,0:T(8,128)(2,1)}, u32[]{:S(2)}, u32[]{:S(2)}) async-start(bf16[2,256,1536]{2,1,0:T(8,128)(2,1)} %broadcast_in_dim.5), calls=%async_computation.1 | async-start | bytes 3145728 | tf_op jit(solution)/shard_map/all_to_all | solution.py:16
  42.4 3.5 %convolution_convert_fusion.2 = bf16[1536,663]{0,1:T(8,128)(2,1)} fusion(bf16[256,663]{0,1:T(8,128)(2,1)S(1)} %fusion.4, f32[256,1536]{1,0:T(8,128)} %copy-done.1), kind=kOutput, calls=%fused_computation.6 | convolution fusion | flops 524388864 | bytes 3949056 | tf_op jit(solution)/shard_map/dot_general | solution.py:57
  45.9 4.1 %copy.14 = bf16[1536,663]{1,0:T(8,128)(2,1)} copy(bf16[1536,663]{0,1:T(8,128)(2,1)} %convolution_convert_fusion.2) | data formatting | bytes 4073472 | tf_op jit(solution)/shard_map/convert_element_type | solution.py:82
  50.0 10.4 %all-to-all-done.1 = bf16[2,256,1536]{2,1,0:T(8,128)(2,1)} async-done(((bf16[2,256,1536]{2,1,0:T(8,128)(2,1)}), bf16[2,256,1536]{2,1,0:T(8,128)(2,1)}, u32[]{:S(2)}, u32[]{:S(2)}) %all-to-all-start.1) | async-done | bytes 1572896 | tf_op jit(solution)/shard_map/all_to_all | solution.py:16
  60.5 12.6 %all-to-all-start.4 = ((bf16[64,24,663]{2,1,0:T(8,128)(2,1)}), bf16[64,24,663]{2,1,0:T(8,128)(2,1)}, u32[]{:S(2)}, u32[]{:S(2)}) async-start(bf16[64,24,663]{2,1,0:T(8,128)(2,1)} %bitcast.23), calls=%async_computation.4 | async-start | bytes 4718592 | tf_op jit(solution)/shard_map/all_to_all | solution.py:33
  73.1 0.0 copy-start.2
  73.1 2.0 convert_reduce_fusion.3
  75.1 0.0 copy-done.2
  75.1 0.0 copy-start.7
  75.1 0.6 multiply_convert_fusion
  75.7 0.5 copy-done.7
  76.2 2.3 convolution_convert_fusion.1
  78.5 4.3 %copy.13 = bf16[768,1536]{0,1:T(8,128)(2,1)} copy(bf16[768,1536]{1,0:T(8,128)(2,1)} %convolution_convert_fusion.1) | data formatting | bytes 4718592 | tf_op jit(solution)/shard_map/convert_element_type | solution.py:80
  82.8 23.9 %all-to-all-done.4 = bf16[64,24,663]{2,1,0:T(8,128)(2,1)} async-done(((bf16[64,24,663]{2,1,0:T(8,128)(2,1)}), bf16[64,24,663]{2,1,0:T(8,128)(2,1)}, u32[]{:S(2)}, u32[]{:S(2)}) %all-to-all-start.4) | async-done | bytes 2036768 | tf_op jit(solution)/shard_map/all_to_all | solution.py:33
  106.7 5.1 %all-to-all-start.3 = ((bf16[64,768,24]{1,2,0:T(8,128)(2,1)}), bf16[64,768,24]{1,2,0:T(8,128)(2,1)}, u32[]{:S(2)}, u32[]{:S(2)}) async-start(bf16[64,768,24]{1,2,0:T(8,128)(2,1)} %bitcast.24), calls=%async_computation.3 | async-start | bytes 4718592 | tf_op jit(solution)/shard_map/all_to_all | solution.py:33
  111.8 5.5 %fusion = bf16[2652,768]{1,0:T(8,128)(2,1)} fusion(bf16[256,2652]{0,1:T(8,128)(2,1)} %param.6, bf16[256,1536]{1,0:T(8,128)(2,1)S(1)} %multiply_convert_fusion, bf16[768,1536]{1,0:T(8,128)(2,1)S(1)} %copy-done, f32[256,768]{1,0:T(8,128)} %copy-done.6), kind=kOutput, calls=%fused_computation.4 | convolution fusion | flops 1650594816 | bytes 9363456 | tf_op jit(solution)/shard_map/dot_general | solution.py:64
  117.3 6.4 %copy.12 = bf16[2652,768]{0,1:T(8,128)(2,1)} copy(bf16[2652,768]{1,0:T(8,128)(2,1)} %fusion) | data formatting | bytes 8146944 | tf_op jit(solution)/shard_map/convert_element_type | solution.py:79
  123.7 7.1 %reshape.34 = bf16[2652,64,12]{0,2,1:T(8,128)(2,1)} reshape(bf16[2652,768]{0,1:T(8,128)(2,1)} %copy.12) | data formatting | bytes 8146944 | tf_op jit(solution)/shard_map/reshape | solution.py:27
  130.9 14.5 %all-to-all-done.3 = bf16[64,768,24]{1,2,0:T(8,128)(2,1)} async-done(((bf16[64,768,24]{1,2,0:T(8,128)(2,1)}), bf16[64,768,24]{1,2,0:T(8,128)(2,1)}, u32[]{:S(2)}, u32[]{:S(2)}) %all-to-all-start.3) | async-done | bytes 2359328 | tf_op jit(solution)/shard_map/all_to_all | solution.py:33
  145.3 5.4 %all-to-all-start.2 = ((bf16[64,2652,12]{1,2,0:T(8,128)(2,1)}), bf16[64,2652,12]{1,2,0:T(8,128)(2,1)}, u32[]{:S(2)}, u32[]{:S(2)}) async-start(bf16[64,2652,12]{1,2,0:T(8,128)(2,1)} %bitcast.22), calls=%async_computation.2 | async-start | bytes 11010048 | tf_op jit(solution)/shard_map/all_to_all | solution.py:33
  150.8 2.0 convert_reduce_fusion.1
  152.8 0.6 multiply_reduce_fusion.1
  153.4 2.0 convert_reduce_fusion.2
  155.4 0.6 multiply_reduce_fusion.2
  156.1 62.7 %all-to-all-done.2 = bf16[64,2652,12]{1,2,0:T(8,128)(2,1)} async-done(((bf16[64,2652,12]{1,2,0:T(8,128)(2,1)}), bf16[64,2652,12]{1,2,0:T(8,128)(2,1)}, u32[]{:S(2)}, u32[]{:S(2)}) %all-to-all-start.2) | async-done | bytes 4073504 | tf_op jit(solution)/shard_map/all_to_all | solution.py:33
  218.8 3.5 %convert_reduce_fusion = f32[2652,12]{0,1:T(8,128)S(1)} fusion(bf16[64,2652,12]{1,2,0:T(8,128)(2,1)} %all-to-all-done.2), kind=kLoop, calls=%fused_computation | loop fusion | flops 4041648 | bytes 4200768 | tf_op jit(solution)/shard_map/reduce_sum | solution.py:34
  222.3 0.6 multiply_reduce_fusion
  224.9 7.2 %psum.35 = f32[]{:T(128)} all-reduce(f32[]{:T(128)S(6)} %add.44), channel_id=1, replica_groups=mesh['dp_0'=4,'dp_1'=2,'dp_2'=4,'dp_3'=2,'mp'=2] {'dp_0'}, use_global_device_ids=true, to_apply=%region_8.9 | all-reduce | flops 1 | bytes 8 | tf_op jit(solution)/shard_map/psum | solution.py:39
  232.2 5.9 %psum.36 = f32[]{:T(128)} all-reduce(f32[]{:T(128)} %psum.35), channel_id=1, replica_groups=mesh['dp_0'=4,'dp_1'=2,'dp_2'=4,'dp_3'=2,'mp'=2] {'dp_1'}, use_global_device_ids=true, to_apply=%region_9.10 | all-reduce | flops 1 | bytes 8 | tf_op jit(solution)/shard_map/psum | solution.py:39
  238.1 7.8 %psum.37 = f32[]{:T(128)} all-reduce(f32[]{:T(128)} %psum.36), channel_id=1, replica_groups=mesh['dp_0'=4,'dp_1'=2,'dp_2'=4,'dp_3'=2,'mp'=2] {'dp_2'}, use_global_device_ids=true, to_apply=%region_10.11 | all-reduce | flops 1 | bytes 8 | tf_op jit(solution)/shard_map/psum | solution.py:39
  245.9 9.4 %psum.38 = f32[]{:T(128)} all-reduce(f32[]{:T(128)} %psum.37), channel_id=1, replica_groups=mesh['dp_0'=4,'dp_1'=2,'dp_2'=4,'dp_3'=2,'mp'=2] {'dp_3'}, use_global_device_ids=true, to_apply=%region_11.12 | all-reduce | flops 1 | bytes 8 | tf_op jit(solution)/shard_map/psum | solution.py:39
  255.3 4.4 %psum.39 = f32[]{:T(128)} all-reduce(f32[]{:T(128)} %psum.38), channel_id=1, replica_groups=mesh['dp_0'=4,'dp_1'=2,'dp_2'=4,'dp_3'=2,'mp'=2] {'mp'}, use_global_device_ids=true, to_apply=%region_12.13 | all-reduce | flops 1 | bytes 8 | tf_op jit(solution)/shard_map/psum | solution.py:39
  260.4 0.6 broadcast_multiply_fusion.1
  261.1 0.6 broadcast_multiply_fusion.2
  261.7 0.7 broadcast_multiply_fusion
Async XLA Ops:
  0.6 5.0 %copy-start = (bf16[768,1536]{1,0:T(8,128)(2,1)S(1)}, bf16[768,1536]{1,0:T(8,128)(2,1)}, u32[]{:S(2)}) copy-start(bf16[768,1536]{1,0:T(8,128)(2,1)} %param.10) | copy-start | bytes 7077892
  4.7 0.9 copy-start.6
  7.7 4.7 %copy-start.5 = (s32[2]{0:T(128)S(1)}, s32[2]{0:T(128)}, u32[]{:S(2)}) copy-start(s32[2]{0:T(128)} %param.8) | copy-start | bytes 28
  7.7 24.8 %all-to-all-start = ((bf16[2,256,1536]{2,1,0:T(8,128)(2,1)}), bf16[2,256,1536]{2,1,0:T(8,128)(2,1)}, u32[]{:S(2)}, u32[]{:S(2)}) async-start(bf16[2,256,1536]{2,1,0:T(8,128)(2,1)} %broadcast_in_dim.4), calls=%async_computation | async-start | bytes 3145728 | tf_op jit(solution)/shard_map/all_to_all | solution.py:16
  12.5 22.0 %copy-start.4 = (bf16[256,1326]{0,1:T(8,128)(2,1)S(1)}, bf16[256,1326]{0,1:T(8,128)(2,1)}, u32[]{:S(2)}) copy-start(bf16[256,1326]{0,1:T(8,128)(2,1)} %param.7) | copy-start | bytes 2036740
  32.4 2.0 copy-start.3
  34.5 1.1 copy-start.1
  37.7 22.7 %all-to-all-start.1 = ((bf16[2,256,1536]{2,1,0:T(8,128)(2,1)}), bf16[2,256,1536]{2,1,0:T(8,128)(2,1)}, u32[]{:S(2)}, u32[]{:S(2)}) async-start(bf16[2,256,1536]{2,1,0:T(8,128)(2,1)} %broadcast_in_dim.5), calls=%async_computation.1 | async-start | bytes 3145728 | tf_op jit(solution)/shard_map/all_to_all | solution.py:16
  60.5 46.2 %all-to-all-start.4 = ((bf16[64,24,663]{2,1,0:T(8,128)(2,1)}), bf16[64,24,663]{2,1,0:T(8,128)(2,1)}, u32[]{:S(2)}, u32[]{:S(2)}) async-start(bf16[64,24,663]{2,1,0:T(8,128)(2,1)} %bitcast.23), calls=%async_computation.4 | async-start | bytes 4718592 | tf_op jit(solution)/shard_map/all_to_all | solution.py:33
  73.1 2.0 copy-start.2
  75.1 1.1 copy-start.7
  106.7 38.6 %all-to-all-start.3 = ((bf16[64,768,24]{1,2,0:T(8,128)(2,1)}), bf16[64,768,24]{1,2,0:T(8,128)(2,1)}, u32[]{:S(2)}, u32[]{:S(2)}) async-start(bf16[64,768,24]{1,2,0:T(8,128)(2,1)} %bitcast.24), calls=%async_computation.3 | async-start | bytes 4718592 | tf_op jit(solution)/shard_map/all_to_all | solution.py:33
  145.3 73.5 %all-to-all-start.2 = ((bf16[64,2652,12]{1,2,0:T(8,128)(2,1)}), bf16[64,2652,12]{1,2,0:T(8,128)(2,1)}, u32[]{:S(2)}, u32[]{:S(2)}) async-start(bf16[64,2652,12]{1,2,0:T(8,128)(2,1)} %bitcast.22), calls=%async_computation.2 | async-start | bytes 11010048 | tf_op jit(solution)/shard_map/all_to_all | solution.py:33
where the time goes:
time: 264 us; the launch traced here: 262 us
  waiting for transfers between devices  132 us (50%)
  blocking collectives  34.8 us (13%)
  starting transfers between devices  32.5 us (12%)
  local copies, waits for them, and re-layouts  26.3 us (10%)
  matrix products  17.8 us (7%)
  other arithmetic  16 us (6%)
  between operations  3.43 us (1%)
    all_to_all x3, waiting for transfers between devices, sum_at_owner(): blocks = lax.all_to_all(cut_along(shard, dim, size), axis, 0, 0, tiled=True)  101 us
    psum x5, blocking collectives, one_axis_at_a_time(): shard = lax.psum(shard, axis)  34.8 us
    all_to_all x2, waiting for transfers between devices, copy_for_each(): lax.all_to_all(jnp.broadcast_to(shard[None], (size, *shard.shape)), axis,...  30.4 us
    all_to_all x3, starting transfers between devices, sum_at_owner(): blocks = lax.all_to_all(cut_along(shard, dim, size), axis, 0, 0, tiled=True)  23.2 us
    all_to_all x2, starting transfers between devices, copy_for_each(): lax.all_to_all(jnp.broadcast_to(shard[None], (size, *shard.shape)), axis,...  9.34 us
    reduce_sum x3, other arithmetic, sum_at_owner(): return jnp.sum(blocks.astype(jnp.float32), axis=0)  7.58 us
    reshape x1, local copies, waits for them, and re-layouts, cut_along(): shard.reshape(*lengths[:dim], size, lengths[dim] // size, *lengths[dim +...  7.11 us
    convert_element_type x1, local copies, waits for them, and re-layouts, per_device(): raw_first.astype(jnp.bfloat16)  6.42 us
  transfers between devices with their start and end apart: 5, of which 5 were waited for; matrix products, arithmetic and copies ran while one was open for 16% of the time, Pallas kernels for 0%

commit v1 on v0

v1 whole, which is shorter than its diff:
```python
import jax
import jax.numpy as jnp
from jax import lax
from jax.sharding import Mesh
from jax.sharding import PartitionSpec as P

BLOCK = 128
PARAMS = 8469504
DP = ("dp_0", "dp_1", "dp_2", "dp_3")
MP_DP = ("mp", "dp_0", "dp_1", "dp_2", "dp_3")
ALL = DP + ("mp",)
Y, ZH, X, CORE = DP
LANES = 128


def swap(shard, axis):
    return lax.ppermute(shard, axis, [(0, 1), (1, 0)])


def across_hi(shard):
    return lax.ppermute(shard, (ZH, "mp"), [(0, 3), (3, 0), (1, 2), (2, 1)])


def pick(blocks, index, dim):
    return lax.dynamic_index_in_dim(blocks, index, dim, keepdims=False)


def wide(shard):
    return shard.astype(jnp.float32)


def narrow(shard):
    return shard.astype(jnp.bfloat16)


def sum_over_ring(blocks, axis, dim):
    size = lax.axis_size(axis)
    me = lax.axis_index(axis)
    total = wide(pick(blocks, me, dim))
    for step in (2, 1, 3) if size == 4 else (1,):
        part = pick(blocks, lax.rem(me + step, size), dim)
        total += wide(lax.ppermute(part, axis, [(i, (i + step) % size) for i in range(size)]))
    return total


def silu_slope(pre_act):
    sigmoid_of = jax.nn.sigmoid(pre_act)
    return sigmoid_of * (1.0 + pre_act * (1.0 - sigmoid_of))


def dot(left, right):
    return jnp.dot(left, right, preferred_element_type=jnp.float32)


def other_half_of(w_last, core):
    rows = w_last.shape[0] // 2
    width = w_last.shape[1]
    half = lax.dynamic_slice_in_dim(w_last, core * rows, rows, 0)
    first, second = 104, 384
    pieces = (
        swap(half[:, :first], "mp"),
        across_hi(half[:, first:second]),
        across_hi(half[:, second:width]),
    )
    mine = jnp.concatenate(pieces, 1)
    theirs = jnp.concatenate([swap(piece, CORE) for piece in pieces], 1)
    is_first = core == 0
    return jnp.concatenate(
        [jnp.where(is_first, mine, theirs), jnp.where(is_first, theirs, mine)], 0
    )


def per_device(belief, target_value, counts, w_first, w_middle, w_last):
    total_rows = belief.shape[0]
    own_width = w_last.shape[1]
    units = w_first.shape[1]
    core = lax.axis_index(CORE)
    mp = lax.axis_index("mp")
    w_other = other_half_of(w_last, core)
    live_rows = (counts[:, None] > jnp.arange(BLOCK, dtype=jnp.int32)[None, :]).reshape(total_rows)
    live_mask = live_rows.astype(jnp.float32)[:, None]

    pre_first = dot(belief, w_first)
    act_first = narrow(jax.nn.silu(pre_first))
    partial_middle = dot(act_first, w_middle)
    pre_middle = partial_middle + wide(swap(narrow(partial_middle), "mp"))
    act_middle = narrow(jax.nn.silu(pre_middle))

    def slope_of(weights, owner):
        target = lax.dynamic_slice_in_dim(target_value, owner * own_width, own_width, 1)
        mismatch = dot(act_middle, weights) - wide(target)
        return narrow(jnp.clip(mismatch, -1.0, 1.0) * live_mask)

    slope_own = slope_of(w_last, mp)
    slope_other = slope_of(w_other, 1 - mp)
    back_middle = dot(slope_own, w_last.T) + dot(slope_other, w_other.T)
    slope_middle = narrow(back_middle * silu_slope(pre_middle))
    back_first = dot(slope_middle, w_middle.T)
    slope_first = narrow(back_first * silu_slope(pre_first))

    block = units // 64
    place = jnp.arange(units, dtype=jnp.int32)
    source = (place % (32 * block) // block * 2 + place // (32 * block)) * block + place % block
    onehot = (place[:, None] == source[None, :]).astype(jnp.bfloat16)
    slope_first = narrow(dot(slope_first, onehot))

    def half_sum(blocks_of):
        sent = swap(narrow(blocks_of(1 - core)), CORE)
        return narrow(blocks_of(core) + wide(sent))

    def first_blocks(which):
        columns = lax.dynamic_slice_in_dim(slope_first, which * (units // 2), units // 2, 1)
        return dot(columns.T, belief)

    raw_last_t = dot(act_middle.T, slope_own).reshape(32, 2, 24, own_width)
    raw_middle_t = dot(slope_middle.T, act_first).reshape(32, 2, 24, units)
    half_last = half_sum(lambda which: pick(raw_last_t, which, 1))
    half_middle = half_sum(lambda which: pick(raw_middle_t, which, 1))
    half_first = half_sum(first_blocks)

    def shard_of(half, order):
        lengths = half.shape[-2:]
        blocks = half.reshape(4, 2, 4, *lengths)
        names = [Y, ZH, X]
        for axis in order:
            dim = names.index(axis)
            names.pop(dim)
            blocks = sum_over_ring(narrow(blocks), axis, dim)
        return blocks

    shard_last = shard_of(half_last, (X, Y, ZH))
    shard_middle = shard_of(half_middle, (X, Y, ZH))
    shard_first = shard_of(half_first.reshape(32, block, -1), (Y, X, ZH))

    local_squares = (
        jnp.sum(shard_first * shard_first)
        + jnp.sum(shard_middle * shard_middle)
        + jnp.sum(shard_last * shard_last)
    )
    gathered = lax.all_to_all(
        jnp.broadcast_to(local_squares, (128, 8, LANES)), ALL, 0, 0, tiled=True
    )
    square_sum = jnp.sum(gathered[:, 0, 0])
    norm_scale = lax.rsqrt(square_sum / PARAMS + 1e-06)
    return ((shard_first * norm_scale).T, (shard_middle * norm_scale).T, shard_last * norm_scale)


def solution(mesh):
    finer = Mesh(mesh.devices.reshape(4, 2, 4, 2, mesh.shape["mp"]), ALL)
    return jax.shard_map(
        per_device,
        mesh=finer,
        in_specs=(P(DP, None), P(DP, None), P(DP), P(None, "mp"), P("mp", None), P(None, "mp")),
        out_specs=(P(None, MP_DP), P("mp", DP), P(DP, "mp")),
        check_vma=False,
    )
```

time: 264 us -> 187 us (0.71)
  waiting for transfers between devices: 132 us -> 44.5 us
  matrix products: 17.8 us -> 31.3 us
  starting transfers between devices: 32.5 us -> 41.1 us
  blocking collectives: 34.8 us -> 27.1 us
    all_to_all x5 -> x0, waiting for transfers between devices: 132 us -> none  [the longest x3 101 us: sum_at_owner(): blocks = lax.all_to_all(cut_along(shard, dim, size), axis, 0, 0, tiled=True)]
    ppermute x0 -> x31, waiting for transfers between devices: none -> 44.5 us  [the longest x21 32.2 us: sum_over_ring(): lax.ppermute(part, axis, [(i, (i + step) % size) for i in range(size)])]
    ppermute x0 -> x31, starting transfers between devices: none -> 41.1 us  [the longest x21 27.5 us: sum_over_ring(): lax.ppermute(part, axis, [(i, (i + step) % size) for i in range(size)])]
    psum x5 -> x0, blocking collectives: 34.8 us -> none  [one_axis_at_a_time(): shard = lax.psum(shard, axis)]
    all_to_all x5 -> x0, starting transfers between devices: 32.5 us -> none  [the longest x3 23.2 us: sum_at_owner(): blocks = lax.all_to_all(cut_along(shard, dim, size), axis, 0, 0, tiled=True)]
    all_to_all x0 -> x1, blocking collectives: none -> 27.1 us  [per_device(): lax.all_to_all(jnp.broadcast_to(local_squares, (128, 8, LANES)), ALL, 0,...]
    dot_general x7 -> x10, matrix products: 17.8 us -> 31.3 us  [dot(): return jnp.dot(left, right, preferred_element_type=jnp.float32)]
    reduce_sum x5 -> x1, other arithmetic: 11.5 us -> 0.73 us  [per_device(): square_sum = jnp.sum(gathered[:, 0, 0])]
  transfers between devices with their start and end apart: 5 -> 31, of which waited for: 5 -> 12; matrix products, arithmetic and copies ran while one was open for 16% -> 33% of each run, Pallas kernels for 0% -> 0%
where the time goes in v1:
time: 187 us
  waiting for transfers between devices  44.5 us (24%)
  starting transfers between devices  41.1 us (22%)
  matrix products  31.3 us (17%)
  blocking collectives  27.1 us (14%)
  local copies, waits for them, and re-layouts  23.9 us (13%)
  other arithmetic  15.2 us (8%)
  between operations  3.61 us (2%)
    ppermute x21, waiting for transfers between devices, sum_over_ring(): lax.ppermute(part, axis, [(i, (i + step) % size) for i in range(size)])  32.2 us
    dot_general x10, matrix products, dot(): return jnp.dot(left, right, preferred_element_type=jnp.float32)  31.3 us
    ppermute x21, starting transfers between devices, sum_over_ring(): lax.ppermute(part, axis, [(i, (i + step) % size) for i in range(size)])  27.5 us
    all_to_all x1, blocking collectives, per_device(): lax.all_to_all(jnp.broadcast_to(local_squares, (128, 8, LANES)), ALL, 0,...  27.1 us
    ppermute x8, starting transfers between devices, swap(): return lax.ppermute(shard, axis, [(0, 1), (1, 0)])  10.9 us
    convert_element_type x8, other arithmetic, narrow(): return shard.astype(jnp.bfloat16)  7.39 us
    ppermute x8, waiting for transfers between devices, swap(): return lax.ppermute(shard, axis, [(0, 1), (1, 0)])  6.45 us
    ppermute x2, waiting for transfers between devices, across_hi(): return lax.ppermute(shard, (ZH, 'mp'), [(0, 3), (3, 0), (1, 2), (2, 1)])  5.89 us
  transfers between devices with their start and end apart: 31, of which 12 were waited for; matrix products, arithmetic and copies ran while one was open for 33% of the time, Pallas kernels for 0%

profile of v1, /device:TPU:1, one launch (start us, length us, event | category | flops | bytes accessed | tf_op | source)
XLA Modules:
  0.0 186.6 jit_solution(11142483883836296618)
XLA Ops:
  0.7 1.1 constant_dynamic-slice_fusion
  1.7 2.5 %collective-permute-start.1 = (bf16[768,104]{0,1:T(8,128)(2,1)S(1)}, bf16[768,104]{0,1:T(8,128)(2,1)S(1)}, u32[]{:S(2)}, u32[]{:S(2)}) collective-permute-start(bf16[768,104]{0,1:T(8,128)(2,1)S(1)} %constant_dynamic-slice_fusion), channel_id=1, source_target_pairs={{0,1},{1,0},{2,3},{3,2},{4,5},{5,4},{6,7},{7,6},{8,9},{9,8},{10,11... | collective-permute-start | bytes 479240 | tf_op jit(solution)/shard_map/ppermute | solution.py:17
  4.3 1.8 dynamic-slice.2
  6.1 2.2 %collective-permute-start.3 = (bf16[768,279]{0,1:T(8,128)(2,1)}, bf16[768,279]{0,1:T(8,128)(2,1)S(1)}, u32[]{:S(2)}, u32[]{:S(2)}) collective-permute-start(bf16[768,279]{0,1:T(8,128)(2,1)} %dynamic-slice.2), channel_id=1, source_target_pairs={{0,17},{17,0},{1,16},{16,1},{2,19},{19,2},{3,18},{18,3},{4,21},{21... | collective-permute-start | bytes 1285640 | tf_op jit(solution)/shard_map/ppermute | solution.py:21
  8.4 1.8 dynamic-slice.1
  10.6 3.9 %fusion.86 = f32[256,768]{1,0:T(8,128)S(1)} fusion(bf16[256,2652]{0,1:T(8,128)(2,1)} %param.6, bf16[2652,768]{1,0:T(8,128)(2,1)} %param.9), kind=kOutput, calls=%fused_computation.154 | convolution fusion | flops 1042808832 | bytes 6217728 | tf_op jit(solution)/shard_map/dot_general | solution.py:52
  14.5 2.3 %fusion.85 = (bf16[256,1536]{1,0:T(8,128)(2,1)}, f32[256,1536]{1,0:T(8,128)}) fusion(bf16[768,1536]{1,0:T(8,128)(2,1)S(1)} %copy-done, f32[256,768]{1,0:T(8,128)S(1)} %fusion.86), kind=kOutput, calls=%fused_computation.153 | convolution fusion | flops 605356032 | bytes 5505024 | tf_op jit(solution)/shard_map/dot_general | solution.py:52
  17.2 1.5 collective-permute-start.4
  18.8 1.0 collective-permute-done.4
  19.7 1.6 collective-permute-start.6
  21.3 5.9 %collective-permute-done.2 = bf16[768,280]{0,1:T(8,128)(2,1)S(1)} collective-permute-done((bf16[768,280]{0,1:T(8,128)(2,1)}, bf16[768,280]{0,1:T(8,128)(2,1)S(1)}, u32[]{:S(2)}, u32[]{:S(2)}) %collective-permute-start.2) | collective-permute-done | bytes 430112 | tf_op jit(solution)/shard_map/ppermute | solution.py:21
  27.2 1.9 collective-permute-start.5
  29.1 5.5 %collective-permute-done = bf16[256,1536]{1,0:T(8,128)(2,1)} collective-permute-done((bf16[256,1536]{1,0:T(8,128)(2,1)}, bf16[256,1536]{1,0:T(8,128)(2,1)}, u32[]{:S(2)}, u32[]{:S(2)}) %collective-permute-start) | collective-permute-done | bytes 786464 | tf_op jit(solution)/shard_map/ppermute | solution.py:17
  34.6 2.7 %fusion.16 = bf16[256,663]{0,1:T(8,128)(2,1)S(1)} fusion(bf16[1536,663]{0,1:T(8,128)(2,1)S(1)} %copy-done.5, f32[256]{0:T(256)S(1)} %fusion.76, bf16[256,1326]{0,1:T(8,128)(2,1)} %param.7, s32[]{:T(128)S(6)} %select_n.131, f32[256,1536]{1,0:T(8,128)} %get-tuple-element.24, bf16[256,1536]{1,0:T(8,128)(2,1)} %collective-permute-done), kind=kOutput, calls=%fused_computation.31 | convolution fusion | flops 525005568 | bytes 5075972 | tf_op jit(solution)/shard_map/dot_general | solution.py:52
  37.4 2.3 %fusion.84 = f32[1536,663]{1,0:T(8,128)S(1)} fusion(bf16[256,663]{0,1:T(8,128)(2,1)S(1)} %fusion.16, f32[256,1536]{1,0:T(8,128)S(1)} %copy-done.13, bf16[256,1536]{1,0:T(8,128)(2,1)} %collective-permute-done), kind=kOutput, calls=%fused_computation.152 | convolution fusion | flops 524156928 | bytes 6772224 | tf_op jit(solution)/shard_map/dot_general | solution.py:52
  39.7 1.3 fusion.18
  40.9 2.4 %collective-permute-start.23 = (bf16[32,24,663]{2,1,0:T(8,128)(2,1)}, bf16[32,24,663]{2,1,0:T(8,128)(2,1)}, u32[]{:S(2)}, u32[]{:S(2)}) collective-permute-start(bf16[32,24,663]{2,1,0:T(8,128)(2,1)} %fusion.18), channel_id=1, source_target_pairs={{0,2},{2,0},{1,3},{3,1},{4,6},{6,4},{5,7},{7,5},{8,10},{10,8},{9,1... | collective-permute-start | bytes 3055112 | tf_op jit(solution)/shard_map/ppermute | solution.py:17
  43.3 2.0 %fusion.87 = f32[256,1536]{1,0:T(8,128)} fusion(bf16[256,663]{0,1:T(8,128)(2,1)S(1)} %fusion.16, bf16[1536,663]{0,1:T(8,128)(2,1)S(1)} %copy-done.5), kind=kOutput, calls=%fused_computation.155 | convolution fusion | flops 521404416 | bytes 3949056 | tf_op jit(solution)/shard_map/dot_general | solution.py:52
  45.4 1.5 broadcast_select_fusion.1
  46.9 6.8 %fusion.1 = bf16[256,1536]{1,0:T(8,128)(2,1)S(1)} fusion(f32[256,1536]{1,0:T(8,128)} %fusion.87, bf16[768,663]{0,1:T(8,128)(2,1)} %get-tuple-element.7, bf16[768,663]{0,1:T(8,128)(2,1)} %get-tuple-element.6, f32[256,1536]{1,0:T(8,128)} %get-tuple-element.24, bf16[256,1536]{1,0:T(8,128)(2,1)} %collective-permute-done, bf16[256,1326]{0,1:T(8,128)(2,1)} %param.7, ...), kind=kOutput, calls=%fused_computation.4 | convolution fusion | flops 1059275520 | bytes 11498500 | tf_op jit(solution)/shard_map/dot_general | solution.py:52
  53.7 3.3 %fusion.15 = bf16[256,768]{1,0:T(8,128)(2,1)} fusion(s32[768]{0:T(1024)S(1)} %fusion.66, bf16[256,1536]{1,0:T(8,128)(2,1)S(1)} %fusion.1, bf16[768,1536]{1,0:T(8,128)(2,1)S(1)} %copy-done, f32[256,768]{1,0:T(8,128)} %copy-done.7), kind=kOutput, calls=%fused_computation.30 | convolution fusion | flops 908525568 | bytes 4328448 | tf_op jit(solution)/shard_map/dot_general | solution.py:52
  57.0 2.0 %fusion.82 = f32[1536,768]{1,0:T(8,128)S(1)} fusion(bf16[256,1536]{1,0:T(8,128)(2,1)S(1)} %fusion.1, f32[256,768]{1,0:T(8,128)} %copy-done.7), kind=kOutput, calls=%fused_computation.150 | convolution fusion | flops 604962816 | bytes 6291456 | tf_op jit(solution)/shard_map/dot_general | solution.py:52
  59.0 2.2 %copy-done.1 = f32[1536,768]{1,0:T(8,128)} copy-done((f32[1536,768]{1,0:T(8,128)}, f32[1536,768]{1,0:T(8,128)S(1)}, u32[]{:S(2)}) %copy-start.1) | copy-done | bytes 4718616
  61.7 2.3 %convolution_convert_fusion = bf16[384,2652]{0,1:T(8,128)(2,1)} fusion(bf16[256,2652]{0,1:T(8,128)(2,1)S(1)} %copy-done.3, bf16[256,768]{1,0:T(8,128)(2,1)S(1)} %copy-done.10, s32[]{:T(128)S(6)} %select_n.142), kind=kOutput, calls=%fused_computation | convolution fusion | flops 522422784 | bytes 3593220 | tf_op jit(solution)/shard_map/dot_general | solution.py:52
  64.3 2.4 %fusion.2 = bf16[32,24,663]{2,1,0:T(8,128)(2,1)S(1)} fusion(bf16[32,24,663]{2,1,0:T(8,128)(2,1)} %collective-permute-done.23, f32[32,2,24,663]{3,2,1,0:T(8,128)} %bitcast.120, s32[]{:T(128)S(6)} %select_n.153), kind=kLoop, calls=%fused_computation.7 | loop fusion | flops 1527552 | bytes 4073476 | tf_op jit(solution)/shard_map/convert_element_type | solution.py:33
  66.9 2.8 %collective-permute-start.24 = (bf16[4,2,24,663]{3,2,1,0:T(8,128)(2,1)S(1)}, bf16[4,2,24,663]{3,2,1,0:T(8,128)(2,1)S(1)}, u32[]{:S(2)}, u32[]{:S(2)}) collective-permute-start(bf16[4,2,24,663]{3,2,1,0:T(8,128)(2,1)S(1)} %get-tuple-element.8), channel_id=1, source_target_pairs={{0,8},{4,12},{8,0},{12,4},{1,9},{5,13},{9,1},{13,5},{2,10},{6,14},... | collective-permute-start | bytes 763784 | tf_op jit(solution)/shard_map/ppermute | solution.py:42
  69.7 0.8 collective-permute-start.26
  71.2 1.6 fusion.3
  72.7 4.2 %collective-permute-done.24 = bf16[4,2,24,663]{3,2,1,0:T(8,128)(2,1)S(1)} collective-permute-done((bf16[4,2,24,663]{3,2,1,0:T(8,128)(2,1)S(1)}, bf16[4,2,24,663]{3,2,1,0:T(8,128)(2,1)S(1)}, u32[]{:S(2)}, u32[]{:S(2)}) %collective-permute-start.24) | collective-permute-done | bytes 254624 | tf_op jit(solution)/shard_map/ppermute | solution.py:42
  77.0 6.4 %collective-permute-done.26 = bf16[4,2,24,663]{3,2,1,0:T(8,128)(2,1)S(1)} collective-permute-done((bf16[4,2,24,663]{3,2,1,0:T(8,128)(2,1)S(1)}, bf16[4,2,24,663]{3,2,1,0:T(8,128)(2,1)S(1)}, u32[]{:S(2)}, u32[]{:S(2)}) %collective-permute-start.26) | collective-permute-done | bytes 254624 | tf_op jit(solution)/shard_map/ppermute | solution.py:42
  83.9 3.0 %collective-permute-start.27 = (bf16[2,24,663]{2,1,0:T(8,128)(2,1)S(1)}, bf16[2,24,663]{2,1,0:T(8,128)(2,1)S(1)}, u32[]{:S(2)}, u32[]{:S(2)}) collective-permute-start(bf16[2,24,663]{2,1,0:T(8,128)(2,1)S(1)} %get-tuple-element.17), channel_id=1, source_target_pairs={{0,64},{32,96},{64,0},{96,32},{1,65},{33,97},{65,1},{97,33},{2,66}... | collective-permute-start | bytes 190952 | tf_op jit(solution)/shard_map/ppermute | solution.py:42
  86.9 0.8 collective-permute-start.29
  87.7 0.7 collective-permute-start.28
  88.4 1.0 dynamic-slice_bitcast_fusion.5
  89.4 2.7 %collective-permute-start.16 = (bf16[4,2,24,768]{3,2,1,0:T(8,128)(2,1)}, bf16[4,2,24,768]{3,2,1,0:T(8,128)(2,1)}, u32[]{:S(2)}, u32[]{:S(2)}) collective-permute-start(bf16[4,2,24,768]{3,2,1,0:T(8,128)(2,1)} %get-tuple-element.11), channel_id=1, source_target_pairs={{0,8},{4,12},{8,0},{12,4},{1,9},{5,13},{9,1},{13,5},{2,10},{6,14},... | collective-permute-start | bytes 884744 | tf_op jit(solution)/shard_map/ppermute | solution.py:42
  92.1 0.9 collective-permute-start.18
  94.9 2.1 %collective-permute-start.30 = (bf16[24,663]{1,0:T(8,128)(2,1)}, bf16[24,663]{1,0:T(8,128)(2,1)}, u32[]{:S(2)}, u32[]{:S(2)}) collective-permute-start(bf16[24,663]{1,0:T(8,128)(2,1)} %dynamic-slice_bitcast_fusion.16), channel_id=1, source_target_pairs={{0,16},{16,0},{1,17},{17,1},{2,18},{18,2},{3,19},{19,3},{4,20},{20... | collective-permute-start | bytes 95480 | tf_op jit(solution)/shard_map/ppermute | solution.py:42
  97.0 3.8 %add_convert_fusion = bf16[384,2652]{0,1:T(8,128)(2,1)} fusion(bf16[384,2652]{0,1:T(8,128)(2,1)} %collective-permute-done.7, bf16[256,2652]{0,1:T(8,128)(2,1)S(1)} %copy-done.4, bf16[256,768]{1,0:T(8,128)(2,1)S(1)} %copy-done.11, s32[]{:T(128)S(6)} %select_n.141), kind=kOutput, calls=%fused_computation.1 | convolution fusion | flops 524459520 | bytes 5629956 | tf_op jit(solution)/shard_map/dot_general | solution.py:52
  100.8 4.1 %copy.40 = bf16[384,2652]{1,0:T(8,128)(2,1)} copy(bf16[384,2652]{0,1:T(8,128)(2,1)} %add_convert_fusion) | data formatting | bytes 4073472 | tf_op jit(solution)/shard_map/convert_element_type | solution.py:33
  104.9 4.1 %reshape_reshape.3 = bf16[4,2,4,12,2652]{4,3,2,1,0:T(8,128)(2,1)} reshape(bf16[384,2652]{1,0:T(8,128)(2,1)} %copy.40) | data formatting | bytes 4073472 | tf_op jit(solution)/shard_map/reshape;reshape | solution.py:123
  108.9 1.7 constant_dynamic-slice_fusion.3
  110.6 1.0 copy.61
  111.6 1.0 copy.59
  112.6 1.0 copy.60
  114.0 2.3 %collective-permute-start.10 = (bf16[2,4,12,2652]{3,1,2,0:T(4,128)(2,1)}, bf16[2,4,12,2652]{3,1,2,0:T(4,128)(2,1)}, u32[]{:S(2)}, u32[]{:S(2)}) collective-permute-start(bf16[2,4,12,2652]{3,1,2,0:T(4,128)(2,1)} %bitcast.110), channel_id=1, source_target_pairs={{0,96},{32,0},{64,32},{96,64},{1,97},{33,1},{65,33},{97,65},{2,98}... | collective-permute-start | bytes 1527560 | tf_op jit(solution)/shard_map/ppermute | solution.py:42
  116.9 1.4 multiply_reduce_fusion.1
  118.3 1.3 fusion.30
  119.7 2.5 %collective-permute-start.19 = (bf16[2,24,768]{2,1,0:T(8,128)(2,1)S(1)}, bf16[2,24,768]{2,1,0:T(8,128)(2,1)S(1)}, u32[]{:S(2)}, u32[]{:S(2)}) collective-permute-start(bf16[2,24,768]{2,1,0:T(8,128)(2,1)S(1)} %get-tuple-element.20), channel_id=1, source_target_pairs={{0,64},{32,96},{64,0},{96,32},{1,65},{33,97},{65,1},{97,33},{2,66}... | collective-permute-start | bytes 221192 | tf_op jit(solution)/shard_map/ppermute | solution.py:42
  122.1 0.8 collective-permute-start.21
  122.9 3.0 %collective-permute-done.9 = bf16[2,4,12,2652]{3,1,2,0:T(4,128)(2,1)} collective-permute-done((bf16[2,4,12,2652]{3,1,2,0:T(4,128)(2,1)}, bf16[2,4,12,2652]{3,1,2,0:T(4,128)(2,1)}, u32[]{:S(2)}, u32[]{:S(2)}) %collective-permute-start.9) | collective-permute-done | bytes 509216 | tf_op jit(solution)/shard_map/ppermute | solution.py:42
  125.9 11.6 %collective-permute-done.8 = bf16[2,4,12,2652]{3,1,2,0:T(4,128)(2,1)} collective-permute-done((bf16[2,4,12,2652]{3,1,2,0:T(4,128)(2,1)}, bf16[2,4,12,2652]{3,1,2,0:T(4,128)(2,1)}, u32[]{:S(2)}, u32[]{:S(2)}) %collective-permute-start.8) | collective-permute-done | bytes 509216 | tf_op jit(solution)/shard_map/ppermute | solution.py:42
  137.5 1.8 fusion.7
  139.4 2.6 %collective-permute-start.11 = (bf16[2,12,2652]{2,1,0:T(8,128)(2,1)S(1)}, bf16[2,12,2652]{2,1,0:T(8,128)(2,1)S(1)}, u32[]{:S(2)}, u32[]{:S(2)}) collective-permute-start(bf16[2,12,2652]{2,1,0:T(8,128)(2,1)S(1)} %get-tuple-element.14), channel_id=1, source_target_pairs={{0,8},{4,12},{8,0},{12,4},{1,9},{5,13},{9,1},{13,5},{2,10},{6,14},... | collective-permute-start | bytes 381896 | tf_op jit(solution)/shard_map/ppermute | solution.py:42
  142.2 1.2 collective-permute-start.12
  143.5 0.9 collective-permute-start.22
  144.4 0.8 collective-permute-done.11
  145.2 1.4 collective-permute-done.13
  146.7 1.0 collective-permute-done.12
  147.8 1.0 collective-permute-start.14
  149.4 3.3 %collective-permute-done.14 = bf16[12,2652]{1,0:T(8,128)(2,1)S(1)} collective-permute-done((bf16[12,2652]{1,0:T(8,128)(2,1)S(1)}, bf16[12,2652]{1,0:T(8,128)(2,1)S(1)}, u32[]{:S(2)}, u32[]{:S(2)}) %collective-permute-start.14) | collective-permute-done | bytes 63680 | tf_op jit(solution)/shard_map/ppermute | solution.py:42
  155.3 27.1 %all_to_all.5 = f32[128,8,128]{2,1,0:T(8,128)S(1)} all-to-all(f32[128,8,128]{2,1,0:T(8,128)S(1)} %broadcast_in_dim.2), channel_id=1, replica_groups=mesh['dp_0'=4,'dp_1'=2,'dp_2'=4,'dp_3'=2,'mp'=2] {'dp_0','dp_1','dp_2','..., dimensions={0} | all-to-all | bytes 1048576 | tf_op jit(solution)/shard_map/all_to_all | solution.py:140
  182.4 0.7 slice_reduce_fusion
  183.8 0.7 multiply_bitcast_fusion
  184.5 1.4 fusion.50
  (81 shorter events, 8.5 us)
Async XLA Ops:
  0.6 13.9 %copy-start = (bf16[768,1536]{1,0:T(8,128)(2,1)S(1)}, bf16[768,1536]{1,0:T(8,128)(2,1)}, u32[]{:S(2)}) copy-start(bf16[768,1536]{1,0:T(8,128)(2,1)} %param.10) | copy-start | bytes 7077892
  1.7 15.4 %collective-permute-start.1 = (bf16[768,104]{0,1:T(8,128)(2,1)S(1)}, bf16[768,104]{0,1:T(8,128)(2,1)S(1)}, u32[]{:S(2)}, u32[]{:S(2)}) collective-permute-start(bf16[768,104]{0,1:T(8,128)(2,1)S(1)} %constant_dynamic-slice_fusion), channel_id=1, source_target_pairs={{0,1},{1,0},{2,3},{3,2},{4,5},{5,4},{6,7},{7,6},{8,9},{9,8},{10,11... | collective-permute-start | bytes 479240 | tf_op jit(solution)/shard_map/ppermute | solution.py:17
  6.1 13.6 %collective-permute-start.3 = (bf16[768,279]{0,1:T(8,128)(2,1)}, bf16[768,279]{0,1:T(8,128)(2,1)S(1)}, u32[]{:S(2)}, u32[]{:S(2)}) collective-permute-start(bf16[768,279]{0,1:T(8,128)(2,1)} %dynamic-slice.2), channel_id=1, source_target_pairs={{0,17},{17,0},{1,16},{16,1},{2,19},{19,2},{3,18},{18,3},{4,21},{21... | collective-permute-start | bytes 1285640 | tf_op jit(solution)/shard_map/ppermute | solution.py:21
  10.2 17.1 %collective-permute-start.2 = (bf16[768,280]{0,1:T(8,128)(2,1)}, bf16[768,280]{0,1:T(8,128)(2,1)S(1)}, u32[]{:S(2)}, u32[]{:S(2)}) collective-permute-start(bf16[768,280]{0,1:T(8,128)(2,1)} %dynamic-slice.1), channel_id=1, source_target_pairs={{0,17},{17,0},{1,16},{16,1},{2,19},{19,2},{3,18},{18,3},{4,21},{21... | collective-permute-start | bytes 1290248 | tf_op jit(solution)/shard_map/ppermute | solution.py:21
  14.5 2.3 %copy-start.7 = (f32[256,768]{1,0:T(8,128)}, f32[256,768]{1,0:T(8,128)S(1)}, u32[]{:S(2)}) copy-start(f32[256,768]{1,0:T(8,128)S(1)} %fusion.86) | copy-start | bytes 2359300
  14.5 2.6 %copy-start.12 = (s32[2]{0:T(128)S(1)}, s32[2]{0:T(128)}, u32[]{:S(2)}) copy-start(s32[2]{0:T(128)} %param.8) | copy-start | bytes 28
  16.8 17.8 %collective-permute-start = (bf16[256,1536]{1,0:T(8,128)(2,1)}, bf16[256,1536]{1,0:T(8,128)(2,1)}, u32[]{:S(2)}, u32[]{:S(2)}) collective-permute-start(bf16[256,1536]{1,0:T(8,128)(2,1)} %get-tuple-element.23), channel_id=1, source_target_pairs={{0,1},{1,0},{2,3},{3,2},{4,5},{5,4},{6,7},{7,6},{8,9},{9,8},{10,11... | collective-permute-start | bytes 2359304 | tf_op jit(solution)/shard_map/ppermute | solution.py:17
  17.2 2.5 %collective-permute-start.4 = (bf16[768,104]{0,1:T(8,128)(2,1)S(1)}, bf16[768,104]{0,1:T(8,128)(2,1)S(1)}, u32[]{:S(2)}, u32[]{:S(2)}) collective-permute-start(bf16[768,104]{0,1:T(8,128)(2,1)S(1)} %collective-permute-done.1), channel_id=1, source_target_pairs={{0,2},{2,0},{1,3},{3,1},{4,6},{6,4},{5,7},{7,5},{8,10},{10,8},{9,1... | collective-permute-start | bytes 479240 | tf_op jit(solution)/shard_map/ppermute | solution.py:17
  18.7 15.9 %copy-start.5 = (bf16[1536,663]{0,1:T(8,128)(2,1)S(1)}, bf16[1536,663]{0,1:T(8,128)(2,1)}, u32[]{:S(2)}) copy-start(bf16[1536,663]{0,1:T(8,128)(2,1)} %param.11) | copy-start | bytes 6110212
  19.7 25.7 %collective-permute-start.6 = (bf16[768,279]{0,1:T(8,128)(2,1)S(1)}, bf16[768,279]{0,1:T(8,128)(2,1)S(1)}, u32[]{:S(2)}, u32[]{:S(2)}) collective-permute-start(bf16[768,279]{0,1:T(8,128)(2,1)S(1)} %collective-permute-done.3), channel_id=1, source_target_pairs={{0,2},{2,0},{1,3},{3,1},{4,6},{6,4},{5,7},{7,5},{8,10},{10,8},{9,1... | collective-permute-start | bytes 1285640 | tf_op jit(solution)/shard_map/ppermute | solution.py:17
  27.2 18.1 %collective-permute-start.5 = (bf16[768,280]{0,1:T(8,128)(2,1)S(1)}, bf16[768,280]{0,1:T(8,128)(2,1)S(1)}, u32[]{:S(2)}, u32[]{:S(2)}) collective-permute-start(bf16[768,280]{0,1:T(8,128)(2,1)S(1)} %collective-permute-done.2), channel_id=1, source_target_pairs={{0,2},{2,0},{1,3},{3,1},{4,6},{6,4},{5,7},{7,5},{8,10},{10,8},{9,1... | collective-permute-start | bytes 1290248 | tf_op jit(solution)/shard_map/ppermute | solution.py:17
  34.6 2.7 %copy-start.13 = (f32[256,1536]{1,0:T(8,128)S(1)}, f32[256,1536]{1,0:T(8,128)}, u32[]{:S(2)}) copy-start(f32[256,1536]{1,0:T(8,128)} %get-tuple-element.24) | copy-start | bytes 4718596
  39.7 5.7 %copy-start.6 = (f32[1536,663]{1,0:T(8,128)}, f32[1536,663]{1,0:T(8,128)S(1)}, u32[]{:S(2)}) copy-start(f32[1536,663]{1,0:T(8,128)S(1)} %fusion.84) | copy-start | bytes 12220420
  40.9 23.4 %collective-permute-start.23 = (bf16[32,24,663]{2,1,0:T(8,128)(2,1)}, bf16[32,24,663]{2,1,0:T(8,128)(2,1)}, u32[]{:S(2)}, u32[]{:S(2)}) collective-permute-start(bf16[32,24,663]{2,1,0:T(8,128)(2,1)} %fusion.18), channel_id=1, source_target_pairs={{0,2},{2,0},{1,3},{3,1},{4,6},{6,4},{5,7},{7,5},{8,10},{10,8},{9,1... | collective-permute-start | bytes 3055112 | tf_op jit(solution)/shard_map/ppermute | solution.py:17
  59.0 2.2 %copy-start.1 = (f32[1536,768]{1,0:T(8,128)}, f32[1536,768]{1,0:T(8,128)S(1)}, u32[]{:S(2)}) copy-start(f32[1536,768]{1,0:T(8,128)S(1)} %fusion.82) | copy-start | bytes 14155780
  59.0 2.6 %copy-start.3 = (bf16[256,2652]{0,1:T(8,128)(2,1)S(1)}, bf16[256,2652]{0,1:T(8,128)(2,1)}, u32[]{:S(2)}) copy-start(bf16[256,2652]{0,1:T(8,128)(2,1)} %param.6) | copy-start | bytes 4073476
  59.0 2.7 %copy-start.10 = (bf16[256,768]{1,0:T(8,128)(2,1)S(1)}, bf16[256,768]{1,0:T(8,128)(2,1)}, u32[]{:S(2)}) copy-start(bf16[256,768]{1,0:T(8,128)(2,1)} %fusion.15) | copy-start | bytes 1179652
  61.3 9.9 %collective-permute-start.15 = (bf16[32,24,768]{2,1,0:T(8,128)(2,1)S(1)}, bf16[32,24,768]{2,1,0:T(8,128)(2,1)}, u32[]{:S(2)}, u32[]{:S(2)}) collective-permute-start(bf16[32,24,768]{2,1,0:T(8,128)(2,1)S(1)} %fusion.19), channel_id=1, source_target_pairs={{0,2},{2,0},{1,3},{3,1},{4,6},{6,4},{5,7},{7,5},{8,10},{10,8},{9,1... | collective-permute-start | bytes 3538952 | tf_op jit(solution)/shard_map/ppermute | solution.py:17
  63.9 33.0 %collective-permute-start.7 = (bf16[384,2652]{0,1:T(8,128)(2,1)}, bf16[384,2652]{0,1:T(8,128)(2,1)}, u32[]{:S(2)}, u32[]{:S(2)}) collective-permute-start(bf16[384,2652]{0,1:T(8,128)(2,1)} %convolution_convert_fusion), channel_id=1, source_target_pairs={{0,2},{2,0},{1,3},{3,1},{4,6},{6,4},{5,7},{7,5},{8,10},{10,8},{9,1... | collective-permute-start | bytes 6110216 | tf_op jit(solution)/shard_map/ppermute | solution.py:17
  64.3 6.8 %copy-start.2 = (f32[1536,768]{1,0:T(8,128)S(1)}, f32[1536,768]{1,0:T(8,128)}, u32[]{:S(2)}) copy-start(f32[1536,768]{1,0:T(8,128)} %copy-done.1) | copy-start | bytes 14155780
  66.9 10.1 %collective-permute-start.24 = (bf16[4,2,24,663]{3,2,1,0:T(8,128)(2,1)S(1)}, bf16[4,2,24,663]{3,2,1,0:T(8,128)(2,1)S(1)}, u32[]{:S(2)}, u32[]{:S(2)}) collective-permute-start(bf16[4,2,24,663]{3,2,1,0:T(8,128)(2,1)S(1)} %get-tuple-element.8), channel_id=1, source_target_pairs={{0,8},{4,12},{8,0},{12,4},{1,9},{5,13},{9,1},{13,5},{2,10},{6,14},... | collective-permute-start | bytes 763784 | tf_op jit(solution)/shard_map/ppermute | solution.py:42
  69.7 13.7 %collective-permute-start.26 = (bf16[4,2,24,663]{3,2,1,0:T(8,128)(2,1)S(1)}, bf16[4,2,24,663]{3,2,1,0:T(8,128)(2,1)S(1)}, u32[]{:S(2)}, u32[]{:S(2)}) collective-permute-start(bf16[4,2,24,663]{3,2,1,0:T(8,128)(2,1)S(1)} %get-tuple-element.9), channel_id=1, source_target_pairs={{0,12},{4,0},{8,4},{12,8},{1,13},{5,1},{9,5},{13,9},{2,14},{6,2},{... | collective-permute-start | bytes 763784 | tf_op jit(solution)/shard_map/ppermute | solution.py:42
  70.5 13.2 %collective-permute-start.25 = (bf16[4,2,24,663]{3,2,1,0:T(8,128)(2,1)S(1)}, bf16[4,2,24,663]{3,2,1,0:T(8,128)(2,1)S(1)}, u32[]{:S(2)}, u32[]{:S(2)}) collective-permute-start(bf16[4,2,24,663]{3,2,1,0:T(8,128)(2,1)S(1)} %get-tuple-element.10), channel_id=1, source_target_pairs={{0,4},{4,8},{8,12},{12,0},{1,5},{5,9},{9,13},{13,1},{2,6},{6,10},{... | collective-permute-start | bytes 763784 | tf_op jit(solution)/shard_map/ppermute | solution.py:42
  83.9 13.1 %copy-start.4 = (bf16[256,2652]{0,1:T(8,128)(2,1)S(1)}, bf16[256,2652]{0,1:T(8,128)(2,1)}, u32[]{:S(2)}) copy-start(bf16[256,2652]{0,1:T(8,128)(2,1)} %param.6) | copy-start | bytes 4073476
  83.9 13.1 %copy-start.11 = (bf16[256,768]{1,0:T(8,128)(2,1)S(1)}, bf16[256,768]{1,0:T(8,128)(2,1)}, u32[]{:S(2)}) copy-start(bf16[256,768]{1,0:T(8,128)(2,1)} %fusion.15) | copy-start | bytes 1179652
  83.9 8.2 %collective-permute-start.27 = (bf16[2,24,663]{2,1,0:T(8,128)(2,1)S(1)}, bf16[2,24,663]{2,1,0:T(8,128)(2,1)S(1)}, u32[]{:S(2)}, u32[]{:S(2)}) collective-permute-start(bf16[2,24,663]{2,1,0:T(8,128)(2,1)S(1)} %get-tuple-element.17), channel_id=1, source_target_pairs={{0,64},{32,96},{64,0},{96,32},{1,65},{33,97},{65,1},{97,33},{2,66}... | collective-permute-start | bytes 190952 | tf_op jit(solution)/shard_map/ppermute | solution.py:42
  86.9 6.1 %collective-permute-start.29 = (bf16[2,24,663]{2,1,0:T(8,128)(2,1)S(1)}, bf16[2,24,663]{2,1,0:T(8,128)(2,1)S(1)}, u32[]{:S(2)}, u32[]{:S(2)}) collective-permute-start(bf16[2,24,663]{2,1,0:T(8,128)(2,1)S(1)} %get-tuple-element.18), channel_id=1, source_target_pairs={{0,96},{32,0},{64,32},{96,64},{1,97},{33,1},{65,33},{97,65},{2,98}... | collective-permute-start | bytes 190952 | tf_op jit(solution)/shard_map/ppermute | solution.py:42
  87.7 5.9 %collective-permute-start.28 = (bf16[2,24,663]{2,1,0:T(8,128)(2,1)S(1)}, bf16[2,24,663]{2,1,0:T(8,128)(2,1)S(1)}, u32[]{:S(2)}, u32[]{:S(2)}) collective-permute-start(bf16[2,24,663]{2,1,0:T(8,128)(2,1)S(1)} %get-tuple-element.19), channel_id=1, source_target_pairs={{0,32},{32,64},{64,96},{96,0},{1,33},{33,65},{65,97},{97,1},{2,34}... | collective-permute-start | bytes 190952 | tf_op jit(solution)/shard_map/ppermute | solution.py:42
  89.4 26.9 %collective-permute-start.16 = (bf16[4,2,24,768]{3,2,1,0:T(8,128)(2,1)}, bf16[4,2,24,768]{3,2,1,0:T(8,128)(2,1)}, u32[]{:S(2)}, u32[]{:S(2)}) collective-permute-start(bf16[4,2,24,768]{3,2,1,0:T(8,128)(2,1)} %get-tuple-element.11), channel_id=1, source_target_pairs={{0,8},{4,12},{8,0},{12,4},{1,9},{5,13},{9,1},{13,5},{2,10},{6,14},... | collective-permute-start | bytes 884744 | tf_op jit(solution)/shard_map/ppermute | solution.py:42
  92.1 26.2 %collective-permute-start.18 = (bf16[4,2,24,768]{3,2,1,0:T(8,128)(2,1)}, bf16[4,2,24,768]{3,2,1,0:T(8,128)(2,1)}, u32[]{:S(2)}, u32[]{:S(2)}) collective-permute-start(bf16[4,2,24,768]{3,2,1,0:T(8,128)(2,1)} %get-tuple-element.12), channel_id=1, source_target_pairs={{0,12},{4,0},{8,4},{12,8},{1,13},{5,1},{9,5},{13,9},{2,14},{6,2},{... | collective-permute-start | bytes 884744 | tf_op jit(solution)/shard_map/ppermute | solution.py:42
  93.0 25.3 %collective-permute-start.17 = (bf16[4,2,24,768]{3,2,1,0:T(8,128)(2,1)}, bf16[4,2,24,768]{3,2,1,0:T(8,128)(2,1)}, u32[]{:S(2)}, u32[]{:S(2)}) collective-permute-start(bf16[4,2,24,768]{3,2,1,0:T(8,128)(2,1)} %get-tuple-element.13), channel_id=1, source_target_pairs={{0,4},{4,8},{8,12},{12,0},{1,5},{5,9},{9,13},{13,1},{2,6},{6,10},{... | collective-permute-start | bytes 884744 | tf_op jit(solution)/shard_map/ppermute | solution.py:42
  93.6 0.6 copy-start.8
  94.9 19.1 %collective-permute-start.30 = (bf16[24,663]{1,0:T(8,128)(2,1)}, bf16[24,663]{1,0:T(8,128)(2,1)}, u32[]{:S(2)}, u32[]{:S(2)}) collective-permute-start(bf16[24,663]{1,0:T(8,128)(2,1)} %dynamic-slice_bitcast_fusion.16), channel_id=1, source_target_pairs={{0,16},{16,0},{1,17},{17,1},{2,18},{18,2},{3,19},{19,3},{4,20},{20... | collective-permute-start | bytes 95480 | tf_op jit(solution)/shard_map/ppermute | solution.py:42
  113.6 12.3 %collective-permute-start.9 = (bf16[2,4,12,2652]{3,1,2,0:T(4,128)(2,1)}, bf16[2,4,12,2652]{3,1,2,0:T(4,128)(2,1)}, u32[]{:S(2)}, u32[]{:S(2)}) collective-permute-start(bf16[2,4,12,2652]{3,1,2,0:T(4,128)(2,1)} %bitcast.111), channel_id=1, source_target_pairs={{0,32},{32,64},{64,96},{96,0},{1,33},{33,65},{65,97},{97,1},{2,34}... | collective-permute-start | bytes 1527560 | tf_op jit(solution)/shard_map/ppermute | solution.py:42
  114.0 11.9 %collective-permute-start.10 = (bf16[2,4,12,2652]{3,1,2,0:T(4,128)(2,1)}, bf16[2,4,12,2652]{3,1,2,0:T(4,128)(2,1)}, u32[]{:S(2)}, u32[]{:S(2)}) collective-permute-start(bf16[2,4,12,2652]{3,1,2,0:T(4,128)(2,1)} %bitcast.110), channel_id=1, source_target_pairs={{0,96},{32,0},{64,32},{96,64},{1,97},{33,1},{65,33},{97,65},{2,98}... | collective-permute-start | bytes 1527560 | tf_op jit(solution)/shard_map/ppermute | solution.py:42
  116.3 21.3 %collective-permute-start.8 = (bf16[2,4,12,2652]{3,1,2,0:T(4,128)(2,1)}, bf16[2,4,12,2652]{3,1,2,0:T(4,128)(2,1)}, u32[]{:S(2)}, u32[]{:S(2)}) collective-permute-start(bf16[2,4,12,2652]{3,1,2,0:T(4,128)(2,1)} %bitcast.112), channel_id=1, source_target_pairs={{0,64},{32,96},{64,0},{96,32},{1,65},{33,97},{65,1},{97,33},{2,66}... | collective-permute-start | bytes 1527560 | tf_op jit(solution)/shard_map/ppermute | solution.py:42
  119.7 22.5 %collective-permute-start.19 = (bf16[2,24,768]{2,1,0:T(8,128)(2,1)S(1)}, bf16[2,24,768]{2,1,0:T(8,128)(2,1)S(1)}, u32[]{:S(2)}, u32[]{:S(2)}) collective-permute-start(bf16[2,24,768]{2,1,0:T(8,128)(2,1)S(1)} %get-tuple-element.20), channel_id=1, source_target_pairs={{0,64},{32,96},{64,0},{96,32},{1,65},{33,97},{65,1},{97,33},{2,66}... | collective-permute-start | bytes 221192 | tf_op jit(solution)/shard_map/ppermute | solution.py:42
  122.1 21.3 %collective-permute-start.21 = (bf16[2,24,768]{2,1,0:T(8,128)(2,1)S(1)}, bf16[2,24,768]{2,1,0:T(8,128)(2,1)S(1)}, u32[]{:S(2)}, u32[]{:S(2)}) collective-permute-start(bf16[2,24,768]{2,1,0:T(8,128)(2,1)S(1)} %get-tuple-element.21), channel_id=1, source_target_pairs={{0,96},{32,0},{64,32},{96,64},{1,97},{33,1},{65,33},{97,65},{2,98}... | collective-permute-start | bytes 221192 | tf_op jit(solution)/shard_map/ppermute | solution.py:42
  125.9 17.5 %collective-permute-start.20 = (bf16[2,24,768]{2,1,0:T(8,128)(2,1)S(1)}, bf16[2,24,768]{2,1,0:T(8,128)(2,1)S(1)}, u32[]{:S(2)}, u32[]{:S(2)}) collective-permute-start(bf16[2,24,768]{2,1,0:T(8,128)(2,1)S(1)} %get-tuple-element.22), channel_id=1, source_target_pairs={{0,32},{32,64},{64,96},{96,0},{1,33},{33,65},{65,97},{97,1},{2,34}... | collective-permute-start | bytes 221192 | tf_op jit(solution)/shard_map/ppermute | solution.py:42
  139.4 5.8 %collective-permute-start.11 = (bf16[2,12,2652]{2,1,0:T(8,128)(2,1)S(1)}, bf16[2,12,2652]{2,1,0:T(8,128)(2,1)S(1)}, u32[]{:S(2)}, u32[]{:S(2)}) collective-permute-start(bf16[2,12,2652]{2,1,0:T(8,128)(2,1)S(1)} %get-tuple-element.14), channel_id=1, source_target_pairs={{0,8},{4,12},{8,0},{12,4},{1,9},{5,13},{9,1},{13,5},{2,10},{6,14},... | collective-permute-start | bytes 381896 | tf_op jit(solution)/shard_map/ppermute | solution.py:42
  141.9 4.7 %collective-permute-start.13 = (bf16[2,12,2652]{2,1,0:T(8,128)(2,1)S(1)}, bf16[2,12,2652]{2,1,0:T(8,128)(2,1)S(1)}, u32[]{:S(2)}, u32[]{:S(2)}) collective-permute-start(bf16[2,12,2652]{2,1,0:T(8,128)(2,1)S(1)} %get-tuple-element.15), channel_id=1, source_target_pairs={{0,12},{4,0},{8,4},{12,8},{1,13},{5,1},{9,5},{13,9},{2,14},{6,2},{... | collective-permute-start | bytes 381896 | tf_op jit(solution)/shard_map/ppermute | solution.py:42
  142.2 5.5 %collective-permute-start.12 = (bf16[2,12,2652]{2,1,0:T(8,128)(2,1)S(1)}, bf16[2,12,2652]{2,1,0:T(8,128)(2,1)S(1)}, u32[]{:S(2)}, u32[]{:S(2)}) collective-permute-start(bf16[2,12,2652]{2,1,0:T(8,128)(2,1)S(1)} %get-tuple-element.16), channel_id=1, source_target_pairs={{0,4},{4,8},{8,12},{12,0},{1,5},{5,9},{9,13},{13,1},{2,6},{6,10},{... | collective-permute-start | bytes 381896 | tf_op jit(solution)/shard_map/ppermute | solution.py:42
  143.5 41.0 %copy-start.9 = (bf16[2,24,663]{2,1,0:T(8,128)(2,1)S(1)}, bf16[2,24,663]{2,1,0:T(8,128)(2,1)}, u32[]{:S(2)}) copy-start(bf16[2,24,663]{2,1,0:T(8,128)(2,1)} %copy-done.8) | copy-start | bytes 190948
  143.5 5.3 %collective-permute-start.22 = (bf16[24,768]{1,0:T(8,128)(2,1)S(1)}, bf16[24,768]{1,0:T(8,128)(2,1)S(1)}, u32[]{:S(2)}, u32[]{:S(2)}) collective-permute-start(bf16[24,768]{1,0:T(8,128)(2,1)S(1)} %dynamic-slice_bitcast_fusion.17), channel_id=1, source_target_pairs={{0,16},{16,0},{1,17},{17,1},{2,18},{18,2},{3,19},{19,3},{4,20},{20... | collective-permute-start | bytes 110600 | tf_op jit(solution)/shard_map/ppermute | solution.py:42
  147.8 4.9 %collective-permute-start.14 = (bf16[12,2652]{1,0:T(8,128)(2,1)S(1)}, bf16[12,2652]{1,0:T(8,128)(2,1)S(1)}, u32[]{:S(2)}, u32[]{:S(2)}) collective-permute-start(bf16[12,2652]{1,0:T(8,128)(2,1)S(1)} %dynamic-slice_bitcast_fusion.9), channel_id=1, source_target_pairs={{0,16},{16,0},{1,17},{17,1},{2,18},{18,2},{3,19},{19,3},{4,20},{20... | collective-permute-start | bytes 190952 | tf_op jit(solution)/shard_map/ppermute | solution.py:42

commit v2 on v1

v2 whole, which is shorter than its diff:
```python
import functools

import jax
import jax.numpy as jnp
from jax import lax
from jax.experimental import pallas as pl
from jax.experimental.pallas import tpu as pltpu
from jax.sharding import Mesh
from jax.sharding import PartitionSpec as P

BLOCK = 128
PARAMS = 8469504
DP = ("dp_0", "dp_1", "dp_2", "dp_3")
MP_DP = ("mp", "dp_0", "dp_1", "dp_2", "dp_3")
ALL = DP + ("mp",)
Y, ZH, X, CORE = DP
LANES = 128
FETCHED, SECOND = 343, 320
PIECES = ((0, 48), (48, 192), (192, 343))
VMEM = pl.BlockSpec(memory_space=pltpu.VMEM)
SMEM = pl.BlockSpec(memory_space=pltpu.SMEM)
KERNEL = pltpu.CompilerParams(vmem_limit_bytes=56 << 20)


def swap(shard, axis):
    return lax.ppermute(shard, axis, [(0, 1), (1, 0)])


def across_hi(shard):
    return lax.ppermute(shard, (ZH, "mp"), [(0, 3), (3, 0), (1, 2), (2, 1)])


def pick(blocks, index, dim):
    return lax.dynamic_index_in_dim(blocks, index, dim, keepdims=False)


def wide(shard):
    return shard.astype(jnp.float32)


def narrow(shard):
    return shard.astype(jnp.bfloat16)


def sum_over_ring(blocks, axis, dim):
    size = lax.axis_size(axis)
    me = lax.axis_index(axis)
    total = wide(pick(blocks, me, dim))
    for step in (2, 1, 3) if size == 4 else (1,):
        part = pick(blocks, lax.rem(me + step, size), dim)
        total += wide(lax.ppermute(part, axis, [(i, (i + step) % size) for i in range(size)]))
    return total


def silu_slope(pre_act):
    sigmoid_of = jax.nn.sigmoid(pre_act)
    return sigmoid_of * (1.0 + pre_act * (1.0 - sigmoid_of))


def dot(left, right):
    return jnp.dot(left, right, preferred_element_type=jnp.float32)


def contract(left, right, left_dim, right_dim):
    return lax.dot_general(
        left,
        right,
        (((left_dim,), (right_dim,)), ((), ())),
        preferred_element_type=jnp.float32,
    )


def middle_kernel(
    core_ref,
    partial_ref,
    arrived_ref,
    live_ref,
    target_own_ref,
    target_mine_ref,
    target_theirs_ref,
    w_own_ref,
    w_middle_ref,
    first_slope_ref,
    belief_ref,
    *refs,
):
    count = len(PIECES)
    mine_refs, theirs_refs = refs[:count], refs[count : 2 * count]
    act_ref, slope_own_ref, slope_middle_ref, slope_first_ref, sent_ref = refs[2 * count :]
    live = live_ref[...]
    pre_middle = partial_ref[...] + wide(arrived_ref[...])
    sigmoid_of = 1.0 / (1.0 + jnp.exp(-pre_middle))
    act = narrow(pre_middle * sigmoid_of)
    act_ref[...] = act
    act_slope = sigmoid_of * (1.0 + pre_middle * (1.0 - sigmoid_of))

    def slope_of(weights, target):
        mismatch = contract(weights, act, 1, 1) - wide(target)
        return jnp.clip(mismatch, -1.0, 1.0) * live

    slope_own = narrow(slope_of(w_own_ref[...], target_own_ref[...]))
    slope_own_ref[...] = slope_own
    back = contract(slope_own, w_own_ref[...], 0, 0)
    for side, (w_refs, target_ref) in enumerate(
        ((mine_refs, target_mine_ref), (theirs_refs, target_theirs_ref))
    ):
        repeated = jnp.where(core_ref[0] == side, 0, 2 * FETCHED - SECOND - FETCHED)
        for (start, stop), w_ref in zip(PIECES, w_refs):
            slope = slope_of(w_ref[...], target_ref[start:stop, :])
            column = start + lax.broadcasted_iota(jnp.int32, slope.shape, 0)
            slope = narrow(jnp.where(column >= repeated, slope, 0.0))
            back += contract(slope, w_ref[...], 0, 0)
    slope_middle = narrow(back * act_slope)
    slope_middle_ref[...] = slope_middle
    slope_first = narrow(contract(w_middle_ref[...], slope_middle, 1, 1) * first_slope_ref[...])
    slope_first_ref[...] = slope_first
    half = slope_first.shape[0] // 2
    sent_ref[...] = narrow(contract(slope_first[:half], belief_ref[...], 1, 1)).reshape(sent_ref.shape)


def later_kernel(act_middle_ref, slope_own_ref, slope_middle_ref, act_first_ref, last_ref, middle_ref):
    middle_ref[...] = narrow(contract(slope_middle_ref[...], act_first_ref[...], 0, 0))
    last_ref[...] = narrow(contract(act_middle_ref[...].T, slope_own_ref[...], 1, 1))


def first_kernel(slope_first_ref, belief_ref, arrived_ref, out_ref):
    half = slope_first_ref.shape[0] // 2
    own = contract(slope_first_ref[half:, :], belief_ref[...], 1, 1).reshape(out_ref.shape)
    out_ref[...] = narrow(own + wide(arrived_ref[...]))


def call(body, outs, count, scalars=0, name=None):
    return pl.pallas_call(
        body,
        out_shape=[jax.ShapeDtypeStruct(*out) for out in outs],
        in_specs=[SMEM] * scalars + [VMEM] * (count - scalars),
        out_specs=[VMEM] * len(outs),
        compiler_params=KERNEL,
        name=name,
    )


def per_device(belief, target_value, counts, w_first, w_middle, w_last):
    total_rows = belief.shape[0]
    width = w_last.shape[1]
    units = w_first.shape[1]
    hidden = w_middle.shape[1]
    core = lax.axis_index(CORE)
    mp = lax.axis_index("mp")
    bf16, f32 = jnp.bfloat16, jnp.float32

    w_last_t = w_last.T
    fetched = [
        lax.dynamic_slice_in_dim(w_last_t, core * SECOND + start, stop - start, 0)
        for start, stop in PIECES
    ]
    mine = [swap(fetched[0], "mp"), across_hi(fetched[1]), across_hi(fetched[2])]
    theirs = [swap(piece, CORE) for piece in mine]

    pre_first = dot(belief, w_first)
    act_first = narrow(jax.nn.silu(pre_first))
    partial_middle = dot(act_first, w_middle)
    arrived = swap(narrow(partial_middle), "mp")

    live_rows = (counts[:, None] > jnp.arange(BLOCK, dtype=jnp.int32)[None, :]).reshape(1, total_rows)
    live = live_rows.astype(f32)
    target_t = target_value.T
    target_own = lax.dynamic_slice_in_dim(target_t, mp * width, width, 0)
    target_mine = lax.dynamic_slice_in_dim(target_t, (1 - mp) * width + core * SECOND, FETCHED, 0)
    target_theirs = lax.dynamic_slice_in_dim(
        target_t, (1 - mp) * width + (1 - core) * SECOND, FETCHED, 0
    )
    block = units // 64

    def by_owner(rows):
        rows = rows.reshape(4, 2, 4, 2, block, -1).transpose(3, 0, 2, 1, 4, 5)
        rows = jnp.where(core == 0, rows[::-1], rows)
        return rows.reshape(units, -1)

    w_middle_sorted = by_owner(w_middle)
    first_slope = by_owner(silu_slope(pre_first).T)
    belief_t = belief.T

    operands = (
        core.reshape(1),
        partial_middle,
        arrived,
        live,
        target_own,
        target_mine,
        target_theirs,
        w_last_t,
        w_middle_sorted,
        first_slope,
        belief_t,
        *mine,
        *theirs,
    )
    act_middle, slope_own, slope_middle, slope_first, sent = call(
        middle_kernel,
        [
            ((total_rows, hidden), bf16),
            ((width, total_rows), bf16),
            ((total_rows, hidden), bf16),
            ((units, total_rows), bf16),
            ((4, units // 8, belief.shape[1]), bf16),
        ],
        len(operands),
        1,
        "middle",
    )(*operands)
    sent = swap(sent, CORE)
    raw_last, raw_middle = call(
        later_kernel, [((hidden, width), bf16), ((hidden, units), bf16)], 4, 0, "later"
    )(act_middle, slope_own, slope_middle, act_first)
    (half_first,) = call(first_kernel, [(sent.shape, bf16)], 3, 0, "first")(
        slope_first, belief_t, sent
    )

    def half_sum(blocks):
        arrived = swap(pick(blocks, 1 - core, 1), CORE)
        return narrow(wide(pick(blocks, core, 1)) + wide(arrived))

    half_last = half_sum(raw_last.reshape(32, 2, 24, width))
    half_middle = half_sum(raw_middle.reshape(32, 2, 24, units))

    def shard_of(blocks, names, order):
        names = list(names)
        for axis in order:
            dim = names.index(axis)
            names.pop(dim)
            blocks = sum_over_ring(narrow(blocks), axis, dim)
        return blocks

    shard_last = shard_of(half_last.reshape(4, 2, 4, 24, -1), (Y, ZH, X), (X, Y, ZH))
    shard_middle = shard_of(half_middle.reshape(4, 2, 4, 24, -1), (Y, ZH, X), (X, Y, ZH))
    shard_first = sum_over_ring(half_first, Y, 0).reshape(4, 24, -1)
    shard_first = sum_over_ring(narrow(shard_first), X, 0).reshape(2, 12, -1)
    shard_first = sum_over_ring(narrow(shard_first), ZH, 0)

    local_squares = (
        jnp.sum(shard_first * shard_first)
        + jnp.sum(shard_middle * shard_middle)
        + jnp.sum(shard_last * shard_last)
    )
    gathered = lax.all_to_all(
        jnp.broadcast_to(local_squares, (128, 1, LANES)), ALL, 0, 0, tiled=True
    )
    square_sum = jnp.sum(gathered[:, 0, 0])
    norm_scale = lax.rsqrt(square_sum / PARAMS + 1e-06)
    return ((shard_first * norm_scale).T, (shard_middle * norm_scale).T, shard_last * norm_scale)


def solution(mesh):
    finer = Mesh(mesh.devices.reshape(4, 2, 4, 2, mesh.shape["mp"]), ALL)
    return jax.shard_map(
        per_device,
        mesh=finer,
        in_specs=(P(DP, None), P(DP, None), P(DP), P(None, "mp"), P("mp", None), P(None, "mp")),
        out_specs=(P(None, MP_DP), P("mp", DP), P(DP, "mp")),
        check_vma=False,
    )
```

time: 187 us -> 177 us (0.947)
  matrix products: 31.3 us -> 7.14 us
  Pallas kernels: 0 us -> 21 us
  blocking collectives: 27.1 us -> 15.4 us
  local copies, waits for them, and re-layouts: 23.9 us -> 31.9 us
  other arithmetic: 15.2 us -> 20 us
  starting transfers between devices: 41.1 us -> 36.4 us
  waiting for transfers between devices: 44.5 us -> 40.8 us
    dot_general x10 -> x2, matrix products: 31.3 us -> 7.14 us  [dot(): return jnp.dot(left, right, preferred_element_type=jnp.float32)]
    pallas_call x0 -> x3, Pallas kernels: none -> 21 us  [the longest x1 12 us: per_device(): call(middle_kernel, [((total_rows, hidden), bf16), ((width, total_rows),...]
    reshape x0 -> x4, local copies, waits for them, and re-layouts: none -> 11.7 us  [the longest x2 7.12 us: by_owner(): return rows.reshape(units, -1)]
    all_to_all x1, blocking collectives: 27.1 us -> 15.4 us  [per_device(): lax.all_to_all(jnp.broadcast_to(local_squares, (128, 1, LANES)), ALL, 0,...]
    ppermute x8, starting transfers between devices: 10.9 us -> 4.04 us  [swap(): return lax.ppermute(shard, axis, [(0, 1), (1, 0)])]
    ppermute x21, waiting for transfers between devices: 32.2 us -> 38.3 us  [sum_over_ring(): lax.ppermute(part, axis, [(i, (i + step) % size) for i in range(size)])]
    ppermute x2, waiting for transfers between devices: 5.89 us -> 0.01 us  [across_hi(): return lax.ppermute(shard, (ZH, 'mp'), [(0, 3), (3, 0), (1, 2), (2, 1)])]
    convert_element_type x3 -> x1, local copies, waits for them, and re-layouts: 5.46 us -> 0.03 us  [narrow(): return shard.astype(jnp.bfloat16)]
  transfers between devices with their start and end apart: 31 -> 31, of which waited for: 12 -> 10; matrix products, arithmetic and copies ran while one was open for 33% -> 28% of each run, Pallas kernels for 0% -> 2%
where the time goes in v2:
time: 177 us; the launch traced here: 176 us
  waiting for transfers between devices  40.8 us (23%)
  starting transfers between devices  36.4 us (21%)
  local copies, waits for them, and re-layouts  31.9 us (18%)
  Pallas kernels  21 us (12%)
  other arithmetic  20 us (11%)
  blocking collectives  15.4 us (9%)
  matrix products  7.14 us (4%)
  between operations  3.47 us (2%)
    ppermute x21, waiting for transfers between devices, sum_over_ring(): lax.ppermute(part, axis, [(i, (i + step) % size) for i in range(size)])  38.3 us
    ppermute x21, starting transfers between devices, sum_over_ring(): lax.ppermute(part, axis, [(i, (i + step) % size) for i in range(size)])  27.8 us
    all_to_all x1, blocking collectives, per_device(): lax.all_to_all(jnp.broadcast_to(local_squares, (128, 1, LANES)), ALL, 0,...  15.4 us
    pallas_call x1, Pallas kernels, per_device(): call(middle_kernel, [((total_rows, hidden), bf16), ((width, total_rows),...  12 us
    dot_general x2, matrix products, dot(): return jnp.dot(left, right, preferred_element_type=jnp.float32)  7.14 us
    reshape x2, local copies, waits for them, and re-layouts, by_owner(): return rows.reshape(units, -1)  7.12 us
    select_n x2, other arithmetic, by_owner(): rows = jnp.where(core == 0, rows[::-1], rows)  6.85 us
    convert_element_type x8, other arithmetic, narrow(): return shard.astype(jnp.bfloat16)  6.73 us
  transfers between devices with their start and end apart: 31, of which 10 were waited for; matrix products, arithmetic and copies ran while one was open for 28% of the time, Pallas kernels for 2%

profile of v2, /device:TPU:1, one launch (start us, length us, event | category | flops | bytes accessed | tf_op | source)
XLA Modules:
  0.0 176.0 jit_solution(10255414710232932042)
XLA Ops:
  0.6 1.9 %dynamic-slice_bitcast_fusion.5 = bf16[151,1536]{1,0:T(8,128)(2,1)} fusion(bf16[1536,663]{0,1:T(8,128)(2,1)} %param.11, s32[]{:T(128)S(6)} %select_n.112), kind=kLoop, calls=%fused_computation.31 | loop fusion | bytes 927748 | tf_op jit(solution)/shard_map/dynamic_slice | solution.py:154
  2.5 4.6 %collective-permute-start.3 = (bf16[151,1536]{1,0:T(8,128)(2,1)}, bf16[151,1536]{1,0:T(8,128)(2,1)}, u32[]{:S(2)}, u32[]{:S(2)}) collective-permute-start(bf16[151,1536]{1,0:T(8,128)(2,1)} %dynamic-slice_bitcast_fusion.5), channel_id=1, source_target_pairs={{0,17},{17,0},{1,16},{16,1},{2,19},{19,2},{3,18},{18,3},{4,21},{21... | collective-permute-start | bytes 1391624 | tf_op jit(solution)/shard_map/ppermute | solution.py:30
  7.1 1.9 %dynamic-slice_bitcast_fusion.6 = bf16[144,1536]{1,0:T(8,128)(2,1)} fusion(bf16[1536,663]{0,1:T(8,128)(2,1)} %param.11, s32[]{:T(128)S(6)} %select_n.111), kind=kLoop, calls=%fused_computation.32 | loop fusion | bytes 884740 | tf_op jit(solution)/shard_map/dynamic_slice | solution.py:154
  9.1 1.6 dynamic-slice_bitcast_fusion.16
  10.7 4.9 %multiply_convert_fusion = (bf16[256,768]{1,0:T(8,128)(2,1)S(1)}, f32[256,768]{1,0:T(8,128)}) fusion(bf16[256,2652]{0,1:T(8,128)(2,1)} %param.6, bf16[2652,768]{1,0:T(8,128)(2,1)} %param.9), kind=kOutput, calls=%fused_computation.19 | convolution fusion | flops 1043791872 | bytes 6610944 | tf_op jit(solution)/shard_map/dot_general | solution.py:61
  15.6 2.2 %fusion.26 = (bf16[256,1536]{1,0:T(8,128)(2,1)}, f32[256,1536]{1,0:T(8,128)}) fusion(bf16[256,768]{1,0:T(8,128)(2,1)S(1)} %get-tuple-element.37.act_first_ref, bf16[768,1536]{1,0:T(8,128)(2,1)S(1)} %copy-done), kind=kOutput, calls=%fused_computation.78 | convolution fusion | flops 604372992 | bytes 5111808 | tf_op jit(solution)/shard_map/dot_general | solution.py:61
  17.8 1.3 collective-permute-start
  19.1 2.3 %reshape.89 = bf16[4,2,4,2,12,1536]{5,4,3,2,1,0:T(8,128)(2,1)} reshape(bf16[768,1536]{1,0:T(8,128)(2,1)S(1)} %copy-done) | data formatting | bytes 4718592 | tf_op jit(solution)/shard_map/reshape | solution.py:176
  21.5 4.1 %reverse_select_fusion = bf16[2,4,4,2,12,1536]{5,4,0,2,3,1:T(8,128)(2,1)S(1)} fusion(bf16[2,4,4,2,12,1536]{5,4,0,2,3,1:T(8,128)(2,1)} %bitcast.132, pred[]{:T(512)S(6)} %eq.4), kind=kLoop, calls=%fused_computation | loop fusion | flops 1179648 | bytes 4718593 | tf_op jit(solution)/shard_map/jit(_where)/select_n | solution.py:177
  25.6 1.1 fusion.9
  26.7 2.3 %copy.22 = f32[768,256]{1,0:T(8,128)} copy(f32[768,256]{0,1:T(8,128)} %fusion.9) | data formatting | bytes 1572864 | tf_op jit(solution)/shard_map/mul | solution.py:57
  29.0 2.2 %reshape.91 = f32[4,2,4,2,12,256]{5,4,3,2,1,0:T(8,128)} reshape(f32[768,256]{1,0:T(8,128)} %copy.22) | data formatting | bytes 1572864 | tf_op jit(solution)/shard_map/reshape | solution.py:176
  31.2 2.8 %reverse_select_fusion.1 = f32[2,4,4,2,12,256]{5,4,0,2,3,1:T(8,128)} fusion(f32[2,4,4,2,12,256]{5,4,0,2,3,1:T(8,128)} %bitcast.140, pred[]{:T(512)S(6)} %eq.4), kind=kLoop, calls=%fused_computation.5 | loop fusion | flops 196608 | bytes 1572865 | tf_op jit(solution)/shard_map/jit(_where)/select_n | solution.py:177
  34.0 1.5 collective-permute-start.5
  35.6 0.6 compare_convert_fusion
  36.7 0.8 dynamic-slice_bitcast_fusion.7.target_own_ref
  37.5 2.3 %copy.23 = f32[2,4,4,2,12,256]{5,4,3,2,1,0:T(8,128)} copy(f32[2,4,4,2,12,256]{5,4,0,2,3,1:T(8,128)} %reverse_select_fusion.1) | data formatting | bytes 1572864 | tf_op jit(solution)/shard_map/jit(_where)/select_n | solution.py:177
  39.8 2.2 %reshape.92.first_slope_ref = f32[768,256]{1,0:T(8,128)} reshape(f32[2,4,4,2,12,256]{5,4,3,2,1,0:T(8,128)} %copy.23) | data formatting | bytes 1572864 | tf_op jit(solution)/shard_map/reshape | solution.py:178
  42.0 1.9 %copy.21 = bf16[2,4,4,2,12,1536]{5,4,3,2,1,0:T(8,128)(2,1)} copy(bf16[2,4,4,2,12,1536]{5,4,0,2,3,1:T(8,128)(2,1)S(1)} %reverse_select_fusion) | data formatting | bytes 4718592 | tf_op jit(solution)/shard_map/jit(_where)/select_n | solution.py:177
  43.9 4.9 %reshape.90.w_middle_ref = bf16[768,1536]{1,0:T(8,128)(2,1)} reshape(bf16[2,4,4,2,12,1536]{5,4,3,2,1,0:T(8,128)(2,1)} %copy.21) | data formatting | bytes 4718592 | tf_op jit(solution)/shard_map/reshape | solution.py:178
  48.8 0.8 dynamic-slice_bitcast_fusion.14
  49.7 0.6 copy-done.7
  50.3 12.0 %middle.1 = (bf16[256,1536]{1,0:T(8,128)(2,1)}, bf16[663,256]{1,0:T(8,128)(2,1)}, bf16[256,1536]{1,0:T(8,128)(2,1)}, bf16[768,256]{1,0:T(8,128)(2,1)}, bf16[4,96,2652]{2,1,0:T(8,128)(2,1)}) custom-call(s32[1]{0:T(128)} %bitcast.core_ref, f32[256,1536]{1,0:T(8,128)} %get-tuple-element.40.partial_ref, bf16[256,1536]{1,0:T(8,128)(2,1)} %collective-permute-done.arrived_ref, ...), custom_call_target="tpu_custom_call" | custom-call | tf_op jit(solution)/shard_map/middle/pallas_call | solution.py:199
  62.3 4.8 %later.1 = (bf16[1536,663]{1,0:T(8,128)(2,1)}, bf16[1536,768]{1,0:T(8,128)(2,1)}) custom-call(bf16[256,1536]{1,0:T(8,128)(2,1)} %get-tuple-element.12.act_middle_ref, bf16[663,256]{1,0:T(8,128)(2,1)} %get-tuple-element.13.slope_own_ref, bf16[256,1536]{1,0:T(8,128)(2,1)} %get-tuple-element.14.slope_middle_ref, bf16[256,768]{1,0:T(8,128)(2,1)} %copy-done.2), custom_call_target="tpu_custom_call" | custom-call | tf_op jit(solution)/shard_map/later/pallas_call | solution.py:213
  67.0 2.5 %dynamic-slice_bitcast_fusion = bf16[32,24,663]{2,1,0:T(8,128)(2,1)} fusion(bf16[32,2,24,663]{3,2,1,0:T(8,128)(2,1)} %bitcast.143, s32[]{:T(128)S(6)} %select_n.124), kind=kLoop, calls=%fused_computation.6 | loop fusion | bytes 2036740 | tf_op jit(solution)/shard_map/jit(dynamic_index_in_dim)/squeeze | solution.py:34
  70.3 2.4 %collective-permute-done.23 = bf16[32,24,663]{2,1,0:T(8,128)(2,1)} collective-permute-done((bf16[32,24,663]{2,1,0:T(8,128)(2,1)}, bf16[32,24,663]{2,1,0:T(8,128)(2,1)}, u32[]{:S(2)}, u32[]{:S(2)}) %collective-permute-start.23) | collective-permute-done | bytes 1018400 | tf_op jit(solution)/shard_map/ppermute | solution.py:26
  72.8 1.9 %fusion = bf16[32,24,663]{2,1,0:T(8,128)(2,1)S(1)} fusion(bf16[32,24,663]{2,1,0:T(8,128)(2,1)} %collective-permute-done.23, bf16[32,2,24,663]{3,2,1,0:T(8,128)(2,1)} %bitcast.144, s32[]{:T(128)S(6)} %select_n.123), kind=kLoop, calls=%fused_computation.2 | loop fusion | flops 2036736 | bytes 3055108 | tf_op jit(solution)/shard_map/convert_element_type | solution.py:42
  74.8 2.8 %collective-permute-start.24 = (bf16[4,2,24,663]{3,2,1,0:T(8,128)(2,1)S(1)}, bf16[4,2,24,663]{3,2,1,0:T(8,128)(2,1)S(1)}, u32[]{:S(2)}, u32[]{:S(2)}) collective-permute-start(bf16[4,2,24,663]{3,2,1,0:T(8,128)(2,1)S(1)} %get-tuple-element.20), channel_id=1, source_target_pairs={{0,8},{4,12},{8,0},{12,4},{1,9},{5,13},{9,1},{13,5},{2,10},{6,14},... | collective-permute-start | bytes 763784 | tf_op jit(solution)/shard_map/ppermute | solution.py:51
  77.9 2.4 %collective-permute-start.26 = (bf16[4,2,24,663]{3,2,1,0:T(8,128)(2,1)S(1)}, bf16[4,2,24,663]{3,2,1,0:T(8,128)(2,1)S(1)}, u32[]{:S(2)}, u32[]{:S(2)}) collective-permute-start(bf16[4,2,24,663]{3,2,1,0:T(8,128)(2,1)S(1)} %get-tuple-element.21), channel_id=1, source_target_pairs={{0,12},{4,0},{8,4},{12,8},{1,13},{5,1},{9,5},{13,9},{2,14},{6,2},{... | collective-permute-start | bytes 763784 | tf_op jit(solution)/shard_map/ppermute | solution.py:51
  80.3 1.6 fusion.1
  81.8 3.0 %collective-permute-done.24 = bf16[4,2,24,663]{3,2,1,0:T(8,128)(2,1)S(1)} collective-permute-done((bf16[4,2,24,663]{3,2,1,0:T(8,128)(2,1)S(1)}, bf16[4,2,24,663]{3,2,1,0:T(8,128)(2,1)S(1)}, u32[]{:S(2)}, u32[]{:S(2)}) %collective-permute-start.24) | collective-permute-done | bytes 254624 | tf_op jit(solution)/shard_map/ppermute | solution.py:51
  84.9 6.7 %collective-permute-done.25 = bf16[4,2,24,663]{3,2,1,0:T(8,128)(2,1)S(1)} collective-permute-done((bf16[4,2,24,663]{3,2,1,0:T(8,128)(2,1)S(1)}, bf16[4,2,24,663]{3,2,1,0:T(8,128)(2,1)S(1)}, u32[]{:S(2)}, u32[]{:S(2)}) %collective-permute-start.25) | collective-permute-done | bytes 254624 | tf_op jit(solution)/shard_map/ppermute | solution.py:51
  91.8 3.0 %collective-permute-start.27 = (bf16[2,24,663]{2,1,0:T(8,128)(2,1)S(1)}, bf16[2,24,663]{2,1,0:T(8,128)(2,1)S(1)}, u32[]{:S(2)}, u32[]{:S(2)}) collective-permute-start(bf16[2,24,663]{2,1,0:T(8,128)(2,1)S(1)} %get-tuple-element.31), channel_id=1, source_target_pairs={{0,64},{32,96},{64,0},{96,32},{1,65},{33,97},{65,1},{97,33},{2,66}... | collective-permute-start | bytes 190952 | tf_op jit(solution)/shard_map/ppermute | solution.py:51
  95.2 2.3 %collective-permute-start.29 = (bf16[2,24,663]{2,1,0:T(8,128)(2,1)S(1)}, bf16[2,24,663]{2,1,0:T(8,128)(2,1)S(1)}, u32[]{:S(2)}, u32[]{:S(2)}) collective-permute-start(bf16[2,24,663]{2,1,0:T(8,128)(2,1)S(1)} %get-tuple-element.32), channel_id=1, source_target_pairs={{0,96},{32,0},{64,32},{96,64},{1,97},{33,1},{65,33},{97,65},{2,98}... | collective-permute-start | bytes 190952 | tf_op jit(solution)/shard_map/ppermute | solution.py:51
  97.5 0.9 dynamic-slice_bitcast_fusion.13
  98.4 1.4 collective-permute-start.16
  99.8 1.6 collective-permute-start.17
  101.4 1.0 collective-permute-start.18
  102.5 2.6 %collective-permute-start.30 = (bf16[24,663]{1,0:T(8,128)(2,1)S(1)}, bf16[24,663]{1,0:T(8,128)(2,1)S(1)}, u32[]{:S(2)}, u32[]{:S(2)}) collective-permute-start(bf16[24,663]{1,0:T(8,128)(2,1)S(1)} %dynamic-slice_bitcast_fusion.27), channel_id=1, source_target_pairs={{0,16},{16,0},{1,17},{17,1},{2,18},{18,2},{3,19},{19,3},{4,20},{20... | collective-permute-start | bytes 95480 | tf_op jit(solution)/shard_map/ppermute | solution.py:51
  105.2 4.2 %first.1 = bf16[4,96,2652]{2,1,0:T(8,128)(2,1)} custom-call(bf16[768,256]{1,0:T(8,128)(2,1)} %get-tuple-element.10.slope_first_ref, bf16[2652,256]{1,0:T(8,128)(2,1)} %bitcast.134, bf16[4,96,2652]{2,1,0:T(8,128)(2,1)} %collective-permute-done.7.arrived_ref), custom_call_target="tpu_custom_call" | custom-call | tf_op jit(solution)/shard_map/first/pallas_call | solution.py:216
  109.4 1.5 dynamic-slice_bitcast_fusion.4
  110.9 1.5 collective-permute-start.8
  112.4 0.7 copy-done.6
  113.1 0.6 multiply_reduce_fusion.1
  113.8 1.5 collective-permute-done.17
  115.2 1.3 fusion.15
  116.6 2.1 %collective-permute-start.19 = (bf16[2,24,768]{2,1,0:T(8,128)(2,1)S(1)}, bf16[2,24,768]{2,1,0:T(8,128)(2,1)S(1)}, u32[]{:S(2)}, u32[]{:S(2)}) collective-permute-start(bf16[2,24,768]{2,1,0:T(8,128)(2,1)S(1)} %get-tuple-element.34), channel_id=1, source_target_pairs={{0,64},{32,96},{64,0},{96,32},{1,65},{33,97},{65,1},{97,33},{2,66}... | collective-permute-start | bytes 221192 | tf_op jit(solution)/shard_map/ppermute | solution.py:51
  118.7 2.6 %collective-permute-done.10 = bf16[96,2652]{1,0:T(8,128)(2,1)S(1)} collective-permute-done((bf16[96,2652]{1,0:T(8,128)(2,1)S(1)}, bf16[96,2652]{1,0:T(8,128)(2,1)S(1)}, u32[]{:S(2)}, u32[]{:S(2)}) %collective-permute-start.10) | collective-permute-done | bytes 509216 | tf_op jit(solution)/shard_map/ppermute | solution.py:51
  121.3 1.4 collective-permute-start.21
  123.0 15.1 %collective-permute-done.9 = bf16[96,2652]{1,0:T(8,128)(2,1)} collective-permute-done((bf16[96,2652]{1,0:T(8,128)(2,1)S(1)}, bf16[96,2652]{1,0:T(8,128)(2,1)}, u32[]{:S(2)}, u32[]{:S(2)}) %collective-permute-start.9) | collective-permute-done | bytes 509216 | tf_op jit(solution)/shard_map/ppermute | solution.py:51
  138.1 1.6 fusion.4
  139.8 1.1 collective-permute-start.11
  141.0 1.3 collective-permute-start.12
  142.3 1.3 collective-permute-start.13
  144.2 1.6 collective-permute-done.11
  145.8 3.6 %collective-permute-done.12 = bf16[24,2652]{1,0:T(8,128)(2,1)S(1)} collective-permute-done((bf16[24,2652]{1,0:T(8,128)(2,1)S(1)}, bf16[24,2652]{1,0:T(8,128)(2,1)S(1)}, u32[]{:S(2)}, u32[]{:S(2)}) %collective-permute-start.12) | collective-permute-done | bytes 127328 | tf_op jit(solution)/shard_map/ppermute | solution.py:51
  150.1 0.6 multiply_reduce_fusion.2
  150.7 3.8 %collective-permute-done.14 = bf16[12,2652]{1,0:T(8,128)(2,1)S(1)} collective-permute-done((bf16[12,2652]{1,0:T(8,128)(2,1)S(1)}, bf16[12,2652]{1,0:T(8,128)(2,1)S(1)}, u32[]{:S(2)}, u32[]{:S(2)}) %collective-permute-start.14) | collective-permute-done | bytes 63680 | tf_op jit(solution)/shard_map/ppermute | solution.py:51
  154.5 0.7 multiply_reduce_fusion
  157.2 15.4 %all_to_all.5 = f32[128,1,128]{2,1,0:T(1,128)S(1)} all-to-all(f32[128,1,128]{2,1,0:T(1,128)S(1)} %broadcast_in_dim.2), channel_id=1, replica_groups=mesh['dp_0'=4,'dp_1'=2,'dp_2'=4,'dp_3'=2,'mp'=2] {'dp_0','dp_1','dp_2','..., dimensions={0} | all-to-all | bytes 131072 | tf_op jit(solution)/shard_map/all_to_all | solution.py:246
  172.6 0.7 slice_reduce_fusion
  174.0 0.7 fusion.25
  174.7 0.6 multiply_bitcast_fusion.1
  175.3 0.7 multiply_bitcast_fusion
  (66 shorter events, 4.0 us)
Async XLA Ops:
  2.5 33.0 %collective-permute-start.3 = (bf16[151,1536]{1,0:T(8,128)(2,1)}, bf16[151,1536]{1,0:T(8,128)(2,1)}, u32[]{:S(2)}, u32[]{:S(2)}) collective-permute-start(bf16[151,1536]{1,0:T(8,128)(2,1)} %dynamic-slice_bitcast_fusion.5), channel_id=1, source_target_pairs={{0,17},{17,0},{1,16},{16,1},{2,19},{19,2},{3,18},{18,3},{4,21},{21... | collective-permute-start | bytes 1391624 | tf_op jit(solution)/shard_map/ppermute | solution.py:30
  9.0 24.9 %collective-permute-start.2 = (bf16[144,1536]{1,0:T(8,128)(2,1)}, bf16[144,1536]{1,0:T(8,128)(2,1)}, u32[]{:S(2)}, u32[]{:S(2)}) collective-permute-start(bf16[144,1536]{1,0:T(8,128)(2,1)} %dynamic-slice_bitcast_fusion.6), channel_id=1, source_target_pairs={{0,17},{17,0},{1,16},{16,1},{2,19},{19,2},{3,18},{18,3},{4,21},{21... | collective-permute-start | bytes 1327112 | tf_op jit(solution)/shard_map/ppermute | solution.py:30
  10.7 4.9 %copy-start = (bf16[768,1536]{1,0:T(8,128)(2,1)S(1)}, bf16[768,1536]{1,0:T(8,128)(2,1)}, u32[]{:S(2)}) copy-start(bf16[768,1536]{1,0:T(8,128)(2,1)} %param.10) | copy-start | bytes 7077892
  10.7 25.6 %collective-permute-start.1 = (bf16[48,1536]{1,0:T(8,128)(2,1)}, bf16[48,1536]{1,0:T(8,128)(2,1)}, u32[]{:S(2)}, u32[]{:S(2)}) collective-permute-start(bf16[48,1536]{1,0:T(8,128)(2,1)} %dynamic-slice_bitcast_fusion.16), channel_id=1, source_target_pairs={{0,1},{1,0},{2,3},{3,2},{4,5},{5,4},{6,7},{7,6},{8,9},{9,8},{10,11... | collective-permute-start | bytes 442376 | tf_op jit(solution)/shard_map/ppermute | solution.py:26
  15.6 2.2 %copy-start.2 = (bf16[256,768]{1,0:T(8,128)(2,1)}, bf16[256,768]{1,0:T(8,128)(2,1)S(1)}, u32[]{:S(2)}) copy-start(bf16[256,768]{1,0:T(8,128)(2,1)S(1)} %get-tuple-element.37.act_first_ref) | copy-start | bytes 1179652
  17.8 31.8 %collective-permute-start = (bf16[256,1536]{1,0:T(8,128)(2,1)}, bf16[256,1536]{1,0:T(8,128)(2,1)}, u32[]{:S(2)}, u32[]{:S(2)}) collective-permute-start(bf16[256,1536]{1,0:T(8,128)(2,1)} %get-tuple-element.39), channel_id=1, source_target_pairs={{0,1},{1,0},{2,3},{3,2},{4,5},{5,4},{6,7},{7,6},{8,9},{9,8},{10,11... | collective-permute-start | bytes 2359304 | tf_op jit(solution)/shard_map/ppermute | solution.py:26
  21.5 4.1 %copy-start.3 = (f32[256,768]{1,0:T(8,128)S(1)}, f32[256,768]{1,0:T(8,128)}, u32[]{:S(2)}) copy-start(f32[256,768]{1,0:T(8,128)} %get-tuple-element.38) | copy-start | bytes 2359300
  29.0 6.6 %copy-start.8 = (s32[2]{0:T(128)S(1)}, s32[2]{0:T(128)}, u32[]{:S(2)}) copy-start(s32[2]{0:T(128)} %param.8) | copy-start | bytes 28
  31.2 5.5 %copy-start.4 = (bf16[256,1326]{0,1:T(8,128)(2,1)S(1)}, bf16[256,1326]{0,1:T(8,128)(2,1)}, u32[]{:S(2)}) copy-start(bf16[256,1326]{0,1:T(8,128)(2,1)} %param.7) | copy-start | bytes 2036740
  34.0 15.7 %collective-permute-start.5 = (bf16[144,1536]{1,0:T(8,128)(2,1)}, bf16[144,1536]{1,0:T(8,128)(2,1)}, u32[]{:S(2)}, u32[]{:S(2)}) collective-permute-start(bf16[144,1536]{1,0:T(8,128)(2,1)} %collective-permute-done.2.refs_1_), channel_id=1, source_target_pairs={{0,2},{2,0},{1,3},{3,1},{4,6},{6,4},{5,7},{7,5},{8,10},{10,8},{9,1... | collective-permute-start | bytes 1327112 | tf_op jit(solution)/shard_map/ppermute | solution.py:26
  35.5 14.1 %collective-permute-start.6 = (bf16[151,1536]{1,0:T(8,128)(2,1)}, bf16[151,1536]{1,0:T(8,128)(2,1)}, u32[]{:S(2)}, u32[]{:S(2)}) collective-permute-start(bf16[151,1536]{1,0:T(8,128)(2,1)} %collective-permute-done.3.refs_2_), channel_id=1, source_target_pairs={{0,2},{2,0},{1,3},{3,1},{4,6},{6,4},{5,7},{7,5},{8,10},{10,8},{9,1... | collective-permute-start | bytes 1391624 | tf_op jit(solution)/shard_map/ppermute | solution.py:26
  36.2 13.4 %collective-permute-start.4 = (bf16[48,1536]{1,0:T(8,128)(2,1)}, bf16[48,1536]{1,0:T(8,128)(2,1)S(1)}, u32[]{:S(2)}, u32[]{:S(2)}) collective-permute-start(bf16[48,1536]{1,0:T(8,128)(2,1)} %collective-permute-done.1.refs_0_), channel_id=1, source_target_pairs={{0,2},{2,0},{1,3},{3,1},{4,6},{6,4},{5,7},{7,5},{8,10},{10,8},{9,1... | collective-permute-start | bytes 442376 | tf_op jit(solution)/shard_map/ppermute | solution.py:26
  43.9 4.9 %copy-start.5 = (bf16[256,1326]{0,1:T(8,128)(2,1)S(1)}, bf16[256,1326]{0,1:T(8,128)(2,1)}, u32[]{:S(2)}) copy-start(bf16[256,1326]{0,1:T(8,128)(2,1)} %param.7) | copy-start | bytes 2036740
  49.6 0.7 copy-start.7
  67.0 2.6 %copy-start.1 = (bf16[1536,768]{1,0:T(8,128)(2,1)S(1)}, bf16[1536,768]{1,0:T(8,128)(2,1)}, u32[]{:S(2)}) copy-start(bf16[1536,768]{1,0:T(8,128)(2,1)} %get-tuple-element.15) | copy-start | bytes 7077892
  69.6 3.2 %collective-permute-start.23 = (bf16[32,24,663]{2,1,0:T(8,128)(2,1)}, bf16[32,24,663]{2,1,0:T(8,128)(2,1)}, u32[]{:S(2)}, u32[]{:S(2)}) collective-permute-start(bf16[32,24,663]{2,1,0:T(8,128)(2,1)} %dynamic-slice_bitcast_fusion), channel_id=1, source_target_pairs={{0,2},{2,0},{1,3},{3,1},{4,6},{6,4},{5,7},{7,5},{8,10},{10,8},{9,1... | collective-permute-start | bytes 3055112 | tf_op jit(solution)/shard_map/ppermute | solution.py:26
  69.7 10.5 %collective-permute-start.15 = (bf16[32,24,768]{2,1,0:T(8,128)(2,1)S(1)}, bf16[32,24,768]{2,1,0:T(8,128)(2,1)}, u32[]{:S(2)}, u32[]{:S(2)}) collective-permute-start(bf16[32,24,768]{2,1,0:T(8,128)(2,1)S(1)} %dynamic-slice_bitcast_fusion.1), channel_id=1, source_target_pairs={{0,2},{2,0},{1,3},{3,1},{4,6},{6,4},{5,7},{7,5},{8,10},{10,8},{9,1... | collective-permute-start | bytes 3538952 | tf_op jit(solution)/shard_map/ppermute | solution.py:26
  70.2 34.9 %collective-permute-start.7 = (bf16[4,96,2652]{2,1,0:T(8,128)(2,1)}, bf16[4,96,2652]{2,1,0:T(8,128)(2,1)}, u32[]{:S(2)}, u32[]{:S(2)}) collective-permute-start(bf16[4,96,2652]{2,1,0:T(8,128)(2,1)} %get-tuple-element.11), channel_id=1, source_target_pairs={{0,2},{2,0},{1,3},{3,1},{4,6},{6,4},{5,7},{7,5},{8,10},{10,8},{9,1... | collective-permute-start | bytes 6110216 | tf_op jit(solution)/shard_map/ppermute | solution.py:26
  74.8 10.1 %collective-permute-start.24 = (bf16[4,2,24,663]{3,2,1,0:T(8,128)(2,1)S(1)}, bf16[4,2,24,663]{3,2,1,0:T(8,128)(2,1)S(1)}, u32[]{:S(2)}, u32[]{:S(2)}) collective-permute-start(bf16[4,2,24,663]{3,2,1,0:T(8,128)(2,1)S(1)} %get-tuple-element.20), channel_id=1, source_target_pairs={{0,8},{4,12},{8,0},{12,4},{1,9},{5,13},{9,1},{13,5},{2,10},{6,14},... | collective-permute-start | bytes 763784 | tf_op jit(solution)/shard_map/ppermute | solution.py:51
  77.6 14.0 %collective-permute-start.25 = (bf16[4,2,24,663]{3,2,1,0:T(8,128)(2,1)S(1)}, bf16[4,2,24,663]{3,2,1,0:T(8,128)(2,1)S(1)}, u32[]{:S(2)}, u32[]{:S(2)}) collective-permute-start(bf16[4,2,24,663]{3,2,1,0:T(8,128)(2,1)S(1)} %get-tuple-element.22), channel_id=1, source_target_pairs={{0,4},{4,8},{8,12},{12,0},{1,5},{5,9},{9,13},{13,1},{2,6},{6,10},{... | collective-permute-start | bytes 763784 | tf_op jit(solution)/shard_map/ppermute | solution.py:51
  77.9 13.7 %collective-permute-start.26 = (bf16[4,2,24,663]{3,2,1,0:T(8,128)(2,1)S(1)}, bf16[4,2,24,663]{3,2,1,0:T(8,128)(2,1)S(1)}, u32[]{:S(2)}, u32[]{:S(2)}) collective-permute-start(bf16[4,2,24,663]{3,2,1,0:T(8,128)(2,1)S(1)} %get-tuple-element.21), channel_id=1, source_target_pairs={{0,12},{4,0},{8,4},{12,8},{1,13},{5,1},{9,5},{13,9},{2,14},{6,2},{... | collective-permute-start | bytes 763784 | tf_op jit(solution)/shard_map/ppermute | solution.py:51
  91.8 8.0 %collective-permute-start.27 = (bf16[2,24,663]{2,1,0:T(8,128)(2,1)S(1)}, bf16[2,24,663]{2,1,0:T(8,128)(2,1)S(1)}, u32[]{:S(2)}, u32[]{:S(2)}) collective-permute-start(bf16[2,24,663]{2,1,0:T(8,128)(2,1)S(1)} %get-tuple-element.31), channel_id=1, source_target_pairs={{0,64},{32,96},{64,0},{96,32},{1,65},{33,97},{65,1},{97,33},{2,66}... | collective-permute-start | bytes 190952 | tf_op jit(solution)/shard_map/ppermute | solution.py:51
  94.8 6.6 %collective-permute-start.28 = (bf16[2,24,663]{2,1,0:T(8,128)(2,1)S(1)}, bf16[2,24,663]{2,1,0:T(8,128)(2,1)S(1)}, u32[]{:S(2)}, u32[]{:S(2)}) collective-permute-start(bf16[2,24,663]{2,1,0:T(8,128)(2,1)S(1)} %get-tuple-element.33), channel_id=1, source_target_pairs={{0,32},{32,64},{64,96},{96,0},{1,33},{33,65},{65,97},{97,1},{2,34}... | collective-permute-start | bytes 190952 | tf_op jit(solution)/shard_map/ppermute | solution.py:51
  95.2 7.3 %collective-permute-start.29 = (bf16[2,24,663]{2,1,0:T(8,128)(2,1)S(1)}, bf16[2,24,663]{2,1,0:T(8,128)(2,1)S(1)}, u32[]{:S(2)}, u32[]{:S(2)}) collective-permute-start(bf16[2,24,663]{2,1,0:T(8,128)(2,1)S(1)} %get-tuple-element.32), channel_id=1, source_target_pairs={{0,96},{32,0},{64,32},{96,64},{1,97},{33,1},{65,33},{97,65},{2,98}... | collective-permute-start | bytes 190952 | tf_op jit(solution)/shard_map/ppermute | solution.py:51
  98.4 14.1 %collective-permute-start.16 = (bf16[4,2,24,768]{3,2,1,0:T(8,128)(2,1)S(1)}, bf16[4,2,24,768]{3,2,1,0:T(8,128)(2,1)S(1)}, u32[]{:S(2)}, u32[]{:S(2)}) collective-permute-start(bf16[4,2,24,768]{3,2,1,0:T(8,128)(2,1)S(1)} %get-tuple-element.23), channel_id=1, source_target_pairs={{0,8},{4,12},{8,0},{12,4},{1,9},{5,13},{9,1},{13,5},{2,10},{6,14},... | collective-permute-start | bytes 884744 | tf_op jit(solution)/shard_map/ppermute | solution.py:51
  99.8 15.5 %collective-permute-start.17 = (bf16[4,2,24,768]{3,2,1,0:T(8,128)(2,1)}, bf16[4,2,24,768]{3,2,1,0:T(8,128)(2,1)}, u32[]{:S(2)}, u32[]{:S(2)}) collective-permute-start(bf16[4,2,24,768]{3,2,1,0:T(8,128)(2,1)} %get-tuple-element.25), channel_id=1, source_target_pairs={{0,4},{4,8},{8,12},{12,0},{1,5},{5,9},{9,13},{13,1},{2,6},{6,10},{... | collective-permute-start | bytes 884744 | tf_op jit(solution)/shard_map/ppermute | solution.py:51
  101.4 13.8 %collective-permute-start.18 = (bf16[4,2,24,768]{3,2,1,0:T(8,128)(2,1)}, bf16[4,2,24,768]{3,2,1,0:T(8,128)(2,1)}, u32[]{:S(2)}, u32[]{:S(2)}) collective-permute-start(bf16[4,2,24,768]{3,2,1,0:T(8,128)(2,1)} %get-tuple-element.24), channel_id=1, source_target_pairs={{0,12},{4,0},{8,4},{12,8},{1,13},{5,1},{9,5},{13,9},{2,14},{6,2},{... | collective-permute-start | bytes 884744 | tf_op jit(solution)/shard_map/ppermute | solution.py:51
  102.5 8.4 %collective-permute-start.30 = (bf16[24,663]{1,0:T(8,128)(2,1)S(1)}, bf16[24,663]{1,0:T(8,128)(2,1)S(1)}, u32[]{:S(2)}, u32[]{:S(2)}) collective-permute-start(bf16[24,663]{1,0:T(8,128)(2,1)S(1)} %dynamic-slice_bitcast_fusion.27), channel_id=1, source_target_pairs={{0,16},{16,0},{1,17},{17,1},{2,18},{18,2},{3,19},{19,3},{4,20},{20... | collective-permute-start | bytes 95480 | tf_op jit(solution)/shard_map/ppermute | solution.py:51
  110.8 10.5 %collective-permute-start.10 = (bf16[96,2652]{1,0:T(8,128)(2,1)S(1)}, bf16[96,2652]{1,0:T(8,128)(2,1)S(1)}, u32[]{:S(2)}, u32[]{:S(2)}) collective-permute-start(bf16[96,2652]{1,0:T(8,128)(2,1)S(1)} %get-tuple-element.18), channel_id=1, source_target_pairs={{0,96},{32,0},{64,32},{96,64},{1,97},{33,1},{65,33},{97,65},{2,98}... | collective-permute-start | bytes 1527560 | tf_op jit(solution)/shard_map/ppermute | solution.py:51
  110.9 12.1 %collective-permute-start.8 = (bf16[96,2652]{1,0:T(8,128)(2,1)S(1)}, bf16[96,2652]{1,0:T(8,128)(2,1)}, u32[]{:S(2)}, u32[]{:S(2)}) collective-permute-start(bf16[96,2652]{1,0:T(8,128)(2,1)S(1)} %get-tuple-element.17), channel_id=1, source_target_pairs={{0,64},{32,96},{64,0},{96,32},{1,65},{33,97},{65,1},{97,33},{2,66}... | collective-permute-start | bytes 1527560 | tf_op jit(solution)/shard_map/ppermute | solution.py:51
  112.4 0.7 copy-start.6
  113.1 25.0 %collective-permute-start.9 = (bf16[96,2652]{1,0:T(8,128)(2,1)S(1)}, bf16[96,2652]{1,0:T(8,128)(2,1)}, u32[]{:S(2)}, u32[]{:S(2)}) collective-permute-start(bf16[96,2652]{1,0:T(8,128)(2,1)S(1)} %get-tuple-element.19), channel_id=1, source_target_pairs={{0,32},{32,64},{64,96},{96,0},{1,33},{33,65},{65,97},{97,1},{2,34}... | collective-permute-start | bytes 1527560 | tf_op jit(solution)/shard_map/ppermute | solution.py:51
  116.6 25.7 %collective-permute-start.19 = (bf16[2,24,768]{2,1,0:T(8,128)(2,1)S(1)}, bf16[2,24,768]{2,1,0:T(8,128)(2,1)S(1)}, u32[]{:S(2)}, u32[]{:S(2)}) collective-permute-start(bf16[2,24,768]{2,1,0:T(8,128)(2,1)S(1)} %get-tuple-element.34), channel_id=1, source_target_pairs={{0,64},{32,96},{64,0},{96,32},{1,65},{33,97},{65,1},{97,33},{2,66}... | collective-permute-start | bytes 221192 | tf_op jit(solution)/shard_map/ppermute | solution.py:51
  118.7 24.9 %collective-permute-start.20 = (bf16[2,24,768]{2,1,0:T(8,128)(2,1)S(1)}, bf16[2,24,768]{2,1,0:T(8,128)(2,1)S(1)}, u32[]{:S(2)}, u32[]{:S(2)}) collective-permute-start(bf16[2,24,768]{2,1,0:T(8,128)(2,1)S(1)} %get-tuple-element.36), channel_id=1, source_target_pairs={{0,32},{32,64},{64,96},{96,0},{1,33},{33,65},{65,97},{97,1},{2,34}... | collective-permute-start | bytes 221192 | tf_op jit(solution)/shard_map/ppermute | solution.py:51
  121.3 22.3 %collective-permute-start.21 = (bf16[2,24,768]{2,1,0:T(8,128)(2,1)S(1)}, bf16[2,24,768]{2,1,0:T(8,128)(2,1)S(1)}, u32[]{:S(2)}, u32[]{:S(2)}) collective-permute-start(bf16[2,24,768]{2,1,0:T(8,128)(2,1)S(1)} %get-tuple-element.35), channel_id=1, source_target_pairs={{0,96},{32,0},{64,32},{96,64},{1,97},{33,1},{65,33},{97,65},{2,98}... | collective-permute-start | bytes 221192 | tf_op jit(solution)/shard_map/ppermute | solution.py:51
  139.8 6.0 %collective-permute-start.11 = (bf16[24,2652]{1,0:T(8,128)(2,1)S(1)}, bf16[24,2652]{1,0:T(8,128)(2,1)S(1)}, u32[]{:S(2)}, u32[]{:S(2)}) collective-permute-start(bf16[24,2652]{1,0:T(8,128)(2,1)S(1)} %get-tuple-element.28), channel_id=1, source_target_pairs={{0,8},{4,12},{8,0},{12,4},{1,9},{5,13},{9,1},{13,5},{2,10},{6,14},... | collective-permute-start | bytes 381896 | tf_op jit(solution)/shard_map/ppermute | solution.py:51
  141.0 8.5 %collective-permute-start.12 = (bf16[24,2652]{1,0:T(8,128)(2,1)S(1)}, bf16[24,2652]{1,0:T(8,128)(2,1)S(1)}, u32[]{:S(2)}, u32[]{:S(2)}) collective-permute-start(bf16[24,2652]{1,0:T(8,128)(2,1)S(1)} %get-tuple-element.30), channel_id=1, source_target_pairs={{0,4},{4,8},{8,12},{12,0},{1,5},{5,9},{9,13},{13,1},{2,6},{6,10},{... | collective-permute-start | bytes 381896 | tf_op jit(solution)/shard_map/ppermute | solution.py:51
  142.3 7.2 %collective-permute-start.13 = (bf16[24,2652]{1,0:T(8,128)(2,1)S(1)}, bf16[24,2652]{1,0:T(8,128)(2,1)S(1)}, u32[]{:S(2)}, u32[]{:S(2)}) collective-permute-start(bf16[24,2652]{1,0:T(8,128)(2,1)S(1)} %get-tuple-element.29), channel_id=1, source_target_pairs={{0,12},{4,0},{8,4},{12,8},{1,13},{5,1},{9,5},{13,9},{2,14},{6,2},{... | collective-permute-start | bytes 381896 | tf_op jit(solution)/shard_map/ppermute | solution.py:51
  143.7 6.4 %collective-permute-start.22 = (bf16[24,768]{1,0:T(8,128)(2,1)S(1)}, bf16[24,768]{1,0:T(8,128)(2,1)S(1)}, u32[]{:S(2)}, u32[]{:S(2)}) collective-permute-start(bf16[24,768]{1,0:T(8,128)(2,1)S(1)} %dynamic-slice_bitcast_fusion.28), channel_id=1, source_target_pairs={{0,16},{16,0},{1,17},{17,1},{2,18},{18,2},{3,19},{19,3},{4,20},{20... | collective-permute-start | bytes 110600 | tf_op jit(solution)/shard_map/ppermute | solution.py:51
  149.6 4.9 %collective-permute-start.14 = (bf16[12,2652]{1,0:T(8,128)(2,1)S(1)}, bf16[12,2652]{1,0:T(8,128)(2,1)S(1)}, u32[]{:S(2)}, u32[]{:S(2)}) collective-permute-start(bf16[12,2652]{1,0:T(8,128)(2,1)S(1)} %dynamic-slice_bitcast_fusion.20), channel_id=1, source_target_pairs={{0,16},{16,0},{1,17},{17,1},{2,18},{18,2},{3,19},{19,3},{4,20},{20... | collective-permute-start | bytes 190952 | tf_op jit(solution)/shard_map/ppermute | solution.py:51

commit v3 on v0

v3 whole, which is shorter than its diff:
```python
import jax
import jax.numpy as jnp
from jax import lax
from jax.experimental import pallas as pl
from jax.experimental.pallas import tpu as pltpu
from jax.sharding import Mesh
from jax.sharding import PartitionSpec as P

BLOCK = 128
PARAMS = 8469504
DP = ("dp_0", "dp_1", "dp_2", "dp_3")
MP_DP = ("mp", "dp_0", "dp_1", "dp_2", "dp_3")
ALL = DP + ("mp",)
Y, ZH, X, CORE = DP
LANES = 128
CUT = 480
ROWS, COLS = 24, 384
VMEM = pl.BlockSpec(memory_space=pltpu.VMEM)
SMEM = pl.BlockSpec(memory_space=pltpu.SMEM)
HBM = pl.BlockSpec(memory_space=pl.ANY)
BF16, F32 = jnp.bfloat16, jnp.float32


def wide(shard):
    return shard.astype(F32)


def narrow(shard):
    return shard.astype(BF16)


def swap(shard, axis):
    return lax.ppermute(shard, axis, [(0, 1), (1, 0)])


def rotate(shard, axis, step):
    return lax.ppermute(shard, axis, [(i, (i + step) % 4) for i in range(4)])


def silu_slope(pre_act):
    sigmoid_of = jax.nn.sigmoid(pre_act)
    return sigmoid_of * (1.0 + pre_act * (1.0 - sigmoid_of))


def dot(left, right):
    return jnp.dot(left, right, preferred_element_type=F32)


def contract(left, right, left_dim, right_dim):
    return lax.dot_general(
        left, right, (((left_dim,), (right_dim,)), ((), ())), preferred_element_type=F32
    )


def call(body, name, in_specs, outs, scratch=()):
    return pl.pallas_call(
        body,
        out_shape=[jax.ShapeDtypeStruct(*out) for out in outs],
        in_specs=in_specs,
        out_specs=[VMEM] * len(outs),
        scratch_shapes=list(scratch),
        compiler_params=pltpu.CompilerParams(vmem_limit_bytes=56 << 20),
        name=name,
    )


def by_unit(raw_ref, core, out_ref):
    for unit in range(16):
        for z_hi in range(2):
            first = 2 * ROWS * ((unit // 4 * 2 + z_hi) * 4 + unit % 4)
            rows = pl.ds(pl.multiple_of(first + ROWS * core, 8), ROWS)
            for half in range(2):
                out_ref[unit, 2 * z_hi + half] = narrow(
                    raw_ref[rows, half * COLS : (half + 1) * COLS]
                )


def last_kernel(
    place_ref, partial_ref, arrived_ref, live_ref, target_ref, w_ref,
    act_ref, act_slope_ref, slope_ref, sent_ref, own_ref, raw_ref, padded_ref,
):
    core = place_ref[0]
    width = slope_ref.shape[0]
    pre_middle = partial_ref[...] + wide(arrived_ref[...])
    sigmoid_of = 1.0 / (1.0 + jnp.exp(-pre_middle))
    act = narrow(pre_middle * sigmoid_of)
    act_ref[...] = act
    act_slope_ref[...] = sigmoid_of * (1.0 + pre_middle * (1.0 - sigmoid_of))
    mismatch = contract(w_ref[...], act, 1, 1) - wide(target_ref[...])
    slope = narrow(jnp.clip(mismatch, -1.0, 1.0) * live_ref[...])
    slope_ref[...] = slope
    padded_ref[...] = jnp.zeros_like(padded_ref)
    padded_ref[0:width, :] = slope
    raw_ref[...] = contract(act.T, padded_ref[...], 1, 1)
    by_unit(raw_ref, 1 - core, sent_ref)
    by_unit(raw_ref, core, own_ref)


def slopes_kernel(
    place_ref, act_ref, act_slope_ref, slope_ref, live_ref, target_ref, first_slope_ref,
    onehot_ref, w_own_hbm, hi_hbm, hi_again_hbm, lo_hbm, lo_again_hbm, w_middle_hbm, belief_hbm,
    slope_middle_ref, slope_first_ref, sent_ref,
    w_own, w_hi, w_lo, w_middle, belief, sems,
):
    core = place_ref[0]
    copies = [
        pltpu.make_async_copy(source, target, sems.at[i])
        for i, (source, target) in enumerate(
            ((w_own_hbm, w_own), (w_middle_hbm, w_middle), (belief_hbm, belief))
        )
    ]
    fetched = [
        pltpu.make_async_copy(source, target, sems.at[sem])
        for source, target, sem in (
            (hi_hbm, w_hi, 3), (lo_again_hbm, w_lo, 4), (hi_again_hbm, w_hi, 3), (lo_hbm, w_lo, 4),
        )
    ]
    copies[0].start()

    @pl.when(core == 0)
    def _():
        fetched[0].start()
        fetched[1].start()

    @pl.when(core != 0)
    def _():
        fetched[2].start()
        fetched[3].start()

    copies[1].start()
    copies[2].start()
    act = act_ref[...]
    live = live_ref[...]
    copies[0].wait()
    back = contract(slope_ref[...], w_own[...], 0, 0)
    for part, start, weights in ((0, 0, w_hi), (1, CUT, w_lo)):
        fetched[part].wait()
        stop = start + weights.shape[0]
        mismatch = contract(weights[...], act, 1, 1) - wide(target_ref[start:stop, :])
        slope = narrow(jnp.clip(mismatch, -1.0, 1.0) * live)
        back += contract(slope, weights[...], 0, 0)
    slope_middle = narrow(back * act_slope_ref[...])
    slope_middle_ref[...] = slope_middle
    copies[1].wait()
    slope_first = narrow(contract(w_middle[...], slope_middle, 1, 1) * first_slope_ref[...])
    slope_first = narrow(dot(onehot_ref[...], slope_first))
    slope_first_ref[...] = slope_first
    copies[2].wait()
    half = slope_first.shape[0] // 2
    for start, stop in column_cuts(belief.shape[0]):
        raw = narrow(contract(slope_first[:half], belief[start:stop, :], 1, 1))
        put_columns(raw, start // COLS, sent_ref)


def column_cuts(width):
    return [(start, min(start + COLS, width)) for start in range(0, width, COLS)]


def put_columns(raw, granule, out_ref):
    width = raw.shape[1]
    if width < COLS:
        raw = jnp.concatenate([raw, jnp.zeros((raw.shape[0], COLS - width), raw.dtype)], 1)
    for unit in range(16):
        out_ref[unit, granule] = raw[unit * ROWS : (unit + 1) * ROWS]


def middle_kernel(place_ref, slope_middle_ref, act_first_ref, sent_ref, own_ref, raw_ref):
    core = place_ref[0]
    raw_ref[...] = contract(slope_middle_ref[...], act_first_ref[...], 0, 0)
    by_unit(raw_ref, 1 - core, sent_ref)
    by_unit(raw_ref, core, own_ref)


def others(me):
    return [me] + [lax.rem(me + step, 4) for step in (1, 2, 3)]


def last_cut_kernel(place_ref, own_ref, arrived_ref, *out_refs):
    for x, out_ref in zip(others(place_ref[2]), out_refs):
        for y in range(4):
            out_ref[y] = narrow(wide(own_ref[4 * y + x]) + wide(arrived_ref[4 * y + x]))


def first_cut_kernel(
    place_ref, slope_first_ref, belief_ref, arrived_ref, middle_ref, middle_arrived_ref, *refs
):
    x_refs, y_refs, raw_ref = refs[:4], refs[4:8], refs[8]
    half = slope_first_ref.shape[0] // 2
    slope = slope_first_ref[half:, :]
    for start, stop in column_cuts(belief_ref.shape[0]):
        raw = contract(slope, belief_ref[start:stop, :], 1, 1)
        put_columns(raw, start // COLS, raw_ref)
    for y, out_ref in zip(others(place_ref[1]), y_refs):
        for x in range(4):
            unit = 4 * y + x
            out_ref[x] = narrow(raw_ref[unit, 0:5] + wide(arrived_ref[unit, 0:5]))
    for x, out_ref in zip(others(place_ref[2]), x_refs):
        for y in range(4):
            unit = 4 * y + x
            out_ref[y, 0:4] = narrow(wide(middle_ref[unit]) + wide(middle_arrived_ref[unit]))
            out_ref[y, 4:6] = narrow(raw_ref[unit, 5:7] + wide(arrived_ref[unit, 5:7]))


def sum_of(refs, index):
    return sum(wide(ref[index]) for ref in refs[1:]) + wide(refs[0][index])


def second_cut_kernel(place_ref, *refs):
    last_refs, x_refs, y_refs = refs[0:4], refs[4:8], refs[8:12]
    a_refs, b_refs = refs[12:16], refs[16:20]
    for y, out_ref in zip(others(place_ref[1]), a_refs):
        out_ref[0:4] = narrow(sum_of(last_refs, y))
        out_ref[4:10] = narrow(sum_of(x_refs, y))
    for x, out_ref in zip(others(place_ref[2]), b_refs):
        out_ref[...] = narrow(sum_of(y_refs, x))


def third_cut_kernel(place_ref, *refs):
    a_refs, b_refs = refs[0:4], refs[4:8]
    sent_ref, own_ref, sum_a, sum_b = refs[8:12]
    z_hi = place_ref[3]
    sum_a[...] = sum_of(a_refs, slice(None))
    sum_b[...] = sum_of(b_refs, slice(None))
    for side, out_ref in ((1 - z_hi, sent_ref), (z_hi, own_ref)):
        kind = out_ref.dtype
        out_ref[0:2] = sum_a[pl.ds(2 * side, 2)].astype(kind)
        out_ref[2:4] = sum_a[pl.ds(4 + 2 * side, 2)].astype(kind)
        halves = []
        for granule in range(7):
            rows = sum_b[granule] if granule < 5 else sum_a[granule + 3]
            halves.append(jnp.where(side == 0, rows[0:12], rows[12:24]))
        halves.append(jnp.zeros_like(halves[0]))
        for pair in range(4):
            out_ref[4 + pair] = jnp.concatenate(halves[2 * pair : 2 * pair + 2], 0).astype(kind)


def square_kernel(own_ref, arrived_ref, total_ref, squares_ref):
    total = own_ref[...] + wide(arrived_ref[...])
    total_ref[...] = total
    squares_ref[...] = jnp.broadcast_to(jnp.sum(total * total), squares_ref.shape)


def scale_kernel(total_ref, squares_ref, first_ref, middle_ref, last_ref):
    square_sum = jnp.sum(squares_ref[...], axis=0)
    norm_scale = lax.rsqrt(square_sum / PARAMS + 1e-06)
    norm_scale = jnp.concatenate([norm_scale] * 3, 1)
    for ref, start in ((last_ref, 0), (middle_ref, 2)):
        for half in range(2):
            columns = slice(half * COLS, min((half + 1) * COLS, ref.shape[1]))
            width = columns.stop - columns.start
            ref[:, columns] = (total_ref[start + half] * norm_scale)[:, :width]
    for granule, (start, stop) in enumerate(column_cuts(first_ref.shape[1])):
        row = granule % 2 * 12
        scaled = total_ref[4 + granule // 2, row : row + 12] * norm_scale
        first_ref[:, start:stop] = scaled[:, : stop - start]


def per_device(belief, target_value, counts, w_first, w_middle, w_last):
    total_rows, inputs = belief.shape
    width = w_last.shape[1]
    units = w_first.shape[1]
    hidden = w_middle.shape[1]
    core, mp = lax.axis_index(CORE), lax.axis_index("mp")
    place = jnp.stack([core, lax.axis_index(Y), lax.axis_index(X), lax.axis_index(ZH)])
    belief_t, target_t, w_last_t = belief.T, target_value.T, w_last.T

    around = (ZH, CORE, "mp")
    hi = lax.ppermute(w_last_t[:CUT], around, [(0, 5), (5, 0), (1, 4), (4, 1)])
    lo = lax.ppermute(w_last_t[CUT:], around, [(2, 3), (3, 2), (6, 7), (7, 6)])
    hi_again = lax.ppermute(hi, CORE, [(0, 1)])
    lo_again = lax.ppermute(lo, CORE, [(1, 0)])

    pre_first = dot(belief, w_first)
    act_first = narrow(jax.nn.silu(pre_first))
    partial_middle = dot(act_first, w_middle)
    arrived = swap(narrow(partial_middle), "mp")

    live_rows = (counts[:, None] > jnp.arange(BLOCK, dtype=jnp.int32)[None, :]).reshape(1, total_rows)
    live = live_rows.astype(F32)
    target_own = lax.dynamic_slice_in_dim(target_t, mp * width, width, 0)
    target_other = lax.dynamic_slice_in_dim(target_t, (1 - mp) * width, width, 0)
    order = jnp.arange(units, dtype=jnp.int32).reshape(4, 2, 4, 2, -1).transpose(3, 0, 2, 1, 4)
    order = jnp.where(core == 0, order[::-1], order).reshape(units)
    onehot = (order[:, None] == jnp.arange(units, dtype=jnp.int32)[None, :]).astype(BF16)

    granules = lambda *lead: ((*lead, ROWS, COLS), BF16)
    act, act_slope, slope_own, last_sent, last_own = call(
        last_kernel,
        "last",
        [SMEM] + [VMEM] * 5,
        [
            ((total_rows, hidden), BF16),
            ((total_rows, hidden), F32),
            ((width, total_rows), BF16),
            granules(16, 4),
            granules(16, 4),
        ],
        [pltpu.VMEM((hidden, units), F32), pltpu.VMEM((units, total_rows), BF16)],
    )(place, partial_middle, arrived, live, target_own, w_last_t)
    last_arrived = swap(last_sent, CORE)

    slope_middle, slope_first, first_sent = call(
        slopes_kernel,
        "slopes",
        [SMEM] + [VMEM] * 7 + [HBM] * 7,
        [((total_rows, hidden), BF16), ((units, total_rows), BF16), granules(16, 7)],
        [
            pltpu.VMEM((width, hidden), BF16),
            pltpu.VMEM((CUT, hidden), BF16),
            pltpu.VMEM((width - CUT, hidden), BF16),
            pltpu.VMEM((units, hidden), BF16),
            pltpu.VMEM((inputs, total_rows), BF16),
            pltpu.SemaphoreType.DMA((5,)),
        ],
    )(
        place, act, act_slope, slope_own, live, target_other, silu_slope(pre_first).T, onehot,
        w_last_t, hi, hi_again, lo, lo_again, w_middle, belief_t,
    )
    first_arrived = swap(first_sent, CORE)

    last_parts = call(
        last_cut_kernel, "last_cut", [SMEM] + [VMEM] * 2, [granules(4, 4)] * 4
    )(place, last_own, last_arrived)
    last_parts = [last_parts[0]] + [rotate(last_parts[k], X, k) for k in (1, 2, 3)]

    middle_sent, middle_own = call(
        middle_kernel,
        "middle",
        [SMEM] + [VMEM] * 2,
        [granules(16, 4)] * 2,
        [pltpu.VMEM((hidden, units), F32)],
    )(place, slope_middle, act_first)
    middle_arrived = swap(middle_sent, CORE)

    parts = call(
        first_cut_kernel,
        "first_cut",
        [SMEM] + [VMEM] * 5,
        [granules(4, 6)] * 4 + [granules(4, 5)] * 4,
        [pltpu.VMEM((16, 7, ROWS, COLS), F32)],
    )(place, slope_first, belief_t, first_arrived, middle_own, middle_arrived)
    x_parts = [parts[0]] + [rotate(parts[k], X, k) for k in (1, 2, 3)]
    y_parts = [parts[4]] + [rotate(parts[4 + k], Y, k) for k in (1, 2, 3)]

    parts = call(
        second_cut_kernel,
        "second_cut",
        [SMEM] + [VMEM] * 12,
        [granules(10)] * 4 + [granules(5)] * 4,
    )(place, *last_parts, *x_parts, *y_parts)
    a_parts = [parts[0]] + [rotate(parts[k], Y, k) for k in (1, 2, 3)]
    b_parts = [parts[4]] + [rotate(parts[4 + k], X, k) for k in (1, 2, 3)]

    sent, own = call(
        third_cut_kernel,
        "third_cut",
        [SMEM] + [VMEM] * 8,
        [granules(8), ((8, ROWS, COLS), F32)],
        [pltpu.VMEM((10, ROWS, COLS), F32), pltpu.VMEM((5, ROWS, COLS), F32)],
    )(place, *a_parts, *b_parts)

    total, squares = call(
        square_kernel, "square", [VMEM] * 2, [((8, ROWS, COLS), F32), ((128, 1, LANES), F32)]
    )(own, swap(sent, ZH))
    squares = lax.all_to_all(squares, ALL, 0, 0, tiled=True)
    grad_first, grad_middle, grad_last = call(
        scale_kernel,
        "scale",
        [VMEM] * 2,
        [((units // 64, inputs), F32), ((ROWS, units), F32), ((ROWS, width), F32)],
    )(total, squares)
    return grad_first.T, grad_middle.T, grad_last


def solution(mesh):
    finer = Mesh(mesh.devices.reshape(4, 2, 4, 2, mesh.shape["mp"]), ALL)
    return jax.shard_map(
        per_device,
        mesh=finer,
        in_specs=(P(DP, None), P(DP, None), P(DP), P(None, "mp"), P("mp", None), P(None, "mp")),
        out_specs=(P(None, MP_DP), P("mp", DP), P(DP, "mp")),
        check_vma=False,
    )
```

time: 264 us -> 173 us (0.66)
  waiting for transfers between devices: 132 us -> 41.9 us
  Pallas kernels: 0 us -> 41.9 us
  local copies, waits for them, and re-layouts: 26.3 us -> 11.3 us
  blocking collectives: 34.8 us -> 22 us
  starting transfers between devices: 32.5 us -> 44.8 us
  other arithmetic: 16 us -> 3.79 us
  matrix products: 17.8 us -> 6.34 us
    all_to_all x5 -> x0, waiting for transfers between devices: 132 us -> none  [the longest x3 101 us: sum_at_owner(): blocks = lax.all_to_all(cut_along(shard, dim, size), axis, 0, 0, tiled=True)]
    ppermute x0 -> x24, starting transfers between devices: none -> 44.8 us  [the longest x15 22.5 us: rotate(): return lax.ppermute(shard, axis, [(i, (i + step) % 4) for i in range(4)])]
    pallas_call x0 -> x9, Pallas kernels: none -> 41.9 us  [the longest x1 13.4 us: per_device(): call(slopes_kernel, 'slopes', [SMEM] + [VMEM] * 7 + [HBM] * 7, [((total_r...]
    ppermute x0 -> x24, waiting for transfers between devices: none -> 41.9 us  [the longest x15 27.9 us: rotate(): return lax.ppermute(shard, axis, [(i, (i + step) % 4) for i in range(4)])]
    psum x5 -> x0, blocking collectives: 34.8 us -> none  [one_axis_at_a_time(): shard = lax.psum(shard, axis)]
    all_to_all x5 -> x0, starting transfers between devices: 32.5 us -> none  [the longest x3 23.2 us: sum_at_owner(): blocks = lax.all_to_all(cut_along(shard, dim, size), axis, 0, 0, tiled=True)]
    all_to_all x0 -> x1, blocking collectives: none -> 22 us  [per_device(): squares = lax.all_to_all(squares, ALL, 0, 0, tiled=True)]
    convert_element_type x3 -> x0, local copies, waits for them, and re-layouts: 14.8 us -> none  [the longest x1 6.42 us: per_device(): raw_first.astype(jnp.bfloat16)]
  transfers between devices with their start and end apart: 5 -> 24, of which waited for: 5 -> 9; matrix products, arithmetic and copies ran while one was open for 16% -> 8% of each run, Pallas kernels for 0% -> 11%
where the time goes in v3:
time: 173 us
  starting transfers between devices  44.8 us (26%)
  waiting for transfers between devices  41.9 us (24%)
  Pallas kernels  41.9 us (24%)
  blocking collectives  22 us (13%)
  local copies, waits for them, and re-layouts  11.3 us (7%)
  matrix products  6.34 us (4%)
  other arithmetic  3.79 us (2%)
    ppermute x15, waiting for transfers between devices, rotate(): return lax.ppermute(shard, axis, [(i, (i + step) % 4) for i in range(4)])  27.9 us
    ppermute x15, starting transfers between devices, rotate(): return lax.ppermute(shard, axis, [(i, (i + step) % 4) for i in range(4)])  22.5 us
    all_to_all x1, blocking collectives, per_device(): squares = lax.all_to_all(squares, ALL, 0, 0, tiled=True)  22 us
    pallas_call x1, Pallas kernels, per_device(): call(slopes_kernel, 'slopes', [SMEM] + [VMEM] * 7 + [HBM] * 7, [((total_r...  13.4 us
    ppermute x1, waiting for transfers between devices, per_device(): lo = lax.ppermute(w_last_t[CUT:], around, [(2, 3), (3, 2), (6, 7), (7, 6)])  9.95 us
    ppermute x1, starting transfers between devices, per_device(): lo_again = lax.ppermute(lo, CORE, [(1, 0)])  9.64 us
    ppermute x5, starting transfers between devices, swap(): return lax.ppermute(shard, axis, [(0, 1), (1, 0)])  7.49 us
    pallas_call x1, Pallas kernels, per_device(): call(last_kernel, 'last', [SMEM] + [VMEM] * 5, [((total_rows, hidden), BF...  6.89 us
  transfers between devices with their start and end apart: 24, of which 9 were waited for; matrix products, arithmetic and copies ran while one was open for 8% of the time, Pallas kernels for 11%

profile of v3, /device:TPU:1, one launch (start us, length us, event | category | flops | bytes accessed | tf_op | source)
XLA Modules:
  0.0 172.9 jit_solution(17297228693194362846)
XLA Ops:
  0.6 1.6 slice.8
  2.2 2.0 %collective-permute-start.5 = (bf16[480,1536]{1,0:T(8,128)(2,1)S(1)}, bf16[480,1536]{1,0:T(8,128)(2,1)}, u32[]{:S(2)}, u32[]{:S(2)}) collective-permute-start(bf16[480,1536]{1,0:T(8,128)(2,1)S(1)} %slice.8), channel_id=1, source_target_pairs={{0,17},{17,0},{1,16},{16,1},{4,21},{21,4},{5,20},{20,5},{8,25},{25... | collective-permute-start | bytes 4423688 | tf_op jit(solution)/shard_map/ppermute | solution.py:268
  4.2 4.4 %multiply_convert_fusion = (bf16[256,768]{1,0:T(8,128)(2,1)S(1)}, f32[256,768]{1,0:T(8,128)}) fusion(bf16[256,2652]{0,1:T(8,128)(2,1)S(1)} %copy-done.1, bf16[2652,768]{1,0:T(8,128)(2,1)} %param.9), kind=kOutput, calls=%fused_computation.9 | convolution fusion | flops 1043791872 | bytes 6610944 | tf_op jit(solution)/shard_map/dot_general | solution.py:46
  8.6 1.3 collective-permute-start.6
  9.9 2.0 %fusion.6 = (bf16[256,1536]{1,0:T(8,128)(2,1)S(1)}, f32[256,1536]{1,0:T(8,128)}) fusion(bf16[256,768]{1,0:T(8,128)(2,1)S(1)} %get-tuple-element.79.act_first_ref, bf16[768,1536]{1,0:T(8,128)(2,1)S(1)} %copy-done), kind=kOutput, calls=%fused_computation.16 | convolution fusion | flops 604372992 | bytes 5111808 | tf_op jit(solution)/shard_map/dot_general | solution.py:46
  11.9 2.5 %collective-permute-start = (bf16[256,1536]{1,0:T(8,128)(2,1)S(1)}, bf16[256,1536]{1,0:T(8,128)(2,1)S(1)}, u32[]{:S(2)}, u32[]{:S(2)}) collective-permute-start(bf16[256,1536]{1,0:T(8,128)(2,1)S(1)} %get-tuple-element.81), channel_id=1, source_target_pairs={{0,1},{1,0},{2,3},{3,2},{4,5},{5,4},{6,7},{7,6},{8,9},{9,8},{10,11... | collective-permute-start | bytes 2359304 | tf_op jit(solution)/shard_map/ppermute | solution.py:33
  14.3 1.9 %slice.9 = bf16[183,1536]{1,0:T(8,128)(2,1)} slice(bf16[663,1536]{1,0:T(8,128)(2,1)} %bitcast.33), slice={[480:663], [0:1536]} | slice | bytes 1124352 | tf_op jit(solution)/shard_map/slice | solution.py:269
  16.2 2.0 %collective-permute-start.7 = (bf16[183,1536]{1,0:T(8,128)(2,1)}, bf16[183,1536]{1,0:T(8,128)(2,1)}, u32[]{:S(2)}, u32[]{:S(2)}) collective-permute-start(bf16[183,1536]{1,0:T(8,128)(2,1)} %slice.9), channel_id=1, source_target_pairs={{2,3},{3,2},{18,19},{19,18},{6,7},{7,6},{22,23},{23,22},{10,11},{1... | collective-permute-start | bytes 1686536 | tf_op jit(solution)/shard_map/ppermute | solution.py:269
  18.3 0.6 compare_convert_fusion
  18.9 1.0 dynamic-slice_bitcast_fusion
  19.9 9.9 %collective-permute-done.7.lo_hbm = bf16[183,1536]{1,0:T(8,128)(2,1)} collective-permute-done((bf16[183,1536]{1,0:T(8,128)(2,1)}, bf16[183,1536]{1,0:T(8,128)(2,1)}, u32[]{:S(2)}, u32[]{:S(2)}) %collective-permute-start.7) | collective-permute-done | bytes 562208 | tf_op jit(solution)/shard_map/ppermute | solution.py:269
  29.9 9.6 %collective-permute-start.8 = (bf16[183,1536]{1,0:T(8,128)(2,1)}, bf16[183,1536]{1,0:T(8,128)(2,1)}, u32[]{:S(2)}, u32[]{:S(2)}) collective-permute-start(bf16[183,1536]{1,0:T(8,128)(2,1)} %collective-permute-done.7.lo_hbm), channel_id=1, source_target_pairs={{2,0},{3,1},{6,4},{7,5},{10,8},{11,9},{14,12},{15,13},{18,16},{19,... | collective-permute-start | bytes 1686536 | tf_op jit(solution)/shard_map/ppermute | solution.py:271
  39.5 0.6 pad_add_fusion.place_ref
  40.1 0.3 copy.9
  40.4 0.1 eq.19
  40.5 1.4 fusion.onehot_ref
  41.9 1.2 fusion.5.first_slope_ref
  43.0 0.9 copy-done.6
  44.0 6.9 %last.1 = (bf16[256,1536]{1,0:T(8,128)(2,1)}, f32[256,1536]{1,0:T(8,128)}, bf16[663,256]{1,0:T(8,128)(2,1)}, bf16[16,4,24,384]{3,2,1,0:T(8,128)(2,1)}, bf16[16,4,24,384]{3,2,1,0:T(8,128)(2,1)}) custom-call(s32[4]{0:T(128)} %pad_add_fusion.place_ref, f32[256,1536]{1,0:T(8,128)} %get-tuple-element.82.partial_ref, bf16[256,1536]{1,0:T(8,128)(2,1)} %copy-done.6, ...), custom_call_target="tpu_custom_call" | custom-call | tf_op jit(solution)/shard_map/last/pallas_call | solution.py:287
  50.9 13.4 %slopes.1 = (bf16[256,1536]{1,0:T(8,128)(2,1)}, bf16[768,256]{1,0:T(8,128)(2,1)}, bf16[16,7,24,384]{3,2,1,0:T(8,128)(2,1)}) custom-call(s32[4]{0:T(128)} %pad_add_fusion.place_ref, bf16[256,1536]{1,0:T(8,128)(2,1)} %get-tuple-element.46.act_ref, f32[256,1536]{1,0:T(8,128)} %get-tuple-element.47.act_slope_ref, bf16[663,256]{1,0:T(8,128)(2,1)} %get-tuple-element.48.slope_ref, ...), custom_call_target="tpu_custom_call" | custom-call | tf_op jit(solution)/shard_map/slopes/pallas_call | solution.py:302
  64.3 0.7 collective-permute-start.9
  65.0 0.3 collective-permute-start.1
  65.2 3.6 %middle.1 = (bf16[16,4,24,384]{3,2,1,0:T(8,128)(2,1)}, bf16[16,4,24,384]{3,2,1,0:T(8,128)(2,1)}) custom-call(s32[4]{0:T(128)} %pad_add_fusion.place_ref, bf16[256,1536]{1,0:T(8,128)(2,1)} %get-tuple-element.51.slope_middle_ref, bf16[256,768]{1,0:T(8,128)(2,1)} %copy-done.3), custom_call_target="tpu_custom_call" | custom-call | tf_op jit(solution)/shard_map/middle/pallas_call | solution.py:326
  68.9 0.2 collective-permute-start.10
  69.1 1.3 collective-permute-done.1.arrived_ref
  70.4 1.1 copy-done.4
  71.4 2.8 %last_cut.1 = (bf16[4,4,24,384]{3,2,1,0:T(8,128)(2,1)}, bf16[4,4,24,384]{3,2,1,0:T(8,128)(2,1)}, bf16[4,4,24,384]{3,2,1,0:T(8,128)(2,1)}, bf16[4,4,24,384]{3,2,1,0:T(8,128)(2,1)}) custom-call(s32[4]{0:T(128)} %pad_add_fusion.place_ref, bf16[16,4,24,384]{3,2,1,0:T(8,128)(2,1)} %get-tuple-element.40.own_ref, bf16[16,4,24,384]{3,2,1,0:T(8,128)(2,1)} %copy-done.4), custom_call_target="tpu_custom_call" | custom-call | tf_op jit(solution)/shard_map/last_cut/pallas_call | solution.py:321
  74.3 1.2 collective-permute-start.2
  75.5 1.0 copy-done.5
  76.5 0.7 copy-done.2
  77.2 5.6 %first_cut.1 = (bf16[4,6,24,384]{3,2,1,0:T(8,128)(2,1)}, bf16[4,6,24,384]{3,2,1,0:T(8,128)(2,1)}, bf16[4,6,24,384]{3,2,1,0:T(8,128)(2,1)}, bf16[4,6,24,384]{3,2,...) custom-call(s32[4]{0:T(128)} %pad_add_fusion.place_ref, ...), custom_call_target="tpu_custom_call" | custom-call | tf_op jit(solution)/shard_map/first_cut/pallas_call | solution.py:335
  82.8 1.3 collective-permute-start.14
  84.1 2.5 %collective-permute-start.3 = (bf16[4,4,24,384]{3,2,1,0:T(8,128)(2,1)S(1)}, bf16[4,4,24,384]{3,2,1,0:T(8,128)(2,1)S(1)}, u32[]{:S(2)}, u32[]{:S(2)}) collective-permute-start(bf16[4,4,24,384]{3,2,1,0:T(8,128)(2,1)S(1)} %copy-done.27), channel_id=1, source_target_pairs={{0,8},{4,12},{8,0},{12,4},{1,9},{5,13},{9,1},{13,5},{2,10},{6,14},... | collective-permute-start | bytes 884744 | tf_op jit(solution)/shard_map/ppermute | solution.py:37
  86.6 1.1 collective-permute-start.4
  87.7 0.3 collective-permute-start.11
  88.0 0.9 collective-permute-start.12
  88.9 4.3 %collective-permute-done.3.refs_2_ = bf16[4,4,24,384]{3,2,1,0:T(8,128)(2,1)S(1)} collective-permute-done((bf16[4,4,24,384]{3,2,1,0:T(8,128)(2,1)S(1)}, bf16[4,4,24,384]{3,2,1,0:T(8,128)(2,1)S(1)}, u32[]{:S(2)}, u32[]{:S(2)}) %collective-permute-start.3) | collective-permute-done | bytes 294944 | tf_op jit(solution)/shard_map/ppermute | solution.py:37
  93.2 1.5 collective-permute-start.13
  94.7 5.0 %collective-permute-done.4.refs_3_ = bf16[4,4,24,384]{3,2,1,0:T(8,128)(2,1)S(1)} collective-permute-done((bf16[4,4,24,384]{3,2,1,0:T(8,128)(2,1)S(1)}, bf16[4,4,24,384]{3,2,1,0:T(8,128)(2,1)S(1)}, u32[]{:S(2)}, u32[]{:S(2)}) %collective-permute-start.4) | collective-permute-done | bytes 294944 | tf_op jit(solution)/shard_map/ppermute | solution.py:37
  99.7 2.6 %collective-permute-start.15 = (bf16[4,5,24,384]{3,2,1,0:T(8,128)(2,1)}, bf16[4,5,24,384]{3,2,1,0:T(8,128)(2,1)S(1)}, u32[]{:S(2)}, u32[]{:S(2)}) collective-permute-start(bf16[4,5,24,384]{3,2,1,0:T(8,128)(2,1)} %get-tuple-element.60), channel_id=1, source_target_pairs={{0,64},{32,96},{64,0},{96,32},{1,65},{33,97},{65,1},{97,33},{2,66}... | collective-permute-start | bytes 1105928 | tf_op jit(solution)/shard_map/ppermute | solution.py:37
  102.3 1.1 collective-permute-start.16
  103.4 5.9 %collective-permute-done.15.refs_10_ = bf16[4,5,24,384]{3,2,1,0:T(8,128)(2,1)S(1)} collective-permute-done((bf16[4,5,24,384]{3,2,1,0:T(8,128)(2,1)}, bf16[4,5,24,384]{3,2,1,0:T(8,128)(2,1)S(1)}, u32[]{:S(2)}, u32[]{:S(2)}) %collective-permute-start.15) | collective-permute-done | bytes 368672 | tf_op jit(solution)/shard_map/ppermute | solution.py:37
  109.3 8.6 %collective-permute-done.16.refs_11_ = bf16[4,5,24,384]{3,2,1,0:T(8,128)(2,1)S(1)} collective-permute-done((bf16[4,5,24,384]{3,2,1,0:T(8,128)(2,1)}, bf16[4,5,24,384]{3,2,1,0:T(8,128)(2,1)S(1)}, u32[]{:S(2)}, u32[]{:S(2)}) %collective-permute-start.16) | collective-permute-done | bytes 368672 | tf_op jit(solution)/shard_map/ppermute | solution.py:37
  118.0 0.6 copy-done.14
  118.6 0.2 copy-done.9
  118.8 0.1 copy-done.10
  118.9 0.2 copy-done.11
  119.1 3.6 %second_cut.1 = (bf16[10,24,384]{2,1,0:T(8,128)(2,1)}, bf16[10,24,384]{2,1,0:T(8,128)(2,1)}, bf16[10,24,384]{2,1,0:T(8,128)(2,1)}, bf16[10,24,384]{2,1,0:T(8,128...) custom-call(s32[4]{0:T(128)} %pad_add_fusion.place_ref, ...), custom_call_target="tpu_custom_call" | custom-call | tf_op jit(solution)/shard_map/second_cut/pallas_call | solution.py:345
  122.7 1.3 collective-permute-start.20
  124.0 1.3 collective-permute-start.17
  125.3 2.0 %collective-permute-start.18 = (bf16[10,24,384]{2,1,0:T(8,128)(2,1)}, bf16[10,24,384]{2,1,0:T(8,128)(2,1)S(1)}, u32[]{:S(2)}, u32[]{:S(2)}) collective-permute-start(bf16[10,24,384]{2,1,0:T(8,128)(2,1)} %get-tuple-element.64), channel_id=1, source_target_pairs={{0,64},{32,96},{64,0},{96,32},{1,65},{33,97},{65,1},{97,33},{2,66}... | collective-permute-start | bytes 552968 | tf_op jit(solution)/shard_map/ppermute | solution.py:37
  127.3 1.4 collective-permute-start.19
  128.7 4.0 %collective-permute-start.21 = (bf16[5,24,384]{2,1,0:T(8,128)(2,1)}, bf16[5,24,384]{2,1,0:T(8,128)(2,1)S(1)}, u32[]{:S(2)}, u32[]{:S(2)}) collective-permute-start(bf16[5,24,384]{2,1,0:T(8,128)(2,1)} %get-tuple-element.68), channel_id=1, source_target_pairs={{0,8},{4,12},{8,0},{12,4},{1,9},{5,13},{9,1},{13,5},{2,10},{6,14},... | collective-permute-start | bytes 276488 | tf_op jit(solution)/shard_map/ppermute | solution.py:37
  132.7 2.1 %collective-permute-done.21.refs_6_ = bf16[5,24,384]{2,1,0:T(8,128)(2,1)S(1)} collective-permute-done((bf16[5,24,384]{2,1,0:T(8,128)(2,1)}, bf16[5,24,384]{2,1,0:T(8,128)(2,1)S(1)}, u32[]{:S(2)}, u32[]{:S(2)}) %collective-permute-start.21) | collective-permute-done | bytes 92192 | tf_op jit(solution)/shard_map/ppermute | solution.py:37
  134.9 1.9 %collective-permute-done.22.refs_7_ = bf16[5,24,384]{2,1,0:T(8,128)(2,1)S(1)} collective-permute-done((bf16[5,24,384]{2,1,0:T(8,128)(2,1)}, bf16[5,24,384]{2,1,0:T(8,128)(2,1)S(1)}, u32[]{:S(2)}, u32[]{:S(2)}) %collective-permute-start.22) | collective-permute-done | bytes 92192 | tf_op jit(solution)/shard_map/ppermute | solution.py:37
  136.8 0.6 copy-done.24
  137.4 0.1 copy-done.18
  137.6 2.3 %third_cut.1 = (bf16[8,24,384]{2,1,0:T(8,128)(2,1)}, f32[8,24,384]{2,1,0:T(8,128)}) custom-call(s32[4]{0:T(128)} %pad_add_fusion.place_ref, bf16[10,24,384]{2,1,0:T(8,128)(2,1)} %get-tuple-element.62.refs_0_, bf16[10,24,384]{2,1,0:T(8,128)(2,1)} %copy-done.18, bf16[10,24,384]{2,1,0:T(8,128)(2,1)} %copy-done.19, bf16[10,24,384]{2,1,0:T(8,128)(2,1)} %copy-done.20, ...), custom_call_target="tpu_custom_call" | custom-call | tf_op jit(solution)/shard_map/third_cut/pallas_call | solution.py:354
  139.9 3.8 %collective-permute-start.23 = (bf16[8,24,384]{2,1,0:T(8,128)(2,1)}, bf16[8,24,384]{2,1,0:T(8,128)(2,1)S(1)}, u32[]{:S(2)}, u32[]{:S(2)}) collective-permute-start(bf16[8,24,384]{2,1,0:T(8,128)(2,1)} %get-tuple-element.71), channel_id=1, source_target_pairs={{0,16},{16,0},{1,17},{17,1},{2,18},{18,2},{3,19},{19,3},{4,20},{20... | collective-permute-start | bytes 442376 | tf_op jit(solution)/shard_map/ppermute | solution.py:33
  143.8 2.7 %collective-permute-done.23.arrived_ref = bf16[8,24,384]{2,1,0:T(8,128)(2,1)S(1)} collective-permute-done((bf16[8,24,384]{2,1,0:T(8,128)(2,1)}, bf16[8,24,384]{2,1,0:T(8,128)(2,1)S(1)}, u32[]{:S(2)}, u32[]{:S(2)}) %collective-permute-start.23) | collective-permute-done | bytes 147488 | tf_op jit(solution)/shard_map/ppermute | solution.py:33
  146.5 0.7 copy-done.21
  147.2 1.9 %square.1 = (f32[8,24,384]{2,1,0:T(8,128)}, f32[128,1,128]{2,1,0:T(1,128)}) custom-call(f32[8,24,384]{2,1,0:T(8,128)} %get-tuple-element.70.own_ref, bf16[8,24,384]{2,1,0:T(8,128)(2,1)} %copy-done.21), custom_call_target="tpu_custom_call" | custom-call | tf_op jit(solution)/shard_map/square/pallas_call | solution.py:362
  149.0 22.0 %all_to_all.5.squares_ref = f32[128,1,128]{2,1,0:T(1,128)} all-to-all(f32[128,1,128]{2,1,0:T(1,128)} %get-tuple-element.73), channel_id=1, replica_groups=mesh['dp_0'=4,'dp_1'=2,'dp_2'=4,'dp_3'=2,'mp'=2] {'dp_0','dp_1','dp_2','..., dimensions={0} | all-to-all | bytes 131072 | tf_op jit(solution)/shard_map/all_to_all | solution.py:365
  171.1 1.8 %scale.1 = (f32[12,2652]{1,0:T(8,128)}, f32[24,768]{1,0:T(8,128)}, f32[24,663]{1,0:T(8,128)}) custom-call(f32[8,24,384]{2,1,0:T(8,128)} %get-tuple-element.72.total_ref, f32[128,1,128]{2,1,0:T(1,128)} %all_to_all.5.squares_ref), custom_call_target="tpu_custom_call" | custom-call | tf_op jit(solution)/shard_map/scale/pallas_call | solution.py:366
  (65 shorter events, 0.3 us)
Async XLA Ops:
  0.6 3.6 %copy-start.1 = (bf16[256,2652]{0,1:T(8,128)(2,1)S(1)}, bf16[256,2652]{0,1:T(8,128)(2,1)}, u32[]{:S(2)}) copy-start(bf16[256,2652]{0,1:T(8,128)(2,1)} %param.6) | copy-start | bytes 4073476
  2.2 7.6 %copy-start = (bf16[768,1536]{1,0:T(8,128)(2,1)S(1)}, bf16[768,1536]{1,0:T(8,128)(2,1)}, u32[]{:S(2)}) copy-start(bf16[768,1536]{1,0:T(8,128)(2,1)} %w_middle_hbm.1) | copy-start | bytes 7077892
  2.2 6.3 %collective-permute-start.5 = (bf16[480,1536]{1,0:T(8,128)(2,1)S(1)}, bf16[480,1536]{1,0:T(8,128)(2,1)}, u32[]{:S(2)}, u32[]{:S(2)}) collective-permute-start(bf16[480,1536]{1,0:T(8,128)(2,1)S(1)} %slice.8), channel_id=1, source_target_pairs={{0,17},{17,0},{1,16},{16,1},{4,21},{21,4},{5,20},{20,5},{8,25},{25... | collective-permute-start | bytes 4423688 | tf_op jit(solution)/shard_map/ppermute | solution.py:268
  8.6 3.3 %copy-start.3 = (bf16[256,768]{1,0:T(8,128)(2,1)}, bf16[256,768]{1,0:T(8,128)(2,1)S(1)}, u32[]{:S(2)}) copy-start(bf16[256,768]{1,0:T(8,128)(2,1)S(1)} %get-tuple-element.79.act_first_ref) | copy-start | bytes 1179652
  8.6 42.3 %collective-permute-start.6 = (bf16[480,1536]{1,0:T(8,128)(2,1)}, bf16[480,1536]{1,0:T(8,128)(2,1)}, u32[]{:S(2)}, u32[]{:S(2)}) collective-permute-start(bf16[480,1536]{1,0:T(8,128)(2,1)} %collective-permute-done.5.hi_hbm), channel_id=1, source_target_pairs={{0,2},{1,3},{4,6},{5,7},{8,10},{9,11},{12,14},{13,15},{16,18},{17,... | collective-permute-start | bytes 4423688 | tf_op jit(solution)/shard_map/ppermute | solution.py:270
  9.9 8.4 %copy-start.28 = (s32[2]{0:T(128)S(1)}, s32[2]{0:T(128)}, u32[]{:S(2)}) copy-start(s32[2]{0:T(128)} %param.8) | copy-start | bytes 28
  9.9 9.0 %copy-start.8 = (bf16[256,1326]{0,1:T(8,128)(2,1)S(1)}, bf16[256,1326]{0,1:T(8,128)(2,1)}, u32[]{:S(2)}) copy-start(bf16[256,1326]{0,1:T(8,128)(2,1)} %param.7) | copy-start | bytes 2036740
  11.9 28.3 %copy-start.7 = (f32[256,768]{1,0:T(8,128)S(1)}, f32[256,768]{1,0:T(8,128)}, u32[]{:S(2)}) copy-start(f32[256,768]{1,0:T(8,128)} %get-tuple-element.80) | copy-start | bytes 2359300
  11.9 31.2 %collective-permute-start = (bf16[256,1536]{1,0:T(8,128)(2,1)S(1)}, bf16[256,1536]{1,0:T(8,128)(2,1)S(1)}, u32[]{:S(2)}, u32[]{:S(2)}) collective-permute-start(bf16[256,1536]{1,0:T(8,128)(2,1)S(1)} %get-tuple-element.81), channel_id=1, source_target_pairs={{0,1},{1,0},{2,3},{3,2},{4,5},{5,4},{6,7},{7,6},{8,9},{9,8},{10,11... | collective-permute-start | bytes 2359304 | tf_op jit(solution)/shard_map/ppermute | solution.py:33
  16.2 13.6 %collective-permute-start.7 = (bf16[183,1536]{1,0:T(8,128)(2,1)}, bf16[183,1536]{1,0:T(8,128)(2,1)}, u32[]{:S(2)}, u32[]{:S(2)}) collective-permute-start(bf16[183,1536]{1,0:T(8,128)(2,1)} %slice.9), channel_id=1, source_target_pairs={{2,3},{3,2},{18,19},{19,18},{6,7},{7,6},{22,23},{23,22},{10,11},{1... | collective-permute-start | bytes 1686536 | tf_op jit(solution)/shard_map/ppermute | solution.py:269
  29.9 21.0 %collective-permute-start.8 = (bf16[183,1536]{1,0:T(8,128)(2,1)}, bf16[183,1536]{1,0:T(8,128)(2,1)}, u32[]{:S(2)}, u32[]{:S(2)}) collective-permute-start(bf16[183,1536]{1,0:T(8,128)(2,1)} %collective-permute-done.7.lo_hbm), channel_id=1, source_target_pairs={{2,0},{3,1},{6,4},{7,5},{10,8},{11,9},{14,12},{15,13},{18,16},{19,... | collective-permute-start | bytes 1686536 | tf_op jit(solution)/shard_map/ppermute | solution.py:271
  43.0 0.9 copy-start.6
  50.9 14.1 %copy-start.25 = (bf16[16,4,24,384]{3,2,1,0:T(8,128)(2,1)S(1)}, bf16[16,4,24,384]{3,2,1,0:T(8,128)(2,1)}, u32[]{:S(2)}) copy-start(bf16[16,4,24,384]{3,2,1,0:T(8,128)(2,1)} %get-tuple-element.41) | copy-start | bytes 3538948
  64.3 11.2 %collective-permute-start.9 = (bf16[16,7,24,384]{3,2,1,0:T(8,128)(2,1)}, bf16[16,7,24,384]{3,2,1,0:T(8,128)(2,1)S(1)}, u32[]{:S(2)}, u32[]{:S(2)}) collective-permute-start(bf16[16,7,24,384]{3,2,1,0:T(8,128)(2,1)} %get-tuple-element.50), channel_id=1, source_target_pairs={{0,2},{2,0},{1,3},{3,1},{4,6},{6,4},{5,7},{7,5},{8,10},{10,8},{9,1... | collective-permute-start | bytes 6193160 | tf_op jit(solution)/shard_map/ppermute | solution.py:33
  65.0 5.4 %collective-permute-start.1 = (bf16[16,4,24,384]{3,2,1,0:T(8,128)(2,1)S(1)}, bf16[16,4,24,384]{3,2,1,0:T(8,128)(2,1)S(1)}, u32[]{:S(2)}, u32[]{:S(2)}) collective-permute-start(bf16[16,4,24,384]{3,2,1,0:T(8,128)(2,1)S(1)} %copy-done.25), channel_id=1, source_target_pairs={{0,2},{2,0},{1,3},{3,1},{4,6},{6,4},{5,7},{7,5},{8,10},{10,8},{9,1... | collective-permute-start | bytes 3538952 | tf_op jit(solution)/shard_map/ppermute | solution.py:33
  68.9 6.6 %collective-permute-start.10 = (bf16[16,4,24,384]{3,2,1,0:T(8,128)(2,1)}, bf16[16,4,24,384]{3,2,1,0:T(8,128)(2,1)S(1)}, u32[]{:S(2)}, u32[]{:S(2)}) collective-permute-start(bf16[16,4,24,384]{3,2,1,0:T(8,128)(2,1)} %get-tuple-element.53), channel_id=1, source_target_pairs={{0,2},{2,0},{1,3},{3,1},{4,6},{6,4},{5,7},{7,5},{8,10},{10,8},{9,1... | collective-permute-start | bytes 3538952 | tf_op jit(solution)/shard_map/ppermute | solution.py:33
  70.4 1.1 copy-start.4
  74.3 13.8 %collective-permute-start.2 = (bf16[4,4,24,384]{3,2,1,0:T(8,128)(2,1)}, bf16[4,4,24,384]{3,2,1,0:T(8,128)(2,1)S(1)}, u32[]{:S(2)}, u32[]{:S(2)}) collective-permute-start(bf16[4,4,24,384]{3,2,1,0:T(8,128)(2,1)} %get-tuple-element.43), channel_id=1, source_target_pairs={{0,4},{4,8},{8,12},{12,0},{1,5},{5,9},{9,13},{13,1},{2,6},{6,10},{... | collective-permute-start | bytes 884744 | tf_op jit(solution)/shard_map/ppermute | solution.py:37
  75.5 1.0 copy-start.5
  75.5 1.7 %copy-start.2 = (bf16[16,7,24,384]{3,2,1,0:T(8,128)(2,1)}, bf16[16,7,24,384]{3,2,1,0:T(8,128)(2,1)S(1)}, u32[]{:S(2)}) copy-start(bf16[16,7,24,384]{3,2,1,0:T(8,128)(2,1)S(1)} %collective-permute-done.9.arrived_ref) | copy-start | bytes 6193156
  77.2 6.9 %copy-start.27 = (bf16[4,4,24,384]{3,2,1,0:T(8,128)(2,1)S(1)}, bf16[4,4,24,384]{3,2,1,0:T(8,128)(2,1)}, u32[]{:S(2)}) copy-start(bf16[4,4,24,384]{3,2,1,0:T(8,128)(2,1)} %get-tuple-element.44) | copy-start | bytes 884740
  77.2 9.3 %copy-start.26 = (bf16[4,4,24,384]{3,2,1,0:T(8,128)(2,1)S(1)}, bf16[4,4,24,384]{3,2,1,0:T(8,128)(2,1)}, u32[]{:S(2)}) copy-start(bf16[4,4,24,384]{3,2,1,0:T(8,128)(2,1)} %get-tuple-element.45) | copy-start | bytes 884740
  82.8 19.5 %collective-permute-start.14 = (bf16[4,5,24,384]{3,2,1,0:T(8,128)(2,1)}, bf16[4,5,24,384]{3,2,1,0:T(8,128)(2,1)S(1)}, u32[]{:S(2)}, u32[]{:S(2)}) collective-permute-start(bf16[4,5,24,384]{3,2,1,0:T(8,128)(2,1)} %get-tuple-element.59), channel_id=1, source_target_pairs={{0,32},{32,64},{64,96},{96,0},{1,33},{33,65},{65,97},{97,1},{2,34}... | collective-permute-start | bytes 1105928 | tf_op jit(solution)/shard_map/ppermute | solution.py:37
  84.1 9.1 %collective-permute-start.3 = (bf16[4,4,24,384]{3,2,1,0:T(8,128)(2,1)S(1)}, bf16[4,4,24,384]{3,2,1,0:T(8,128)(2,1)S(1)}, u32[]{:S(2)}, u32[]{:S(2)}) collective-permute-start(bf16[4,4,24,384]{3,2,1,0:T(8,128)(2,1)S(1)} %copy-done.27), channel_id=1, source_target_pairs={{0,8},{4,12},{8,0},{12,4},{1,9},{5,13},{9,1},{13,5},{2,10},{6,14},... | collective-permute-start | bytes 884744 | tf_op jit(solution)/shard_map/ppermute | solution.py:37
  86.6 13.1 %collective-permute-start.4 = (bf16[4,4,24,384]{3,2,1,0:T(8,128)(2,1)S(1)}, bf16[4,4,24,384]{3,2,1,0:T(8,128)(2,1)S(1)}, u32[]{:S(2)}, u32[]{:S(2)}) collective-permute-start(bf16[4,4,24,384]{3,2,1,0:T(8,128)(2,1)S(1)} %copy-done.26), channel_id=1, source_target_pairs={{0,12},{4,0},{8,4},{12,8},{1,13},{5,1},{9,5},{13,9},{2,14},{6,2},{... | collective-permute-start | bytes 884744 | tf_op jit(solution)/shard_map/ppermute | solution.py:37
  87.7 30.2 %collective-permute-start.11 = (bf16[4,6,24,384]{3,2,1,0:T(8,128)(2,1)}, bf16[4,6,24,384]{3,2,1,0:T(8,128)(2,1)S(1)}, u32[]{:S(2)}, u32[]{:S(2)}) collective-permute-start(bf16[4,6,24,384]{3,2,1,0:T(8,128)(2,1)} %get-tuple-element.55), channel_id=1, source_target_pairs={{0,4},{4,8},{8,12},{12,0},{1,5},{5,9},{9,13},{13,1},{2,6},{6,10},{... | collective-permute-start | bytes 1327112 | tf_op jit(solution)/shard_map/ppermute | solution.py:37
  88.0 29.9 %copy-start.15 = (bf16[4,4,24,384]{3,2,1,0:T(8,128)(2,1)}, bf16[4,4,24,384]{3,2,1,0:T(8,128)(2,1)S(1)}, u32[]{:S(2)}) copy-start(bf16[4,4,24,384]{3,2,1,0:T(8,128)(2,1)S(1)} %collective-permute-done.2.refs_1_) | copy-start | bytes 884740
  88.0 29.9 %collective-permute-start.12 = (bf16[4,6,24,384]{3,2,1,0:T(8,128)(2,1)}, bf16[4,6,24,384]{3,2,1,0:T(8,128)(2,1)S(1)}, u32[]{:S(2)}, u32[]{:S(2)}) collective-permute-start(bf16[4,6,24,384]{3,2,1,0:T(8,128)(2,1)} %get-tuple-element.56), channel_id=1, source_target_pairs={{0,8},{4,12},{8,0},{12,4},{1,9},{5,13},{9,1},{13,5},{2,10},{6,14},... | collective-permute-start | bytes 1327112 | tf_op jit(solution)/shard_map/ppermute | solution.py:37
  93.2 24.8 %copy-start.16 = (bf16[4,4,24,384]{3,2,1,0:T(8,128)(2,1)}, bf16[4,4,24,384]{3,2,1,0:T(8,128)(2,1)S(1)}, u32[]{:S(2)}) copy-start(bf16[4,4,24,384]{3,2,1,0:T(8,128)(2,1)S(1)} %collective-permute-done.3.refs_2_) | copy-start | bytes 884740
  93.2 24.8 %collective-permute-start.13 = (bf16[4,6,24,384]{3,2,1,0:T(8,128)(2,1)}, bf16[4,6,24,384]{3,2,1,0:T(8,128)(2,1)S(1)}, u32[]{:S(2)}, u32[]{:S(2)}) collective-permute-start(bf16[4,6,24,384]{3,2,1,0:T(8,128)(2,1)} %get-tuple-element.57), channel_id=1, source_target_pairs={{0,12},{4,0},{8,4},{12,8},{1,13},{5,1},{9,5},{13,9},{2,14},{6,2},{... | collective-permute-start | bytes 1327112 | tf_op jit(solution)/shard_map/ppermute | solution.py:37
  99.7 18.3 %copy-start.17 = (bf16[4,4,24,384]{3,2,1,0:T(8,128)(2,1)}, bf16[4,4,24,384]{3,2,1,0:T(8,128)(2,1)S(1)}, u32[]{:S(2)}) copy-start(bf16[4,4,24,384]{3,2,1,0:T(8,128)(2,1)S(1)} %collective-permute-done.4.refs_3_) | copy-start | bytes 884740
  99.7 9.6 %collective-permute-start.15 = (bf16[4,5,24,384]{3,2,1,0:T(8,128)(2,1)}, bf16[4,5,24,384]{3,2,1,0:T(8,128)(2,1)S(1)}, u32[]{:S(2)}, u32[]{:S(2)}) collective-permute-start(bf16[4,5,24,384]{3,2,1,0:T(8,128)(2,1)} %get-tuple-element.60), channel_id=1, source_target_pairs={{0,64},{32,96},{64,0},{96,32},{1,65},{33,97},{65,1},{97,33},{2,66}... | collective-permute-start | bytes 1105928 | tf_op jit(solution)/shard_map/ppermute | solution.py:37
  102.3 15.6 %copy-start.12 = (bf16[4,5,24,384]{3,2,1,0:T(8,128)(2,1)}, bf16[4,5,24,384]{3,2,1,0:T(8,128)(2,1)S(1)}, u32[]{:S(2)}) copy-start(bf16[4,5,24,384]{3,2,1,0:T(8,128)(2,1)S(1)} %collective-permute-done.14.refs_9_) | copy-start | bytes 1105924
  102.3 15.6 %collective-permute-start.16 = (bf16[4,5,24,384]{3,2,1,0:T(8,128)(2,1)}, bf16[4,5,24,384]{3,2,1,0:T(8,128)(2,1)S(1)}, u32[]{:S(2)}, u32[]{:S(2)}) collective-permute-start(bf16[4,5,24,384]{3,2,1,0:T(8,128)(2,1)} %get-tuple-element.61), channel_id=1, source_target_pairs={{0,96},{32,0},{64,32},{96,64},{1,97},{33,1},{65,33},{97,65},{2,98}... | collective-permute-start | bytes 1105928 | tf_op jit(solution)/shard_map/ppermute | solution.py:37
  109.3 8.7 %copy-start.13 = (bf16[4,5,24,384]{3,2,1,0:T(8,128)(2,1)}, bf16[4,5,24,384]{3,2,1,0:T(8,128)(2,1)S(1)}, u32[]{:S(2)}) copy-start(bf16[4,5,24,384]{3,2,1,0:T(8,128)(2,1)S(1)} %collective-permute-done.15.refs_10_) | copy-start | bytes 1105924
  117.9 0.7 copy-start.14
  117.9 0.9 copy-start.9
  117.9 1.0 copy-start.10
  118.0 1.2 copy-start.11
  122.7 10.0 %collective-permute-start.20 = (bf16[5,24,384]{2,1,0:T(8,128)(2,1)}, bf16[5,24,384]{2,1,0:T(8,128)(2,1)S(1)}, u32[]{:S(2)}, u32[]{:S(2)}) collective-permute-start(bf16[5,24,384]{2,1,0:T(8,128)(2,1)} %get-tuple-element.67), channel_id=1, source_target_pairs={{0,4},{4,8},{8,12},{12,0},{1,5},{5,9},{9,13},{13,1},{2,6},{6,10},{... | collective-permute-start | bytes 276488 | tf_op jit(solution)/shard_map/ppermute | solution.py:37
  124.0 12.7 %collective-permute-start.17 = (bf16[10,24,384]{2,1,0:T(8,128)(2,1)}, bf16[10,24,384]{2,1,0:T(8,128)(2,1)S(1)}, u32[]{:S(2)}, u32[]{:S(2)}) collective-permute-start(bf16[10,24,384]{2,1,0:T(8,128)(2,1)} %get-tuple-element.63), channel_id=1, source_target_pairs={{0,32},{32,64},{64,96},{96,0},{1,33},{33,65},{65,97},{97,1},{2,34}... | collective-permute-start | bytes 552968 | tf_op jit(solution)/shard_map/ppermute | solution.py:37
  125.3 11.4 %collective-permute-start.18 = (bf16[10,24,384]{2,1,0:T(8,128)(2,1)}, bf16[10,24,384]{2,1,0:T(8,128)(2,1)S(1)}, u32[]{:S(2)}, u32[]{:S(2)}) collective-permute-start(bf16[10,24,384]{2,1,0:T(8,128)(2,1)} %get-tuple-element.64), channel_id=1, source_target_pairs={{0,64},{32,96},{64,0},{96,32},{1,65},{33,97},{65,1},{97,33},{2,66}... | collective-permute-start | bytes 552968 | tf_op jit(solution)/shard_map/ppermute | solution.py:37
  127.3 9.5 %collective-permute-start.19 = (bf16[10,24,384]{2,1,0:T(8,128)(2,1)}, bf16[10,24,384]{2,1,0:T(8,128)(2,1)S(1)}, u32[]{:S(2)}, u32[]{:S(2)}) collective-permute-start(bf16[10,24,384]{2,1,0:T(8,128)(2,1)} %get-tuple-element.65), channel_id=1, source_target_pairs={{0,96},{32,0},{64,32},{96,64},{1,97},{33,1},{65,33},{97,65},{2,98}... | collective-permute-start | bytes 552968 | tf_op jit(solution)/shard_map/ppermute | solution.py:37
  128.7 6.1 %collective-permute-start.21 = (bf16[5,24,384]{2,1,0:T(8,128)(2,1)}, bf16[5,24,384]{2,1,0:T(8,128)(2,1)S(1)}, u32[]{:S(2)}, u32[]{:S(2)}) collective-permute-start(bf16[5,24,384]{2,1,0:T(8,128)(2,1)} %get-tuple-element.68), channel_id=1, source_target_pairs={{0,8},{4,12},{8,0},{12,4},{1,9},{5,13},{9,1},{13,5},{2,10},{6,14},... | collective-permute-start | bytes 276488 | tf_op jit(solution)/shard_map/ppermute | solution.py:37
  132.7 4.1 %copy-start.22 = (bf16[5,24,384]{2,1,0:T(8,128)(2,1)}, bf16[5,24,384]{2,1,0:T(8,128)(2,1)S(1)}, u32[]{:S(2)}) copy-start(bf16[5,24,384]{2,1,0:T(8,128)(2,1)S(1)} %collective-permute-done.20.refs_5_) | copy-start | bytes 276484
  132.7 4.0 %collective-permute-start.22 = (bf16[5,24,384]{2,1,0:T(8,128)(2,1)}, bf16[5,24,384]{2,1,0:T(8,128)(2,1)S(1)}, u32[]{:S(2)}, u32[]{:S(2)}) collective-permute-start(bf16[5,24,384]{2,1,0:T(8,128)(2,1)} %get-tuple-element.69), channel_id=1, source_target_pairs={{0,12},{4,0},{8,4},{12,8},{1,13},{5,1},{9,5},{13,9},{2,14},{6,2},{... | collective-permute-start | bytes 276488 | tf_op jit(solution)/shard_map/ppermute | solution.py:37
  134.9 1.9 %copy-start.23 = (bf16[5,24,384]{2,1,0:T(8,128)(2,1)}, bf16[5,24,384]{2,1,0:T(8,128)(2,1)S(1)}, u32[]{:S(2)}) copy-start(bf16[5,24,384]{2,1,0:T(8,128)(2,1)S(1)} %collective-permute-done.21.refs_6_) | copy-start | bytes 276484
  136.8 0.6 copy-start.24
  136.8 0.8 copy-start.18
  136.8 0.8 copy-start.19
  136.8 0.8 copy-start.20
  139.9 6.6 %collective-permute-start.23 = (bf16[8,24,384]{2,1,0:T(8,128)(2,1)}, bf16[8,24,384]{2,1,0:T(8,128)(2,1)S(1)}, u32[]{:S(2)}, u32[]{:S(2)}) collective-permute-start(bf16[8,24,384]{2,1,0:T(8,128)(2,1)} %get-tuple-element.71), channel_id=1, source_target_pairs={{0,16},{16,0},{1,17},{17,1},{2,18},{18,2},{3,19},{19,3},{4,20},{20... | collective-permute-start | bytes 442376 | tf_op jit(solution)/shard_map/ppermute | solution.py:33
  146.5 0.7 copy-start.21

commit v4 on v3

--- a/solution.py
+++ b/solution.py
@@ -17,7 +17,6 @@
 ROWS, COLS = 24, 384
 VMEM = pl.BlockSpec(memory_space=pltpu.VMEM)
 SMEM = pl.BlockSpec(memory_space=pltpu.SMEM)
-HBM = pl.BlockSpec(memory_space=pl.ANY)
 BF16, F32 = jnp.bfloat16, jnp.float32
 
 
@@ -52,16 +51,27 @@
     )
 
 
-def call(body, name, in_specs, outs, scratch=()):
-    return pl.pallas_call(
+def call(body, name, in_specs, outs, scratch=(), final=False):
+    kernel = pl.pallas_call(
         body,
-        out_shape=[jax.ShapeDtypeStruct(*out) for out in outs],
+        out_shape=[(jax.ShapeDtypeStruct if final else pltpu.VMEM)(*out) for out in outs],
         in_specs=in_specs,
         out_specs=[VMEM] * len(outs),
         scratch_shapes=list(scratch),
-        compiler_params=pltpu.CompilerParams(vmem_limit_bytes=56 << 20),
+        compiler_params=pltpu.CompilerParams(vmem_limit_bytes=24 << 20),
+        cost_estimate=pl.CostEstimate(flops=1 << 20, bytes_accessed=1 << 20, transcendentals=0),
         name=name,
     )
+
+    def run(*operands):
+        return kernel(
+            *(
+                pltpu.with_memory_space_constraint(operand, pltpu.VMEM) if spec is VMEM else operand
+                for operand, spec in zip(operands, in_specs)
+            )
+        )
+
+    return run
 
 
 def by_unit(raw_ref, core, out_ref):
@@ -98,57 +108,28 @@
 
 def slopes_kernel(
     place_ref, act_ref, act_slope_ref, slope_ref, live_ref, target_ref, first_slope_ref,
-    onehot_ref, w_own_hbm, hi_hbm, hi_again_hbm, lo_hbm, lo_again_hbm, w_middle_hbm, belief_hbm,
+    onehot_ref, w_own_ref, hi_ref, hi_again_ref, lo_ref, lo_again_ref, w_middle_ref, belief_ref,
     slope_middle_ref, slope_first_ref, sent_ref,
-    w_own, w_hi, w_lo, w_middle, belief, sems,
 ):
-    core = place_ref[0]
-    copies = [
-        pltpu.make_async_copy(source, target, sems.at[i])
-        for i, (source, target) in enumerate(
-            ((w_own_hbm, w_own), (w_middle_hbm, w_middle), (belief_hbm, belief))
-        )
-    ]
-    fetched = [
-        pltpu.make_async_copy(source, target, sems.at[sem])
-        for source, target, sem in (
-            (hi_hbm, w_hi, 3), (lo_again_hbm, w_lo, 4), (hi_again_hbm, w_hi, 3), (lo_hbm, w_lo, 4),
-        )
-    ]
-    copies[0].start()
-
-    @pl.when(core == 0)
-    def _():
-        fetched[0].start()
-        fetched[1].start()
-
-    @pl.when(core != 0)
-    def _():
-        fetched[2].start()
-        fetched[3].start()
-
-    copies[1].start()
-    copies[2].start()
+    is_first = place_ref[0] == 0
     act = act_ref[...]
     live = live_ref[...]
-    copies[0].wait()
-    back = contract(slope_ref[...], w_own[...], 0, 0)
-    for part, start, weights in ((0, 0, w_hi), (1, CUT, w_lo)):
-        fetched[part].wait()
+    back = contract(slope_ref[...], w_own_ref[...], 0, 0)
+    w_hi = jnp.where(is_first, hi_ref[...], hi_again_ref[...])
+    w_lo = jnp.where(is_first, lo_again_ref[...], lo_ref[...])
+    for start, weights in ((0, w_hi), (CUT, w_lo)):
         stop = start + weights.shape[0]
-        mismatch = contract(weights[...], act, 1, 1) - wide(target_ref[start:stop, :])
+        mismatch = contract(weights, act, 1, 1) - wide(target_ref[start:stop, :])
         slope = narrow(jnp.clip(mismatch, -1.0, 1.0) * live)
-        back += contract(slope, weights[...], 0, 0)
+        back += contract(slope, weights, 0, 0)
     slope_middle = narrow(back * act_slope_ref[...])
     slope_middle_ref[...] = slope_middle
-    copies[1].wait()
-    slope_first = narrow(contract(w_middle[...], slope_middle, 1, 1) * first_slope_ref[...])
+    slope_first = narrow(contract(w_middle_ref[...], slope_middle, 1, 1) * first_slope_ref[...])
     slope_first = narrow(dot(onehot_ref[...], slope_first))
     slope_first_ref[...] = slope_first
-    copies[2].wait()
     half = slope_first.shape[0] // 2
-    for start, stop in column_cuts(belief.shape[0]):
-        raw = narrow(contract(slope_first[:half], belief[start:stop, :], 1, 1))
+    for start, stop in column_cuts(belief_ref.shape[0]):
+        raw = narrow(contract(slope_first[:half], belief_ref[start:stop, :], 1, 1))
         put_columns(raw, start // COLS, sent_ref)
 
 
@@ -193,12 +174,11 @@
     for y, out_ref in zip(others(place_ref[1]), y_refs):
         for x in range(4):
             unit = 4 * y + x
-            out_ref[x] = narrow(raw_ref[unit, 0:5] + wide(arrived_ref[unit, 0:5]))
+            out_ref[x] = narrow(raw_ref[unit] + wide(arrived_ref[unit]))
     for x, out_ref in zip(others(place_ref[2]), x_refs):
         for y in range(4):
             unit = 4 * y + x
-            out_ref[y, 0:4] = narrow(wide(middle_ref[unit]) + wide(middle_arrived_ref[unit]))
-            out_ref[y, 4:6] = narrow(raw_ref[unit, 5:7] + wide(arrived_ref[unit, 5:7]))
+            out_ref[y] = narrow(wide(middle_ref[unit]) + wide(middle_arrived_ref[unit]))
 
 
 def sum_of(refs, index):
@@ -210,7 +190,7 @@
     a_refs, b_refs = refs[12:16], refs[16:20]
     for y, out_ref in zip(others(place_ref[1]), a_refs):
         out_ref[0:4] = narrow(sum_of(last_refs, y))
-        out_ref[4:10] = narrow(sum_of(x_refs, y))
+        out_ref[4:8] = narrow(sum_of(x_refs, y))
     for x, out_ref in zip(others(place_ref[2]), b_refs):
         out_ref[...] = narrow(sum_of(y_refs, x))
 
@@ -227,7 +207,7 @@
         out_ref[2:4] = sum_a[pl.ds(4 + 2 * side, 2)].astype(kind)
         halves = []
         for granule in range(7):
-            rows = sum_b[granule] if granule < 5 else sum_a[granule + 3]
+            rows = sum_b[granule]
             halves.append(jnp.where(side == 0, rows[0:12], rows[12:24]))
         halves.append(jnp.zeros_like(halves[0]))
         for pair in range(4):
@@ -267,13 +247,14 @@
     around = (ZH, CORE, "mp")
     hi = lax.ppermute(w_last_t[:CUT], around, [(0, 5), (5, 0), (1, 4), (4, 1)])
     lo = lax.ppermute(w_last_t[CUT:], around, [(2, 3), (3, 2), (6, 7), (7, 6)])
-    hi_again = lax.ppermute(hi, CORE, [(0, 1)])
-    lo_again = lax.ppermute(lo, CORE, [(1, 0)])
 
     pre_first = dot(belief, w_first)
     act_first = narrow(jax.nn.silu(pre_first))
     partial_middle = dot(act_first, w_middle)
     arrived = swap(narrow(partial_middle), "mp")
+    hi, lo, arrived = lax.optimization_barrier((hi, lo, arrived))
+    hi_again = lax.ppermute(hi, CORE, [(0, 1)])
+    lo_again = lax.ppermute(lo, CORE, [(1, 0)])
 
     live_rows = (counts[:, None] > jnp.arange(BLOCK, dtype=jnp.int32)[None, :]).reshape(1, total_rows)
     live = live_rows.astype(F32)
@@ -302,16 +283,8 @@
     slope_middle, slope_first, first_sent = call(
         slopes_kernel,
         "slopes",
-        [SMEM] + [VMEM] * 7 + [HBM] * 7,
+        [SMEM] + [VMEM] * 14,
         [((total_rows, hidden), BF16), ((units, total_rows), BF16), granules(16, 7)],
-        [
-            pltpu.VMEM((width, hidden), BF16),
-            pltpu.VMEM((CUT, hidden), BF16),
-            pltpu.VMEM((width - CUT, hidden), BF16),
-            pltpu.VMEM((units, hidden), BF16),
-            pltpu.VMEM((inputs, total_rows), BF16),
-            pltpu.SemaphoreType.DMA((5,)),
-        ],
     )(
         place, act, act_slope, slope_own, live, target_other, silu_slope(pre_first).T, onehot,
         w_last_t, hi, hi_again, lo, lo_again, w_middle, belief_t,
@@ -336,7 +309,7 @@
         first_cut_kernel,
         "first_cut",
         [SMEM] + [VMEM] * 5,
-        [granules(4, 6)] * 4 + [granules(4, 5)] * 4,
+        [granules(4, 4)] * 4 + [granules(4, 7)] * 4,
         [pltpu.VMEM((16, 7, ROWS, COLS), F32)],
     )(place, slope_first, belief_t, first_arrived, middle_own, middle_arrived)
     x_parts = [parts[0]] + [rotate(parts[k], X, k) for k in (1, 2, 3)]
@@ -346,7 +319,7 @@
         second_cut_kernel,
         "second_cut",
         [SMEM] + [VMEM] * 12,
-        [granules(10)] * 4 + [granules(5)] * 4,
+        [granules(8)] * 4 + [granules(7)] * 4,
     )(place, *last_parts, *x_parts, *y_parts)
     a_parts = [parts[0]] + [rotate(parts[k], Y, k) for k in (1, 2, 3)]
     b_parts = [parts[4]] + [rotate(parts[4 + k], X, k) for k in (1, 2, 3)]
@@ -356,7 +329,7 @@
         "third_cut",
         [SMEM] + [VMEM] * 8,
         [granules(8), ((8, ROWS, COLS), F32)],
-        [pltpu.VMEM((10, ROWS, COLS), F32), pltpu.VMEM((5, ROWS, COLS), F32)],
+        [pltpu.VMEM((8, ROWS, COLS), F32), pltpu.VMEM((7, ROWS, COLS), F32)],
     )(place, *a_parts, *b_parts)
 
     total, squares = call(
@@ -368,6 +341,7 @@
         "scale",
         [VMEM] * 2,
         [((units // 64, inputs), F32), ((ROWS, units), F32), ((ROWS, width), F32)],
+        final=True,
     )(total, squares)
     return grad_first.T, grad_middle.T, grad_last
 

time: 173 us -> 148 us (0.86)
  Pallas kernels: 41.9 us -> 19.3 us
  waiting for transfers between devices: 41.9 us -> 52.5 us
  starting transfers between devices: 44.8 us -> 37.6 us
  local copies, waits for them, and re-layouts: 11.3 us -> 7.94 us
  other arithmetic: 3.79 us -> 1.97 us
    pallas_call x9, Pallas kernels: 41.9 us -> 19.3 us  [run(): kernel(*(pltpu.with_memory_space_constraint(operand, pltpu.VMEM) if spec...]
    ppermute x1, waiting for transfers between devices: 9.95 us -> 21.9 us  [per_device(): lo = lax.ppermute(w_last_t[CUT:], around, [(2, 3), (3, 2), (6, 7), (7, 6)])]
    ppermute x1, starting transfers between devices: 9.64 us -> 5.01 us  [per_device(): lo_again = lax.ppermute(lo, CORE, [(1, 0)])]
    unnamed x58 -> x28, local copies, waits for them, and re-layouts: 6.4 us -> 1.83 us
    ppermute x15, waiting for transfers between devices: 27.9 us -> 24.8 us  [rotate(): return lax.ppermute(shard, axis, [(i, (i + step) % 4) for i in range(4)])]
    dot_general x1, local copies, waits for them, and re-layouts: 0.26 us -> 2.29 us  [dot(): return jnp.dot(left, right, preferred_element_type=F32)]
    ppermute x15, starting transfers between devices: 22.5 us -> 20.5 us  [rotate(): return lax.ppermute(shard, axis, [(i, (i + step) % 4) for i in range(4)])]
    slice x1, local copies, waits for them, and re-layouts: 1.9 us -> 0.04 us  [per_device(): lo = lax.ppermute(w_last_t[CUT:], around, [(2, 3), (3, 2), (6, 7), (7, 6)])]
  transfers between devices with their start and end apart: 24 -> 24, of which waited for: 9 -> 12; matrix products, arithmetic and copies ran while one was open for 8% -> 9% of each run, Pallas kernels for 11% -> 6%
where the time goes in v4:
time: 148 us
  waiting for transfers between devices  52.5 us (35%)
  starting transfers between devices  37.6 us (25%)
  blocking collectives  21.1 us (14%)
  Pallas kernels  19.3 us (13%)
  local copies, waits for them, and re-layouts  7.94 us (5%)
  matrix products  6.36 us (4%)
  other arithmetic  1.97 us (1%)
    ppermute x15, waiting for transfers between devices, rotate(): return lax.ppermute(shard, axis, [(i, (i + step) % 4) for i in range(4)])  24.8 us
    ppermute x1, waiting for transfers between devices, per_device(): lo = lax.ppermute(w_last_t[CUT:], around, [(2, 3), (3, 2), (6, 7), (7, 6)])  21.9 us
    all_to_all x1, blocking collectives, per_device(): squares = lax.all_to_all(squares, ALL, 0, 0, tiled=True)  21.1 us
    ppermute x15, starting transfers between devices, rotate(): return lax.ppermute(shard, axis, [(i, (i + step) % 4) for i in range(4)])  20.5 us
    pallas_call x9, Pallas kernels, run(): kernel(*(pltpu.with_memory_space_constraint(operand, pltpu.VMEM) if spec...  19.3 us
    ppermute x5, starting transfers between devices, swap(): return lax.ppermute(shard, axis, [(0, 1), (1, 0)])  6.91 us
    dot_general x2, matrix products, dot(): return jnp.dot(left, right, preferred_element_type=F32)  6.36 us
    ppermute x5, waiting for transfers between devices, swap(): return lax.ppermute(shard, axis, [(0, 1), (1, 0)])  5.85 us
  transfers between devices with their start and end apart: 24, of which 12 were waited for; matrix products, arithmetic and copies ran while one was open for 9% of the time, Pallas kernels for 6%

profile of v4, /device:TPU:1, one launch (start us, length us, event | category | flops | bytes accessed | tf_op | source)
XLA Modules:
  0.0 147.7 jit_solution(4126754375889489815)
XLA Ops:
  0.6 1.6 %slice.8 = bf16[480,1536]{1,0:T(8,128)(2,1)S(1)} slice(bf16[663,1536]{1,0:T(8,128)(2,1)} %bitcast.32), slice={[0:480], [0:1536]} | slice | bytes 2949120 | tf_op jit(solution)/shard_map/slice | solution.py:248
  2.2 0.0 copy-start.1
  2.2 1.9 %collective-permute-start = (bf16[480,1536]{1,0:T(8,128)(2,1)S(1)}, bf16[480,1536]{1,0:T(8,128)(2,1)}, u32[]{:S(2)}, u32[]{:S(2)}) collective-permute-start(bf16[480,1536]{1,0:T(8,128)(2,1)S(1)} %slice.8), channel_id=1, source_target_pairs={{0,17},{17,0},{1,16},{16,1},{4,21},{21,4},{5,20},{20,5},{8,25},{25... | collective-permute-start | bytes 4423688 | tf_op jit(solution)/shard_map/ppermute | solution.py:248
  4.2 4.4 %multiply_convert_fusion = (bf16[256,768]{1,0:T(8,128)(2,1)S(1)}, f32[256,768]{1,0:T(8,128)}) fusion(bf16[256,2652]{0,1:T(8,128)(2,1)S(1)} %copy-done.4, bf16[2652,768]{1,0:T(8,128)(2,1)} %param.9), kind=kOutput, calls=%fused_computation.9 | convolution fusion | flops 1043791872 | bytes 6610944 | tf_op jit(solution)/shard_map/dot_general | solution.py:45
  8.6 2.0 %fusion.6 = (bf16[256,1536]{1,0:T(8,128)(2,1)S(1)}, f32[256,1536]{1,0:T(8,128)}) fusion(bf16[256,768]{1,0:T(8,128)(2,1)S(1)} %get-tuple-element.85.act_first_ref, bf16[768,1536]{1,0:T(8,128)(2,1)S(1)} %copy-done.1), kind=kOutput, calls=%fused_computation.16 | convolution fusion | flops 604372992 | bytes 5111808 | tf_op jit(solution)/shard_map/dot_general | solution.py:45
  10.5 2.5 %collective-permute-start.2 = (bf16[256,1536]{1,0:T(8,128)(2,1)S(1)}, bf16[256,1536]{1,0:T(8,128)(2,1)S(1)}, u32[]{:S(2)}, u32[]{:S(2)}) collective-permute-start(bf16[256,1536]{1,0:T(8,128)(2,1)S(1)} %get-tuple-element.87), channel_id=1, source_target_pairs={{0,1},{1,0},{2,3},{3,2},{4,5},{5,4},{6,7},{7,6},{8,9},{9,8},{10,11... | collective-permute-start | bytes 2359304 | tf_op jit(solution)/shard_map/ppermute | solution.py:32
  13.1 1.9 %collective-permute-start.1 = (bf16[183,1536]{1,0:T(8,128)(2,1)S(1)}, bf16[183,1536]{1,0:T(8,128)(2,1)S(1)}, u32[]{:S(2)}, u32[]{:S(2)}) collective-permute-start(bf16[183,1536]{1,0:T(8,128)(2,1)S(1)} %slice.9), channel_id=1, source_target_pairs={{2,3},{3,2},{18,19},{19,18},{6,7},{7,6},{22,23},{23,22},{10,11},{1... | collective-permute-start | bytes 1686536 | tf_op jit(solution)/shard_map/ppermute | solution.py:249
  15.0 21.9 %collective-permute-done.1.lo_ref = bf16[183,1536]{1,0:T(8,128)(2,1)S(1)} collective-permute-done((bf16[183,1536]{1,0:T(8,128)(2,1)S(1)}, bf16[183,1536]{1,0:T(8,128)(2,1)S(1)}, u32[]{:S(2)}, u32[]{:S(2)}) %collective-permute-start.1) | collective-permute-done | bytes 562208 | tf_op jit(solution)/shard_map/ppermute | solution.py:249
  36.9 0.0 collective-permute-done.2.arrived_ref
  36.9 0.8 copy-done.11
  37.7 0.9 copy-done.9
  38.6 1.3 collective-permute-start.7
  39.9 2.1 %dynamic-slice_bitcast_fusion = (bf16[663,256]{1,0:T(8,128)(2,1)}, bf16[663,256]{1,0:T(8,128)(2,1)}) fusion(bf16[256,1326]{0,1:T(8,128)(2,1)} %param.7, s32[]{:T(128)S(6)} %select_n.15, s32[]{:T(128)S(6)} %select_n.14), kind=kLoop, calls=%fused_computation.10 | loop fusion | bytes 1357832 | tf_op jit(solution)/shard_map/dynamic_slice | solution.py:262
  42.0 0.1 compare_convert_fusion
  42.1 5.0 %collective-permute-start.8 = (bf16[183,1536]{1,0:T(8,128)(2,1)}, bf16[183,1536]{1,0:T(8,128)(2,1)}, u32[]{:S(2)}, u32[]{:S(2)}) collective-permute-start(bf16[183,1536]{1,0:T(8,128)(2,1)} %copy-done.11), channel_id=1, source_target_pairs={{2,0},{3,1},{6,4},{7,5},{10,8},{11,9},{14,12},{15,13},{18,16},{19,... | collective-permute-start | bytes 1686536 | tf_op jit(solution)/shard_map/ppermute | solution.py:257
  47.1 0.1 pad_add_fusion.place_ref
  47.2 2.3 %copy.9 = f32[256,768]{0,1:T(8,128)} copy(f32[256,768]{1,0:T(8,128)} %get-tuple-element.86) | data formatting | bytes 1572864 | tf_op jit(solution)/shard_map/dot_general | solution.py:45
  49.5 0.1 eq.19
  49.6 0.3 fusion.onehot_ref
  49.9 1.5 %fusion.5.first_slope_ref = f32[768,256]{1,0:T(8,128)S(1)} fusion(f32[256,768]{0,1:T(8,128)} %copy.9), kind=kLoop, calls=%fused_computation.8 | loop fusion | flops 1376256 | bytes 1572864 | tf_op jit(solution)/shard_map/mul | solution.py:41
  51.4 0.1 copy-done.10
  51.5 3.3 %last.1 = (bf16[256,1536]{1,0:T(8,128)(2,1)S(1)}, f32[256,1536]{1,0:T(8,128)S(1)}, bf16[663,256]{1,0:T(8,128)(2,1)S(1)}, bf16[16,4,24,384]{3,2,1,0:T(8,128)(2,1)S(1)}, bf16[16,4,24,384]{3,2,1,0:T(8,128)(2,1)S(1)}) custom-call(s32[4]{0:T(128)S(1)} %pad_add_fusion.place_ref, f32[256,1536]{1,0:T(8,128)S(1)} %copy-done.3, bf16[256,1536]{1,0:T(8,128)(2,1)S(1)} %copy-done.10, ...), custom_call_target="tpu_custom_call" | custom-call | flops 1048576 | bytes 1048576 | tf_op jit(solution)/shard_map/last/pallas_call | solution.py:67
  54.8 0.0 collective-permute-done.7.hi_again_ref
  54.9 8.1 %slopes.1 = (bf16[256,1536]{1,0:T(8,128)(2,1)S(1)}, bf16[768,256]{1,0:T(8,128)(2,1)S(1)}, bf16[16,7,24,384]{3,2,1,0:T(8,128)(2,1)S(1)}) custom-call(s32[4]{0:T(128)S(1)} %pad_add_fusion.place_ref, bf16[256,1536]{1,0:T(8,128)(2,1)S(1)} %get-tuple-element.50.act_ref, f32[256,1536]{1,0:T(8,128)S(1)} %get-tuple-element.51.act_slope_ref, ...), custom_call_target="tpu_custom_call" | custom-call | flops 1048576 | bytes 1048576 | tf_op jit(solution)/shard_map/slopes/pallas_call | solution.py:67
  63.0 0.1 collective-permute-start.9
  63.1 0.5 collective-permute-start.3
  63.6 1.6 %middle.1 = (bf16[16,4,24,384]{3,2,1,0:T(8,128)(2,1)S(1)}, bf16[16,4,24,384]{3,2,1,0:T(8,128)(2,1)S(1)}) custom-call(s32[4]{0:T(128)S(1)} %pad_add_fusion.place_ref, bf16[256,1536]{1,0:T(8,128)(2,1)S(1)} %get-tuple-element.57.slope_middle_ref, bf16[256,768]{1,0:T(8,128)(2,1)S(1)} %copy-done.6), custom_call_target="tpu_custom_call" | custom-call | flops 1048576 | bytes 1048576 | tf_op jit(solution)/shard_map/middle/pallas_call | solution.py:67
  65.2 0.4 collective-permute-start.10
  65.6 3.3 %collective-permute-done.3.arrived_ref = bf16[16,4,24,384]{3,2,1,0:T(8,128)(2,1)S(1)} collective-permute-done((bf16[16,4,24,384]{3,2,1,0:T(8,128)(2,1)S(1)}, bf16[16,4,24,384]{3,2,1,0:T(8,128)(2,1)S(1)}, u32[]{:S(2)}, u32[]{:S(2)}) %collective-permute-start.3) | collective-permute-done | bytes 1179680 | tf_op jit(solution)/shard_map/ppermute | solution.py:32
  68.9 0.8 last_cut.1
  69.7 1.3 collective-permute-start.4
  71.0 2.5 %collective-permute-start.5 = (bf16[4,4,24,384]{3,2,1,0:T(8,128)(2,1)S(1)}, bf16[4,4,24,384]{3,2,1,0:T(8,128)(2,1)S(1)}, u32[]{:S(2)}, u32[]{:S(2)}) collective-permute-start(bf16[4,4,24,384]{3,2,1,0:T(8,128)(2,1)S(1)} %get-tuple-element.48), channel_id=1, source_target_pairs={{0,8},{4,12},{8,0},{12,4},{1,9},{5,13},{9,1},{13,5},{2,10},{6,14},... | collective-permute-start | bytes 884744 | tf_op jit(solution)/shard_map/ppermute | solution.py:36
  73.4 1.2 collective-permute-start.6
  74.6 0.0 collective-permute-done.10.middle_arrived_ref
  74.6 0.0 collective-permute-done.9.arrived_ref
  74.6 2.5 %first_cut.1 = (bf16[4,4,24,384]{3,2,1,0:T(8,128)(2,1)S(1)}, bf16[4,4,24,384]{3,2,1,0:T(8,128)(2,1)S(1)}, bf16[4,4,24,384]{3,2,1,0:T(8,128)(2,1)S(1)}, bf16[4,4,...) custom-call(s32[4]{0:T(128)S(1)} %pad_add_fusion.place_ref, ...), custom_call_target="tpu_custom_call" | custom-call | flops 1048576 | bytes 1048576 | tf_op jit(solution)/shard_map/first_cut/pallas_call | solution.py:67
  77.1 0.4 collective-permute-start.11
  77.5 1.3 collective-permute-start.14
  78.8 0.7 collective-permute-done.4.refs_1_
  79.5 2.9 %collective-permute-start.15 = (bf16[4,7,24,384]{3,2,1,0:T(8,128)(2,1)S(1)}, bf16[4,7,24,384]{3,2,1,0:T(8,128)(2,1)S(1)}, u32[]{:S(2)}, u32[]{:S(2)}) collective-permute-start(bf16[4,7,24,384]{3,2,1,0:T(8,128)(2,1)S(1)} %get-tuple-element.66), channel_id=1, source_target_pairs={{0,64},{32,96},{64,0},{96,32},{1,65},{33,97},{65,1},{97,33},{2,66}... | collective-permute-start | bytes 1548296 | tf_op jit(solution)/shard_map/ppermute | solution.py:36
  82.4 4.4 %collective-permute-done.5.refs_2_ = bf16[4,4,24,384]{3,2,1,0:T(8,128)(2,1)S(1)} collective-permute-done((bf16[4,4,24,384]{3,2,1,0:T(8,128)(2,1)S(1)}, bf16[4,4,24,384]{3,2,1,0:T(8,128)(2,1)S(1)}, u32[]{:S(2)}, u32[]{:S(2)}) %collective-permute-start.5) | collective-permute-done | bytes 294944 | tf_op jit(solution)/shard_map/ppermute | solution.py:36
  86.8 2.7 %collective-permute-start.16 = (bf16[4,7,24,384]{3,2,1,0:T(8,128)(2,1)S(1)}, bf16[4,7,24,384]{3,2,1,0:T(8,128)(2,1)S(1)}, u32[]{:S(2)}, u32[]{:S(2)}) collective-permute-start(bf16[4,7,24,384]{3,2,1,0:T(8,128)(2,1)S(1)} %get-tuple-element.67), channel_id=1, source_target_pairs={{0,96},{32,0},{64,32},{96,64},{1,97},{33,1},{65,33},{97,65},{2,98}... | collective-permute-start | bytes 1548296 | tf_op jit(solution)/shard_map/ppermute | solution.py:36
  89.5 0.0 collective-permute-done.6.refs_3_
  89.6 0.5 collective-permute-start.12
  90.1 3.0 %collective-permute-done.11.refs_5_ = bf16[4,4,24,384]{3,2,1,0:T(8,128)(2,1)S(1)} collective-permute-done((bf16[4,4,24,384]{3,2,1,0:T(8,128)(2,1)S(1)}, bf16[4,4,24,384]{3,2,1,0:T(8,128)(2,1)S(1)}, u32[]{:S(2)}, u32[]{:S(2)}) %collective-permute-start.11) | collective-permute-done | bytes 294944 | tf_op jit(solution)/shard_map/ppermute | solution.py:36
  93.1 0.4 collective-permute-start.13
  93.4 4.4 %collective-permute-done.12.refs_6_ = bf16[4,4,24,384]{3,2,1,0:T(8,128)(2,1)S(1)} collective-permute-done((bf16[4,4,24,384]{3,2,1,0:T(8,128)(2,1)S(1)}, bf16[4,4,24,384]{3,2,1,0:T(8,128)(2,1)S(1)}, u32[]{:S(2)}, u32[]{:S(2)}) %collective-permute-start.12) | collective-permute-done | bytes 294944 | tf_op jit(solution)/shard_map/ppermute | solution.py:36
  97.8 5.0 %collective-permute-done.13.refs_7_ = bf16[4,4,24,384]{3,2,1,0:T(8,128)(2,1)S(1)} collective-permute-done((bf16[4,4,24,384]{3,2,1,0:T(8,128)(2,1)S(1)}, bf16[4,4,24,384]{3,2,1,0:T(8,128)(2,1)S(1)}, u32[]{:S(2)}, u32[]{:S(2)}) %collective-permute-start.13) | collective-permute-done | bytes 294944 | tf_op jit(solution)/shard_map/ppermute | solution.py:36
  102.7 0.2 collective-permute-done.15.refs_10_
  102.9 2.1 %collective-permute-done.16.refs_11_ = bf16[4,7,24,384]{3,2,1,0:T(8,128)(2,1)S(1)} collective-permute-done((bf16[4,7,24,384]{3,2,1,0:T(8,128)(2,1)S(1)}, bf16[4,7,24,384]{3,2,1,0:T(8,128)(2,1)S(1)}, u32[]{:S(2)}, u32[]{:S(2)}) %collective-permute-start.16) | collective-permute-done | bytes 516128 | tf_op jit(solution)/shard_map/ppermute | solution.py:36
  105.0 1.1 second_cut.1
  106.2 0.1 collective-permute-start.20
  106.2 2.0 %collective-permute-start.17 = (bf16[8,24,384]{2,1,0:T(8,128)(2,1)S(1)}, bf16[8,24,384]{2,1,0:T(8,128)(2,1)S(1)}, u32[]{:S(2)}, u32[]{:S(2)}) collective-permute-start(bf16[8,24,384]{2,1,0:T(8,128)(2,1)S(1)} %get-tuple-element.69), channel_id=1, source_target_pairs={{0,32},{32,64},{64,96},{96,0},{1,33},{33,65},{65,97},{97,1},{2,34}... | collective-permute-start | bytes 442376 | tf_op jit(solution)/shard_map/ppermute | solution.py:36
  108.3 2.6 %collective-permute-start.18 = (bf16[8,24,384]{2,1,0:T(8,128)(2,1)S(1)}, bf16[8,24,384]{2,1,0:T(8,128)(2,1)S(1)}, u32[]{:S(2)}, u32[]{:S(2)}) collective-permute-start(bf16[8,24,384]{2,1,0:T(8,128)(2,1)S(1)} %get-tuple-element.70), channel_id=1, source_target_pairs={{0,64},{32,96},{64,0},{96,32},{1,65},{33,97},{65,1},{97,33},{2,66}... | collective-permute-start | bytes 442376 | tf_op jit(solution)/shard_map/ppermute | solution.py:36
  110.9 2.6 %collective-permute-start.21 = (bf16[7,24,384]{2,1,0:T(8,128)(2,1)S(1)}, bf16[7,24,384]{2,1,0:T(8,128)(2,1)S(1)}, u32[]{:S(2)}, u32[]{:S(2)}) collective-permute-start(bf16[7,24,384]{2,1,0:T(8,128)(2,1)S(1)} %get-tuple-element.74), channel_id=1, source_target_pairs={{0,8},{4,12},{8,0},{12,4},{1,9},{5,13},{9,1},{13,5},{2,10},{6,14},... | collective-permute-start | bytes 387080 | tf_op jit(solution)/shard_map/ppermute | solution.py:36
  113.5 0.1 collective-permute-start.22
  113.6 2.9 %collective-permute-done.21.refs_6_ = bf16[7,24,384]{2,1,0:T(8,128)(2,1)S(1)} collective-permute-done((bf16[7,24,384]{2,1,0:T(8,128)(2,1)S(1)}, bf16[7,24,384]{2,1,0:T(8,128)(2,1)S(1)}, u32[]{:S(2)}, u32[]{:S(2)}) %collective-permute-start.21) | collective-permute-done | bytes 129056 | tf_op jit(solution)/shard_map/ppermute | solution.py:36
  116.5 2.1 %collective-permute-done.22.refs_7_ = bf16[7,24,384]{2,1,0:T(8,128)(2,1)S(1)} collective-permute-done((bf16[7,24,384]{2,1,0:T(8,128)(2,1)S(1)}, bf16[7,24,384]{2,1,0:T(8,128)(2,1)S(1)}, u32[]{:S(2)}, u32[]{:S(2)}) %collective-permute-start.22) | collective-permute-done | bytes 129056 | tf_op jit(solution)/shard_map/ppermute | solution.py:36
  118.6 0.8 third_cut.1
  119.4 3.5 %collective-permute-start.23 = (bf16[8,24,384]{2,1,0:T(8,128)(2,1)S(1)}, bf16[8,24,384]{2,1,0:T(8,128)(2,1)S(1)}, u32[]{:S(2)}, u32[]{:S(2)}) collective-permute-start(bf16[8,24,384]{2,1,0:T(8,128)(2,1)S(1)} %get-tuple-element.77), channel_id=1, source_target_pairs={{0,16},{16,0},{1,17},{17,1},{2,18},{18,2},{3,19},{19,3},{4,20},{20... | collective-permute-start | bytes 442376 | tf_op jit(solution)/shard_map/ppermute | solution.py:32
  122.9 2.5 %collective-permute-done.23.arrived_ref = bf16[8,24,384]{2,1,0:T(8,128)(2,1)S(1)} collective-permute-done((bf16[8,24,384]{2,1,0:T(8,128)(2,1)S(1)}, bf16[8,24,384]{2,1,0:T(8,128)(2,1)S(1)}, u32[]{:S(2)}, u32[]{:S(2)}) %collective-permute-start.23) | collective-permute-done | bytes 147488 | tf_op jit(solution)/shard_map/ppermute | solution.py:32
  125.5 0.3 square.1
  125.7 21.1 %all_to_all.5.squares_ref = f32[128,1,128]{2,1,0:T(1,128)S(1)} all-to-all(f32[128,1,128]{2,1,0:T(1,128)S(1)} %get-tuple-element.79), channel_id=1, replica_groups=mesh['dp_0'=4,'dp_1'=2,'dp_2'=4,'dp_3'=2,'mp'=2] {'dp_0','dp_1','dp_2','..., dimensions={0} | all-to-all | bytes 131072 | tf_op jit(solution)/shard_map/all_to_all | solution.py:338
  146.8 0.9 scale.1
  (35 shorter events, 0.1 us)
Async XLA Ops:
  0.6 3.5 %copy-start.4 = (bf16[256,2652]{0,1:T(8,128)(2,1)S(1)}, bf16[256,2652]{0,1:T(8,128)(2,1)}, u32[]{:S(2)}) copy-start(bf16[256,2652]{0,1:T(8,128)(2,1)} %param.6) | copy-start | bytes 4073476
  2.2 6.4 %copy-start.1 = (bf16[768,1536]{1,0:T(8,128)(2,1)S(1)}, bf16[768,1536]{1,0:T(8,128)(2,1)}, u32[]{:S(2)}) copy-start(bf16[768,1536]{1,0:T(8,128)(2,1)} %w_middle_ref.1) | copy-start | bytes 7077892
  2.2 36.3 %collective-permute-start = (bf16[480,1536]{1,0:T(8,128)(2,1)S(1)}, bf16[480,1536]{1,0:T(8,128)(2,1)}, u32[]{:S(2)}, u32[]{:S(2)}) collective-permute-start(bf16[480,1536]{1,0:T(8,128)(2,1)S(1)} %slice.8), channel_id=1, source_target_pairs={{0,17},{17,0},{1,16},{16,1},{4,21},{21,4},{5,20},{20,5},{8,25},{25... | collective-permute-start | bytes 4423688 | tf_op jit(solution)/shard_map/ppermute | solution.py:248
  8.6 2.0 %copy-start.5 = (bf16[256,768]{1,0:T(8,128)(2,1)}, bf16[256,768]{1,0:T(8,128)(2,1)S(1)}, u32[]{:S(2)}) copy-start(bf16[256,768]{1,0:T(8,128)(2,1)S(1)} %get-tuple-element.85.act_first_ref) | copy-start | bytes 1179652
  8.6 4.4 %copy-start = (bf16[1536,663]{0,1:T(8,128)(2,1)S(1)}, bf16[1536,663]{0,1:T(8,128)(2,1)}, u32[]{:S(2)}) copy-start(bf16[1536,663]{0,1:T(8,128)(2,1)} %param.11) | copy-start | bytes 6110212
  10.5 31.5 %copy-start.13 = (s32[2]{0:T(128)S(1)}, s32[2]{0:T(128)}, u32[]{:S(2)}) copy-start(s32[2]{0:T(128)} %param.8) | copy-start | bytes 28
  10.5 26.3 %collective-permute-start.2 = (bf16[256,1536]{1,0:T(8,128)(2,1)S(1)}, bf16[256,1536]{1,0:T(8,128)(2,1)S(1)}, u32[]{:S(2)}, u32[]{:S(2)}) collective-permute-start(bf16[256,1536]{1,0:T(8,128)(2,1)S(1)} %get-tuple-element.87), channel_id=1, source_target_pairs={{0,1},{1,0},{2,3},{3,2},{4,5},{5,4},{6,7},{7,6},{8,9},{9,8},{10,11... | collective-permute-start | bytes 2359304 | tf_op jit(solution)/shard_map/ppermute | solution.py:32
  13.1 23.8 %collective-permute-start.1 = (bf16[183,1536]{1,0:T(8,128)(2,1)S(1)}, bf16[183,1536]{1,0:T(8,128)(2,1)S(1)}, u32[]{:S(2)}, u32[]{:S(2)}) collective-permute-start(bf16[183,1536]{1,0:T(8,128)(2,1)S(1)} %slice.9), channel_id=1, source_target_pairs={{2,3},{3,2},{18,19},{19,18},{6,7},{7,6},{22,23},{23,22},{10,11},{1... | collective-permute-start | bytes 1686536 | tf_op jit(solution)/shard_map/ppermute | solution.py:249
  36.9 0.8 copy-start.11
  37.7 0.9 copy-start.9
  38.6 16.3 %collective-permute-start.7 = (bf16[480,1536]{1,0:T(8,128)(2,1)}, bf16[480,1536]{1,0:T(8,128)(2,1)}, u32[]{:S(2)}, u32[]{:S(2)}) collective-permute-start(bf16[480,1536]{1,0:T(8,128)(2,1)} %collective-permute-done.hi_ref), channel_id=1, source_target_pairs={{0,2},{1,3},{4,6},{5,7},{8,10},{9,11},{12,14},{13,15},{16,18},{17,... | collective-permute-start | bytes 4423688 | tf_op jit(solution)/shard_map/ppermute | solution.py:256
  42.1 12.7 %collective-permute-start.8 = (bf16[183,1536]{1,0:T(8,128)(2,1)}, bf16[183,1536]{1,0:T(8,128)(2,1)}, u32[]{:S(2)}, u32[]{:S(2)}) collective-permute-start(bf16[183,1536]{1,0:T(8,128)(2,1)} %copy-done.11), channel_id=1, source_target_pairs={{2,0},{3,1},{6,4},{7,5},{10,8},{11,9},{14,12},{15,13},{18,16},{19,... | collective-permute-start | bytes 1686536 | tf_op jit(solution)/shard_map/ppermute | solution.py:257
  49.6 1.8 %copy-start.3 = (f32[256,1536]{1,0:T(8,128)S(1)}, f32[256,1536]{1,0:T(8,128)}, u32[]{:S(2)}) copy-start(f32[256,1536]{1,0:T(8,128)} %get-tuple-element.88.partial_ref) | copy-start | bytes 4718596
  49.6 1.8 %copy-start.7 = (bf16[663,256]{1,0:T(8,128)(2,1)S(1)}, bf16[663,256]{1,0:T(8,128)(2,1)}, u32[]{:S(2)}) copy-start(bf16[663,256]{1,0:T(8,128)(2,1)} %get-tuple-element.84.target_ref) | copy-start | bytes 1018372
  49.6 1.9 %copy-start.10 = (bf16[256,1536]{1,0:T(8,128)(2,1)S(1)}, bf16[256,1536]{1,0:T(8,128)(2,1)}, u32[]{:S(2)}) copy-start(bf16[256,1536]{1,0:T(8,128)(2,1)} %copy-done.9) | copy-start | bytes 2359300
  51.5 3.3 %copy-start.2 = (bf16[768,1536]{1,0:T(8,128)(2,1)S(1)}, bf16[768,1536]{1,0:T(8,128)(2,1)}, u32[]{:S(2)}) copy-start(bf16[768,1536]{1,0:T(8,128)(2,1)} %w_middle_ref.1) | copy-start | bytes 7077892
  51.5 3.3 %copy-start.8 = (bf16[663,256]{1,0:T(8,128)(2,1)S(1)}, bf16[663,256]{1,0:T(8,128)(2,1)}, u32[]{:S(2)}) copy-start(bf16[663,256]{1,0:T(8,128)(2,1)} %get-tuple-element.83.target_ref) | copy-start | bytes 1018372
  51.5 3.3 %copy-start.12 = (bf16[183,1536]{1,0:T(8,128)(2,1)S(1)}, bf16[183,1536]{1,0:T(8,128)(2,1)}, u32[]{:S(2)}) copy-start(bf16[183,1536]{1,0:T(8,128)(2,1)} %copy-done.11) | copy-start | bytes 1686532
  54.9 8.7 %copy-start.6 = (bf16[256,768]{1,0:T(8,128)(2,1)S(1)}, bf16[256,768]{1,0:T(8,128)(2,1)}, u32[]{:S(2)}) copy-start(bf16[256,768]{1,0:T(8,128)(2,1)} %copy-done.5) | copy-start | bytes 1179652
  63.0 11.6 %collective-permute-start.9 = (bf16[16,7,24,384]{3,2,1,0:T(8,128)(2,1)S(1)}, bf16[16,7,24,384]{3,2,1,0:T(8,128)(2,1)S(1)}, u32[]{:S(2)}, u32[]{:S(2)}) collective-permute-start(bf16[16,7,24,384]{3,2,1,0:T(8,128)(2,1)S(1)} %get-tuple-element.56), channel_id=1, source_target_pairs={{0,2},{2,0},{1,3},{3,1},{4,6},{6,4},{5,7},{7,5},{8,10},{10,8},{9,1... | collective-permute-start | bytes 6193160 | tf_op jit(solution)/shard_map/ppermute | solution.py:32
  63.1 5.8 %collective-permute-start.3 = (bf16[16,4,24,384]{3,2,1,0:T(8,128)(2,1)S(1)}, bf16[16,4,24,384]{3,2,1,0:T(8,128)(2,1)S(1)}, u32[]{:S(2)}, u32[]{:S(2)}) collective-permute-start(bf16[16,4,24,384]{3,2,1,0:T(8,128)(2,1)S(1)} %get-tuple-element.45), channel_id=1, source_target_pairs={{0,2},{2,0},{1,3},{3,1},{4,6},{6,4},{5,7},{7,5},{8,10},{10,8},{9,1... | collective-permute-start | bytes 3538952 | tf_op jit(solution)/shard_map/ppermute | solution.py:32
  65.2 9.4 %collective-permute-start.10 = (bf16[16,4,24,384]{3,2,1,0:T(8,128)(2,1)S(1)}, bf16[16,4,24,384]{3,2,1,0:T(8,128)(2,1)S(1)}, u32[]{:S(2)}, u32[]{:S(2)}) collective-permute-start(bf16[16,4,24,384]{3,2,1,0:T(8,128)(2,1)S(1)} %get-tuple-element.59), channel_id=1, source_target_pairs={{0,2},{2,0},{1,3},{3,1},{4,6},{6,4},{5,7},{7,5},{8,10},{10,8},{9,1... | collective-permute-start | bytes 3538952 | tf_op jit(solution)/shard_map/ppermute | solution.py:32
  69.7 9.7 %collective-permute-start.4 = (bf16[4,4,24,384]{3,2,1,0:T(8,128)(2,1)S(1)}, bf16[4,4,24,384]{3,2,1,0:T(8,128)(2,1)S(1)}, u32[]{:S(2)}, u32[]{:S(2)}) collective-permute-start(bf16[4,4,24,384]{3,2,1,0:T(8,128)(2,1)S(1)} %get-tuple-element.47), channel_id=1, source_target_pairs={{0,4},{4,8},{8,12},{12,0},{1,5},{5,9},{9,13},{13,1},{2,6},{6,10},{... | collective-permute-start | bytes 884744 | tf_op jit(solution)/shard_map/ppermute | solution.py:36
  71.0 15.8 %collective-permute-start.5 = (bf16[4,4,24,384]{3,2,1,0:T(8,128)(2,1)S(1)}, bf16[4,4,24,384]{3,2,1,0:T(8,128)(2,1)S(1)}, u32[]{:S(2)}, u32[]{:S(2)}) collective-permute-start(bf16[4,4,24,384]{3,2,1,0:T(8,128)(2,1)S(1)} %get-tuple-element.48), channel_id=1, source_target_pairs={{0,8},{4,12},{8,0},{12,4},{1,9},{5,13},{9,1},{13,5},{2,10},{6,14},... | collective-permute-start | bytes 884744 | tf_op jit(solution)/shard_map/ppermute | solution.py:36
  73.4 16.1 %collective-permute-start.6 = (bf16[4,4,24,384]{3,2,1,0:T(8,128)(2,1)S(1)}, bf16[4,4,24,384]{3,2,1,0:T(8,128)(2,1)S(1)}, u32[]{:S(2)}, u32[]{:S(2)}) collective-permute-start(bf16[4,4,24,384]{3,2,1,0:T(8,128)(2,1)S(1)} %get-tuple-element.49), channel_id=1, source_target_pairs={{0,12},{4,0},{8,4},{12,8},{1,13},{5,1},{9,5},{13,9},{2,14},{6,2},{... | collective-permute-start | bytes 884744 | tf_op jit(solution)/shard_map/ppermute | solution.py:36
  77.1 16.0 %collective-permute-start.11 = (bf16[4,4,24,384]{3,2,1,0:T(8,128)(2,1)S(1)}, bf16[4,4,24,384]{3,2,1,0:T(8,128)(2,1)S(1)}, u32[]{:S(2)}, u32[]{:S(2)}) collective-permute-start(bf16[4,4,24,384]{3,2,1,0:T(8,128)(2,1)S(1)} %get-tuple-element.61), channel_id=1, source_target_pairs={{0,4},{4,8},{8,12},{12,0},{1,5},{5,9},{9,13},{13,1},{2,6},{6,10},{... | collective-permute-start | bytes 884744 | tf_op jit(solution)/shard_map/ppermute | solution.py:36
  77.5 25.3 %collective-permute-start.14 = (bf16[4,7,24,384]{3,2,1,0:T(8,128)(2,1)S(1)}, bf16[4,7,24,384]{3,2,1,0:T(8,128)(2,1)S(1)}, u32[]{:S(2)}, u32[]{:S(2)}) collective-permute-start(bf16[4,7,24,384]{3,2,1,0:T(8,128)(2,1)S(1)} %get-tuple-element.65), channel_id=1, source_target_pairs={{0,32},{32,64},{64,96},{96,0},{1,33},{33,65},{65,97},{97,1},{2,34}... | collective-permute-start | bytes 1548296 | tf_op jit(solution)/shard_map/ppermute | solution.py:36
  79.5 23.5 %collective-permute-start.15 = (bf16[4,7,24,384]{3,2,1,0:T(8,128)(2,1)S(1)}, bf16[4,7,24,384]{3,2,1,0:T(8,128)(2,1)S(1)}, u32[]{:S(2)}, u32[]{:S(2)}) collective-permute-start(bf16[4,7,24,384]{3,2,1,0:T(8,128)(2,1)S(1)} %get-tuple-element.66), channel_id=1, source_target_pairs={{0,64},{32,96},{64,0},{96,32},{1,65},{33,97},{65,1},{97,33},{2,66}... | collective-permute-start | bytes 1548296 | tf_op jit(solution)/shard_map/ppermute | solution.py:36
  86.8 18.2 %collective-permute-start.16 = (bf16[4,7,24,384]{3,2,1,0:T(8,128)(2,1)S(1)}, bf16[4,7,24,384]{3,2,1,0:T(8,128)(2,1)S(1)}, u32[]{:S(2)}, u32[]{:S(2)}) collective-permute-start(bf16[4,7,24,384]{3,2,1,0:T(8,128)(2,1)S(1)} %get-tuple-element.67), channel_id=1, source_target_pairs={{0,96},{32,0},{64,32},{96,64},{1,97},{33,1},{65,33},{97,65},{2,98}... | collective-permute-start | bytes 1548296 | tf_op jit(solution)/shard_map/ppermute | solution.py:36
  89.6 8.2 %collective-permute-start.12 = (bf16[4,4,24,384]{3,2,1,0:T(8,128)(2,1)S(1)}, bf16[4,4,24,384]{3,2,1,0:T(8,128)(2,1)S(1)}, u32[]{:S(2)}, u32[]{:S(2)}) collective-permute-start(bf16[4,4,24,384]{3,2,1,0:T(8,128)(2,1)S(1)} %get-tuple-element.62), channel_id=1, source_target_pairs={{0,8},{4,12},{8,0},{12,4},{1,9},{5,13},{9,1},{13,5},{2,10},{6,14},... | collective-permute-start | bytes 884744 | tf_op jit(solution)/shard_map/ppermute | solution.py:36
  93.1 9.7 %collective-permute-start.13 = (bf16[4,4,24,384]{3,2,1,0:T(8,128)(2,1)S(1)}, bf16[4,4,24,384]{3,2,1,0:T(8,128)(2,1)S(1)}, u32[]{:S(2)}, u32[]{:S(2)}) collective-permute-start(bf16[4,4,24,384]{3,2,1,0:T(8,128)(2,1)S(1)} %get-tuple-element.63), channel_id=1, source_target_pairs={{0,12},{4,0},{8,4},{12,8},{1,13},{5,1},{9,5},{13,9},{2,14},{6,2},{... | collective-permute-start | bytes 884744 | tf_op jit(solution)/shard_map/ppermute | solution.py:36
  106.2 7.3 %collective-permute-start.20 = (bf16[7,24,384]{2,1,0:T(8,128)(2,1)S(1)}, bf16[7,24,384]{2,1,0:T(8,128)(2,1)S(1)}, u32[]{:S(2)}, u32[]{:S(2)}) collective-permute-start(bf16[7,24,384]{2,1,0:T(8,128)(2,1)S(1)} %get-tuple-element.73), channel_id=1, source_target_pairs={{0,4},{4,8},{8,12},{12,0},{1,5},{5,9},{9,13},{13,1},{2,6},{6,10},{... | collective-permute-start | bytes 387080 | tf_op jit(solution)/shard_map/ppermute | solution.py:36
  106.2 12.4 %collective-permute-start.17 = (bf16[8,24,384]{2,1,0:T(8,128)(2,1)S(1)}, bf16[8,24,384]{2,1,0:T(8,128)(2,1)S(1)}, u32[]{:S(2)}, u32[]{:S(2)}) collective-permute-start(bf16[8,24,384]{2,1,0:T(8,128)(2,1)S(1)} %get-tuple-element.69), channel_id=1, source_target_pairs={{0,32},{32,64},{64,96},{96,0},{1,33},{33,65},{65,97},{97,1},{2,34}... | collective-permute-start | bytes 442376 | tf_op jit(solution)/shard_map/ppermute | solution.py:36
  108.3 10.4 %collective-permute-start.18 = (bf16[8,24,384]{2,1,0:T(8,128)(2,1)S(1)}, bf16[8,24,384]{2,1,0:T(8,128)(2,1)S(1)}, u32[]{:S(2)}, u32[]{:S(2)}) collective-permute-start(bf16[8,24,384]{2,1,0:T(8,128)(2,1)S(1)} %get-tuple-element.70), channel_id=1, source_target_pairs={{0,64},{32,96},{64,0},{96,32},{1,65},{33,97},{65,1},{97,33},{2,66}... | collective-permute-start | bytes 442376 | tf_op jit(solution)/shard_map/ppermute | solution.py:36
  110.9 7.7 %collective-permute-start.19 = (bf16[8,24,384]{2,1,0:T(8,128)(2,1)S(1)}, bf16[8,24,384]{2,1,0:T(8,128)(2,1)S(1)}, u32[]{:S(2)}, u32[]{:S(2)}) collective-permute-start(bf16[8,24,384]{2,1,0:T(8,128)(2,1)S(1)} %get-tuple-element.71), channel_id=1, source_target_pairs={{0,96},{32,0},{64,32},{96,64},{1,97},{33,1},{65,33},{97,65},{2,98}... | collective-permute-start | bytes 442376 | tf_op jit(solution)/shard_map/ppermute | solution.py:36
  110.9 5.6 %collective-permute-start.21 = (bf16[7,24,384]{2,1,0:T(8,128)(2,1)S(1)}, bf16[7,24,384]{2,1,0:T(8,128)(2,1)S(1)}, u32[]{:S(2)}, u32[]{:S(2)}) collective-permute-start(bf16[7,24,384]{2,1,0:T(8,128)(2,1)S(1)} %get-tuple-element.74), channel_id=1, source_target_pairs={{0,8},{4,12},{8,0},{12,4},{1,9},{5,13},{9,1},{13,5},{2,10},{6,14},... | collective-permute-start | bytes 387080 | tf_op jit(solution)/shard_map/ppermute | solution.py:36
  113.5 5.2 %collective-permute-start.22 = (bf16[7,24,384]{2,1,0:T(8,128)(2,1)S(1)}, bf16[7,24,384]{2,1,0:T(8,128)(2,1)S(1)}, u32[]{:S(2)}, u32[]{:S(2)}) collective-permute-start(bf16[7,24,384]{2,1,0:T(8,128)(2,1)S(1)} %get-tuple-element.75), channel_id=1, source_target_pairs={{0,12},{4,0},{8,4},{12,8},{1,13},{5,1},{9,5},{13,9},{2,14},{6,2},{... | collective-permute-start | bytes 387080 | tf_op jit(solution)/shard_map/ppermute | solution.py:36
  119.4 6.0 %collective-permute-start.23 = (bf16[8,24,384]{2,1,0:T(8,128)(2,1)S(1)}, bf16[8,24,384]{2,1,0:T(8,128)(2,1)S(1)}, u32[]{:S(2)}, u32[]{:S(2)}) collective-permute-start(bf16[8,24,384]{2,1,0:T(8,128)(2,1)S(1)} %get-tuple-element.77), channel_id=1, source_target_pairs={{0,16},{16,0},{1,17},{17,1},{2,18},{18,2},{3,19},{19,3},{4,20},{20... | collective-permute-start | bytes 442376 | tf_op jit(solution)/shard_map/ppermute | solution.py:32

commit v5 on v4

v5 whole, which is shorter than its diff:
```python
import jax
import jax.numpy as jnp
from jax import lax
from jax.experimental import pallas as pl
from jax.experimental.pallas import tpu as pltpu
from jax.sharding import Mesh
from jax.sharding import PartitionSpec as P

BLOCK = 128
PARAMS = 8469504
DP = ("dp_0", "dp_1", "dp_2", "dp_3")
MP_DP = ("mp", "dp_0", "dp_1", "dp_2", "dp_3")
ALL = DP + ("mp",)
Y, ZH, X, CORE = DP
LANES = 128
ROWS, COLS = 24, 384
VMEM = pl.BlockSpec(memory_space=pltpu.VMEM)
SMEM = pl.BlockSpec(memory_space=pltpu.SMEM)
BF16, F32 = jnp.bfloat16, jnp.float32


def wide(shard):
    return shard.astype(F32)


def narrow(shard):
    return shard.astype(BF16)


def swap(shard, axis):
    return lax.ppermute(shard, axis, [(0, 1), (1, 0)])


def to_pair(shard, axis, order):
    pairs = [(i, i ^ 1) for i in range(4)] if order == 0 else [(i, 3 - i) for i in range(4)]
    return lax.ppermute(shard, axis, pairs)


def silu_slope(pre_act):
    sigmoid_of = jax.nn.sigmoid(pre_act)
    return sigmoid_of * (1.0 + pre_act * (1.0 - sigmoid_of))


def dot(left, right):
    return jnp.dot(left, right, preferred_element_type=F32)


def contract(left, right, left_dim, right_dim):
    return lax.dot_general(
        left, right, (((left_dim,), (right_dim,)), ((), ())), preferred_element_type=F32
    )


def call(body, name, in_specs, outs, scratch=(), final=False):
    kernel = pl.pallas_call(
        body,
        out_shape=[(jax.ShapeDtypeStruct if final else pltpu.VMEM)(*out) for out in outs],
        in_specs=in_specs,
        out_specs=[VMEM] * len(outs),
        scratch_shapes=list(scratch),
        compiler_params=pltpu.CompilerParams(vmem_limit_bytes=24 << 20),
        cost_estimate=pl.CostEstimate(flops=1 << 34, bytes_accessed=1 << 26, transcendentals=0),
        name=name,
    )

    def run(*operands):
        return kernel(
            *(
                pltpu.with_memory_space_constraint(operand, pltpu.VMEM) if spec is VMEM else operand
                for operand, spec in zip(operands, in_specs)
            )
        )

    return run


def by_unit(raw_ref, core, out_ref, start):
    for unit in range(16):
        for z_hi in range(2):
            first = 2 * ROWS * ((unit // 4 * 2 + z_hi) * 4 + unit % 4)
            rows = pl.ds(pl.multiple_of(first + ROWS * core, 8), ROWS)
            for half in range(2):
                out_ref[unit, start + 2 * z_hi + half] = narrow(
                    raw_ref[rows, half * COLS : (half + 1) * COLS]
                )


def hidden_kernel(
    partial_ref, arrived_ref, live_ref, target_ref, w_ref,
    act_ref, act_slope_ref, slope_ref, back_ref,
):
    pre_middle = partial_ref[...] + wide(arrived_ref[...])
    sigmoid_of = 1.0 / (1.0 + jnp.exp(-pre_middle))
    act = narrow(pre_middle * sigmoid_of)
    act_ref[...] = act
    act_slope_ref[...] = sigmoid_of * (1.0 + pre_middle * (1.0 - sigmoid_of))
    slope = slope_of(w_ref[...], act, target_ref[...], live_ref[...])
    slope_ref[...] = slope
    back_ref[...] = contract(slope, w_ref[...], 0, 0)


def slope_of(weights, act, target, live):
    mismatch = contract(weights, act, 1, 1) - wide(target)
    return narrow(jnp.clip(mismatch, -1.0, 1.0) * live)


def slopes_kernel(
    place_ref, act_ref, act_slope_ref, back_ref, live_ref, target_ref, first_slope_ref,
    onehot_ref, fetched_ref, relayed_ref, w_middle_ref, belief_ref,
    slope_middle_ref, slope_first_ref, sent_ref,
):
    w_other = jnp.where(place_ref[0] == 0, fetched_ref[...], relayed_ref[...])
    slope = slope_of(w_other, act_ref[...], target_ref[...], live_ref[...])
    back = back_ref[...] + contract(slope, w_other, 0, 0)
    slope_middle = narrow(back * act_slope_ref[...])
    slope_middle_ref[...] = slope_middle
    slope_first = narrow(contract(w_middle_ref[...], slope_middle, 1, 1) * first_slope_ref[...])
    slope_first = narrow(dot(onehot_ref[...], slope_first))
    slope_first_ref[...] = slope_first
    half = slope_first.shape[0] // 2
    for start, stop in column_cuts(belief_ref.shape[0]):
        raw = narrow(contract(slope_first[:half], belief_ref[start:stop, :], 1, 1))
        put_columns(raw, start // COLS, sent_ref)


def column_cuts(width):
    return [(start, min(start + COLS, width)) for start in range(0, width, COLS)]


def put_columns(raw, granule, out_ref):
    width = raw.shape[1]
    if width < COLS:
        raw = jnp.concatenate([raw, jnp.zeros((raw.shape[0], COLS - width), raw.dtype)], 1)
    for unit in range(16):
        out_ref[unit, granule] = raw[unit * ROWS : (unit + 1) * ROWS]


def later_kernel(
    place_ref, act_ref, slope_ref, slope_middle_ref, act_first_ref, sent_ref, own_ref, raw_ref, padded_ref
):
    core = place_ref[0]
    padded_ref[...] = jnp.zeros_like(padded_ref)
    padded_ref[0 : slope_ref.shape[0], :] = slope_ref[...]
    raw_ref[...] = contract(act_ref[...].T, padded_ref[...], 1, 1)
    by_unit(raw_ref, 1 - core, sent_ref, 0)
    by_unit(raw_ref, core, own_ref, 0)
    raw_ref[...] = contract(slope_middle_ref[...], act_first_ref[...], 0, 0)
    by_unit(raw_ref, 1 - core, sent_ref, 4)
    by_unit(raw_ref, core, own_ref, 4)


def kept_and_sent(me, order):
    near, far, opposite = lax.bitwise_xor(me, 1), 3 - me, lax.bitwise_xor(me, 2)
    return ((me, far), (near, opposite)) if order == 0 else ((me, near), (far, opposite))


def cut_first_kernel(place_ref, slope_first_ref, belief_ref, arrived_ref, *refs):
    raw_ref = refs[-1]
    half = slope_first_ref.shape[0] // 2
    slope = slope_first_ref[half:, :]
    for start, stop in column_cuts(belief_ref.shape[0]):
        raw = contract(slope, belief_ref[start:stop, :], 1, 1)
        put_columns(raw, start // COLS, raw_ref)
    for order, part in enumerate((slice(0, 4), slice(4, 7))):
        for side, blocks in enumerate(kept_and_sent(place_ref[1], order)):
            out_ref = refs[2 * order + side]
            for position, y in enumerate(blocks):
                for x in range(4):
                    total = raw_ref[4 * y + x, part] + wide(arrived_ref[4 * y + x, part])
                    out_ref[position, x] = total.astype(out_ref.dtype)


def cut_rest_kernel(place_ref, own_ref, arrived_ref, *refs):
    for order, part in enumerate((slice(0, 4), slice(4, 8))):
        for side, blocks in enumerate(kept_and_sent(place_ref[2], order)):
            out_ref = refs[2 * order + side]
            for position, x in enumerate(blocks):
                for y in range(4):
                    total = wide(own_ref[4 * y + x, part]) + wide(arrived_ref[4 * y + x, part])
                    out_ref[position, y] = total.astype(out_ref.dtype)


def halve_kernel(*refs):
    for part in range(4):
        kept_ref, arrived_ref = refs[2 * part : 2 * part + 2]
        kept_out, sent_out = refs[8 + 2 * part : 10 + 2 * part]
        kept_out[...] = kept_ref[0] + wide(arrived_ref[0])
        sent_out[...] = narrow(kept_ref[1] + wide(arrived_ref[1]))


def turn_kernel(place_ref, *refs):
    scratch = refs[16:]
    for part in range(4):
        kept_ref, arrived_ref = refs[2 * part : 2 * part + 2]
        scratch[part][...] = kept_ref[...] + wide(arrived_ref[...])
        for side, blocks in enumerate(kept_and_sent(place_ref[2 if part < 2 else 1], part % 2)):
            out_ref = refs[8 + 2 * part + side]
            for position, block in enumerate(blocks):
                out_ref[position] = scratch[part][block].astype(out_ref.dtype)


def z_cut_kernel(place_ref, *refs):
    sent_ref, own_ref, last_sum, middle_sum = refs[8:12]
    z_hi = place_ref[3]
    low, high, last, middle = (
        refs[2 * part][...] + wide(refs[2 * part + 1][...]) for part in range(4)
    )
    last_sum[...] = last
    middle_sum[...] = middle
    rows = [low[granule] for granule in range(4)] + [high[granule] for granule in range(3)]
    for side, out_ref in ((1 - z_hi, sent_ref), (z_hi, own_ref)):
        kind = out_ref.dtype
        out_ref[0:2] = last_sum[pl.ds(2 * side, 2)].astype(kind)
        out_ref[2:4] = middle_sum[pl.ds(2 * side, 2)].astype(kind)
        halves = [jnp.where(side == 0, row[0:12], row[12:24]) for row in rows]
        halves.append(jnp.zeros_like(halves[0]))
        for pair in range(4):
            out_ref[4 + pair] = jnp.concatenate(halves[2 * pair : 2 * pair + 2], 0).astype(kind)


def square_kernel(own_ref, arrived_ref, total_ref, squares_ref):
    total = own_ref[...] + wide(arrived_ref[...])
    total_ref[...] = total
    squares_ref[...] = jnp.broadcast_to(jnp.sum(total * total), squares_ref.shape)


def scale_kernel(total_ref, squares_ref, first_ref, middle_ref, last_ref):
    square_sum = jnp.sum(squares_ref[...], axis=0)
    norm_scale = lax.rsqrt(square_sum / PARAMS + 1e-06)
    norm_scale = jnp.concatenate([norm_scale] * 3, 1)
    for ref, start in ((last_ref, 0), (middle_ref, 2)):
        for half in range(2):
            columns = slice(half * COLS, min((half + 1) * COLS, ref.shape[1]))
            width = columns.stop - columns.start
            ref[:, columns] = (total_ref[start + half] * norm_scale)[:, :width]
    for granule, (start, stop) in enumerate(column_cuts(first_ref.shape[1])):
        row = granule % 2 * 12
        scaled = total_ref[4 + granule // 2, row : row + 12] * norm_scale
        first_ref[:, start:stop] = scaled[:, : stop - start]


def granules(*lead, kind=BF16):
    return ((*lead, ROWS, COLS), kind)


def per_device(belief, target_value, counts, w_first, w_middle, w_last):
    total_rows, inputs = belief.shape
    width = w_last.shape[1]
    units = w_first.shape[1]
    hidden = w_middle.shape[1]
    belief_t, w_last_t = belief.T, w_last.T

    around = (ZH, CORE, "mp")
    fetched = lax.ppermute(w_last_t, around, [(0, 5), (5, 0), (1, 4), (4, 1)])

    pre_first = dot(belief, w_first)
    act_first = narrow(jax.nn.silu(pre_first))
    partial_middle = dot(act_first, w_middle)
    hidden_sent = narrow(partial_middle)
    arrived = swap(hidden_sent, "mp")

    indices = jnp.stack([lax.axis_index(axis) for axis in (CORE, Y, X, ZH, "mp")])
    indices, pre_first, target_value, hidden_sent = lax.optimization_barrier(
        (indices, pre_first, target_value, hidden_sent)
    )
    core, mp = indices[0], indices[4]
    live_rows = (counts[:, None] > jnp.arange(BLOCK, dtype=jnp.int32)[None, :]).reshape(1, total_rows)
    live = live_rows.astype(F32)
    target_t = target_value.T
    target_own = lax.dynamic_slice_in_dim(target_t, mp * width, width, 0)
    target_other = lax.dynamic_slice_in_dim(target_t, (1 - mp) * width, width, 0)
    order = jnp.arange(units, dtype=jnp.int32).reshape(4, 2, 4, 2, -1).transpose(3, 0, 2, 1, 4)
    order = jnp.where(core == 0, order[::-1], order).reshape(units)
    onehot = (order[:, None] == jnp.arange(units, dtype=jnp.int32)[None, :]).astype(BF16)
    first_slope = silu_slope(pre_first).T
    fetched, place, live, target_own, target_other, onehot, first_slope = lax.optimization_barrier(
        (fetched, indices[:4], live, target_own, target_other, onehot, first_slope)
    )
    relayed = lax.ppermute(fetched, CORE, [(0, 1)])

    act, act_slope, slope_own, back_own = call(
        hidden_kernel,
        "hidden",
        [VMEM] * 5,
        [
            ((total_rows, hidden), BF16),
            ((total_rows, hidden), F32),
            ((width, total_rows), BF16),
            ((total_rows, hidden), F32),
        ],
    )(partial_middle, arrived, live, target_own, w_last_t)

    slope_middle, slope_first, first_sent = call(
        slopes_kernel,
        "slopes",
        [SMEM] + [VMEM] * 11,
        [((total_rows, hidden), BF16), ((units, total_rows), BF16), granules(16, 7)],
    )(
        place, act, act_slope, back_own, live, target_other, first_slope, onehot,
        fetched, relayed, w_middle, belief_t,
    )
    first_arrived = swap(first_sent, CORE)

    rest_sent, rest_own = call(
        later_kernel,
        "later",
        [SMEM] + [VMEM] * 4,
        [granules(16, 8)] * 2,
        [pltpu.VMEM((hidden, units), F32), pltpu.VMEM((units, total_rows), BF16)],
    )(place, act, slope_own, slope_middle, act_first)
    rest_arrived = swap(rest_sent, CORE)

    def pairs(*sizes):
        return [out for size in sizes for out in (granules(*size, kind=F32), granules(*size))]

    def exchange(parts, axes, orders):
        return [
            part if side == 0 else to_pair(part, axes[i], orders[i])
            for i in range(len(parts) // 2)
            for side, part in enumerate(parts[2 * i : 2 * i + 2])
        ]

    parts = exchange(
        call(
            cut_first_kernel,
            "cut_first",
            [SMEM] + [VMEM] * 3,
            pairs((2, 4, 4), (2, 4, 3)),
            [pltpu.VMEM((16, 7, ROWS, COLS), F32)],
        )(place, slope_first, belief_t, first_arrived),
        (Y, Y),
        (0, 1),
    )
    parts += exchange(
        call(cut_rest_kernel, "cut_rest", [SMEM] + [VMEM] * 2, pairs((2, 4, 4), (2, 4, 4)))(
            place, rest_own, rest_arrived
        ),
        (X, X),
        (0, 1),
    )
    sizes = (4, 3, 4, 4)
    parts = exchange(
        call(halve_kernel, "halve", [VMEM] * 8, pairs(*((4, size) for size in sizes)))(*parts),
        (Y, Y, X, X),
        (1, 0, 1, 0),
    )
    parts = exchange(
        call(
            turn_kernel,
            "turn",
            [SMEM] + [VMEM] * 8,
            pairs(*((2, size) for size in sizes)),
            [pltpu.VMEM((4, size, ROWS, COLS), F32) for size in sizes],
        )(place, *parts),
        (X, X, Y, Y),
        (0, 1, 0, 1),
    )
    parts = exchange(
        call(halve_kernel, "halve", [VMEM] * 8, pairs(*((size,) for size in sizes)))(*parts),
        (X, X, Y, Y),
        (1, 0, 1, 0),
    )
    sent, own = call(
        z_cut_kernel,
        "z_cut",
        [SMEM] + [VMEM] * 8,
        [granules(8), granules(8, kind=F32)],
        [pltpu.VMEM((4, ROWS, COLS), F32)] * 2,
    )(place, *parts)

    total, squares = call(
        square_kernel, "square", [VMEM] * 2, [((8, ROWS, COLS), F32), ((128, 1, LANES), F32)]
    )(own, swap(sent, ZH))
    squares = lax.all_to_all(squares, ALL, 0, 0, tiled=True)
    grad_first, grad_middle, grad_last = call(
        scale_kernel,
        "scale",
        [VMEM] * 2,
        [((units // 64, inputs), F32), ((ROWS, units), F32), ((ROWS, width), F32)],
        final=True,
    )(total, squares)
    return grad_first.T, grad_middle.T, grad_last


def solution(mesh):
    finer = Mesh(mesh.devices.reshape(4, 2, 4, 2, mesh.shape["mp"]), ALL)
    return jax.shard_map(
        per_device,
        mesh=finer,
        in_specs=(P(DP, None), P(DP, None), P(DP), P(None, "mp"), P("mp", None), P(None, "mp")),
        out_specs=(P(None, MP_DP), P("mp", DP), P(DP, "mp")),
        check_vma=False,
    )
```

time: 148 us -> 134 us (0.905)
  waiting for transfers between devices: 52.5 us -> 35.4 us
  starting transfers between devices: 37.6 us -> 33.6 us
  blocking collectives: 21.1 us -> 23.6 us
  between operations: 0.9 us -> 2.75 us
    ppermute x19 -> x18, waiting for transfers between devices: 46.7 us -> 27 us  [the longest x16 24.4 us: to_pair(): return lax.ppermute(shard, axis, pairs)]
    ppermute x19 -> x18, starting transfers between devices: 30.7 us -> 21.5 us  [the longest x16 18.1 us: to_pair(): return lax.ppermute(shard, axis, pairs)]
    ppermute x5 -> x4, starting transfers between devices: 6.91 us -> 12.1 us  [swap(): return lax.ppermute(shard, axis, [(0, 1), (1, 0)])]
    all_to_all x1, blocking collectives: 21.1 us -> 23.6 us  [per_device(): squares = lax.all_to_all(squares, ALL, 0, 0, tiled=True)]
    ppermute x5 -> x4, waiting for transfers between devices: 5.85 us -> 8.37 us  [swap(): return lax.ppermute(shard, axis, [(0, 1), (1, 0)])]
    transpose x0 -> x1, other arithmetic: none -> 2.38 us  [per_device(): first_slope = silu_slope(pre_first).T]
    optimization_barrier x0 -> x1, local copies, waits for them, and re-layouts: none -> 2.37 us  [per_device(): lax.optimization_barrier((fetched, indices[:4], live, target_own, target_...]
    dot_general x1 -> x0, local copies, waits for them, and re-layouts: 2.29 us -> none  [dot(): return jnp.dot(left, right, preferred_element_type=F32)]
  transfers between devices with their start and end apart: 24 -> 22, of which waited for: 12 -> 13; matrix products, arithmetic and copies ran while one was open for 9% -> 11% of each run, Pallas kernels for 6% -> 7%
where the time goes in v5:
time: 134 us; the launch traced here: 133 us
  waiting for transfers between devices  35.4 us (26%)
  starting transfers between devices  33.6 us (25%)
  blocking collectives  23.6 us (18%)
  Pallas kernels  19.1 us (14%)
  local copies, waits for them, and re-layouts  9.22 us (7%)
  matrix products  7 us (5%)
  between operations  2.75 us (2%)
  other arithmetic  2.73 us (2%)
    ppermute x16, waiting for transfers between devices, to_pair(): return lax.ppermute(shard, axis, pairs)  24.4 us
    all_to_all x1, blocking collectives, per_device(): squares = lax.all_to_all(squares, ALL, 0, 0, tiled=True)  23.6 us
    pallas_call x11, Pallas kernels, run(): kernel(*(pltpu.with_memory_space_constraint(operand, pltpu.VMEM) if spec...  19.1 us
    ppermute x16, starting transfers between devices, to_pair(): return lax.ppermute(shard, axis, pairs)  18.1 us
    ppermute x4, starting transfers between devices, swap(): return lax.ppermute(shard, axis, [(0, 1), (1, 0)])  12.1 us
    ppermute x4, waiting for transfers between devices, swap(): return lax.ppermute(shard, axis, [(0, 1), (1, 0)])  8.37 us
    dot_general x2, matrix products, dot(): return jnp.dot(left, right, preferred_element_type=F32)  7 us
    unnamed x20, local copies, waits for them, and re-layouts  3.98 us
  transfers between devices with their start and end apart: 22, of which 13 were waited for; matrix products, arithmetic and copies ran while one was open for 11% of the time, Pallas kernels for 7%

profile of v5, /device:TPU:1, one launch (start us, length us, event | category | flops | bytes accessed | tf_op | source)
XLA Modules:
  0.0 133.4 jit_solution(11309766707349158418)
XLA Ops:
  0.6 2.1 %collective-permute-start = (bf16[663,1536]{1,0:T(8,128)(2,1)}, bf16[663,1536]{1,0:T(8,128)(2,1)}, u32[]{:S(2)}, u32[]{:S(2)}) collective-permute-start(bf16[663,1536]{1,0:T(8,128)(2,1)} %bitcast.30), channel_id=1, source_target_pairs={{0,17},{17,0},{1,16},{16,1},{4,21},{21,4},{5,20},{20,5},{8,25},{25... | collective-permute-start | bytes 6110216 | tf_op jit(solution)/shard_map/ppermute | solution.py:254
  2.8 4.8 %multiply_convert_fusion = (bf16[256,768]{1,0:T(8,128)(2,1)S(1)}, f32[256,768]{1,0:T(8,128)}) fusion(bf16[256,2652]{0,1:T(8,128)(2,1)} %param.6, bf16[2652,768]{1,0:T(8,128)(2,1)} %param.9), kind=kOutput, calls=%fused_computation.3 | convolution fusion | flops 1043791872 | bytes 6610944 | tf_op jit(solution)/shard_map/dot_general | solution.py:45
  7.6 2.2 %fusion.2 = (bf16[256,1536]{1,0:T(8,128)(2,1)}, f32[256,1536]{1,0:T(8,128)}) fusion(bf16[256,768]{1,0:T(8,128)(2,1)S(1)} %get-tuple-element.123.act_first_ref, bf16[768,1536]{1,0:T(8,128)(2,1)S(1)} %copy-done), kind=kOutput, calls=%fused_computation.10 | convolution fusion | flops 604372992 | bytes 5111808 | tf_op jit(solution)/shard_map/dot_general | solution.py:45
  9.8 2.5 %collective-permute-start.1 = (bf16[256,1536]{1,0:T(8,128)(2,1)}, bf16[256,1536]{1,0:T(8,128)(2,1)}, u32[]{:S(2)}, u32[]{:S(2)}) collective-permute-start(bf16[256,1536]{1,0:T(8,128)(2,1)} %get-tuple-element.125), channel_id=1, source_target_pairs={{0,1},{1,0},{2,3},{3,2},{4,5},{5,4},{6,7},{7,6},{8,9},{9,8},{10,11... | collective-permute-start | bytes 2359304 | tf_op jit(solution)/shard_map/ppermute | solution.py:31
  12.3 0.1 stack.23
  12.3 0.6 fusion.1
  14.9 0.1 eq.23
  15.1 0.1 compare_convert_fusion
  15.1 0.3 fusion.onehot_ref
  15.4 2.1 %dynamic-slice_bitcast_fusion = (bf16[663,256]{1,0:T(8,128)(2,1)}, bf16[663,256]{1,0:T(8,128)(2,1)}) fusion(bf16[256,1326]{0,1:T(8,128)(2,1)} %param.7, s32[]{:T(128)S(6)} %select_n.15, s32[]{:T(128)S(6)} %select_n.14), kind=kLoop, calls=%fused_computation.4 | loop fusion | bytes 1357832 | tf_op jit(solution)/shard_map/dynamic_slice | solution.py:271
  17.5 2.4 %multiply_bitcast_fusion = f32[768,256]{0,1:T(8,128)} fusion(f32[256,768]{1,0:T(8,128)} %get-tuple-element.63), kind=kLoop, calls=%fused_computation.2 | loop fusion | flops 1376256 | bytes 1572864 | tf_op jit(solution)/shard_map/transpose | solution.py:275
  19.9 0.0 collective-permute-done.fetched_ref
  19.9 1.3 collective-permute-start.2
  21.2 2.4 %copy.9.first_slope_ref = f32[768,256]{1,0:T(8,128)} copy(f32[768,256]{0,1:T(8,128)} %multiply_bitcast_fusion) | data formatting | bytes 1572864 | tf_op jit(solution)/shard_map/optimization_barrier | solution.py:276
  23.5 3.2 %collective-permute-done.1.arrived_ref = bf16[256,1536]{1,0:T(8,128)(2,1)} collective-permute-done((bf16[256,1536]{1,0:T(8,128)(2,1)}, bf16[256,1536]{1,0:T(8,128)(2,1)}, u32[]{:S(2)}, u32[]{:S(2)}) %collective-permute-start.1) | collective-permute-done | bytes 786464 | tf_op jit(solution)/shard_map/ppermute | solution.py:31
  26.7 1.4 %copy-done.1 = f32[256,1536]{1,0:T(8,128)S(1)} copy-done((f32[256,1536]{1,0:T(8,128)S(1)}, f32[256,1536]{1,0:T(8,128)}, u32[]{:S(2)}) %copy-start.1) | copy-done | bytes 1572888
  28.1 1.0 copy-done.6
  29.1 1.6 %copy-done.7 = bf16[1536,663]{0,1:T(8,128)(2,1)S(1)} copy-done((bf16[1536,663]{0,1:T(8,128)(2,1)S(1)}, bf16[1536,663]{0,1:T(8,128)(2,1)}, u32[]{:S(2)}) %copy-start.7) | copy-done | bytes 2036760
  30.7 3.8 %hidden.1 = (bf16[256,1536]{1,0:T(8,128)(2,1)S(1)}, f32[256,1536]{1,0:T(8,128)S(1)}, bf16[663,256]{1,0:T(8,128)(2,1)S(1)}, f32[256,1536]{1,0:T(8,128)S(1)}) custom-call(f32[256,1536]{1,0:T(8,128)S(1)} %copy-done.1, bf16[256,1536]{1,0:T(8,128)(2,1)} %collective-permute-done.1.arrived_ref, f32[1,256]{1,0:T(1,128)S(1)} %bitcast.34, ...), custom_call_target="tpu_custom_call" | custom-call | flops 17179869184 | bytes 67108864 | tf_op jit(solution)/shard_map/hidden/pallas_call | solution.py:67
  34.5 2.6 %collective-permute-done.2.relayed_ref = bf16[663,1536]{1,0:T(8,128)(2,1)} collective-permute-done((bf16[663,1536]{1,0:T(8,128)(2,1)}, bf16[663,1536]{1,0:T(8,128)(2,1)}, u32[]{:S(2)}, u32[]{:S(2)}) %collective-permute-start.2) | collective-permute-done | bytes 2036768 | tf_op jit(solution)/shard_map/ppermute | solution.py:279
  37.1 6.6 %slopes.1 = (bf16[256,1536]{1,0:T(8,128)(2,1)S(1)}, bf16[768,256]{1,0:T(8,128)(2,1)S(1)}, bf16[16,7,24,384]{3,2,1,0:T(8,128)(2,1)S(1)}) custom-call(s32[4]{0:T(128)S(1)} %bitcast.24, bf16[256,1536]{1,0:T(8,128)(2,1)S(1)} %get-tuple-element.67.act_ref, f32[256,1536]{1,0:T(8,128)S(1)} %get-tuple-element.68.act_slope_ref, ...), custom_call_target="tpu_custom_call" | custom-call | flops 17179869184 | bytes 67108864 | tf_op jit(solution)/shard_map/slopes/pallas_call | solution.py:67
  43.8 7.7 %collective-permute-start.3 = (bf16[16,7,24,384]{3,2,1,0:T(8,128)(2,1)S(1)}, bf16[16,7,24,384]{3,2,1,0:T(8,128)(2,1)S(1)}, u32[]{:S(2)}, u32[]{:S(2)}) collective-permute-start(bf16[16,7,24,384]{3,2,1,0:T(8,128)(2,1)S(1)} %get-tuple-element.75), channel_id=1, source_target_pairs={{0,2},{2,0},{1,3},{3,1},{4,6},{6,4},{5,7},{7,5},{8,10},{10,8},{9,1... | collective-permute-start | bytes 6193160 | tf_op jit(solution)/shard_map/ppermute | solution.py:31
  51.5 2.5 %later.1 = (bf16[16,8,24,384]{3,2,1,0:T(8,128)(2,1)S(1)}, bf16[16,8,24,384]{3,2,1,0:T(8,128)(2,1)S(1)}) custom-call(s32[4]{0:T(128)S(1)} %bitcast.25, bf16[256,1536]{1,0:T(8,128)(2,1)S(1)} %get-tuple-element.67.act_ref, bf16[663,256]{1,0:T(8,128)(2,1)S(1)} %get-tuple-element.80.slope_ref, bf16[256,1536]{1,0:T(8,128)(2,1)S(1)} %get-tuple-element.81.slope_middle_ref, ...), custom_call_target="tpu_custom_call" | custom-call | flops 17179869184 | bytes 67108864 | tf_op jit(solution)/shard_map/later/pallas_call | solution.py:67
  54.0 0.3 collective-permute-start.6
  54.3 0.9 collective-permute-done.3.arrived_ref
  55.2 1.8 %cut_first.1 = (f32[2,4,4,24,384]{4,3,2,1,0:T(8,128)S(1)}, bf16[2,4,4,24,384]{4,3,2,1,0:T(8,128)(2,1)S(1)}, f32[2,4,3,24,384]{4,3,2,1,0:T(8,128)S(1)}, bf16[2,4,3,24,384]{4,3,2,1,0:T(8,128)(2,1)S(1)}) custom-call(s32[4]{0:T(128)S(1)} %bitcast.26, bf16[768,256]{1,0:T(8,128)(2,1)S(1)} %get-tuple-element.74.slope_first_ref, bf16[2652,256]{1,0:T(8,128)(2,1)S(1)} %bitcast.33, ...), custom_call_target="tpu_custom_call" | custom-call | flops 17179869184 | bytes 67108864 | tf_op jit(solution)/shard_map/cut_first/pallas_call | solution.py:67
  57.1 1.4 %collective-permute-start.4 = (bf16[2,4,4,24,384]{4,3,2,1,0:T(8,128)(2,1)S(1)}, bf16[2,4,4,24,384]{4,3,2,1,0:T(8,128)(2,1)S(1)}, u32[]{:S(2)}, u32[]{:S(2)}) collective-permute-start(bf16[2,4,4,24,384]{4,3,2,1,0:T(8,128)(2,1)S(1)} %get-tuple-element.77), channel_id=1, source_target_pairs={{0,32},{32,0},{64,96},{96,64},{1,33},{33,1},{65,97},{97,65},{2,34}... | collective-permute-start | bytes 1769480 | tf_op jit(solution)/shard_map/ppermute | solution.py:36
  58.4 0.4 collective-permute-done.6.arrived_ref
  58.8 1.1 cut_rest.1
  59.9 1.3 collective-permute-start.7
  61.2 1.8 %collective-permute-start.8 = (bf16[2,4,4,24,384]{4,3,2,1,0:T(8,128)(2,1)S(1)}, bf16[2,4,4,24,384]{4,3,2,1,0:T(8,128)(2,1)S(1)}, u32[]{:S(2)}, u32[]{:S(2)}) collective-permute-start(bf16[2,4,4,24,384]{4,3,2,1,0:T(8,128)(2,1)S(1)} %get-tuple-element.87), channel_id=1, source_target_pairs={{0,12},{4,8},{8,4},{12,0},{1,13},{5,9},{9,5},{13,1},{2,14},{6,10},... | collective-permute-start | bytes 1769480 | tf_op jit(solution)/shard_map/ppermute | solution.py:36
  63.0 2.7 %collective-permute-start.5 = (bf16[2,4,3,24,384]{4,3,2,1,0:T(8,128)(2,1)S(1)}, bf16[2,4,3,24,384]{4,3,2,1,0:T(8,128)(2,1)S(1)}, u32[]{:S(2)}, u32[]{:S(2)}) collective-permute-start(bf16[2,4,3,24,384]{4,3,2,1,0:T(8,128)(2,1)S(1)} %get-tuple-element.79), channel_id=1, source_target_pairs={{0,96},{32,64},{64,32},{96,0},{1,97},{33,65},{65,33},{97,1},{2,98}... | collective-permute-start | bytes 1327112 | tf_op jit(solution)/shard_map/ppermute | solution.py:36
  65.7 9.5 %collective-permute-done.5.refs_3_ = bf16[2,4,3,24,384]{4,3,2,1,0:T(8,128)(2,1)S(1)} collective-permute-done((bf16[2,4,3,24,384]{4,3,2,1,0:T(8,128)(2,1)S(1)}, bf16[2,4,3,24,384]{4,3,2,1,0:T(8,128)(2,1)S(1)}, u32[]{:S(2)}, u32[]{:S(2)}) %collective-permute-start.5) | collective-permute-done | bytes 442400 | tf_op jit(solution)/shard_map/ppermute | solution.py:36
  75.2 0.0 collective-permute-done.4.refs_1_
  75.2 0.0 collective-permute-done.7.refs_5_
  75.2 1.5 %collective-permute-done.8.refs_7_ = bf16[2,4,4,24,384]{4,3,2,1,0:T(8,128)(2,1)S(1)} collective-permute-done((bf16[2,4,4,24,384]{4,3,2,1,0:T(8,128)(2,1)S(1)}, bf16[2,4,4,24,384]{4,3,2,1,0:T(8,128)(2,1)S(1)}, u32[]{:S(2)}, u32[]{:S(2)}) %collective-permute-start.8) | collective-permute-done | bytes 589856 | tf_op jit(solution)/shard_map/ppermute | solution.py:36
  76.7 0.4 halve.2
  77.1 2.9 %collective-permute-start.9 = (bf16[4,4,24,384]{3,2,1,0:T(8,128)(2,1)S(1)}, bf16[4,4,24,384]{3,2,1,0:T(8,128)(2,1)S(1)}, u32[]{:S(2)}, u32[]{:S(2)}) collective-permute-start(bf16[4,4,24,384]{3,2,1,0:T(8,128)(2,1)S(1)} %get-tuple-element.89), channel_id=1, source_target_pairs={{0,96},{32,64},{64,32},{96,0},{1,97},{33,65},{65,33},{97,1},{2,98}... | collective-permute-start | bytes 884744 | tf_op jit(solution)/shard_map/ppermute | solution.py:36
  80.0 1.8 %collective-permute-start.11 = (bf16[4,4,24,384]{3,2,1,0:T(8,128)(2,1)S(1)}, bf16[4,4,24,384]{3,2,1,0:T(8,128)(2,1)S(1)}, u32[]{:S(2)}, u32[]{:S(2)}) collective-permute-start(bf16[4,4,24,384]{3,2,1,0:T(8,128)(2,1)S(1)} %get-tuple-element.93), channel_id=1, source_target_pairs={{0,12},{4,8},{8,4},{12,0},{1,13},{5,9},{9,5},{13,1},{2,14},{6,10},... | collective-permute-start | bytes 884744 | tf_op jit(solution)/shard_map/ppermute | solution.py:36
  81.8 0.0 collective-permute-start.12
  81.8 0.0 collective-permute-start.10
  81.8 5.1 %collective-permute-done.10.refs_3_ = bf16[4,3,24,384]{3,2,1,0:T(8,128)(2,1)S(1)} collective-permute-done((bf16[4,3,24,384]{3,2,1,0:T(8,128)(2,1)S(1)}, bf16[4,3,24,384]{3,2,1,0:T(8,128)(2,1)S(1)}, u32[]{:S(2)}, u32[]{:S(2)}) %collective-permute-start.10) | collective-permute-done | bytes 221216 | tf_op jit(solution)/shard_map/ppermute | solution.py:36
  86.9 0.0 collective-permute-done.9.refs_1_
  86.9 1.3 collective-permute-done.11.refs_5_
  88.2 0.3 collective-permute-done.12.refs_7_
  88.5 0.9 turn.1
  89.4 0.4 collective-permute-start.13
  89.8 0.0 collective-permute-start.15
  89.8 0.6 collective-permute-start.16
  90.4 1.3 collective-permute-start.14
  91.7 3.5 %collective-permute-done.14.refs_3_ = bf16[2,3,24,384]{3,2,1,0:T(8,128)(2,1)S(1)} collective-permute-done((bf16[2,3,24,384]{3,2,1,0:T(8,128)(2,1)S(1)}, bf16[2,3,24,384]{3,2,1,0:T(8,128)(2,1)S(1)}, u32[]{:S(2)}, u32[]{:S(2)}) %collective-permute-start.14) | collective-permute-done | bytes 110624 | tf_op jit(solution)/shard_map/ppermute | solution.py:36
  95.3 0.0 collective-permute-done.15.refs_5_
  95.3 0.0 collective-permute-done.16.refs_7_
  95.3 0.1 halve.3
  95.4 1.4 %collective-permute-start.17 = (bf16[4,24,384]{2,1,0:T(8,128)(2,1)S(1)}, bf16[4,24,384]{2,1,0:T(8,128)(2,1)S(1)}, u32[]{:S(2)}, u32[]{:S(2)}) collective-permute-start(bf16[4,24,384]{2,1,0:T(8,128)(2,1)S(1)} %get-tuple-element.105), channel_id=1, source_target_pairs={{0,12},{4,8},{8,4},{12,0},{1,13},{5,9},{9,5},{13,1},{2,14},{6,10},... | collective-permute-start | bytes 221192 | tf_op jit(solution)/shard_map/ppermute | solution.py:36
  96.8 2.4 %collective-permute-start.19 = (bf16[4,24,384]{2,1,0:T(8,128)(2,1)S(1)}, bf16[4,24,384]{2,1,0:T(8,128)(2,1)S(1)}, u32[]{:S(2)}, u32[]{:S(2)}) collective-permute-start(bf16[4,24,384]{2,1,0:T(8,128)(2,1)S(1)} %get-tuple-element.109), channel_id=1, source_target_pairs={{0,96},{32,64},{64,32},{96,0},{1,97},{33,65},{65,33},{97,1},{2,98}... | collective-permute-start | bytes 221192 | tf_op jit(solution)/shard_map/ppermute | solution.py:36
  99.2 3.0 %collective-permute-done.18.refs_3_ = bf16[3,24,384]{2,1,0:T(8,128)(2,1)S(1)} collective-permute-done((bf16[3,24,384]{2,1,0:T(8,128)(2,1)S(1)}, bf16[3,24,384]{2,1,0:T(8,128)(2,1)S(1)}, u32[]{:S(2)}, u32[]{:S(2)}) %collective-permute-start.18) | collective-permute-done | bytes 55328 | tf_op jit(solution)/shard_map/ppermute | solution.py:36
  102.2 0.2 collective-permute-done.20.refs_7_
  102.4 0.6 z_cut.1
  103.0 1.7 %collective-permute-start.21 = (bf16[8,24,384]{2,1,0:T(8,128)(2,1)S(1)}, bf16[8,24,384]{2,1,0:T(8,128)(2,1)S(1)}, u32[]{:S(2)}, u32[]{:S(2)}) collective-permute-start(bf16[8,24,384]{2,1,0:T(8,128)(2,1)S(1)} %get-tuple-element.113), channel_id=1, source_target_pairs={{0,16},{16,0},{1,17},{17,1},{2,18},{18,2},{3,19},{19,3},{4,20},{20... | collective-permute-start | bytes 442376 | tf_op jit(solution)/shard_map/ppermute | solution.py:31
  104.7 3.9 %collective-permute-done.21.arrived_ref = bf16[8,24,384]{2,1,0:T(8,128)(2,1)S(1)} collective-permute-done((bf16[8,24,384]{2,1,0:T(8,128)(2,1)S(1)}, bf16[8,24,384]{2,1,0:T(8,128)(2,1)S(1)}, u32[]{:S(2)}, u32[]{:S(2)}) %collective-permute-start.21) | collective-permute-done | bytes 147488 | tf_op jit(solution)/shard_map/ppermute | solution.py:31
  108.6 0.3 square.1
  108.9 23.6 %all_to_all.5.squares_ref = f32[128,1,128]{2,1,0:T(1,128)S(1)} all-to-all(f32[128,1,128]{2,1,0:T(1,128)S(1)} %get-tuple-element.115), channel_id=1, replica_groups=mesh['dp_0'=4,'dp_1'=2,'dp_2'=4,'dp_3'=2,'mp'=2] {'dp_0','dp_1','dp_2','..., dimensions={0} | all-to-all | bytes 131072 | tf_op jit(solution)/shard_map/all_to_all | solution.py:374
  132.5 0.9 scale.1
  (24 shorter events, 0.1 us)
Async XLA Ops:
  0.6 7.0 %copy-start = (bf16[768,1536]{1,0:T(8,128)(2,1)S(1)}, bf16[768,1536]{1,0:T(8,128)(2,1)}, u32[]{:S(2)}) copy-start(bf16[768,1536]{1,0:T(8,128)(2,1)} %w_middle_ref.1) | copy-start | bytes 7077892
  0.6 19.2 %collective-permute-start = (bf16[663,1536]{1,0:T(8,128)(2,1)}, bf16[663,1536]{1,0:T(8,128)(2,1)}, u32[]{:S(2)}, u32[]{:S(2)}) collective-permute-start(bf16[663,1536]{1,0:T(8,128)(2,1)} %bitcast.30), channel_id=1, source_target_pairs={{0,17},{17,0},{1,16},{16,1},{4,21},{21,4},{5,20},{20,5},{8,25},{25... | collective-permute-start | bytes 6110216 | tf_op jit(solution)/shard_map/ppermute | solution.py:254
  7.6 2.2 %copy-start.3 = (bf16[256,768]{1,0:T(8,128)(2,1)}, bf16[256,768]{1,0:T(8,128)(2,1)S(1)}, u32[]{:S(2)}) copy-start(bf16[256,768]{1,0:T(8,128)(2,1)S(1)} %get-tuple-element.123.act_first_ref) | copy-start | bytes 1179652
  7.6 7.5 %copy-start.9 = (s32[2]{0:T(128)S(1)}, s32[2]{0:T(128)}, u32[]{:S(2)}) copy-start(s32[2]{0:T(128)} %param.8) | copy-start | bytes 28
  9.8 16.9 %collective-permute-start.1 = (bf16[256,1536]{1,0:T(8,128)(2,1)}, bf16[256,1536]{1,0:T(8,128)(2,1)}, u32[]{:S(2)}, u32[]{:S(2)}) collective-permute-start(bf16[256,1536]{1,0:T(8,128)(2,1)} %get-tuple-element.125), channel_id=1, source_target_pairs={{0,1},{1,0},{2,3},{3,2},{4,5},{5,4},{6,7},{7,6},{8,9},{9,8},{10,11... | collective-permute-start | bytes 2359304 | tf_op jit(solution)/shard_map/ppermute | solution.py:31
  19.9 17.2 %collective-permute-start.2 = (bf16[663,1536]{1,0:T(8,128)(2,1)}, bf16[663,1536]{1,0:T(8,128)(2,1)}, u32[]{:S(2)}, u32[]{:S(2)}) collective-permute-start(bf16[663,1536]{1,0:T(8,128)(2,1)} %collective-permute-done.fetched_ref), channel_id=1, source_target_pairs={{0,2},{1,3},{4,6},{5,7},{8,10},{9,11},{12,14},{13,15},{16,18},{17,... | collective-permute-start | bytes 6110216 | tf_op jit(solution)/shard_map/ppermute | solution.py:279
  26.7 1.4 %copy-start.1 = (f32[256,1536]{1,0:T(8,128)S(1)}, f32[256,1536]{1,0:T(8,128)}, u32[]{:S(2)}) copy-start(f32[256,1536]{1,0:T(8,128)} %get-tuple-element.126.partial_ref) | copy-start | bytes 4718596
  28.1 1.0 copy-start.6
  29.1 1.6 %copy-start.7 = (bf16[1536,663]{0,1:T(8,128)(2,1)S(1)}, bf16[1536,663]{0,1:T(8,128)(2,1)}, u32[]{:S(2)}) copy-start(bf16[1536,663]{0,1:T(8,128)(2,1)} %param.11) | copy-start | bytes 6110212
  30.7 6.4 %copy-start.2 = (f32[768,256]{1,0:T(8,128)S(1)}, f32[768,256]{1,0:T(8,128)}, u32[]{:S(2)}) copy-start(f32[768,256]{1,0:T(8,128)} %copy.9.first_slope_ref) | copy-start | bytes 2359300
  30.7 6.4 %copy-start.5 = (bf16[663,256]{1,0:T(8,128)(2,1)S(1)}, bf16[663,256]{1,0:T(8,128)(2,1)}, u32[]{:S(2)}) copy-start(bf16[663,256]{1,0:T(8,128)(2,1)} %get-tuple-element.70.target_ref) | copy-start | bytes 1018372
  30.7 6.4 %copy-start.8 = (bf16[256,2652]{0,1:T(8,128)(2,1)S(1)}, bf16[256,2652]{0,1:T(8,128)(2,1)}, u32[]{:S(2)}) copy-start(bf16[256,2652]{0,1:T(8,128)(2,1)} %param.6) | copy-start | bytes 4073476
  37.1 14.3 %copy-start.4 = (bf16[256,768]{1,0:T(8,128)(2,1)S(1)}, bf16[256,768]{1,0:T(8,128)(2,1)}, u32[]{:S(2)}) copy-start(bf16[256,768]{1,0:T(8,128)(2,1)} %copy-done.3) | copy-start | bytes 1179652
  43.8 11.4 %collective-permute-start.3 = (bf16[16,7,24,384]{3,2,1,0:T(8,128)(2,1)S(1)}, bf16[16,7,24,384]{3,2,1,0:T(8,128)(2,1)S(1)}, u32[]{:S(2)}, u32[]{:S(2)}) collective-permute-start(bf16[16,7,24,384]{3,2,1,0:T(8,128)(2,1)S(1)} %get-tuple-element.75), channel_id=1, source_target_pairs={{0,2},{2,0},{1,3},{3,1},{4,6},{6,4},{5,7},{7,5},{8,10},{10,8},{9,1... | collective-permute-start | bytes 6193160 | tf_op jit(solution)/shard_map/ppermute | solution.py:31
  54.0 4.8 %collective-permute-start.6 = (bf16[16,8,24,384]{3,2,1,0:T(8,128)(2,1)S(1)}, bf16[16,8,24,384]{3,2,1,0:T(8,128)(2,1)S(1)}, u32[]{:S(2)}, u32[]{:S(2)}) collective-permute-start(bf16[16,8,24,384]{3,2,1,0:T(8,128)(2,1)S(1)} %get-tuple-element.83), channel_id=1, source_target_pairs={{0,2},{2,0},{1,3},{3,1},{4,6},{6,4},{5,7},{7,5},{8,10},{10,8},{9,1... | collective-permute-start | bytes 7077896 | tf_op jit(solution)/shard_map/ppermute | solution.py:31
  57.1 18.1 %collective-permute-start.4 = (bf16[2,4,4,24,384]{4,3,2,1,0:T(8,128)(2,1)S(1)}, bf16[2,4,4,24,384]{4,3,2,1,0:T(8,128)(2,1)S(1)}, u32[]{:S(2)}, u32[]{:S(2)}) collective-permute-start(bf16[2,4,4,24,384]{4,3,2,1,0:T(8,128)(2,1)S(1)} %get-tuple-element.77), channel_id=1, source_target_pairs={{0,32},{32,0},{64,96},{96,64},{1,33},{33,1},{65,97},{97,65},{2,34}... | collective-permute-start | bytes 1769480 | tf_op jit(solution)/shard_map/ppermute | solution.py:36
  59.9 15.3 %collective-permute-start.7 = (bf16[2,4,4,24,384]{4,3,2,1,0:T(8,128)(2,1)S(1)}, bf16[2,4,4,24,384]{4,3,2,1,0:T(8,128)(2,1)S(1)}, u32[]{:S(2)}, u32[]{:S(2)}) collective-permute-start(bf16[2,4,4,24,384]{4,3,2,1,0:T(8,128)(2,1)S(1)} %get-tuple-element.85), channel_id=1, source_target_pairs={{0,4},{4,0},{8,12},{12,8},{1,5},{5,1},{9,13},{13,9},{2,6},{6,2},{1... | collective-permute-start | bytes 1769480 | tf_op jit(solution)/shard_map/ppermute | solution.py:36
  61.2 15.5 %collective-permute-start.8 = (bf16[2,4,4,24,384]{4,3,2,1,0:T(8,128)(2,1)S(1)}, bf16[2,4,4,24,384]{4,3,2,1,0:T(8,128)(2,1)S(1)}, u32[]{:S(2)}, u32[]{:S(2)}) collective-permute-start(bf16[2,4,4,24,384]{4,3,2,1,0:T(8,128)(2,1)S(1)} %get-tuple-element.87), channel_id=1, source_target_pairs={{0,12},{4,8},{8,4},{12,0},{1,13},{5,9},{9,5},{13,1},{2,14},{6,10},... | collective-permute-start | bytes 1769480 | tf_op jit(solution)/shard_map/ppermute | solution.py:36
  63.0 12.2 %collective-permute-start.5 = (bf16[2,4,3,24,384]{4,3,2,1,0:T(8,128)(2,1)S(1)}, bf16[2,4,3,24,384]{4,3,2,1,0:T(8,128)(2,1)S(1)}, u32[]{:S(2)}, u32[]{:S(2)}) collective-permute-start(bf16[2,4,3,24,384]{4,3,2,1,0:T(8,128)(2,1)S(1)} %get-tuple-element.79), channel_id=1, source_target_pairs={{0,96},{32,64},{64,32},{96,0},{1,97},{33,65},{65,33},{97,1},{2,98}... | collective-permute-start | bytes 1327112 | tf_op jit(solution)/shard_map/ppermute | solution.py:36
  77.1 9.8 %collective-permute-start.9 = (bf16[4,4,24,384]{3,2,1,0:T(8,128)(2,1)S(1)}, bf16[4,4,24,384]{3,2,1,0:T(8,128)(2,1)S(1)}, u32[]{:S(2)}, u32[]{:S(2)}) collective-permute-start(bf16[4,4,24,384]{3,2,1,0:T(8,128)(2,1)S(1)} %get-tuple-element.89), channel_id=1, source_target_pairs={{0,96},{32,64},{64,32},{96,0},{1,97},{33,65},{65,33},{97,1},{2,98}... | collective-permute-start | bytes 884744 | tf_op jit(solution)/shard_map/ppermute | solution.py:36
  80.0 8.2 %collective-permute-start.11 = (bf16[4,4,24,384]{3,2,1,0:T(8,128)(2,1)S(1)}, bf16[4,4,24,384]{3,2,1,0:T(8,128)(2,1)S(1)}, u32[]{:S(2)}, u32[]{:S(2)}) collective-permute-start(bf16[4,4,24,384]{3,2,1,0:T(8,128)(2,1)S(1)} %get-tuple-element.93), channel_id=1, source_target_pairs={{0,12},{4,8},{8,4},{12,0},{1,13},{5,9},{9,5},{13,1},{2,14},{6,10},... | collective-permute-start | bytes 884744 | tf_op jit(solution)/shard_map/ppermute | solution.py:36
  81.8 6.7 %collective-permute-start.12 = (bf16[4,4,24,384]{3,2,1,0:T(8,128)(2,1)S(1)}, bf16[4,4,24,384]{3,2,1,0:T(8,128)(2,1)S(1)}, u32[]{:S(2)}, u32[]{:S(2)}) collective-permute-start(bf16[4,4,24,384]{3,2,1,0:T(8,128)(2,1)S(1)} %get-tuple-element.95), channel_id=1, source_target_pairs={{0,4},{4,0},{8,12},{12,8},{1,5},{5,1},{9,13},{13,9},{2,6},{6,2},{1... | collective-permute-start | bytes 884744 | tf_op jit(solution)/shard_map/ppermute | solution.py:36
  81.8 5.1 %collective-permute-start.10 = (bf16[4,3,24,384]{3,2,1,0:T(8,128)(2,1)S(1)}, bf16[4,3,24,384]{3,2,1,0:T(8,128)(2,1)S(1)}, u32[]{:S(2)}, u32[]{:S(2)}) collective-permute-start(bf16[4,3,24,384]{3,2,1,0:T(8,128)(2,1)S(1)} %get-tuple-element.91), channel_id=1, source_target_pairs={{0,32},{32,0},{64,96},{96,64},{1,33},{33,1},{65,97},{97,65},{2,34}... | collective-permute-start | bytes 663560 | tf_op jit(solution)/shard_map/ppermute | solution.py:36
  89.4 5.8 %collective-permute-start.13 = (bf16[2,4,24,384]{3,2,1,0:T(8,128)(2,1)S(1)}, bf16[2,4,24,384]{3,2,1,0:T(8,128)(2,1)S(1)}, u32[]{:S(2)}, u32[]{:S(2)}) collective-permute-start(bf16[2,4,24,384]{3,2,1,0:T(8,128)(2,1)S(1)} %get-tuple-element.97), channel_id=1, source_target_pairs={{0,4},{4,0},{8,12},{12,8},{1,5},{5,1},{9,13},{13,9},{2,6},{6,2},{1... | collective-permute-start | bytes 442376 | tf_op jit(solution)/shard_map/ppermute | solution.py:36
  89.8 5.5 %collective-permute-start.15 = (bf16[2,4,24,384]{3,2,1,0:T(8,128)(2,1)S(1)}, bf16[2,4,24,384]{3,2,1,0:T(8,128)(2,1)S(1)}, u32[]{:S(2)}, u32[]{:S(2)}) collective-permute-start(bf16[2,4,24,384]{3,2,1,0:T(8,128)(2,1)S(1)} %get-tuple-element.101), channel_id=1, source_target_pairs={{0,32},{32,0},{64,96},{96,64},{1,33},{33,1},{65,97},{97,65},{2,34}... | collective-permute-start | bytes 442376 | tf_op jit(solution)/shard_map/ppermute | solution.py:36
  89.8 5.5 %collective-permute-start.16 = (bf16[2,4,24,384]{3,2,1,0:T(8,128)(2,1)S(1)}, bf16[2,4,24,384]{3,2,1,0:T(8,128)(2,1)S(1)}, u32[]{:S(2)}, u32[]{:S(2)}) collective-permute-start(bf16[2,4,24,384]{3,2,1,0:T(8,128)(2,1)S(1)} %get-tuple-element.103), channel_id=1, source_target_pairs={{0,96},{32,64},{64,32},{96,0},{1,97},{33,65},{65,33},{97,1},{2,98}... | collective-permute-start | bytes 442376 | tf_op jit(solution)/shard_map/ppermute | solution.py:36
  90.4 4.8 %collective-permute-start.14 = (bf16[2,3,24,384]{3,2,1,0:T(8,128)(2,1)S(1)}, bf16[2,3,24,384]{3,2,1,0:T(8,128)(2,1)S(1)}, u32[]{:S(2)}, u32[]{:S(2)}) collective-permute-start(bf16[2,3,24,384]{3,2,1,0:T(8,128)(2,1)S(1)} %get-tuple-element.99), channel_id=1, source_target_pairs={{0,12},{4,8},{8,4},{12,0},{1,13},{5,9},{9,5},{13,1},{2,14},{6,10},... | collective-permute-start | bytes 331784 | tf_op jit(solution)/shard_map/ppermute | solution.py:36
  95.4 6.8 %collective-permute-start.17 = (bf16[4,24,384]{2,1,0:T(8,128)(2,1)S(1)}, bf16[4,24,384]{2,1,0:T(8,128)(2,1)S(1)}, u32[]{:S(2)}, u32[]{:S(2)}) collective-permute-start(bf16[4,24,384]{2,1,0:T(8,128)(2,1)S(1)} %get-tuple-element.105), channel_id=1, source_target_pairs={{0,12},{4,8},{8,4},{12,0},{1,13},{5,9},{9,5},{13,1},{2,14},{6,10},... | collective-permute-start | bytes 221192 | tf_op jit(solution)/shard_map/ppermute | solution.py:36
  96.8 5.4 %collective-permute-start.19 = (bf16[4,24,384]{2,1,0:T(8,128)(2,1)S(1)}, bf16[4,24,384]{2,1,0:T(8,128)(2,1)S(1)}, u32[]{:S(2)}, u32[]{:S(2)}) collective-permute-start(bf16[4,24,384]{2,1,0:T(8,128)(2,1)S(1)} %get-tuple-element.109), channel_id=1, source_target_pairs={{0,96},{32,64},{64,32},{96,0},{1,97},{33,65},{65,33},{97,1},{2,98}... | collective-permute-start | bytes 221192 | tf_op jit(solution)/shard_map/ppermute | solution.py:36
  99.2 3.2 %collective-permute-start.20 = (bf16[4,24,384]{2,1,0:T(8,128)(2,1)S(1)}, bf16[4,24,384]{2,1,0:T(8,128)(2,1)S(1)}, u32[]{:S(2)}, u32[]{:S(2)}) collective-permute-start(bf16[4,24,384]{2,1,0:T(8,128)(2,1)S(1)} %get-tuple-element.111), channel_id=1, source_target_pairs={{0,32},{32,0},{64,96},{96,64},{1,33},{33,1},{65,97},{97,65},{2,34}... | collective-permute-start | bytes 221192 | tf_op jit(solution)/shard_map/ppermute | solution.py:36
  99.2 3.0 %collective-permute-start.18 = (bf16[3,24,384]{2,1,0:T(8,128)(2,1)S(1)}, bf16[3,24,384]{2,1,0:T(8,128)(2,1)S(1)}, u32[]{:S(2)}, u32[]{:S(2)}) collective-permute-start(bf16[3,24,384]{2,1,0:T(8,128)(2,1)S(1)} %get-tuple-element.107), channel_id=1, source_target_pairs={{0,4},{4,0},{8,12},{12,8},{1,5},{5,1},{9,13},{13,9},{2,6},{6,2},{1... | collective-permute-start | bytes 165896 | tf_op jit(solution)/shard_map/ppermute | solution.py:36
  103.0 5.6 %collective-permute-start.21 = (bf16[8,24,384]{2,1,0:T(8,128)(2,1)S(1)}, bf16[8,24,384]{2,1,0:T(8,128)(2,1)S(1)}, u32[]{:S(2)}, u32[]{:S(2)}) collective-permute-start(bf16[8,24,384]{2,1,0:T(8,128)(2,1)S(1)} %get-tuple-element.113), channel_id=1, source_target_pairs={{0,16},{16,0},{1,17},{17,1},{2,18},{18,2},{3,19},{19,3},{4,20},{20... | collective-permute-start | bytes 442376 | tf_op jit(solution)/shard_map/ppermute | solution.py:31

commit v6 on v5

--- a/solution.py
+++ b/solution.py
@@ -1,5 +1,6 @@
 import jax
 import jax.numpy as jnp
+import numpy as np
 from jax import lax
 from jax.experimental import pallas as pl
 from jax.experimental.pallas import tpu as pltpu
@@ -16,6 +17,7 @@
 ROWS, COLS = 24, 384
 VMEM = pl.BlockSpec(memory_space=pltpu.VMEM)
 SMEM = pl.BlockSpec(memory_space=pltpu.SMEM)
+HBM = pl.BlockSpec(memory_space=pl.ANY)
 BF16, F32 = jnp.bfloat16, jnp.float32
 
 
@@ -37,7 +39,7 @@
 
 
 def silu_slope(pre_act):
-    sigmoid_of = jax.nn.sigmoid(pre_act)
+    sigmoid_of = 1.0 / (1.0 + jnp.exp(-pre_act))
     return sigmoid_of * (1.0 + pre_act * (1.0 - sigmoid_of))
 
 
@@ -85,11 +87,48 @@
                 )
 
 
+def forward_kernel(
+    belief_ref, w_first_ref, w_middle_ref, pre_first_ref, act_first_ref, sent_ref
+):
+    pre_first = contract(belief_ref[...], w_first_ref[...], 0, 0)
+    pre_first_ref[...] = pre_first
+    act_first = narrow(pre_first / (1.0 + jnp.exp(-pre_first)))
+    act_first_ref[...] = act_first
+    sent_ref[...] = narrow(dot(act_first, w_middle_ref[...]))
+
+
+def stage_kernel(
+    place_ref, counts_ref, pre_first_ref, orders_ref, target_hbm, w_last_hbm,
+    w_own_ref, target_own_ref, target_other_ref, first_slope_ref, onehot_ref, live_ref,
+    target_ref, sems,
+):
+    copies = (
+        pltpu.make_async_copy(target_hbm, target_ref, sems.at[0]),
+        pltpu.make_async_copy(w_last_hbm, w_own_ref, sems.at[1]),
+    )
+    for copy in copies:
+        copy.start()
+    first_slope_ref[...] = silu_slope(pre_first_ref[...])
+    order = jnp.where(place_ref[0] == 0, orders_ref[0], orders_ref[1])
+    units = lax.broadcasted_iota(jnp.int32, onehot_ref.shape, 1)
+    onehot_ref[...] = jnp.where(order == units, 1.0, 0.0).astype(BF16)
+    row = lax.broadcasted_iota(jnp.int32, live_ref.shape, 1)
+    count = jnp.where(row < BLOCK, counts_ref[0], counts_ref[1] + BLOCK)
+    live_ref[...] = jnp.where(row < count, 1.0, 0.0)
+    copies[0].wait()
+    width = target_own_ref.shape[0]
+    low, high = target_ref[0:width, :], target_ref[width : 2 * width, :]
+    is_low = place_ref[4] == 0
+    target_own_ref[...] = jnp.where(is_low, low, high)
+    target_other_ref[...] = jnp.where(is_low, high, low)
+    copies[1].wait()
+
+
 def hidden_kernel(
     partial_ref, arrived_ref, live_ref, target_ref, w_ref,
     act_ref, act_slope_ref, slope_ref, back_ref,
 ):
-    pre_middle = partial_ref[...] + wide(arrived_ref[...])
+    pre_middle = wide(partial_ref[...]) + wide(arrived_ref[...])
     sigmoid_of = 1.0 / (1.0 + jnp.exp(-pre_middle))
     act = narrow(pre_middle * sigmoid_of)
     act_ref[...] = act
@@ -114,8 +153,8 @@
     back = back_ref[...] + contract(slope, w_other, 0, 0)
     slope_middle = narrow(back * act_slope_ref[...])
     slope_middle_ref[...] = slope_middle
-    slope_first = narrow(contract(w_middle_ref[...], slope_middle, 1, 1) * first_slope_ref[...])
-    slope_first = narrow(dot(onehot_ref[...], slope_first))
+    slope_first = narrow(contract(slope_middle, w_middle_ref[...], 1, 1) * first_slope_ref[...])
+    slope_first = narrow(contract(onehot_ref[...], slope_first, 1, 1))
     slope_first_ref[...] = slope_first
     half = slope_first.shape[0] // 2
     for start, stop in column_cuts(belief_ref.shape[0]):
@@ -253,29 +292,38 @@
     around = (ZH, CORE, "mp")
     fetched = lax.ppermute(w_last_t, around, [(0, 5), (5, 0), (1, 4), (4, 1)])
 
-    pre_first = dot(belief, w_first)
-    act_first = narrow(jax.nn.silu(pre_first))
-    partial_middle = dot(act_first, w_middle)
-    hidden_sent = narrow(partial_middle)
+    indices = (CORE, Y, X, ZH, "mp")
+    place = jnp.stack([lax.axis_index(axis) for axis in indices])
+    pre_first, act_first, hidden_sent = call(
+        forward_kernel,
+        "forward",
+        [VMEM] * 3,
+        [
+            ((total_rows, units), F32),
+            ((total_rows, units), BF16),
+            ((total_rows, hidden), BF16),
+        ],
+        final=True,
+    )(belief_t, w_first, w_middle)
     arrived = swap(hidden_sent, "mp")
 
-    indices = jnp.stack([lax.axis_index(axis) for axis in (CORE, Y, X, ZH, "mp")])
-    indices, pre_first, target_value, hidden_sent = lax.optimization_barrier(
-        (indices, pre_first, target_value, hidden_sent)
-    )
-    core, mp = indices[0], indices[4]
-    live_rows = (counts[:, None] > jnp.arange(BLOCK, dtype=jnp.int32)[None, :]).reshape(1, total_rows)
-    live = live_rows.astype(F32)
-    target_t = target_value.T
-    target_own = lax.dynamic_slice_in_dim(target_t, mp * width, width, 0)
-    target_other = lax.dynamic_slice_in_dim(target_t, (1 - mp) * width, width, 0)
-    order = jnp.arange(units, dtype=jnp.int32).reshape(4, 2, 4, 2, -1).transpose(3, 0, 2, 1, 4)
-    order = jnp.where(core == 0, order[::-1], order).reshape(units)
-    onehot = (order[:, None] == jnp.arange(units, dtype=jnp.int32)[None, :]).astype(BF16)
-    first_slope = silu_slope(pre_first).T
-    fetched, place, live, target_own, target_other, onehot, first_slope = lax.optimization_barrier(
-        (fetched, indices[:4], live, target_own, target_other, onehot, first_slope)
-    )
+    order = np.arange(units, dtype=np.int32).reshape(4, 2, 4, 2, -1).transpose(3, 0, 2, 1, 4)
+    orders = np.stack([order[::-1], order]).reshape(2, units, 1)
+    w_own, target_own, target_other, first_slope, onehot, live = call(
+        stage_kernel,
+        "stage",
+        [SMEM, SMEM, VMEM, VMEM, HBM, HBM],
+        [
+            ((width, hidden), BF16),
+            ((width, total_rows), BF16),
+            ((width, total_rows), BF16),
+            ((total_rows, units), F32),
+            ((units, units), BF16),
+            ((1, total_rows), F32),
+        ],
+        [pltpu.VMEM((2 * width, total_rows), BF16), pltpu.SemaphoreType.DMA((2,))],
+    )(place, counts, pre_first, jnp.asarray(orders), target_value.T, w_last_t)
+    fetched, live = lax.optimization_barrier((fetched, live))
     relayed = lax.ppermute(fetched, CORE, [(0, 1)])
 
     act, act_slope, slope_own, back_own = call(
@@ -288,7 +336,7 @@
             ((width, total_rows), BF16),
             ((total_rows, hidden), F32),
         ],
-    )(partial_middle, arrived, live, target_own, w_last_t)
+    )(hidden_sent, arrived, live, target_own, w_own)
 
     slope_middle, slope_first, first_sent = call(
         slopes_kernel,

time: 134 us -> 126 us (0.940)
  matrix products: 7 us -> 0 us
  starting transfers between devices: 33.6 us -> 28.5 us
  waiting for transfers between devices: 35.4 us -> 40.2 us
  Pallas kernels: 19.1 us -> 23.4 us
  other arithmetic: 2.73 us -> 0 us
  between operations: 2.75 us -> 0.77 us
    dot_general x2 -> x0, matrix products: 7 us -> none  [dot(): return jnp.dot(left, right, preferred_element_type=F32)]
    unnamed x20 -> x26, local copies, waits for them, and re-layouts: 3.98 us -> 9.09 us
    ppermute x4, starting transfers between devices: 12.1 us -> 7.34 us  [swap(): return lax.ppermute(shard, axis, [(0, 1), (1, 0)])]
    pallas_call x11 -> x13, Pallas kernels: 19.1 us -> 23.4 us  [run(): kernel(*(pltpu.with_memory_space_constraint(operand, pltpu.VMEM) if spec...]
    ppermute x4, waiting for transfers between devices: 8.37 us -> 11.9 us  [swap(): return lax.ppermute(shard, axis, [(0, 1), (1, 0)])]
    transpose x1 -> x0, other arithmetic: 2.38 us -> none  [per_device(): first_slope = silu_slope(pre_first).T]
    optimization_barrier x1 -> x0, local copies, waits for them, and re-layouts: 2.37 us -> none  [per_device(): lax.optimization_barrier((fetched, indices[:4], live, target_own, target_...]
    dynamic_slice x1 -> x0, local copies, waits for them, and re-layouts: 2.09 us -> none  [per_device(): lax.dynamic_slice_in_dim(target_t, (1 - mp) * width, width, 0)]
  transfers between devices with their start and end apart: 22 -> 22, of which waited for: 13 -> 12; matrix products, arithmetic and copies ran while one was open for 11% -> 0% of each run, Pallas kernels for 7% -> 11%
where the time goes in v6:
time: 126 us
  waiting for transfers between devices  40.2 us (32%)
  starting transfers between devices  28.5 us (23%)
  blocking collectives  23.9 us (19%)
  Pallas kernels  23.4 us (19%)
  local copies, waits for them, and re-layouts  9.17 us (7%)
    ppermute x16, waiting for transfers between devices, to_pair(): return lax.ppermute(shard, axis, pairs)  24.1 us
    all_to_all x1, blocking collectives, per_device(): squares = lax.all_to_all(squares, ALL, 0, 0, tiled=True)  23.9 us
    pallas_call x13, Pallas kernels, run(): kernel(*(pltpu.with_memory_space_constraint(operand, pltpu.VMEM) if spec...  23.4 us
    ppermute x16, starting transfers between devices, to_pair(): return lax.ppermute(shard, axis, pairs)  17.9 us
    ppermute x4, waiting for transfers between devices, swap(): return lax.ppermute(shard, axis, [(0, 1), (1, 0)])  11.9 us
    unnamed x26, local copies, waits for them, and re-layouts  9.09 us
    ppermute x4, starting transfers between devices, swap(): return lax.ppermute(shard, axis, [(0, 1), (1, 0)])  7.34 us
    ppermute x1, waiting for transfers between devices, per_device(): relayed = lax.ppermute(fetched, CORE, [(0, 1)])  4.26 us
  transfers between devices with their start and end apart: 22, of which 12 were waited for; matrix products, arithmetic and copies ran while one was open for 0% of the time, Pallas kernels for 11%

profile of v6, /device:TPU:1, one launch (start us, length us, event | category | flops | bytes accessed | tf_op | source)
XLA Modules:
  0.0 125.8 jit_solution(10722981825470921335)
XLA Ops:
  0.6 2.0 %collective-permute-start.1 = (bf16[663,1536]{1,0:T(8,128)(2,1)}, bf16[663,1536]{1,0:T(8,128)(2,1)}, u32[]{:S(2)}, u32[]{:S(2)}) collective-permute-start(bf16[663,1536]{1,0:T(8,128)(2,1)} %bitcast.10), channel_id=1, source_target_pairs={{0,17},{17,0},{1,16},{16,1},{4,21},{21,4},{5,20},{20,5},{8,25},{25... | collective-permute-start | bytes 6110216 | tf_op jit(solution)/shard_map/ppermute | solution.py:293
  2.6 2.2 %copy-done = bf16[2652,768]{1,0:T(8,128)(2,1)S(1)} copy-done((bf16[2652,768]{1,0:T(8,128)(2,1)S(1)}, bf16[2652,768]{1,0:T(8,128)(2,1)}, u32[]{:S(2)}) %copy-start) | copy-done | bytes 4073496
  4.8 1.7 %copy-done.1 = bf16[768,1536]{1,0:T(8,128)(2,1)S(1)} copy-done((bf16[768,1536]{1,0:T(8,128)(2,1)S(1)}, bf16[768,1536]{1,0:T(8,128)(2,1)}, u32[]{:S(2)}) %copy-start.1) | copy-done | bytes 2359320
  6.5 1.3 %copy-done.4 = bf16[256,2652]{0,1:T(8,128)(2,1)S(1)} copy-done((bf16[256,2652]{0,1:T(8,128)(2,1)S(1)}, bf16[256,2652]{0,1:T(8,128)(2,1)}, u32[]{:S(2)}) %copy-start.4) | copy-done | bytes 1357848
  7.8 2.7 %forward.1 = (f32[256,768]{1,0:T(8,128)S(1)}, bf16[256,768]{1,0:T(8,128)(2,1)S(1)}, bf16[256,1536]{1,0:T(8,128)(2,1)S(1)}) custom-call(bf16[2652,256]{1,0:T(8,128)(2,1)S(1)} %bitcast.12, bf16[2652,768]{1,0:T(8,128)(2,1)S(1)} %copy-done, bf16[768,1536]{1,0:T(8,128)(2,1)S(1)} %copy-done.1), custom_call_target="tpu_custom_call" | custom-call | flops 17179869184 | bytes 67108864 | tf_op jit(solution)/shard_map/forward/pallas_call | solution.py:69
  10.5 0.9 copy-done.9
  11.4 0.8 copy-done.11
  12.1 2.5 %collective-permute-start = (bf16[256,1536]{1,0:T(8,128)(2,1)S(1)}, bf16[256,1536]{1,0:T(8,128)(2,1)}, u32[]{:S(2)}, u32[]{:S(2)}) collective-permute-start(bf16[256,1536]{1,0:T(8,128)(2,1)S(1)} %get-tuple-element.62.partial_ref), channel_id=1, source_target_pairs={{0,1},{1,0},{2,3},{3,2},{4,5},{5,4},{6,7},{7,6},{8,9},{9,8},{10,11... | collective-permute-start | bytes 2359304 | tf_op jit(solution)/shard_map/ppermute | solution.py:33
  14.6 0.1 stack.23.place_ref
  14.7 0.0 copy-start.8
  14.7 1.1 copy-done.8
  15.8 1.1 copy-done.10
  17.0 2.2 %stage.1 = (bf16[663,1536]{1,0:T(8,128)(2,1)S(1)}, bf16[663,256]{1,0:T(8,128)(2,1)S(1)}, bf16[663,256]{1,0:T(8,128)(2,1)S(1)}, f32[256,768]{1,0:T(8,128)S(1)}, b...) custom-call(s32[5]{0:T(128)S(1)} %stack.23.place_ref, s32[2]{0:T(128)S(1)} %copy-done.7, f32[256,768]{1,0:T(8,128)S(1)} %copy-done.10, ...), custom_call_target="tpu_custom_call" | custom-call | flops 17179869184 | bytes 67108864 | tf_op jit(solution)/shard_map/stage/pallas_call | solution.py:69
  19.2 0.0 collective-permute-done.1.fetched_ref
  19.2 1.3 %collective-permute-start.2 = (bf16[663,1536]{1,0:T(8,128)(2,1)}, bf16[663,1536]{1,0:T(8,128)(2,1)S(1)}, u32[]{:S(2)}, u32[]{:S(2)}) collective-permute-start(bf16[663,1536]{1,0:T(8,128)(2,1)} %collective-permute-done.1.fetched_ref), channel_id=1, source_target_pairs={{0,2},{1,3},{4,6},{5,7},{8,10},{9,11},{12,14},{13,15},{16,18},{17,... | collective-permute-start | bytes 6110216 | tf_op jit(solution)/shard_map/ppermute | solution.py:327
  20.5 8.3 %collective-permute-done.arrived_ref = bf16[256,1536]{1,0:T(8,128)(2,1)} collective-permute-done((bf16[256,1536]{1,0:T(8,128)(2,1)S(1)}, bf16[256,1536]{1,0:T(8,128)(2,1)}, u32[]{:S(2)}, u32[]{:S(2)}) %collective-permute-start) | collective-permute-done | bytes 786464 | tf_op jit(solution)/shard_map/ppermute | solution.py:33
  28.8 3.8 %hidden.1 = (bf16[256,1536]{1,0:T(8,128)(2,1)S(1)}, f32[256,1536]{1,0:T(8,128)S(1)}, bf16[663,256]{1,0:T(8,128)(2,1)S(1)}, f32[256,1536]{1,0:T(8,128)S(1)}) custom-call(bf16[256,1536]{1,0:T(8,128)(2,1)S(1)} %get-tuple-element.62.partial_ref, bf16[256,1536]{1,0:T(8,128)(2,1)} %collective-permute-done.arrived_ref, f32[1,256]{1,0:T(1,128)S(1)} %get-tuple-element.65.live_ref, ...), custom_call_target="tpu_custom_call" | custom-call | flops 17179869184 | bytes 67108864 | tf_op jit(solution)/shard_map/hidden/pallas_call | solution.py:69
  32.6 4.3 %collective-permute-done.2.relayed_ref = bf16[663,1536]{1,0:T(8,128)(2,1)S(1)} collective-permute-done((bf16[663,1536]{1,0:T(8,128)(2,1)}, bf16[663,1536]{1,0:T(8,128)(2,1)S(1)}, u32[]{:S(2)}, u32[]{:S(2)}) %collective-permute-start.2) | collective-permute-done | bytes 2036768 | tf_op jit(solution)/shard_map/ppermute | solution.py:327
  36.8 6.0 %slopes.1 = (bf16[256,1536]{1,0:T(8,128)(2,1)S(1)}, bf16[768,256]{1,0:T(8,128)(2,1)S(1)}, bf16[16,7,24,384]{3,2,1,0:T(8,128)(2,1)S(1)}) custom-call(s32[5]{0:T(128)S(1)} %stack.23.place_ref, bf16[256,1536]{1,0:T(8,128)(2,1)S(1)} %get-tuple-element.68.act_ref, f32[256,1536]{1,0:T(8,128)S(1)} %get-tuple-element.69.act_slope_ref, ...), custom_call_target="tpu_custom_call" | custom-call | flops 17179869184 | bytes 67108864 | tf_op jit(solution)/shard_map/slopes/pallas_call | solution.py:69
  42.9 0.3 collective-permute-start.3
  43.2 2.5 %later.1 = (bf16[16,8,24,384]{3,2,1,0:T(8,128)(2,1)S(1)}, bf16[16,8,24,384]{3,2,1,0:T(8,128)(2,1)S(1)}) custom-call(s32[5]{0:T(128)S(1)} %stack.23.place_ref, bf16[256,1536]{1,0:T(8,128)(2,1)S(1)} %get-tuple-element.68.act_ref, bf16[663,256]{1,0:T(8,128)(2,1)S(1)} %get-tuple-element.81.slope_ref, bf16[256,1536]{1,0:T(8,128)(2,1)S(1)} %get-tuple-element.82.slope_middle_ref, ...), custom_call_target="tpu_custom_call" | custom-call | flops 17179869184 | bytes 67108864 | tf_op jit(solution)/shard_map/later/pallas_call | solution.py:69
  45.8 0.5 collective-permute-start.6
  46.3 0.8 collective-permute-done.3.arrived_ref
  47.1 1.8 %cut_first.1 = (f32[2,4,4,24,384]{4,3,2,1,0:T(8,128)S(1)}, bf16[2,4,4,24,384]{4,3,2,1,0:T(8,128)(2,1)S(1)}, f32[2,4,3,24,384]{4,3,2,1,0:T(8,128)S(1)}, bf16[2,4,3,24,384]{4,3,2,1,0:T(8,128)(2,1)S(1)}) custom-call(s32[5]{0:T(128)S(1)} %stack.23.place_ref, bf16[768,256]{1,0:T(8,128)(2,1)S(1)} %get-tuple-element.75.slope_first_ref, ...), custom_call_target="tpu_custom_call" | custom-call | flops 17179869184 | bytes 67108864 | tf_op jit(solution)/shard_map/cut_first/pallas_call | solution.py:69
  48.9 1.4 %collective-permute-start.4 = (bf16[2,4,4,24,384]{4,3,2,1,0:T(8,128)(2,1)S(1)}, bf16[2,4,4,24,384]{4,3,2,1,0:T(8,128)(2,1)S(1)}, u32[]{:S(2)}, u32[]{:S(2)}) collective-permute-start(bf16[2,4,4,24,384]{4,3,2,1,0:T(8,128)(2,1)S(1)} %get-tuple-element.78), channel_id=1, source_target_pairs={{0,32},{32,0},{64,96},{96,64},{1,33},{33,1},{65,97},{97,65},{2,34}... | collective-permute-start | bytes 1769480 | tf_op jit(solution)/shard_map/ppermute | solution.py:38
  50.3 0.2 collective-permute-done.6.arrived_ref
  50.6 1.1 cut_rest.1
  51.6 1.3 %collective-permute-start.7 = (bf16[2,4,4,24,384]{4,3,2,1,0:T(8,128)(2,1)S(1)}, bf16[2,4,4,24,384]{4,3,2,1,0:T(8,128)(2,1)S(1)}, u32[]{:S(2)}, u32[]{:S(2)}) collective-permute-start(bf16[2,4,4,24,384]{4,3,2,1,0:T(8,128)(2,1)S(1)} %get-tuple-element.87), channel_id=1, source_target_pairs={{0,4},{4,0},{8,12},{12,8},{1,5},{5,1},{9,13},{13,9},{2,6},{6,2},{1... | collective-permute-start | bytes 1769480 | tf_op jit(solution)/shard_map/ppermute | solution.py:38
  52.9 1.8 %collective-permute-start.8 = (bf16[2,4,4,24,384]{4,3,2,1,0:T(8,128)(2,1)S(1)}, bf16[2,4,4,24,384]{4,3,2,1,0:T(8,128)(2,1)S(1)}, u32[]{:S(2)}, u32[]{:S(2)}) collective-permute-start(bf16[2,4,4,24,384]{4,3,2,1,0:T(8,128)(2,1)S(1)} %get-tuple-element.89), channel_id=1, source_target_pairs={{0,12},{4,8},{8,4},{12,0},{1,13},{5,9},{9,5},{13,1},{2,14},{6,10},... | collective-permute-start | bytes 1769480 | tf_op jit(solution)/shard_map/ppermute | solution.py:38
  54.7 2.7 %collective-permute-start.5 = (bf16[2,4,3,24,384]{4,3,2,1,0:T(8,128)(2,1)S(1)}, bf16[2,4,3,24,384]{4,3,2,1,0:T(8,128)(2,1)S(1)}, u32[]{:S(2)}, u32[]{:S(2)}) collective-permute-start(bf16[2,4,3,24,384]{4,3,2,1,0:T(8,128)(2,1)S(1)} %get-tuple-element.80), channel_id=1, source_target_pairs={{0,96},{32,64},{64,32},{96,0},{1,97},{33,65},{65,33},{97,1},{2,98}... | collective-permute-start | bytes 1327112 | tf_op jit(solution)/shard_map/ppermute | solution.py:38
  57.5 9.4 %collective-permute-done.5.refs_3_ = bf16[2,4,3,24,384]{4,3,2,1,0:T(8,128)(2,1)S(1)} collective-permute-done((bf16[2,4,3,24,384]{4,3,2,1,0:T(8,128)(2,1)S(1)}, bf16[2,4,3,24,384]{4,3,2,1,0:T(8,128)(2,1)S(1)}, u32[]{:S(2)}, u32[]{:S(2)}) %collective-permute-start.5) | collective-permute-done | bytes 442400 | tf_op jit(solution)/shard_map/ppermute | solution.py:38
  66.9 0.0 collective-permute-done.4.refs_1_
  66.9 0.0 collective-permute-done.7.refs_5_
  66.9 1.5 %collective-permute-done.8.refs_7_ = bf16[2,4,4,24,384]{4,3,2,1,0:T(8,128)(2,1)S(1)} collective-permute-done((bf16[2,4,4,24,384]{4,3,2,1,0:T(8,128)(2,1)S(1)}, bf16[2,4,4,24,384]{4,3,2,1,0:T(8,128)(2,1)S(1)}, u32[]{:S(2)}, u32[]{:S(2)}) %collective-permute-start.8) | collective-permute-done | bytes 589856 | tf_op jit(solution)/shard_map/ppermute | solution.py:38
  68.4 0.4 halve.2
  68.9 2.8 %collective-permute-start.9 = (bf16[4,4,24,384]{3,2,1,0:T(8,128)(2,1)S(1)}, bf16[4,4,24,384]{3,2,1,0:T(8,128)(2,1)S(1)}, u32[]{:S(2)}, u32[]{:S(2)}) collective-permute-start(bf16[4,4,24,384]{3,2,1,0:T(8,128)(2,1)S(1)} %get-tuple-element.91), channel_id=1, source_target_pairs={{0,96},{32,64},{64,32},{96,0},{1,97},{33,65},{65,33},{97,1},{2,98}... | collective-permute-start | bytes 884744 | tf_op jit(solution)/shard_map/ppermute | solution.py:38
  71.7 1.8 %collective-permute-start.11 = (bf16[4,4,24,384]{3,2,1,0:T(8,128)(2,1)S(1)}, bf16[4,4,24,384]{3,2,1,0:T(8,128)(2,1)S(1)}, u32[]{:S(2)}, u32[]{:S(2)}) collective-permute-start(bf16[4,4,24,384]{3,2,1,0:T(8,128)(2,1)S(1)} %get-tuple-element.95), channel_id=1, source_target_pairs={{0,12},{4,8},{8,4},{12,0},{1,13},{5,9},{9,5},{13,1},{2,14},{6,10},... | collective-permute-start | bytes 884744 | tf_op jit(solution)/shard_map/ppermute | solution.py:38
  73.5 0.0 collective-permute-start.12
  73.5 0.0 collective-permute-start.10
  73.5 5.1 %collective-permute-done.10.refs_3_ = bf16[4,3,24,384]{3,2,1,0:T(8,128)(2,1)S(1)} collective-permute-done((bf16[4,3,24,384]{3,2,1,0:T(8,128)(2,1)S(1)}, bf16[4,3,24,384]{3,2,1,0:T(8,128)(2,1)S(1)}, u32[]{:S(2)}, u32[]{:S(2)}) %collective-permute-start.10) | collective-permute-done | bytes 221216 | tf_op jit(solution)/shard_map/ppermute | solution.py:38
  78.6 0.0 collective-permute-done.9.refs_1_
  78.6 1.1 collective-permute-done.11.refs_5_
  79.8 0.3 collective-permute-done.12.refs_7_
  80.1 0.9 turn.1
  81.0 0.4 collective-permute-start.13
  81.4 0.6 collective-permute-start.16
  82.0 1.3 %collective-permute-start.14 = (bf16[2,3,24,384]{3,2,1,0:T(8,128)(2,1)S(1)}, bf16[2,3,24,384]{3,2,1,0:T(8,128)(2,1)S(1)}, u32[]{:S(2)}, u32[]{:S(2)}) collective-permute-start(bf16[2,3,24,384]{3,2,1,0:T(8,128)(2,1)S(1)} %get-tuple-element.101), channel_id=1, source_target_pairs={{0,12},{4,8},{8,4},{12,0},{1,13},{5,9},{9,5},{13,1},{2,14},{6,10},... | collective-permute-start | bytes 331784 | tf_op jit(solution)/shard_map/ppermute | solution.py:38
  83.3 3.5 %collective-permute-done.14.refs_3_ = bf16[2,3,24,384]{3,2,1,0:T(8,128)(2,1)S(1)} collective-permute-done((bf16[2,3,24,384]{3,2,1,0:T(8,128)(2,1)S(1)}, bf16[2,3,24,384]{3,2,1,0:T(8,128)(2,1)S(1)}, u32[]{:S(2)}, u32[]{:S(2)}) %collective-permute-start.14) | collective-permute-done | bytes 110624 | tf_op jit(solution)/shard_map/ppermute | solution.py:38
  86.8 0.0 collective-permute-done.13.refs_1_
  86.8 0.0 collective-permute-done.15.refs_5_
  86.8 0.0 collective-permute-done.16.refs_7_
  86.8 0.1 halve.3
  86.9 1.4 %collective-permute-start.17 = (bf16[4,24,384]{2,1,0:T(8,128)(2,1)S(1)}, bf16[4,24,384]{2,1,0:T(8,128)(2,1)S(1)}, u32[]{:S(2)}, u32[]{:S(2)}) collective-permute-start(bf16[4,24,384]{2,1,0:T(8,128)(2,1)S(1)} %get-tuple-element.107), channel_id=1, source_target_pairs={{0,12},{4,8},{8,4},{12,0},{1,13},{5,9},{9,5},{13,1},{2,14},{6,10},... | collective-permute-start | bytes 221192 | tf_op jit(solution)/shard_map/ppermute | solution.py:38
  88.3 2.1 %collective-permute-start.19 = (bf16[4,24,384]{2,1,0:T(8,128)(2,1)S(1)}, bf16[4,24,384]{2,1,0:T(8,128)(2,1)S(1)}, u32[]{:S(2)}, u32[]{:S(2)}) collective-permute-start(bf16[4,24,384]{2,1,0:T(8,128)(2,1)S(1)} %get-tuple-element.111), channel_id=1, source_target_pairs={{0,96},{32,64},{64,32},{96,0},{1,97},{33,65},{65,33},{97,1},{2,98}... | collective-permute-start | bytes 221192 | tf_op jit(solution)/shard_map/ppermute | solution.py:38
  90.4 0.2 collective-permute-start.20
  90.6 3.0 %collective-permute-done.18.refs_3_ = bf16[3,24,384]{2,1,0:T(8,128)(2,1)S(1)} collective-permute-done((bf16[3,24,384]{2,1,0:T(8,128)(2,1)S(1)}, bf16[3,24,384]{2,1,0:T(8,128)(2,1)S(1)}, u32[]{:S(2)}, u32[]{:S(2)}) %collective-permute-start.18) | collective-permute-done | bytes 55328 | tf_op jit(solution)/shard_map/ppermute | solution.py:38
  93.6 0.0 collective-permute-done.17.refs_1_
  93.6 0.0 collective-permute-done.20.refs_7_
  93.6 0.6 z_cut.1
  94.3 4.0 %collective-permute-start.21 = (bf16[8,24,384]{2,1,0:T(8,128)(2,1)S(1)}, bf16[8,24,384]{2,1,0:T(8,128)(2,1)S(1)}, u32[]{:S(2)}, u32[]{:S(2)}) collective-permute-start(bf16[8,24,384]{2,1,0:T(8,128)(2,1)S(1)} %get-tuple-element.115), channel_id=1, source_target_pairs={{0,16},{16,0},{1,17},{17,1},{2,18},{18,2},{3,19},{19,3},{4,20},{20... | collective-permute-start | bytes 442376 | tf_op jit(solution)/shard_map/ppermute | solution.py:33
  98.3 2.5 %collective-permute-done.21.arrived_ref = bf16[8,24,384]{2,1,0:T(8,128)(2,1)S(1)} collective-permute-done((bf16[8,24,384]{2,1,0:T(8,128)(2,1)S(1)}, bf16[8,24,384]{2,1,0:T(8,128)(2,1)S(1)}, u32[]{:S(2)}, u32[]{:S(2)}) %collective-permute-start.21) | collective-permute-done | bytes 147488 | tf_op jit(solution)/shard_map/ppermute | solution.py:33
  100.8 0.3 square.1
  101.1 23.9 %all_to_all.5.squares_ref = f32[128,1,128]{2,1,0:T(1,128)S(1)} all-to-all(f32[128,1,128]{2,1,0:T(1,128)S(1)} %get-tuple-element.117), channel_id=1, replica_groups=mesh['dp_0'=4,'dp_1'=2,'dp_2'=4,'dp_3'=2,'mp'=2] {'dp_0','dp_1','dp_2','..., dimensions={0} | all-to-all | bytes 131072 | tf_op jit(solution)/shard_map/all_to_all | solution.py:422
  125.0 0.9 scale.1
  (21 shorter events, 0.0 us)
Async XLA Ops:
  0.6 18.5 %collective-permute-start.1 = (bf16[663,1536]{1,0:T(8,128)(2,1)}, bf16[663,1536]{1,0:T(8,128)(2,1)}, u32[]{:S(2)}, u32[]{:S(2)}) collective-permute-start(bf16[663,1536]{1,0:T(8,128)(2,1)} %bitcast.10), channel_id=1, source_target_pairs={{0,17},{17,0},{1,16},{16,1},{4,21},{21,4},{5,20},{20,5},{8,25},{25... | collective-permute-start | bytes 6110216 | tf_op jit(solution)/shard_map/ppermute | solution.py:293
  2.6 2.2 %copy-start = (bf16[2652,768]{1,0:T(8,128)(2,1)S(1)}, bf16[2652,768]{1,0:T(8,128)(2,1)}, u32[]{:S(2)}) copy-start(bf16[2652,768]{1,0:T(8,128)(2,1)} %w_first_ref.1) | copy-start | bytes 12220420
  4.8 1.7 %copy-start.1 = (bf16[768,1536]{1,0:T(8,128)(2,1)S(1)}, bf16[768,1536]{1,0:T(8,128)(2,1)}, u32[]{:S(2)}) copy-start(bf16[768,1536]{1,0:T(8,128)(2,1)} %w_middle_ref.3) | copy-start | bytes 7077892
  6.5 1.3 %copy-start.4 = (bf16[256,2652]{0,1:T(8,128)(2,1)S(1)}, bf16[256,2652]{0,1:T(8,128)(2,1)}, u32[]{:S(2)}) copy-start(bf16[256,2652]{0,1:T(8,128)(2,1)} %param.7) | copy-start | bytes 4073476
  7.8 6.9 %copy-start.3 = (bf16[1536,663]{0,1:T(8,128)(2,1)S(1)}, bf16[1536,663]{0,1:T(8,128)(2,1)}, u32[]{:S(2)}) copy-start(bf16[1536,663]{0,1:T(8,128)(2,1)} %param.12) | copy-start | bytes 6110212
  7.8 6.9 %copy-start.6 = (bf16[256,1326]{0,1:T(8,128)(2,1)S(1)}, bf16[256,1326]{0,1:T(8,128)(2,1)}, u32[]{:S(2)}) copy-start(bf16[256,1326]{0,1:T(8,128)(2,1)} %param.8) | copy-start | bytes 2036740
  7.8 6.9 %copy-start.7 = (s32[2]{0:T(128)S(1)}, s32[2]{0:T(128)}, u32[]{:S(2)}) copy-start(s32[2]{0:T(128)} %counts_ref.1) | copy-start | bytes 28
  10.5 0.9 copy-start.9
  11.4 0.8 copy-start.11
  12.1 16.6 %collective-permute-start = (bf16[256,1536]{1,0:T(8,128)(2,1)S(1)}, bf16[256,1536]{1,0:T(8,128)(2,1)}, u32[]{:S(2)}, u32[]{:S(2)}) collective-permute-start(bf16[256,1536]{1,0:T(8,128)(2,1)S(1)} %get-tuple-element.62.partial_ref), channel_id=1, source_target_pairs={{0,1},{1,0},{2,3},{3,2},{4,5},{5,4},{6,7},{7,6},{8,9},{9,8},{10,11... | collective-permute-start | bytes 2359304 | tf_op jit(solution)/shard_map/ppermute | solution.py:33
  14.7 1.1 copy-start.8
  15.8 1.1 copy-start.10
  19.2 17.7 %collective-permute-start.2 = (bf16[663,1536]{1,0:T(8,128)(2,1)}, bf16[663,1536]{1,0:T(8,128)(2,1)S(1)}, u32[]{:S(2)}, u32[]{:S(2)}) collective-permute-start(bf16[663,1536]{1,0:T(8,128)(2,1)} %collective-permute-done.1.fetched_ref), channel_id=1, source_target_pairs={{0,2},{1,3},{4,6},{5,7},{8,10},{9,11},{12,14},{13,15},{16,18},{17,... | collective-permute-start | bytes 6110216 | tf_op jit(solution)/shard_map/ppermute | solution.py:327
  28.8 8.1 %copy-start.2 = (bf16[768,1536]{1,0:T(8,128)(2,1)S(1)}, bf16[768,1536]{1,0:T(8,128)(2,1)}, u32[]{:S(2)}) copy-start(bf16[768,1536]{1,0:T(8,128)(2,1)} %w_middle_ref.3) | copy-start | bytes 7077892
  28.8 8.1 %copy-start.5 = (bf16[256,2652]{0,1:T(8,128)(2,1)S(1)}, bf16[256,2652]{0,1:T(8,128)(2,1)}, u32[]{:S(2)}) copy-start(bf16[256,2652]{0,1:T(8,128)(2,1)} %param.7) | copy-start | bytes 4073476
  36.8 6.4 %copy-start.12 = (bf16[256,768]{1,0:T(8,128)(2,1)S(1)}, bf16[256,768]{1,0:T(8,128)(2,1)}, u32[]{:S(2)}) copy-start(bf16[256,768]{1,0:T(8,128)(2,1)} %copy-done.11) | copy-start | bytes 1179652
  42.9 4.2 %collective-permute-start.3 = (bf16[16,7,24,384]{3,2,1,0:T(8,128)(2,1)S(1)}, bf16[16,7,24,384]{3,2,1,0:T(8,128)(2,1)S(1)}, u32[]{:S(2)}, u32[]{:S(2)}) collective-permute-start(bf16[16,7,24,384]{3,2,1,0:T(8,128)(2,1)S(1)} %get-tuple-element.76), channel_id=1, source_target_pairs={{0,2},{2,0},{1,3},{3,1},{4,6},{6,4},{5,7},{7,5},{8,10},{10,8},{9,1... | collective-permute-start | bytes 6193160 | tf_op jit(solution)/shard_map/ppermute | solution.py:33
  45.8 4.8 %collective-permute-start.6 = (bf16[16,8,24,384]{3,2,1,0:T(8,128)(2,1)S(1)}, bf16[16,8,24,384]{3,2,1,0:T(8,128)(2,1)S(1)}, u32[]{:S(2)}, u32[]{:S(2)}) collective-permute-start(bf16[16,8,24,384]{3,2,1,0:T(8,128)(2,1)S(1)} %get-tuple-element.85), channel_id=1, source_target_pairs={{0,2},{2,0},{1,3},{3,1},{4,6},{6,4},{5,7},{7,5},{8,10},{10,8},{9,1... | collective-permute-start | bytes 7077896 | tf_op jit(solution)/shard_map/ppermute | solution.py:33
  48.9 18.0 %collective-permute-start.4 = (bf16[2,4,4,24,384]{4,3,2,1,0:T(8,128)(2,1)S(1)}, bf16[2,4,4,24,384]{4,3,2,1,0:T(8,128)(2,1)S(1)}, u32[]{:S(2)}, u32[]{:S(2)}) collective-permute-start(bf16[2,4,4,24,384]{4,3,2,1,0:T(8,128)(2,1)S(1)} %get-tuple-element.78), channel_id=1, source_target_pairs={{0,32},{32,0},{64,96},{96,64},{1,33},{33,1},{65,97},{97,65},{2,34}... | collective-permute-start | bytes 1769480 | tf_op jit(solution)/shard_map/ppermute | solution.py:38
  51.6 15.3 %collective-permute-start.7 = (bf16[2,4,4,24,384]{4,3,2,1,0:T(8,128)(2,1)S(1)}, bf16[2,4,4,24,384]{4,3,2,1,0:T(8,128)(2,1)S(1)}, u32[]{:S(2)}, u32[]{:S(2)}) collective-permute-start(bf16[2,4,4,24,384]{4,3,2,1,0:T(8,128)(2,1)S(1)} %get-tuple-element.87), channel_id=1, source_target_pairs={{0,4},{4,0},{8,12},{12,8},{1,5},{5,1},{9,13},{13,9},{2,6},{6,2},{1... | collective-permute-start | bytes 1769480 | tf_op jit(solution)/shard_map/ppermute | solution.py:38
  52.9 15.5 %collective-permute-start.8 = (bf16[2,4,4,24,384]{4,3,2,1,0:T(8,128)(2,1)S(1)}, bf16[2,4,4,24,384]{4,3,2,1,0:T(8,128)(2,1)S(1)}, u32[]{:S(2)}, u32[]{:S(2)}) collective-permute-start(bf16[2,4,4,24,384]{4,3,2,1,0:T(8,128)(2,1)S(1)} %get-tuple-element.89), channel_id=1, source_target_pairs={{0,12},{4,8},{8,4},{12,0},{1,13},{5,9},{9,5},{13,1},{2,14},{6,10},... | collective-permute-start | bytes 1769480 | tf_op jit(solution)/shard_map/ppermute | solution.py:38
  54.7 12.2 %collective-permute-start.5 = (bf16[2,4,3,24,384]{4,3,2,1,0:T(8,128)(2,1)S(1)}, bf16[2,4,3,24,384]{4,3,2,1,0:T(8,128)(2,1)S(1)}, u32[]{:S(2)}, u32[]{:S(2)}) collective-permute-start(bf16[2,4,3,24,384]{4,3,2,1,0:T(8,128)(2,1)S(1)} %get-tuple-element.80), channel_id=1, source_target_pairs={{0,96},{32,64},{64,32},{96,0},{1,97},{33,65},{65,33},{97,1},{2,98}... | collective-permute-start | bytes 1327112 | tf_op jit(solution)/shard_map/ppermute | solution.py:38
  68.9 9.7 %collective-permute-start.9 = (bf16[4,4,24,384]{3,2,1,0:T(8,128)(2,1)S(1)}, bf16[4,4,24,384]{3,2,1,0:T(8,128)(2,1)S(1)}, u32[]{:S(2)}, u32[]{:S(2)}) collective-permute-start(bf16[4,4,24,384]{3,2,1,0:T(8,128)(2,1)S(1)} %get-tuple-element.91), channel_id=1, source_target_pairs={{0,96},{32,64},{64,32},{96,0},{1,97},{33,65},{65,33},{97,1},{2,98}... | collective-permute-start | bytes 884744 | tf_op jit(solution)/shard_map/ppermute | solution.py:38
  71.7 8.0 %collective-permute-start.11 = (bf16[4,4,24,384]{3,2,1,0:T(8,128)(2,1)S(1)}, bf16[4,4,24,384]{3,2,1,0:T(8,128)(2,1)S(1)}, u32[]{:S(2)}, u32[]{:S(2)}) collective-permute-start(bf16[4,4,24,384]{3,2,1,0:T(8,128)(2,1)S(1)} %get-tuple-element.95), channel_id=1, source_target_pairs={{0,12},{4,8},{8,4},{12,0},{1,13},{5,9},{9,5},{13,1},{2,14},{6,10},... | collective-permute-start | bytes 884744 | tf_op jit(solution)/shard_map/ppermute | solution.py:38
  73.5 6.5 %collective-permute-start.12 = (bf16[4,4,24,384]{3,2,1,0:T(8,128)(2,1)S(1)}, bf16[4,4,24,384]{3,2,1,0:T(8,128)(2,1)S(1)}, u32[]{:S(2)}, u32[]{:S(2)}) collective-permute-start(bf16[4,4,24,384]{3,2,1,0:T(8,128)(2,1)S(1)} %get-tuple-element.97), channel_id=1, source_target_pairs={{0,4},{4,0},{8,12},{12,8},{1,5},{5,1},{9,13},{13,9},{2,6},{6,2},{1... | collective-permute-start | bytes 884744 | tf_op jit(solution)/shard_map/ppermute | solution.py:38
  73.5 5.1 %collective-permute-start.10 = (bf16[4,3,24,384]{3,2,1,0:T(8,128)(2,1)S(1)}, bf16[4,3,24,384]{3,2,1,0:T(8,128)(2,1)S(1)}, u32[]{:S(2)}, u32[]{:S(2)}) collective-permute-start(bf16[4,3,24,384]{3,2,1,0:T(8,128)(2,1)S(1)} %get-tuple-element.93), channel_id=1, source_target_pairs={{0,32},{32,0},{64,96},{96,64},{1,33},{33,1},{65,97},{97,65},{2,34}... | collective-permute-start | bytes 663560 | tf_op jit(solution)/shard_map/ppermute | solution.py:38
  81.0 5.8 %collective-permute-start.13 = (bf16[2,4,24,384]{3,2,1,0:T(8,128)(2,1)S(1)}, bf16[2,4,24,384]{3,2,1,0:T(8,128)(2,1)S(1)}, u32[]{:S(2)}, u32[]{:S(2)}) collective-permute-start(bf16[2,4,24,384]{3,2,1,0:T(8,128)(2,1)S(1)} %get-tuple-element.99), channel_id=1, source_target_pairs={{0,4},{4,0},{8,12},{12,8},{1,5},{5,1},{9,13},{13,9},{2,6},{6,2},{1... | collective-permute-start | bytes 442376 | tf_op jit(solution)/shard_map/ppermute | solution.py:38
  81.4 5.4 %collective-permute-start.15 = (bf16[2,4,24,384]{3,2,1,0:T(8,128)(2,1)S(1)}, bf16[2,4,24,384]{3,2,1,0:T(8,128)(2,1)S(1)}, u32[]{:S(2)}, u32[]{:S(2)}) collective-permute-start(bf16[2,4,24,384]{3,2,1,0:T(8,128)(2,1)S(1)} %get-tuple-element.103), channel_id=1, source_target_pairs={{0,32},{32,0},{64,96},{96,64},{1,33},{33,1},{65,97},{97,65},{2,34}... | collective-permute-start | bytes 442376 | tf_op jit(solution)/shard_map/ppermute | solution.py:38
  81.4 5.4 %collective-permute-start.16 = (bf16[2,4,24,384]{3,2,1,0:T(8,128)(2,1)S(1)}, bf16[2,4,24,384]{3,2,1,0:T(8,128)(2,1)S(1)}, u32[]{:S(2)}, u32[]{:S(2)}) collective-permute-start(bf16[2,4,24,384]{3,2,1,0:T(8,128)(2,1)S(1)} %get-tuple-element.105), channel_id=1, source_target_pairs={{0,96},{32,64},{64,32},{96,0},{1,97},{33,65},{65,33},{97,1},{2,98}... | collective-permute-start | bytes 442376 | tf_op jit(solution)/shard_map/ppermute | solution.py:38
  82.0 4.8 %collective-permute-start.14 = (bf16[2,3,24,384]{3,2,1,0:T(8,128)(2,1)S(1)}, bf16[2,3,24,384]{3,2,1,0:T(8,128)(2,1)S(1)}, u32[]{:S(2)}, u32[]{:S(2)}) collective-permute-start(bf16[2,3,24,384]{3,2,1,0:T(8,128)(2,1)S(1)} %get-tuple-element.101), channel_id=1, source_target_pairs={{0,12},{4,8},{8,4},{12,0},{1,13},{5,9},{9,5},{13,1},{2,14},{6,10},... | collective-permute-start | bytes 331784 | tf_op jit(solution)/shard_map/ppermute | solution.py:38
  86.9 6.7 %collective-permute-start.17 = (bf16[4,24,384]{2,1,0:T(8,128)(2,1)S(1)}, bf16[4,24,384]{2,1,0:T(8,128)(2,1)S(1)}, u32[]{:S(2)}, u32[]{:S(2)}) collective-permute-start(bf16[4,24,384]{2,1,0:T(8,128)(2,1)S(1)} %get-tuple-element.107), channel_id=1, source_target_pairs={{0,12},{4,8},{8,4},{12,0},{1,13},{5,9},{9,5},{13,1},{2,14},{6,10},... | collective-permute-start | bytes 221192 | tf_op jit(solution)/shard_map/ppermute | solution.py:38
  88.3 5.3 %collective-permute-start.19 = (bf16[4,24,384]{2,1,0:T(8,128)(2,1)S(1)}, bf16[4,24,384]{2,1,0:T(8,128)(2,1)S(1)}, u32[]{:S(2)}, u32[]{:S(2)}) collective-permute-start(bf16[4,24,384]{2,1,0:T(8,128)(2,1)S(1)} %get-tuple-element.111), channel_id=1, source_target_pairs={{0,96},{32,64},{64,32},{96,0},{1,97},{33,65},{65,33},{97,1},{2,98}... | collective-permute-start | bytes 221192 | tf_op jit(solution)/shard_map/ppermute | solution.py:38
  90.4 3.2 %collective-permute-start.20 = (bf16[4,24,384]{2,1,0:T(8,128)(2,1)S(1)}, bf16[4,24,384]{2,1,0:T(8,128)(2,1)S(1)}, u32[]{:S(2)}, u32[]{:S(2)}) collective-permute-start(bf16[4,24,384]{2,1,0:T(8,128)(2,1)S(1)} %get-tuple-element.113), channel_id=1, source_target_pairs={{0,32},{32,0},{64,96},{96,64},{1,33},{33,1},{65,97},{97,65},{2,34}... | collective-permute-start | bytes 221192 | tf_op jit(solution)/shard_map/ppermute | solution.py:38
  90.6 3.0 %collective-permute-start.18 = (bf16[3,24,384]{2,1,0:T(8,128)(2,1)S(1)}, bf16[3,24,384]{2,1,0:T(8,128)(2,1)S(1)}, u32[]{:S(2)}, u32[]{:S(2)}) collective-permute-start(bf16[3,24,384]{2,1,0:T(8,128)(2,1)S(1)} %get-tuple-element.109), channel_id=1, source_target_pairs={{0,4},{4,0},{8,12},{12,8},{1,5},{5,1},{9,13},{13,9},{2,6},{6,2},{1... | collective-permute-start | bytes 165896 | tf_op jit(solution)/shard_map/ppermute | solution.py:38
  94.3 6.5 %collective-permute-start.21 = (bf16[8,24,384]{2,1,0:T(8,128)(2,1)S(1)}, bf16[8,24,384]{2,1,0:T(8,128)(2,1)S(1)}, u32[]{:S(2)}, u32[]{:S(2)}) collective-permute-start(bf16[8,24,384]{2,1,0:T(8,128)(2,1)S(1)} %get-tuple-element.115), channel_id=1, source_target_pairs={{0,16},{16,0},{1,17},{17,1},{2,18},{18,2},{3,19},{19,3},{4,20},{20... | collective-permute-start | bytes 442376 | tf_op jit(solution)/shard_map/ppermute | solution.py:33

commit v7 on v6

--- a/solution.py
+++ b/solution.py
@@ -15,6 +15,7 @@
 Y, ZH, X, CORE = DP
 LANES = 128
 ROWS, COLS = 24, 384
+DEPTH = 512
 VMEM = pl.BlockSpec(memory_space=pltpu.VMEM)
 SMEM = pl.BlockSpec(memory_space=pltpu.SMEM)
 HBM = pl.BlockSpec(memory_space=pl.ANY)
@@ -53,10 +54,10 @@
     )
 
 
-def call(body, name, in_specs, outs, scratch=(), final=False):
+def call(body, name, in_specs, outs, scratch=(), kind=pltpu.VMEM):
     kernel = pl.pallas_call(
         body,
-        out_shape=[(jax.ShapeDtypeStruct if final else pltpu.VMEM)(*out) for out in outs],
+        out_shape=[kind(*out) for out in outs],
         in_specs=in_specs,
         out_specs=[VMEM] * len(outs),
         scratch_shapes=list(scratch),
@@ -76,25 +77,43 @@
     return run
 
 
-def by_unit(raw_ref, core, out_ref, start):
-    for unit in range(16):
-        for z_hi in range(2):
-            first = 2 * ROWS * ((unit // 4 * 2 + z_hi) * 4 + unit % 4)
-            rows = pl.ds(pl.multiple_of(first + ROWS * core, 8), ROWS)
-            for half in range(2):
-                out_ref[unit, start + 2 * z_hi + half] = narrow(
-                    raw_ref[rows, half * COLS : (half + 1) * COLS]
-                )
+def rows_of_core(rows_ref, core, out_ref):
+    for block in range(32):
+        y, x, z_hi = block // 8, block // 2 % 4, block % 2
+        first = 2 * ROWS * ((2 * y + z_hi) * 4 + x)
+        rows = pl.ds(pl.multiple_of(first + ROWS * core, 8), ROWS)
+        out_ref[ROWS * block : ROWS * (block + 1), :] = narrow(rows_ref[rows, :])
 
 
 def forward_kernel(
-    belief_ref, w_first_ref, w_middle_ref, pre_first_ref, act_first_ref, sent_ref
+    belief_hbm, w_first_hbm, w_middle_hbm, pre_first_ref, act_first_ref, sent_ref,
+    belief, w_first, w_middle, sems,
 ):
-    pre_first = contract(belief_ref[...], w_first_ref[...], 0, 0)
+    inputs = belief.shape[0]
+    cuts = [(start, min(start + DEPTH, inputs)) for start in range(0, inputs, DEPTH)]
+    copies = []
+    for i, (start, stop) in enumerate(cuts):
+        rows = pl.ds(start, stop - start)
+        copies.append(
+            (
+                pltpu.make_async_copy(belief_hbm.at[rows], belief.at[rows], sems.at[2 * i]),
+                pltpu.make_async_copy(w_first_hbm.at[rows], w_first.at[rows], sems.at[2 * i + 1]),
+            )
+        )
+    copies.append((pltpu.make_async_copy(w_middle_hbm, w_middle, sems.at[2 * len(cuts)]),))
+    for pair in copies:
+        for copy in pair:
+            copy.start()
+    pre_first = jnp.zeros(pre_first_ref.shape, F32)
+    for (start, stop), pair in zip(cuts, copies):
+        for copy in pair:
+            copy.wait()
+        pre_first += contract(belief[start:stop, :], w_first[start:stop, :], 0, 0)
     pre_first_ref[...] = pre_first
     act_first = narrow(pre_first / (1.0 + jnp.exp(-pre_first)))
     act_first_ref[...] = act_first
-    sent_ref[...] = narrow(dot(act_first, w_middle_ref[...]))
+    copies[-1][0].wait()
+    sent_ref[...] = narrow(dot(act_first, w_middle[...]))
 
 
 def stage_kernel(
@@ -125,17 +144,22 @@
 
 
 def hidden_kernel(
-    partial_ref, arrived_ref, live_ref, target_ref, w_ref,
-    act_ref, act_slope_ref, slope_ref, back_ref,
+    place_ref, partial_ref, arrived_ref, live_ref, target_ref, w_ref,
+    act_ref, act_slope_ref, back_ref, sent_ref, own_ref, rows_ref,
 ):
+    core = place_ref[0]
     pre_middle = wide(partial_ref[...]) + wide(arrived_ref[...])
     sigmoid_of = 1.0 / (1.0 + jnp.exp(-pre_middle))
     act = narrow(pre_middle * sigmoid_of)
     act_ref[...] = act
     act_slope_ref[...] = sigmoid_of * (1.0 + pre_middle * (1.0 - sigmoid_of))
     slope = slope_of(w_ref[...], act, target_ref[...], live_ref[...])
-    slope_ref[...] = slope
+    half = own_ref.shape[0]
+    sent_ref[half:, :] = slope
     back_ref[...] = contract(slope, w_ref[...], 0, 0)
+    rows_ref[...] = wide(act).T
+    rows_of_core(rows_ref, 1 - core, sent_ref)
+    rows_of_core(rows_ref, core, own_ref)
 
 
 def slope_of(weights, act, target, live):
@@ -145,21 +169,21 @@
 
 def slopes_kernel(
     place_ref, act_ref, act_slope_ref, back_ref, live_ref, target_ref, first_slope_ref,
-    onehot_ref, fetched_ref, relayed_ref, w_middle_ref, belief_ref,
-    slope_middle_ref, slope_first_ref, sent_ref,
+    onehot_ref, fetched_ref, relayed_ref, w_middle_ref, sent_ref, own_ref, rows_ref,
 ):
-    w_other = jnp.where(place_ref[0] == 0, fetched_ref[...], relayed_ref[...])
+    core = place_ref[0]
+    w_other = jnp.where(core == 0, fetched_ref[...], relayed_ref[...])
     slope = slope_of(w_other, act_ref[...], target_ref[...], live_ref[...])
     back = back_ref[...] + contract(slope, w_other, 0, 0)
     slope_middle = narrow(back * act_slope_ref[...])
-    slope_middle_ref[...] = slope_middle
     slope_first = narrow(contract(slope_middle, w_middle_ref[...], 1, 1) * first_slope_ref[...])
     slope_first = narrow(contract(onehot_ref[...], slope_first, 1, 1))
-    slope_first_ref[...] = slope_first
     half = slope_first.shape[0] // 2
-    for start, stop in column_cuts(belief_ref.shape[0]):
-        raw = narrow(contract(slope_first[:half], belief_ref[start:stop, :], 1, 1))
-        put_columns(raw, start // COLS, sent_ref)
+    sent_ref[2 * half :, :] = slope_first[:half]
+    own_ref[2 * half :, :] = slope_first[half:]
+    rows_ref[...] = wide(slope_middle).T
+    rows_of_core(rows_ref, 1 - core, sent_ref)
+    rows_of_core(rows_ref, core, own_ref)
 
 
 def column_cuts(width):
@@ -174,49 +198,59 @@
         out_ref[unit, granule] = raw[unit * ROWS : (unit + 1) * ROWS]
 
 
-def later_kernel(
-    place_ref, act_ref, slope_ref, slope_middle_ref, act_first_ref, sent_ref, own_ref, raw_ref, padded_ref
-):
-    core = place_ref[0]
-    padded_ref[...] = jnp.zeros_like(padded_ref)
-    padded_ref[0 : slope_ref.shape[0], :] = slope_ref[...]
-    raw_ref[...] = contract(act_ref[...].T, padded_ref[...], 1, 1)
-    by_unit(raw_ref, 1 - core, sent_ref, 0)
-    by_unit(raw_ref, core, own_ref, 0)
-    raw_ref[...] = contract(slope_middle_ref[...], act_first_ref[...], 0, 0)
-    by_unit(raw_ref, 1 - core, sent_ref, 4)
-    by_unit(raw_ref, core, own_ref, 4)
-
-
 def kept_and_sent(me, order):
     near, far, opposite = lax.bitwise_xor(me, 1), 3 - me, lax.bitwise_xor(me, 2)
     return ((me, far), (near, opposite)) if order == 0 else ((me, near), (far, opposite))
 
 
-def cut_first_kernel(place_ref, slope_first_ref, belief_ref, arrived_ref, *refs):
+def cut_rows(raw_ref, me, order, kept_ref, sent_ref):
+    for out_ref, blocks in zip((kept_ref, sent_ref), kept_and_sent(me, order)):
+        for position, x in enumerate(blocks):
+            for y in range(4):
+                for granule in range(4):
+                    first = ROWS * (2 * (4 * y + x) + granule // 2)
+                    columns = slice(granule % 2 * COLS, (granule % 2 + 1) * COLS)
+                    rows = raw_ref[pl.ds(pl.multiple_of(first, 8), ROWS), columns]
+                    out_ref[position, y, granule] = rows.astype(out_ref.dtype)
+
+
+def last_kernel(place_ref, own_ref, sent_ref, arrived_ref, kept_out, sent_out, raw_ref, padded_ref):
+    half = own_ref.shape[0]
+    width = sent_ref.shape[0] - half
+    padded_ref[...] = jnp.zeros_like(padded_ref)
+    padded_ref[0, 0:width, :] = sent_ref[half:, :]
+    padded_ref[1, 0:width, :] = arrived_ref[half:, :]
+    raw_ref[...] = contract(own_ref[...], padded_ref[0], 1, 1) + contract(
+        arrived_ref[0:half, :], padded_ref[1], 1, 1
+    )
+    cut_rows(raw_ref, place_ref[2], 0, kept_out, sent_out)
+
+
+def middle_kernel(
+    place_ref, own_ref, arrived_ref, act_ref, sibling_act_ref, kept_out, sent_out, raw_ref
+):
+    half = raw_ref.shape[0]
+    raw_ref[...] = dot(own_ref[0:half, :], act_ref[...]) + dot(
+        arrived_ref[0:half, :], sibling_act_ref[...]
+    )
+    cut_rows(raw_ref, place_ref[2], 1, kept_out, sent_out)
+
+
+def first_kernel(place_ref, own_ref, arrived_ref, belief_ref, sibling_belief_ref, *refs):
     raw_ref = refs[-1]
-    half = slope_first_ref.shape[0] // 2
-    slope = slope_first_ref[half:, :]
+    start_row = own_ref.shape[0] // 3 * 2
+    own, arrived = own_ref[start_row:, :], arrived_ref[start_row:, :]
     for start, stop in column_cuts(belief_ref.shape[0]):
-        raw = contract(slope, belief_ref[start:stop, :], 1, 1)
+        raw = contract(own, belief_ref[start:stop, :], 1, 1) + contract(
+            arrived, sibling_belief_ref[start:stop, :], 1, 1
+        )
         put_columns(raw, start // COLS, raw_ref)
     for order, part in enumerate((slice(0, 4), slice(4, 7))):
         for side, blocks in enumerate(kept_and_sent(place_ref[1], order)):
             out_ref = refs[2 * order + side]
             for position, y in enumerate(blocks):
                 for x in range(4):
-                    total = raw_ref[4 * y + x, part] + wide(arrived_ref[4 * y + x, part])
-                    out_ref[position, x] = total.astype(out_ref.dtype)
-
-
-def cut_rest_kernel(place_ref, own_ref, arrived_ref, *refs):
-    for order, part in enumerate((slice(0, 4), slice(4, 8))):
-        for side, blocks in enumerate(kept_and_sent(place_ref[2], order)):
-            out_ref = refs[2 * order + side]
-            for position, x in enumerate(blocks):
-                for y in range(4):
-                    total = wide(own_ref[4 * y + x, part]) + wide(arrived_ref[4 * y + x, part])
-                    out_ref[position, y] = total.astype(out_ref.dtype)
+                    out_ref[position, x] = raw_ref[4 * y + x, part].astype(out_ref.dtype)
 
 
 def halve_kernel(*refs):
@@ -297,15 +331,24 @@
     pre_first, act_first, hidden_sent = call(
         forward_kernel,
         "forward",
-        [VMEM] * 3,
+        [HBM] * 3,
         [
             ((total_rows, units), F32),
             ((total_rows, units), BF16),
             ((total_rows, hidden), BF16),
         ],
-        final=True,
+        [
+            pltpu.VMEM((inputs, total_rows), BF16),
+            pltpu.VMEM((inputs, units), BF16),
+            pltpu.VMEM((units, hidden), BF16),
+            pltpu.SemaphoreType.DMA((2 * pl.cdiv(inputs, DEPTH) + 1,)),
+        ],
+        kind=pltpu.HBM,
     )(belief_t, w_first, w_middle)
     arrived = swap(hidden_sent, "mp")
+    belief_swapped, act_first = lax.optimization_barrier((belief_t, act_first))
+    sibling_belief = swap(belief_swapped, CORE)
+    sibling_act = swap(act_first, CORE)
 
     order = np.arange(units, dtype=np.int32).reshape(4, 2, 4, 2, -1).transpose(3, 0, 2, 1, 4)
     orders = np.stack([order[::-1], order]).reshape(2, units, 1)
@@ -326,37 +369,32 @@
     fetched, live = lax.optimization_barrier((fetched, live))
     relayed = lax.ppermute(fetched, CORE, [(0, 1)])
 
-    act, act_slope, slope_own, back_own = call(
+    act, act_slope, back_own, last_sent, last_own = call(
         hidden_kernel,
         "hidden",
-        [VMEM] * 5,
+        [SMEM] + [VMEM] * 5,
         [
             ((total_rows, hidden), BF16),
             ((total_rows, hidden), F32),
-            ((width, total_rows), BF16),
             ((total_rows, hidden), F32),
+            ((hidden // 2 + width, total_rows), BF16),
+            ((hidden // 2, total_rows), BF16),
         ],
-    )(hidden_sent, arrived, live, target_own, w_own)
-
-    slope_middle, slope_first, first_sent = call(
+        [pltpu.VMEM((hidden, total_rows), F32)],
+    )(place, hidden_sent, arrived, live, target_own, w_own)
+    last_arrived = swap(last_sent, CORE)
+
+    slopes_sent, slopes_own = call(
         slopes_kernel,
         "slopes",
-        [SMEM] + [VMEM] * 11,
-        [((total_rows, hidden), BF16), ((units, total_rows), BF16), granules(16, 7)],
+        [SMEM] + [VMEM] * 10,
+        [((hidden // 2 + units // 2, total_rows), BF16)] * 2,
+        [pltpu.VMEM((hidden, total_rows), F32)],
     )(
         place, act, act_slope, back_own, live, target_other, first_slope, onehot,
-        fetched, relayed, w_middle, belief_t,
-    )
-    first_arrived = swap(first_sent, CORE)
-
-    rest_sent, rest_own = call(
-        later_kernel,
-        "later",
-        [SMEM] + [VMEM] * 4,
-        [granules(16, 8)] * 2,
-        [pltpu.VMEM((hidden, units), F32), pltpu.VMEM((units, total_rows), BF16)],
-    )(place, act, slope_own, slope_middle, act_first)
-    rest_arrived = swap(rest_sent, CORE)
+        fetched, relayed, w_middle,
+    )
+    slopes_arrived = swap(slopes_sent, CORE)
 
     def pairs(*sizes):
         return [out for size in sizes for out in (granules(*size, kind=F32), granules(*size))]
@@ -368,24 +406,25 @@
             for side, part in enumerate(parts[2 * i : 2 * i + 2])
         ]
 
-    parts = exchange(
-        call(
-            cut_first_kernel,
-            "cut_first",
-            [SMEM] + [VMEM] * 3,
-            pairs((2, 4, 4), (2, 4, 3)),
-            [pltpu.VMEM((16, 7, ROWS, COLS), F32)],
-        )(place, slope_first, belief_t, first_arrived),
-        (Y, Y),
-        (0, 1),
-    )
-    parts += exchange(
-        call(cut_rest_kernel, "cut_rest", [SMEM] + [VMEM] * 2, pairs((2, 4, 4), (2, 4, 4)))(
-            place, rest_own, rest_arrived
-        ),
-        (X, X),
-        (0, 1),
-    )
+    raw = pltpu.VMEM((hidden // 2, units), F32)
+    last_parts = call(
+        last_kernel,
+        "last",
+        [SMEM] + [VMEM] * 3,
+        pairs((2, 4, 4)),
+        [raw, pltpu.VMEM((2, units, total_rows), BF16)],
+    )(place, last_own, last_sent, last_arrived)
+    first_parts = call(
+        first_kernel,
+        "first",
+        [SMEM] + [VMEM] * 4,
+        pairs((2, 4, 4), (2, 4, 3)),
+        [pltpu.VMEM((16, 7, ROWS, COLS), F32)],
+    )(place, slopes_own, slopes_arrived, belief_t, sibling_belief)
+    middle_parts = call(
+        middle_kernel, "middle", [SMEM] + [VMEM] * 4, pairs((2, 4, 4)), [raw]
+    )(place, slopes_own, slopes_arrived, act_first, sibling_act)
+    parts = exchange([*first_parts, *last_parts, *middle_parts], (Y, Y, X, X), (0, 1, 0, 1))
     sizes = (4, 3, 4, 4)
     parts = exchange(
         call(halve_kernel, "halve", [VMEM] * 8, pairs(*((4, size) for size in sizes)))(*parts),
@@ -425,7 +464,7 @@
         "scale",
         [VMEM] * 2,
         [((units // 64, inputs), F32), ((ROWS, units), F32), ((ROWS, width), F32)],
-        final=True,
+        kind=jax.ShapeDtypeStruct,
     )(total, squares)
     return grad_first.T, grad_middle.T, grad_last
 

time: 126 us -> 123 us (0.976)
  waiting for transfers between devices: 40.2 us -> 26.2 us
  starting transfers between devices: 28.5 us -> 38.9 us
  local copies, waits for them, and re-layouts: 9.17 us -> 7.52 us
  blocking collectives: 23.9 us -> 25.4 us
    ppermute x4 -> x6, starting transfers between devices: 7.34 us -> 19 us  [swap(): return lax.ppermute(shard, axis, [(0, 1), (1, 0)])]
    ppermute x4 -> x6, waiting for transfers between devices: 11.9 us -> 2.55 us  [swap(): return lax.ppermute(shard, axis, [(0, 1), (1, 0)])]
    ppermute x1, waiting for transfers between devices: 4.26 us -> 0.01 us  [per_device(): relayed = lax.ppermute(fetched, CORE, [(0, 1)])]
    unnamed x26 -> x24, local copies, waits for them, and re-layouts: 9.09 us -> 7.44 us
    all_to_all x1, blocking collectives: 23.9 us -> 25.4 us  [per_device(): squares = lax.all_to_all(squares, ALL, 0, 0, tiled=True)]
  transfers between devices with their start and end apart: 22 -> 24, of which waited for: 12 -> 8; matrix products, arithmetic and copies ran while one was open for 0% -> 0% of each run, Pallas kernels for 11% -> 17%
where the time goes in v7:
time: 123 us
  starting transfers between devices  38.9 us (32%)
  waiting for transfers between devices  26.2 us (21%)
  blocking collectives  25.4 us (21%)
  Pallas kernels  24 us (20%)
  local copies, waits for them, and re-layouts  7.52 us (6%)
    all_to_all x1, blocking collectives, per_device(): squares = lax.all_to_all(squares, ALL, 0, 0, tiled=True)  25.4 us
    pallas_call x13, Pallas kernels, run(): kernel(*(pltpu.with_memory_space_constraint(operand, pltpu.VMEM) if spec...  24 us
    ppermute x16, waiting for transfers between devices, to_pair(): return lax.ppermute(shard, axis, pairs)  23.6 us
    ppermute x6, starting transfers between devices, swap(): return lax.ppermute(shard, axis, [(0, 1), (1, 0)])  19 us
    ppermute x16, starting transfers between devices, to_pair(): return lax.ppermute(shard, axis, pairs)  16.6 us
    unnamed x24, local copies, waits for them, and re-layouts  7.44 us
    ppermute x6, waiting for transfers between devices, swap(): return lax.ppermute(shard, axis, [(0, 1), (1, 0)])  2.55 us
  transfers between devices with their start and end apart: 24, of which 8 were waited for; matrix products, arithmetic and copies ran while one was open for 0% of the time, Pallas kernels for 17%

profile of v7, /device:TPU:1, one launch (start us, length us, event | category | flops | bytes accessed | tf_op | source)
XLA Modules:
  0.0 122.8 jit_solution(17449394463461263755)
XLA Ops:
  0.6 2.0 %collective-permute-start.1 = (bf16[663,1536]{1,0:T(8,128)(2,1)}, bf16[663,1536]{1,0:T(8,128)(2,1)}, u32[]{:S(2)}, u32[]{:S(2)}) collective-permute-start(bf16[663,1536]{1,0:T(8,128)(2,1)} %bitcast.10), channel_id=1, source_target_pairs={{0,17},{17,0},{1,16},{16,1},{4,21},{21,4},{5,20},{20,5},{8,25},{25... | collective-permute-start | bytes 6110216 | tf_op jit(solution)/shard_map/ppermute | solution.py:327
  2.6 2.2 %copy-done = bf16[2652,768]{1,0:T(8,128)(2,1)S(1)} copy-done((bf16[2652,768]{1,0:T(8,128)(2,1)S(1)}, bf16[2652,768]{1,0:T(8,128)(2,1)}, u32[]{:S(2)}) %copy-start) | copy-done | bytes 4073496
  4.8 1.7 %copy-done.1 = bf16[768,1536]{1,0:T(8,128)(2,1)S(1)} copy-done((bf16[768,1536]{1,0:T(8,128)(2,1)S(1)}, bf16[768,1536]{1,0:T(8,128)(2,1)}, u32[]{:S(2)}) %copy-start.1) | copy-done | bytes 2359320
  6.5 1.3 %copy-done.4 = bf16[256,2652]{0,1:T(8,128)(2,1)S(1)} copy-done((bf16[256,2652]{0,1:T(8,128)(2,1)S(1)}, bf16[256,2652]{0,1:T(8,128)(2,1)}, u32[]{:S(2)}) %copy-start.4) | copy-done | bytes 1357848
  7.8 5.1 %forward.1 = (f32[256,768]{1,0:T(8,128)}, bf16[256,768]{1,0:T(8,128)(2,1)}, bf16[256,1536]{1,0:T(8,128)(2,1)}) custom-call(bf16[2652,256]{1,0:T(8,128)(2,1)S(1)} %bitcast.12, bf16[2652,768]{1,0:T(8,128)(2,1)S(1)} %copy-done, bf16[768,1536]{1,0:T(8,128)(2,1)S(1)} %copy-done.1), custom_call_target="tpu_custom_call" | custom-call | flops 17179869184 | bytes 67108864 | tf_op jit(solution)/shard_map/forward/pallas_call | solution.py:70
  12.9 2.6 %collective-permute-start = (bf16[256,1536]{1,0:T(8,128)(2,1)}, bf16[256,1536]{1,0:T(8,128)(2,1)S(1)}, u32[]{:S(2)}, u32[]{:S(2)}) collective-permute-start(bf16[256,1536]{1,0:T(8,128)(2,1)} %get-tuple-element.62.partial_ref), channel_id=1, source_target_pairs={{0,1},{1,0},{2,3},{3,2},{4,5},{5,4},{6,7},{7,6},{8,9},{9,8},{10,11... | collective-permute-start | bytes 2359304 | tf_op jit(solution)/shard_map/ppermute | solution.py:34
  15.5 0.1 stack.23.place_ref
  15.5 0.0 copy-start.10
  15.6 1.1 copy-done.10
  16.7 1.1 copy-done.11
  17.8 2.2 %stage.1 = (bf16[663,1536]{1,0:T(8,128)(2,1)S(1)}, bf16[663,256]{1,0:T(8,128)(2,1)S(1)}, bf16[663,256]{1,0:T(8,128)(2,1)S(1)}, f32[256,768]{1,0:T(8,128)S(1)}, b...) custom-call(s32[5]{0:T(128)S(1)} %stack.23.place_ref, s32[2]{0:T(128)S(1)} %copy-done.9, f32[256,768]{1,0:T(8,128)S(1)} %copy-done.11, ...), custom_call_target="tpu_custom_call" | custom-call | flops 17179869184 | bytes 67108864 | tf_op jit(solution)/shard_map/stage/pallas_call | solution.py:70
  20.0 0.0 collective-permute-done.1.fetched_ref
  20.0 1.3 %collective-permute-start.2 = (bf16[663,1536]{1,0:T(8,128)(2,1)}, bf16[663,1536]{1,0:T(8,128)(2,1)S(1)}, u32[]{:S(2)}, u32[]{:S(2)}) collective-permute-start(bf16[663,1536]{1,0:T(8,128)(2,1)} %collective-permute-done.1.fetched_ref), channel_id=1, source_target_pairs={{0,2},{1,3},{4,6},{5,7},{8,10},{9,11},{12,14},{13,15},{16,18},{17,... | collective-permute-start | bytes 6110216 | tf_op jit(solution)/shard_map/ppermute | solution.py:370
  21.3 12.0 %collective-permute-start.9 = (bf16[256,768]{1,0:T(8,128)(2,1)S(1)}, bf16[256,768]{1,0:T(8,128)(2,1)S(1)}, u32[]{:S(2)}, u32[]{:S(2)}) collective-permute-start(bf16[256,768]{1,0:T(8,128)(2,1)S(1)} %copy-done.8), channel_id=1, source_target_pairs={{0,2},{2,0},{1,3},{3,1},{4,6},{6,4},{5,7},{7,5},{8,10},{10,8},{9,1... | collective-permute-start | bytes 1179656 | tf_op jit(solution)/shard_map/ppermute | solution.py:34
  33.3 0.1 collective-permute-start.4
  33.4 0.0 collective-permute-done.arrived_ref
  33.4 3.1 %hidden.1 = (bf16[256,1536]{1,0:T(8,128)(2,1)S(1)}, f32[256,1536]{1,0:T(8,128)S(1)}, f32[256,1536]{1,0:T(8,128)S(1)}, bf16[1431,256]{1,0:T(8,128)(2,1)S(1)}, bf16[768,256]{1,0:T(8,128)(2,1)S(1)}) custom-call(s32[5]{0:T(128)S(1)} %stack.23.place_ref, bf16[256,1536]{1,0:T(8,128)(2,1)S(1)} %copy-done.6, bf16[256,1536]{1,0:T(8,128)(2,1)S(1)} %collective-permute-done.arrived_ref, ...), custom_call_target="tpu_custom_call" | custom-call | flops 17179869184 | bytes 67108864 | tf_op jit(solution)/shard_map/hidden/pallas_call | solution.py:70
  36.5 0.8 collective-permute-start.7
  37.3 0.0 collective-permute-done.2.relayed_ref
  37.3 5.1 %slopes.1 = (bf16[1152,256]{1,0:T(8,128)(2,1)S(1)}, bf16[1152,256]{1,0:T(8,128)(2,1)S(1)}) custom-call(s32[5]{0:T(128)S(1)} %stack.23.place_ref, bf16[256,1536]{1,0:T(8,128)(2,1)S(1)} %get-tuple-element.68.act_ref, f32[256,1536]{1,0:T(8,128)S(1)} %get-tuple-element.69.act_slope_ref, f32[256,1536]{1,0:T(8,128)S(1)} %get-tuple-element.70.back_ref, ...), custom_call_target="tpu_custom_call" | custom-call | flops 17179869184 | bytes 67108864 | tf_op jit(solution)/shard_map/slopes/pallas_call | solution.py:70
  42.4 0.2 collective-permute-start.3
  42.6 0.0 collective-permute-done.7.arrived_ref
  42.6 1.5 %last.1 = (f32[2,4,4,24,384]{4,3,2,1,0:T(8,128)S(1)}, bf16[2,4,4,24,384]{4,3,2,1,0:T(8,128)(2,1)S(1)}) custom-call(s32[5]{0:T(128)S(1)} %stack.23.place_ref, bf16[768,256]{1,0:T(8,128)(2,1)S(1)} %get-tuple-element.83.own_ref, bf16[1431,256]{1,0:T(8,128)(2,1)S(1)} %get-tuple-element.84.sent_ref, bf16[1431,256]{1,0:T(8,128)(2,1)S(1)} %collective-permute-done.7.arrived_ref), custom_call_target="tpu_custom_call" | custom-call | flops 17179869184 | bytes 67108864 | tf_op jit(solution)/shard_map/last/pallas_call | solution.py:70
  44.1 1.3 %collective-permute-start.8 = (bf16[2,4,4,24,384]{4,3,2,1,0:T(8,128)(2,1)S(1)}, bf16[2,4,4,24,384]{4,3,2,1,0:T(8,128)(2,1)S(1)}, u32[]{:S(2)}, u32[]{:S(2)}) collective-permute-start(bf16[2,4,4,24,384]{4,3,2,1,0:T(8,128)(2,1)S(1)} %get-tuple-element.86), channel_id=1, source_target_pairs={{0,4},{4,0},{8,12},{12,8},{1,5},{5,1},{9,13},{13,9},{2,6},{6,2},{1... | collective-permute-start | bytes 1769480 | tf_op jit(solution)/shard_map/ppermute | solution.py:39
  45.4 0.0 collective-permute-done.9.sibling_act_ref
  45.4 0.0 collective-permute-done.3.arrived_ref
  45.4 1.5 %middle.1 = (f32[2,4,4,24,384]{4,3,2,1,0:T(8,128)S(1)}, bf16[2,4,4,24,384]{4,3,2,1,0:T(8,128)(2,1)S(1)}) custom-call(s32[5]{0:T(128)S(1)} %stack.23.place_ref, bf16[1152,256]{1,0:T(8,128)(2,1)S(1)} %get-tuple-element.75.own_ref, bf16[1152,256]{1,0:T(8,128)(2,1)S(1)} %collective-permute-done.3.arrived_ref, bf16[256,768]{1,0:T(8,128)(2,1)S(1)} %copy-done.8, ...), custom_call_target="tpu_custom_call" | custom-call | flops 17179869184 | bytes 67108864 | tf_op jit(solution)/shard_map/middle/pallas_call | solution.py:70
  46.9 2.1 %collective-permute-start.10 = (bf16[2,4,4,24,384]{4,3,2,1,0:T(8,128)(2,1)S(1)}, bf16[2,4,4,24,384]{4,3,2,1,0:T(8,128)(2,1)S(1)}, u32[]{:S(2)}, u32[]{:S(2)}) collective-permute-start(bf16[2,4,4,24,384]{4,3,2,1,0:T(8,128)(2,1)S(1)} %get-tuple-element.89), channel_id=1, source_target_pairs={{0,12},{4,8},{8,4},{12,0},{1,13},{5,9},{9,5},{13,1},{2,14},{6,10},... | collective-permute-start | bytes 1769480 | tf_op jit(solution)/shard_map/ppermute | solution.py:39
  49.0 2.4 %first.1 = (f32[2,4,4,24,384]{4,3,2,1,0:T(8,128)S(1)}, bf16[2,4,4,24,384]{4,3,2,1,0:T(8,128)(2,1)S(1)}, f32[2,4,3,24,384]{4,3,2,1,0:T(8,128)S(1)}, bf16[2,4,3,24,384]{4,3,2,1,0:T(8,128)(2,1)S(1)}) custom-call(s32[5]{0:T(128)S(1)} %stack.23.place_ref, bf16[1152,256]{1,0:T(8,128)(2,1)S(1)} %get-tuple-element.75.own_ref, ...), custom_call_target="tpu_custom_call" | custom-call | flops 17179869184 | bytes 67108864 | tf_op jit(solution)/shard_map/first/pallas_call | solution.py:70
  51.4 1.4 %collective-permute-start.5 = (bf16[2,4,4,24,384]{4,3,2,1,0:T(8,128)(2,1)S(1)}, bf16[2,4,4,24,384]{4,3,2,1,0:T(8,128)(2,1)S(1)}, u32[]{:S(2)}, u32[]{:S(2)}) collective-permute-start(bf16[2,4,4,24,384]{4,3,2,1,0:T(8,128)(2,1)S(1)} %get-tuple-element.80), channel_id=1, source_target_pairs={{0,32},{32,0},{64,96},{96,64},{1,33},{33,1},{65,97},{97,65},{2,34}... | collective-permute-start | bytes 1769480 | tf_op jit(solution)/shard_map/ppermute | solution.py:39
  52.7 1.9 %collective-permute-start.6 = (bf16[2,4,3,24,384]{4,3,2,1,0:T(8,128)(2,1)S(1)}, bf16[2,4,3,24,384]{4,3,2,1,0:T(8,128)(2,1)S(1)}, u32[]{:S(2)}, u32[]{:S(2)}) collective-permute-start(bf16[2,4,3,24,384]{4,3,2,1,0:T(8,128)(2,1)S(1)} %get-tuple-element.82), channel_id=1, source_target_pairs={{0,96},{32,64},{64,32},{96,0},{1,97},{33,65},{65,33},{97,1},{2,98}... | collective-permute-start | bytes 1327112 | tf_op jit(solution)/shard_map/ppermute | solution.py:39
  54.6 4.1 %collective-permute-done.8.refs_5_ = bf16[2,4,4,24,384]{4,3,2,1,0:T(8,128)(2,1)S(1)} collective-permute-done((bf16[2,4,4,24,384]{4,3,2,1,0:T(8,128)(2,1)S(1)}, bf16[2,4,4,24,384]{4,3,2,1,0:T(8,128)(2,1)S(1)}, u32[]{:S(2)}, u32[]{:S(2)}) %collective-permute-start.8) | collective-permute-done | bytes 589856 | tf_op jit(solution)/shard_map/ppermute | solution.py:39
  58.7 5.7 %collective-permute-done.6.refs_3_ = bf16[2,4,3,24,384]{4,3,2,1,0:T(8,128)(2,1)S(1)} collective-permute-done((bf16[2,4,3,24,384]{4,3,2,1,0:T(8,128)(2,1)S(1)}, bf16[2,4,3,24,384]{4,3,2,1,0:T(8,128)(2,1)S(1)}, u32[]{:S(2)}, u32[]{:S(2)}) %collective-permute-start.6) | collective-permute-done | bytes 442400 | tf_op jit(solution)/shard_map/ppermute | solution.py:39
  64.4 0.9 collective-permute-done.5.refs_1_
  65.3 0.4 halve.2
  65.7 2.8 %collective-permute-start.11 = (bf16[4,4,24,384]{3,2,1,0:T(8,128)(2,1)S(1)}, bf16[4,4,24,384]{3,2,1,0:T(8,128)(2,1)S(1)}, u32[]{:S(2)}, u32[]{:S(2)}) collective-permute-start(bf16[4,4,24,384]{3,2,1,0:T(8,128)(2,1)S(1)} %get-tuple-element.91), channel_id=1, source_target_pairs={{0,96},{32,64},{64,32},{96,0},{1,97},{33,65},{65,33},{97,1},{2,98}... | collective-permute-start | bytes 884744 | tf_op jit(solution)/shard_map/ppermute | solution.py:39
  68.5 0.8 collective-permute-start.13
  69.4 0.0 collective-permute-start.14
  69.4 0.0 collective-permute-start.12
  69.4 5.1 %collective-permute-done.12.refs_3_ = bf16[4,3,24,384]{3,2,1,0:T(8,128)(2,1)S(1)} collective-permute-done((bf16[4,3,24,384]{3,2,1,0:T(8,128)(2,1)S(1)}, bf16[4,3,24,384]{3,2,1,0:T(8,128)(2,1)S(1)}, u32[]{:S(2)}, u32[]{:S(2)}) %collective-permute-start.12) | collective-permute-done | bytes 221216 | tf_op jit(solution)/shard_map/ppermute | solution.py:39
  74.5 1.6 %collective-permute-done.13.refs_5_ = bf16[4,4,24,384]{3,2,1,0:T(8,128)(2,1)S(1)} collective-permute-done((bf16[4,4,24,384]{3,2,1,0:T(8,128)(2,1)S(1)}, bf16[4,4,24,384]{3,2,1,0:T(8,128)(2,1)S(1)}, u32[]{:S(2)}, u32[]{:S(2)}) %collective-permute-start.13) | collective-permute-done | bytes 294944 | tf_op jit(solution)/shard_map/ppermute | solution.py:39
  76.1 0.0 collective-permute-done.14.refs_7_
  76.1 0.9 turn.1
  77.0 0.1 collective-permute-start.15
  77.1 0.1 collective-permute-start.17
  77.2 0.6 collective-permute-start.18
  77.8 1.6 %collective-permute-start.16 = (bf16[2,3,24,384]{3,2,1,0:T(8,128)(2,1)S(1)}, bf16[2,3,24,384]{3,2,1,0:T(8,128)(2,1)S(1)}, u32[]{:S(2)}, u32[]{:S(2)}) collective-permute-start(bf16[2,3,24,384]{3,2,1,0:T(8,128)(2,1)S(1)} %get-tuple-element.101), channel_id=1, source_target_pairs={{0,12},{4,8},{8,4},{12,0},{1,13},{5,9},{9,5},{13,1},{2,14},{6,10},... | collective-permute-start | bytes 331784 | tf_op jit(solution)/shard_map/ppermute | solution.py:39
  79.4 3.2 %collective-permute-done.16.refs_3_ = bf16[2,3,24,384]{3,2,1,0:T(8,128)(2,1)S(1)} collective-permute-done((bf16[2,3,24,384]{3,2,1,0:T(8,128)(2,1)S(1)}, bf16[2,3,24,384]{3,2,1,0:T(8,128)(2,1)S(1)}, u32[]{:S(2)}, u32[]{:S(2)}) %collective-permute-start.16) | collective-permute-done | bytes 110624 | tf_op jit(solution)/shard_map/ppermute | solution.py:39
  82.6 0.0 collective-permute-done.15.refs_1_
  82.6 0.1 halve.3
  82.8 1.7 %collective-permute-start.19 = (bf16[4,24,384]{2,1,0:T(8,128)(2,1)S(1)}, bf16[4,24,384]{2,1,0:T(8,128)(2,1)S(1)}, u32[]{:S(2)}, u32[]{:S(2)}) collective-permute-start(bf16[4,24,384]{2,1,0:T(8,128)(2,1)S(1)} %get-tuple-element.107), channel_id=1, source_target_pairs={{0,12},{4,8},{8,4},{12,0},{1,13},{5,9},{9,5},{13,1},{2,14},{6,10},... | collective-permute-start | bytes 221192 | tf_op jit(solution)/shard_map/ppermute | solution.py:39
  84.4 2.0 %collective-permute-start.21 = (bf16[4,24,384]{2,1,0:T(8,128)(2,1)S(1)}, bf16[4,24,384]{2,1,0:T(8,128)(2,1)S(1)}, u32[]{:S(2)}, u32[]{:S(2)}) collective-permute-start(bf16[4,24,384]{2,1,0:T(8,128)(2,1)S(1)} %get-tuple-element.111), channel_id=1, source_target_pairs={{0,96},{32,64},{64,32},{96,0},{1,97},{33,65},{65,33},{97,1},{2,98}... | collective-permute-start | bytes 221192 | tf_op jit(solution)/shard_map/ppermute | solution.py:39
  86.5 0.3 collective-permute-start.22
  86.7 0.0 collective-permute-start.20
  86.7 3.0 %collective-permute-done.20.refs_3_ = bf16[3,24,384]{2,1,0:T(8,128)(2,1)S(1)} collective-permute-done((bf16[3,24,384]{2,1,0:T(8,128)(2,1)S(1)}, bf16[3,24,384]{2,1,0:T(8,128)(2,1)S(1)}, u32[]{:S(2)}, u32[]{:S(2)}) %collective-permute-start.20) | collective-permute-done | bytes 55328 | tf_op jit(solution)/shard_map/ppermute | solution.py:39
  89.7 0.0 collective-permute-done.19.refs_1_
  89.7 0.0 collective-permute-done.21.refs_5_
  89.7 0.0 collective-permute-done.22.refs_7_
  89.7 0.6 z_cut.1
  90.4 3.3 %collective-permute-start.23 = (bf16[8,24,384]{2,1,0:T(8,128)(2,1)S(1)}, bf16[8,24,384]{2,1,0:T(8,128)(2,1)S(1)}, u32[]{:S(2)}, u32[]{:S(2)}) collective-permute-start(bf16[8,24,384]{2,1,0:T(8,128)(2,1)S(1)} %get-tuple-element.115), channel_id=1, source_target_pairs={{0,16},{16,0},{1,17},{17,1},{2,18},{18,2},{3,19},{19,3},{4,20},{20... | collective-permute-start | bytes 442376 | tf_op jit(solution)/shard_map/ppermute | solution.py:34
  93.7 2.5 %collective-permute-done.23.arrived_ref = bf16[8,24,384]{2,1,0:T(8,128)(2,1)S(1)} collective-permute-done((bf16[8,24,384]{2,1,0:T(8,128)(2,1)S(1)}, bf16[8,24,384]{2,1,0:T(8,128)(2,1)S(1)}, u32[]{:S(2)}, u32[]{:S(2)}) %collective-permute-start.23) | collective-permute-done | bytes 147488 | tf_op jit(solution)/shard_map/ppermute | solution.py:34
  96.2 0.3 square.1
  96.5 25.4 %all_to_all.5.squares_ref = f32[128,1,128]{2,1,0:T(1,128)S(1)} all-to-all(f32[128,1,128]{2,1,0:T(1,128)S(1)} %get-tuple-element.117), channel_id=1, replica_groups=mesh['dp_0'=4,'dp_1'=2,'dp_2'=4,'dp_3'=2,'mp'=2] {'dp_0','dp_1','dp_2','..., dimensions={0} | all-to-all | bytes 131072 | tf_op jit(solution)/shard_map/all_to_all | solution.py:461
  121.9 0.9 scale.1
  (23 shorter events, 0.0 us)
Async XLA Ops:
  0.6 19.4 %collective-permute-start.1 = (bf16[663,1536]{1,0:T(8,128)(2,1)}, bf16[663,1536]{1,0:T(8,128)(2,1)}, u32[]{:S(2)}, u32[]{:S(2)}) collective-permute-start(bf16[663,1536]{1,0:T(8,128)(2,1)} %bitcast.10), channel_id=1, source_target_pairs={{0,17},{17,0},{1,16},{16,1},{4,21},{21,4},{5,20},{20,5},{8,25},{25... | collective-permute-start | bytes 6110216 | tf_op jit(solution)/shard_map/ppermute | solution.py:327
  2.6 2.2 %copy-start = (bf16[2652,768]{1,0:T(8,128)(2,1)S(1)}, bf16[2652,768]{1,0:T(8,128)(2,1)}, u32[]{:S(2)}) copy-start(bf16[2652,768]{1,0:T(8,128)(2,1)} %w_first_hbm.1) | copy-start | bytes 12220420
  4.8 1.7 %copy-start.1 = (bf16[768,1536]{1,0:T(8,128)(2,1)S(1)}, bf16[768,1536]{1,0:T(8,128)(2,1)}, u32[]{:S(2)}) copy-start(bf16[768,1536]{1,0:T(8,128)(2,1)} %w_middle_ref.1) | copy-start | bytes 7077892
  6.5 1.3 %copy-start.4 = (bf16[256,2652]{0,1:T(8,128)(2,1)S(1)}, bf16[256,2652]{0,1:T(8,128)(2,1)}, u32[]{:S(2)}) copy-start(bf16[256,2652]{0,1:T(8,128)(2,1)} %param.7) | copy-start | bytes 4073476
  7.8 7.7 %copy-start.3 = (bf16[1536,663]{0,1:T(8,128)(2,1)S(1)}, bf16[1536,663]{0,1:T(8,128)(2,1)}, u32[]{:S(2)}) copy-start(bf16[1536,663]{0,1:T(8,128)(2,1)} %param.12) | copy-start | bytes 6110212
  7.8 7.7 %copy-start.7 = (bf16[256,1326]{0,1:T(8,128)(2,1)S(1)}, bf16[256,1326]{0,1:T(8,128)(2,1)}, u32[]{:S(2)}) copy-start(bf16[256,1326]{0,1:T(8,128)(2,1)} %param.8) | copy-start | bytes 2036740
  7.8 7.7 %copy-start.9 = (s32[2]{0:T(128)S(1)}, s32[2]{0:T(128)}, u32[]{:S(2)}) copy-start(s32[2]{0:T(128)} %counts_ref.1) | copy-start | bytes 28
  12.9 20.5 %collective-permute-start = (bf16[256,1536]{1,0:T(8,128)(2,1)}, bf16[256,1536]{1,0:T(8,128)(2,1)S(1)}, u32[]{:S(2)}, u32[]{:S(2)}) collective-permute-start(bf16[256,1536]{1,0:T(8,128)(2,1)} %get-tuple-element.62.partial_ref), channel_id=1, source_target_pairs={{0,1},{1,0},{2,3},{3,2},{4,5},{5,4},{6,7},{7,6},{8,9},{9,8},{10,11... | collective-permute-start | bytes 2359304 | tf_op jit(solution)/shard_map/ppermute | solution.py:34
  15.5 1.1 copy-start.10
  16.7 1.1 copy-start.11
  17.8 3.5 %copy-start.8 = (bf16[256,768]{1,0:T(8,128)(2,1)S(1)}, bf16[256,768]{1,0:T(8,128)(2,1)}, u32[]{:S(2)}) copy-start(bf16[256,768]{1,0:T(8,128)(2,1)} %get-tuple-element.87.act_ref) | copy-start | bytes 1179652
  17.8 15.5 %copy-start.5 = (bf16[256,2652]{0,1:T(8,128)(2,1)S(1)}, bf16[256,2652]{0,1:T(8,128)(2,1)}, u32[]{:S(2)}) copy-start(bf16[256,2652]{0,1:T(8,128)(2,1)} %param.7) | copy-start | bytes 4073476
  17.8 15.6 %copy-start.6 = (bf16[256,1536]{1,0:T(8,128)(2,1)S(1)}, bf16[256,1536]{1,0:T(8,128)(2,1)}, u32[]{:S(2)}) copy-start(bf16[256,1536]{1,0:T(8,128)(2,1)} %get-tuple-element.62.partial_ref) | copy-start | bytes 2359300
  20.0 17.3 %collective-permute-start.2 = (bf16[663,1536]{1,0:T(8,128)(2,1)}, bf16[663,1536]{1,0:T(8,128)(2,1)S(1)}, u32[]{:S(2)}, u32[]{:S(2)}) collective-permute-start(bf16[663,1536]{1,0:T(8,128)(2,1)} %collective-permute-done.1.fetched_ref), channel_id=1, source_target_pairs={{0,2},{1,3},{4,6},{5,7},{8,10},{9,11},{12,14},{13,15},{16,18},{17,... | collective-permute-start | bytes 6110216 | tf_op jit(solution)/shard_map/ppermute | solution.py:370
  21.3 24.1 %collective-permute-start.9 = (bf16[256,768]{1,0:T(8,128)(2,1)S(1)}, bf16[256,768]{1,0:T(8,128)(2,1)S(1)}, u32[]{:S(2)}, u32[]{:S(2)}) collective-permute-start(bf16[256,768]{1,0:T(8,128)(2,1)S(1)} %copy-done.8), channel_id=1, source_target_pairs={{0,2},{2,0},{1,3},{3,1},{4,6},{6,4},{5,7},{7,5},{8,10},{10,8},{9,1... | collective-permute-start | bytes 1179656 | tf_op jit(solution)/shard_map/ppermute | solution.py:34
  33.3 15.7 %collective-permute-start.4 = (bf16[2652,256]{1,0:T(8,128)(2,1)S(1)}, bf16[2652,256]{1,0:T(8,128)(2,1)S(1)}, u32[]{:S(2)}, u32[]{:S(2)}) collective-permute-start(bf16[2652,256]{1,0:T(8,128)(2,1)S(1)} %bitcast.13), channel_id=1, source_target_pairs={{0,2},{2,0},{1,3},{3,1},{4,6},{6,4},{5,7},{7,5},{8,10},{10,8},{9,1... | collective-permute-start | bytes 4073480 | tf_op jit(solution)/shard_map/ppermute | solution.py:34
  33.4 3.9 %copy-start.2 = (bf16[768,1536]{1,0:T(8,128)(2,1)S(1)}, bf16[768,1536]{1,0:T(8,128)(2,1)}, u32[]{:S(2)}) copy-start(bf16[768,1536]{1,0:T(8,128)(2,1)} %w_middle_ref.1) | copy-start | bytes 7077892
  36.5 6.1 %collective-permute-start.7 = (bf16[1431,256]{1,0:T(8,128)(2,1)S(1)}, bf16[1431,256]{1,0:T(8,128)(2,1)S(1)}, u32[]{:S(2)}, u32[]{:S(2)}) collective-permute-start(bf16[1431,256]{1,0:T(8,128)(2,1)S(1)} %get-tuple-element.84.sent_ref), channel_id=1, source_target_pairs={{0,2},{2,0},{1,3},{3,1},{4,6},{6,4},{5,7},{7,5},{8,10},{10,8},{9,1... | collective-permute-start | bytes 2198024 | tf_op jit(solution)/shard_map/ppermute | solution.py:34
  42.4 3.0 %collective-permute-start.3 = (bf16[1152,256]{1,0:T(8,128)(2,1)S(1)}, bf16[1152,256]{1,0:T(8,128)(2,1)S(1)}, u32[]{:S(2)}, u32[]{:S(2)}) collective-permute-start(bf16[1152,256]{1,0:T(8,128)(2,1)S(1)} %get-tuple-element.76), channel_id=1, source_target_pairs={{0,2},{2,0},{1,3},{3,1},{4,6},{6,4},{5,7},{7,5},{8,10},{10,8},{9,1... | collective-permute-start | bytes 1769480 | tf_op jit(solution)/shard_map/ppermute | solution.py:34
  44.1 14.6 %collective-permute-start.8 = (bf16[2,4,4,24,384]{4,3,2,1,0:T(8,128)(2,1)S(1)}, bf16[2,4,4,24,384]{4,3,2,1,0:T(8,128)(2,1)S(1)}, u32[]{:S(2)}, u32[]{:S(2)}) collective-permute-start(bf16[2,4,4,24,384]{4,3,2,1,0:T(8,128)(2,1)S(1)} %get-tuple-element.86), channel_id=1, source_target_pairs={{0,4},{4,0},{8,12},{12,8},{1,5},{5,1},{9,13},{13,9},{2,6},{6,2},{1... | collective-permute-start | bytes 1769480 | tf_op jit(solution)/shard_map/ppermute | solution.py:39
  46.9 17.5 %collective-permute-start.10 = (bf16[2,4,4,24,384]{4,3,2,1,0:T(8,128)(2,1)S(1)}, bf16[2,4,4,24,384]{4,3,2,1,0:T(8,128)(2,1)S(1)}, u32[]{:S(2)}, u32[]{:S(2)}) collective-permute-start(bf16[2,4,4,24,384]{4,3,2,1,0:T(8,128)(2,1)S(1)} %get-tuple-element.89), channel_id=1, source_target_pairs={{0,12},{4,8},{8,4},{12,0},{1,13},{5,9},{9,5},{13,1},{2,14},{6,10},... | collective-permute-start | bytes 1769480 | tf_op jit(solution)/shard_map/ppermute | solution.py:39
  51.4 14.0 %collective-permute-start.5 = (bf16[2,4,4,24,384]{4,3,2,1,0:T(8,128)(2,1)S(1)}, bf16[2,4,4,24,384]{4,3,2,1,0:T(8,128)(2,1)S(1)}, u32[]{:S(2)}, u32[]{:S(2)}) collective-permute-start(bf16[2,4,4,24,384]{4,3,2,1,0:T(8,128)(2,1)S(1)} %get-tuple-element.80), channel_id=1, source_target_pairs={{0,32},{32,0},{64,96},{96,64},{1,33},{33,1},{65,97},{97,65},{2,34}... | collective-permute-start | bytes 1769480 | tf_op jit(solution)/shard_map/ppermute | solution.py:39
  52.7 11.6 %collective-permute-start.6 = (bf16[2,4,3,24,384]{4,3,2,1,0:T(8,128)(2,1)S(1)}, bf16[2,4,3,24,384]{4,3,2,1,0:T(8,128)(2,1)S(1)}, u32[]{:S(2)}, u32[]{:S(2)}) collective-permute-start(bf16[2,4,3,24,384]{4,3,2,1,0:T(8,128)(2,1)S(1)} %get-tuple-element.82), channel_id=1, source_target_pairs={{0,96},{32,64},{64,32},{96,0},{1,97},{33,65},{65,33},{97,1},{2,98}... | collective-permute-start | bytes 1327112 | tf_op jit(solution)/shard_map/ppermute | solution.py:39
  65.7 8.7 %collective-permute-start.11 = (bf16[4,4,24,384]{3,2,1,0:T(8,128)(2,1)S(1)}, bf16[4,4,24,384]{3,2,1,0:T(8,128)(2,1)S(1)}, u32[]{:S(2)}, u32[]{:S(2)}) collective-permute-start(bf16[4,4,24,384]{3,2,1,0:T(8,128)(2,1)S(1)} %get-tuple-element.91), channel_id=1, source_target_pairs={{0,96},{32,64},{64,32},{96,0},{1,97},{33,65},{65,33},{97,1},{2,98}... | collective-permute-start | bytes 884744 | tf_op jit(solution)/shard_map/ppermute | solution.py:39
  68.5 7.6 %collective-permute-start.13 = (bf16[4,4,24,384]{3,2,1,0:T(8,128)(2,1)S(1)}, bf16[4,4,24,384]{3,2,1,0:T(8,128)(2,1)S(1)}, u32[]{:S(2)}, u32[]{:S(2)}) collective-permute-start(bf16[4,4,24,384]{3,2,1,0:T(8,128)(2,1)S(1)} %get-tuple-element.95), channel_id=1, source_target_pairs={{0,12},{4,8},{8,4},{12,0},{1,13},{5,9},{9,5},{13,1},{2,14},{6,10},... | collective-permute-start | bytes 884744 | tf_op jit(solution)/shard_map/ppermute | solution.py:39
  69.4 6.7 %collective-permute-start.14 = (bf16[4,4,24,384]{3,2,1,0:T(8,128)(2,1)S(1)}, bf16[4,4,24,384]{3,2,1,0:T(8,128)(2,1)S(1)}, u32[]{:S(2)}, u32[]{:S(2)}) collective-permute-start(bf16[4,4,24,384]{3,2,1,0:T(8,128)(2,1)S(1)} %get-tuple-element.97), channel_id=1, source_target_pairs={{0,4},{4,0},{8,12},{12,8},{1,5},{5,1},{9,13},{13,9},{2,6},{6,2},{1... | collective-permute-start | bytes 884744 | tf_op jit(solution)/shard_map/ppermute | solution.py:39
  69.4 5.1 %collective-permute-start.12 = (bf16[4,3,24,384]{3,2,1,0:T(8,128)(2,1)S(1)}, bf16[4,3,24,384]{3,2,1,0:T(8,128)(2,1)S(1)}, u32[]{:S(2)}, u32[]{:S(2)}) collective-permute-start(bf16[4,3,24,384]{3,2,1,0:T(8,128)(2,1)S(1)} %get-tuple-element.93), channel_id=1, source_target_pairs={{0,32},{32,0},{64,96},{96,64},{1,33},{33,1},{65,97},{97,65},{2,34}... | collective-permute-start | bytes 663560 | tf_op jit(solution)/shard_map/ppermute | solution.py:39
  77.0 5.6 %collective-permute-start.15 = (bf16[2,4,24,384]{3,2,1,0:T(8,128)(2,1)S(1)}, bf16[2,4,24,384]{3,2,1,0:T(8,128)(2,1)S(1)}, u32[]{:S(2)}, u32[]{:S(2)}) collective-permute-start(bf16[2,4,24,384]{3,2,1,0:T(8,128)(2,1)S(1)} %get-tuple-element.99), channel_id=1, source_target_pairs={{0,4},{4,0},{8,12},{12,8},{1,5},{5,1},{9,13},{13,9},{2,6},{6,2},{1... | collective-permute-start | bytes 442376 | tf_op jit(solution)/shard_map/ppermute | solution.py:39
  77.1 5.5 %collective-permute-start.17 = (bf16[2,4,24,384]{3,2,1,0:T(8,128)(2,1)S(1)}, bf16[2,4,24,384]{3,2,1,0:T(8,128)(2,1)S(1)}, u32[]{:S(2)}, u32[]{:S(2)}) collective-permute-start(bf16[2,4,24,384]{3,2,1,0:T(8,128)(2,1)S(1)} %get-tuple-element.103), channel_id=1, source_target_pairs={{0,32},{32,0},{64,96},{96,64},{1,33},{33,1},{65,97},{97,65},{2,34}... | collective-permute-start | bytes 442376 | tf_op jit(solution)/shard_map/ppermute | solution.py:39
  77.2 5.4 %collective-permute-start.18 = (bf16[2,4,24,384]{3,2,1,0:T(8,128)(2,1)S(1)}, bf16[2,4,24,384]{3,2,1,0:T(8,128)(2,1)S(1)}, u32[]{:S(2)}, u32[]{:S(2)}) collective-permute-start(bf16[2,4,24,384]{3,2,1,0:T(8,128)(2,1)S(1)} %get-tuple-element.105), channel_id=1, source_target_pairs={{0,96},{32,64},{64,32},{96,0},{1,97},{33,65},{65,33},{97,1},{2,98}... | collective-permute-start | bytes 442376 | tf_op jit(solution)/shard_map/ppermute | solution.py:39
  77.8 4.8 %collective-permute-start.16 = (bf16[2,3,24,384]{3,2,1,0:T(8,128)(2,1)S(1)}, bf16[2,3,24,384]{3,2,1,0:T(8,128)(2,1)S(1)}, u32[]{:S(2)}, u32[]{:S(2)}) collective-permute-start(bf16[2,3,24,384]{3,2,1,0:T(8,128)(2,1)S(1)} %get-tuple-element.101), channel_id=1, source_target_pairs={{0,12},{4,8},{8,4},{12,0},{1,13},{5,9},{9,5},{13,1},{2,14},{6,10},... | collective-permute-start | bytes 331784 | tf_op jit(solution)/shard_map/ppermute | solution.py:39
  82.8 7.0 %collective-permute-start.19 = (bf16[4,24,384]{2,1,0:T(8,128)(2,1)S(1)}, bf16[4,24,384]{2,1,0:T(8,128)(2,1)S(1)}, u32[]{:S(2)}, u32[]{:S(2)}) collective-permute-start(bf16[4,24,384]{2,1,0:T(8,128)(2,1)S(1)} %get-tuple-element.107), channel_id=1, source_target_pairs={{0,12},{4,8},{8,4},{12,0},{1,13},{5,9},{9,5},{13,1},{2,14},{6,10},... | collective-permute-start | bytes 221192 | tf_op jit(solution)/shard_map/ppermute | solution.py:39
  84.4 5.3 %collective-permute-start.21 = (bf16[4,24,384]{2,1,0:T(8,128)(2,1)S(1)}, bf16[4,24,384]{2,1,0:T(8,128)(2,1)S(1)}, u32[]{:S(2)}, u32[]{:S(2)}) collective-permute-start(bf16[4,24,384]{2,1,0:T(8,128)(2,1)S(1)} %get-tuple-element.111), channel_id=1, source_target_pairs={{0,96},{32,64},{64,32},{96,0},{1,97},{33,65},{65,33},{97,1},{2,98}... | collective-permute-start | bytes 221192 | tf_op jit(solution)/shard_map/ppermute | solution.py:39
  86.5 3.3 %collective-permute-start.22 = (bf16[4,24,384]{2,1,0:T(8,128)(2,1)S(1)}, bf16[4,24,384]{2,1,0:T(8,128)(2,1)S(1)}, u32[]{:S(2)}, u32[]{:S(2)}) collective-permute-start(bf16[4,24,384]{2,1,0:T(8,128)(2,1)S(1)} %get-tuple-element.113), channel_id=1, source_target_pairs={{0,32},{32,0},{64,96},{96,64},{1,33},{33,1},{65,97},{97,65},{2,34}... | collective-permute-start | bytes 221192 | tf_op jit(solution)/shard_map/ppermute | solution.py:39
  86.7 3.0 %collective-permute-start.20 = (bf16[3,24,384]{2,1,0:T(8,128)(2,1)S(1)}, bf16[3,24,384]{2,1,0:T(8,128)(2,1)S(1)}, u32[]{:S(2)}, u32[]{:S(2)}) collective-permute-start(bf16[3,24,384]{2,1,0:T(8,128)(2,1)S(1)} %get-tuple-element.109), channel_id=1, source_target_pairs={{0,4},{4,0},{8,12},{12,8},{1,5},{5,1},{9,13},{13,9},{2,6},{6,2},{1... | collective-permute-start | bytes 165896 | tf_op jit(solution)/shard_map/ppermute | solution.py:39
  90.4 5.8 %collective-permute-start.23 = (bf16[8,24,384]{2,1,0:T(8,128)(2,1)S(1)}, bf16[8,24,384]{2,1,0:T(8,128)(2,1)S(1)}, u32[]{:S(2)}, u32[]{:S(2)}) collective-permute-start(bf16[8,24,384]{2,1,0:T(8,128)(2,1)S(1)} %get-tuple-element.115), channel_id=1, source_target_pairs={{0,16},{16,0},{1,17},{17,1},{2,18},{18,2},{3,19},{19,3},{4,20},{20... | collective-permute-start | bytes 442376 | tf_op jit(solution)/shard_map/ppermute | solution.py:34

commit v8 on v7

--- a/solution.py
+++ b/solution.py
@@ -69,7 +69,9 @@
     def run(*operands):
         return kernel(
             *(
-                pltpu.with_memory_space_constraint(operand, pltpu.VMEM) if spec is VMEM else operand
+                operand if spec is SMEM else pltpu.with_memory_space_constraint(
+                    operand, pltpu.VMEM if spec is VMEM else pltpu.HBM
+                )
                 for operand, spec in zip(operands, in_specs)
             )
         )
@@ -366,7 +368,9 @@
         ],
         [pltpu.VMEM((2 * width, total_rows), BF16), pltpu.SemaphoreType.DMA((2,))],
     )(place, counts, pre_first, jnp.asarray(orders), target_value.T, w_last_t)
-    fetched, live = lax.optimization_barrier((fetched, live))
+    fetched, live, sibling_belief, sibling_act = lax.optimization_barrier(
+        (fetched, live, sibling_belief, sibling_act)
+    )
     relayed = lax.ppermute(fetched, CORE, [(0, 1)])
 
     act, act_slope, back_own, last_sent, last_own = call(

time: 123 us -> 124 us (level)
  waiting for transfers between devices: 26.2 us -> 41.9 us
  starting transfers between devices: 38.9 us -> 27.5 us
  local copies, waits for them, and re-layouts: 7.52 us -> 2.37 us
  Pallas kernels: 24 us -> 26 us
    ppermute x6, waiting for transfers between devices: 2.55 us -> 18.3 us  [swap(): return lax.ppermute(shard, axis, [(0, 1), (1, 0)])]
    ppermute x6, starting transfers between devices: 19 us -> 8.43 us  [swap(): return lax.ppermute(shard, axis, [(0, 1), (1, 0)])]
    unnamed x24 -> x14, local copies, waits for them, and re-layouts: 7.44 us -> 2.29 us
    pallas_call x13, Pallas kernels: 24 us -> 26 us  [run(): kernel(*(operand if spec is SMEM else pltpu.with_memory_space_constraint(...]
  transfers between devices with their start and end apart: 24 -> 24, of which waited for: 8 -> 11; matrix products, arithmetic and copies ran while one was open for 0% -> 0% of each run, Pallas kernels for 17% -> 19%
where the time goes in v8:
time: 124 us; the launch traced here: 123 us
  waiting for transfers between devices  41.9 us (34%)
  starting transfers between devices  27.5 us (22%)
  Pallas kernels  26 us (21%)
  blocking collectives  24.7 us (20%)
  local copies, waits for them, and re-layouts  2.37 us (2%)
    pallas_call x13, Pallas kernels, run(): kernel(*(operand if spec is SMEM else pltpu.with_memory_space_constraint(...  26 us
    all_to_all x1, blocking collectives, per_device(): squares = lax.all_to_all(squares, ALL, 0, 0, tiled=True)  24.7 us
    ppermute x16, waiting for transfers between devices, to_pair(): return lax.ppermute(shard, axis, pairs)  23.6 us
    ppermute x6, waiting for transfers between devices, swap(): return lax.ppermute(shard, axis, [(0, 1), (1, 0)])  18.3 us
    ppermute x16, starting transfers between devices, to_pair(): return lax.ppermute(shard, axis, pairs)  16.9 us
    ppermute x6, starting transfers between devices, swap(): return lax.ppermute(shard, axis, [(0, 1), (1, 0)])  8.43 us
  transfers between devices with their start and end apart: 24, of which 11 were waited for; matrix products, arithmetic and copies ran while one was open for 0% of the time, Pallas kernels for 19%

profile of v8, /device:TPU:1, one launch (start us, length us, event | category | flops | bytes accessed | tf_op | source)
XLA Modules:
  0.0 123.2 jit_solution(931335090115529839)
XLA Ops:
  0.6 0.8 collective-permute-start.1
  1.4 5.9 %forward.1 = (f32[256,768]{1,0:T(8,128)}, bf16[256,768]{1,0:T(8,128)(2,1)}, bf16[256,1536]{1,0:T(8,128)(2,1)}) custom-call(bf16[2652,256]{1,0:T(8,128)(2,1)} %bitcast.10, bf16[2652,768]{1,0:T(8,128)(2,1)} %w_first_hbm.1, bf16[768,1536]{1,0:T(8,128)(2,1)} %w_middle_ref.1), custom_call_target="tpu_custom_call" | custom-call | flops 17179869184 | bytes 67108864 | tf_op jit(solution)/shard_map/forward/pallas_call | solution.py:70
  7.3 6.7 %collective-permute-start.3 = (bf16[256,768]{1,0:T(8,128)(2,1)}, bf16[256,768]{1,0:T(8,128)(2,1)}, u32[]{:S(2)}, u32[]{:S(2)}) collective-permute-start(bf16[256,768]{1,0:T(8,128)(2,1)} %get-tuple-element.69.act_ref), channel_id=1, source_target_pairs={{0,2},{2,0},{1,3},{3,1},{4,6},{6,4},{5,7},{7,5},{8,10},{10,8},{9,1... | collective-permute-start | bytes 1179656 | tf_op jit(solution)/shard_map/ppermute | solution.py:34
  14.1 0.0 collective-permute-start
  14.1 0.2 collective-permute-start.2
  14.3 0.1 stack.23.place_ref
  14.4 1.1 copy-done.5
  15.5 1.1 copy-done.6
  16.6 2.4 %stage.1 = (bf16[663,1536]{1,0:T(8,128)(2,1)S(1)}, bf16[663,256]{1,0:T(8,128)(2,1)S(1)}, bf16[663,256]{1,0:T(8,128)(2,1)S(1)}, f32[256,768]{1,0:T(8,128)S(1)}, b...) custom-call(s32[5]{0:T(128)S(1)} %stack.23.place_ref, s32[2]{0:T(128)S(1)} %copy-done.4, f32[256,768]{1,0:T(8,128)S(1)} %copy-done.6, ...), custom_call_target="tpu_custom_call" | custom-call | flops 17179869184 | bytes 67108864 | tf_op jit(solution)/shard_map/stage/pallas_call | solution.py:70
  19.0 0.0 collective-permute-done.3.sibling_act_ref
  19.0 0.0 collective-permute-done.2.sibling_belief_ref
  19.0 0.0 collective-permute-done.1.fetched_ref
  19.0 1.3 %collective-permute-start.4 = (bf16[663,1536]{1,0:T(8,128)(2,1)S(1)}, bf16[663,1536]{1,0:T(8,128)(2,1)S(1)}, u32[]{:S(2)}, u32[]{:S(2)}) collective-permute-start(bf16[663,1536]{1,0:T(8,128)(2,1)S(1)} %collective-permute-done.1.fetched_ref), channel_id=1, source_target_pairs={{0,2},{1,3},{4,6},{5,7},{8,10},{9,11},{12,14},{13,15},{16,18},{17,... | collective-permute-start | bytes 6110216 | tf_op jit(solution)/shard_map/ppermute | solution.py:374
  20.3 13.2 %collective-permute-done.arrived_ref = bf16[256,1536]{1,0:T(8,128)(2,1)} collective-permute-done((bf16[256,1536]{1,0:T(8,128)(2,1)}, bf16[256,1536]{1,0:T(8,128)(2,1)}, u32[]{:S(2)}, u32[]{:S(2)}) %collective-permute-start) | collective-permute-done | bytes 786464 | tf_op jit(solution)/shard_map/ppermute | solution.py:34
  33.5 3.9 %hidden.1 = (bf16[256,1536]{1,0:T(8,128)(2,1)S(1)}, f32[256,1536]{1,0:T(8,128)S(1)}, f32[256,1536]{1,0:T(8,128)S(1)}, bf16[1431,256]{1,0:T(8,128)(2,1)S(1)}, bf16[768,256]{1,0:T(8,128)(2,1)S(1)}) custom-call(s32[5]{0:T(128)S(1)} %stack.23.place_ref, bf16[256,1536]{1,0:T(8,128)(2,1)S(1)} %copy-done.2, bf16[256,1536]{1,0:T(8,128)(2,1)} %collective-permute-done.arrived_ref, ...), custom_call_target="tpu_custom_call" | custom-call | flops 17179869184 | bytes 67108864 | tf_op jit(solution)/shard_map/hidden/pallas_call | solution.py:70
  37.4 0.9 collective-permute-start.8
  38.3 0.0 collective-permute-done.4.relayed_ref
  38.3 4.0 %slopes.1 = (bf16[1152,256]{1,0:T(8,128)(2,1)S(1)}, bf16[1152,256]{1,0:T(8,128)(2,1)S(1)}) custom-call(s32[5]{0:T(128)S(1)} %stack.23.place_ref, bf16[256,1536]{1,0:T(8,128)(2,1)S(1)} %get-tuple-element.73.act_ref, f32[256,1536]{1,0:T(8,128)S(1)} %get-tuple-element.74.act_slope_ref, f32[256,1536]{1,0:T(8,128)S(1)} %get-tuple-element.75.back_ref, ...), custom_call_target="tpu_custom_call" | custom-call | flops 17179869184 | bytes 67108864 | tf_op jit(solution)/shard_map/slopes/pallas_call | solution.py:70
  42.4 0.1 collective-permute-start.5
  42.5 0.0 collective-permute-done.8.arrived_ref
  42.5 1.5 %last.1 = (f32[2,4,4,24,384]{4,3,2,1,0:T(8,128)S(1)}, bf16[2,4,4,24,384]{4,3,2,1,0:T(8,128)(2,1)S(1)}) custom-call(s32[5]{0:T(128)S(1)} %stack.23.place_ref, bf16[768,256]{1,0:T(8,128)(2,1)S(1)} %get-tuple-element.87.own_ref, bf16[1431,256]{1,0:T(8,128)(2,1)S(1)} %get-tuple-element.88.sent_ref, bf16[1431,256]{1,0:T(8,128)(2,1)S(1)} %collective-permute-done.8.arrived_ref), custom_call_target="tpu_custom_call" | custom-call | flops 17179869184 | bytes 67108864 | tf_op jit(solution)/shard_map/last/pallas_call | solution.py:70
  44.0 1.5 %collective-permute-start.9 = (bf16[2,4,4,24,384]{4,3,2,1,0:T(8,128)(2,1)S(1)}, bf16[2,4,4,24,384]{4,3,2,1,0:T(8,128)(2,1)S(1)}, u32[]{:S(2)}, u32[]{:S(2)}) collective-permute-start(bf16[2,4,4,24,384]{4,3,2,1,0:T(8,128)(2,1)S(1)} %get-tuple-element.90), channel_id=1, source_target_pairs={{0,4},{4,0},{8,12},{12,8},{1,5},{5,1},{9,13},{13,9},{2,6},{6,2},{1... | collective-permute-start | bytes 1769480 | tf_op jit(solution)/shard_map/ppermute | solution.py:39
  45.5 3.2 %first.1 = (f32[2,4,4,24,384]{4,3,2,1,0:T(8,128)S(1)}, bf16[2,4,4,24,384]{4,3,2,1,0:T(8,128)(2,1)S(1)}, f32[2,4,3,24,384]{4,3,2,1,0:T(8,128)S(1)}, bf16[2,4,3,24,384]{4,3,2,1,0:T(8,128)(2,1)S(1)}) custom-call(s32[5]{0:T(128)S(1)} %stack.23.place_ref, bf16[1152,256]{1,0:T(8,128)(2,1)S(1)} %get-tuple-element.80.own_ref, ...), custom_call_target="tpu_custom_call" | custom-call | flops 17179869184 | bytes 67108864 | tf_op jit(solution)/shard_map/first/pallas_call | solution.py:70
  48.7 1.4 %collective-permute-start.6 = (bf16[2,4,4,24,384]{4,3,2,1,0:T(8,128)(2,1)S(1)}, bf16[2,4,4,24,384]{4,3,2,1,0:T(8,128)(2,1)S(1)}, u32[]{:S(2)}, u32[]{:S(2)}) collective-permute-start(bf16[2,4,4,24,384]{4,3,2,1,0:T(8,128)(2,1)S(1)} %get-tuple-element.84), channel_id=1, source_target_pairs={{0,32},{32,0},{64,96},{96,64},{1,33},{33,1},{65,97},{97,65},{2,34}... | collective-permute-start | bytes 1769480 | tf_op jit(solution)/shard_map/ppermute | solution.py:39
  50.1 1.9 %middle.1 = (f32[2,4,4,24,384]{4,3,2,1,0:T(8,128)S(1)}, bf16[2,4,4,24,384]{4,3,2,1,0:T(8,128)(2,1)S(1)}) custom-call(s32[5]{0:T(128)S(1)} %stack.23.place_ref, bf16[1152,256]{1,0:T(8,128)(2,1)S(1)} %get-tuple-element.80.own_ref, bf16[1152,256]{1,0:T(8,128)(2,1)S(1)} %collective-permute-done.5.arrived_ref, bf16[256,768]{1,0:T(8,128)(2,1)S(1)} %copy-done.3, ...), custom_call_target="tpu_custom_call" | custom-call | flops 17179869184 | bytes 67108864 | tf_op jit(solution)/shard_map/middle/pallas_call | solution.py:70
  52.0 1.9 %collective-permute-start.10 = (bf16[2,4,4,24,384]{4,3,2,1,0:T(8,128)(2,1)S(1)}, bf16[2,4,4,24,384]{4,3,2,1,0:T(8,128)(2,1)S(1)}, u32[]{:S(2)}, u32[]{:S(2)}) collective-permute-start(bf16[2,4,4,24,384]{4,3,2,1,0:T(8,128)(2,1)S(1)} %get-tuple-element.93), channel_id=1, source_target_pairs={{0,12},{4,8},{8,4},{12,0},{1,13},{5,9},{9,5},{13,1},{2,14},{6,10},... | collective-permute-start | bytes 1769480 | tf_op jit(solution)/shard_map/ppermute | solution.py:39
  53.9 1.9 %collective-permute-start.7 = (bf16[2,4,3,24,384]{4,3,2,1,0:T(8,128)(2,1)S(1)}, bf16[2,4,3,24,384]{4,3,2,1,0:T(8,128)(2,1)S(1)}, u32[]{:S(2)}, u32[]{:S(2)}) collective-permute-start(bf16[2,4,3,24,384]{4,3,2,1,0:T(8,128)(2,1)S(1)} %get-tuple-element.86), channel_id=1, source_target_pairs={{0,96},{32,64},{64,32},{96,0},{1,97},{33,65},{65,33},{97,1},{2,98}... | collective-permute-start | bytes 1327112 | tf_op jit(solution)/shard_map/ppermute | solution.py:39
  55.8 2.8 %collective-permute-done.9.refs_5_ = bf16[2,4,4,24,384]{4,3,2,1,0:T(8,128)(2,1)S(1)} collective-permute-done((bf16[2,4,4,24,384]{4,3,2,1,0:T(8,128)(2,1)S(1)}, bf16[2,4,4,24,384]{4,3,2,1,0:T(8,128)(2,1)S(1)}, u32[]{:S(2)}, u32[]{:S(2)}) %collective-permute-start.9) | collective-permute-done | bytes 589856 | tf_op jit(solution)/shard_map/ppermute | solution.py:39
  58.7 6.8 %collective-permute-done.7.refs_3_ = bf16[2,4,3,24,384]{4,3,2,1,0:T(8,128)(2,1)S(1)} collective-permute-done((bf16[2,4,3,24,384]{4,3,2,1,0:T(8,128)(2,1)S(1)}, bf16[2,4,3,24,384]{4,3,2,1,0:T(8,128)(2,1)S(1)}, u32[]{:S(2)}, u32[]{:S(2)}) %collective-permute-start.7) | collective-permute-done | bytes 442400 | tf_op jit(solution)/shard_map/ppermute | solution.py:39
  65.5 0.0 collective-permute-done.6.refs_1_
  65.5 1.6 %collective-permute-done.10.refs_7_ = bf16[2,4,4,24,384]{4,3,2,1,0:T(8,128)(2,1)S(1)} collective-permute-done((bf16[2,4,4,24,384]{4,3,2,1,0:T(8,128)(2,1)S(1)}, bf16[2,4,4,24,384]{4,3,2,1,0:T(8,128)(2,1)S(1)}, u32[]{:S(2)}, u32[]{:S(2)}) %collective-permute-start.10) | collective-permute-done | bytes 589856 | tf_op jit(solution)/shard_map/ppermute | solution.py:39
  67.1 0.4 halve.2
  67.5 2.0 %collective-permute-start.11 = (bf16[4,4,24,384]{3,2,1,0:T(8,128)(2,1)S(1)}, bf16[4,4,24,384]{3,2,1,0:T(8,128)(2,1)S(1)}, u32[]{:S(2)}, u32[]{:S(2)}) collective-permute-start(bf16[4,4,24,384]{3,2,1,0:T(8,128)(2,1)S(1)} %get-tuple-element.95), channel_id=1, source_target_pairs={{0,96},{32,64},{64,32},{96,0},{1,97},{33,65},{65,33},{97,1},{2,98}... | collective-permute-start | bytes 884744 | tf_op jit(solution)/shard_map/ppermute | solution.py:39
  69.5 1.8 %collective-permute-start.13 = (bf16[4,4,24,384]{3,2,1,0:T(8,128)(2,1)S(1)}, bf16[4,4,24,384]{3,2,1,0:T(8,128)(2,1)S(1)}, u32[]{:S(2)}, u32[]{:S(2)}) collective-permute-start(bf16[4,4,24,384]{3,2,1,0:T(8,128)(2,1)S(1)} %get-tuple-element.99), channel_id=1, source_target_pairs={{0,12},{4,8},{8,4},{12,0},{1,13},{5,9},{9,5},{13,1},{2,14},{6,10},... | collective-permute-start | bytes 884744 | tf_op jit(solution)/shard_map/ppermute | solution.py:39
  71.3 0.0 collective-permute-start.14
  71.3 0.4 collective-permute-start.12
  71.7 4.7 %collective-permute-done.12.refs_3_ = bf16[4,3,24,384]{3,2,1,0:T(8,128)(2,1)S(1)} collective-permute-done((bf16[4,3,24,384]{3,2,1,0:T(8,128)(2,1)S(1)}, bf16[4,3,24,384]{3,2,1,0:T(8,128)(2,1)S(1)}, u32[]{:S(2)}, u32[]{:S(2)}) %collective-permute-start.12) | collective-permute-done | bytes 221216 | tf_op jit(solution)/shard_map/ppermute | solution.py:39
  76.4 0.0 collective-permute-done.11.refs_1_
  76.4 0.6 collective-permute-done.13.refs_5_
  77.0 0.3 collective-permute-done.14.refs_7_
  77.3 0.9 turn.1
  78.2 0.7 collective-permute-start.15
  78.9 0.4 collective-permute-start.17
  79.3 0.7 collective-permute-start.18
  80.0 1.3 %collective-permute-start.16 = (bf16[2,3,24,384]{3,2,1,0:T(8,128)(2,1)S(1)}, bf16[2,3,24,384]{3,2,1,0:T(8,128)(2,1)S(1)}, u32[]{:S(2)}, u32[]{:S(2)}) collective-permute-start(bf16[2,3,24,384]{3,2,1,0:T(8,128)(2,1)S(1)} %get-tuple-element.105), channel_id=1, source_target_pairs={{0,12},{4,8},{8,4},{12,0},{1,13},{5,9},{9,5},{13,1},{2,14},{6,10},... | collective-permute-start | bytes 331784 | tf_op jit(solution)/shard_map/ppermute | solution.py:39
  81.3 3.5 %collective-permute-done.16.refs_3_ = bf16[2,3,24,384]{3,2,1,0:T(8,128)(2,1)S(1)} collective-permute-done((bf16[2,3,24,384]{3,2,1,0:T(8,128)(2,1)S(1)}, bf16[2,3,24,384]{3,2,1,0:T(8,128)(2,1)S(1)}, u32[]{:S(2)}, u32[]{:S(2)}) %collective-permute-start.16) | collective-permute-done | bytes 110624 | tf_op jit(solution)/shard_map/ppermute | solution.py:39
  84.8 0.0 collective-permute-done.15.refs_1_
  84.8 0.0 collective-permute-done.17.refs_5_
  84.8 0.0 collective-permute-done.18.refs_7_
  84.8 0.1 halve.3
  84.9 1.4 %collective-permute-start.19 = (bf16[4,24,384]{2,1,0:T(8,128)(2,1)S(1)}, bf16[4,24,384]{2,1,0:T(8,128)(2,1)S(1)}, u32[]{:S(2)}, u32[]{:S(2)}) collective-permute-start(bf16[4,24,384]{2,1,0:T(8,128)(2,1)S(1)} %get-tuple-element.111), channel_id=1, source_target_pairs={{0,12},{4,8},{8,4},{12,0},{1,13},{5,9},{9,5},{13,1},{2,14},{6,10},... | collective-permute-start | bytes 221192 | tf_op jit(solution)/shard_map/ppermute | solution.py:39
  86.3 1.7 %collective-permute-start.21 = (bf16[4,24,384]{2,1,0:T(8,128)(2,1)S(1)}, bf16[4,24,384]{2,1,0:T(8,128)(2,1)S(1)}, u32[]{:S(2)}, u32[]{:S(2)}) collective-permute-start(bf16[4,24,384]{2,1,0:T(8,128)(2,1)S(1)} %get-tuple-element.115), channel_id=1, source_target_pairs={{0,96},{32,64},{64,32},{96,0},{1,97},{33,65},{65,33},{97,1},{2,98}... | collective-permute-start | bytes 221192 | tf_op jit(solution)/shard_map/ppermute | solution.py:39
  88.0 0.0 collective-permute-start.22
  88.0 0.0 collective-permute-start.20
  88.0 3.0 %collective-permute-done.20.refs_3_ = bf16[3,24,384]{2,1,0:T(8,128)(2,1)S(1)} collective-permute-done((bf16[3,24,384]{2,1,0:T(8,128)(2,1)S(1)}, bf16[3,24,384]{2,1,0:T(8,128)(2,1)S(1)}, u32[]{:S(2)}, u32[]{:S(2)}) %collective-permute-start.20) | collective-permute-done | bytes 55328 | tf_op jit(solution)/shard_map/ppermute | solution.py:39
  91.0 0.0 collective-permute-done.19.refs_1_
  91.0 0.0 collective-permute-done.21.refs_5_
  91.0 0.2 collective-permute-done.22.refs_7_
  91.2 0.6 z_cut.1
  91.8 0.4 collective-permute-start.23
  92.3 5.1 %collective-permute-done.23.arrived_ref = bf16[8,24,384]{2,1,0:T(8,128)(2,1)S(1)} collective-permute-done((bf16[8,24,384]{2,1,0:T(8,128)(2,1)S(1)}, bf16[8,24,384]{2,1,0:T(8,128)(2,1)S(1)}, u32[]{:S(2)}, u32[]{:S(2)}) %collective-permute-start.23) | collective-permute-done | bytes 147488 | tf_op jit(solution)/shard_map/ppermute | solution.py:34
  97.4 0.3 square.1
  97.7 24.7 %all_to_all.5.squares_ref = f32[128,1,128]{2,1,0:T(1,128)S(1)} all-to-all(f32[128,1,128]{2,1,0:T(1,128)S(1)} %get-tuple-element.121), channel_id=1, replica_groups=mesh['dp_0'=4,'dp_1'=2,'dp_2'=4,'dp_3'=2,'mp'=2] {'dp_0','dp_1','dp_2','..., dimensions={0} | all-to-all | bytes 131072 | tf_op jit(solution)/shard_map/all_to_all | solution.py:465
  122.4 0.9 scale.1
  (13 shorter events, 0.0 us)
Async XLA Ops:
  0.6 18.4 %collective-permute-start.1 = (bf16[663,1536]{1,0:T(8,128)(2,1)}, bf16[663,1536]{1,0:T(8,128)(2,1)S(1)}, u32[]{:S(2)}, u32[]{:S(2)}) collective-permute-start(bf16[663,1536]{1,0:T(8,128)(2,1)} %bitcast.13), channel_id=1, source_target_pairs={{0,17},{17,0},{1,16},{16,1},{4,21},{21,4},{5,20},{20,5},{8,25},{25... | collective-permute-start | bytes 6110216 | tf_op jit(solution)/shard_map/ppermute | solution.py:329
  1.4 12.7 %copy-start.1 = (bf16[256,2652]{0,1:T(8,128)(2,1)S(1)}, bf16[256,2652]{0,1:T(8,128)(2,1)}, u32[]{:S(2)}) copy-start(bf16[256,2652]{0,1:T(8,128)(2,1)} %param.7) | copy-start | bytes 4073476
  1.4 12.9 %copy-start.4 = (s32[2]{0:T(128)S(1)}, s32[2]{0:T(128)}, u32[]{:S(2)}) copy-start(s32[2]{0:T(128)} %counts_ref.1) | copy-start | bytes 28
  7.3 11.7 %collective-permute-start.3 = (bf16[256,768]{1,0:T(8,128)(2,1)}, bf16[256,768]{1,0:T(8,128)(2,1)}, u32[]{:S(2)}, u32[]{:S(2)}) collective-permute-start(bf16[256,768]{1,0:T(8,128)(2,1)} %get-tuple-element.69.act_ref), channel_id=1, source_target_pairs={{0,2},{2,0},{1,3},{3,1},{4,6},{6,4},{5,7},{7,5},{8,10},{10,8},{9,1... | collective-permute-start | bytes 1179656 | tf_op jit(solution)/shard_map/ppermute | solution.py:34
  14.1 19.4 %collective-permute-start = (bf16[256,1536]{1,0:T(8,128)(2,1)}, bf16[256,1536]{1,0:T(8,128)(2,1)}, u32[]{:S(2)}, u32[]{:S(2)}) collective-permute-start(bf16[256,1536]{1,0:T(8,128)(2,1)} %get-tuple-element.64.partial_ref), channel_id=1, source_target_pairs={{0,1},{1,0},{2,3},{3,2},{4,5},{5,4},{6,7},{7,6},{8,9},{9,8},{10,11... | collective-permute-start | bytes 2359304 | tf_op jit(solution)/shard_map/ppermute | solution.py:34
  14.1 4.9 %collective-permute-start.2 = (bf16[2652,256]{1,0:T(8,128)(2,1)S(1)}, bf16[2652,256]{1,0:T(8,128)(2,1)}, u32[]{:S(2)}, u32[]{:S(2)}) collective-permute-start(bf16[2652,256]{1,0:T(8,128)(2,1)S(1)} %bitcast.11), channel_id=1, source_target_pairs={{0,2},{2,0},{1,3},{3,1},{4,6},{6,4},{5,7},{7,5},{8,10},{10,8},{9,1... | collective-permute-start | bytes 4073480 | tf_op jit(solution)/shard_map/ppermute | solution.py:34
  14.4 1.1 copy-start.5
  15.5 1.1 copy-start.6
  16.6 16.9 %copy-start.2 = (bf16[256,1536]{1,0:T(8,128)(2,1)S(1)}, bf16[256,1536]{1,0:T(8,128)(2,1)}, u32[]{:S(2)}) copy-start(bf16[256,1536]{1,0:T(8,128)(2,1)} %get-tuple-element.64.partial_ref) | copy-start | bytes 2359300
  19.0 19.3 %collective-permute-start.4 = (bf16[663,1536]{1,0:T(8,128)(2,1)S(1)}, bf16[663,1536]{1,0:T(8,128)(2,1)S(1)}, u32[]{:S(2)}, u32[]{:S(2)}) collective-permute-start(bf16[663,1536]{1,0:T(8,128)(2,1)S(1)} %collective-permute-done.1.fetched_ref), channel_id=1, source_target_pairs={{0,2},{1,3},{4,6},{5,7},{8,10},{9,11},{12,14},{13,15},{16,18},{17,... | collective-permute-start | bytes 6110216 | tf_op jit(solution)/shard_map/ppermute | solution.py:374
  33.5 4.8 %copy-start = (bf16[768,1536]{1,0:T(8,128)(2,1)S(1)}, bf16[768,1536]{1,0:T(8,128)(2,1)}, u32[]{:S(2)}) copy-start(bf16[768,1536]{1,0:T(8,128)(2,1)} %w_middle_ref.1) | copy-start | bytes 7077892
  37.4 5.1 %collective-permute-start.8 = (bf16[1431,256]{1,0:T(8,128)(2,1)S(1)}, bf16[1431,256]{1,0:T(8,128)(2,1)S(1)}, u32[]{:S(2)}, u32[]{:S(2)}) collective-permute-start(bf16[1431,256]{1,0:T(8,128)(2,1)S(1)} %get-tuple-element.88.sent_ref), channel_id=1, source_target_pairs={{0,2},{2,0},{1,3},{3,1},{4,6},{6,4},{5,7},{7,5},{8,10},{10,8},{9,1... | collective-permute-start | bytes 2198024 | tf_op jit(solution)/shard_map/ppermute | solution.py:34
  42.4 3.1 %collective-permute-start.5 = (bf16[1152,256]{1,0:T(8,128)(2,1)S(1)}, bf16[1152,256]{1,0:T(8,128)(2,1)S(1)}, u32[]{:S(2)}, u32[]{:S(2)}) collective-permute-start(bf16[1152,256]{1,0:T(8,128)(2,1)S(1)} %get-tuple-element.81), channel_id=1, source_target_pairs={{0,2},{2,0},{1,3},{3,1},{4,6},{6,4},{5,7},{7,5},{8,10},{10,8},{9,1... | collective-permute-start | bytes 1769480 | tf_op jit(solution)/shard_map/ppermute | solution.py:34
  44.0 14.7 %collective-permute-start.9 = (bf16[2,4,4,24,384]{4,3,2,1,0:T(8,128)(2,1)S(1)}, bf16[2,4,4,24,384]{4,3,2,1,0:T(8,128)(2,1)S(1)}, u32[]{:S(2)}, u32[]{:S(2)}) collective-permute-start(bf16[2,4,4,24,384]{4,3,2,1,0:T(8,128)(2,1)S(1)} %get-tuple-element.90), channel_id=1, source_target_pairs={{0,4},{4,0},{8,12},{12,8},{1,5},{5,1},{9,13},{13,9},{2,6},{6,2},{1... | collective-permute-start | bytes 1769480 | tf_op jit(solution)/shard_map/ppermute | solution.py:39
  45.5 4.6 %copy-start.3 = (bf16[256,768]{1,0:T(8,128)(2,1)S(1)}, bf16[256,768]{1,0:T(8,128)(2,1)}, u32[]{:S(2)}) copy-start(bf16[256,768]{1,0:T(8,128)(2,1)} %get-tuple-element.69.act_ref) | copy-start | bytes 1179652
  48.7 16.8 %collective-permute-start.6 = (bf16[2,4,4,24,384]{4,3,2,1,0:T(8,128)(2,1)S(1)}, bf16[2,4,4,24,384]{4,3,2,1,0:T(8,128)(2,1)S(1)}, u32[]{:S(2)}, u32[]{:S(2)}) collective-permute-start(bf16[2,4,4,24,384]{4,3,2,1,0:T(8,128)(2,1)S(1)} %get-tuple-element.84), channel_id=1, source_target_pairs={{0,32},{32,0},{64,96},{96,64},{1,33},{33,1},{65,97},{97,65},{2,34}... | collective-permute-start | bytes 1769480 | tf_op jit(solution)/shard_map/ppermute | solution.py:39
  52.0 15.1 %collective-permute-start.10 = (bf16[2,4,4,24,384]{4,3,2,1,0:T(8,128)(2,1)S(1)}, bf16[2,4,4,24,384]{4,3,2,1,0:T(8,128)(2,1)S(1)}, u32[]{:S(2)}, u32[]{:S(2)}) collective-permute-start(bf16[2,4,4,24,384]{4,3,2,1,0:T(8,128)(2,1)S(1)} %get-tuple-element.93), channel_id=1, source_target_pairs={{0,12},{4,8},{8,4},{12,0},{1,13},{5,9},{9,5},{13,1},{2,14},{6,10},... | collective-permute-start | bytes 1769480 | tf_op jit(solution)/shard_map/ppermute | solution.py:39
  53.9 11.6 %collective-permute-start.7 = (bf16[2,4,3,24,384]{4,3,2,1,0:T(8,128)(2,1)S(1)}, bf16[2,4,3,24,384]{4,3,2,1,0:T(8,128)(2,1)S(1)}, u32[]{:S(2)}, u32[]{:S(2)}) collective-permute-start(bf16[2,4,3,24,384]{4,3,2,1,0:T(8,128)(2,1)S(1)} %get-tuple-element.86), channel_id=1, source_target_pairs={{0,96},{32,64},{64,32},{96,0},{1,97},{33,65},{65,33},{97,1},{2,98}... | collective-permute-start | bytes 1327112 | tf_op jit(solution)/shard_map/ppermute | solution.py:39
  67.5 8.9 %collective-permute-start.11 = (bf16[4,4,24,384]{3,2,1,0:T(8,128)(2,1)S(1)}, bf16[4,4,24,384]{3,2,1,0:T(8,128)(2,1)S(1)}, u32[]{:S(2)}, u32[]{:S(2)}) collective-permute-start(bf16[4,4,24,384]{3,2,1,0:T(8,128)(2,1)S(1)} %get-tuple-element.95), channel_id=1, source_target_pairs={{0,96},{32,64},{64,32},{96,0},{1,97},{33,65},{65,33},{97,1},{2,98}... | collective-permute-start | bytes 884744 | tf_op jit(solution)/shard_map/ppermute | solution.py:39
  69.5 7.5 %collective-permute-start.13 = (bf16[4,4,24,384]{3,2,1,0:T(8,128)(2,1)S(1)}, bf16[4,4,24,384]{3,2,1,0:T(8,128)(2,1)S(1)}, u32[]{:S(2)}, u32[]{:S(2)}) collective-permute-start(bf16[4,4,24,384]{3,2,1,0:T(8,128)(2,1)S(1)} %get-tuple-element.99), channel_id=1, source_target_pairs={{0,12},{4,8},{8,4},{12,0},{1,13},{5,9},{9,5},{13,1},{2,14},{6,10},... | collective-permute-start | bytes 884744 | tf_op jit(solution)/shard_map/ppermute | solution.py:39
  71.3 6.0 %collective-permute-start.14 = (bf16[4,4,24,384]{3,2,1,0:T(8,128)(2,1)S(1)}, bf16[4,4,24,384]{3,2,1,0:T(8,128)(2,1)S(1)}, u32[]{:S(2)}, u32[]{:S(2)}) collective-permute-start(bf16[4,4,24,384]{3,2,1,0:T(8,128)(2,1)S(1)} %get-tuple-element.101), channel_id=1, source_target_pairs={{0,4},{4,0},{8,12},{12,8},{1,5},{5,1},{9,13},{13,9},{2,6},{6,2},{1... | collective-permute-start | bytes 884744 | tf_op jit(solution)/shard_map/ppermute | solution.py:39
  71.3 5.1 %collective-permute-start.12 = (bf16[4,3,24,384]{3,2,1,0:T(8,128)(2,1)S(1)}, bf16[4,3,24,384]{3,2,1,0:T(8,128)(2,1)S(1)}, u32[]{:S(2)}, u32[]{:S(2)}) collective-permute-start(bf16[4,3,24,384]{3,2,1,0:T(8,128)(2,1)S(1)} %get-tuple-element.97), channel_id=1, source_target_pairs={{0,32},{32,0},{64,96},{96,64},{1,33},{33,1},{65,97},{97,65},{2,34}... | collective-permute-start | bytes 663560 | tf_op jit(solution)/shard_map/ppermute | solution.py:39
  78.2 6.6 %collective-permute-start.15 = (bf16[2,4,24,384]{3,2,1,0:T(8,128)(2,1)S(1)}, bf16[2,4,24,384]{3,2,1,0:T(8,128)(2,1)S(1)}, u32[]{:S(2)}, u32[]{:S(2)}) collective-permute-start(bf16[2,4,24,384]{3,2,1,0:T(8,128)(2,1)S(1)} %get-tuple-element.103), channel_id=1, source_target_pairs={{0,4},{4,0},{8,12},{12,8},{1,5},{5,1},{9,13},{13,9},{2,6},{6,2},{1... | collective-permute-start | bytes 442376 | tf_op jit(solution)/shard_map/ppermute | solution.py:39
  78.9 5.9 %collective-permute-start.17 = (bf16[2,4,24,384]{3,2,1,0:T(8,128)(2,1)S(1)}, bf16[2,4,24,384]{3,2,1,0:T(8,128)(2,1)S(1)}, u32[]{:S(2)}, u32[]{:S(2)}) collective-permute-start(bf16[2,4,24,384]{3,2,1,0:T(8,128)(2,1)S(1)} %get-tuple-element.107), channel_id=1, source_target_pairs={{0,32},{32,0},{64,96},{96,64},{1,33},{33,1},{65,97},{97,65},{2,34}... | collective-permute-start | bytes 442376 | tf_op jit(solution)/shard_map/ppermute | solution.py:39
  79.3 5.5 %collective-permute-start.18 = (bf16[2,4,24,384]{3,2,1,0:T(8,128)(2,1)S(1)}, bf16[2,4,24,384]{3,2,1,0:T(8,128)(2,1)S(1)}, u32[]{:S(2)}, u32[]{:S(2)}) collective-permute-start(bf16[2,4,24,384]{3,2,1,0:T(8,128)(2,1)S(1)} %get-tuple-element.109), channel_id=1, source_target_pairs={{0,96},{32,64},{64,32},{96,0},{1,97},{33,65},{65,33},{97,1},{2,98}... | collective-permute-start | bytes 442376 | tf_op jit(solution)/shard_map/ppermute | solution.py:39
  80.0 4.8 %collective-permute-start.16 = (bf16[2,3,24,384]{3,2,1,0:T(8,128)(2,1)S(1)}, bf16[2,3,24,384]{3,2,1,0:T(8,128)(2,1)S(1)}, u32[]{:S(2)}, u32[]{:S(2)}) collective-permute-start(bf16[2,3,24,384]{3,2,1,0:T(8,128)(2,1)S(1)} %get-tuple-element.105), channel_id=1, source_target_pairs={{0,12},{4,8},{8,4},{12,0},{1,13},{5,9},{9,5},{13,1},{2,14},{6,10},... | collective-permute-start | bytes 331784 | tf_op jit(solution)/shard_map/ppermute | solution.py:39
  84.9 6.1 %collective-permute-start.19 = (bf16[4,24,384]{2,1,0:T(8,128)(2,1)S(1)}, bf16[4,24,384]{2,1,0:T(8,128)(2,1)S(1)}, u32[]{:S(2)}, u32[]{:S(2)}) collective-permute-start(bf16[4,24,384]{2,1,0:T(8,128)(2,1)S(1)} %get-tuple-element.111), channel_id=1, source_target_pairs={{0,12},{4,8},{8,4},{12,0},{1,13},{5,9},{9,5},{13,1},{2,14},{6,10},... | collective-permute-start | bytes 221192 | tf_op jit(solution)/shard_map/ppermute | solution.py:39
  86.3 4.7 %collective-permute-start.21 = (bf16[4,24,384]{2,1,0:T(8,128)(2,1)S(1)}, bf16[4,24,384]{2,1,0:T(8,128)(2,1)S(1)}, u32[]{:S(2)}, u32[]{:S(2)}) collective-permute-start(bf16[4,24,384]{2,1,0:T(8,128)(2,1)S(1)} %get-tuple-element.115), channel_id=1, source_target_pairs={{0,96},{32,64},{64,32},{96,0},{1,97},{33,65},{65,33},{97,1},{2,98}... | collective-permute-start | bytes 221192 | tf_op jit(solution)/shard_map/ppermute | solution.py:39
  88.0 3.2 %collective-permute-start.22 = (bf16[4,24,384]{2,1,0:T(8,128)(2,1)S(1)}, bf16[4,24,384]{2,1,0:T(8,128)(2,1)S(1)}, u32[]{:S(2)}, u32[]{:S(2)}) collective-permute-start(bf16[4,24,384]{2,1,0:T(8,128)(2,1)S(1)} %get-tuple-element.117), channel_id=1, source_target_pairs={{0,32},{32,0},{64,96},{96,64},{1,33},{33,1},{65,97},{97,65},{2,34}... | collective-permute-start | bytes 221192 | tf_op jit(solution)/shard_map/ppermute | solution.py:39
  88.0 3.0 %collective-permute-start.20 = (bf16[3,24,384]{2,1,0:T(8,128)(2,1)S(1)}, bf16[3,24,384]{2,1,0:T(8,128)(2,1)S(1)}, u32[]{:S(2)}, u32[]{:S(2)}) collective-permute-start(bf16[3,24,384]{2,1,0:T(8,128)(2,1)S(1)} %get-tuple-element.113), channel_id=1, source_target_pairs={{0,4},{4,0},{8,12},{12,8},{1,5},{5,1},{9,13},{13,9},{2,6},{6,2},{1... | collective-permute-start | bytes 165896 | tf_op jit(solution)/shard_map/ppermute | solution.py:39
  91.8 5.6 %collective-permute-start.23 = (bf16[8,24,384]{2,1,0:T(8,128)(2,1)S(1)}, bf16[8,24,384]{2,1,0:T(8,128)(2,1)S(1)}, u32[]{:S(2)}, u32[]{:S(2)}) collective-permute-start(bf16[8,24,384]{2,1,0:T(8,128)(2,1)S(1)} %get-tuple-element.119), channel_id=1, source_target_pairs={{0,16},{16,0},{1,17},{17,1},{2,18},{18,2},{3,19},{19,3},{4,20},{20... | collective-permute-start | bytes 442376 | tf_op jit(solution)/shard_map/ppermute | solution.py:34

commit v9 on v8

--- a/solution.py
+++ b/solution.py
@@ -15,6 +15,7 @@
 Y, ZH, X, CORE = DP
 LANES = 128
 ROWS, COLS = 24, 384
+SIZE, SECOND = 344, 320
 DEPTH = 512
 VMEM = pl.BlockSpec(memory_space=pltpu.VMEM)
 SMEM = pl.BlockSpec(memory_space=pltpu.SMEM)
@@ -118,6 +119,22 @@
     sent_ref[...] = narrow(dot(act_first, w_middle[...]))
 
 
+def half_kernel(place_ref, w_last_hbm, half_ref, w_last, sem):
+    copy = pltpu.make_async_copy(w_last_hbm, w_last, sem)
+    copy.start()
+    copy.wait()
+    size, total = half_ref.shape[0], w_last.shape[0]
+
+    @pl.when(place_ref[0] == 0)
+    def _():
+        half_ref[...] = w_last[0:size, :]
+
+    @pl.when(place_ref[0] != 0)
+    def _():
+        half_ref[size - 8 :, :] = jnp.zeros((8, half_ref.shape[1]), half_ref.dtype)
+        half_ref[0 : total - SECOND, :] = w_last[SECOND:total, :]
+
+
 def stage_kernel(
     place_ref, counts_ref, pre_first_ref, orders_ref, target_hbm, w_last_hbm,
     w_own_ref, target_own_ref, target_other_ref, first_slope_ref, onehot_ref, live_ref,
@@ -174,9 +191,17 @@
     onehot_ref, fetched_ref, relayed_ref, w_middle_ref, sent_ref, own_ref, rows_ref,
 ):
     core = place_ref[0]
-    w_other = jnp.where(core == 0, fetched_ref[...], relayed_ref[...])
-    slope = slope_of(w_other, act_ref[...], target_ref[...], live_ref[...])
-    back = back_ref[...] + contract(slope, w_other, 0, 0)
+    size, total = fetched_ref.shape[0], target_ref.shape[0]
+    act, live = act_ref[...], live_ref[...]
+    back = back_ref[...]
+    for is_own, start, stop in ((core == 0, 0, size), (core != 0, SECOND, total)):
+        rows = slice(0, stop - start)
+        weights = jnp.where(is_own, fetched_ref[rows, :], relayed_ref[rows, :])
+        slope = slope_of(weights, act, target_ref[start:stop, :], live)
+        if start:
+            column = lax.broadcasted_iota(jnp.int32, slope.shape, 0) + start
+            slope = jnp.where(column >= size, slope, jnp.zeros_like(slope))
+        back += contract(slope, weights, 0, 0)
     slope_middle = narrow(back * act_slope_ref[...])
     slope_first = narrow(contract(slope_middle, w_middle_ref[...], 1, 1) * first_slope_ref[...])
     slope_first = narrow(contract(onehot_ref[...], slope_first, 1, 1))
@@ -325,11 +350,19 @@
     hidden = w_middle.shape[1]
     belief_t, w_last_t = belief.T, w_last.T
 
-    around = (ZH, CORE, "mp")
-    fetched = lax.ppermute(w_last_t, around, [(0, 5), (5, 0), (1, 4), (4, 1)])
-
     indices = (CORE, Y, X, ZH, "mp")
     place = jnp.stack([lax.axis_index(axis) for axis in indices])
+
+    (half,) = call(
+        half_kernel,
+        "half",
+        [SMEM, HBM],
+        [((SIZE, hidden), BF16)],
+        [pltpu.VMEM(w_last_t.shape, BF16), pltpu.SemaphoreType.DMA],
+    )(place, w_last_t)
+    fetched = lax.ppermute(half, (ZH, "mp"), [(0, 3), (3, 0), (1, 2), (2, 1)])
+    belief_first, half = lax.optimization_barrier((belief_t, half))
+
     pre_first, act_first, hidden_sent = call(
         forward_kernel,
         "forward",
@@ -346,11 +379,8 @@
             pltpu.SemaphoreType.DMA((2 * pl.cdiv(inputs, DEPTH) + 1,)),
         ],
         kind=pltpu.HBM,
-    )(belief_t, w_first, w_middle)
+    )(belief_first, w_first, w_middle)
     arrived = swap(hidden_sent, "mp")
-    belief_swapped, act_first = lax.optimization_barrier((belief_t, act_first))
-    sibling_belief = swap(belief_swapped, CORE)
-    sibling_act = swap(act_first, CORE)
 
     order = np.arange(units, dtype=np.int32).reshape(4, 2, 4, 2, -1).transpose(3, 0, 2, 1, 4)
     orders = np.stack([order[::-1], order]).reshape(2, units, 1)
@@ -368,10 +398,11 @@
         ],
         [pltpu.VMEM((2 * width, total_rows), BF16), pltpu.SemaphoreType.DMA((2,))],
     )(place, counts, pre_first, jnp.asarray(orders), target_value.T, w_last_t)
-    fetched, live, sibling_belief, sibling_act = lax.optimization_barrier(
-        (fetched, live, sibling_belief, sibling_act)
-    )
-    relayed = lax.ppermute(fetched, CORE, [(0, 1)])
+    fetched, live = lax.optimization_barrier((fetched, live))
+    relayed = swap(fetched, CORE)
+    belief_swapped, act_swapped = lax.optimization_barrier((belief_t, act_first))
+    sibling_belief = swap(belief_swapped, CORE)
+    sibling_act = swap(act_swapped, CORE)
 
     act, act_slope, back_own, last_sent, last_own = call(
         hidden_kernel,

time: 124 us -> 119 us (0.960)
  blocking collectives: 24.7 us -> 22.8 us
  starting transfers between devices: 27.5 us -> 26.1 us
    ppermute x6 -> x7, waiting for transfers between devices: 18.3 us -> 5.52 us  [swap(): return lax.ppermute(shard, axis, [(0, 1), (1, 0)])]
    ppermute x2 -> x1, waiting for transfers between devices: 0.01 us -> 12.4 us  [per_device(): fetched = lax.ppermute(half, (ZH, 'mp'), [(0, 3), (3, 0), (1, 2), (2, 1)])]
    ppermute x6 -> x7, starting transfers between devices: 8.43 us -> 4.61 us  [swap(): return lax.ppermute(shard, axis, [(0, 1), (1, 0)])]
    ppermute x2 -> x1, starting transfers between devices: 2.08 us -> 4.67 us  [per_device(): fetched = lax.ppermute(half, (ZH, 'mp'), [(0, 3), (3, 0), (1, 2), (2, 1)])]
    all_to_all x1, blocking collectives: 24.7 us -> 22.8 us  [per_device(): squares = lax.all_to_all(squares, ALL, 0, 0, tiled=True)]
    pallas_call x13 -> x14, Pallas kernels: 26 us -> 27 us  [run(): kernel(*(operand if spec is SMEM else pltpu.with_memory_space_constraint(...]
  transfers between devices with their start and end apart: 24 -> 24, of which waited for: 11 -> 9; matrix products, arithmetic and copies ran while one was open for 0% -> 0% of each run, Pallas kernels for 19% -> 18%
where the time goes in v9:
time: 119 us
  waiting for transfers between devices  41.3 us (35%)
  Pallas kernels  27 us (23%)
  starting transfers between devices  26.1 us (22%)
  blocking collectives  22.8 us (19%)
  local copies, waits for them, and re-layouts  1.24 us (1%)
    pallas_call x14, Pallas kernels, run(): kernel(*(operand if spec is SMEM else pltpu.with_memory_space_constraint(...  27 us
    ppermute x16, waiting for transfers between devices, to_pair(): return lax.ppermute(shard, axis, pairs)  23.4 us
    all_to_all x1, blocking collectives, per_device(): squares = lax.all_to_all(squares, ALL, 0, 0, tiled=True)  22.8 us
    ppermute x16, starting transfers between devices, to_pair(): return lax.ppermute(shard, axis, pairs)  16.8 us
    ppermute x1, waiting for transfers between devices, per_device(): fetched = lax.ppermute(half, (ZH, 'mp'), [(0, 3), (3, 0), (1, 2), (2, 1)])  12.4 us
    ppermute x7, waiting for transfers between devices, swap(): return lax.ppermute(shard, axis, [(0, 1), (1, 0)])  5.52 us
    ppermute x1, starting transfers between devices, per_device(): fetched = lax.ppermute(half, (ZH, 'mp'), [(0, 3), (3, 0), (1, 2), (2, 1)])  4.67 us
    ppermute x7, starting transfers between devices, swap(): return lax.ppermute(shard, axis, [(0, 1), (1, 0)])  4.61 us
  transfers between devices with their start and end apart: 24, of which 9 were waited for; matrix products, arithmetic and copies ran while one was open for 0% of the time, Pallas kernels for 18%

profile of v9, /device:TPU:1, one launch (start us, length us, event | category | flops | bytes accessed | tf_op | source)
XLA Modules:
  0.0 119.2 jit_solution(12347963370143326436)
XLA Ops:
  0.6 0.1 stack.23.place_ref
  0.7 2.2 %half.1 = bf16[344,1536]{1,0:T(8,128)(2,1)S(1)} custom-call(s32[5]{0:T(128)S(1)} %stack.23.place_ref, bf16[663,1536]{1,0:T(8,128)(2,1)} %bitcast.13), custom_call_target="tpu_custom_call" | custom-call | flops 17179869184 | bytes 67108864 | tf_op jit(solution)/shard_map/half/pallas_call | solution.py:71
  2.9 4.7 %collective-permute-start.1 = (bf16[344,1536]{1,0:T(8,128)(2,1)S(1)}, bf16[344,1536]{1,0:T(8,128)(2,1)S(1)}, u32[]{:S(2)}, u32[]{:S(2)}) collective-permute-start(bf16[344,1536]{1,0:T(8,128)(2,1)S(1)} %half.1), channel_id=1, source_target_pairs={{0,17},{17,0},{1,16},{16,1},{2,19},{19,2},{3,18},{18,3},{4,21},{21... | collective-permute-start | bytes 3170312 | tf_op jit(solution)/shard_map/ppermute | solution.py:363
  7.6 5.9 %forward.1 = (f32[256,768]{1,0:T(8,128)}, bf16[256,768]{1,0:T(8,128)(2,1)}, bf16[256,1536]{1,0:T(8,128)(2,1)}) custom-call(bf16[2652,256]{1,0:T(8,128)(2,1)} %bitcast.10, bf16[2652,768]{1,0:T(8,128)(2,1)} %w_first_hbm.1, bf16[768,1536]{1,0:T(8,128)(2,1)} %w_middle_ref.1), custom_call_target="tpu_custom_call" | custom-call | flops 17179869184 | bytes 67108864 | tf_op jit(solution)/shard_map/forward/pallas_call | solution.py:71
  13.5 0.1 collective-permute-start
  13.6 1.0 collective-permute-start.9
  14.7 0.1 collective-permute-start.4
  14.8 1.1 copy-done.6
  15.9 2.4 %stage.1 = (bf16[663,1536]{1,0:T(8,128)(2,1)S(1)}, bf16[663,256]{1,0:T(8,128)(2,1)S(1)}, bf16[663,256]{1,0:T(8,128)(2,1)S(1)}, f32[256,768]{1,0:T(8,128)S(1)}, b...) custom-call(s32[5]{0:T(128)S(1)} %stack.23.place_ref, s32[2]{0:T(128)S(1)} %copy-done.4, f32[256,768]{1,0:T(8,128)S(1)} %copy-done.6, ...), custom_call_target="tpu_custom_call" | custom-call | flops 17179869184 | bytes 67108864 | tf_op jit(solution)/shard_map/stage/pallas_call | solution.py:71
  18.3 12.4 %collective-permute-done.1.fetched_ref = bf16[344,1536]{1,0:T(8,128)(2,1)S(1)} collective-permute-done((bf16[344,1536]{1,0:T(8,128)(2,1)S(1)}, bf16[344,1536]{1,0:T(8,128)(2,1)S(1)}, u32[]{:S(2)}, u32[]{:S(2)}) %collective-permute-start.1) | collective-permute-done | bytes 1056800 | tf_op jit(solution)/shard_map/ppermute | solution.py:363
  30.6 1.2 %collective-permute-start.2 = (bf16[344,1536]{1,0:T(8,128)(2,1)S(1)}, bf16[344,1536]{1,0:T(8,128)(2,1)S(1)}, u32[]{:S(2)}, u32[]{:S(2)}) collective-permute-start(bf16[344,1536]{1,0:T(8,128)(2,1)S(1)} %collective-permute-done.1.fetched_ref), channel_id=1, source_target_pairs={{0,2},{2,0},{1,3},{3,1},{4,6},{6,4},{5,7},{7,5},{8,10},{10,8},{9,1... | collective-permute-start | bytes 3170312 | tf_op jit(solution)/shard_map/ppermute | solution.py:35
  31.9 0.0 collective-permute-done.arrived_ref
  31.9 3.1 %hidden.1 = (bf16[256,1536]{1,0:T(8,128)(2,1)S(1)}, f32[256,1536]{1,0:T(8,128)S(1)}, f32[256,1536]{1,0:T(8,128)S(1)}, bf16[1431,256]{1,0:T(8,128)(2,1)S(1)}, bf16[768,256]{1,0:T(8,128)(2,1)S(1)}) custom-call(s32[5]{0:T(128)S(1)} %stack.23.place_ref, bf16[256,1536]{1,0:T(8,128)(2,1)S(1)} %copy-done.2, bf16[256,1536]{1,0:T(8,128)(2,1)S(1)} %collective-permute-done.arrived_ref, ...), custom_call_target="tpu_custom_call" | custom-call | flops 17179869184 | bytes 67108864 | tf_op jit(solution)/shard_map/hidden/pallas_call | solution.py:71
  35.0 2.0 %collective-permute-start.7 = (bf16[1431,256]{1,0:T(8,128)(2,1)S(1)}, bf16[1431,256]{1,0:T(8,128)(2,1)S(1)}, u32[]{:S(2)}, u32[]{:S(2)}) collective-permute-start(bf16[1431,256]{1,0:T(8,128)(2,1)S(1)} %get-tuple-element.86.sent_ref), channel_id=1, source_target_pairs={{0,2},{2,0},{1,3},{3,1},{4,6},{6,4},{5,7},{7,5},{8,10},{10,8},{9,1... | collective-permute-start | bytes 2198024 | tf_op jit(solution)/shard_map/ppermute | solution.py:35
  36.9 0.0 collective-permute-done.2.relayed_ref
  37.0 5.0 %slopes.1 = (bf16[1152,256]{1,0:T(8,128)(2,1)S(1)}, bf16[1152,256]{1,0:T(8,128)(2,1)S(1)}) custom-call(s32[5]{0:T(128)S(1)} %stack.23.place_ref, bf16[256,1536]{1,0:T(8,128)(2,1)S(1)} %get-tuple-element.70.act_ref, f32[256,1536]{1,0:T(8,128)S(1)} %get-tuple-element.71.act_slope_ref, f32[256,1536]{1,0:T(8,128)S(1)} %get-tuple-element.72.back_ref, ...), custom_call_target="tpu_custom_call" | custom-call | flops 17179869184 | bytes 67108864 | tf_op jit(solution)/shard_map/slopes/pallas_call | solution.py:71
  41.9 0.1 collective-permute-start.3
  42.0 0.0 collective-permute-done.7.arrived_ref
  42.1 1.5 %last.1 = (f32[2,4,4,24,384]{4,3,2,1,0:T(8,128)S(1)}, bf16[2,4,4,24,384]{4,3,2,1,0:T(8,128)(2,1)S(1)}) custom-call(s32[5]{0:T(128)S(1)} %stack.23.place_ref, bf16[768,256]{1,0:T(8,128)(2,1)S(1)} %get-tuple-element.85.own_ref, bf16[1431,256]{1,0:T(8,128)(2,1)S(1)} %get-tuple-element.86.sent_ref, bf16[1431,256]{1,0:T(8,128)(2,1)S(1)} %collective-permute-done.7.arrived_ref), custom_call_target="tpu_custom_call" | custom-call | flops 17179869184 | bytes 67108864 | tf_op jit(solution)/shard_map/last/pallas_call | solution.py:71
  43.6 1.5 %collective-permute-start.8 = (bf16[2,4,4,24,384]{4,3,2,1,0:T(8,128)(2,1)S(1)}, bf16[2,4,4,24,384]{4,3,2,1,0:T(8,128)(2,1)S(1)}, u32[]{:S(2)}, u32[]{:S(2)}) collective-permute-start(bf16[2,4,4,24,384]{4,3,2,1,0:T(8,128)(2,1)S(1)} %get-tuple-element.88), channel_id=1, source_target_pairs={{0,4},{4,0},{8,12},{12,8},{1,5},{5,1},{9,13},{13,9},{2,6},{6,2},{1... | collective-permute-start | bytes 1769480 | tf_op jit(solution)/shard_map/ppermute | solution.py:40
  45.0 0.0 collective-permute-done.9.sibling_act_ref
  45.0 0.0 collective-permute-done.3.arrived_ref
  45.0 1.5 %middle.1 = (f32[2,4,4,24,384]{4,3,2,1,0:T(8,128)S(1)}, bf16[2,4,4,24,384]{4,3,2,1,0:T(8,128)(2,1)S(1)}) custom-call(s32[5]{0:T(128)S(1)} %stack.23.place_ref, bf16[1152,256]{1,0:T(8,128)(2,1)S(1)} %get-tuple-element.77.own_ref, bf16[1152,256]{1,0:T(8,128)(2,1)S(1)} %collective-permute-done.3.arrived_ref, bf16[256,768]{1,0:T(8,128)(2,1)S(1)} %copy-done.3, ...), custom_call_target="tpu_custom_call" | custom-call | flops 17179869184 | bytes 67108864 | tf_op jit(solution)/shard_map/middle/pallas_call | solution.py:71
  46.5 1.9 %collective-permute-start.10 = (bf16[2,4,4,24,384]{4,3,2,1,0:T(8,128)(2,1)S(1)}, bf16[2,4,4,24,384]{4,3,2,1,0:T(8,128)(2,1)S(1)}, u32[]{:S(2)}, u32[]{:S(2)}) collective-permute-start(bf16[2,4,4,24,384]{4,3,2,1,0:T(8,128)(2,1)S(1)} %get-tuple-element.91), channel_id=1, source_target_pairs={{0,12},{4,8},{8,4},{12,0},{1,13},{5,9},{9,5},{13,1},{2,14},{6,10},... | collective-permute-start | bytes 1769480 | tf_op jit(solution)/shard_map/ppermute | solution.py:40
  48.4 0.0 collective-permute-done.4.sibling_belief_ref
  48.4 2.4 %first.1 = (f32[2,4,4,24,384]{4,3,2,1,0:T(8,128)S(1)}, bf16[2,4,4,24,384]{4,3,2,1,0:T(8,128)(2,1)S(1)}, f32[2,4,3,24,384]{4,3,2,1,0:T(8,128)S(1)}, bf16[2,4,3,24,384]{4,3,2,1,0:T(8,128)(2,1)S(1)}) custom-call(s32[5]{0:T(128)S(1)} %stack.23.place_ref, bf16[1152,256]{1,0:T(8,128)(2,1)S(1)} %get-tuple-element.77.own_ref, ...), custom_call_target="tpu_custom_call" | custom-call | flops 17179869184 | bytes 67108864 | tf_op jit(solution)/shard_map/first/pallas_call | solution.py:71
  50.8 1.4 %collective-permute-start.5 = (bf16[2,4,4,24,384]{4,3,2,1,0:T(8,128)(2,1)S(1)}, bf16[2,4,4,24,384]{4,3,2,1,0:T(8,128)(2,1)S(1)}, u32[]{:S(2)}, u32[]{:S(2)}) collective-permute-start(bf16[2,4,4,24,384]{4,3,2,1,0:T(8,128)(2,1)S(1)} %get-tuple-element.82), channel_id=1, source_target_pairs={{0,32},{32,0},{64,96},{96,64},{1,33},{33,1},{65,97},{97,65},{2,34}... | collective-permute-start | bytes 1769480 | tf_op jit(solution)/shard_map/ppermute | solution.py:40
  52.2 1.9 %collective-permute-start.6 = (bf16[2,4,3,24,384]{4,3,2,1,0:T(8,128)(2,1)S(1)}, bf16[2,4,3,24,384]{4,3,2,1,0:T(8,128)(2,1)S(1)}, u32[]{:S(2)}, u32[]{:S(2)}) collective-permute-start(bf16[2,4,3,24,384]{4,3,2,1,0:T(8,128)(2,1)S(1)} %get-tuple-element.84), channel_id=1, source_target_pairs={{0,96},{32,64},{64,32},{96,0},{1,97},{33,65},{65,33},{97,1},{2,98}... | collective-permute-start | bytes 1327112 | tf_op jit(solution)/shard_map/ppermute | solution.py:40
  54.1 4.2 %collective-permute-done.8.refs_5_ = bf16[2,4,4,24,384]{4,3,2,1,0:T(8,128)(2,1)S(1)} collective-permute-done((bf16[2,4,4,24,384]{4,3,2,1,0:T(8,128)(2,1)S(1)}, bf16[2,4,4,24,384]{4,3,2,1,0:T(8,128)(2,1)S(1)}, u32[]{:S(2)}, u32[]{:S(2)}) %collective-permute-start.8) | collective-permute-done | bytes 589856 | tf_op jit(solution)/shard_map/ppermute | solution.py:40
  58.2 5.5 %collective-permute-done.6.refs_3_ = bf16[2,4,3,24,384]{4,3,2,1,0:T(8,128)(2,1)S(1)} collective-permute-done((bf16[2,4,3,24,384]{4,3,2,1,0:T(8,128)(2,1)S(1)}, bf16[2,4,3,24,384]{4,3,2,1,0:T(8,128)(2,1)S(1)}, u32[]{:S(2)}, u32[]{:S(2)}) %collective-permute-start.6) | collective-permute-done | bytes 442400 | tf_op jit(solution)/shard_map/ppermute | solution.py:40
  63.7 0.0 collective-permute-done.10.refs_7_
  63.7 1.0 collective-permute-done.5.refs_1_
  64.7 0.4 halve.2
  65.1 2.8 %collective-permute-start.11 = (bf16[4,4,24,384]{3,2,1,0:T(8,128)(2,1)S(1)}, bf16[4,4,24,384]{3,2,1,0:T(8,128)(2,1)S(1)}, u32[]{:S(2)}, u32[]{:S(2)}) collective-permute-start(bf16[4,4,24,384]{3,2,1,0:T(8,128)(2,1)S(1)} %get-tuple-element.93), channel_id=1, source_target_pairs={{0,96},{32,64},{64,32},{96,0},{1,97},{33,65},{65,33},{97,1},{2,98}... | collective-permute-start | bytes 884744 | tf_op jit(solution)/shard_map/ppermute | solution.py:40
  67.8 0.9 collective-permute-start.13
  68.7 0.0 collective-permute-start.14
  68.7 0.0 collective-permute-start.12
  68.7 5.1 %collective-permute-done.12.refs_3_ = bf16[4,3,24,384]{3,2,1,0:T(8,128)(2,1)S(1)} collective-permute-done((bf16[4,3,24,384]{3,2,1,0:T(8,128)(2,1)S(1)}, bf16[4,3,24,384]{3,2,1,0:T(8,128)(2,1)S(1)}, u32[]{:S(2)}, u32[]{:S(2)}) %collective-permute-start.12) | collective-permute-done | bytes 221216 | tf_op jit(solution)/shard_map/ppermute | solution.py:40
  73.8 0.0 collective-permute-done.11.refs_1_
  73.8 1.5 %collective-permute-done.13.refs_5_ = bf16[4,4,24,384]{3,2,1,0:T(8,128)(2,1)S(1)} collective-permute-done((bf16[4,4,24,384]{3,2,1,0:T(8,128)(2,1)S(1)}, bf16[4,4,24,384]{3,2,1,0:T(8,128)(2,1)S(1)}, u32[]{:S(2)}, u32[]{:S(2)}) %collective-permute-start.13) | collective-permute-done | bytes 294944 | tf_op jit(solution)/shard_map/ppermute | solution.py:40
  75.3 0.0 collective-permute-done.14.refs_7_
  75.3 0.9 turn.1
  76.2 0.1 collective-permute-start.15
  76.3 0.1 collective-permute-start.17
  76.4 0.6 collective-permute-start.18
  77.0 1.7 %collective-permute-start.16 = (bf16[2,3,24,384]{3,2,1,0:T(8,128)(2,1)S(1)}, bf16[2,3,24,384]{3,2,1,0:T(8,128)(2,1)S(1)}, u32[]{:S(2)}, u32[]{:S(2)}) collective-permute-start(bf16[2,3,24,384]{3,2,1,0:T(8,128)(2,1)S(1)} %get-tuple-element.103), channel_id=1, source_target_pairs={{0,12},{4,8},{8,4},{12,0},{1,13},{5,9},{9,5},{13,1},{2,14},{6,10},... | collective-permute-start | bytes 331784 | tf_op jit(solution)/shard_map/ppermute | solution.py:40
  78.7 3.1 %collective-permute-done.16.refs_3_ = bf16[2,3,24,384]{3,2,1,0:T(8,128)(2,1)S(1)} collective-permute-done((bf16[2,3,24,384]{3,2,1,0:T(8,128)(2,1)S(1)}, bf16[2,3,24,384]{3,2,1,0:T(8,128)(2,1)S(1)}, u32[]{:S(2)}, u32[]{:S(2)}) %collective-permute-start.16) | collective-permute-done | bytes 110624 | tf_op jit(solution)/shard_map/ppermute | solution.py:40
  81.8 0.0 collective-permute-done.15.refs_1_
  81.8 0.0 collective-permute-done.17.refs_5_
  81.9 0.0 collective-permute-done.18.refs_7_
  81.9 0.1 halve.3
  82.0 1.8 %collective-permute-start.19 = (bf16[4,24,384]{2,1,0:T(8,128)(2,1)S(1)}, bf16[4,24,384]{2,1,0:T(8,128)(2,1)S(1)}, u32[]{:S(2)}, u32[]{:S(2)}) collective-permute-start(bf16[4,24,384]{2,1,0:T(8,128)(2,1)S(1)} %get-tuple-element.109), channel_id=1, source_target_pairs={{0,12},{4,8},{8,4},{12,0},{1,13},{5,9},{9,5},{13,1},{2,14},{6,10},... | collective-permute-start | bytes 221192 | tf_op jit(solution)/shard_map/ppermute | solution.py:40
  83.7 2.0 %collective-permute-start.21 = (bf16[4,24,384]{2,1,0:T(8,128)(2,1)S(1)}, bf16[4,24,384]{2,1,0:T(8,128)(2,1)S(1)}, u32[]{:S(2)}, u32[]{:S(2)}) collective-permute-start(bf16[4,24,384]{2,1,0:T(8,128)(2,1)S(1)} %get-tuple-element.113), channel_id=1, source_target_pairs={{0,96},{32,64},{64,32},{96,0},{1,97},{33,65},{65,33},{97,1},{2,98}... | collective-permute-start | bytes 221192 | tf_op jit(solution)/shard_map/ppermute | solution.py:40
  85.8 0.3 collective-permute-start.22
  86.0 0.0 collective-permute-start.20
  86.0 3.0 %collective-permute-done.20.refs_3_ = bf16[3,24,384]{2,1,0:T(8,128)(2,1)S(1)} collective-permute-done((bf16[3,24,384]{2,1,0:T(8,128)(2,1)S(1)}, bf16[3,24,384]{2,1,0:T(8,128)(2,1)S(1)}, u32[]{:S(2)}, u32[]{:S(2)}) %collective-permute-start.20) | collective-permute-done | bytes 55328 | tf_op jit(solution)/shard_map/ppermute | solution.py:40
  89.0 0.0 collective-permute-done.19.refs_1_
  89.0 0.0 collective-permute-done.22.refs_7_
  89.0 0.6 z_cut.1
  89.7 0.1 collective-permute-start.23
  89.8 5.5 %collective-permute-done.23.arrived_ref = bf16[8,24,384]{2,1,0:T(8,128)(2,1)S(1)} collective-permute-done((bf16[8,24,384]{2,1,0:T(8,128)(2,1)S(1)}, bf16[8,24,384]{2,1,0:T(8,128)(2,1)S(1)}, u32[]{:S(2)}, u32[]{:S(2)}) %collective-permute-start.23) | collective-permute-done | bytes 147488 | tf_op jit(solution)/shard_map/ppermute | solution.py:35
  95.3 0.3 square.1
  95.5 22.8 %all_to_all.5.squares_ref = f32[128,1,128]{2,1,0:T(1,128)S(1)} all-to-all(f32[128,1,128]{2,1,0:T(1,128)S(1)} %get-tuple-element.119), channel_id=1, replica_groups=mesh['dp_0'=4,'dp_1'=2,'dp_2'=4,'dp_3'=2,'mp'=2] {'dp_0','dp_1','dp_2','..., dimensions={0} | all-to-all | bytes 131072 | tf_op jit(solution)/shard_map/all_to_all | solution.py:496
  118.3 0.9 scale.1
  (14 shorter events, 0.0 us)
Async XLA Ops:
  2.9 27.7 %collective-permute-start.1 = (bf16[344,1536]{1,0:T(8,128)(2,1)S(1)}, bf16[344,1536]{1,0:T(8,128)(2,1)S(1)}, u32[]{:S(2)}, u32[]{:S(2)}) collective-permute-start(bf16[344,1536]{1,0:T(8,128)(2,1)S(1)} %half.1), channel_id=1, source_target_pairs={{0,17},{17,0},{1,16},{16,1},{2,19},{19,2},{3,18},{18,3},{4,21},{21... | collective-permute-start | bytes 3170312 | tf_op jit(solution)/shard_map/ppermute | solution.py:363
  7.6 7.1 %copy-start.1 = (bf16[256,2652]{0,1:T(8,128)(2,1)S(1)}, bf16[256,2652]{0,1:T(8,128)(2,1)}, u32[]{:S(2)}) copy-start(bf16[256,2652]{0,1:T(8,128)(2,1)} %param.7) | copy-start | bytes 4073476
  7.6 7.2 %copy-start.4 = (s32[2]{0:T(128)S(1)}, s32[2]{0:T(128)}, u32[]{:S(2)}) copy-start(s32[2]{0:T(128)} %counts_ref.1) | copy-start | bytes 28
  7.6 7.2 %copy-start.5 = (s32[2,768,1]{2,1,0:T(8,128)S(1)}, s32[2,768,1]{2,1,0:T(8,128)}, u32[]{:S(2)}) copy-start(s32[2,768,1]{2,1,0:T(8,128)} %constant.21.clone.orders_ref) | copy-start | bytes 18436
  13.5 18.4 %collective-permute-start = (bf16[256,1536]{1,0:T(8,128)(2,1)}, bf16[256,1536]{1,0:T(8,128)(2,1)S(1)}, u32[]{:S(2)}, u32[]{:S(2)}) collective-permute-start(bf16[256,1536]{1,0:T(8,128)(2,1)} %get-tuple-element.64.partial_ref), channel_id=1, source_target_pairs={{0,1},{1,0},{2,3},{3,2},{4,5},{5,4},{6,7},{7,6},{8,9},{9,8},{10,11... | collective-permute-start | bytes 2359304 | tf_op jit(solution)/shard_map/ppermute | solution.py:35
  13.6 31.4 %collective-permute-start.9 = (bf16[256,768]{1,0:T(8,128)(2,1)}, bf16[256,768]{1,0:T(8,128)(2,1)S(1)}, u32[]{:S(2)}, u32[]{:S(2)}) collective-permute-start(bf16[256,768]{1,0:T(8,128)(2,1)} %get-tuple-element.89.act_ref), channel_id=1, source_target_pairs={{0,2},{2,0},{1,3},{3,1},{4,6},{6,4},{5,7},{7,5},{8,10},{10,8},{9,1... | collective-permute-start | bytes 1179656 | tf_op jit(solution)/shard_map/ppermute | solution.py:35
  14.7 33.8 %collective-permute-start.4 = (bf16[2652,256]{1,0:T(8,128)(2,1)S(1)}, bf16[2652,256]{1,0:T(8,128)(2,1)S(1)}, u32[]{:S(2)}, u32[]{:S(2)}) collective-permute-start(bf16[2652,256]{1,0:T(8,128)(2,1)S(1)} %bitcast.11), channel_id=1, source_target_pairs={{0,2},{2,0},{1,3},{3,1},{4,6},{6,4},{5,7},{7,5},{8,10},{10,8},{9,1... | collective-permute-start | bytes 4073480 | tf_op jit(solution)/shard_map/ppermute | solution.py:35
  14.8 1.1 copy-start.6
  15.9 16.0 %copy-start.2 = (bf16[256,1536]{1,0:T(8,128)(2,1)S(1)}, bf16[256,1536]{1,0:T(8,128)(2,1)}, u32[]{:S(2)}) copy-start(bf16[256,1536]{1,0:T(8,128)(2,1)} %get-tuple-element.64.partial_ref) | copy-start | bytes 2359300
  30.6 6.3 %collective-permute-start.2 = (bf16[344,1536]{1,0:T(8,128)(2,1)S(1)}, bf16[344,1536]{1,0:T(8,128)(2,1)S(1)}, u32[]{:S(2)}, u32[]{:S(2)}) collective-permute-start(bf16[344,1536]{1,0:T(8,128)(2,1)S(1)} %collective-permute-done.1.fetched_ref), channel_id=1, source_target_pairs={{0,2},{2,0},{1,3},{3,1},{4,6},{6,4},{5,7},{7,5},{8,10},{10,8},{9,1... | collective-permute-start | bytes 3170312 | tf_op jit(solution)/shard_map/ppermute | solution.py:35
  31.9 5.0 %copy-start = (bf16[768,1536]{1,0:T(8,128)(2,1)S(1)}, bf16[768,1536]{1,0:T(8,128)(2,1)}, u32[]{:S(2)}) copy-start(bf16[768,1536]{1,0:T(8,128)(2,1)} %w_middle_ref.1) | copy-start | bytes 7077892
  35.0 7.1 %collective-permute-start.7 = (bf16[1431,256]{1,0:T(8,128)(2,1)S(1)}, bf16[1431,256]{1,0:T(8,128)(2,1)S(1)}, u32[]{:S(2)}, u32[]{:S(2)}) collective-permute-start(bf16[1431,256]{1,0:T(8,128)(2,1)S(1)} %get-tuple-element.86.sent_ref), channel_id=1, source_target_pairs={{0,2},{2,0},{1,3},{3,1},{4,6},{6,4},{5,7},{7,5},{8,10},{10,8},{9,1... | collective-permute-start | bytes 2198024 | tf_op jit(solution)/shard_map/ppermute | solution.py:35
  41.9 3.1 %collective-permute-start.3 = (bf16[1152,256]{1,0:T(8,128)(2,1)S(1)}, bf16[1152,256]{1,0:T(8,128)(2,1)S(1)}, u32[]{:S(2)}, u32[]{:S(2)}) collective-permute-start(bf16[1152,256]{1,0:T(8,128)(2,1)S(1)} %get-tuple-element.78), channel_id=1, source_target_pairs={{0,2},{2,0},{1,3},{3,1},{4,6},{6,4},{5,7},{7,5},{8,10},{10,8},{9,1... | collective-permute-start | bytes 1769480 | tf_op jit(solution)/shard_map/ppermute | solution.py:35
  42.1 3.0 %copy-start.3 = (bf16[256,768]{1,0:T(8,128)(2,1)S(1)}, bf16[256,768]{1,0:T(8,128)(2,1)}, u32[]{:S(2)}) copy-start(bf16[256,768]{1,0:T(8,128)(2,1)} %get-tuple-element.89.act_ref) | copy-start | bytes 1179652
  43.6 14.7 %collective-permute-start.8 = (bf16[2,4,4,24,384]{4,3,2,1,0:T(8,128)(2,1)S(1)}, bf16[2,4,4,24,384]{4,3,2,1,0:T(8,128)(2,1)S(1)}, u32[]{:S(2)}, u32[]{:S(2)}) collective-permute-start(bf16[2,4,4,24,384]{4,3,2,1,0:T(8,128)(2,1)S(1)} %get-tuple-element.88), channel_id=1, source_target_pairs={{0,4},{4,0},{8,12},{12,8},{1,5},{5,1},{9,13},{13,9},{2,6},{6,2},{1... | collective-permute-start | bytes 1769480 | tf_op jit(solution)/shard_map/ppermute | solution.py:40
  46.5 17.2 %collective-permute-start.10 = (bf16[2,4,4,24,384]{4,3,2,1,0:T(8,128)(2,1)S(1)}, bf16[2,4,4,24,384]{4,3,2,1,0:T(8,128)(2,1)S(1)}, u32[]{:S(2)}, u32[]{:S(2)}) collective-permute-start(bf16[2,4,4,24,384]{4,3,2,1,0:T(8,128)(2,1)S(1)} %get-tuple-element.91), channel_id=1, source_target_pairs={{0,12},{4,8},{8,4},{12,0},{1,13},{5,9},{9,5},{13,1},{2,14},{6,10},... | collective-permute-start | bytes 1769480 | tf_op jit(solution)/shard_map/ppermute | solution.py:40
  50.8 13.9 %collective-permute-start.5 = (bf16[2,4,4,24,384]{4,3,2,1,0:T(8,128)(2,1)S(1)}, bf16[2,4,4,24,384]{4,3,2,1,0:T(8,128)(2,1)S(1)}, u32[]{:S(2)}, u32[]{:S(2)}) collective-permute-start(bf16[2,4,4,24,384]{4,3,2,1,0:T(8,128)(2,1)S(1)} %get-tuple-element.82), channel_id=1, source_target_pairs={{0,32},{32,0},{64,96},{96,64},{1,33},{33,1},{65,97},{97,65},{2,34}... | collective-permute-start | bytes 1769480 | tf_op jit(solution)/shard_map/ppermute | solution.py:40
  52.2 11.6 %collective-permute-start.6 = (bf16[2,4,3,24,384]{4,3,2,1,0:T(8,128)(2,1)S(1)}, bf16[2,4,3,24,384]{4,3,2,1,0:T(8,128)(2,1)S(1)}, u32[]{:S(2)}, u32[]{:S(2)}) collective-permute-start(bf16[2,4,3,24,384]{4,3,2,1,0:T(8,128)(2,1)S(1)} %get-tuple-element.84), channel_id=1, source_target_pairs={{0,96},{32,64},{64,32},{96,0},{1,97},{33,65},{65,33},{97,1},{2,98}... | collective-permute-start | bytes 1327112 | tf_op jit(solution)/shard_map/ppermute | solution.py:40
  65.1 8.7 %collective-permute-start.11 = (bf16[4,4,24,384]{3,2,1,0:T(8,128)(2,1)S(1)}, bf16[4,4,24,384]{3,2,1,0:T(8,128)(2,1)S(1)}, u32[]{:S(2)}, u32[]{:S(2)}) collective-permute-start(bf16[4,4,24,384]{3,2,1,0:T(8,128)(2,1)S(1)} %get-tuple-element.93), channel_id=1, source_target_pairs={{0,96},{32,64},{64,32},{96,0},{1,97},{33,65},{65,33},{97,1},{2,98}... | collective-permute-start | bytes 884744 | tf_op jit(solution)/shard_map/ppermute | solution.py:40
  67.8 7.5 %collective-permute-start.13 = (bf16[4,4,24,384]{3,2,1,0:T(8,128)(2,1)S(1)}, bf16[4,4,24,384]{3,2,1,0:T(8,128)(2,1)S(1)}, u32[]{:S(2)}, u32[]{:S(2)}) collective-permute-start(bf16[4,4,24,384]{3,2,1,0:T(8,128)(2,1)S(1)} %get-tuple-element.97), channel_id=1, source_target_pairs={{0,12},{4,8},{8,4},{12,0},{1,13},{5,9},{9,5},{13,1},{2,14},{6,10},... | collective-permute-start | bytes 884744 | tf_op jit(solution)/shard_map/ppermute | solution.py:40
  68.7 6.6 %collective-permute-start.14 = (bf16[4,4,24,384]{3,2,1,0:T(8,128)(2,1)S(1)}, bf16[4,4,24,384]{3,2,1,0:T(8,128)(2,1)S(1)}, u32[]{:S(2)}, u32[]{:S(2)}) collective-permute-start(bf16[4,4,24,384]{3,2,1,0:T(8,128)(2,1)S(1)} %get-tuple-element.99), channel_id=1, source_target_pairs={{0,4},{4,0},{8,12},{12,8},{1,5},{5,1},{9,13},{13,9},{2,6},{6,2},{1... | collective-permute-start | bytes 884744 | tf_op jit(solution)/shard_map/ppermute | solution.py:40
  68.7 5.1 %collective-permute-start.12 = (bf16[4,3,24,384]{3,2,1,0:T(8,128)(2,1)S(1)}, bf16[4,3,24,384]{3,2,1,0:T(8,128)(2,1)S(1)}, u32[]{:S(2)}, u32[]{:S(2)}) collective-permute-start(bf16[4,3,24,384]{3,2,1,0:T(8,128)(2,1)S(1)} %get-tuple-element.95), channel_id=1, source_target_pairs={{0,32},{32,0},{64,96},{96,64},{1,33},{33,1},{65,97},{97,65},{2,34}... | collective-permute-start | bytes 663560 | tf_op jit(solution)/shard_map/ppermute | solution.py:40
  76.2 5.6 %collective-permute-start.15 = (bf16[2,4,24,384]{3,2,1,0:T(8,128)(2,1)S(1)}, bf16[2,4,24,384]{3,2,1,0:T(8,128)(2,1)S(1)}, u32[]{:S(2)}, u32[]{:S(2)}) collective-permute-start(bf16[2,4,24,384]{3,2,1,0:T(8,128)(2,1)S(1)} %get-tuple-element.101), channel_id=1, source_target_pairs={{0,4},{4,0},{8,12},{12,8},{1,5},{5,1},{9,13},{13,9},{2,6},{6,2},{1... | collective-permute-start | bytes 442376 | tf_op jit(solution)/shard_map/ppermute | solution.py:40
  76.3 5.5 %collective-permute-start.17 = (bf16[2,4,24,384]{3,2,1,0:T(8,128)(2,1)S(1)}, bf16[2,4,24,384]{3,2,1,0:T(8,128)(2,1)S(1)}, u32[]{:S(2)}, u32[]{:S(2)}) collective-permute-start(bf16[2,4,24,384]{3,2,1,0:T(8,128)(2,1)S(1)} %get-tuple-element.105), channel_id=1, source_target_pairs={{0,32},{32,0},{64,96},{96,64},{1,33},{33,1},{65,97},{97,65},{2,34}... | collective-permute-start | bytes 442376 | tf_op jit(solution)/shard_map/ppermute | solution.py:40
  76.4 5.4 %collective-permute-start.18 = (bf16[2,4,24,384]{3,2,1,0:T(8,128)(2,1)S(1)}, bf16[2,4,24,384]{3,2,1,0:T(8,128)(2,1)S(1)}, u32[]{:S(2)}, u32[]{:S(2)}) collective-permute-start(bf16[2,4,24,384]{3,2,1,0:T(8,128)(2,1)S(1)} %get-tuple-element.107), channel_id=1, source_target_pairs={{0,96},{32,64},{64,32},{96,0},{1,97},{33,65},{65,33},{97,1},{2,98}... | collective-permute-start | bytes 442376 | tf_op jit(solution)/shard_map/ppermute | solution.py:40
  77.0 4.8 %collective-permute-start.16 = (bf16[2,3,24,384]{3,2,1,0:T(8,128)(2,1)S(1)}, bf16[2,3,24,384]{3,2,1,0:T(8,128)(2,1)S(1)}, u32[]{:S(2)}, u32[]{:S(2)}) collective-permute-start(bf16[2,3,24,384]{3,2,1,0:T(8,128)(2,1)S(1)} %get-tuple-element.103), channel_id=1, source_target_pairs={{0,12},{4,8},{8,4},{12,0},{1,13},{5,9},{9,5},{13,1},{2,14},{6,10},... | collective-permute-start | bytes 331784 | tf_op jit(solution)/shard_map/ppermute | solution.py:40
  82.0 7.1 %collective-permute-start.19 = (bf16[4,24,384]{2,1,0:T(8,128)(2,1)S(1)}, bf16[4,24,384]{2,1,0:T(8,128)(2,1)S(1)}, u32[]{:S(2)}, u32[]{:S(2)}) collective-permute-start(bf16[4,24,384]{2,1,0:T(8,128)(2,1)S(1)} %get-tuple-element.109), channel_id=1, source_target_pairs={{0,12},{4,8},{8,4},{12,0},{1,13},{5,9},{9,5},{13,1},{2,14},{6,10},... | collective-permute-start | bytes 221192 | tf_op jit(solution)/shard_map/ppermute | solution.py:40
  83.7 5.3 %collective-permute-start.21 = (bf16[4,24,384]{2,1,0:T(8,128)(2,1)S(1)}, bf16[4,24,384]{2,1,0:T(8,128)(2,1)S(1)}, u32[]{:S(2)}, u32[]{:S(2)}) collective-permute-start(bf16[4,24,384]{2,1,0:T(8,128)(2,1)S(1)} %get-tuple-element.113), channel_id=1, source_target_pairs={{0,96},{32,64},{64,32},{96,0},{1,97},{33,65},{65,33},{97,1},{2,98}... | collective-permute-start | bytes 221192 | tf_op jit(solution)/shard_map/ppermute | solution.py:40
  85.8 3.3 %collective-permute-start.22 = (bf16[4,24,384]{2,1,0:T(8,128)(2,1)S(1)}, bf16[4,24,384]{2,1,0:T(8,128)(2,1)S(1)}, u32[]{:S(2)}, u32[]{:S(2)}) collective-permute-start(bf16[4,24,384]{2,1,0:T(8,128)(2,1)S(1)} %get-tuple-element.115), channel_id=1, source_target_pairs={{0,32},{32,0},{64,96},{96,64},{1,33},{33,1},{65,97},{97,65},{2,34}... | collective-permute-start | bytes 221192 | tf_op jit(solution)/shard_map/ppermute | solution.py:40
  86.0 3.0 %collective-permute-start.20 = (bf16[3,24,384]{2,1,0:T(8,128)(2,1)S(1)}, bf16[3,24,384]{2,1,0:T(8,128)(2,1)S(1)}, u32[]{:S(2)}, u32[]{:S(2)}) collective-permute-start(bf16[3,24,384]{2,1,0:T(8,128)(2,1)S(1)} %get-tuple-element.111), channel_id=1, source_target_pairs={{0,4},{4,0},{8,12},{12,8},{1,5},{5,1},{9,13},{13,9},{2,6},{6,2},{1... | collective-permute-start | bytes 165896 | tf_op jit(solution)/shard_map/ppermute | solution.py:40
  89.7 5.6 %collective-permute-start.23 = (bf16[8,24,384]{2,1,0:T(8,128)(2,1)S(1)}, bf16[8,24,384]{2,1,0:T(8,128)(2,1)S(1)}, u32[]{:S(2)}, u32[]{:S(2)}) collective-permute-start(bf16[8,24,384]{2,1,0:T(8,128)(2,1)S(1)} %get-tuple-element.117), channel_id=1, source_target_pairs={{0,16},{16,0},{1,17},{17,1},{2,18},{18,2},{3,19},{19,3},{4,20},{20... | collective-permute-start | bytes 442376 | tf_op jit(solution)/shard_map/ppermute | solution.py:35

commit v10 on v9

--- a/solution.py
+++ b/solution.py
@@ -1,3 +1,5 @@
+import functools
+
 import jax
 import jax.numpy as jnp
 import numpy as np
@@ -280,23 +282,16 @@
                     out_ref[position, x] = raw_ref[4 * y + x, part].astype(out_ref.dtype)
 
 
-def halve_kernel(*refs):
-    for part in range(4):
-        kept_ref, arrived_ref = refs[2 * part : 2 * part + 2]
-        kept_out, sent_out = refs[8 + 2 * part : 10 + 2 * part]
-        kept_out[...] = kept_ref[0] + wide(arrived_ref[0])
-        sent_out[...] = narrow(kept_ref[1] + wide(arrived_ref[1]))
-
-
-def turn_kernel(place_ref, *refs):
-    scratch = refs[16:]
-    for part in range(4):
-        kept_ref, arrived_ref = refs[2 * part : 2 * part + 2]
-        scratch[part][...] = kept_ref[...] + wide(arrived_ref[...])
-        for side, blocks in enumerate(kept_and_sent(place_ref[2 if part < 2 else 1], part % 2)):
-            out_ref = refs[8 + 2 * part + side]
-            for position, block in enumerate(blocks):
-                out_ref[position] = scratch[part][block].astype(out_ref.dtype)
+def halve_kernel(kept_ref, arrived_ref, kept_out, sent_out):
+    kept_out[...] = kept_ref[0] + wide(arrived_ref[0])
+    sent_out[...] = narrow(kept_ref[1] + wide(arrived_ref[1]))
+
+
+def turn_kernel(axis, order, place_ref, kept_ref, arrived_ref, kept_out, sent_out, sum_ref):
+    sum_ref[...] = kept_ref[...] + wide(arrived_ref[...])
+    for out_ref, blocks in zip((kept_out, sent_out), kept_and_sent(place_ref[axis], order)):
+        for position, block in enumerate(blocks):
+            out_ref[position] = sum_ref[block].astype(out_ref.dtype)
 
 
 def z_cut_kernel(place_ref, *refs):
@@ -435,13 +430,28 @@
         return [out for size in sizes for out in (granules(*size, kind=F32), granules(*size))]
 
     def exchange(parts, axes, orders):
+        sent = [part[1] for part in parts]
+        arrived = [to_pair(*sending) for sending in zip(sent, axes, orders)]
         return [
-            part if side == 0 else to_pair(part, axes[i], orders[i])
-            for i in range(len(parts) // 2)
-            for side, part in enumerate(parts[2 * i : 2 * i + 2])
+            (part[0], lax.optimization_barrier((coming, *sent))[0])
+            for part, coming in zip(parts, arrived)
         ]
 
+    def halve(part, *lead):
+        return call(halve_kernel, "halve", [VMEM] * 2, pairs((*lead, part[0].shape[-3])))(*part)
+
+    def turn(part, axis, order):
+        size = part[0].shape[-3]
+        return call(
+            functools.partial(turn_kernel, 1 if axis == Y else 2, order),
+            "turn",
+            [SMEM] + [VMEM] * 2,
+            pairs((2, size)),
+            [pltpu.VMEM((4, size, ROWS, COLS), F32)],
+        )(place, *part)
+
     raw = pltpu.VMEM((hidden // 2, units), F32)
+    last_own, slopes_own = lax.optimization_barrier((last_own, slopes_own))
     last_parts = call(
         last_kernel,
         "last",
@@ -459,29 +469,15 @@
     middle_parts = call(
         middle_kernel, "middle", [SMEM] + [VMEM] * 4, pairs((2, 4, 4)), [raw]
     )(place, slopes_own, slopes_arrived, act_first, sibling_act)
-    parts = exchange([*first_parts, *last_parts, *middle_parts], (Y, Y, X, X), (0, 1, 0, 1))
-    sizes = (4, 3, 4, 4)
-    parts = exchange(
-        call(halve_kernel, "halve", [VMEM] * 8, pairs(*((4, size) for size in sizes)))(*parts),
-        (Y, Y, X, X),
-        (1, 0, 1, 0),
-    )
-    parts = exchange(
-        call(
-            turn_kernel,
-            "turn",
-            [SMEM] + [VMEM] * 8,
-            pairs(*((2, size) for size in sizes)),
-            [pltpu.VMEM((4, size, ROWS, COLS), F32) for size in sizes],
-        )(place, *parts),
-        (X, X, Y, Y),
-        (0, 1, 0, 1),
-    )
-    parts = exchange(
-        call(halve_kernel, "halve", [VMEM] * 8, pairs(*((size,) for size in sizes)))(*parts),
-        (X, X, Y, Y),
-        (1, 0, 1, 0),
-    )
+    axes, turned, orders, swapped = (X, X, Y, Y), (Y, Y, X, X), (0, 1, 0, 1), (1, 0, 1, 0)
+    parts = (last_parts, middle_parts, first_parts[0:2], first_parts[2:4])
+    parts = [halve(part, 4) for part in exchange(parts, axes, orders)]
+    parts = [
+        turn(part, turned[i], orders[i]) for i, part in enumerate(exchange(parts, axes, swapped))
+    ]
+    parts = [halve(part) for part in exchange(parts, turned, orders)]
+    last_parts, middle_parts, *first_parts = exchange(parts, turned, swapped)
+    parts = (*first_parts[0], *first_parts[1], *last_parts, *middle_parts)
     sent, own = call(
         z_cut_kernel,
         "z_cut",

time: 119 us -> 118 us (level)
  waiting for transfers between devices: 41.3 us -> 38.8 us
  Pallas kernels: 27 us -> 28.8 us
    ppermute x16, waiting for transfers between devices: 23.4 us -> 20.9 us  [to_pair(): return lax.ppermute(shard, axis, pairs)]
    pallas_call x14 -> x23, Pallas kernels: 27 us -> 28.8 us  [run(): kernel(*(operand if spec is SMEM else pltpu.with_memory_space_constraint(...]
  transfers between devices with their start and end apart: 24 -> 24, of which waited for: 9 -> 11; matrix products, arithmetic and copies ran while one was open for 0% -> 0% of each run, Pallas kernels for 18% -> 21%
where the time goes in v10:
time: 118 us; the launch traced here: 117 us
  waiting for transfers between devices  38.8 us (33%)
  Pallas kernels  28.8 us (24%)
  starting transfers between devices  25.2 us (21%)
  blocking collectives  22.6 us (19%)
  local copies, waits for them, and re-layouts  1.24 us (1%)
    pallas_call x23, Pallas kernels, run(): kernel(*(operand if spec is SMEM else pltpu.with_memory_space_constraint(...  28.8 us
    all_to_all x1, blocking collectives, per_device(): squares = lax.all_to_all(squares, ALL, 0, 0, tiled=True)  22.6 us
    ppermute x16, waiting for transfers between devices, to_pair(): return lax.ppermute(shard, axis, pairs)  20.9 us
    ppermute x16, starting transfers between devices, to_pair(): return lax.ppermute(shard, axis, pairs)  15.9 us
    ppermute x1, waiting for transfers between devices, per_device(): fetched = lax.ppermute(half, (ZH, 'mp'), [(0, 3), (3, 0), (1, 2), (2, 1)])  12.4 us
    ppermute x7, waiting for transfers between devices, swap(): return lax.ppermute(shard, axis, [(0, 1), (1, 0)])  5.54 us
    ppermute x1, starting transfers between devices, per_device(): fetched = lax.ppermute(half, (ZH, 'mp'), [(0, 3), (3, 0), (1, 2), (2, 1)])  4.67 us
    ppermute x7, starting transfers between devices, swap(): return lax.ppermute(shard, axis, [(0, 1), (1, 0)])  4.61 us
  transfers between devices with their start and end apart: 24, of which 11 were waited for; matrix products, arithmetic and copies ran while one was open for 0% of the time, Pallas kernels for 21%

profile of v10, /device:TPU:1, one launch (start us, length us, event | category | flops | bytes accessed | tf_op | source)
XLA Modules:
  0.0 117.5 jit_solution(3552685911750015407)
XLA Ops:
  0.6 0.1 stack.23.place_ref
  0.7 2.2 %half.1 = bf16[344,1536]{1,0:T(8,128)(2,1)S(1)} custom-call(s32[5]{0:T(128)S(1)} %stack.23.place_ref, bf16[663,1536]{1,0:T(8,128)(2,1)} %bitcast.13), custom_call_target="tpu_custom_call" | custom-call | flops 17179869184 | bytes 67108864 | tf_op jit(solution)/shard_map/half/pallas_call | solution.py:73
  2.9 4.7 %collective-permute-start.1 = (bf16[344,1536]{1,0:T(8,128)(2,1)S(1)}, bf16[344,1536]{1,0:T(8,128)(2,1)S(1)}, u32[]{:S(2)}, u32[]{:S(2)}) collective-permute-start(bf16[344,1536]{1,0:T(8,128)(2,1)S(1)} %half.1), channel_id=1, source_target_pairs={{0,17},{17,0},{1,16},{16,1},{2,19},{19,2},{3,18},{18,3},{4,21},{21... | collective-permute-start | bytes 3170312 | tf_op jit(solution)/shard_map/ppermute | solution.py:358
  7.6 5.9 %forward.1 = (f32[256,768]{1,0:T(8,128)}, bf16[256,768]{1,0:T(8,128)(2,1)}, bf16[256,1536]{1,0:T(8,128)(2,1)}) custom-call(bf16[2652,256]{1,0:T(8,128)(2,1)} %bitcast.10, bf16[2652,768]{1,0:T(8,128)(2,1)} %w_first_hbm.1, bf16[768,1536]{1,0:T(8,128)(2,1)} %w_middle_ref.1), custom_call_target="tpu_custom_call" | custom-call | flops 17179869184 | bytes 67108864 | tf_op jit(solution)/shard_map/forward/pallas_call | solution.py:73
  13.5 0.1 collective-permute-start
  13.6 1.0 collective-permute-start.7
  14.7 0.1 collective-permute-start.4
  14.8 1.1 copy-done.6
  15.9 2.4 %stage.1 = (bf16[663,1536]{1,0:T(8,128)(2,1)S(1)}, bf16[663,256]{1,0:T(8,128)(2,1)S(1)}, bf16[663,256]{1,0:T(8,128)(2,1)S(1)}, f32[256,768]{1,0:T(8,128)S(1)}, b...) custom-call(s32[5]{0:T(128)S(1)} %stack.23.place_ref, s32[2]{0:T(128)S(1)} %copy-done.4, f32[256,768]{1,0:T(8,128)S(1)} %copy-done.6, ...), custom_call_target="tpu_custom_call" | custom-call | flops 17179869184 | bytes 67108864 | tf_op jit(solution)/shard_map/stage/pallas_call | solution.py:73
  18.3 12.4 %collective-permute-done.1.fetched_ref = bf16[344,1536]{1,0:T(8,128)(2,1)S(1)} collective-permute-done((bf16[344,1536]{1,0:T(8,128)(2,1)S(1)}, bf16[344,1536]{1,0:T(8,128)(2,1)S(1)}, u32[]{:S(2)}, u32[]{:S(2)}) %collective-permute-start.1) | collective-permute-done | bytes 1056800 | tf_op jit(solution)/shard_map/ppermute | solution.py:358
  30.6 1.2 %collective-permute-start.2 = (bf16[344,1536]{1,0:T(8,128)(2,1)S(1)}, bf16[344,1536]{1,0:T(8,128)(2,1)S(1)}, u32[]{:S(2)}, u32[]{:S(2)}) collective-permute-start(bf16[344,1536]{1,0:T(8,128)(2,1)S(1)} %collective-permute-done.1.fetched_ref), channel_id=1, source_target_pairs={{0,2},{2,0},{1,3},{3,1},{4,6},{6,4},{5,7},{7,5},{8,10},{10,8},{9,1... | collective-permute-start | bytes 3170312 | tf_op jit(solution)/shard_map/ppermute | solution.py:37
  31.9 0.0 collective-permute-done.arrived_ref
  31.9 3.1 %hidden.1 = (bf16[256,1536]{1,0:T(8,128)(2,1)S(1)}, f32[256,1536]{1,0:T(8,128)S(1)}, f32[256,1536]{1,0:T(8,128)S(1)}, bf16[1431,256]{1,0:T(8,128)(2,1)S(1)}, bf16[768,256]{1,0:T(8,128)(2,1)S(1)}) custom-call(s32[5]{0:T(128)S(1)} %stack.23.place_ref, bf16[256,1536]{1,0:T(8,128)(2,1)S(1)} %copy-done.2, bf16[256,1536]{1,0:T(8,128)(2,1)S(1)} %collective-permute-done.arrived_ref, ...), custom_call_target="tpu_custom_call" | custom-call | flops 17179869184 | bytes 67108864 | tf_op jit(solution)/shard_map/hidden/pallas_call | solution.py:73
  35.0 2.0 %collective-permute-start.6 = (bf16[1431,256]{1,0:T(8,128)(2,1)S(1)}, bf16[1431,256]{1,0:T(8,128)(2,1)S(1)}, u32[]{:S(2)}, u32[]{:S(2)}) collective-permute-start(bf16[1431,256]{1,0:T(8,128)(2,1)S(1)} %get-tuple-element.104.sent_ref), channel_id=1, source_target_pairs={{0,2},{2,0},{1,3},{3,1},{4,6},{6,4},{5,7},{7,5},{8,10},{10,8},{9,1... | collective-permute-start | bytes 2198024 | tf_op jit(solution)/shard_map/ppermute | solution.py:37
  37.0 5.0 %slopes.1 = (bf16[1152,256]{1,0:T(8,128)(2,1)S(1)}, bf16[1152,256]{1,0:T(8,128)(2,1)S(1)}) custom-call(s32[5]{0:T(128)S(1)} %stack.23.place_ref, bf16[256,1536]{1,0:T(8,128)(2,1)S(1)} %get-tuple-element.89.act_ref, f32[256,1536]{1,0:T(8,128)S(1)} %get-tuple-element.90.act_slope_ref, f32[256,1536]{1,0:T(8,128)S(1)} %get-tuple-element.91.back_ref, ...), custom_call_target="tpu_custom_call" | custom-call | flops 17179869184 | bytes 67108864 | tf_op jit(solution)/shard_map/slopes/pallas_call | solution.py:73
  42.0 0.1 collective-permute-start.3
  42.1 0.0 collective-permute-done.6.arrived_ref
  42.1 1.5 %last.1 = (f32[2,4,4,24,384]{4,3,2,1,0:T(8,128)S(1)}, bf16[2,4,4,24,384]{4,3,2,1,0:T(8,128)(2,1)S(1)}) custom-call(s32[5]{0:T(128)S(1)} %stack.23.place_ref, bf16[768,256]{1,0:T(8,128)(2,1)S(1)} %get-tuple-element.103.own_ref, bf16[1431,256]{1,0:T(8,128)(2,1)S(1)} %get-tuple-element.104.sent_ref, bf16[1431,256]{1,0:T(8,128)(2,1)S(1)} %collective-permute-done.6.arrived_ref), custom_call_target="tpu_custom_call" | custom-call | flops 17179869184 | bytes 67108864 | tf_op jit(solution)/shard_map/last/pallas_call | solution.py:73
  43.6 1.5 %collective-permute-start.9 = (bf16[2,4,4,24,384]{4,3,2,1,0:T(8,128)(2,1)S(1)}, bf16[2,4,4,24,384]{4,3,2,1,0:T(8,128)(2,1)S(1)}, u32[]{:S(2)}, u32[]{:S(2)}) collective-permute-start(bf16[2,4,4,24,384]{4,3,2,1,0:T(8,128)(2,1)S(1)} %get-tuple-element.105), channel_id=1, source_target_pairs={{0,4},{4,0},{8,12},{12,8},{1,5},{5,1},{9,13},{13,9},{2,6},{6,2},{1... | collective-permute-start | bytes 1769480 | tf_op jit(solution)/shard_map/ppermute | solution.py:42
  45.0 0.0 collective-permute-done.4.sibling_belief_ref
  45.1 0.0 collective-permute-done.3.arrived_ref
  45.1 2.4 %first.1 = (f32[2,4,4,24,384]{4,3,2,1,0:T(8,128)S(1)}, bf16[2,4,4,24,384]{4,3,2,1,0:T(8,128)(2,1)S(1)}, f32[2,4,3,24,384]{4,3,2,1,0:T(8,128)S(1)}, bf16[2,4,3,24,384]{4,3,2,1,0:T(8,128)(2,1)S(1)}) custom-call(s32[5]{0:T(128)S(1)} %stack.23.place_ref, bf16[1152,256]{1,0:T(8,128)(2,1)S(1)} %get-tuple-element.97.own_ref, ...), custom_call_target="tpu_custom_call" | custom-call | flops 17179869184 | bytes 67108864 | tf_op jit(solution)/shard_map/first/pallas_call | solution.py:73
  47.5 2.8 %collective-permute-start.11 = (bf16[2,4,3,24,384]{4,3,2,1,0:T(8,128)(2,1)S(1)}, bf16[2,4,3,24,384]{4,3,2,1,0:T(8,128)(2,1)S(1)}, u32[]{:S(2)}, u32[]{:S(2)}) collective-permute-start(bf16[2,4,3,24,384]{4,3,2,1,0:T(8,128)(2,1)S(1)} %get-tuple-element.108), channel_id=1, source_target_pairs={{0,96},{32,64},{64,32},{96,0},{1,97},{33,65},{65,33},{97,1},{2,98}... | collective-permute-start | bytes 1327112 | tf_op jit(solution)/shard_map/ppermute | solution.py:42
  50.3 1.5 %middle.1 = (f32[2,4,4,24,384]{4,3,2,1,0:T(8,128)S(1)}, bf16[2,4,4,24,384]{4,3,2,1,0:T(8,128)(2,1)S(1)}) custom-call(s32[5]{0:T(128)S(1)} %stack.23.place_ref, bf16[1152,256]{1,0:T(8,128)(2,1)S(1)} %get-tuple-element.97.own_ref, bf16[1152,256]{1,0:T(8,128)(2,1)S(1)} %collective-permute-done.3.arrived_ref, bf16[256,768]{1,0:T(8,128)(2,1)S(1)} %copy-done.3, ...), custom_call_target="tpu_custom_call" | custom-call | flops 17179869184 | bytes 67108864 | tf_op jit(solution)/shard_map/middle/pallas_call | solution.py:73
  51.7 1.9 %collective-permute-start.10 = (bf16[2,4,4,24,384]{4,3,2,1,0:T(8,128)(2,1)S(1)}, bf16[2,4,4,24,384]{4,3,2,1,0:T(8,128)(2,1)S(1)}, u32[]{:S(2)}, u32[]{:S(2)}) collective-permute-start(bf16[2,4,4,24,384]{4,3,2,1,0:T(8,128)(2,1)S(1)} %get-tuple-element.107), channel_id=1, source_target_pairs={{0,12},{4,8},{8,4},{12,0},{1,13},{5,9},{9,5},{13,1},{2,14},{6,10},... | collective-permute-start | bytes 1769480 | tf_op jit(solution)/shard_map/ppermute | solution.py:42
  53.6 4.6 %collective-permute-done.9.arrived_ref = bf16[2,4,4,24,384]{4,3,2,1,0:T(8,128)(2,1)S(1)} collective-permute-done((bf16[2,4,4,24,384]{4,3,2,1,0:T(8,128)(2,1)S(1)}, bf16[2,4,4,24,384]{4,3,2,1,0:T(8,128)(2,1)S(1)}, u32[]{:S(2)}, u32[]{:S(2)}) %collective-permute-start.9) | collective-permute-done | bytes 589856 | tf_op jit(solution)/shard_map/ppermute | solution.py:42
  58.3 0.1 halve.9
  58.4 2.6 %collective-permute-start.13 = (bf16[4,4,24,384]{3,2,1,0:T(8,128)(2,1)S(1)}, bf16[4,4,24,384]{3,2,1,0:T(8,128)(2,1)S(1)}, u32[]{:S(2)}, u32[]{:S(2)}) collective-permute-start(bf16[4,4,24,384]{3,2,1,0:T(8,128)(2,1)S(1)} %get-tuple-element.114), channel_id=1, source_target_pairs={{0,12},{4,8},{8,4},{12,0},{1,13},{5,9},{9,5},{13,1},{2,14},{6,10},... | collective-permute-start | bytes 884744 | tf_op jit(solution)/shard_map/ppermute | solution.py:42
  61.0 0.1 halve.11
  61.1 1.4 %collective-permute-start.15 = (bf16[4,3,24,384]{3,2,1,0:T(8,128)(2,1)S(1)}, bf16[4,3,24,384]{3,2,1,0:T(8,128)(2,1)S(1)}, u32[]{:S(2)}, u32[]{:S(2)}) collective-permute-start(bf16[4,3,24,384]{3,2,1,0:T(8,128)(2,1)S(1)} %get-tuple-element.120), channel_id=1, source_target_pairs={{0,32},{32,0},{64,96},{96,64},{1,33},{33,1},{65,97},{97,65},{2,34}... | collective-permute-start | bytes 663560 | tf_op jit(solution)/shard_map/ppermute | solution.py:42
  62.5 4.4 %collective-permute-done.10.arrived_ref = bf16[2,4,4,24,384]{4,3,2,1,0:T(8,128)(2,1)S(1)} collective-permute-done((bf16[2,4,4,24,384]{4,3,2,1,0:T(8,128)(2,1)S(1)}, bf16[2,4,4,24,384]{4,3,2,1,0:T(8,128)(2,1)S(1)}, u32[]{:S(2)}, u32[]{:S(2)}) %collective-permute-start.10) | collective-permute-done | bytes 589856 | tf_op jit(solution)/shard_map/ppermute | solution.py:42
  66.8 0.3 collective-permute-done.5.arrived_ref
  67.1 0.1 halve.10
  67.2 0.4 collective-permute-start.14
  67.6 0.1 halve.8
  67.8 0.2 collective-permute-start.8
  68.0 5.2 %collective-permute-done.13.arrived_ref = bf16[4,4,24,384]{3,2,1,0:T(8,128)(2,1)S(1)} collective-permute-done((bf16[4,4,24,384]{3,2,1,0:T(8,128)(2,1)S(1)}, bf16[4,4,24,384]{3,2,1,0:T(8,128)(2,1)S(1)}, u32[]{:S(2)}, u32[]{:S(2)}) %collective-permute-start.13) | collective-permute-done | bytes 294944 | tf_op jit(solution)/shard_map/ppermute | solution.py:42
  73.1 0.6 turn.5
  73.8 0.1 collective-permute-start.17
  73.9 0.0 collective-permute-done.15.arrived_ref
  73.9 0.6 turn.7
  74.5 1.9 %collective-permute-start.19 = (bf16[2,3,24,384]{3,2,1,0:T(8,128)(2,1)S(1)}, bf16[2,3,24,384]{3,2,1,0:T(8,128)(2,1)S(1)}, u32[]{:S(2)}, u32[]{:S(2)}) collective-permute-start(bf16[2,3,24,384]{3,2,1,0:T(8,128)(2,1)S(1)} %get-tuple-element.132), channel_id=1, source_target_pairs={{0,12},{4,8},{8,4},{12,0},{1,13},{5,9},{9,5},{13,1},{2,14},{6,10},... | collective-permute-start | bytes 331784 | tf_op jit(solution)/shard_map/ppermute | solution.py:42
  76.4 0.0 collective-permute-done.14.arrived_ref
  76.4 0.0 collective-permute-done.8.arrived_ref
  76.4 0.6 turn.6
  77.1 0.7 collective-permute-start.18
  77.7 0.6 turn.4
  78.4 0.1 collective-permute-start.12
  78.5 1.2 collective-permute-done.19.arrived_ref
  79.7 1.0 collective-permute-start.21
  80.7 1.6 %collective-permute-done.18.arrived_ref = bf16[2,4,24,384]{3,2,1,0:T(8,128)(2,1)S(1)} collective-permute-done((bf16[2,4,24,384]{3,2,1,0:T(8,128)(2,1)S(1)}, bf16[2,4,24,384]{3,2,1,0:T(8,128)(2,1)S(1)}, u32[]{:S(2)}, u32[]{:S(2)}) %collective-permute-start.18) | collective-permute-done | bytes 147488 | tf_op jit(solution)/shard_map/ppermute | solution.py:42
  82.4 0.6 collective-permute-start.22
  83.0 0.0 collective-permute-done.12.arrived_ref
  83.0 0.7 collective-permute-start.16
  83.8 0.1 collective-permute-start.20
  83.9 0.2 collective-permute-done.21.refs_5_
  84.1 2.8 %collective-permute-done.20.refs_3_ = bf16[3,24,384]{2,1,0:T(8,128)(2,1)S(1)} collective-permute-done((bf16[3,24,384]{2,1,0:T(8,128)(2,1)S(1)}, bf16[3,24,384]{2,1,0:T(8,128)(2,1)S(1)}, u32[]{:S(2)}, u32[]{:S(2)}) %collective-permute-start.20) | collective-permute-done | bytes 55328 | tf_op jit(solution)/shard_map/ppermute | solution.py:42
  86.9 0.6 collective-permute-done.16.refs_1_
  87.5 0.6 z_cut.1
  88.2 0.1 collective-permute-start.23
  88.3 5.5 %collective-permute-done.23.arrived_ref = bf16[8,24,384]{2,1,0:T(8,128)(2,1)S(1)} collective-permute-done((bf16[8,24,384]{2,1,0:T(8,128)(2,1)S(1)}, bf16[8,24,384]{2,1,0:T(8,128)(2,1)S(1)}, u32[]{:S(2)}, u32[]{:S(2)}) %collective-permute-start.23) | collective-permute-done | bytes 147488 | tf_op jit(solution)/shard_map/ppermute | solution.py:37
  93.8 0.3 square.1
  94.0 22.6 %all_to_all.5.squares_ref = f32[128,1,128]{2,1,0:T(1,128)S(1)} all-to-all(f32[128,1,128]{2,1,0:T(1,128)S(1)} %get-tuple-element.155), channel_id=1, replica_groups=mesh['dp_0'=4,'dp_1'=2,'dp_2'=4,'dp_3'=2,'mp'=2] {'dp_0','dp_1','dp_2','..., dimensions={0} | all-to-all | bytes 131072 | tf_op jit(solution)/shard_map/all_to_all | solution.py:492
  116.6 0.9 scale.1
  (23 shorter events, 0.2 us)
Async XLA Ops:
  2.9 27.7 %collective-permute-start.1 = (bf16[344,1536]{1,0:T(8,128)(2,1)S(1)}, bf16[344,1536]{1,0:T(8,128)(2,1)S(1)}, u32[]{:S(2)}, u32[]{:S(2)}) collective-permute-start(bf16[344,1536]{1,0:T(8,128)(2,1)S(1)} %half.1), channel_id=1, source_target_pairs={{0,17},{17,0},{1,16},{16,1},{2,19},{19,2},{3,18},{18,3},{4,21},{21... | collective-permute-start | bytes 3170312 | tf_op jit(solution)/shard_map/ppermute | solution.py:358
  7.6 7.1 %copy-start.1 = (bf16[256,2652]{0,1:T(8,128)(2,1)S(1)}, bf16[256,2652]{0,1:T(8,128)(2,1)}, u32[]{:S(2)}) copy-start(bf16[256,2652]{0,1:T(8,128)(2,1)} %param.7) | copy-start | bytes 4073476
  7.6 7.2 %copy-start.4 = (s32[2]{0:T(128)S(1)}, s32[2]{0:T(128)}, u32[]{:S(2)}) copy-start(s32[2]{0:T(128)} %counts_ref.1) | copy-start | bytes 28
  7.6 7.2 %copy-start.5 = (s32[2,768,1]{2,1,0:T(8,128)S(1)}, s32[2,768,1]{2,1,0:T(8,128)}, u32[]{:S(2)}) copy-start(s32[2,768,1]{2,1,0:T(8,128)} %constant.21.clone.orders_ref) | copy-start | bytes 18436
  13.5 18.4 %collective-permute-start = (bf16[256,1536]{1,0:T(8,128)(2,1)}, bf16[256,1536]{1,0:T(8,128)(2,1)S(1)}, u32[]{:S(2)}, u32[]{:S(2)}) collective-permute-start(bf16[256,1536]{1,0:T(8,128)(2,1)} %get-tuple-element.82.partial_ref), channel_id=1, source_target_pairs={{0,1},{1,0},{2,3},{3,2},{4,5},{5,4},{6,7},{7,6},{8,9},{9,8},{10,11... | collective-permute-start | bytes 2359304 | tf_op jit(solution)/shard_map/ppermute | solution.py:37
  13.6 36.6 %collective-permute-start.7 = (bf16[256,768]{1,0:T(8,128)(2,1)}, bf16[256,768]{1,0:T(8,128)(2,1)S(1)}, u32[]{:S(2)}, u32[]{:S(2)}) collective-permute-start(bf16[256,768]{1,0:T(8,128)(2,1)} %get-tuple-element.106.act_ref), channel_id=1, source_target_pairs={{0,2},{2,0},{1,3},{3,1},{4,6},{6,4},{5,7},{7,5},{8,10},{10,8},{9,1... | collective-permute-start | bytes 1179656 | tf_op jit(solution)/shard_map/ppermute | solution.py:37
  14.7 30.4 %collective-permute-start.4 = (bf16[2652,256]{1,0:T(8,128)(2,1)S(1)}, bf16[2652,256]{1,0:T(8,128)(2,1)S(1)}, u32[]{:S(2)}, u32[]{:S(2)}) collective-permute-start(bf16[2652,256]{1,0:T(8,128)(2,1)S(1)} %bitcast.11), channel_id=1, source_target_pairs={{0,2},{2,0},{1,3},{3,1},{4,6},{6,4},{5,7},{7,5},{8,10},{10,8},{9,1... | collective-permute-start | bytes 4073480 | tf_op jit(solution)/shard_map/ppermute | solution.py:37
  14.8 1.1 copy-start.6
  15.9 16.0 %copy-start.2 = (bf16[256,1536]{1,0:T(8,128)(2,1)S(1)}, bf16[256,1536]{1,0:T(8,128)(2,1)}, u32[]{:S(2)}) copy-start(bf16[256,1536]{1,0:T(8,128)(2,1)} %get-tuple-element.82.partial_ref) | copy-start | bytes 2359300
  30.6 6.3 %collective-permute-start.2 = (bf16[344,1536]{1,0:T(8,128)(2,1)S(1)}, bf16[344,1536]{1,0:T(8,128)(2,1)S(1)}, u32[]{:S(2)}, u32[]{:S(2)}) collective-permute-start(bf16[344,1536]{1,0:T(8,128)(2,1)S(1)} %collective-permute-done.1.fetched_ref), channel_id=1, source_target_pairs={{0,2},{2,0},{1,3},{3,1},{4,6},{6,4},{5,7},{7,5},{8,10},{10,8},{9,1... | collective-permute-start | bytes 3170312 | tf_op jit(solution)/shard_map/ppermute | solution.py:37
  31.9 5.0 %copy-start = (bf16[768,1536]{1,0:T(8,128)(2,1)S(1)}, bf16[768,1536]{1,0:T(8,128)(2,1)}, u32[]{:S(2)}) copy-start(bf16[768,1536]{1,0:T(8,128)(2,1)} %w_middle_ref.1) | copy-start | bytes 7077892
  35.0 7.1 %collective-permute-start.6 = (bf16[1431,256]{1,0:T(8,128)(2,1)S(1)}, bf16[1431,256]{1,0:T(8,128)(2,1)S(1)}, u32[]{:S(2)}, u32[]{:S(2)}) collective-permute-start(bf16[1431,256]{1,0:T(8,128)(2,1)S(1)} %get-tuple-element.104.sent_ref), channel_id=1, source_target_pairs={{0,2},{2,0},{1,3},{3,1},{4,6},{6,4},{5,7},{7,5},{8,10},{10,8},{9,1... | collective-permute-start | bytes 2198024 | tf_op jit(solution)/shard_map/ppermute | solution.py:37
  42.0 3.1 %collective-permute-start.3 = (bf16[1152,256]{1,0:T(8,128)(2,1)S(1)}, bf16[1152,256]{1,0:T(8,128)(2,1)S(1)}, u32[]{:S(2)}, u32[]{:S(2)}) collective-permute-start(bf16[1152,256]{1,0:T(8,128)(2,1)S(1)} %get-tuple-element.98), channel_id=1, source_target_pairs={{0,2},{2,0},{1,3},{3,1},{4,6},{6,4},{5,7},{7,5},{8,10},{10,8},{9,1... | collective-permute-start | bytes 1769480 | tf_op jit(solution)/shard_map/ppermute | solution.py:37
  43.6 6.7 %copy-start.3 = (bf16[256,768]{1,0:T(8,128)(2,1)S(1)}, bf16[256,768]{1,0:T(8,128)(2,1)}, u32[]{:S(2)}) copy-start(bf16[256,768]{1,0:T(8,128)(2,1)} %get-tuple-element.106.act_ref) | copy-start | bytes 1179652
  43.6 14.7 %collective-permute-start.9 = (bf16[2,4,4,24,384]{4,3,2,1,0:T(8,128)(2,1)S(1)}, bf16[2,4,4,24,384]{4,3,2,1,0:T(8,128)(2,1)S(1)}, u32[]{:S(2)}, u32[]{:S(2)}) collective-permute-start(bf16[2,4,4,24,384]{4,3,2,1,0:T(8,128)(2,1)S(1)} %get-tuple-element.105), channel_id=1, source_target_pairs={{0,4},{4,0},{8,12},{12,8},{1,5},{5,1},{9,13},{13,9},{2,6},{6,2},{1... | collective-permute-start | bytes 1769480 | tf_op jit(solution)/shard_map/ppermute | solution.py:42
  47.5 13.5 %collective-permute-start.11 = (bf16[2,4,3,24,384]{4,3,2,1,0:T(8,128)(2,1)S(1)}, bf16[2,4,3,24,384]{4,3,2,1,0:T(8,128)(2,1)S(1)}, u32[]{:S(2)}, u32[]{:S(2)}) collective-permute-start(bf16[2,4,3,24,384]{4,3,2,1,0:T(8,128)(2,1)S(1)} %get-tuple-element.108), channel_id=1, source_target_pairs={{0,96},{32,64},{64,32},{96,0},{1,97},{33,65},{65,33},{97,1},{2,98}... | collective-permute-start | bytes 1327112 | tf_op jit(solution)/shard_map/ppermute | solution.py:42
  51.7 15.1 %collective-permute-start.10 = (bf16[2,4,4,24,384]{4,3,2,1,0:T(8,128)(2,1)S(1)}, bf16[2,4,4,24,384]{4,3,2,1,0:T(8,128)(2,1)S(1)}, u32[]{:S(2)}, u32[]{:S(2)}) collective-permute-start(bf16[2,4,4,24,384]{4,3,2,1,0:T(8,128)(2,1)S(1)} %get-tuple-element.107), channel_id=1, source_target_pairs={{0,12},{4,8},{8,4},{12,0},{1,13},{5,9},{9,5},{13,1},{2,14},{6,10},... | collective-permute-start | bytes 1769480 | tf_op jit(solution)/shard_map/ppermute | solution.py:42
  53.6 13.5 %collective-permute-start.5 = (bf16[2,4,4,24,384]{4,3,2,1,0:T(8,128)(2,1)S(1)}, bf16[2,4,4,24,384]{4,3,2,1,0:T(8,128)(2,1)S(1)}, u32[]{:S(2)}, u32[]{:S(2)}) collective-permute-start(bf16[2,4,4,24,384]{4,3,2,1,0:T(8,128)(2,1)S(1)} %get-tuple-element.102), channel_id=1, source_target_pairs={{0,32},{32,0},{64,96},{96,64},{1,33},{33,1},{65,97},{97,65},{2,34}... | collective-permute-start | bytes 1769480 | tf_op jit(solution)/shard_map/ppermute | solution.py:42
  58.4 14.7 %collective-permute-start.13 = (bf16[4,4,24,384]{3,2,1,0:T(8,128)(2,1)S(1)}, bf16[4,4,24,384]{3,2,1,0:T(8,128)(2,1)S(1)}, u32[]{:S(2)}, u32[]{:S(2)}) collective-permute-start(bf16[4,4,24,384]{3,2,1,0:T(8,128)(2,1)S(1)} %get-tuple-element.114), channel_id=1, source_target_pairs={{0,12},{4,8},{8,4},{12,0},{1,13},{5,9},{9,5},{13,1},{2,14},{6,10},... | collective-permute-start | bytes 884744 | tf_op jit(solution)/shard_map/ppermute | solution.py:42
  61.1 12.8 %collective-permute-start.15 = (bf16[4,3,24,384]{3,2,1,0:T(8,128)(2,1)S(1)}, bf16[4,3,24,384]{3,2,1,0:T(8,128)(2,1)S(1)}, u32[]{:S(2)}, u32[]{:S(2)}) collective-permute-start(bf16[4,3,24,384]{3,2,1,0:T(8,128)(2,1)S(1)} %get-tuple-element.120), channel_id=1, source_target_pairs={{0,32},{32,0},{64,96},{96,64},{1,33},{33,1},{65,97},{97,65},{2,34}... | collective-permute-start | bytes 663560 | tf_op jit(solution)/shard_map/ppermute | solution.py:42
  67.2 9.2 %collective-permute-start.14 = (bf16[4,4,24,384]{3,2,1,0:T(8,128)(2,1)S(1)}, bf16[4,4,24,384]{3,2,1,0:T(8,128)(2,1)S(1)}, u32[]{:S(2)}, u32[]{:S(2)}) collective-permute-start(bf16[4,4,24,384]{3,2,1,0:T(8,128)(2,1)S(1)} %get-tuple-element.117), channel_id=1, source_target_pairs={{0,4},{4,0},{8,12},{12,8},{1,5},{5,1},{9,13},{13,9},{2,6},{6,2},{1... | collective-permute-start | bytes 884744 | tf_op jit(solution)/shard_map/ppermute | solution.py:42
  67.8 8.6 %collective-permute-start.8 = (bf16[4,4,24,384]{3,2,1,0:T(8,128)(2,1)S(1)}, bf16[4,4,24,384]{3,2,1,0:T(8,128)(2,1)S(1)}, u32[]{:S(2)}, u32[]{:S(2)}) collective-permute-start(bf16[4,4,24,384]{3,2,1,0:T(8,128)(2,1)S(1)} %get-tuple-element.111), channel_id=1, source_target_pairs={{0,96},{32,64},{64,32},{96,0},{1,97},{33,65},{65,33},{97,1},{2,98}... | collective-permute-start | bytes 884744 | tf_op jit(solution)/shard_map/ppermute | solution.py:42
  73.8 4.7 %collective-permute-start.17 = (bf16[2,4,24,384]{3,2,1,0:T(8,128)(2,1)S(1)}, bf16[2,4,24,384]{3,2,1,0:T(8,128)(2,1)S(1)}, u32[]{:S(2)}, u32[]{:S(2)}) collective-permute-start(bf16[2,4,24,384]{3,2,1,0:T(8,128)(2,1)S(1)} %get-tuple-element.126), channel_id=1, source_target_pairs={{0,32},{32,0},{64,96},{96,64},{1,33},{33,1},{65,97},{97,65},{2,34}... | collective-permute-start | bytes 442376 | tf_op jit(solution)/shard_map/ppermute | solution.py:42
  74.5 5.2 %collective-permute-start.19 = (bf16[2,3,24,384]{3,2,1,0:T(8,128)(2,1)S(1)}, bf16[2,3,24,384]{3,2,1,0:T(8,128)(2,1)S(1)}, u32[]{:S(2)}, u32[]{:S(2)}) collective-permute-start(bf16[2,3,24,384]{3,2,1,0:T(8,128)(2,1)S(1)} %get-tuple-element.132), channel_id=1, source_target_pairs={{0,12},{4,8},{8,4},{12,0},{1,13},{5,9},{9,5},{13,1},{2,14},{6,10},... | collective-permute-start | bytes 331784 | tf_op jit(solution)/shard_map/ppermute | solution.py:42
  77.1 5.3 %collective-permute-start.18 = (bf16[2,4,24,384]{3,2,1,0:T(8,128)(2,1)S(1)}, bf16[2,4,24,384]{3,2,1,0:T(8,128)(2,1)S(1)}, u32[]{:S(2)}, u32[]{:S(2)}) collective-permute-start(bf16[2,4,24,384]{3,2,1,0:T(8,128)(2,1)S(1)} %get-tuple-element.129), channel_id=1, source_target_pairs={{0,96},{32,64},{64,32},{96,0},{1,97},{33,65},{65,33},{97,1},{2,98}... | collective-permute-start | bytes 442376 | tf_op jit(solution)/shard_map/ppermute | solution.py:42
  78.4 4.6 %collective-permute-start.12 = (bf16[2,4,24,384]{3,2,1,0:T(8,128)(2,1)S(1)}, bf16[2,4,24,384]{3,2,1,0:T(8,128)(2,1)S(1)}, u32[]{:S(2)}, u32[]{:S(2)}) collective-permute-start(bf16[2,4,24,384]{3,2,1,0:T(8,128)(2,1)S(1)} %get-tuple-element.123), channel_id=1, source_target_pairs={{0,4},{4,0},{8,12},{12,8},{1,5},{5,1},{9,13},{13,9},{2,6},{6,2},{1... | collective-permute-start | bytes 442376 | tf_op jit(solution)/shard_map/ppermute | solution.py:42
  79.7 4.4 %collective-permute-start.21 = (bf16[4,24,384]{2,1,0:T(8,128)(2,1)S(1)}, bf16[4,24,384]{2,1,0:T(8,128)(2,1)S(1)}, u32[]{:S(2)}, u32[]{:S(2)}) collective-permute-start(bf16[4,24,384]{2,1,0:T(8,128)(2,1)S(1)} %get-tuple-element.138), channel_id=1, source_target_pairs={{0,96},{32,64},{64,32},{96,0},{1,97},{33,65},{65,33},{97,1},{2,98}... | collective-permute-start | bytes 221192 | tf_op jit(solution)/shard_map/ppermute | solution.py:42
  82.4 4.5 %collective-permute-start.22 = (bf16[4,24,384]{2,1,0:T(8,128)(2,1)S(1)}, bf16[4,24,384]{2,1,0:T(8,128)(2,1)S(1)}, u32[]{:S(2)}, u32[]{:S(2)}) collective-permute-start(bf16[4,24,384]{2,1,0:T(8,128)(2,1)S(1)} %get-tuple-element.141), channel_id=1, source_target_pairs={{0,32},{32,0},{64,96},{96,64},{1,33},{33,1},{65,97},{97,65},{2,34}... | collective-permute-start | bytes 221192 | tf_op jit(solution)/shard_map/ppermute | solution.py:42
  83.0 4.5 %collective-permute-start.16 = (bf16[4,24,384]{2,1,0:T(8,128)(2,1)S(1)}, bf16[4,24,384]{2,1,0:T(8,128)(2,1)S(1)}, u32[]{:S(2)}, u32[]{:S(2)}) collective-permute-start(bf16[4,24,384]{2,1,0:T(8,128)(2,1)S(1)} %get-tuple-element.135), channel_id=1, source_target_pairs={{0,12},{4,8},{8,4},{12,0},{1,13},{5,9},{9,5},{13,1},{2,14},{6,10},... | collective-permute-start | bytes 221192 | tf_op jit(solution)/shard_map/ppermute | solution.py:42
  83.8 3.1 %collective-permute-start.20 = (bf16[3,24,384]{2,1,0:T(8,128)(2,1)S(1)}, bf16[3,24,384]{2,1,0:T(8,128)(2,1)S(1)}, u32[]{:S(2)}, u32[]{:S(2)}) collective-permute-start(bf16[3,24,384]{2,1,0:T(8,128)(2,1)S(1)} %get-tuple-element.144), channel_id=1, source_target_pairs={{0,4},{4,0},{8,12},{12,8},{1,5},{5,1},{9,13},{13,9},{2,6},{6,2},{1... | collective-permute-start | bytes 165896 | tf_op jit(solution)/shard_map/ppermute | solution.py:42
  88.2 5.6 %collective-permute-start.23 = (bf16[8,24,384]{2,1,0:T(8,128)(2,1)S(1)}, bf16[8,24,384]{2,1,0:T(8,128)(2,1)S(1)}, u32[]{:S(2)}, u32[]{:S(2)}) collective-permute-start(bf16[8,24,384]{2,1,0:T(8,128)(2,1)S(1)} %get-tuple-element.153), channel_id=1, source_target_pairs={{0,16},{16,0},{1,17},{17,1},{2,18},{18,2},{3,19},{19,3},{4,20},{20... | collective-permute-start | bytes 442376 | tf_op jit(solution)/shard_map/ppermute | solution.py:37

commit v11 on v10

--- a/solution.py
+++ b/solution.py
@@ -57,12 +57,12 @@
     )
 
 
-def call(body, name, in_specs, outs, scratch=(), kind=pltpu.VMEM):
+def call(body, name, in_specs, outs, scratch=(), kind=pltpu.VMEM, far=0):
     kernel = pl.pallas_call(
         body,
-        out_shape=[kind(*out) for out in outs],
+        out_shape=[(pltpu.HBM if i < far else kind)(*out) for i, out in enumerate(outs)],
         in_specs=in_specs,
-        out_specs=[VMEM] * len(outs),
+        out_specs=[HBM if i < far else VMEM for i in range(len(outs))],
         scratch_shapes=list(scratch),
         compiler_params=pltpu.CompilerParams(vmem_limit_bytes=24 << 20),
         cost_estimate=pl.CostEstimate(flops=1 << 34, bytes_accessed=1 << 26, transcendentals=0),
@@ -91,8 +91,8 @@
 
 
 def forward_kernel(
-    belief_hbm, w_first_hbm, w_middle_hbm, pre_first_ref, act_first_ref, sent_ref,
-    belief, w_first, w_middle, sems,
+    belief_hbm, w_first_hbm, w_middle_hbm, pre_first_hbm, act_first_hbm, sent_ref,
+    belief, w_first, w_middle, pre_first_ref, act_first_ref, sems,
 ):
     inputs = belief.shape[0]
     cuts = [(start, min(start + DEPTH, inputs)) for start in range(0, inputs, DEPTH)]
@@ -109,32 +109,42 @@
     for pair in copies:
         for copy in pair:
             copy.start()
+    results = (
+        pltpu.make_async_copy(pre_first_ref, pre_first_hbm, sems.at[2 * len(cuts) + 1]),
+        pltpu.make_async_copy(act_first_ref, act_first_hbm, sems.at[2 * len(cuts) + 2]),
+    )
     pre_first = jnp.zeros(pre_first_ref.shape, F32)
     for (start, stop), pair in zip(cuts, copies):
         for copy in pair:
             copy.wait()
         pre_first += contract(belief[start:stop, :], w_first[start:stop, :], 0, 0)
     pre_first_ref[...] = pre_first
+    results[0].start()
     act_first = narrow(pre_first / (1.0 + jnp.exp(-pre_first)))
     act_first_ref[...] = act_first
+    results[1].start()
     copies[-1][0].wait()
     sent_ref[...] = narrow(dot(act_first, w_middle[...]))
-
-
-def half_kernel(place_ref, w_last_hbm, half_ref, w_last, sem):
-    copy = pltpu.make_async_copy(w_last_hbm, w_last, sem)
-    copy.start()
-    copy.wait()
-    size, total = half_ref.shape[0], w_last.shape[0]
+    for copy in results:
+        copy.wait()
+
+
+def half_kernel(place_ref, w_last_hbm, half_ref, last_ref, sem):
+    size, total = half_ref.shape[0], w_last_hbm.shape[0]
 
     @pl.when(place_ref[0] == 0)
     def _():
-        half_ref[...] = w_last[0:size, :]
+        copy = pltpu.make_async_copy(w_last_hbm.at[pl.ds(0, size)], half_ref, sem)
+        copy.start()
+        copy.wait()
 
     @pl.when(place_ref[0] != 0)
     def _():
+        copy = pltpu.make_async_copy(w_last_hbm.at[pl.ds(SECOND, total - SECOND)], last_ref, sem)
+        copy.start()
         half_ref[size - 8 :, :] = jnp.zeros((8, half_ref.shape[1]), half_ref.dtype)
-        half_ref[0 : total - SECOND, :] = w_last[SECOND:total, :]
+        copy.wait()
+        half_ref[0 : total - SECOND, :] = last_ref[...]
 
 
 def stage_kernel(
@@ -160,7 +170,16 @@
     low, high = target_ref[0:width, :], target_ref[width : 2 * width, :]
     is_low = place_ref[4] == 0
     target_own_ref[...] = jnp.where(is_low, low, high)
-    target_other_ref[...] = jnp.where(is_low, high, low)
+    other = jnp.where(is_low, high, low)
+    size = target_other_ref.shape[1]
+    for side in range(2):
+
+        @pl.when(place_ref[0] == side)
+        def _():
+            target_other_ref[side] = other[0:size]
+            target_other_ref[1 - side, size - 8 :, :] = jnp.zeros((8, other.shape[1]), other.dtype)
+            target_other_ref[1 - side, 0 : width - SECOND, :] = other[SECOND:]
+
     copies[1].wait()
 
 
@@ -193,16 +212,14 @@
     onehot_ref, fetched_ref, relayed_ref, w_middle_ref, sent_ref, own_ref, rows_ref,
 ):
     core = place_ref[0]
-    size, total = fetched_ref.shape[0], target_ref.shape[0]
     act, live = act_ref[...], live_ref[...]
     back = back_ref[...]
-    for is_own, start, stop in ((core == 0, 0, size), (core != 0, SECOND, total)):
-        rows = slice(0, stop - start)
-        weights = jnp.where(is_own, fetched_ref[rows, :], relayed_ref[rows, :])
-        slope = slope_of(weights, act, target_ref[start:stop, :], live)
-        if start:
-            column = lax.broadcasted_iota(jnp.int32, slope.shape, 0) + start
-            slope = jnp.where(column >= size, slope, jnp.zeros_like(slope))
+    for side, w_ref in enumerate((fetched_ref, relayed_ref)):
+        weights = w_ref[...]
+        slope = slope_of(weights, act, target_ref[side], live)
+        repeated = jnp.where(core == side, 0, SIZE - SECOND)
+        column = lax.broadcasted_iota(jnp.int32, slope.shape, 0)
+        slope = jnp.where(column >= repeated, slope, jnp.zeros_like(slope))
         back += contract(slope, weights, 0, 0)
     slope_middle = narrow(back * act_slope_ref[...])
     slope_first = narrow(contract(slope_middle, w_middle_ref[...], 1, 1) * first_slope_ref[...])
@@ -287,11 +304,11 @@
     sent_out[...] = narrow(kept_ref[1] + wide(arrived_ref[1]))
 
 
-def turn_kernel(axis, order, place_ref, kept_ref, arrived_ref, kept_out, sent_out, sum_ref):
-    sum_ref[...] = kept_ref[...] + wide(arrived_ref[...])
+def turn_kernel(axis, order, place_ref, kept_ref, arrived_ref, kept_out, sent_out):
     for out_ref, blocks in zip((kept_out, sent_out), kept_and_sent(place_ref[axis], order)):
         for position, block in enumerate(blocks):
-            out_ref[position] = sum_ref[block].astype(out_ref.dtype)
+            total = kept_ref[block] + wide(arrived_ref[block])
+            out_ref[position] = total.astype(out_ref.dtype)
 
 
 def z_cut_kernel(place_ref, *refs):
@@ -353,7 +370,7 @@
         "half",
         [SMEM, HBM],
         [((SIZE, hidden), BF16)],
-        [pltpu.VMEM(w_last_t.shape, BF16), pltpu.SemaphoreType.DMA],
+        [pltpu.VMEM((width - SECOND, hidden), BF16), pltpu.SemaphoreType.DMA],
     )(place, w_last_t)
     fetched = lax.ppermute(half, (ZH, "mp"), [(0, 3), (3, 0), (1, 2), (2, 1)])
     belief_first, half = lax.optimization_barrier((belief_t, half))
@@ -371,9 +388,11 @@
             pltpu.VMEM((inputs, total_rows), BF16),
             pltpu.VMEM((inputs, units), BF16),
             pltpu.VMEM((units, hidden), BF16),
-            pltpu.SemaphoreType.DMA((2 * pl.cdiv(inputs, DEPTH) + 1,)),
+            pltpu.VMEM((total_rows, units), F32),
+            pltpu.VMEM((total_rows, units), BF16),
+            pltpu.SemaphoreType.DMA((2 * pl.cdiv(inputs, DEPTH) + 3,)),
         ],
-        kind=pltpu.HBM,
+        far=2,
     )(belief_first, w_first, w_middle)
     arrived = swap(hidden_sent, "mp")
 
@@ -386,7 +405,7 @@
         [
             ((width, hidden), BF16),
             ((width, total_rows), BF16),
-            ((width, total_rows), BF16),
+            ((2, SIZE, total_rows), BF16),
             ((total_rows, units), F32),
             ((units, units), BF16),
             ((1, total_rows), F32),
@@ -447,7 +466,6 @@
             "turn",
             [SMEM] + [VMEM] * 2,
             pairs((2, size)),
-            [pltpu.VMEM((4, size, ROWS, COLS), F32)],
         )(place, *part)
 
     raw = pltpu.VMEM((hidden // 2, units), F32)

time: 118 us -> 117 us (level)
  Pallas kernels: 28.8 us -> 27.5 us
    ppermute x7, waiting for transfers between devices: 5.54 us -> 3.97 us  [swap(): return lax.ppermute(shard, axis, [(0, 1), (1, 0)])]
    pallas_call x23, Pallas kernels: 28.8 us -> 27.5 us  [run(): kernel(*(operand if spec is SMEM else pltpu.with_memory_space_constraint(...]
  transfers between devices with their start and end apart: 24 -> 24, of which waited for: 11 -> 11; matrix products, arithmetic and copies ran while one was open for 0% -> 0% of each run, Pallas kernels for 21% -> 20%
where the time goes in v11:
time: 117 us
  waiting for transfers between devices  38.4 us (33%)
  Pallas kernels  27.5 us (24%)
  starting transfers between devices  25.4 us (22%)
  blocking collectives  23.7 us (20%)
  local copies, waits for them, and re-layouts  1.24 us (1%)
    pallas_call x23, Pallas kernels, run(): kernel(*(operand if spec is SMEM else pltpu.with_memory_space_constraint(...  27.5 us
    all_to_all x1, blocking collectives, per_device(): squares = lax.all_to_all(squares, ALL, 0, 0, tiled=True)  23.7 us
    ppermute x16, waiting for transfers between devices, to_pair(): return lax.ppermute(shard, axis, pairs)  21 us
    ppermute x16, starting transfers between devices, to_pair(): return lax.ppermute(shard, axis, pairs)  15.8 us
    ppermute x1, waiting for transfers between devices, per_device(): fetched = lax.ppermute(half, (ZH, 'mp'), [(0, 3), (3, 0), (1, 2), (2, 1)])  13.4 us
    ppermute x7, starting transfers between devices, swap(): return lax.ppermute(shard, axis, [(0, 1), (1, 0)])  4.93 us
    ppermute x1, starting transfers between devices, per_device(): fetched = lax.ppermute(half, (ZH, 'mp'), [(0, 3), (3, 0), (1, 2), (2, 1)])  4.67 us
    ppermute x7, waiting for transfers between devices, swap(): return lax.ppermute(shard, axis, [(0, 1), (1, 0)])  3.97 us
  transfers between devices with their start and end apart: 24, of which 11 were waited for; matrix products, arithmetic and copies ran while one was open for 0% of the time, Pallas kernels for 20%

profile of v11, /device:TPU:1, one launch (start us, length us, event | category | flops | bytes accessed | tf_op | source)
XLA Modules:
  0.0 117.1 jit_solution(17712326805631170977)
XLA Ops:
  0.6 0.1 stack.23.place_ref
  0.7 1.9 %half.1 = bf16[344,1536]{1,0:T(8,128)(2,1)S(1)} custom-call(s32[5]{0:T(128)S(1)} %stack.23.place_ref, bf16[663,1536]{1,0:T(8,128)(2,1)} %bitcast.13), custom_call_target="tpu_custom_call" | custom-call | flops 17179869184 | bytes 67108864 | tf_op jit(solution)/shard_map/half/pallas_call | solution.py:73
  2.6 4.7 %collective-permute-start.1 = (bf16[344,1536]{1,0:T(8,128)(2,1)S(1)}, bf16[344,1536]{1,0:T(8,128)(2,1)S(1)}, u32[]{:S(2)}, u32[]{:S(2)}) collective-permute-start(bf16[344,1536]{1,0:T(8,128)(2,1)S(1)} %half.1), channel_id=1, source_target_pairs={{0,17},{17,0},{1,16},{16,1},{2,19},{19,2},{3,18},{18,3},{4,21},{21... | collective-permute-start | bytes 3170312 | tf_op jit(solution)/shard_map/ppermute | solution.py:375
  7.3 5.1 %forward.1 = (f32[256,768]{1,0:T(8,128)}, bf16[256,768]{1,0:T(8,128)(2,1)}, bf16[256,1536]{1,0:T(8,128)(2,1)S(1)}) custom-call(bf16[2652,256]{1,0:T(8,128)(2,1)} %bitcast.10, bf16[2652,768]{1,0:T(8,128)(2,1)} %w_first_hbm.1, bf16[768,1536]{1,0:T(8,128)(2,1)} %w_middle_ref.1), custom_call_target="tpu_custom_call" | custom-call | flops 17179869184 | bytes 67108864 | tf_op jit(solution)/shard_map/forward/pallas_call | solution.py:73
  12.3 0.1 collective-permute-start
  12.4 1.0 collective-permute-start.7
  13.4 0.1 collective-permute-start.4
  13.5 1.1 copy-done.5
  14.6 2.4 %stage.1 = (bf16[663,1536]{1,0:T(8,128)(2,1)S(1)}, bf16[663,256]{1,0:T(8,128)(2,1)S(1)}, bf16[2,344,256]{2,1,0:T(8,128)(2,1)S(1)}, f32[256,768]{1,0:T(8,128)S(1)...) custom-call(s32[5]{0:T(128)S(1)} %stack.23.place_ref, s32[2]{0:T(128)S(1)} %copy-done.3, f32[256,768]{1,0:T(8,128)S(1)} %copy-done.5, ...), custom_call_target="tpu_custom_call" | custom-call | flops 17179869184 | bytes 67108864 | tf_op jit(solution)/shard_map/stage/pallas_call | solution.py:73
  17.0 13.4 %collective-permute-done.1.fetched_ref = bf16[344,1536]{1,0:T(8,128)(2,1)S(1)} collective-permute-done((bf16[344,1536]{1,0:T(8,128)(2,1)S(1)}, bf16[344,1536]{1,0:T(8,128)(2,1)S(1)}, u32[]{:S(2)}, u32[]{:S(2)}) %collective-permute-start.1) | collective-permute-done | bytes 1056800 | tf_op jit(solution)/shard_map/ppermute | solution.py:375
  30.4 1.1 collective-permute-start.2
  31.5 0.0 collective-permute-done.arrived_ref
  31.5 3.1 %hidden.1 = (bf16[256,1536]{1,0:T(8,128)(2,1)S(1)}, f32[256,1536]{1,0:T(8,128)S(1)}, f32[256,1536]{1,0:T(8,128)S(1)}, bf16[1431,256]{1,0:T(8,128)(2,1)S(1)}, bf16[768,256]{1,0:T(8,128)(2,1)S(1)}) custom-call(s32[5]{0:T(128)S(1)} %stack.23.place_ref, bf16[256,1536]{1,0:T(8,128)(2,1)S(1)} %get-tuple-element.82.partial_ref, ...), custom_call_target="tpu_custom_call" | custom-call | flops 17179869184 | bytes 67108864 | tf_op jit(solution)/shard_map/hidden/pallas_call | solution.py:73
  34.7 0.9 collective-permute-start.6
  35.6 0.0 collective-permute-done.2.relayed_ref
  35.6 4.9 %slopes.1 = (bf16[1152,256]{1,0:T(8,128)(2,1)S(1)}, bf16[1152,256]{1,0:T(8,128)(2,1)S(1)}) custom-call(s32[5]{0:T(128)S(1)} %stack.23.place_ref, bf16[256,1536]{1,0:T(8,128)(2,1)S(1)} %get-tuple-element.89.act_ref, f32[256,1536]{1,0:T(8,128)S(1)} %get-tuple-element.90.act_slope_ref, f32[256,1536]{1,0:T(8,128)S(1)} %get-tuple-element.91.back_ref, ...), custom_call_target="tpu_custom_call" | custom-call | flops 17179869184 | bytes 67108864 | tf_op jit(solution)/shard_map/slopes/pallas_call | solution.py:73
  40.5 0.1 collective-permute-start.3
  40.6 0.0 collective-permute-done.6.arrived_ref
  40.7 1.5 %last.1 = (f32[2,4,4,24,384]{4,3,2,1,0:T(8,128)S(1)}, bf16[2,4,4,24,384]{4,3,2,1,0:T(8,128)(2,1)S(1)}) custom-call(s32[5]{0:T(128)S(1)} %stack.23.place_ref, bf16[768,256]{1,0:T(8,128)(2,1)S(1)} %get-tuple-element.103.own_ref, bf16[1431,256]{1,0:T(8,128)(2,1)S(1)} %get-tuple-element.104.sent_ref, bf16[1431,256]{1,0:T(8,128)(2,1)S(1)} %collective-permute-done.6.arrived_ref), custom_call_target="tpu_custom_call" | custom-call | flops 17179869184 | bytes 67108864 | tf_op jit(solution)/shard_map/last/pallas_call | solution.py:73
  42.2 1.5 %collective-permute-start.9 = (bf16[2,4,4,24,384]{4,3,2,1,0:T(8,128)(2,1)S(1)}, bf16[2,4,4,24,384]{4,3,2,1,0:T(8,128)(2,1)S(1)}, u32[]{:S(2)}, u32[]{:S(2)}) collective-permute-start(bf16[2,4,4,24,384]{4,3,2,1,0:T(8,128)(2,1)S(1)} %get-tuple-element.105), channel_id=1, source_target_pairs={{0,4},{4,0},{8,12},{12,8},{1,5},{5,1},{9,13},{13,9},{2,6},{6,2},{1... | collective-permute-start | bytes 1769480 | tf_op jit(solution)/shard_map/ppermute | solution.py:42
  43.6 0.0 collective-permute-done.4.sibling_belief_ref
  43.6 0.0 collective-permute-done.3.arrived_ref
  43.6 2.4 %first.1 = (f32[2,4,4,24,384]{4,3,2,1,0:T(8,128)S(1)}, bf16[2,4,4,24,384]{4,3,2,1,0:T(8,128)(2,1)S(1)}, f32[2,4,3,24,384]{4,3,2,1,0:T(8,128)S(1)}, bf16[2,4,3,24,384]{4,3,2,1,0:T(8,128)(2,1)S(1)}) custom-call(s32[5]{0:T(128)S(1)} %stack.23.place_ref, bf16[1152,256]{1,0:T(8,128)(2,1)S(1)} %get-tuple-element.97.own_ref, ...), custom_call_target="tpu_custom_call" | custom-call | flops 17179869184 | bytes 67108864 | tf_op jit(solution)/shard_map/first/pallas_call | solution.py:73
  46.0 2.8 %collective-permute-start.11 = (bf16[2,4,3,24,384]{4,3,2,1,0:T(8,128)(2,1)S(1)}, bf16[2,4,3,24,384]{4,3,2,1,0:T(8,128)(2,1)S(1)}, u32[]{:S(2)}, u32[]{:S(2)}) collective-permute-start(bf16[2,4,3,24,384]{4,3,2,1,0:T(8,128)(2,1)S(1)} %get-tuple-element.108), channel_id=1, source_target_pairs={{0,96},{32,64},{64,32},{96,0},{1,97},{33,65},{65,33},{97,1},{2,98}... | collective-permute-start | bytes 1327112 | tf_op jit(solution)/shard_map/ppermute | solution.py:42
  48.8 0.0 collective-permute-done.7.sibling_act_ref
  48.8 1.5 %middle.1 = (f32[2,4,4,24,384]{4,3,2,1,0:T(8,128)S(1)}, bf16[2,4,4,24,384]{4,3,2,1,0:T(8,128)(2,1)S(1)}) custom-call(s32[5]{0:T(128)S(1)} %stack.23.place_ref, bf16[1152,256]{1,0:T(8,128)(2,1)S(1)} %get-tuple-element.97.own_ref, bf16[1152,256]{1,0:T(8,128)(2,1)S(1)} %collective-permute-done.3.arrived_ref, bf16[256,768]{1,0:T(8,128)(2,1)S(1)} %copy-done.2, ...), custom_call_target="tpu_custom_call" | custom-call | flops 17179869184 | bytes 67108864 | tf_op jit(solution)/shard_map/middle/pallas_call | solution.py:73
  50.3 1.9 %collective-permute-start.10 = (bf16[2,4,4,24,384]{4,3,2,1,0:T(8,128)(2,1)S(1)}, bf16[2,4,4,24,384]{4,3,2,1,0:T(8,128)(2,1)S(1)}, u32[]{:S(2)}, u32[]{:S(2)}) collective-permute-start(bf16[2,4,4,24,384]{4,3,2,1,0:T(8,128)(2,1)S(1)} %get-tuple-element.107), channel_id=1, source_target_pairs={{0,12},{4,8},{8,4},{12,0},{1,13},{5,9},{9,5},{13,1},{2,14},{6,10},... | collective-permute-start | bytes 1769480 | tf_op jit(solution)/shard_map/ppermute | solution.py:42
  52.2 0.0 collective-permute-start.5
  52.2 4.6 %collective-permute-done.9.arrived_ref = bf16[2,4,4,24,384]{4,3,2,1,0:T(8,128)(2,1)S(1)} collective-permute-done((bf16[2,4,4,24,384]{4,3,2,1,0:T(8,128)(2,1)S(1)}, bf16[2,4,4,24,384]{4,3,2,1,0:T(8,128)(2,1)S(1)}, u32[]{:S(2)}, u32[]{:S(2)}) %collective-permute-start.9) | collective-permute-done | bytes 589856 | tf_op jit(solution)/shard_map/ppermute | solution.py:42
  56.8 0.1 halve.9
  57.0 2.6 %collective-permute-start.13 = (bf16[4,4,24,384]{3,2,1,0:T(8,128)(2,1)S(1)}, bf16[4,4,24,384]{3,2,1,0:T(8,128)(2,1)S(1)}, u32[]{:S(2)}, u32[]{:S(2)}) collective-permute-start(bf16[4,4,24,384]{3,2,1,0:T(8,128)(2,1)S(1)} %get-tuple-element.114), channel_id=1, source_target_pairs={{0,12},{4,8},{8,4},{12,0},{1,13},{5,9},{9,5},{13,1},{2,14},{6,10},... | collective-permute-start | bytes 884744 | tf_op jit(solution)/shard_map/ppermute | solution.py:42
  59.5 0.0 collective-permute-done.11.arrived_ref
  59.5 0.1 halve.11
  59.7 1.4 %collective-permute-start.15 = (bf16[4,3,24,384]{3,2,1,0:T(8,128)(2,1)S(1)}, bf16[4,3,24,384]{3,2,1,0:T(8,128)(2,1)S(1)}, u32[]{:S(2)}, u32[]{:S(2)}) collective-permute-start(bf16[4,3,24,384]{3,2,1,0:T(8,128)(2,1)S(1)} %get-tuple-element.120), channel_id=1, source_target_pairs={{0,32},{32,0},{64,96},{96,64},{1,33},{33,1},{65,97},{97,65},{2,34}... | collective-permute-start | bytes 663560 | tf_op jit(solution)/shard_map/ppermute | solution.py:42
  61.0 4.3 %collective-permute-done.10.arrived_ref = bf16[2,4,4,24,384]{4,3,2,1,0:T(8,128)(2,1)S(1)} collective-permute-done((bf16[2,4,4,24,384]{4,3,2,1,0:T(8,128)(2,1)S(1)}, bf16[2,4,4,24,384]{4,3,2,1,0:T(8,128)(2,1)S(1)}, u32[]{:S(2)}, u32[]{:S(2)}) %collective-permute-start.10) | collective-permute-done | bytes 589856 | tf_op jit(solution)/shard_map/ppermute | solution.py:42
  65.4 0.3 collective-permute-done.5.arrived_ref
  65.7 0.1 halve.10
  65.8 0.4 collective-permute-start.14
  66.2 0.1 halve.8
  66.3 0.2 collective-permute-start.8
  66.5 5.2 %collective-permute-done.13.arrived_ref = bf16[4,4,24,384]{3,2,1,0:T(8,128)(2,1)S(1)} collective-permute-done((bf16[4,4,24,384]{3,2,1,0:T(8,128)(2,1)S(1)}, bf16[4,4,24,384]{3,2,1,0:T(8,128)(2,1)S(1)}, u32[]{:S(2)}, u32[]{:S(2)}) %collective-permute-start.13) | collective-permute-done | bytes 294944 | tf_op jit(solution)/shard_map/ppermute | solution.py:42
  71.7 0.6 turn.5
  72.3 0.1 collective-permute-start.17
  72.4 0.6 turn.7
  73.0 1.9 %collective-permute-start.19 = (bf16[2,3,24,384]{3,2,1,0:T(8,128)(2,1)S(1)}, bf16[2,3,24,384]{3,2,1,0:T(8,128)(2,1)S(1)}, u32[]{:S(2)}, u32[]{:S(2)}) collective-permute-start(bf16[2,3,24,384]{3,2,1,0:T(8,128)(2,1)S(1)} %get-tuple-element.132), channel_id=1, source_target_pairs={{0,12},{4,8},{8,4},{12,0},{1,13},{5,9},{9,5},{13,1},{2,14},{6,10},... | collective-permute-start | bytes 331784 | tf_op jit(solution)/shard_map/ppermute | solution.py:42
  74.9 0.6 turn.6
  75.5 0.7 collective-permute-start.18
  76.2 0.6 turn.4
  76.8 0.1 collective-permute-start.12
  77.0 1.2 %collective-permute-done.19.arrived_ref = bf16[2,3,24,384]{3,2,1,0:T(8,128)(2,1)S(1)} collective-permute-done((bf16[2,3,24,384]{3,2,1,0:T(8,128)(2,1)S(1)}, bf16[2,3,24,384]{3,2,1,0:T(8,128)(2,1)S(1)}, u32[]{:S(2)}, u32[]{:S(2)}) %collective-permute-start.19) | collective-permute-done | bytes 110624 | tf_op jit(solution)/shard_map/ppermute | solution.py:42
  78.2 0.9 collective-permute-start.21
  79.1 1.7 %collective-permute-done.18.arrived_ref = bf16[2,4,24,384]{3,2,1,0:T(8,128)(2,1)S(1)} collective-permute-done((bf16[2,4,24,384]{3,2,1,0:T(8,128)(2,1)S(1)}, bf16[2,4,24,384]{3,2,1,0:T(8,128)(2,1)S(1)}, u32[]{:S(2)}, u32[]{:S(2)}) %collective-permute-start.18) | collective-permute-done | bytes 147488 | tf_op jit(solution)/shard_map/ppermute | solution.py:42
  80.9 0.6 collective-permute-start.22
  81.5 0.7 collective-permute-start.16
  82.3 0.1 collective-permute-start.20
  82.4 0.3 collective-permute-done.21.refs_5_
  82.6 2.8 %collective-permute-done.20.refs_3_ = bf16[3,24,384]{2,1,0:T(8,128)(2,1)S(1)} collective-permute-done((bf16[3,24,384]{2,1,0:T(8,128)(2,1)S(1)}, bf16[3,24,384]{2,1,0:T(8,128)(2,1)S(1)}, u32[]{:S(2)}, u32[]{:S(2)}) %collective-permute-start.20) | collective-permute-done | bytes 55328 | tf_op jit(solution)/shard_map/ppermute | solution.py:42
  85.4 0.6 collective-permute-done.16.refs_1_
  86.0 0.6 z_cut.1
  86.6 1.6 %collective-permute-start.23 = (bf16[8,24,384]{2,1,0:T(8,128)(2,1)S(1)}, bf16[8,24,384]{2,1,0:T(8,128)(2,1)S(1)}, u32[]{:S(2)}, u32[]{:S(2)}) collective-permute-start(bf16[8,24,384]{2,1,0:T(8,128)(2,1)S(1)} %get-tuple-element.153), channel_id=1, source_target_pairs={{0,16},{16,0},{1,17},{17,1},{2,18},{18,2},{3,19},{19,3},{4,20},{20... | collective-permute-start | bytes 442376 | tf_op jit(solution)/shard_map/ppermute | solution.py:37
  88.3 4.0 %collective-permute-done.23.arrived_ref = bf16[8,24,384]{2,1,0:T(8,128)(2,1)S(1)} collective-permute-done((bf16[8,24,384]{2,1,0:T(8,128)(2,1)S(1)}, bf16[8,24,384]{2,1,0:T(8,128)(2,1)S(1)}, u32[]{:S(2)}, u32[]{:S(2)}) %collective-permute-start.23) | collective-permute-done | bytes 147488 | tf_op jit(solution)/shard_map/ppermute | solution.py:37
  92.2 0.3 square.1
  92.5 23.7 %all_to_all.5.squares_ref = f32[128,1,128]{2,1,0:T(1,128)S(1)} all-to-all(f32[128,1,128]{2,1,0:T(1,128)S(1)} %get-tuple-element.155), channel_id=1, replica_groups=mesh['dp_0'=4,'dp_1'=2,'dp_2'=4,'dp_3'=2,'mp'=2] {'dp_0','dp_1','dp_2','..., dimensions={0} | all-to-all | bytes 131072 | tf_op jit(solution)/shard_map/all_to_all | solution.py:510
  116.2 0.9 scale.1
  (21 shorter events, 0.2 us)
Async XLA Ops:
  2.6 27.8 %collective-permute-start.1 = (bf16[344,1536]{1,0:T(8,128)(2,1)S(1)}, bf16[344,1536]{1,0:T(8,128)(2,1)S(1)}, u32[]{:S(2)}, u32[]{:S(2)}) collective-permute-start(bf16[344,1536]{1,0:T(8,128)(2,1)S(1)} %half.1), channel_id=1, source_target_pairs={{0,17},{17,0},{1,16},{16,1},{2,19},{19,2},{3,18},{18,3},{4,21},{21... | collective-permute-start | bytes 3170312 | tf_op jit(solution)/shard_map/ppermute | solution.py:375
  7.3 6.1 %copy-start.1 = (bf16[256,2652]{0,1:T(8,128)(2,1)S(1)}, bf16[256,2652]{0,1:T(8,128)(2,1)}, u32[]{:S(2)}) copy-start(bf16[256,2652]{0,1:T(8,128)(2,1)} %param.7) | copy-start | bytes 4073476
  7.3 6.2 %copy-start.3 = (s32[2]{0:T(128)S(1)}, s32[2]{0:T(128)}, u32[]{:S(2)}) copy-start(s32[2]{0:T(128)} %counts_ref.1) | copy-start | bytes 28
  7.3 6.2 %copy-start.4 = (s32[2,768,1]{2,1,0:T(8,128)S(1)}, s32[2,768,1]{2,1,0:T(8,128)}, u32[]{:S(2)}) copy-start(s32[2,768,1]{2,1,0:T(8,128)} %constant.21.clone.orders_ref) | copy-start | bytes 18436
  12.3 19.2 %collective-permute-start = (bf16[256,1536]{1,0:T(8,128)(2,1)S(1)}, bf16[256,1536]{1,0:T(8,128)(2,1)S(1)}, u32[]{:S(2)}, u32[]{:S(2)}) collective-permute-start(bf16[256,1536]{1,0:T(8,128)(2,1)S(1)} %get-tuple-element.82.partial_ref), channel_id=1, source_target_pairs={{0,1},{1,0},{2,3},{3,2},{4,5},{5,4},{6,7},{7,6},{8,9},{9,8},{10,11... | collective-permute-start | bytes 2359304 | tf_op jit(solution)/shard_map/ppermute | solution.py:37
  12.4 36.4 %collective-permute-start.7 = (bf16[256,768]{1,0:T(8,128)(2,1)}, bf16[256,768]{1,0:T(8,128)(2,1)S(1)}, u32[]{:S(2)}, u32[]{:S(2)}) collective-permute-start(bf16[256,768]{1,0:T(8,128)(2,1)} %get-tuple-element.106.act_ref), channel_id=1, source_target_pairs={{0,2},{2,0},{1,3},{3,1},{4,6},{6,4},{5,7},{7,5},{8,10},{10,8},{9,1... | collective-permute-start | bytes 1179656 | tf_op jit(solution)/shard_map/ppermute | solution.py:37
  13.4 30.2 %collective-permute-start.4 = (bf16[2652,256]{1,0:T(8,128)(2,1)S(1)}, bf16[2652,256]{1,0:T(8,128)(2,1)S(1)}, u32[]{:S(2)}, u32[]{:S(2)}) collective-permute-start(bf16[2652,256]{1,0:T(8,128)(2,1)S(1)} %bitcast.11), channel_id=1, source_target_pairs={{0,2},{2,0},{1,3},{3,1},{4,6},{6,4},{5,7},{7,5},{8,10},{10,8},{9,1... | collective-permute-start | bytes 4073480 | tf_op jit(solution)/shard_map/ppermute | solution.py:37
  13.5 1.1 copy-start.5
  30.4 5.2 %collective-permute-start.2 = (bf16[344,1536]{1,0:T(8,128)(2,1)S(1)}, bf16[344,1536]{1,0:T(8,128)(2,1)S(1)}, u32[]{:S(2)}, u32[]{:S(2)}) collective-permute-start(bf16[344,1536]{1,0:T(8,128)(2,1)S(1)} %collective-permute-done.1.fetched_ref), channel_id=1, source_target_pairs={{0,2},{2,0},{1,3},{3,1},{4,6},{6,4},{5,7},{7,5},{8,10},{10,8},{9,1... | collective-permute-start | bytes 3170312 | tf_op jit(solution)/shard_map/ppermute | solution.py:37
  31.5 4.0 %copy-start = (bf16[768,1536]{1,0:T(8,128)(2,1)S(1)}, bf16[768,1536]{1,0:T(8,128)(2,1)}, u32[]{:S(2)}) copy-start(bf16[768,1536]{1,0:T(8,128)(2,1)} %w_middle_ref.1) | copy-start | bytes 7077892
  34.7 6.0 %collective-permute-start.6 = (bf16[1431,256]{1,0:T(8,128)(2,1)S(1)}, bf16[1431,256]{1,0:T(8,128)(2,1)S(1)}, u32[]{:S(2)}, u32[]{:S(2)}) collective-permute-start(bf16[1431,256]{1,0:T(8,128)(2,1)S(1)} %get-tuple-element.104.sent_ref), channel_id=1, source_target_pairs={{0,2},{2,0},{1,3},{3,1},{4,6},{6,4},{5,7},{7,5},{8,10},{10,8},{9,1... | collective-permute-start | bytes 2198024 | tf_op jit(solution)/shard_map/ppermute | solution.py:37
  40.5 3.1 %collective-permute-start.3 = (bf16[1152,256]{1,0:T(8,128)(2,1)S(1)}, bf16[1152,256]{1,0:T(8,128)(2,1)S(1)}, u32[]{:S(2)}, u32[]{:S(2)}) collective-permute-start(bf16[1152,256]{1,0:T(8,128)(2,1)S(1)} %get-tuple-element.98), channel_id=1, source_target_pairs={{0,2},{2,0},{1,3},{3,1},{4,6},{6,4},{5,7},{7,5},{8,10},{10,8},{9,1... | collective-permute-start | bytes 1769480 | tf_op jit(solution)/shard_map/ppermute | solution.py:37
  42.2 6.7 %copy-start.2 = (bf16[256,768]{1,0:T(8,128)(2,1)S(1)}, bf16[256,768]{1,0:T(8,128)(2,1)}, u32[]{:S(2)}) copy-start(bf16[256,768]{1,0:T(8,128)(2,1)} %get-tuple-element.106.act_ref) | copy-start | bytes 1179652
  42.2 14.7 %collective-permute-start.9 = (bf16[2,4,4,24,384]{4,3,2,1,0:T(8,128)(2,1)S(1)}, bf16[2,4,4,24,384]{4,3,2,1,0:T(8,128)(2,1)S(1)}, u32[]{:S(2)}, u32[]{:S(2)}) collective-permute-start(bf16[2,4,4,24,384]{4,3,2,1,0:T(8,128)(2,1)S(1)} %get-tuple-element.105), channel_id=1, source_target_pairs={{0,4},{4,0},{8,12},{12,8},{1,5},{5,1},{9,13},{13,9},{2,6},{6,2},{1... | collective-permute-start | bytes 1769480 | tf_op jit(solution)/shard_map/ppermute | solution.py:42
  46.0 13.5 %collective-permute-start.11 = (bf16[2,4,3,24,384]{4,3,2,1,0:T(8,128)(2,1)S(1)}, bf16[2,4,3,24,384]{4,3,2,1,0:T(8,128)(2,1)S(1)}, u32[]{:S(2)}, u32[]{:S(2)}) collective-permute-start(bf16[2,4,3,24,384]{4,3,2,1,0:T(8,128)(2,1)S(1)} %get-tuple-element.108), channel_id=1, source_target_pairs={{0,96},{32,64},{64,32},{96,0},{1,97},{33,65},{65,33},{97,1},{2,98}... | collective-permute-start | bytes 1327112 | tf_op jit(solution)/shard_map/ppermute | solution.py:42
  50.3 15.1 %collective-permute-start.10 = (bf16[2,4,4,24,384]{4,3,2,1,0:T(8,128)(2,1)S(1)}, bf16[2,4,4,24,384]{4,3,2,1,0:T(8,128)(2,1)S(1)}, u32[]{:S(2)}, u32[]{:S(2)}) collective-permute-start(bf16[2,4,4,24,384]{4,3,2,1,0:T(8,128)(2,1)S(1)} %get-tuple-element.107), channel_id=1, source_target_pairs={{0,12},{4,8},{8,4},{12,0},{1,13},{5,9},{9,5},{13,1},{2,14},{6,10},... | collective-permute-start | bytes 1769480 | tf_op jit(solution)/shard_map/ppermute | solution.py:42
  52.2 13.5 %collective-permute-start.5 = (bf16[2,4,4,24,384]{4,3,2,1,0:T(8,128)(2,1)S(1)}, bf16[2,4,4,24,384]{4,3,2,1,0:T(8,128)(2,1)S(1)}, u32[]{:S(2)}, u32[]{:S(2)}) collective-permute-start(bf16[2,4,4,24,384]{4,3,2,1,0:T(8,128)(2,1)S(1)} %get-tuple-element.102), channel_id=1, source_target_pairs={{0,32},{32,0},{64,96},{96,64},{1,33},{33,1},{65,97},{97,65},{2,34}... | collective-permute-start | bytes 1769480 | tf_op jit(solution)/shard_map/ppermute | solution.py:42
  57.0 14.7 %collective-permute-start.13 = (bf16[4,4,24,384]{3,2,1,0:T(8,128)(2,1)S(1)}, bf16[4,4,24,384]{3,2,1,0:T(8,128)(2,1)S(1)}, u32[]{:S(2)}, u32[]{:S(2)}) collective-permute-start(bf16[4,4,24,384]{3,2,1,0:T(8,128)(2,1)S(1)} %get-tuple-element.114), channel_id=1, source_target_pairs={{0,12},{4,8},{8,4},{12,0},{1,13},{5,9},{9,5},{13,1},{2,14},{6,10},... | collective-permute-start | bytes 884744 | tf_op jit(solution)/shard_map/ppermute | solution.py:42
  59.7 12.7 %collective-permute-start.15 = (bf16[4,3,24,384]{3,2,1,0:T(8,128)(2,1)S(1)}, bf16[4,3,24,384]{3,2,1,0:T(8,128)(2,1)S(1)}, u32[]{:S(2)}, u32[]{:S(2)}) collective-permute-start(bf16[4,3,24,384]{3,2,1,0:T(8,128)(2,1)S(1)} %get-tuple-element.120), channel_id=1, source_target_pairs={{0,32},{32,0},{64,96},{96,64},{1,33},{33,1},{65,97},{97,65},{2,34}... | collective-permute-start | bytes 663560 | tf_op jit(solution)/shard_map/ppermute | solution.py:42
  65.8 9.1 %collective-permute-start.14 = (bf16[4,4,24,384]{3,2,1,0:T(8,128)(2,1)S(1)}, bf16[4,4,24,384]{3,2,1,0:T(8,128)(2,1)S(1)}, u32[]{:S(2)}, u32[]{:S(2)}) collective-permute-start(bf16[4,4,24,384]{3,2,1,0:T(8,128)(2,1)S(1)} %get-tuple-element.117), channel_id=1, source_target_pairs={{0,4},{4,0},{8,12},{12,8},{1,5},{5,1},{9,13},{13,9},{2,6},{6,2},{1... | collective-permute-start | bytes 884744 | tf_op jit(solution)/shard_map/ppermute | solution.py:42
  66.3 8.6 %collective-permute-start.8 = (bf16[4,4,24,384]{3,2,1,0:T(8,128)(2,1)S(1)}, bf16[4,4,24,384]{3,2,1,0:T(8,128)(2,1)S(1)}, u32[]{:S(2)}, u32[]{:S(2)}) collective-permute-start(bf16[4,4,24,384]{3,2,1,0:T(8,128)(2,1)S(1)} %get-tuple-element.111), channel_id=1, source_target_pairs={{0,96},{32,64},{64,32},{96,0},{1,97},{33,65},{65,33},{97,1},{2,98}... | collective-permute-start | bytes 884744 | tf_op jit(solution)/shard_map/ppermute | solution.py:42
  72.3 4.6 %collective-permute-start.17 = (bf16[2,4,24,384]{3,2,1,0:T(8,128)(2,1)S(1)}, bf16[2,4,24,384]{3,2,1,0:T(8,128)(2,1)S(1)}, u32[]{:S(2)}, u32[]{:S(2)}) collective-permute-start(bf16[2,4,24,384]{3,2,1,0:T(8,128)(2,1)S(1)} %get-tuple-element.126), channel_id=1, source_target_pairs={{0,32},{32,0},{64,96},{96,64},{1,33},{33,1},{65,97},{97,65},{2,34}... | collective-permute-start | bytes 442376 | tf_op jit(solution)/shard_map/ppermute | solution.py:42
  73.0 5.2 %collective-permute-start.19 = (bf16[2,3,24,384]{3,2,1,0:T(8,128)(2,1)S(1)}, bf16[2,3,24,384]{3,2,1,0:T(8,128)(2,1)S(1)}, u32[]{:S(2)}, u32[]{:S(2)}) collective-permute-start(bf16[2,3,24,384]{3,2,1,0:T(8,128)(2,1)S(1)} %get-tuple-element.132), channel_id=1, source_target_pairs={{0,12},{4,8},{8,4},{12,0},{1,13},{5,9},{9,5},{13,1},{2,14},{6,10},... | collective-permute-start | bytes 331784 | tf_op jit(solution)/shard_map/ppermute | solution.py:42
  75.5 5.3 %collective-permute-start.18 = (bf16[2,4,24,384]{3,2,1,0:T(8,128)(2,1)S(1)}, bf16[2,4,24,384]{3,2,1,0:T(8,128)(2,1)S(1)}, u32[]{:S(2)}, u32[]{:S(2)}) collective-permute-start(bf16[2,4,24,384]{3,2,1,0:T(8,128)(2,1)S(1)} %get-tuple-element.129), channel_id=1, source_target_pairs={{0,96},{32,64},{64,32},{96,0},{1,97},{33,65},{65,33},{97,1},{2,98}... | collective-permute-start | bytes 442376 | tf_op jit(solution)/shard_map/ppermute | solution.py:42
  76.8 4.6 %collective-permute-start.12 = (bf16[2,4,24,384]{3,2,1,0:T(8,128)(2,1)S(1)}, bf16[2,4,24,384]{3,2,1,0:T(8,128)(2,1)S(1)}, u32[]{:S(2)}, u32[]{:S(2)}) collective-permute-start(bf16[2,4,24,384]{3,2,1,0:T(8,128)(2,1)S(1)} %get-tuple-element.123), channel_id=1, source_target_pairs={{0,4},{4,0},{8,12},{12,8},{1,5},{5,1},{9,13},{13,9},{2,6},{6,2},{1... | collective-permute-start | bytes 442376 | tf_op jit(solution)/shard_map/ppermute | solution.py:42
  78.2 4.4 %collective-permute-start.21 = (bf16[4,24,384]{2,1,0:T(8,128)(2,1)S(1)}, bf16[4,24,384]{2,1,0:T(8,128)(2,1)S(1)}, u32[]{:S(2)}, u32[]{:S(2)}) collective-permute-start(bf16[4,24,384]{2,1,0:T(8,128)(2,1)S(1)} %get-tuple-element.138), channel_id=1, source_target_pairs={{0,96},{32,64},{64,32},{96,0},{1,97},{33,65},{65,33},{97,1},{2,98}... | collective-permute-start | bytes 221192 | tf_op jit(solution)/shard_map/ppermute | solution.py:42
  80.9 4.5 %collective-permute-start.22 = (bf16[4,24,384]{2,1,0:T(8,128)(2,1)S(1)}, bf16[4,24,384]{2,1,0:T(8,128)(2,1)S(1)}, u32[]{:S(2)}, u32[]{:S(2)}) collective-permute-start(bf16[4,24,384]{2,1,0:T(8,128)(2,1)S(1)} %get-tuple-element.141), channel_id=1, source_target_pairs={{0,32},{32,0},{64,96},{96,64},{1,33},{33,1},{65,97},{97,65},{2,34}... | collective-permute-start | bytes 221192 | tf_op jit(solution)/shard_map/ppermute | solution.py:42
  81.5 4.5 %collective-permute-start.16 = (bf16[4,24,384]{2,1,0:T(8,128)(2,1)S(1)}, bf16[4,24,384]{2,1,0:T(8,128)(2,1)S(1)}, u32[]{:S(2)}, u32[]{:S(2)}) collective-permute-start(bf16[4,24,384]{2,1,0:T(8,128)(2,1)S(1)} %get-tuple-element.135), channel_id=1, source_target_pairs={{0,12},{4,8},{8,4},{12,0},{1,13},{5,9},{9,5},{13,1},{2,14},{6,10},... | collective-permute-start | bytes 221192 | tf_op jit(solution)/shard_map/ppermute | solution.py:42
  82.3 3.1 %collective-permute-start.20 = (bf16[3,24,384]{2,1,0:T(8,128)(2,1)S(1)}, bf16[3,24,384]{2,1,0:T(8,128)(2,1)S(1)}, u32[]{:S(2)}, u32[]{:S(2)}) collective-permute-start(bf16[3,24,384]{2,1,0:T(8,128)(2,1)S(1)} %get-tuple-element.144), channel_id=1, source_target_pairs={{0,4},{4,0},{8,12},{12,8},{1,5},{5,1},{9,13},{13,9},{2,6},{6,2},{1... | collective-permute-start | bytes 165896 | tf_op jit(solution)/shard_map/ppermute | solution.py:42
  86.6 5.6 %collective-permute-start.23 = (bf16[8,24,384]{2,1,0:T(8,128)(2,1)S(1)}, bf16[8,24,384]{2,1,0:T(8,128)(2,1)S(1)}, u32[]{:S(2)}, u32[]{:S(2)}) collective-permute-start(bf16[8,24,384]{2,1,0:T(8,128)(2,1)S(1)} %get-tuple-element.153), channel_id=1, source_target_pairs={{0,16},{16,0},{1,17},{17,1},{2,18},{18,2},{3,19},{19,3},{4,20},{20... | collective-permute-start | bytes 442376 | tf_op jit(solution)/shard_map/ppermute | solution.py:37

commit v12 on v11

--- a/solution.py
+++ b/solution.py
@@ -291,7 +291,7 @@
             arrived, sibling_belief_ref[start:stop, :], 1, 1
         )
         put_columns(raw, start // COLS, raw_ref)
-    for order, part in enumerate((slice(0, 4), slice(4, 7))):
+    for order, part in enumerate((slice(0, 3), slice(3, 7))):
         for side, blocks in enumerate(kept_and_sent(place_ref[1], order)):
             out_ref = refs[2 * order + side]
             for position, y in enumerate(blocks):
@@ -319,7 +319,7 @@
     )
     last_sum[...] = last
     middle_sum[...] = middle
-    rows = [low[granule] for granule in range(4)] + [high[granule] for granule in range(3)]
+    rows = [low[granule] for granule in range(3)] + [high[granule] for granule in range(4)]
     for side, out_ref in ((1 - z_hi, sent_ref), (z_hi, own_ref)):
         kind = out_ref.dtype
         out_ref[0:2] = last_sum[pl.ds(2 * side, 2)].astype(kind)
@@ -477,16 +477,17 @@
         pairs((2, 4, 4)),
         [raw, pltpu.VMEM((2, units, total_rows), BF16)],
     )(place, last_own, last_sent, last_arrived)
+    middle_parts = call(
+        middle_kernel, "middle", [SMEM] + [VMEM] * 4, pairs((2, 4, 4)), [raw]
+    )(place, slopes_own, slopes_arrived, act_first, sibling_act)
+    slopes_own, _ = lax.optimization_barrier((slopes_own, middle_parts[1]))
     first_parts = call(
         first_kernel,
         "first",
         [SMEM] + [VMEM] * 4,
-        pairs((2, 4, 4), (2, 4, 3)),
+        pairs((2, 4, 3), (2, 4, 4)),
         [pltpu.VMEM((16, 7, ROWS, COLS), F32)],
     )(place, slopes_own, slopes_arrived, belief_t, sibling_belief)
-    middle_parts = call(
-        middle_kernel, "middle", [SMEM] + [VMEM] * 4, pairs((2, 4, 4)), [raw]
-    )(place, slopes_own, slopes_arrived, act_first, sibling_act)
     axes, turned, orders, swapped = (X, X, Y, Y), (Y, Y, X, X), (0, 1, 0, 1), (1, 0, 1, 0)
     parts = (last_parts, middle_parts, first_parts[0:2], first_parts[2:4])
     parts = [halve(part, 4) for part in exchange(parts, axes, orders)]

time: 117 us -> 118 us (level)
  waiting for transfers between devices: 38.4 us -> 31.8 us
  starting transfers between devices: 25.4 us -> 29.4 us
  blocking collectives: 23.7 us -> 27.5 us
    ppermute x16, waiting for transfers between devices: 21 us -> 15.3 us  [to_pair(): return lax.ppermute(shard, axis, pairs)]
    all_to_all x1, blocking collectives: 23.7 us -> 27.5 us  [per_device(): squares = lax.all_to_all(squares, ALL, 0, 0, tiled=True)]
    ppermute x16, starting transfers between devices: 15.8 us -> 18.9 us  [to_pair(): return lax.ppermute(shard, axis, pairs)]
  transfers between devices with their start and end apart: 24 -> 24, of which waited for: 11 -> 9; matrix products, arithmetic and copies ran while one was open for 0% -> 0% of each run, Pallas kernels for 20% -> 20%
where the time goes in v12:
time: 118 us
  waiting for transfers between devices  31.8 us (27%)
  starting transfers between devices  29.4 us (25%)
  Pallas kernels  27.5 us (23%)
  blocking collectives  27.5 us (23%)
  local copies, waits for them, and re-layouts  1.24 us (1%)
    pallas_call x23, Pallas kernels, run(): kernel(*(operand if spec is SMEM else pltpu.with_memory_space_constraint(...  27.5 us
    all_to_all x1, blocking collectives, per_device(): squares = lax.all_to_all(squares, ALL, 0, 0, tiled=True)  27.5 us
    ppermute x16, starting transfers between devices, to_pair(): return lax.ppermute(shard, axis, pairs)  18.9 us
    ppermute x16, waiting for transfers between devices, to_pair(): return lax.ppermute(shard, axis, pairs)  15.3 us
    ppermute x1, waiting for transfers between devices, per_device(): fetched = lax.ppermute(half, (ZH, 'mp'), [(0, 3), (3, 0), (1, 2), (2, 1)])  13.4 us
    ppermute x7, starting transfers between devices, swap(): return lax.ppermute(shard, axis, [(0, 1), (1, 0)])  5.81 us
    ppermute x1, starting transfers between devices, per_device(): fetched = lax.ppermute(half, (ZH, 'mp'), [(0, 3), (3, 0), (1, 2), (2, 1)])  4.67 us
    ppermute x7, waiting for transfers between devices, swap(): return lax.ppermute(shard, axis, [(0, 1), (1, 0)])  3.09 us
  transfers between devices with their start and end apart: 24, of which 9 were waited for; matrix products, arithmetic and copies ran while one was open for 0% of the time, Pallas kernels for 20%

profile of v12, /device:TPU:1, one launch (start us, length us, event | category | flops | bytes accessed | tf_op | source)
XLA Modules:
  0.0 118.2 jit_solution(4696200889827681933)
XLA Ops:
  0.6 0.1 stack.23.place_ref
  0.7 1.9 %half.1 = bf16[344,1536]{1,0:T(8,128)(2,1)S(1)} custom-call(s32[5]{0:T(128)S(1)} %stack.23.place_ref, bf16[663,1536]{1,0:T(8,128)(2,1)} %bitcast.13), custom_call_target="tpu_custom_call" | custom-call | flops 17179869184 | bytes 67108864 | tf_op jit(solution)/shard_map/half/pallas_call | solution.py:73
  2.6 4.7 %collective-permute-start.1 = (bf16[344,1536]{1,0:T(8,128)(2,1)S(1)}, bf16[344,1536]{1,0:T(8,128)(2,1)S(1)}, u32[]{:S(2)}, u32[]{:S(2)}) collective-permute-start(bf16[344,1536]{1,0:T(8,128)(2,1)S(1)} %half.1), channel_id=1, source_target_pairs={{0,17},{17,0},{1,16},{16,1},{2,19},{19,2},{3,18},{18,3},{4,21},{21... | collective-permute-start | bytes 3170312 | tf_op jit(solution)/shard_map/ppermute | solution.py:375
  7.3 5.1 %forward.1 = (f32[256,768]{1,0:T(8,128)}, bf16[256,768]{1,0:T(8,128)(2,1)}, bf16[256,1536]{1,0:T(8,128)(2,1)S(1)}) custom-call(bf16[2652,256]{1,0:T(8,128)(2,1)} %bitcast.10, bf16[2652,768]{1,0:T(8,128)(2,1)} %w_first_hbm.1, bf16[768,1536]{1,0:T(8,128)(2,1)} %w_middle_ref.1), custom_call_target="tpu_custom_call" | custom-call | flops 17179869184 | bytes 67108864 | tf_op jit(solution)/shard_map/forward/pallas_call | solution.py:73
  12.3 0.1 collective-permute-start
  12.4 1.0 collective-permute-start.4
  13.4 0.1 collective-permute-start.5
  13.5 1.1 copy-done.5
  14.6 2.4 %stage.1 = (bf16[663,1536]{1,0:T(8,128)(2,1)S(1)}, bf16[663,256]{1,0:T(8,128)(2,1)S(1)}, bf16[2,344,256]{2,1,0:T(8,128)(2,1)S(1)}, f32[256,768]{1,0:T(8,128)S(1)...) custom-call(s32[5]{0:T(128)S(1)} %stack.23.place_ref, s32[2]{0:T(128)S(1)} %copy-done.3, f32[256,768]{1,0:T(8,128)S(1)} %copy-done.5, ...), custom_call_target="tpu_custom_call" | custom-call | flops 17179869184 | bytes 67108864 | tf_op jit(solution)/shard_map/stage/pallas_call | solution.py:73
  17.0 13.4 %collective-permute-done.1.fetched_ref = bf16[344,1536]{1,0:T(8,128)(2,1)S(1)} collective-permute-done((bf16[344,1536]{1,0:T(8,128)(2,1)S(1)}, bf16[344,1536]{1,0:T(8,128)(2,1)S(1)}, u32[]{:S(2)}, u32[]{:S(2)}) %collective-permute-start.1) | collective-permute-done | bytes 1056800 | tf_op jit(solution)/shard_map/ppermute | solution.py:375
  30.4 1.1 collective-permute-start.2
  31.5 0.0 collective-permute-done.arrived_ref
  31.5 3.1 %hidden.1 = (bf16[256,1536]{1,0:T(8,128)(2,1)S(1)}, f32[256,1536]{1,0:T(8,128)S(1)}, f32[256,1536]{1,0:T(8,128)S(1)}, bf16[1431,256]{1,0:T(8,128)(2,1)S(1)}, bf16[768,256]{1,0:T(8,128)(2,1)S(1)}) custom-call(s32[5]{0:T(128)S(1)} %stack.23.place_ref, bf16[256,1536]{1,0:T(8,128)(2,1)S(1)} %get-tuple-element.83.partial_ref, ...), custom_call_target="tpu_custom_call" | custom-call | flops 17179869184 | bytes 67108864 | tf_op jit(solution)/shard_map/hidden/pallas_call | solution.py:73
  34.7 0.9 collective-permute-start.7
  35.6 0.0 collective-permute-done.2.relayed_ref
  35.6 4.9 %slopes.1 = (bf16[1152,256]{1,0:T(8,128)(2,1)S(1)}, bf16[1152,256]{1,0:T(8,128)(2,1)S(1)}) custom-call(s32[5]{0:T(128)S(1)} %stack.23.place_ref, bf16[256,1536]{1,0:T(8,128)(2,1)S(1)} %get-tuple-element.90.act_ref, f32[256,1536]{1,0:T(8,128)S(1)} %get-tuple-element.91.act_slope_ref, f32[256,1536]{1,0:T(8,128)S(1)} %get-tuple-element.92.back_ref, ...), custom_call_target="tpu_custom_call" | custom-call | flops 17179869184 | bytes 67108864 | tf_op jit(solution)/shard_map/slopes/pallas_call | solution.py:73
  40.5 0.1 collective-permute-start.3
  40.7 1.5 %last.1 = (f32[2,4,4,24,384]{4,3,2,1,0:T(8,128)S(1)}, bf16[2,4,4,24,384]{4,3,2,1,0:T(8,128)(2,1)S(1)}) custom-call(s32[5]{0:T(128)S(1)} %stack.23.place_ref, bf16[768,256]{1,0:T(8,128)(2,1)S(1)} %get-tuple-element.107.own_ref, bf16[1431,256]{1,0:T(8,128)(2,1)S(1)} %get-tuple-element.108.sent_ref, bf16[1431,256]{1,0:T(8,128)(2,1)S(1)} %collective-permute-done.7.arrived_ref), custom_call_target="tpu_custom_call" | custom-call | flops 17179869184 | bytes 67108864 | tf_op jit(solution)/shard_map/last/pallas_call | solution.py:73
  42.2 1.5 %collective-permute-start.9 = (bf16[2,4,4,24,384]{4,3,2,1,0:T(8,128)(2,1)S(1)}, bf16[2,4,4,24,384]{4,3,2,1,0:T(8,128)(2,1)S(1)}, u32[]{:S(2)}, u32[]{:S(2)}) collective-permute-start(bf16[2,4,4,24,384]{4,3,2,1,0:T(8,128)(2,1)S(1)} %get-tuple-element.109), channel_id=1, source_target_pairs={{0,4},{4,0},{8,12},{12,8},{1,5},{5,1},{9,13},{13,9},{2,6},{6,2},{1... | collective-permute-start | bytes 1769480 | tf_op jit(solution)/shard_map/ppermute | solution.py:42
  43.6 0.0 collective-permute-done.4.sibling_act_ref
  43.6 0.0 collective-permute-done.3.arrived_ref
  43.6 1.5 %middle.1 = (f32[2,4,4,24,384]{4,3,2,1,0:T(8,128)S(1)}, bf16[2,4,4,24,384]{4,3,2,1,0:T(8,128)(2,1)S(1)}) custom-call(s32[5]{0:T(128)S(1)} %stack.23.place_ref, bf16[1152,256]{1,0:T(8,128)(2,1)S(1)} %get-tuple-element.103.own_ref, bf16[1152,256]{1,0:T(8,128)(2,1)S(1)} %collective-permute-done.3.arrived_ref, bf16[256,768]{1,0:T(8,128)(2,1)S(1)} %copy-done.2, ...), custom_call_target="tpu_custom_call" | custom-call | flops 17179869184 | bytes 67108864 | tf_op jit(solution)/shard_map/middle/pallas_call | solution.py:73
  45.1 1.9 %collective-permute-start.10 = (bf16[2,4,4,24,384]{4,3,2,1,0:T(8,128)(2,1)S(1)}, bf16[2,4,4,24,384]{4,3,2,1,0:T(8,128)(2,1)S(1)}, u32[]{:S(2)}, u32[]{:S(2)}) collective-permute-start(bf16[2,4,4,24,384]{4,3,2,1,0:T(8,128)(2,1)S(1)} %get-tuple-element.102), channel_id=1, source_target_pairs={{0,12},{4,8},{8,4},{12,0},{1,13},{5,9},{9,5},{13,1},{2,14},{6,10},... | collective-permute-start | bytes 1769480 | tf_op jit(solution)/shard_map/ppermute | solution.py:42
  47.0 0.0 collective-permute-done.5.sibling_belief_ref
  47.0 2.4 %first.1 = (f32[2,4,3,24,384]{4,3,2,1,0:T(8,128)S(1)}, bf16[2,4,3,24,384]{4,3,2,1,0:T(8,128)(2,1)S(1)}, f32[2,4,4,24,384]{4,3,2,1,0:T(8,128)S(1)}, bf16[2,4,4,24,384]{4,3,2,1,0:T(8,128)(2,1)S(1)}) custom-call(s32[5]{0:T(128)S(1)} %stack.23.place_ref, bf16[1152,256]{1,0:T(8,128)(2,1)S(1)} %get-tuple-element.103.own_ref, ...), custom_call_target="tpu_custom_call" | custom-call | flops 17179869184 | bytes 67108864 | tf_op jit(solution)/shard_map/first/pallas_call | solution.py:73
  49.4 2.8 %collective-permute-start.11 = (bf16[2,4,4,24,384]{4,3,2,1,0:T(8,128)(2,1)S(1)}, bf16[2,4,4,24,384]{4,3,2,1,0:T(8,128)(2,1)S(1)}, u32[]{:S(2)}, u32[]{:S(2)}) collective-permute-start(bf16[2,4,4,24,384]{4,3,2,1,0:T(8,128)(2,1)S(1)} %get-tuple-element.110), channel_id=1, source_target_pairs={{0,96},{32,64},{64,32},{96,0},{1,97},{33,65},{65,33},{97,1},{2,98}... | collective-permute-start | bytes 1769480 | tf_op jit(solution)/shard_map/ppermute | solution.py:42
  52.2 4.6 %collective-permute-done.9.arrived_ref = bf16[2,4,4,24,384]{4,3,2,1,0:T(8,128)(2,1)S(1)} collective-permute-done((bf16[2,4,4,24,384]{4,3,2,1,0:T(8,128)(2,1)S(1)}, bf16[2,4,4,24,384]{4,3,2,1,0:T(8,128)(2,1)S(1)}, u32[]{:S(2)}, u32[]{:S(2)}) %collective-permute-start.9) | collective-permute-done | bytes 589856 | tf_op jit(solution)/shard_map/ppermute | solution.py:42
  56.8 0.1 halve.9
  57.0 2.6 %collective-permute-start.13 = (bf16[4,4,24,384]{3,2,1,0:T(8,128)(2,1)S(1)}, bf16[4,4,24,384]{3,2,1,0:T(8,128)(2,1)S(1)}, u32[]{:S(2)}, u32[]{:S(2)}) collective-permute-start(bf16[4,4,24,384]{3,2,1,0:T(8,128)(2,1)S(1)} %get-tuple-element.116), channel_id=1, source_target_pairs={{0,12},{4,8},{8,4},{12,0},{1,13},{5,9},{9,5},{13,1},{2,14},{6,10},... | collective-permute-start | bytes 884744 | tf_op jit(solution)/shard_map/ppermute | solution.py:42
  59.5 3.0 %collective-permute-done.6.arrived_ref = bf16[2,4,3,24,384]{4,3,2,1,0:T(8,128)(2,1)S(1)} collective-permute-done((bf16[2,4,3,24,384]{4,3,2,1,0:T(8,128)(2,1)S(1)}, bf16[2,4,3,24,384]{4,3,2,1,0:T(8,128)(2,1)S(1)}, u32[]{:S(2)}, u32[]{:S(2)}) %collective-permute-start.6) | collective-permute-done | bytes 442400 | tf_op jit(solution)/shard_map/ppermute | solution.py:42
  62.5 0.1 halve.8
  62.6 0.3 collective-permute-start.8
  62.9 1.6 %collective-permute-done.11.arrived_ref = bf16[2,4,4,24,384]{4,3,2,1,0:T(8,128)(2,1)S(1)} collective-permute-done((bf16[2,4,4,24,384]{4,3,2,1,0:T(8,128)(2,1)S(1)}, bf16[2,4,4,24,384]{4,3,2,1,0:T(8,128)(2,1)S(1)}, u32[]{:S(2)}, u32[]{:S(2)}) %collective-permute-start.11) | collective-permute-done | bytes 589856 | tf_op jit(solution)/shard_map/ppermute | solution.py:42
  64.6 0.1 halve.11
  64.7 0.1 collective-permute-start.15
  64.8 0.0 collective-permute-done.10.arrived_ref
  64.8 0.1 halve.10
  65.0 0.4 collective-permute-start.14
  65.4 1.6 %collective-permute-done.13.arrived_ref = bf16[4,4,24,384]{3,2,1,0:T(8,128)(2,1)S(1)} collective-permute-done((bf16[4,4,24,384]{3,2,1,0:T(8,128)(2,1)S(1)}, bf16[4,4,24,384]{3,2,1,0:T(8,128)(2,1)S(1)}, u32[]{:S(2)}, u32[]{:S(2)}) %collective-permute-start.13) | collective-permute-done | bytes 294944 | tf_op jit(solution)/shard_map/ppermute | solution.py:42
  67.0 0.6 turn.5
  67.6 1.4 %collective-permute-start.17 = (bf16[2,4,24,384]{3,2,1,0:T(8,128)(2,1)S(1)}, bf16[2,4,24,384]{3,2,1,0:T(8,128)(2,1)S(1)}, u32[]{:S(2)}, u32[]{:S(2)}) collective-permute-start(bf16[2,4,24,384]{3,2,1,0:T(8,128)(2,1)S(1)} %get-tuple-element.128), channel_id=1, source_target_pairs={{0,32},{32,0},{64,96},{96,64},{1,33},{33,1},{65,97},{97,65},{2,34}... | collective-permute-start | bytes 442376 | tf_op jit(solution)/shard_map/ppermute | solution.py:42
  69.0 0.0 collective-permute-done.8.arrived_ref
  69.0 0.6 turn.4
  69.6 0.1 collective-permute-start.12
  69.7 1.0 collective-permute-done.15.arrived_ref
  70.7 0.6 turn.7
  71.3 1.0 collective-permute-start.19
  72.2 0.0 collective-permute-done.14.arrived_ref
  72.2 0.6 turn.6
  72.9 2.7 %collective-permute-start.18 = (bf16[2,4,24,384]{3,2,1,0:T(8,128)(2,1)S(1)}, bf16[2,4,24,384]{3,2,1,0:T(8,128)(2,1)S(1)}, u32[]{:S(2)}, u32[]{:S(2)}) collective-permute-start(bf16[2,4,24,384]{3,2,1,0:T(8,128)(2,1)S(1)} %get-tuple-element.131), channel_id=1, source_target_pairs={{0,96},{32,64},{64,32},{96,0},{1,97},{33,65},{65,33},{97,1},{2,98}... | collective-permute-start | bytes 442376 | tf_op jit(solution)/shard_map/ppermute | solution.py:42
  75.5 0.0 collective-permute-done.17.arrived_ref
  75.6 0.0 collective-permute-done.12.arrived_ref
  75.6 2.1 %collective-permute-start.21 = (bf16[4,24,384]{2,1,0:T(8,128)(2,1)S(1)}, bf16[4,24,384]{2,1,0:T(8,128)(2,1)S(1)}, u32[]{:S(2)}, u32[]{:S(2)}) collective-permute-start(bf16[4,24,384]{2,1,0:T(8,128)(2,1)S(1)} %get-tuple-element.140), channel_id=1, source_target_pairs={{0,96},{32,64},{64,32},{96,0},{1,97},{33,65},{65,33},{97,1},{2,98}... | collective-permute-start | bytes 221192 | tf_op jit(solution)/shard_map/ppermute | solution.py:42
  77.7 0.5 collective-permute-done.18.arrived_ref
  78.2 0.1 collective-permute-start.22
  78.3 0.4 collective-permute-start.20
  78.8 1.7 %collective-permute-start.16 = (bf16[3,24,384]{2,1,0:T(8,128)(2,1)S(1)}, bf16[3,24,384]{2,1,0:T(8,128)(2,1)S(1)}, u32[]{:S(2)}, u32[]{:S(2)}) collective-permute-start(bf16[3,24,384]{2,1,0:T(8,128)(2,1)S(1)} %get-tuple-element.137), channel_id=1, source_target_pairs={{0,12},{4,8},{8,4},{12,0},{1,13},{5,9},{9,5},{13,1},{2,14},{6,10},... | collective-permute-start | bytes 165896 | tf_op jit(solution)/shard_map/ppermute | solution.py:42
  80.4 2.9 %collective-permute-done.16.refs_1_ = bf16[3,24,384]{2,1,0:T(8,128)(2,1)S(1)} collective-permute-done((bf16[3,24,384]{2,1,0:T(8,128)(2,1)S(1)}, bf16[3,24,384]{2,1,0:T(8,128)(2,1)S(1)}, u32[]{:S(2)}, u32[]{:S(2)}) %collective-permute-start.16) | collective-permute-done | bytes 55328 | tf_op jit(solution)/shard_map/ppermute | solution.py:42
  83.4 0.6 z_cut.1
  84.0 2.5 %collective-permute-start.23 = (bf16[8,24,384]{2,1,0:T(8,128)(2,1)S(1)}, bf16[8,24,384]{2,1,0:T(8,128)(2,1)S(1)}, u32[]{:S(2)}, u32[]{:S(2)}) collective-permute-start(bf16[8,24,384]{2,1,0:T(8,128)(2,1)S(1)} %get-tuple-element.155), channel_id=1, source_target_pairs={{0,16},{16,0},{1,17},{17,1},{2,18},{18,2},{3,19},{19,3},{4,20},{20... | collective-permute-start | bytes 442376 | tf_op jit(solution)/shard_map/ppermute | solution.py:37
  86.5 3.1 %collective-permute-done.23.arrived_ref = bf16[8,24,384]{2,1,0:T(8,128)(2,1)S(1)} collective-permute-done((bf16[8,24,384]{2,1,0:T(8,128)(2,1)S(1)}, bf16[8,24,384]{2,1,0:T(8,128)(2,1)S(1)}, u32[]{:S(2)}, u32[]{:S(2)}) %collective-permute-start.23) | collective-permute-done | bytes 147488 | tf_op jit(solution)/shard_map/ppermute | solution.py:37
  89.6 0.3 square.1
  89.9 27.5 %all_to_all.5.squares_ref = f32[128,1,128]{2,1,0:T(1,128)S(1)} all-to-all(f32[128,1,128]{2,1,0:T(1,128)S(1)} %get-tuple-element.157), channel_id=1, replica_groups=mesh['dp_0'=4,'dp_1'=2,'dp_2'=4,'dp_3'=2,'mp'=2] {'dp_0','dp_1','dp_2','..., dimensions={0} | all-to-all | bytes 131072 | tf_op jit(solution)/shard_map/all_to_all | solution.py:511
  117.3 0.9 scale.1
  (21 shorter events, 0.2 us)
Async XLA Ops:
  2.6 27.8 %collective-permute-start.1 = (bf16[344,1536]{1,0:T(8,128)(2,1)S(1)}, bf16[344,1536]{1,0:T(8,128)(2,1)S(1)}, u32[]{:S(2)}, u32[]{:S(2)}) collective-permute-start(bf16[344,1536]{1,0:T(8,128)(2,1)S(1)} %half.1), channel_id=1, source_target_pairs={{0,17},{17,0},{1,16},{16,1},{2,19},{19,2},{3,18},{18,3},{4,21},{21... | collective-permute-start | bytes 3170312 | tf_op jit(solution)/shard_map/ppermute | solution.py:375
  7.3 6.1 %copy-start.1 = (bf16[256,2652]{0,1:T(8,128)(2,1)S(1)}, bf16[256,2652]{0,1:T(8,128)(2,1)}, u32[]{:S(2)}) copy-start(bf16[256,2652]{0,1:T(8,128)(2,1)} %param.7) | copy-start | bytes 4073476
  7.3 6.2 %copy-start.3 = (s32[2]{0:T(128)S(1)}, s32[2]{0:T(128)}, u32[]{:S(2)}) copy-start(s32[2]{0:T(128)} %counts_ref.1) | copy-start | bytes 28
  7.3 6.2 %copy-start.4 = (s32[2,768,1]{2,1,0:T(8,128)S(1)}, s32[2,768,1]{2,1,0:T(8,128)}, u32[]{:S(2)}) copy-start(s32[2,768,1]{2,1,0:T(8,128)} %constant.21.clone.orders_ref) | copy-start | bytes 18436
  12.3 19.2 %collective-permute-start = (bf16[256,1536]{1,0:T(8,128)(2,1)S(1)}, bf16[256,1536]{1,0:T(8,128)(2,1)S(1)}, u32[]{:S(2)}, u32[]{:S(2)}) collective-permute-start(bf16[256,1536]{1,0:T(8,128)(2,1)S(1)} %get-tuple-element.83.partial_ref), channel_id=1, source_target_pairs={{0,1},{1,0},{2,3},{3,2},{4,5},{5,4},{6,7},{7,6},{8,9},{9,8},{10,11... | collective-permute-start | bytes 2359304 | tf_op jit(solution)/shard_map/ppermute | solution.py:37
  12.4 31.2 %collective-permute-start.4 = (bf16[256,768]{1,0:T(8,128)(2,1)}, bf16[256,768]{1,0:T(8,128)(2,1)S(1)}, u32[]{:S(2)}, u32[]{:S(2)}) collective-permute-start(bf16[256,768]{1,0:T(8,128)(2,1)} %get-tuple-element.101.act_ref), channel_id=1, source_target_pairs={{0,2},{2,0},{1,3},{3,1},{4,6},{6,4},{5,7},{7,5},{8,10},{10,8},{9,1... | collective-permute-start | bytes 1179656 | tf_op jit(solution)/shard_map/ppermute | solution.py:37
  13.4 33.6 %collective-permute-start.5 = (bf16[2652,256]{1,0:T(8,128)(2,1)S(1)}, bf16[2652,256]{1,0:T(8,128)(2,1)S(1)}, u32[]{:S(2)}, u32[]{:S(2)}) collective-permute-start(bf16[2652,256]{1,0:T(8,128)(2,1)S(1)} %bitcast.11), channel_id=1, source_target_pairs={{0,2},{2,0},{1,3},{3,1},{4,6},{6,4},{5,7},{7,5},{8,10},{10,8},{9,1... | collective-permute-start | bytes 4073480 | tf_op jit(solution)/shard_map/ppermute | solution.py:37
  13.5 1.1 copy-start.5
  30.4 5.2 %collective-permute-start.2 = (bf16[344,1536]{1,0:T(8,128)(2,1)S(1)}, bf16[344,1536]{1,0:T(8,128)(2,1)S(1)}, u32[]{:S(2)}, u32[]{:S(2)}) collective-permute-start(bf16[344,1536]{1,0:T(8,128)(2,1)S(1)} %collective-permute-done.1.fetched_ref), channel_id=1, source_target_pairs={{0,2},{2,0},{1,3},{3,1},{4,6},{6,4},{5,7},{7,5},{8,10},{10,8},{9,1... | collective-permute-start | bytes 3170312 | tf_op jit(solution)/shard_map/ppermute | solution.py:37
  31.5 4.0 %copy-start = (bf16[768,1536]{1,0:T(8,128)(2,1)S(1)}, bf16[768,1536]{1,0:T(8,128)(2,1)}, u32[]{:S(2)}) copy-start(bf16[768,1536]{1,0:T(8,128)(2,1)} %w_middle_ref.1) | copy-start | bytes 7077892
  34.7 6.0 %collective-permute-start.7 = (bf16[1431,256]{1,0:T(8,128)(2,1)S(1)}, bf16[1431,256]{1,0:T(8,128)(2,1)S(1)}, u32[]{:S(2)}, u32[]{:S(2)}) collective-permute-start(bf16[1431,256]{1,0:T(8,128)(2,1)S(1)} %get-tuple-element.108.sent_ref), channel_id=1, source_target_pairs={{0,2},{2,0},{1,3},{3,1},{4,6},{6,4},{5,7},{7,5},{8,10},{10,8},{9,1... | collective-permute-start | bytes 2198024 | tf_op jit(solution)/shard_map/ppermute | solution.py:37
  40.5 3.1 %copy-start.2 = (bf16[256,768]{1,0:T(8,128)(2,1)S(1)}, bf16[256,768]{1,0:T(8,128)(2,1)}, u32[]{:S(2)}) copy-start(bf16[256,768]{1,0:T(8,128)(2,1)} %get-tuple-element.101.act_ref) | copy-start | bytes 1179652
  40.5 3.1 %collective-permute-start.3 = (bf16[1152,256]{1,0:T(8,128)(2,1)S(1)}, bf16[1152,256]{1,0:T(8,128)(2,1)S(1)}, u32[]{:S(2)}, u32[]{:S(2)}) collective-permute-start(bf16[1152,256]{1,0:T(8,128)(2,1)S(1)} %get-tuple-element.99), channel_id=1, source_target_pairs={{0,2},{2,0},{1,3},{3,1},{4,6},{6,4},{5,7},{7,5},{8,10},{10,8},{9,1... | collective-permute-start | bytes 1769480 | tf_op jit(solution)/shard_map/ppermute | solution.py:37
  42.2 14.7 %collective-permute-start.9 = (bf16[2,4,4,24,384]{4,3,2,1,0:T(8,128)(2,1)S(1)}, bf16[2,4,4,24,384]{4,3,2,1,0:T(8,128)(2,1)S(1)}, u32[]{:S(2)}, u32[]{:S(2)}) collective-permute-start(bf16[2,4,4,24,384]{4,3,2,1,0:T(8,128)(2,1)S(1)} %get-tuple-element.109), channel_id=1, source_target_pairs={{0,4},{4,0},{8,12},{12,8},{1,5},{5,1},{9,13},{13,9},{2,6},{6,2},{1... | collective-permute-start | bytes 1769480 | tf_op jit(solution)/shard_map/ppermute | solution.py:42
  45.1 19.7 %collective-permute-start.10 = (bf16[2,4,4,24,384]{4,3,2,1,0:T(8,128)(2,1)S(1)}, bf16[2,4,4,24,384]{4,3,2,1,0:T(8,128)(2,1)S(1)}, u32[]{:S(2)}, u32[]{:S(2)}) collective-permute-start(bf16[2,4,4,24,384]{4,3,2,1,0:T(8,128)(2,1)S(1)} %get-tuple-element.102), channel_id=1, source_target_pairs={{0,12},{4,8},{8,4},{12,0},{1,13},{5,9},{9,5},{13,1},{2,14},{6,10},... | collective-permute-start | bytes 1769480 | tf_op jit(solution)/shard_map/ppermute | solution.py:42
  49.4 15.2 %collective-permute-start.11 = (bf16[2,4,4,24,384]{4,3,2,1,0:T(8,128)(2,1)S(1)}, bf16[2,4,4,24,384]{4,3,2,1,0:T(8,128)(2,1)S(1)}, u32[]{:S(2)}, u32[]{:S(2)}) collective-permute-start(bf16[2,4,4,24,384]{4,3,2,1,0:T(8,128)(2,1)S(1)} %get-tuple-element.110), channel_id=1, source_target_pairs={{0,96},{32,64},{64,32},{96,0},{1,97},{33,65},{65,33},{97,1},{2,98}... | collective-permute-start | bytes 1769480 | tf_op jit(solution)/shard_map/ppermute | solution.py:42
  52.2 10.3 %collective-permute-start.6 = (bf16[2,4,3,24,384]{4,3,2,1,0:T(8,128)(2,1)S(1)}, bf16[2,4,3,24,384]{4,3,2,1,0:T(8,128)(2,1)S(1)}, u32[]{:S(2)}, u32[]{:S(2)}) collective-permute-start(bf16[2,4,3,24,384]{4,3,2,1,0:T(8,128)(2,1)S(1)} %get-tuple-element.106), channel_id=1, source_target_pairs={{0,32},{32,0},{64,96},{96,64},{1,33},{33,1},{65,97},{97,65},{2,34}... | collective-permute-start | bytes 1327112 | tf_op jit(solution)/shard_map/ppermute | solution.py:42
  57.0 10.0 %collective-permute-start.13 = (bf16[4,4,24,384]{3,2,1,0:T(8,128)(2,1)S(1)}, bf16[4,4,24,384]{3,2,1,0:T(8,128)(2,1)S(1)}, u32[]{:S(2)}, u32[]{:S(2)}) collective-permute-start(bf16[4,4,24,384]{3,2,1,0:T(8,128)(2,1)S(1)} %get-tuple-element.116), channel_id=1, source_target_pairs={{0,12},{4,8},{8,4},{12,0},{1,13},{5,9},{9,5},{13,1},{2,14},{6,10},... | collective-permute-start | bytes 884744 | tf_op jit(solution)/shard_map/ppermute | solution.py:42
  62.6 6.3 %collective-permute-start.8 = (bf16[4,3,24,384]{3,2,1,0:T(8,128)(2,1)S(1)}, bf16[4,3,24,384]{3,2,1,0:T(8,128)(2,1)S(1)}, u32[]{:S(2)}, u32[]{:S(2)}) collective-permute-start(bf16[4,3,24,384]{3,2,1,0:T(8,128)(2,1)S(1)} %get-tuple-element.113), channel_id=1, source_target_pairs={{0,96},{32,64},{64,32},{96,0},{1,97},{33,65},{65,33},{97,1},{2,98}... | collective-permute-start | bytes 663560 | tf_op jit(solution)/shard_map/ppermute | solution.py:42
  64.7 5.9 %collective-permute-start.15 = (bf16[4,4,24,384]{3,2,1,0:T(8,128)(2,1)S(1)}, bf16[4,4,24,384]{3,2,1,0:T(8,128)(2,1)S(1)}, u32[]{:S(2)}, u32[]{:S(2)}) collective-permute-start(bf16[4,4,24,384]{3,2,1,0:T(8,128)(2,1)S(1)} %get-tuple-element.122), channel_id=1, source_target_pairs={{0,32},{32,0},{64,96},{96,64},{1,33},{33,1},{65,97},{97,65},{2,34}... | collective-permute-start | bytes 884744 | tf_op jit(solution)/shard_map/ppermute | solution.py:42
  65.0 7.3 %collective-permute-start.14 = (bf16[4,4,24,384]{3,2,1,0:T(8,128)(2,1)S(1)}, bf16[4,4,24,384]{3,2,1,0:T(8,128)(2,1)S(1)}, u32[]{:S(2)}, u32[]{:S(2)}) collective-permute-start(bf16[4,4,24,384]{3,2,1,0:T(8,128)(2,1)S(1)} %get-tuple-element.119), channel_id=1, source_target_pairs={{0,4},{4,0},{8,12},{12,8},{1,5},{5,1},{9,13},{13,9},{2,6},{6,2},{1... | collective-permute-start | bytes 884744 | tf_op jit(solution)/shard_map/ppermute | solution.py:42
  67.6 7.9 %collective-permute-start.17 = (bf16[2,4,24,384]{3,2,1,0:T(8,128)(2,1)S(1)}, bf16[2,4,24,384]{3,2,1,0:T(8,128)(2,1)S(1)}, u32[]{:S(2)}, u32[]{:S(2)}) collective-permute-start(bf16[2,4,24,384]{3,2,1,0:T(8,128)(2,1)S(1)} %get-tuple-element.128), channel_id=1, source_target_pairs={{0,32},{32,0},{64,96},{96,64},{1,33},{33,1},{65,97},{97,65},{2,34}... | collective-permute-start | bytes 442376 | tf_op jit(solution)/shard_map/ppermute | solution.py:42
  69.6 6.0 %collective-permute-start.12 = (bf16[2,3,24,384]{3,2,1,0:T(8,128)(2,1)S(1)}, bf16[2,3,24,384]{3,2,1,0:T(8,128)(2,1)S(1)}, u32[]{:S(2)}, u32[]{:S(2)}) collective-permute-start(bf16[2,3,24,384]{3,2,1,0:T(8,128)(2,1)S(1)} %get-tuple-element.125), channel_id=1, source_target_pairs={{0,4},{4,0},{8,12},{12,8},{1,5},{5,1},{9,13},{13,9},{2,6},{6,2},{1... | collective-permute-start | bytes 331784 | tf_op jit(solution)/shard_map/ppermute | solution.py:42
  71.3 6.4 %collective-permute-start.19 = (bf16[2,4,24,384]{3,2,1,0:T(8,128)(2,1)S(1)}, bf16[2,4,24,384]{3,2,1,0:T(8,128)(2,1)S(1)}, u32[]{:S(2)}, u32[]{:S(2)}) collective-permute-start(bf16[2,4,24,384]{3,2,1,0:T(8,128)(2,1)S(1)} %get-tuple-element.134), channel_id=1, source_target_pairs={{0,12},{4,8},{8,4},{12,0},{1,13},{5,9},{9,5},{13,1},{2,14},{6,10},... | collective-permute-start | bytes 442376 | tf_op jit(solution)/shard_map/ppermute | solution.py:42
  72.9 5.3 %collective-permute-start.18 = (bf16[2,4,24,384]{3,2,1,0:T(8,128)(2,1)S(1)}, bf16[2,4,24,384]{3,2,1,0:T(8,128)(2,1)S(1)}, u32[]{:S(2)}, u32[]{:S(2)}) collective-permute-start(bf16[2,4,24,384]{3,2,1,0:T(8,128)(2,1)S(1)} %get-tuple-element.131), channel_id=1, source_target_pairs={{0,96},{32,64},{64,32},{96,0},{1,97},{33,65},{65,33},{97,1},{2,98}... | collective-permute-start | bytes 442376 | tf_op jit(solution)/shard_map/ppermute | solution.py:42
  75.6 4.9 %collective-permute-start.21 = (bf16[4,24,384]{2,1,0:T(8,128)(2,1)S(1)}, bf16[4,24,384]{2,1,0:T(8,128)(2,1)S(1)}, u32[]{:S(2)}, u32[]{:S(2)}) collective-permute-start(bf16[4,24,384]{2,1,0:T(8,128)(2,1)S(1)} %get-tuple-element.140), channel_id=1, source_target_pairs={{0,96},{32,64},{64,32},{96,0},{1,97},{33,65},{65,33},{97,1},{2,98}... | collective-permute-start | bytes 221192 | tf_op jit(solution)/shard_map/ppermute | solution.py:42
  78.2 5.2 %collective-permute-start.22 = (bf16[4,24,384]{2,1,0:T(8,128)(2,1)S(1)}, bf16[4,24,384]{2,1,0:T(8,128)(2,1)S(1)}, u32[]{:S(2)}, u32[]{:S(2)}) collective-permute-start(bf16[4,24,384]{2,1,0:T(8,128)(2,1)S(1)} %get-tuple-element.143), channel_id=1, source_target_pairs={{0,32},{32,0},{64,96},{96,64},{1,33},{33,1},{65,97},{97,65},{2,34}... | collective-permute-start | bytes 221192 | tf_op jit(solution)/shard_map/ppermute | solution.py:42
  78.3 5.0 %collective-permute-start.20 = (bf16[4,24,384]{2,1,0:T(8,128)(2,1)S(1)}, bf16[4,24,384]{2,1,0:T(8,128)(2,1)S(1)}, u32[]{:S(2)}, u32[]{:S(2)}) collective-permute-start(bf16[4,24,384]{2,1,0:T(8,128)(2,1)S(1)} %get-tuple-element.146), channel_id=1, source_target_pairs={{0,4},{4,0},{8,12},{12,8},{1,5},{5,1},{9,13},{13,9},{2,6},{6,2},{1... | collective-permute-start | bytes 221192 | tf_op jit(solution)/shard_map/ppermute | solution.py:42
  78.8 4.6 %collective-permute-start.16 = (bf16[3,24,384]{2,1,0:T(8,128)(2,1)S(1)}, bf16[3,24,384]{2,1,0:T(8,128)(2,1)S(1)}, u32[]{:S(2)}, u32[]{:S(2)}) collective-permute-start(bf16[3,24,384]{2,1,0:T(8,128)(2,1)S(1)} %get-tuple-element.137), channel_id=1, source_target_pairs={{0,12},{4,8},{8,4},{12,0},{1,13},{5,9},{9,5},{13,1},{2,14},{6,10},... | collective-permute-start | bytes 165896 | tf_op jit(solution)/shard_map/ppermute | solution.py:42
  84.0 5.6 %collective-permute-start.23 = (bf16[8,24,384]{2,1,0:T(8,128)(2,1)S(1)}, bf16[8,24,384]{2,1,0:T(8,128)(2,1)S(1)}, u32[]{:S(2)}, u32[]{:S(2)}) collective-permute-start(bf16[8,24,384]{2,1,0:T(8,128)(2,1)S(1)} %get-tuple-element.155), channel_id=1, source_target_pairs={{0,16},{16,0},{1,17},{17,1},{2,18},{18,2},{3,19},{19,3},{4,20},{20... | collective-permute-start | bytes 442376 | tf_op jit(solution)/shard_map/ppermute | solution.py:37

commit v13 on v12

--- a/solution.py
+++ b/solution.py
@@ -488,15 +488,23 @@
         pairs((2, 4, 3), (2, 4, 4)),
         [pltpu.VMEM((16, 7, ROWS, COLS), F32)],
     )(place, slopes_own, slopes_arrived, belief_t, sibling_belief)
-    axes, turned, orders, swapped = (X, X, Y, Y), (Y, Y, X, X), (0, 1, 0, 1), (1, 0, 1, 0)
-    parts = (last_parts, middle_parts, first_parts[0:2], first_parts[2:4])
-    parts = [halve(part, 4) for part in exchange(parts, axes, orders)]
-    parts = [
-        turn(part, turned[i], orders[i]) for i, part in enumerate(exchange(parts, axes, swapped))
-    ]
-    parts = [halve(part) for part in exchange(parts, turned, orders)]
-    last_parts, middle_parts, *first_parts = exchange(parts, turned, swapped)
-    parts = (*first_parts[0], *first_parts[1], *last_parts, *middle_parts)
+    def in_turn(step, parts):
+        done = []
+        for i, (kept, arrived) in enumerate(parts):
+            if done:
+                arrived, _ = lax.optimization_barrier((arrived, done[-1][1]))
+            done.append(step(i, (kept, arrived)))
+        return done
+
+    axes, turned, orders, swapped = (X, X, Y, Y), (Y, Y, X, X), (0, 1, 1, 0), (1, 0, 0, 1)
+    parts = (last_parts, middle_parts, first_parts[2:4], first_parts[0:2])
+    parts = in_turn(lambda i, part: halve(part, 4), exchange(parts, axes, orders))
+    parts = in_turn(
+        lambda i, part: turn(part, turned[i], orders[i]), exchange(parts, axes, swapped)
+    )
+    parts = in_turn(lambda i, part: halve(part), exchange(parts, turned, orders))
+    last_parts, middle_parts, high_parts, low_parts = exchange(parts, turned, swapped)
+    parts = (*low_parts, *high_parts, *last_parts, *middle_parts)
     sent, own = call(
         z_cut_kernel,
         "z_cut",

time: 118 us -> 119 us (level)
  waiting for transfers between devices: 31.8 us -> 35.3 us
  blocking collectives: 27.5 us -> 24.9 us
    ppermute x16, waiting for transfers between devices: 15.3 us -> 18 us  [to_pair(): return lax.ppermute(shard, axis, pairs)]
    all_to_all x1, blocking collectives: 27.5 us -> 24.9 us  [per_device(): squares = lax.all_to_all(squares, ALL, 0, 0, tiled=True)]
where the time goes in v13:
time: 119 us
  waiting for transfers between devices  35.3 us (30%)
  starting transfers between devices  29.3 us (25%)
  Pallas kernels  27.4 us (23%)
  blocking collectives  24.9 us (21%)
  local copies, waits for them, and re-layouts  1.24 us (1%)
    pallas_call x23, Pallas kernels, run(): kernel(*(operand if spec is SMEM else pltpu.with_memory_space_constraint(...  27.4 us
    all_to_all x1, blocking collectives, per_device(): squares = lax.all_to_all(squares, ALL, 0, 0, tiled=True)  24.9 us
    ppermute x16, starting transfers between devices, to_pair(): return lax.ppermute(shard, axis, pairs)  19.6 us
    ppermute x16, waiting for transfers between devices, to_pair(): return lax.ppermute(shard, axis, pairs)  18 us
    ppermute x1, waiting for transfers between devices, per_device(): fetched = lax.ppermute(half, (ZH, 'mp'), [(0, 3), (3, 0), (1, 2), (2, 1)])  13.4 us
    ppermute x7, starting transfers between devices, swap(): return lax.ppermute(shard, axis, [(0, 1), (1, 0)])  5.03 us
    ppermute x1, starting transfers between devices, per_device(): fetched = lax.ppermute(half, (ZH, 'mp'), [(0, 3), (3, 0), (1, 2), (2, 1)])  4.67 us
    ppermute x7, waiting for transfers between devices, swap(): return lax.ppermute(shard, axis, [(0, 1), (1, 0)])  3.86 us
  transfers between devices with their start and end apart: 24, of which 9 were waited for; matrix products, arithmetic and copies ran while one was open for 0% of the time, Pallas kernels for 20%

profile of v13, /device:TPU:1, one launch (start us, length us, event | category | flops | bytes accessed | tf_op | source)
XLA Modules:
  0.0 118.9 jit_solution(3943979641660438652)
XLA Ops:
  0.6 0.1 stack.23.place_ref
  0.7 1.9 %half.1 = bf16[344,1536]{1,0:T(8,128)(2,1)S(1)} custom-call(s32[5]{0:T(128)S(1)} %stack.23.place_ref, bf16[663,1536]{1,0:T(8,128)(2,1)} %bitcast.13), custom_call_target="tpu_custom_call" | custom-call | flops 17179869184 | bytes 67108864 | tf_op jit(solution)/shard_map/half/pallas_call | solution.py:73
  2.6 4.7 %collective-permute-start.1 = (bf16[344,1536]{1,0:T(8,128)(2,1)S(1)}, bf16[344,1536]{1,0:T(8,128)(2,1)S(1)}, u32[]{:S(2)}, u32[]{:S(2)}) collective-permute-start(bf16[344,1536]{1,0:T(8,128)(2,1)S(1)} %half.1), channel_id=1, source_target_pairs={{0,17},{17,0},{1,16},{16,1},{2,19},{19,2},{3,18},{18,3},{4,21},{21... | collective-permute-start | bytes 3170312 | tf_op jit(solution)/shard_map/ppermute | solution.py:375
  7.3 5.1 %forward.1 = (f32[256,768]{1,0:T(8,128)}, bf16[256,768]{1,0:T(8,128)(2,1)}, bf16[256,1536]{1,0:T(8,128)(2,1)S(1)}) custom-call(bf16[2652,256]{1,0:T(8,128)(2,1)} %bitcast.10, bf16[2652,768]{1,0:T(8,128)(2,1)} %w_first_hbm.1, bf16[768,1536]{1,0:T(8,128)(2,1)} %w_middle_ref.1), custom_call_target="tpu_custom_call" | custom-call | flops 17179869184 | bytes 67108864 | tf_op jit(solution)/shard_map/forward/pallas_call | solution.py:73
  12.3 0.1 collective-permute-start
  12.4 1.0 collective-permute-start.4
  13.4 0.1 collective-permute-start.5
  13.5 1.1 copy-done.5
  14.6 2.4 %stage.1 = (bf16[663,1536]{1,0:T(8,128)(2,1)S(1)}, bf16[663,256]{1,0:T(8,128)(2,1)S(1)}, bf16[2,344,256]{2,1,0:T(8,128)(2,1)S(1)}, f32[256,768]{1,0:T(8,128)S(1)...) custom-call(s32[5]{0:T(128)S(1)} %stack.23.place_ref, s32[2]{0:T(128)S(1)} %copy-done.3, f32[256,768]{1,0:T(8,128)S(1)} %copy-done.5, ...), custom_call_target="tpu_custom_call" | custom-call | flops 17179869184 | bytes 67108864 | tf_op jit(solution)/shard_map/stage/pallas_call | solution.py:73
  17.0 13.4 %collective-permute-done.1.fetched_ref = bf16[344,1536]{1,0:T(8,128)(2,1)S(1)} collective-permute-done((bf16[344,1536]{1,0:T(8,128)(2,1)S(1)}, bf16[344,1536]{1,0:T(8,128)(2,1)S(1)}, u32[]{:S(2)}, u32[]{:S(2)}) %collective-permute-start.1) | collective-permute-done | bytes 1056800 | tf_op jit(solution)/shard_map/ppermute | solution.py:375
  30.4 1.1 collective-permute-start.2
  31.5 0.0 collective-permute-done.arrived_ref
  31.5 3.1 %hidden.1 = (bf16[256,1536]{1,0:T(8,128)(2,1)S(1)}, f32[256,1536]{1,0:T(8,128)S(1)}, f32[256,1536]{1,0:T(8,128)S(1)}, bf16[1431,256]{1,0:T(8,128)(2,1)S(1)}, bf16[768,256]{1,0:T(8,128)(2,1)S(1)}) custom-call(s32[5]{0:T(128)S(1)} %stack.23.place_ref, bf16[256,1536]{1,0:T(8,128)(2,1)S(1)} %get-tuple-element.92.partial_ref, ...), custom_call_target="tpu_custom_call" | custom-call | flops 17179869184 | bytes 67108864 | tf_op jit(solution)/shard_map/hidden/pallas_call | solution.py:73
  34.7 0.9 collective-permute-start.7
  35.6 0.0 collective-permute-done.2.relayed_ref
  35.6 4.9 %slopes.1 = (bf16[1152,256]{1,0:T(8,128)(2,1)S(1)}, bf16[1152,256]{1,0:T(8,128)(2,1)S(1)}) custom-call(s32[5]{0:T(128)S(1)} %stack.23.place_ref, bf16[256,1536]{1,0:T(8,128)(2,1)S(1)} %get-tuple-element.99.act_ref, f32[256,1536]{1,0:T(8,128)S(1)} %get-tuple-element.100.act_slope_ref, f32[256,1536]{1,0:T(8,128)S(1)} %get-tuple-element.101.back_ref, ...), custom_call_target="tpu_custom_call" | custom-call | flops 17179869184 | bytes 67108864 | tf_op jit(solution)/shard_map/slopes/pallas_call | solution.py:73
  40.5 0.1 collective-permute-start.3
  40.7 0.0 collective-permute-done.7.arrived_ref
  40.7 1.5 %last.1 = (f32[2,4,4,24,384]{4,3,2,1,0:T(8,128)S(1)}, bf16[2,4,4,24,384]{4,3,2,1,0:T(8,128)(2,1)S(1)}) custom-call(s32[5]{0:T(128)S(1)} %stack.23.place_ref, bf16[768,256]{1,0:T(8,128)(2,1)S(1)} %get-tuple-element.116.own_ref, bf16[1431,256]{1,0:T(8,128)(2,1)S(1)} %get-tuple-element.117.sent_ref, bf16[1431,256]{1,0:T(8,128)(2,1)S(1)} %collective-permute-done.7.arrived_ref), custom_call_target="tpu_custom_call" | custom-call | flops 17179869184 | bytes 67108864 | tf_op jit(solution)/shard_map/last/pallas_call | solution.py:73
  42.2 1.5 %collective-permute-start.10 = (bf16[2,4,4,24,384]{4,3,2,1,0:T(8,128)(2,1)S(1)}, bf16[2,4,4,24,384]{4,3,2,1,0:T(8,128)(2,1)S(1)}, u32[]{:S(2)}, u32[]{:S(2)}) collective-permute-start(bf16[2,4,4,24,384]{4,3,2,1,0:T(8,128)(2,1)S(1)} %get-tuple-element.118), channel_id=1, source_target_pairs={{0,4},{4,0},{8,12},{12,8},{1,5},{5,1},{9,13},{13,9},{2,6},{6,2},{1... | collective-permute-start | bytes 1769480 | tf_op jit(solution)/shard_map/ppermute | solution.py:42
  43.6 0.0 collective-permute-done.4.sibling_act_ref
  43.6 0.0 collective-permute-done.3.arrived_ref
  43.6 1.5 %middle.1 = (f32[2,4,4,24,384]{4,3,2,1,0:T(8,128)S(1)}, bf16[2,4,4,24,384]{4,3,2,1,0:T(8,128)(2,1)S(1)}) custom-call(s32[5]{0:T(128)S(1)} %stack.23.place_ref, bf16[1152,256]{1,0:T(8,128)(2,1)S(1)} %get-tuple-element.112.own_ref, bf16[1152,256]{1,0:T(8,128)(2,1)S(1)} %collective-permute-done.3.arrived_ref, bf16[256,768]{1,0:T(8,128)(2,1)S(1)} %copy-done.2, ...), custom_call_target="tpu_custom_call" | custom-call | flops 17179869184 | bytes 67108864 | tf_op jit(solution)/shard_map/middle/pallas_call | solution.py:73
  45.1 1.9 %collective-permute-start.9 = (bf16[2,4,4,24,384]{4,3,2,1,0:T(8,128)(2,1)S(1)}, bf16[2,4,4,24,384]{4,3,2,1,0:T(8,128)(2,1)S(1)}, u32[]{:S(2)}, u32[]{:S(2)}) collective-permute-start(bf16[2,4,4,24,384]{4,3,2,1,0:T(8,128)(2,1)S(1)} %get-tuple-element.111), channel_id=1, source_target_pairs={{0,12},{4,8},{8,4},{12,0},{1,13},{5,9},{9,5},{13,1},{2,14},{6,10},... | collective-permute-start | bytes 1769480 | tf_op jit(solution)/shard_map/ppermute | solution.py:42
  47.0 0.0 collective-permute-done.5.sibling_belief_ref
  47.0 2.4 %first.1 = (f32[2,4,3,24,384]{4,3,2,1,0:T(8,128)S(1)}, bf16[2,4,3,24,384]{4,3,2,1,0:T(8,128)(2,1)S(1)}, f32[2,4,4,24,384]{4,3,2,1,0:T(8,128)S(1)}, bf16[2,4,4,24,384]{4,3,2,1,0:T(8,128)(2,1)S(1)}) custom-call(s32[5]{0:T(128)S(1)} %stack.23.place_ref, bf16[1152,256]{1,0:T(8,128)(2,1)S(1)} %get-tuple-element.112.own_ref, ...), custom_call_target="tpu_custom_call" | custom-call | flops 17179869184 | bytes 67108864 | tf_op jit(solution)/shard_map/first/pallas_call | solution.py:73
  49.4 2.8 %collective-permute-start.8 = (bf16[2,4,4,24,384]{4,3,2,1,0:T(8,128)(2,1)S(1)}, bf16[2,4,4,24,384]{4,3,2,1,0:T(8,128)(2,1)S(1)}, u32[]{:S(2)}, u32[]{:S(2)}) collective-permute-start(bf16[2,4,4,24,384]{4,3,2,1,0:T(8,128)(2,1)S(1)} %get-tuple-element.119), channel_id=1, source_target_pairs={{0,96},{32,64},{64,32},{96,0},{1,97},{33,65},{65,33},{97,1},{2,98}... | collective-permute-start | bytes 1769480 | tf_op jit(solution)/shard_map/ppermute | solution.py:42
  52.2 0.0 collective-permute-start.6
  52.2 4.6 %collective-permute-done.10.arrived_ref = bf16[2,4,4,24,384]{4,3,2,1,0:T(8,128)(2,1)S(1)} collective-permute-done((bf16[2,4,4,24,384]{4,3,2,1,0:T(8,128)(2,1)S(1)}, bf16[2,4,4,24,384]{4,3,2,1,0:T(8,128)(2,1)S(1)}, u32[]{:S(2)}, u32[]{:S(2)}) %collective-permute-start.10) | collective-permute-done | bytes 589856 | tf_op jit(solution)/shard_map/ppermute | solution.py:42
  56.8 0.1 halve.8
  56.9 2.6 %collective-permute-start.14 = (bf16[4,4,24,384]{3,2,1,0:T(8,128)(2,1)S(1)}, bf16[4,4,24,384]{3,2,1,0:T(8,128)(2,1)S(1)}, u32[]{:S(2)}, u32[]{:S(2)}) collective-permute-start(bf16[4,4,24,384]{3,2,1,0:T(8,128)(2,1)S(1)} %get-tuple-element.127), channel_id=1, source_target_pairs={{0,12},{4,8},{8,4},{12,0},{1,13},{5,9},{9,5},{13,1},{2,14},{6,10},... | collective-permute-start | bytes 884744 | tf_op jit(solution)/shard_map/ppermute | solution.py:42
  59.5 3.0 %collective-permute-done.6.arrived_ref = bf16[2,4,3,24,384]{4,3,2,1,0:T(8,128)(2,1)S(1)} collective-permute-done((bf16[2,4,3,24,384]{4,3,2,1,0:T(8,128)(2,1)S(1)}, bf16[2,4,3,24,384]{4,3,2,1,0:T(8,128)(2,1)S(1)}, u32[]{:S(2)}, u32[]{:S(2)}) %collective-permute-start.6) | collective-permute-done | bytes 442400 | tf_op jit(solution)/shard_map/ppermute | solution.py:42
  62.5 0.0 collective-permute-done.9.arrived_ref
  62.5 2.0 %collective-permute-done.8.arrived_ref = bf16[2,4,4,24,384]{4,3,2,1,0:T(8,128)(2,1)S(1)} collective-permute-done((bf16[2,4,4,24,384]{4,3,2,1,0:T(8,128)(2,1)S(1)}, bf16[2,4,4,24,384]{4,3,2,1,0:T(8,128)(2,1)S(1)}, u32[]{:S(2)}, u32[]{:S(2)}) %collective-permute-start.8) | collective-permute-done | bytes 589856 | tf_op jit(solution)/shard_map/ppermute | solution.py:42
  64.6 0.1 halve.9
  64.7 0.4 collective-permute-start.13
  65.1 0.1 halve.10
  65.2 0.1 collective-permute-start.12
  65.3 0.1 halve.11
  65.4 2.7 %collective-permute-start.11 = (bf16[4,3,24,384]{3,2,1,0:T(8,128)(2,1)S(1)}, bf16[4,3,24,384]{3,2,1,0:T(8,128)(2,1)S(1)}, u32[]{:S(2)}, u32[]{:S(2)}) collective-permute-start(bf16[4,3,24,384]{3,2,1,0:T(8,128)(2,1)S(1)} %get-tuple-element.134), channel_id=1, source_target_pairs={{0,96},{32,64},{64,32},{96,0},{1,97},{33,65},{65,33},{97,1},{2,98}... | collective-permute-start | bytes 663560 | tf_op jit(solution)/shard_map/ppermute | solution.py:42
  68.1 0.0 collective-permute-done.14.arrived_ref
  68.1 0.6 turn.4
  68.7 0.9 collective-permute-start.18
  69.6 1.9 %collective-permute-done.11.arrived_ref = bf16[4,3,24,384]{3,2,1,0:T(8,128)(2,1)S(1)} collective-permute-done((bf16[4,3,24,384]{3,2,1,0:T(8,128)(2,1)S(1)}, bf16[4,3,24,384]{3,2,1,0:T(8,128)(2,1)S(1)}, u32[]{:S(2)}, u32[]{:S(2)}) %collective-permute-start.11) | collective-permute-done | bytes 221216 | tf_op jit(solution)/shard_map/ppermute | solution.py:42
  71.5 0.1 collective-permute-done.12.arrived_ref
  71.6 0.6 turn.5
  72.3 2.6 %collective-permute-start.17 = (bf16[2,4,24,384]{3,2,1,0:T(8,128)(2,1)S(1)}, bf16[2,4,24,384]{3,2,1,0:T(8,128)(2,1)S(1)}, u32[]{:S(2)}, u32[]{:S(2)}) collective-permute-start(bf16[2,4,24,384]{3,2,1,0:T(8,128)(2,1)S(1)} %get-tuple-element.144), channel_id=1, source_target_pairs={{0,96},{32,64},{64,32},{96,0},{1,97},{33,65},{65,33},{97,1},{2,98}... | collective-permute-start | bytes 442376 | tf_op jit(solution)/shard_map/ppermute | solution.py:42
  74.9 0.6 turn.6
  75.5 1.3 %collective-permute-start.16 = (bf16[2,4,24,384]{3,2,1,0:T(8,128)(2,1)S(1)}, bf16[2,4,24,384]{3,2,1,0:T(8,128)(2,1)S(1)}, u32[]{:S(2)}, u32[]{:S(2)}) collective-permute-start(bf16[2,4,24,384]{3,2,1,0:T(8,128)(2,1)S(1)} %get-tuple-element.146), channel_id=1, source_target_pairs={{0,12},{4,8},{8,4},{12,0},{1,13},{5,9},{9,5},{13,1},{2,14},{6,10},... | collective-permute-start | bytes 442376 | tf_op jit(solution)/shard_map/ppermute | solution.py:42
  76.8 0.6 turn.7
  77.4 0.2 collective-permute-start.15
  77.7 0.2 collective-permute-start.21
  77.9 3.2 %collective-permute-done.15.arrived_ref = bf16[2,3,24,384]{3,2,1,0:T(8,128)(2,1)S(1)} collective-permute-done((bf16[2,3,24,384]{3,2,1,0:T(8,128)(2,1)S(1)}, bf16[2,3,24,384]{3,2,1,0:T(8,128)(2,1)S(1)}, u32[]{:S(2)}, u32[]{:S(2)}) %collective-permute-start.15) | collective-permute-done | bytes 110624 | tf_op jit(solution)/shard_map/ppermute | solution.py:42
  81.1 0.1 collective-permute-start.22
  81.3 0.2 collective-permute-start.20
  81.5 2.0 %collective-permute-start.19 = (bf16[3,24,384]{2,1,0:T(8,128)(2,1)S(1)}, bf16[3,24,384]{2,1,0:T(8,128)(2,1)S(1)}, u32[]{:S(2)}, u32[]{:S(2)}) collective-permute-start(bf16[3,24,384]{2,1,0:T(8,128)(2,1)S(1)} %get-tuple-element.164), channel_id=1, source_target_pairs={{0,12},{4,8},{8,4},{12,0},{1,13},{5,9},{9,5},{13,1},{2,14},{6,10},... | collective-permute-start | bytes 165896 | tf_op jit(solution)/shard_map/ppermute | solution.py:42
  83.6 0.0 collective-permute-done.21.refs_5_
  83.6 3.1 %collective-permute-done.19.refs_1_ = bf16[3,24,384]{2,1,0:T(8,128)(2,1)S(1)} collective-permute-done((bf16[3,24,384]{2,1,0:T(8,128)(2,1)S(1)}, bf16[3,24,384]{2,1,0:T(8,128)(2,1)S(1)}, u32[]{:S(2)}, u32[]{:S(2)}) %collective-permute-start.19) | collective-permute-done | bytes 55328 | tf_op jit(solution)/shard_map/ppermute | solution.py:42
  86.7 0.6 z_cut.1
  87.3 1.7 %collective-permute-start.23 = (bf16[8,24,384]{2,1,0:T(8,128)(2,1)S(1)}, bf16[8,24,384]{2,1,0:T(8,128)(2,1)S(1)}, u32[]{:S(2)}, u32[]{:S(2)}) collective-permute-start(bf16[8,24,384]{2,1,0:T(8,128)(2,1)S(1)} %get-tuple-element.173), channel_id=1, source_target_pairs={{0,16},{16,0},{1,17},{17,1},{2,18},{18,2},{3,19},{19,3},{4,20},{20... | collective-permute-start | bytes 442376 | tf_op jit(solution)/shard_map/ppermute | solution.py:37
  89.1 3.8 %collective-permute-done.23.arrived_ref = bf16[8,24,384]{2,1,0:T(8,128)(2,1)S(1)} collective-permute-done((bf16[8,24,384]{2,1,0:T(8,128)(2,1)S(1)}, bf16[8,24,384]{2,1,0:T(8,128)(2,1)S(1)}, u32[]{:S(2)}, u32[]{:S(2)}) %collective-permute-start.23) | collective-permute-done | bytes 147488 | tf_op jit(solution)/shard_map/ppermute | solution.py:37
  92.9 0.3 square.1
  93.2 24.9 %all_to_all.5.squares_ref = f32[128,1,128]{2,1,0:T(1,128)S(1)} all-to-all(f32[128,1,128]{2,1,0:T(1,128)S(1)} %get-tuple-element.175), channel_id=1, replica_groups=mesh['dp_0'=4,'dp_1'=2,'dp_2'=4,'dp_3'=2,'mp'=2] {'dp_0','dp_1','dp_2','..., dimensions={0} | all-to-all | bytes 131072 | tf_op jit(solution)/shard_map/all_to_all | solution.py:519
  118.0 0.9 scale.1
  (21 shorter events, 0.2 us)
Async XLA Ops:
  2.6 27.8 %collective-permute-start.1 = (bf16[344,1536]{1,0:T(8,128)(2,1)S(1)}, bf16[344,1536]{1,0:T(8,128)(2,1)S(1)}, u32[]{:S(2)}, u32[]{:S(2)}) collective-permute-start(bf16[344,1536]{1,0:T(8,128)(2,1)S(1)} %half.1), channel_id=1, source_target_pairs={{0,17},{17,0},{1,16},{16,1},{2,19},{19,2},{3,18},{18,3},{4,21},{21... | collective-permute-start | bytes 3170312 | tf_op jit(solution)/shard_map/ppermute | solution.py:375
  7.3 6.1 %copy-start.1 = (bf16[256,2652]{0,1:T(8,128)(2,1)S(1)}, bf16[256,2652]{0,1:T(8,128)(2,1)}, u32[]{:S(2)}) copy-start(bf16[256,2652]{0,1:T(8,128)(2,1)} %param.7) | copy-start | bytes 4073476
  7.3 6.2 %copy-start.3 = (s32[2]{0:T(128)S(1)}, s32[2]{0:T(128)}, u32[]{:S(2)}) copy-start(s32[2]{0:T(128)} %counts_ref.1) | copy-start | bytes 28
  7.3 6.2 %copy-start.4 = (s32[2,768,1]{2,1,0:T(8,128)S(1)}, s32[2,768,1]{2,1,0:T(8,128)}, u32[]{:S(2)}) copy-start(s32[2,768,1]{2,1,0:T(8,128)} %constant.21.clone.orders_ref) | copy-start | bytes 18436
  12.3 19.2 %collective-permute-start = (bf16[256,1536]{1,0:T(8,128)(2,1)S(1)}, bf16[256,1536]{1,0:T(8,128)(2,1)S(1)}, u32[]{:S(2)}, u32[]{:S(2)}) collective-permute-start(bf16[256,1536]{1,0:T(8,128)(2,1)S(1)} %get-tuple-element.92.partial_ref), channel_id=1, source_target_pairs={{0,1},{1,0},{2,3},{3,2},{4,5},{5,4},{6,7},{7,6},{8,9},{9,8},{10,11... | collective-permute-start | bytes 2359304 | tf_op jit(solution)/shard_map/ppermute | solution.py:37
  12.4 31.2 %collective-permute-start.4 = (bf16[256,768]{1,0:T(8,128)(2,1)}, bf16[256,768]{1,0:T(8,128)(2,1)S(1)}, u32[]{:S(2)}, u32[]{:S(2)}) collective-permute-start(bf16[256,768]{1,0:T(8,128)(2,1)} %get-tuple-element.110.act_ref), channel_id=1, source_target_pairs={{0,2},{2,0},{1,3},{3,1},{4,6},{6,4},{5,7},{7,5},{8,10},{10,8},{9,1... | collective-permute-start | bytes 1179656 | tf_op jit(solution)/shard_map/ppermute | solution.py:37
  13.4 33.6 %collective-permute-start.5 = (bf16[2652,256]{1,0:T(8,128)(2,1)S(1)}, bf16[2652,256]{1,0:T(8,128)(2,1)S(1)}, u32[]{:S(2)}, u32[]{:S(2)}) collective-permute-start(bf16[2652,256]{1,0:T(8,128)(2,1)S(1)} %bitcast.11), channel_id=1, source_target_pairs={{0,2},{2,0},{1,3},{3,1},{4,6},{6,4},{5,7},{7,5},{8,10},{10,8},{9,1... | collective-permute-start | bytes 4073480 | tf_op jit(solution)/shard_map/ppermute | solution.py:37
  13.5 1.1 copy-start.5
  30.4 5.2 %collective-permute-start.2 = (bf16[344,1536]{1,0:T(8,128)(2,1)S(1)}, bf16[344,1536]{1,0:T(8,128)(2,1)S(1)}, u32[]{:S(2)}, u32[]{:S(2)}) collective-permute-start(bf16[344,1536]{1,0:T(8,128)(2,1)S(1)} %collective-permute-done.1.fetched_ref), channel_id=1, source_target_pairs={{0,2},{2,0},{1,3},{3,1},{4,6},{6,4},{5,7},{7,5},{8,10},{10,8},{9,1... | collective-permute-start | bytes 3170312 | tf_op jit(solution)/shard_map/ppermute | solution.py:37
  31.5 4.0 %copy-start = (bf16[768,1536]{1,0:T(8,128)(2,1)S(1)}, bf16[768,1536]{1,0:T(8,128)(2,1)}, u32[]{:S(2)}) copy-start(bf16[768,1536]{1,0:T(8,128)(2,1)} %w_middle_ref.1) | copy-start | bytes 7077892
  34.7 6.0 %collective-permute-start.7 = (bf16[1431,256]{1,0:T(8,128)(2,1)S(1)}, bf16[1431,256]{1,0:T(8,128)(2,1)S(1)}, u32[]{:S(2)}, u32[]{:S(2)}) collective-permute-start(bf16[1431,256]{1,0:T(8,128)(2,1)S(1)} %get-tuple-element.117.sent_ref), channel_id=1, source_target_pairs={{0,2},{2,0},{1,3},{3,1},{4,6},{6,4},{5,7},{7,5},{8,10},{10,8},{9,1... | collective-permute-start | bytes 2198024 | tf_op jit(solution)/shard_map/ppermute | solution.py:37
  40.5 3.1 %copy-start.2 = (bf16[256,768]{1,0:T(8,128)(2,1)S(1)}, bf16[256,768]{1,0:T(8,128)(2,1)}, u32[]{:S(2)}) copy-start(bf16[256,768]{1,0:T(8,128)(2,1)} %get-tuple-element.110.act_ref) | copy-start | bytes 1179652
  40.5 3.1 %collective-permute-start.3 = (bf16[1152,256]{1,0:T(8,128)(2,1)S(1)}, bf16[1152,256]{1,0:T(8,128)(2,1)S(1)}, u32[]{:S(2)}, u32[]{:S(2)}) collective-permute-start(bf16[1152,256]{1,0:T(8,128)(2,1)S(1)} %get-tuple-element.108), channel_id=1, source_target_pairs={{0,2},{2,0},{1,3},{3,1},{4,6},{6,4},{5,7},{7,5},{8,10},{10,8},{9,1... | collective-permute-start | bytes 1769480 | tf_op jit(solution)/shard_map/ppermute | solution.py:37
  42.2 14.7 %collective-permute-start.10 = (bf16[2,4,4,24,384]{4,3,2,1,0:T(8,128)(2,1)S(1)}, bf16[2,4,4,24,384]{4,3,2,1,0:T(8,128)(2,1)S(1)}, u32[]{:S(2)}, u32[]{:S(2)}) collective-permute-start(bf16[2,4,4,24,384]{4,3,2,1,0:T(8,128)(2,1)S(1)} %get-tuple-element.118), channel_id=1, source_target_pairs={{0,4},{4,0},{8,12},{12,8},{1,5},{5,1},{9,13},{13,9},{2,6},{6,2},{1... | collective-permute-start | bytes 1769480 | tf_op jit(solution)/shard_map/ppermute | solution.py:42
  45.1 17.4 %collective-permute-start.9 = (bf16[2,4,4,24,384]{4,3,2,1,0:T(8,128)(2,1)S(1)}, bf16[2,4,4,24,384]{4,3,2,1,0:T(8,128)(2,1)S(1)}, u32[]{:S(2)}, u32[]{:S(2)}) collective-permute-start(bf16[2,4,4,24,384]{4,3,2,1,0:T(8,128)(2,1)S(1)} %get-tuple-element.111), channel_id=1, source_target_pairs={{0,12},{4,8},{8,4},{12,0},{1,13},{5,9},{9,5},{13,1},{2,14},{6,10},... | collective-permute-start | bytes 1769480 | tf_op jit(solution)/shard_map/ppermute | solution.py:42
  49.4 15.2 %collective-permute-start.8 = (bf16[2,4,4,24,384]{4,3,2,1,0:T(8,128)(2,1)S(1)}, bf16[2,4,4,24,384]{4,3,2,1,0:T(8,128)(2,1)S(1)}, u32[]{:S(2)}, u32[]{:S(2)}) collective-permute-start(bf16[2,4,4,24,384]{4,3,2,1,0:T(8,128)(2,1)S(1)} %get-tuple-element.119), channel_id=1, source_target_pairs={{0,96},{32,64},{64,32},{96,0},{1,97},{33,65},{65,33},{97,1},{2,98}... | collective-permute-start | bytes 1769480 | tf_op jit(solution)/shard_map/ppermute | solution.py:42
  52.2 10.3 %collective-permute-start.6 = (bf16[2,4,3,24,384]{4,3,2,1,0:T(8,128)(2,1)S(1)}, bf16[2,4,3,24,384]{4,3,2,1,0:T(8,128)(2,1)S(1)}, u32[]{:S(2)}, u32[]{:S(2)}) collective-permute-start(bf16[2,4,3,24,384]{4,3,2,1,0:T(8,128)(2,1)S(1)} %get-tuple-element.115), channel_id=1, source_target_pairs={{0,32},{32,0},{64,96},{96,64},{1,33},{33,1},{65,97},{97,65},{2,34}... | collective-permute-start | bytes 1327112 | tf_op jit(solution)/shard_map/ppermute | solution.py:42
  56.9 11.2 %collective-permute-start.14 = (bf16[4,4,24,384]{3,2,1,0:T(8,128)(2,1)S(1)}, bf16[4,4,24,384]{3,2,1,0:T(8,128)(2,1)S(1)}, u32[]{:S(2)}, u32[]{:S(2)}) collective-permute-start(bf16[4,4,24,384]{3,2,1,0:T(8,128)(2,1)S(1)} %get-tuple-element.127), channel_id=1, source_target_pairs={{0,12},{4,8},{8,4},{12,0},{1,13},{5,9},{9,5},{13,1},{2,14},{6,10},... | collective-permute-start | bytes 884744 | tf_op jit(solution)/shard_map/ppermute | solution.py:42
  64.7 6.8 %collective-permute-start.13 = (bf16[4,4,24,384]{3,2,1,0:T(8,128)(2,1)S(1)}, bf16[4,4,24,384]{3,2,1,0:T(8,128)(2,1)S(1)}, u32[]{:S(2)}, u32[]{:S(2)}) collective-permute-start(bf16[4,4,24,384]{3,2,1,0:T(8,128)(2,1)S(1)} %get-tuple-element.129), channel_id=1, source_target_pairs={{0,4},{4,0},{8,12},{12,8},{1,5},{5,1},{9,13},{13,9},{2,6},{6,2},{1... | collective-permute-start | bytes 884744 | tf_op jit(solution)/shard_map/ppermute | solution.py:42
  65.2 6.4 %collective-permute-start.12 = (bf16[4,4,24,384]{3,2,1,0:T(8,128)(2,1)S(1)}, bf16[4,4,24,384]{3,2,1,0:T(8,128)(2,1)S(1)}, u32[]{:S(2)}, u32[]{:S(2)}) collective-permute-start(bf16[4,4,24,384]{3,2,1,0:T(8,128)(2,1)S(1)} %get-tuple-element.131), channel_id=1, source_target_pairs={{0,32},{32,0},{64,96},{96,64},{1,33},{33,1},{65,97},{97,65},{2,34}... | collective-permute-start | bytes 884744 | tf_op jit(solution)/shard_map/ppermute | solution.py:42
  65.4 6.1 %collective-permute-start.11 = (bf16[4,3,24,384]{3,2,1,0:T(8,128)(2,1)S(1)}, bf16[4,3,24,384]{3,2,1,0:T(8,128)(2,1)S(1)}, u32[]{:S(2)}, u32[]{:S(2)}) collective-permute-start(bf16[4,3,24,384]{3,2,1,0:T(8,128)(2,1)S(1)} %get-tuple-element.134), channel_id=1, source_target_pairs={{0,96},{32,64},{64,32},{96,0},{1,97},{33,65},{65,33},{97,1},{2,98}... | collective-permute-start | bytes 663560 | tf_op jit(solution)/shard_map/ppermute | solution.py:42
  68.7 8.9 %collective-permute-start.18 = (bf16[2,4,24,384]{3,2,1,0:T(8,128)(2,1)S(1)}, bf16[2,4,24,384]{3,2,1,0:T(8,128)(2,1)S(1)}, u32[]{:S(2)}, u32[]{:S(2)}) collective-permute-start(bf16[2,4,24,384]{3,2,1,0:T(8,128)(2,1)S(1)} %get-tuple-element.142), channel_id=1, source_target_pairs={{0,32},{32,0},{64,96},{96,64},{1,33},{33,1},{65,97},{97,65},{2,34}... | collective-permute-start | bytes 442376 | tf_op jit(solution)/shard_map/ppermute | solution.py:42
  72.3 8.8 %collective-permute-start.17 = (bf16[2,4,24,384]{3,2,1,0:T(8,128)(2,1)S(1)}, bf16[2,4,24,384]{3,2,1,0:T(8,128)(2,1)S(1)}, u32[]{:S(2)}, u32[]{:S(2)}) collective-permute-start(bf16[2,4,24,384]{3,2,1,0:T(8,128)(2,1)S(1)} %get-tuple-element.144), channel_id=1, source_target_pairs={{0,96},{32,64},{64,32},{96,0},{1,97},{33,65},{65,33},{97,1},{2,98}... | collective-permute-start | bytes 442376 | tf_op jit(solution)/shard_map/ppermute | solution.py:42
  75.5 5.6 %collective-permute-start.16 = (bf16[2,4,24,384]{3,2,1,0:T(8,128)(2,1)S(1)}, bf16[2,4,24,384]{3,2,1,0:T(8,128)(2,1)S(1)}, u32[]{:S(2)}, u32[]{:S(2)}) collective-permute-start(bf16[2,4,24,384]{3,2,1,0:T(8,128)(2,1)S(1)} %get-tuple-element.146), channel_id=1, source_target_pairs={{0,12},{4,8},{8,4},{12,0},{1,13},{5,9},{9,5},{13,1},{2,14},{6,10},... | collective-permute-start | bytes 442376 | tf_op jit(solution)/shard_map/ppermute | solution.py:42
  77.4 3.7 %collective-permute-start.15 = (bf16[2,3,24,384]{3,2,1,0:T(8,128)(2,1)S(1)}, bf16[2,3,24,384]{3,2,1,0:T(8,128)(2,1)S(1)}, u32[]{:S(2)}, u32[]{:S(2)}) collective-permute-start(bf16[2,3,24,384]{3,2,1,0:T(8,128)(2,1)S(1)} %get-tuple-element.149), channel_id=1, source_target_pairs={{0,4},{4,0},{8,12},{12,8},{1,5},{5,1},{9,13},{13,9},{2,6},{6,2},{1... | collective-permute-start | bytes 331784 | tf_op jit(solution)/shard_map/ppermute | solution.py:42
  77.7 5.9 %collective-permute-start.21 = (bf16[4,24,384]{2,1,0:T(8,128)(2,1)S(1)}, bf16[4,24,384]{2,1,0:T(8,128)(2,1)S(1)}, u32[]{:S(2)}, u32[]{:S(2)}) collective-permute-start(bf16[4,24,384]{2,1,0:T(8,128)(2,1)S(1)} %get-tuple-element.157), channel_id=1, source_target_pairs={{0,96},{32,64},{64,32},{96,0},{1,97},{33,65},{65,33},{97,1},{2,98}... | collective-permute-start | bytes 221192 | tf_op jit(solution)/shard_map/ppermute | solution.py:42
  81.1 5.5 %collective-permute-start.22 = (bf16[4,24,384]{2,1,0:T(8,128)(2,1)S(1)}, bf16[4,24,384]{2,1,0:T(8,128)(2,1)S(1)}, u32[]{:S(2)}, u32[]{:S(2)}) collective-permute-start(bf16[4,24,384]{2,1,0:T(8,128)(2,1)S(1)} %get-tuple-element.159), channel_id=1, source_target_pairs={{0,32},{32,0},{64,96},{96,64},{1,33},{33,1},{65,97},{97,65},{2,34}... | collective-permute-start | bytes 221192 | tf_op jit(solution)/shard_map/ppermute | solution.py:42
  81.3 5.4 %collective-permute-start.20 = (bf16[4,24,384]{2,1,0:T(8,128)(2,1)S(1)}, bf16[4,24,384]{2,1,0:T(8,128)(2,1)S(1)}, u32[]{:S(2)}, u32[]{:S(2)}) collective-permute-start(bf16[4,24,384]{2,1,0:T(8,128)(2,1)S(1)} %get-tuple-element.161), channel_id=1, source_target_pairs={{0,4},{4,0},{8,12},{12,8},{1,5},{5,1},{9,13},{13,9},{2,6},{6,2},{1... | collective-permute-start | bytes 221192 | tf_op jit(solution)/shard_map/ppermute | solution.py:42
  81.5 5.1 %collective-permute-start.19 = (bf16[3,24,384]{2,1,0:T(8,128)(2,1)S(1)}, bf16[3,24,384]{2,1,0:T(8,128)(2,1)S(1)}, u32[]{:S(2)}, u32[]{:S(2)}) collective-permute-start(bf16[3,24,384]{2,1,0:T(8,128)(2,1)S(1)} %get-tuple-element.164), channel_id=1, source_target_pairs={{0,12},{4,8},{8,4},{12,0},{1,13},{5,9},{9,5},{13,1},{2,14},{6,10},... | collective-permute-start | bytes 165896 | tf_op jit(solution)/shard_map/ppermute | solution.py:42
  87.3 5.6 %collective-permute-start.23 = (bf16[8,24,384]{2,1,0:T(8,128)(2,1)S(1)}, bf16[8,24,384]{2,1,0:T(8,128)(2,1)S(1)}, u32[]{:S(2)}, u32[]{:S(2)}) collective-permute-start(bf16[8,24,384]{2,1,0:T(8,128)(2,1)S(1)} %get-tuple-element.173), channel_id=1, source_target_pairs={{0,16},{16,0},{1,17},{17,1},{2,18},{18,2},{3,19},{19,3},{4,20},{20... | collective-permute-start | bytes 442376 | tf_op jit(solution)/shard_map/ppermute | solution.py:37

commit v14 on v11

--- a/solution.py
+++ b/solution.py
@@ -17,7 +17,7 @@
 Y, ZH, X, CORE = DP
 LANES = 128
 ROWS, COLS = 24, 384
-SIZE, SECOND = 344, 320
+SIZE, SECOND = 336, 328
 DEPTH = 512
 VMEM = pl.BlockSpec(memory_space=pltpu.VMEM)
 SMEM = pl.BlockSpec(memory_space=pltpu.SMEM)
@@ -148,8 +148,8 @@
 
 
 def stage_kernel(
-    place_ref, counts_ref, pre_first_ref, orders_ref, target_hbm, w_last_hbm,
-    w_own_ref, target_own_ref, target_other_ref, first_slope_ref, onehot_ref, live_ref,
+    place_ref, counts_ref, pre_first_ref, orders_ref, w_middle_ref, target_hbm, w_last_hbm,
+    w_own_ref, target_own_ref, target_other_ref, first_slope_ref, w_sorted_ref, live_ref,
     target_ref, sems,
 ):
     copies = (
@@ -158,10 +158,17 @@
     )
     for copy in copies:
         copy.start()
-    first_slope_ref[...] = silu_slope(pre_first_ref[...])
     order = jnp.where(place_ref[0] == 0, orders_ref[0], orders_ref[1])
-    units = lax.broadcasted_iota(jnp.int32, onehot_ref.shape, 1)
-    onehot_ref[...] = jnp.where(order == units, 1.0, 0.0).astype(BF16)
+    units = lax.broadcasted_iota(jnp.int32, (order.shape[0], order.shape[0]), 1)
+    onehot = jnp.where(order == units, 1.0, 0.0)
+    w_sorted_ref[...] = narrow(dot(narrow(onehot), w_middle_ref[...]))
+    first_slope_ref[...] = lax.dot_general(
+        onehot,
+        silu_slope(pre_first_ref[...]),
+        (((1,), (1,)), ((), ())),
+        precision=lax.Precision.HIGHEST,
+        preferred_element_type=F32,
+    )
     row = lax.broadcasted_iota(jnp.int32, live_ref.shape, 1)
     count = jnp.where(row < BLOCK, counts_ref[0], counts_ref[1] + BLOCK)
     live_ref[...] = jnp.where(row < count, 1.0, 0.0)
@@ -209,7 +216,7 @@
 
 def slopes_kernel(
     place_ref, act_ref, act_slope_ref, back_ref, live_ref, target_ref, first_slope_ref,
-    onehot_ref, fetched_ref, relayed_ref, w_middle_ref, sent_ref, own_ref, rows_ref,
+    fetched_ref, relayed_ref, w_sorted_ref, sent_ref, own_ref, rows_ref,
 ):
     core = place_ref[0]
     act, live = act_ref[...], live_ref[...]
@@ -222,8 +229,7 @@
         slope = jnp.where(column >= repeated, slope, jnp.zeros_like(slope))
         back += contract(slope, weights, 0, 0)
     slope_middle = narrow(back * act_slope_ref[...])
-    slope_first = narrow(contract(slope_middle, w_middle_ref[...], 1, 1) * first_slope_ref[...])
-    slope_first = narrow(contract(onehot_ref[...], slope_first, 1, 1))
+    slope_first = narrow(contract(w_sorted_ref[...], slope_middle, 1, 1) * first_slope_ref[...])
     half = slope_first.shape[0] // 2
     sent_ref[2 * half :, :] = slope_first[:half]
     own_ref[2 * half :, :] = slope_first[half:]
@@ -398,20 +404,20 @@
 
     order = np.arange(units, dtype=np.int32).reshape(4, 2, 4, 2, -1).transpose(3, 0, 2, 1, 4)
     orders = np.stack([order[::-1], order]).reshape(2, units, 1)
-    w_own, target_own, target_other, first_slope, onehot, live = call(
+    w_own, target_own, target_other, first_slope, w_sorted, live = call(
         stage_kernel,
         "stage",
-        [SMEM, SMEM, VMEM, VMEM, HBM, HBM],
+        [SMEM, SMEM, VMEM, VMEM, VMEM, HBM, HBM],
         [
             ((width, hidden), BF16),
             ((width, total_rows), BF16),
             ((2, SIZE, total_rows), BF16),
-            ((total_rows, units), F32),
-            ((units, units), BF16),
+            ((units, total_rows), F32),
+            ((units, hidden), BF16),
             ((1, total_rows), F32),
         ],
         [pltpu.VMEM((2 * width, total_rows), BF16), pltpu.SemaphoreType.DMA((2,))],
-    )(place, counts, pre_first, jnp.asarray(orders), target_value.T, w_last_t)
+    )(place, counts, pre_first, jnp.asarray(orders), w_middle, target_value.T, w_last_t)
     fetched, live = lax.optimization_barrier((fetched, live))
     relayed = swap(fetched, CORE)
     belief_swapped, act_swapped = lax.optimization_barrier((belief_t, act_first))
@@ -436,12 +442,12 @@
     slopes_sent, slopes_own = call(
         slopes_kernel,
         "slopes",
-        [SMEM] + [VMEM] * 10,
+        [SMEM] + [VMEM] * 9,
         [((hidden // 2 + units // 2, total_rows), BF16)] * 2,
         [pltpu.VMEM((hidden, total_rows), F32)],
     )(
-        place, act, act_slope, back_own, live, target_other, first_slope, onehot,
-        fetched, relayed, w_middle,
+        place, act, act_slope, back_own, live, target_other, first_slope,
+        fetched, relayed, w_sorted,
     )
     slopes_arrived = swap(slopes_sent, CORE)
 

time: 117 us -> 116 us (level)
  waiting for transfers between devices: 38.4 us -> 36 us
  Pallas kernels: 27.5 us -> 29.3 us
    ppermute x1, waiting for transfers between devices: 13.4 us -> 10.3 us  [per_device(): fetched = lax.ppermute(half, (ZH, 'mp'), [(0, 3), (3, 0), (1, 2), (2, 1)])]
    pallas_call x23, Pallas kernels: 27.5 us -> 29.3 us  [run(): kernel(*(operand if spec is SMEM else pltpu.with_memory_space_constraint(...]
  transfers between devices with their start and end apart: 24 -> 24, of which waited for: 11 -> 11; matrix products, arithmetic and copies ran while one was open for 0% -> 0% of each run, Pallas kernels for 20% -> 22%
where the time goes in v14:
time: 116 us
  waiting for transfers between devices  36 us (31%)
  Pallas kernels  29.3 us (25%)
  starting transfers between devices  25.4 us (22%)
  blocking collectives  23.2 us (20%)
  local copies, waits for them, and re-layouts  1.24 us (1%)
    pallas_call x23, Pallas kernels, run(): kernel(*(operand if spec is SMEM else pltpu.with_memory_space_constraint(...  29.3 us
    all_to_all x1, blocking collectives, per_device(): squares = lax.all_to_all(squares, ALL, 0, 0, tiled=True)  23.2 us
    ppermute x16, waiting for transfers between devices, to_pair(): return lax.ppermute(shard, axis, pairs)  21.1 us
    ppermute x16, starting transfers between devices, to_pair(): return lax.ppermute(shard, axis, pairs)  15.6 us
    ppermute x1, waiting for transfers between devices, per_device(): fetched = lax.ppermute(half, (ZH, 'mp'), [(0, 3), (3, 0), (1, 2), (2, 1)])  10.3 us
    ppermute x7, starting transfers between devices, swap(): return lax.ppermute(shard, axis, [(0, 1), (1, 0)])  5.06 us
    ppermute x1, starting transfers between devices, per_device(): fetched = lax.ppermute(half, (ZH, 'mp'), [(0, 3), (3, 0), (1, 2), (2, 1)])  4.67 us
    ppermute x7, waiting for transfers between devices, swap(): return lax.ppermute(shard, axis, [(0, 1), (1, 0)])  4.53 us
  transfers between devices with their start and end apart: 24, of which 11 were waited for; matrix products, arithmetic and copies ran while one was open for 0% of the time, Pallas kernels for 22%

profile of v14, /device:TPU:1, one launch (start us, length us, event | category | flops | bytes accessed | tf_op | source)
XLA Modules:
  0.0 115.8 jit_solution(9228190180576805360)
XLA Ops:
  0.6 0.1 stack.23.place_ref
  0.7 1.8 %half.1 = bf16[336,1536]{1,0:T(8,128)(2,1)S(1)} custom-call(s32[5]{0:T(128)S(1)} %stack.23.place_ref, bf16[663,1536]{1,0:T(8,128)(2,1)} %bitcast.13), custom_call_target="tpu_custom_call" | custom-call | flops 17179869184 | bytes 67108864 | tf_op jit(solution)/shard_map/half/pallas_call | solution.py:73
  2.6 4.7 %collective-permute-start.1 = (bf16[336,1536]{1,0:T(8,128)(2,1)S(1)}, bf16[336,1536]{1,0:T(8,128)(2,1)S(1)}, u32[]{:S(2)}, u32[]{:S(2)}) collective-permute-start(bf16[336,1536]{1,0:T(8,128)(2,1)S(1)} %half.1), channel_id=1, source_target_pairs={{0,17},{17,0},{1,16},{16,1},{2,19},{19,2},{3,18},{18,3},{4,21},{21... | collective-permute-start | bytes 3096584 | tf_op jit(solution)/shard_map/ppermute | solution.py:381
  7.3 5.1 %forward.1 = (f32[256,768]{1,0:T(8,128)}, bf16[256,768]{1,0:T(8,128)(2,1)}, bf16[256,1536]{1,0:T(8,128)(2,1)S(1)}) custom-call(bf16[2652,256]{1,0:T(8,128)(2,1)} %bitcast.10, bf16[2652,768]{1,0:T(8,128)(2,1)} %w_first_hbm.1, bf16[768,1536]{1,0:T(8,128)(2,1)} %w_middle_ref.1), custom_call_target="tpu_custom_call" | custom-call | flops 17179869184 | bytes 67108864 | tf_op jit(solution)/shard_map/forward/pallas_call | solution.py:73
  12.3 0.1 collective-permute-start
  12.4 1.0 collective-permute-start.7
  13.4 0.1 collective-permute-start.4
  13.5 1.1 copy-done.5
  14.6 4.9 %stage.1 = (bf16[663,1536]{1,0:T(8,128)(2,1)S(1)}, bf16[663,256]{1,0:T(8,128)(2,1)S(1)}, bf16[2,336,256]{2,1,0:T(8,128)(2,1)S(1)}, f32[768,256]{1,0:T(8,128)S(1)...) custom-call(s32[5]{0:T(128)S(1)} %stack.23.place_ref, s32[2]{0:T(128)S(1)} %copy-done.3, f32[256,768]{1,0:T(8,128)S(1)} %copy-done.5, ...), custom_call_target="tpu_custom_call" | custom-call | flops 17179869184 | bytes 67108864 | tf_op jit(solution)/shard_map/stage/pallas_call | solution.py:73
  19.5 10.3 %collective-permute-done.1.fetched_ref = bf16[336,1536]{1,0:T(8,128)(2,1)S(1)} collective-permute-done((bf16[336,1536]{1,0:T(8,128)(2,1)S(1)}, bf16[336,1536]{1,0:T(8,128)(2,1)S(1)}, u32[]{:S(2)}, u32[]{:S(2)}) %collective-permute-start.1) | collective-permute-done | bytes 1032224 | tf_op jit(solution)/shard_map/ppermute | solution.py:381
  29.9 1.1 collective-permute-start.2
  31.0 0.0 collective-permute-done.arrived_ref
  31.0 3.1 %hidden.1 = (bf16[256,1536]{1,0:T(8,128)(2,1)S(1)}, f32[256,1536]{1,0:T(8,128)S(1)}, f32[256,1536]{1,0:T(8,128)S(1)}, bf16[1431,256]{1,0:T(8,128)(2,1)S(1)}, bf16[768,256]{1,0:T(8,128)(2,1)S(1)}) custom-call(s32[5]{0:T(128)S(1)} %stack.23.place_ref, bf16[256,1536]{1,0:T(8,128)(2,1)S(1)} %get-tuple-element.82.partial_ref, ...), custom_call_target="tpu_custom_call" | custom-call | flops 17179869184 | bytes 67108864 | tf_op jit(solution)/shard_map/hidden/pallas_call | solution.py:73
  34.1 1.6 %collective-permute-start.6 = (bf16[1431,256]{1,0:T(8,128)(2,1)S(1)}, bf16[1431,256]{1,0:T(8,128)(2,1)S(1)}, u32[]{:S(2)}, u32[]{:S(2)}) collective-permute-start(bf16[1431,256]{1,0:T(8,128)(2,1)S(1)} %get-tuple-element.104.sent_ref), channel_id=1, source_target_pairs={{0,2},{2,0},{1,3},{3,1},{4,6},{6,4},{5,7},{7,5},{8,10},{10,8},{9,1... | collective-permute-start | bytes 2198024 | tf_op jit(solution)/shard_map/ppermute | solution.py:37
  35.7 0.0 collective-permute-done.2.relayed_ref
  35.7 4.3 %slopes.1 = (bf16[1152,256]{1,0:T(8,128)(2,1)S(1)}, bf16[1152,256]{1,0:T(8,128)(2,1)S(1)}) custom-call(s32[5]{0:T(128)S(1)} %stack.23.place_ref, bf16[256,1536]{1,0:T(8,128)(2,1)S(1)} %get-tuple-element.89.act_ref, f32[256,1536]{1,0:T(8,128)S(1)} %get-tuple-element.90.act_slope_ref, f32[256,1536]{1,0:T(8,128)S(1)} %get-tuple-element.91.back_ref, ...), custom_call_target="tpu_custom_call" | custom-call | flops 17179869184 | bytes 67108864 | tf_op jit(solution)/shard_map/slopes/pallas_call | solution.py:73
  40.0 0.1 collective-permute-start.3
  40.1 0.0 collective-permute-done.6.arrived_ref
  40.1 1.5 %last.1 = (f32[2,4,4,24,384]{4,3,2,1,0:T(8,128)S(1)}, bf16[2,4,4,24,384]{4,3,2,1,0:T(8,128)(2,1)S(1)}) custom-call(s32[5]{0:T(128)S(1)} %stack.23.place_ref, bf16[768,256]{1,0:T(8,128)(2,1)S(1)} %get-tuple-element.103.own_ref, bf16[1431,256]{1,0:T(8,128)(2,1)S(1)} %get-tuple-element.104.sent_ref, bf16[1431,256]{1,0:T(8,128)(2,1)S(1)} %collective-permute-done.6.arrived_ref), custom_call_target="tpu_custom_call" | custom-call | flops 17179869184 | bytes 67108864 | tf_op jit(solution)/shard_map/last/pallas_call | solution.py:73
  41.6 1.3 %collective-permute-start.9 = (bf16[2,4,4,24,384]{4,3,2,1,0:T(8,128)(2,1)S(1)}, bf16[2,4,4,24,384]{4,3,2,1,0:T(8,128)(2,1)S(1)}, u32[]{:S(2)}, u32[]{:S(2)}) collective-permute-start(bf16[2,4,4,24,384]{4,3,2,1,0:T(8,128)(2,1)S(1)} %get-tuple-element.105), channel_id=1, source_target_pairs={{0,4},{4,0},{8,12},{12,8},{1,5},{5,1},{9,13},{13,9},{2,6},{6,2},{1... | collective-permute-start | bytes 1769480 | tf_op jit(solution)/shard_map/ppermute | solution.py:42
  42.9 0.0 collective-permute-done.4.sibling_belief_ref
  42.9 0.0 collective-permute-done.3.arrived_ref
  42.9 2.4 %first.1 = (f32[2,4,4,24,384]{4,3,2,1,0:T(8,128)S(1)}, bf16[2,4,4,24,384]{4,3,2,1,0:T(8,128)(2,1)S(1)}, f32[2,4,3,24,384]{4,3,2,1,0:T(8,128)S(1)}, bf16[2,4,3,24,384]{4,3,2,1,0:T(8,128)(2,1)S(1)}) custom-call(s32[5]{0:T(128)S(1)} %stack.23.place_ref, bf16[1152,256]{1,0:T(8,128)(2,1)S(1)} %get-tuple-element.97.own_ref, ...), custom_call_target="tpu_custom_call" | custom-call | flops 17179869184 | bytes 67108864 | tf_op jit(solution)/shard_map/first/pallas_call | solution.py:73
  45.3 2.8 %collective-permute-start.11 = (bf16[2,4,3,24,384]{4,3,2,1,0:T(8,128)(2,1)S(1)}, bf16[2,4,3,24,384]{4,3,2,1,0:T(8,128)(2,1)S(1)}, u32[]{:S(2)}, u32[]{:S(2)}) collective-permute-start(bf16[2,4,3,24,384]{4,3,2,1,0:T(8,128)(2,1)S(1)} %get-tuple-element.108), channel_id=1, source_target_pairs={{0,96},{32,64},{64,32},{96,0},{1,97},{33,65},{65,33},{97,1},{2,98}... | collective-permute-start | bytes 1327112 | tf_op jit(solution)/shard_map/ppermute | solution.py:42
  48.1 0.0 collective-permute-done.7.sibling_act_ref
  48.2 1.5 %middle.1 = (f32[2,4,4,24,384]{4,3,2,1,0:T(8,128)S(1)}, bf16[2,4,4,24,384]{4,3,2,1,0:T(8,128)(2,1)S(1)}) custom-call(s32[5]{0:T(128)S(1)} %stack.23.place_ref, bf16[1152,256]{1,0:T(8,128)(2,1)S(1)} %get-tuple-element.97.own_ref, bf16[1152,256]{1,0:T(8,128)(2,1)S(1)} %collective-permute-done.3.arrived_ref, bf16[256,768]{1,0:T(8,128)(2,1)S(1)} %copy-done.2, ...), custom_call_target="tpu_custom_call" | custom-call | flops 17179869184 | bytes 67108864 | tf_op jit(solution)/shard_map/middle/pallas_call | solution.py:73
  49.6 1.9 %collective-permute-start.10 = (bf16[2,4,4,24,384]{4,3,2,1,0:T(8,128)(2,1)S(1)}, bf16[2,4,4,24,384]{4,3,2,1,0:T(8,128)(2,1)S(1)}, u32[]{:S(2)}, u32[]{:S(2)}) collective-permute-start(bf16[2,4,4,24,384]{4,3,2,1,0:T(8,128)(2,1)S(1)} %get-tuple-element.107), channel_id=1, source_target_pairs={{0,12},{4,8},{8,4},{12,0},{1,13},{5,9},{9,5},{13,1},{2,14},{6,10},... | collective-permute-start | bytes 1769480 | tf_op jit(solution)/shard_map/ppermute | solution.py:42
  51.5 4.6 %collective-permute-done.9.arrived_ref = bf16[2,4,4,24,384]{4,3,2,1,0:T(8,128)(2,1)S(1)} collective-permute-done((bf16[2,4,4,24,384]{4,3,2,1,0:T(8,128)(2,1)S(1)}, bf16[2,4,4,24,384]{4,3,2,1,0:T(8,128)(2,1)S(1)}, u32[]{:S(2)}, u32[]{:S(2)}) %collective-permute-start.9) | collective-permute-done | bytes 589856 | tf_op jit(solution)/shard_map/ppermute | solution.py:42
  56.1 0.1 halve.9
  56.3 2.6 %collective-permute-start.13 = (bf16[4,4,24,384]{3,2,1,0:T(8,128)(2,1)S(1)}, bf16[4,4,24,384]{3,2,1,0:T(8,128)(2,1)S(1)}, u32[]{:S(2)}, u32[]{:S(2)}) collective-permute-start(bf16[4,4,24,384]{3,2,1,0:T(8,128)(2,1)S(1)} %get-tuple-element.114), channel_id=1, source_target_pairs={{0,12},{4,8},{8,4},{12,0},{1,13},{5,9},{9,5},{13,1},{2,14},{6,10},... | collective-permute-start | bytes 884744 | tf_op jit(solution)/shard_map/ppermute | solution.py:42
  58.8 0.1 halve.11
  58.9 1.4 %collective-permute-start.15 = (bf16[4,3,24,384]{3,2,1,0:T(8,128)(2,1)S(1)}, bf16[4,3,24,384]{3,2,1,0:T(8,128)(2,1)S(1)}, u32[]{:S(2)}, u32[]{:S(2)}) collective-permute-start(bf16[4,3,24,384]{3,2,1,0:T(8,128)(2,1)S(1)} %get-tuple-element.120), channel_id=1, source_target_pairs={{0,32},{32,0},{64,96},{96,64},{1,33},{33,1},{65,97},{97,65},{2,34}... | collective-permute-start | bytes 663560 | tf_op jit(solution)/shard_map/ppermute | solution.py:42
  60.3 4.4 %collective-permute-done.10.arrived_ref = bf16[2,4,4,24,384]{4,3,2,1,0:T(8,128)(2,1)S(1)} collective-permute-done((bf16[2,4,4,24,384]{4,3,2,1,0:T(8,128)(2,1)S(1)}, bf16[2,4,4,24,384]{4,3,2,1,0:T(8,128)(2,1)S(1)}, u32[]{:S(2)}, u32[]{:S(2)}) %collective-permute-start.10) | collective-permute-done | bytes 589856 | tf_op jit(solution)/shard_map/ppermute | solution.py:42
  64.7 0.3 collective-permute-done.5.arrived_ref
  65.0 0.1 halve.10
  65.1 0.4 collective-permute-start.14
  65.5 0.1 halve.8
  65.6 0.2 collective-permute-start.8
  65.8 5.2 %collective-permute-done.13.arrived_ref = bf16[4,4,24,384]{3,2,1,0:T(8,128)(2,1)S(1)} collective-permute-done((bf16[4,4,24,384]{3,2,1,0:T(8,128)(2,1)S(1)}, bf16[4,4,24,384]{3,2,1,0:T(8,128)(2,1)S(1)}, u32[]{:S(2)}, u32[]{:S(2)}) %collective-permute-start.13) | collective-permute-done | bytes 294944 | tf_op jit(solution)/shard_map/ppermute | solution.py:42
  71.0 0.6 turn.5
  71.6 0.1 collective-permute-start.17
  71.7 0.6 turn.7
  72.3 1.9 %collective-permute-start.19 = (bf16[2,3,24,384]{3,2,1,0:T(8,128)(2,1)S(1)}, bf16[2,3,24,384]{3,2,1,0:T(8,128)(2,1)S(1)}, u32[]{:S(2)}, u32[]{:S(2)}) collective-permute-start(bf16[2,3,24,384]{3,2,1,0:T(8,128)(2,1)S(1)} %get-tuple-element.132), channel_id=1, source_target_pairs={{0,12},{4,8},{8,4},{12,0},{1,13},{5,9},{9,5},{13,1},{2,14},{6,10},... | collective-permute-start | bytes 331784 | tf_op jit(solution)/shard_map/ppermute | solution.py:42
  74.2 0.6 turn.6
  74.8 0.7 collective-permute-start.18
  75.5 0.6 turn.4
  76.1 0.1 collective-permute-start.12
  76.2 0.0 collective-permute-done.17.arrived_ref
  76.3 1.2 %collective-permute-done.19.arrived_ref = bf16[2,3,24,384]{3,2,1,0:T(8,128)(2,1)S(1)} collective-permute-done((bf16[2,3,24,384]{3,2,1,0:T(8,128)(2,1)S(1)}, bf16[2,3,24,384]{3,2,1,0:T(8,128)(2,1)S(1)}, u32[]{:S(2)}, u32[]{:S(2)}) %collective-permute-start.19) | collective-permute-done | bytes 110624 | tf_op jit(solution)/shard_map/ppermute | solution.py:42
  77.5 0.9 collective-permute-start.21
  78.4 1.7 %collective-permute-done.18.arrived_ref = bf16[2,4,24,384]{3,2,1,0:T(8,128)(2,1)S(1)} collective-permute-done((bf16[2,4,24,384]{3,2,1,0:T(8,128)(2,1)S(1)}, bf16[2,4,24,384]{3,2,1,0:T(8,128)(2,1)S(1)}, u32[]{:S(2)}, u32[]{:S(2)}) %collective-permute-start.18) | collective-permute-done | bytes 147488 | tf_op jit(solution)/shard_map/ppermute | solution.py:42
  80.2 0.6 collective-permute-start.22
  80.8 0.7 collective-permute-start.16
  81.6 0.1 collective-permute-start.20
  81.7 0.3 collective-permute-done.21.refs_5_
  81.9 2.8 %collective-permute-done.20.refs_3_ = bf16[3,24,384]{2,1,0:T(8,128)(2,1)S(1)} collective-permute-done((bf16[3,24,384]{2,1,0:T(8,128)(2,1)S(1)}, bf16[3,24,384]{2,1,0:T(8,128)(2,1)S(1)}, u32[]{:S(2)}, u32[]{:S(2)}) %collective-permute-start.20) | collective-permute-done | bytes 55328 | tf_op jit(solution)/shard_map/ppermute | solution.py:42
  84.7 0.0 collective-permute-done.22.refs_7_
  84.7 0.6 collective-permute-done.16.refs_1_
  85.3 0.6 z_cut.1
  86.0 1.1 collective-permute-start.23
  87.0 4.5 %collective-permute-done.23.arrived_ref = bf16[8,24,384]{2,1,0:T(8,128)(2,1)S(1)} collective-permute-done((bf16[8,24,384]{2,1,0:T(8,128)(2,1)S(1)}, bf16[8,24,384]{2,1,0:T(8,128)(2,1)S(1)}, u32[]{:S(2)}, u32[]{:S(2)}) %collective-permute-start.23) | collective-permute-done | bytes 147488 | tf_op jit(solution)/shard_map/ppermute | solution.py:37
  91.5 0.3 square.1
  91.8 23.2 %all_to_all.5.squares_ref = f32[128,1,128]{2,1,0:T(1,128)S(1)} all-to-all(f32[128,1,128]{2,1,0:T(1,128)S(1)} %get-tuple-element.155), channel_id=1, replica_groups=mesh['dp_0'=4,'dp_1'=2,'dp_2'=4,'dp_3'=2,'mp'=2] {'dp_0','dp_1','dp_2','..., dimensions={0} | all-to-all | bytes 131072 | tf_op jit(solution)/shard_map/all_to_all | solution.py:516
  115.0 0.9 scale.1
  (21 shorter events, 0.2 us)
Async XLA Ops:
  2.6 27.3 %collective-permute-start.1 = (bf16[336,1536]{1,0:T(8,128)(2,1)S(1)}, bf16[336,1536]{1,0:T(8,128)(2,1)S(1)}, u32[]{:S(2)}, u32[]{:S(2)}) collective-permute-start(bf16[336,1536]{1,0:T(8,128)(2,1)S(1)} %half.1), channel_id=1, source_target_pairs={{0,17},{17,0},{1,16},{16,1},{2,19},{19,2},{3,18},{18,3},{4,21},{21... | collective-permute-start | bytes 3096584 | tf_op jit(solution)/shard_map/ppermute | solution.py:381
  7.2 6.1 %copy-start.1 = (bf16[256,2652]{0,1:T(8,128)(2,1)S(1)}, bf16[256,2652]{0,1:T(8,128)(2,1)}, u32[]{:S(2)}) copy-start(bf16[256,2652]{0,1:T(8,128)(2,1)} %param.7) | copy-start | bytes 4073476
  7.2 6.2 %copy-start = (bf16[768,1536]{1,0:T(8,128)(2,1)S(1)}, bf16[768,1536]{1,0:T(8,128)(2,1)}, u32[]{:S(2)}) copy-start(bf16[768,1536]{1,0:T(8,128)(2,1)} %w_middle_ref.1) | copy-start | bytes 7077892
  7.2 6.2 %copy-start.3 = (s32[2]{0:T(128)S(1)}, s32[2]{0:T(128)}, u32[]{:S(2)}) copy-start(s32[2]{0:T(128)} %counts_ref.1) | copy-start | bytes 28
  7.2 6.2 %copy-start.4 = (s32[2,768,1]{2,1,0:T(8,128)S(1)}, s32[2,768,1]{2,1,0:T(8,128)}, u32[]{:S(2)}) copy-start(s32[2,768,1]{2,1,0:T(8,128)} %constant.21.clone.orders_ref) | copy-start | bytes 18436
  12.3 18.7 %collective-permute-start = (bf16[256,1536]{1,0:T(8,128)(2,1)S(1)}, bf16[256,1536]{1,0:T(8,128)(2,1)S(1)}, u32[]{:S(2)}, u32[]{:S(2)}) collective-permute-start(bf16[256,1536]{1,0:T(8,128)(2,1)S(1)} %get-tuple-element.82.partial_ref), channel_id=1, source_target_pairs={{0,1},{1,0},{2,3},{3,2},{4,5},{5,4},{6,7},{7,6},{8,9},{9,8},{10,11... | collective-permute-start | bytes 2359304 | tf_op jit(solution)/shard_map/ppermute | solution.py:37
  12.4 35.7 %collective-permute-start.7 = (bf16[256,768]{1,0:T(8,128)(2,1)}, bf16[256,768]{1,0:T(8,128)(2,1)S(1)}, u32[]{:S(2)}, u32[]{:S(2)}) collective-permute-start(bf16[256,768]{1,0:T(8,128)(2,1)} %get-tuple-element.106.act_ref), channel_id=1, source_target_pairs={{0,2},{2,0},{1,3},{3,1},{4,6},{6,4},{5,7},{7,5},{8,10},{10,8},{9,1... | collective-permute-start | bytes 1179656 | tf_op jit(solution)/shard_map/ppermute | solution.py:37
  13.4 29.5 %collective-permute-start.4 = (bf16[2652,256]{1,0:T(8,128)(2,1)S(1)}, bf16[2652,256]{1,0:T(8,128)(2,1)S(1)}, u32[]{:S(2)}, u32[]{:S(2)}) collective-permute-start(bf16[2652,256]{1,0:T(8,128)(2,1)S(1)} %bitcast.11), channel_id=1, source_target_pairs={{0,2},{2,0},{1,3},{3,1},{4,6},{6,4},{5,7},{7,5},{8,10},{10,8},{9,1... | collective-permute-start | bytes 4073480 | tf_op jit(solution)/shard_map/ppermute | solution.py:37
  13.5 1.1 copy-start.5
  29.9 5.9 %collective-permute-start.2 = (bf16[336,1536]{1,0:T(8,128)(2,1)S(1)}, bf16[336,1536]{1,0:T(8,128)(2,1)S(1)}, u32[]{:S(2)}, u32[]{:S(2)}) collective-permute-start(bf16[336,1536]{1,0:T(8,128)(2,1)S(1)} %collective-permute-done.1.fetched_ref), channel_id=1, source_target_pairs={{0,2},{2,0},{1,3},{3,1},{4,6},{6,4},{5,7},{7,5},{8,10},{10,8},{9,1... | collective-permute-start | bytes 3096584 | tf_op jit(solution)/shard_map/ppermute | solution.py:37
  34.1 6.0 %collective-permute-start.6 = (bf16[1431,256]{1,0:T(8,128)(2,1)S(1)}, bf16[1431,256]{1,0:T(8,128)(2,1)S(1)}, u32[]{:S(2)}, u32[]{:S(2)}) collective-permute-start(bf16[1431,256]{1,0:T(8,128)(2,1)S(1)} %get-tuple-element.104.sent_ref), channel_id=1, source_target_pairs={{0,2},{2,0},{1,3},{3,1},{4,6},{6,4},{5,7},{7,5},{8,10},{10,8},{9,1... | collective-permute-start | bytes 2198024 | tf_op jit(solution)/shard_map/ppermute | solution.py:37
  40.0 2.9 %collective-permute-start.3 = (bf16[1152,256]{1,0:T(8,128)(2,1)S(1)}, bf16[1152,256]{1,0:T(8,128)(2,1)S(1)}, u32[]{:S(2)}, u32[]{:S(2)}) collective-permute-start(bf16[1152,256]{1,0:T(8,128)(2,1)S(1)} %get-tuple-element.98), channel_id=1, source_target_pairs={{0,2},{2,0},{1,3},{3,1},{4,6},{6,4},{5,7},{7,5},{8,10},{10,8},{9,1... | collective-permute-start | bytes 1769480 | tf_op jit(solution)/shard_map/ppermute | solution.py:37
  41.6 6.5 %copy-start.2 = (bf16[256,768]{1,0:T(8,128)(2,1)S(1)}, bf16[256,768]{1,0:T(8,128)(2,1)}, u32[]{:S(2)}) copy-start(bf16[256,768]{1,0:T(8,128)(2,1)} %get-tuple-element.106.act_ref) | copy-start | bytes 1179652
  41.6 14.5 %collective-permute-start.9 = (bf16[2,4,4,24,384]{4,3,2,1,0:T(8,128)(2,1)S(1)}, bf16[2,4,4,24,384]{4,3,2,1,0:T(8,128)(2,1)S(1)}, u32[]{:S(2)}, u32[]{:S(2)}) collective-permute-start(bf16[2,4,4,24,384]{4,3,2,1,0:T(8,128)(2,1)S(1)} %get-tuple-element.105), channel_id=1, source_target_pairs={{0,4},{4,0},{8,12},{12,8},{1,5},{5,1},{9,13},{13,9},{2,6},{6,2},{1... | collective-permute-start | bytes 1769480 | tf_op jit(solution)/shard_map/ppermute | solution.py:42
  45.3 13.5 %collective-permute-start.11 = (bf16[2,4,3,24,384]{4,3,2,1,0:T(8,128)(2,1)S(1)}, bf16[2,4,3,24,384]{4,3,2,1,0:T(8,128)(2,1)S(1)}, u32[]{:S(2)}, u32[]{:S(2)}) collective-permute-start(bf16[2,4,3,24,384]{4,3,2,1,0:T(8,128)(2,1)S(1)} %get-tuple-element.108), channel_id=1, source_target_pairs={{0,96},{32,64},{64,32},{96,0},{1,97},{33,65},{65,33},{97,1},{2,98}... | collective-permute-start | bytes 1327112 | tf_op jit(solution)/shard_map/ppermute | solution.py:42
  49.6 15.1 %collective-permute-start.10 = (bf16[2,4,4,24,384]{4,3,2,1,0:T(8,128)(2,1)S(1)}, bf16[2,4,4,24,384]{4,3,2,1,0:T(8,128)(2,1)S(1)}, u32[]{:S(2)}, u32[]{:S(2)}) collective-permute-start(bf16[2,4,4,24,384]{4,3,2,1,0:T(8,128)(2,1)S(1)} %get-tuple-element.107), channel_id=1, source_target_pairs={{0,12},{4,8},{8,4},{12,0},{1,13},{5,9},{9,5},{13,1},{2,14},{6,10},... | collective-permute-start | bytes 1769480 | tf_op jit(solution)/shard_map/ppermute | solution.py:42
  51.5 13.5 %collective-permute-start.5 = (bf16[2,4,4,24,384]{4,3,2,1,0:T(8,128)(2,1)S(1)}, bf16[2,4,4,24,384]{4,3,2,1,0:T(8,128)(2,1)S(1)}, u32[]{:S(2)}, u32[]{:S(2)}) collective-permute-start(bf16[2,4,4,24,384]{4,3,2,1,0:T(8,128)(2,1)S(1)} %get-tuple-element.102), channel_id=1, source_target_pairs={{0,32},{32,0},{64,96},{96,64},{1,33},{33,1},{65,97},{97,65},{2,34}... | collective-permute-start | bytes 1769480 | tf_op jit(solution)/shard_map/ppermute | solution.py:42
  56.3 14.7 %collective-permute-start.13 = (bf16[4,4,24,384]{3,2,1,0:T(8,128)(2,1)S(1)}, bf16[4,4,24,384]{3,2,1,0:T(8,128)(2,1)S(1)}, u32[]{:S(2)}, u32[]{:S(2)}) collective-permute-start(bf16[4,4,24,384]{3,2,1,0:T(8,128)(2,1)S(1)} %get-tuple-element.114), channel_id=1, source_target_pairs={{0,12},{4,8},{8,4},{12,0},{1,13},{5,9},{9,5},{13,1},{2,14},{6,10},... | collective-permute-start | bytes 884744 | tf_op jit(solution)/shard_map/ppermute | solution.py:42
  58.9 12.8 %collective-permute-start.15 = (bf16[4,3,24,384]{3,2,1,0:T(8,128)(2,1)S(1)}, bf16[4,3,24,384]{3,2,1,0:T(8,128)(2,1)S(1)}, u32[]{:S(2)}, u32[]{:S(2)}) collective-permute-start(bf16[4,3,24,384]{3,2,1,0:T(8,128)(2,1)S(1)} %get-tuple-element.120), channel_id=1, source_target_pairs={{0,32},{32,0},{64,96},{96,64},{1,33},{33,1},{65,97},{97,65},{2,34}... | collective-permute-start | bytes 663560 | tf_op jit(solution)/shard_map/ppermute | solution.py:42
  65.1 9.1 %collective-permute-start.14 = (bf16[4,4,24,384]{3,2,1,0:T(8,128)(2,1)S(1)}, bf16[4,4,24,384]{3,2,1,0:T(8,128)(2,1)S(1)}, u32[]{:S(2)}, u32[]{:S(2)}) collective-permute-start(bf16[4,4,24,384]{3,2,1,0:T(8,128)(2,1)S(1)} %get-tuple-element.117), channel_id=1, source_target_pairs={{0,4},{4,0},{8,12},{12,8},{1,5},{5,1},{9,13},{13,9},{2,6},{6,2},{1... | collective-permute-start | bytes 884744 | tf_op jit(solution)/shard_map/ppermute | solution.py:42
  65.6 8.6 %collective-permute-start.8 = (bf16[4,4,24,384]{3,2,1,0:T(8,128)(2,1)S(1)}, bf16[4,4,24,384]{3,2,1,0:T(8,128)(2,1)S(1)}, u32[]{:S(2)}, u32[]{:S(2)}) collective-permute-start(bf16[4,4,24,384]{3,2,1,0:T(8,128)(2,1)S(1)} %get-tuple-element.111), channel_id=1, source_target_pairs={{0,96},{32,64},{64,32},{96,0},{1,97},{33,65},{65,33},{97,1},{2,98}... | collective-permute-start | bytes 884744 | tf_op jit(solution)/shard_map/ppermute | solution.py:42
  71.6 4.6 %collective-permute-start.17 = (bf16[2,4,24,384]{3,2,1,0:T(8,128)(2,1)S(1)}, bf16[2,4,24,384]{3,2,1,0:T(8,128)(2,1)S(1)}, u32[]{:S(2)}, u32[]{:S(2)}) collective-permute-start(bf16[2,4,24,384]{3,2,1,0:T(8,128)(2,1)S(1)} %get-tuple-element.126), channel_id=1, source_target_pairs={{0,32},{32,0},{64,96},{96,64},{1,33},{33,1},{65,97},{97,65},{2,34}... | collective-permute-start | bytes 442376 | tf_op jit(solution)/shard_map/ppermute | solution.py:42
  72.3 5.2 %collective-permute-start.19 = (bf16[2,3,24,384]{3,2,1,0:T(8,128)(2,1)S(1)}, bf16[2,3,24,384]{3,2,1,0:T(8,128)(2,1)S(1)}, u32[]{:S(2)}, u32[]{:S(2)}) collective-permute-start(bf16[2,3,24,384]{3,2,1,0:T(8,128)(2,1)S(1)} %get-tuple-element.132), channel_id=1, source_target_pairs={{0,12},{4,8},{8,4},{12,0},{1,13},{5,9},{9,5},{13,1},{2,14},{6,10},... | collective-permute-start | bytes 331784 | tf_op jit(solution)/shard_map/ppermute | solution.py:42
  74.8 5.3 %collective-permute-start.18 = (bf16[2,4,24,384]{3,2,1,0:T(8,128)(2,1)S(1)}, bf16[2,4,24,384]{3,2,1,0:T(8,128)(2,1)S(1)}, u32[]{:S(2)}, u32[]{:S(2)}) collective-permute-start(bf16[2,4,24,384]{3,2,1,0:T(8,128)(2,1)S(1)} %get-tuple-element.129), channel_id=1, source_target_pairs={{0,96},{32,64},{64,32},{96,0},{1,97},{33,65},{65,33},{97,1},{2,98}... | collective-permute-start | bytes 442376 | tf_op jit(solution)/shard_map/ppermute | solution.py:42
  76.1 4.6 %collective-permute-start.12 = (bf16[2,4,24,384]{3,2,1,0:T(8,128)(2,1)S(1)}, bf16[2,4,24,384]{3,2,1,0:T(8,128)(2,1)S(1)}, u32[]{:S(2)}, u32[]{:S(2)}) collective-permute-start(bf16[2,4,24,384]{3,2,1,0:T(8,128)(2,1)S(1)} %get-tuple-element.123), channel_id=1, source_target_pairs={{0,4},{4,0},{8,12},{12,8},{1,5},{5,1},{9,13},{13,9},{2,6},{6,2},{1... | collective-permute-start | bytes 442376 | tf_op jit(solution)/shard_map/ppermute | solution.py:42
  77.5 4.4 %collective-permute-start.21 = (bf16[4,24,384]{2,1,0:T(8,128)(2,1)S(1)}, bf16[4,24,384]{2,1,0:T(8,128)(2,1)S(1)}, u32[]{:S(2)}, u32[]{:S(2)}) collective-permute-start(bf16[4,24,384]{2,1,0:T(8,128)(2,1)S(1)} %get-tuple-element.138), channel_id=1, source_target_pairs={{0,96},{32,64},{64,32},{96,0},{1,97},{33,65},{65,33},{97,1},{2,98}... | collective-permute-start | bytes 221192 | tf_op jit(solution)/shard_map/ppermute | solution.py:42
  80.2 4.5 %collective-permute-start.22 = (bf16[4,24,384]{2,1,0:T(8,128)(2,1)S(1)}, bf16[4,24,384]{2,1,0:T(8,128)(2,1)S(1)}, u32[]{:S(2)}, u32[]{:S(2)}) collective-permute-start(bf16[4,24,384]{2,1,0:T(8,128)(2,1)S(1)} %get-tuple-element.141), channel_id=1, source_target_pairs={{0,32},{32,0},{64,96},{96,64},{1,33},{33,1},{65,97},{97,65},{2,34}... | collective-permute-start | bytes 221192 | tf_op jit(solution)/shard_map/ppermute | solution.py:42
  80.8 4.5 %collective-permute-start.16 = (bf16[4,24,384]{2,1,0:T(8,128)(2,1)S(1)}, bf16[4,24,384]{2,1,0:T(8,128)(2,1)S(1)}, u32[]{:S(2)}, u32[]{:S(2)}) collective-permute-start(bf16[4,24,384]{2,1,0:T(8,128)(2,1)S(1)} %get-tuple-element.135), channel_id=1, source_target_pairs={{0,12},{4,8},{8,4},{12,0},{1,13},{5,9},{9,5},{13,1},{2,14},{6,10},... | collective-permute-start | bytes 221192 | tf_op jit(solution)/shard_map/ppermute | solution.py:42
  81.6 3.1 %collective-permute-start.20 = (bf16[3,24,384]{2,1,0:T(8,128)(2,1)S(1)}, bf16[3,24,384]{2,1,0:T(8,128)(2,1)S(1)}, u32[]{:S(2)}, u32[]{:S(2)}) collective-permute-start(bf16[3,24,384]{2,1,0:T(8,128)(2,1)S(1)} %get-tuple-element.144), channel_id=1, source_target_pairs={{0,4},{4,0},{8,12},{12,8},{1,5},{5,1},{9,13},{13,9},{2,6},{6,2},{1... | collective-permute-start | bytes 165896 | tf_op jit(solution)/shard_map/ppermute | solution.py:42
  86.0 5.6 %collective-permute-start.23 = (bf16[8,24,384]{2,1,0:T(8,128)(2,1)S(1)}, bf16[8,24,384]{2,1,0:T(8,128)(2,1)S(1)}, u32[]{:S(2)}, u32[]{:S(2)}) collective-permute-start(bf16[8,24,384]{2,1,0:T(8,128)(2,1)S(1)} %get-tuple-element.153), channel_id=1, source_target_pairs={{0,16},{16,0},{1,17},{17,1},{2,18},{18,2},{3,19},{19,3},{4,20},{20... | collective-permute-start | bytes 442376 | tf_op jit(solution)/shard_map/ppermute | solution.py:37

commit v15 on v14

--- a/solution.py
+++ b/solution.py
@@ -242,67 +242,72 @@
     return [(start, min(start + COLS, width)) for start in range(0, width, COLS)]
 
 
-def put_columns(raw, granule, out_ref):
-    width = raw.shape[1]
-    if width < COLS:
-        raw = jnp.concatenate([raw, jnp.zeros((raw.shape[0], COLS - width), raw.dtype)], 1)
-    for unit in range(16):
-        out_ref[unit, granule] = raw[unit * ROWS : (unit + 1) * ROWS]
-
-
 def kept_and_sent(me, order):
     near, far, opposite = lax.bitwise_xor(me, 1), 3 - me, lax.bitwise_xor(me, 2)
     return ((me, far), (near, opposite)) if order == 0 else ((me, near), (far, opposite))
 
 
-def cut_rows(raw_ref, me, order, kept_ref, sent_ref):
-    for out_ref, blocks in zip((kept_ref, sent_ref), kept_and_sent(me, order)):
-        for position, x in enumerate(blocks):
-            for y in range(4):
-                for granule in range(4):
-                    first = ROWS * (2 * (4 * y + x) + granule // 2)
-                    columns = slice(granule % 2 * COLS, (granule % 2 + 1) * COLS)
-                    rows = raw_ref[pl.ds(pl.multiple_of(first, 8), ROWS), columns]
-                    out_ref[position, y, granule] = rows.astype(out_ref.dtype)
-
-
-def last_kernel(place_ref, own_ref, sent_ref, arrived_ref, kept_out, sent_out, raw_ref, padded_ref):
+def rows_along_x(ref, me, order):
+    kept, sent = kept_and_sent(me, order)
+    firsts = [2 * ROWS * (4 * y + x) for x in (*kept, *sent) for y in range(4)]
+    return jnp.concatenate(
+        [ref[pl.ds(pl.multiple_of(first, 16), 2 * ROWS), :] for first in firsts], 0
+    )
+
+
+def put_rows(raw, kept_ref, sent_ref):
+    for block in range(16):
+        out_ref = (kept_ref, sent_ref)[block // 8]
+        for granule in range(4):
+            first = ROWS * (2 * block + granule // 2)
+            columns = slice(granule % 2 * COLS, (granule % 2 + 1) * COLS)
+            rows = raw[first : first + ROWS, columns]
+            out_ref[block // 4 % 2, block % 4, granule] = rows.astype(out_ref.dtype)
+
+
+def last_kernel(place_ref, own_ref, sent_ref, arrived_ref, kept_out, sent_out, padded_ref):
     half = own_ref.shape[0]
     width = sent_ref.shape[0] - half
     padded_ref[...] = jnp.zeros_like(padded_ref)
     padded_ref[0, 0:width, :] = sent_ref[half:, :]
     padded_ref[1, 0:width, :] = arrived_ref[half:, :]
-    raw_ref[...] = contract(own_ref[...], padded_ref[0], 1, 1) + contract(
-        arrived_ref[0:half, :], padded_ref[1], 1, 1
-    )
-    cut_rows(raw_ref, place_ref[2], 0, kept_out, sent_out)
-
-
-def middle_kernel(
-    place_ref, own_ref, arrived_ref, act_ref, sibling_act_ref, kept_out, sent_out, raw_ref
-):
-    half = raw_ref.shape[0]
-    raw_ref[...] = dot(own_ref[0:half, :], act_ref[...]) + dot(
-        arrived_ref[0:half, :], sibling_act_ref[...]
-    )
-    cut_rows(raw_ref, place_ref[2], 1, kept_out, sent_out)
-
-
-def first_kernel(place_ref, own_ref, arrived_ref, belief_ref, sibling_belief_ref, *refs):
-    raw_ref = refs[-1]
+    own, arrived = (rows_along_x(ref, place_ref[2], 0) for ref in (own_ref, arrived_ref))
+    raw = contract(own, padded_ref[0], 1, 1) + contract(arrived, padded_ref[1], 1, 1)
+    put_rows(raw, kept_out, sent_out)
+
+
+def middle_kernel(place_ref, own_ref, arrived_ref, act_ref, sibling_act_ref, kept_out, sent_out):
+    own, arrived = (rows_along_x(ref, place_ref[2], 1) for ref in (own_ref, arrived_ref))
+    raw = dot(own, act_ref[...]) + dot(arrived, sibling_act_ref[...])
+    put_rows(raw, kept_out, sent_out)
+
+
+def first_kernel(place_ref, own_ref, arrived_ref, belief_ref, sibling_belief_ref, *out_refs):
     start_row = own_ref.shape[0] // 3 * 2
-    own, arrived = own_ref[start_row:, :], arrived_ref[start_row:, :]
-    for start, stop in column_cuts(belief_ref.shape[0]):
-        raw = contract(own, belief_ref[start:stop, :], 1, 1) + contract(
-            arrived, sibling_belief_ref[start:stop, :], 1, 1
+    cuts = column_cuts(belief_ref.shape[0])
+    for order, part in enumerate((cuts[0:4], cuts[4:7])):
+        kept, sent = kept_and_sent(place_ref[1], order)
+        own, arrived = (
+            jnp.concatenate(
+                [
+                    ref[pl.ds(pl.multiple_of(start_row + 4 * ROWS * y, 32), 4 * ROWS), :]
+                    for y in (*kept, *sent)
+                ],
+                0,
+            )
+            for ref in (own_ref, arrived_ref)
         )
-        put_columns(raw, start // COLS, raw_ref)
-    for order, part in enumerate((slice(0, 4), slice(4, 7))):
-        for side, blocks in enumerate(kept_and_sent(place_ref[1], order)):
-            out_ref = refs[2 * order + side]
-            for position, y in enumerate(blocks):
-                for x in range(4):
-                    out_ref[position, x] = raw_ref[4 * y + x, part].astype(out_ref.dtype)
+        for granule, (start, stop) in enumerate(part):
+            raw = contract(own, belief_ref[start:stop, :], 1, 1) + contract(
+                arrived, sibling_belief_ref[start:stop, :], 1, 1
+            )
+            if stop - start < COLS:
+                pad = jnp.zeros((raw.shape[0], COLS - raw.shape[1]), raw.dtype)
+                raw = jnp.concatenate([raw, pad], 1)
+            for unit in range(16):
+                out_ref = out_refs[2 * order + unit // 8]
+                rows = raw[unit * ROWS : (unit + 1) * ROWS]
+                out_ref[unit // 4 % 2, unit % 4, granule] = rows.astype(out_ref.dtype)
 
 
 def halve_kernel(kept_ref, arrived_ref, kept_out, sent_out):
@@ -474,24 +479,22 @@
             pairs((2, size)),
         )(place, *part)
 
-    raw = pltpu.VMEM((hidden // 2, units), F32)
     last_own, slopes_own = lax.optimization_barrier((last_own, slopes_own))
     last_parts = call(
         last_kernel,
         "last",
         [SMEM] + [VMEM] * 3,
         pairs((2, 4, 4)),
-        [raw, pltpu.VMEM((2, units, total_rows), BF16)],
+        [pltpu.VMEM((2, units, total_rows), BF16)],
     )(place, last_own, last_sent, last_arrived)
     first_parts = call(
         first_kernel,
         "first",
         [SMEM] + [VMEM] * 4,
         pairs((2, 4, 4), (2, 4, 3)),
-        [pltpu.VMEM((16, 7, ROWS, COLS), F32)],
     )(place, slopes_own, slopes_arrived, belief_t, sibling_belief)
     middle_parts = call(
-        middle_kernel, "middle", [SMEM] + [VMEM] * 4, pairs((2, 4, 4)), [raw]
+        middle_kernel, "middle", [SMEM] + [VMEM] * 4, pairs((2, 4, 4))
     )(place, slopes_own, slopes_arrived, act_first, sibling_act)
     axes, turned, orders, swapped = (X, X, Y, Y), (Y, Y, X, X), (0, 1, 0, 1), (1, 0, 1, 0)
     parts = (last_parts, middle_parts, first_parts[0:2], first_parts[2:4])

time: 116 us -> 116 us (level)
  no operation moved by 1% of the time
where the time goes in v15:
time: 116 us; the launch traced here: 115 us
  waiting for transfers between devices  36 us (31%)
  Pallas kernels  28.8 us (25%)
  starting transfers between devices  25.3 us (22%)
  blocking collectives  23.2 us (20%)
  local copies, waits for them, and re-layouts  1.24 us (1%)
    pallas_call x23, Pallas kernels, run(): kernel(*(operand if spec is SMEM else pltpu.with_memory_space_constraint(...  28.8 us
    all_to_all x1, blocking collectives, per_device(): squares = lax.all_to_all(squares, ALL, 0, 0, tiled=True)  23.2 us
    ppermute x16, waiting for transfers between devices, to_pair(): return lax.ppermute(shard, axis, pairs)  21.1 us
    ppermute x16, starting transfers between devices, to_pair(): return lax.ppermute(shard, axis, pairs)  15.6 us
    ppermute x1, waiting for transfers between devices, per_device(): fetched = lax.ppermute(half, (ZH, 'mp'), [(0, 3), (3, 0), (1, 2), (2, 1)])  10.3 us
    ppermute x7, starting transfers between devices, swap(): return lax.ppermute(shard, axis, [(0, 1), (1, 0)])  5.04 us
    ppermute x1, starting transfers between devices, per_device(): fetched = lax.ppermute(half, (ZH, 'mp'), [(0, 3), (3, 0), (1, 2), (2, 1)])  4.67 us
    ppermute x7, waiting for transfers between devices, swap(): return lax.ppermute(shard, axis, [(0, 1), (1, 0)])  4.55 us
  transfers between devices with their start and end apart: 24, of which 11 were waited for; matrix products, arithmetic and copies ran while one was open for 0% of the time, Pallas kernels for 22%

profile of v15, /device:TPU:1, one launch (start us, length us, event | category | flops | bytes accessed | tf_op | source)
XLA Modules:
  0.0 115.3 jit_solution(16075949947464921413)
XLA Ops:
  0.6 0.1 stack.23.place_ref
  0.7 1.8 %half.1 = bf16[336,1536]{1,0:T(8,128)(2,1)S(1)} custom-call(s32[5]{0:T(128)S(1)} %stack.23.place_ref, bf16[663,1536]{1,0:T(8,128)(2,1)} %bitcast.13), custom_call_target="tpu_custom_call" | custom-call | flops 17179869184 | bytes 67108864 | tf_op jit(solution)/shard_map/half/pallas_call | solution.py:73
  2.6 4.7 %collective-permute-start.1 = (bf16[336,1536]{1,0:T(8,128)(2,1)S(1)}, bf16[336,1536]{1,0:T(8,128)(2,1)S(1)}, u32[]{:S(2)}, u32[]{:S(2)}) collective-permute-start(bf16[336,1536]{1,0:T(8,128)(2,1)S(1)} %half.1), channel_id=1, source_target_pairs={{0,17},{17,0},{1,16},{16,1},{2,19},{19,2},{3,18},{18,3},{4,21},{21... | collective-permute-start | bytes 3096584 | tf_op jit(solution)/shard_map/ppermute | solution.py:386
  7.3 5.1 %forward.1 = (f32[256,768]{1,0:T(8,128)}, bf16[256,768]{1,0:T(8,128)(2,1)}, bf16[256,1536]{1,0:T(8,128)(2,1)S(1)}) custom-call(bf16[2652,256]{1,0:T(8,128)(2,1)} %bitcast.10, bf16[2652,768]{1,0:T(8,128)(2,1)} %w_first_hbm.1, bf16[768,1536]{1,0:T(8,128)(2,1)} %w_middle_ref.1), custom_call_target="tpu_custom_call" | custom-call | flops 17179869184 | bytes 67108864 | tf_op jit(solution)/shard_map/forward/pallas_call | solution.py:73
  12.3 0.1 collective-permute-start
  12.4 1.0 collective-permute-start.7
  13.4 0.1 collective-permute-start.4
  13.5 1.1 copy-done.5
  14.6 4.9 %stage.1 = (bf16[663,1536]{1,0:T(8,128)(2,1)S(1)}, bf16[663,256]{1,0:T(8,128)(2,1)S(1)}, bf16[2,336,256]{2,1,0:T(8,128)(2,1)S(1)}, f32[768,256]{1,0:T(8,128)S(1)...) custom-call(s32[5]{0:T(128)S(1)} %stack.23.place_ref, s32[2]{0:T(128)S(1)} %copy-done.3, f32[256,768]{1,0:T(8,128)S(1)} %copy-done.5, ...), custom_call_target="tpu_custom_call" | custom-call | flops 17179869184 | bytes 67108864 | tf_op jit(solution)/shard_map/stage/pallas_call | solution.py:73
  19.5 10.3 %collective-permute-done.1.fetched_ref = bf16[336,1536]{1,0:T(8,128)(2,1)S(1)} collective-permute-done((bf16[336,1536]{1,0:T(8,128)(2,1)S(1)}, bf16[336,1536]{1,0:T(8,128)(2,1)S(1)}, u32[]{:S(2)}, u32[]{:S(2)}) %collective-permute-start.1) | collective-permute-done | bytes 1032224 | tf_op jit(solution)/shard_map/ppermute | solution.py:386
  29.9 1.1 collective-permute-start.2
  31.0 0.0 collective-permute-done.arrived_ref
  31.0 3.1 %hidden.1 = (bf16[256,1536]{1,0:T(8,128)(2,1)S(1)}, f32[256,1536]{1,0:T(8,128)S(1)}, f32[256,1536]{1,0:T(8,128)S(1)}, bf16[1431,256]{1,0:T(8,128)(2,1)S(1)}, bf16[768,256]{1,0:T(8,128)(2,1)S(1)}) custom-call(s32[5]{0:T(128)S(1)} %stack.23.place_ref, bf16[256,1536]{1,0:T(8,128)(2,1)S(1)} %get-tuple-element.82.partial_ref, ...), custom_call_target="tpu_custom_call" | custom-call | flops 17179869184 | bytes 67108864 | tf_op jit(solution)/shard_map/hidden/pallas_call | solution.py:73
  34.1 1.6 %collective-permute-start.6 = (bf16[1431,256]{1,0:T(8,128)(2,1)S(1)}, bf16[1431,256]{1,0:T(8,128)(2,1)S(1)}, u32[]{:S(2)}, u32[]{:S(2)}) collective-permute-start(bf16[1431,256]{1,0:T(8,128)(2,1)S(1)} %get-tuple-element.104.sent_ref), channel_id=1, source_target_pairs={{0,2},{2,0},{1,3},{3,1},{4,6},{6,4},{5,7},{7,5},{8,10},{10,8},{9,1... | collective-permute-start | bytes 2198024 | tf_op jit(solution)/shard_map/ppermute | solution.py:37
  35.7 0.0 collective-permute-done.2.relayed_ref
  35.7 4.3 %slopes.1 = (bf16[1152,256]{1,0:T(8,128)(2,1)S(1)}, bf16[1152,256]{1,0:T(8,128)(2,1)S(1)}) custom-call(s32[5]{0:T(128)S(1)} %stack.23.place_ref, bf16[256,1536]{1,0:T(8,128)(2,1)S(1)} %get-tuple-element.89.act_ref, f32[256,1536]{1,0:T(8,128)S(1)} %get-tuple-element.90.act_slope_ref, f32[256,1536]{1,0:T(8,128)S(1)} %get-tuple-element.91.back_ref, ...), custom_call_target="tpu_custom_call" | custom-call | flops 17179869184 | bytes 67108864 | tf_op jit(solution)/shard_map/slopes/pallas_call | solution.py:73
  40.0 0.1 collective-permute-start.3
  40.1 0.0 collective-permute-done.6.arrived_ref
  40.1 1.4 %last.1 = (f32[2,4,4,24,384]{4,3,2,1,0:T(8,128)S(1)}, bf16[2,4,4,24,384]{4,3,2,1,0:T(8,128)(2,1)S(1)}) custom-call(s32[5]{0:T(128)S(1)} %stack.23.place_ref, bf16[768,256]{1,0:T(8,128)(2,1)S(1)} %get-tuple-element.103.own_ref, bf16[1431,256]{1,0:T(8,128)(2,1)S(1)} %get-tuple-element.104.sent_ref, bf16[1431,256]{1,0:T(8,128)(2,1)S(1)} %collective-permute-done.6.arrived_ref), custom_call_target="tpu_custom_call" | custom-call | flops 17179869184 | bytes 67108864 | tf_op jit(solution)/shard_map/last/pallas_call | solution.py:73
  41.5 1.3 %collective-permute-start.9 = (bf16[2,4,4,24,384]{4,3,2,1,0:T(8,128)(2,1)S(1)}, bf16[2,4,4,24,384]{4,3,2,1,0:T(8,128)(2,1)S(1)}, u32[]{:S(2)}, u32[]{:S(2)}) collective-permute-start(bf16[2,4,4,24,384]{4,3,2,1,0:T(8,128)(2,1)S(1)} %get-tuple-element.105), channel_id=1, source_target_pairs={{0,4},{4,0},{8,12},{12,8},{1,5},{5,1},{9,13},{13,9},{2,6},{6,2},{1... | collective-permute-start | bytes 1769480 | tf_op jit(solution)/shard_map/ppermute | solution.py:42
  42.8 0.0 collective-permute-done.4.sibling_belief_ref
  42.8 2.1 %first.1 = (f32[2,4,4,24,384]{4,3,2,1,0:T(8,128)S(1)}, bf16[2,4,4,24,384]{4,3,2,1,0:T(8,128)(2,1)S(1)}, f32[2,4,3,24,384]{4,3,2,1,0:T(8,128)S(1)}, bf16[2,4,3,24,384]{4,3,2,1,0:T(8,128)(2,1)S(1)}) custom-call(s32[5]{0:T(128)S(1)} %stack.23.place_ref, bf16[1152,256]{1,0:T(8,128)(2,1)S(1)} %get-tuple-element.97.own_ref, ...), custom_call_target="tpu_custom_call" | custom-call | flops 17179869184 | bytes 67108864 | tf_op jit(solution)/shard_map/first/pallas_call | solution.py:73
  44.9 2.8 %collective-permute-start.11 = (bf16[2,4,3,24,384]{4,3,2,1,0:T(8,128)(2,1)S(1)}, bf16[2,4,3,24,384]{4,3,2,1,0:T(8,128)(2,1)S(1)}, u32[]{:S(2)}, u32[]{:S(2)}) collective-permute-start(bf16[2,4,3,24,384]{4,3,2,1,0:T(8,128)(2,1)S(1)} %get-tuple-element.108), channel_id=1, source_target_pairs={{0,96},{32,64},{64,32},{96,0},{1,97},{33,65},{65,33},{97,1},{2,98}... | collective-permute-start | bytes 1327112 | tf_op jit(solution)/shard_map/ppermute | solution.py:42
  47.8 1.3 %middle.1 = (f32[2,4,4,24,384]{4,3,2,1,0:T(8,128)S(1)}, bf16[2,4,4,24,384]{4,3,2,1,0:T(8,128)(2,1)S(1)}) custom-call(s32[5]{0:T(128)S(1)} %stack.23.place_ref, bf16[1152,256]{1,0:T(8,128)(2,1)S(1)} %get-tuple-element.97.own_ref, bf16[1152,256]{1,0:T(8,128)(2,1)S(1)} %collective-permute-done.3.arrived_ref, bf16[256,768]{1,0:T(8,128)(2,1)S(1)} %copy-done.2, ...), custom_call_target="tpu_custom_call" | custom-call | flops 17179869184 | bytes 67108864 | tf_op jit(solution)/shard_map/middle/pallas_call | solution.py:73
  49.1 1.9 %collective-permute-start.10 = (bf16[2,4,4,24,384]{4,3,2,1,0:T(8,128)(2,1)S(1)}, bf16[2,4,4,24,384]{4,3,2,1,0:T(8,128)(2,1)S(1)}, u32[]{:S(2)}, u32[]{:S(2)}) collective-permute-start(bf16[2,4,4,24,384]{4,3,2,1,0:T(8,128)(2,1)S(1)} %get-tuple-element.107), channel_id=1, source_target_pairs={{0,12},{4,8},{8,4},{12,0},{1,13},{5,9},{9,5},{13,1},{2,14},{6,10},... | collective-permute-start | bytes 1769480 | tf_op jit(solution)/shard_map/ppermute | solution.py:42
  51.0 0.0 collective-permute-start.5
  51.0 5.0 %collective-permute-done.9.arrived_ref = bf16[2,4,4,24,384]{4,3,2,1,0:T(8,128)(2,1)S(1)} collective-permute-done((bf16[2,4,4,24,384]{4,3,2,1,0:T(8,128)(2,1)S(1)}, bf16[2,4,4,24,384]{4,3,2,1,0:T(8,128)(2,1)S(1)}, u32[]{:S(2)}, u32[]{:S(2)}) %collective-permute-start.9) | collective-permute-done | bytes 589856 | tf_op jit(solution)/shard_map/ppermute | solution.py:42
  56.0 0.1 halve.9
  56.1 2.5 %collective-permute-start.13 = (bf16[4,4,24,384]{3,2,1,0:T(8,128)(2,1)S(1)}, bf16[4,4,24,384]{3,2,1,0:T(8,128)(2,1)S(1)}, u32[]{:S(2)}, u32[]{:S(2)}) collective-permute-start(bf16[4,4,24,384]{3,2,1,0:T(8,128)(2,1)S(1)} %get-tuple-element.114), channel_id=1, source_target_pairs={{0,12},{4,8},{8,4},{12,0},{1,13},{5,9},{9,5},{13,1},{2,14},{6,10},... | collective-permute-start | bytes 884744 | tf_op jit(solution)/shard_map/ppermute | solution.py:42
  58.7 0.1 halve.11
  58.8 1.4 %collective-permute-start.15 = (bf16[4,3,24,384]{3,2,1,0:T(8,128)(2,1)S(1)}, bf16[4,3,24,384]{3,2,1,0:T(8,128)(2,1)S(1)}, u32[]{:S(2)}, u32[]{:S(2)}) collective-permute-start(bf16[4,3,24,384]{3,2,1,0:T(8,128)(2,1)S(1)} %get-tuple-element.120), channel_id=1, source_target_pairs={{0,32},{32,0},{64,96},{96,64},{1,33},{33,1},{65,97},{97,65},{2,34}... | collective-permute-start | bytes 663560 | tf_op jit(solution)/shard_map/ppermute | solution.py:42
  60.1 4.0 %collective-permute-done.10.arrived_ref = bf16[2,4,4,24,384]{4,3,2,1,0:T(8,128)(2,1)S(1)} collective-permute-done((bf16[2,4,4,24,384]{4,3,2,1,0:T(8,128)(2,1)S(1)}, bf16[2,4,4,24,384]{4,3,2,1,0:T(8,128)(2,1)S(1)}, u32[]{:S(2)}, u32[]{:S(2)}) %collective-permute-start.10) | collective-permute-done | bytes 589856 | tf_op jit(solution)/shard_map/ppermute | solution.py:42
  64.1 0.4 collective-permute-done.5.arrived_ref
  64.5 0.1 halve.10
  64.6 0.4 collective-permute-start.14
  65.0 0.1 halve.8
  65.1 0.2 collective-permute-start.8
  65.3 5.2 %collective-permute-done.13.arrived_ref = bf16[4,4,24,384]{3,2,1,0:T(8,128)(2,1)S(1)} collective-permute-done((bf16[4,4,24,384]{3,2,1,0:T(8,128)(2,1)S(1)}, bf16[4,4,24,384]{3,2,1,0:T(8,128)(2,1)S(1)}, u32[]{:S(2)}, u32[]{:S(2)}) %collective-permute-start.13) | collective-permute-done | bytes 294944 | tf_op jit(solution)/shard_map/ppermute | solution.py:42
  70.5 0.6 turn.5
  71.1 0.1 collective-permute-start.17
  71.2 0.0 collective-permute-done.15.arrived_ref
  71.2 0.6 turn.7
  71.8 1.9 %collective-permute-start.19 = (bf16[2,3,24,384]{3,2,1,0:T(8,128)(2,1)S(1)}, bf16[2,3,24,384]{3,2,1,0:T(8,128)(2,1)S(1)}, u32[]{:S(2)}, u32[]{:S(2)}) collective-permute-start(bf16[2,3,24,384]{3,2,1,0:T(8,128)(2,1)S(1)} %get-tuple-element.132), channel_id=1, source_target_pairs={{0,12},{4,8},{8,4},{12,0},{1,13},{5,9},{9,5},{13,1},{2,14},{6,10},... | collective-permute-start | bytes 331784 | tf_op jit(solution)/shard_map/ppermute | solution.py:42
  73.7 0.0 collective-permute-done.14.arrived_ref
  73.7 0.0 collective-permute-done.8.arrived_ref
  73.7 0.6 turn.6
  74.3 0.7 collective-permute-start.18
  75.0 0.6 turn.4
  75.6 0.1 collective-permute-start.12
  75.8 1.2 %collective-permute-done.19.arrived_ref = bf16[2,3,24,384]{3,2,1,0:T(8,128)(2,1)S(1)} collective-permute-done((bf16[2,3,24,384]{3,2,1,0:T(8,128)(2,1)S(1)}, bf16[2,3,24,384]{3,2,1,0:T(8,128)(2,1)S(1)}, u32[]{:S(2)}, u32[]{:S(2)}) %collective-permute-start.19) | collective-permute-done | bytes 110624 | tf_op jit(solution)/shard_map/ppermute | solution.py:42
  77.0 1.0 collective-permute-start.21
  77.9 1.7 %collective-permute-done.18.arrived_ref = bf16[2,4,24,384]{3,2,1,0:T(8,128)(2,1)S(1)} collective-permute-done((bf16[2,4,24,384]{3,2,1,0:T(8,128)(2,1)S(1)}, bf16[2,4,24,384]{3,2,1,0:T(8,128)(2,1)S(1)}, u32[]{:S(2)}, u32[]{:S(2)}) %collective-permute-start.18) | collective-permute-done | bytes 147488 | tf_op jit(solution)/shard_map/ppermute | solution.py:42
  79.7 0.6 collective-permute-start.22
  80.3 0.7 collective-permute-start.16
  81.0 0.1 collective-permute-start.20
  81.1 0.3 collective-permute-done.21.refs_5_
  81.4 2.8 %collective-permute-done.20.refs_3_ = bf16[3,24,384]{2,1,0:T(8,128)(2,1)S(1)} collective-permute-done((bf16[3,24,384]{2,1,0:T(8,128)(2,1)S(1)}, bf16[3,24,384]{2,1,0:T(8,128)(2,1)S(1)}, u32[]{:S(2)}, u32[]{:S(2)}) %collective-permute-start.20) | collective-permute-done | bytes 55328 | tf_op jit(solution)/shard_map/ppermute | solution.py:42
  84.1 0.7 collective-permute-done.16.refs_1_
  84.8 0.6 z_cut.1
  85.5 1.0 collective-permute-start.23
  86.5 4.5 %collective-permute-done.23.arrived_ref = bf16[8,24,384]{2,1,0:T(8,128)(2,1)S(1)} collective-permute-done((bf16[8,24,384]{2,1,0:T(8,128)(2,1)S(1)}, bf16[8,24,384]{2,1,0:T(8,128)(2,1)S(1)}, u32[]{:S(2)}, u32[]{:S(2)}) %collective-permute-start.23) | collective-permute-done | bytes 147488 | tf_op jit(solution)/shard_map/ppermute | solution.py:37
  91.0 0.3 square.1
  91.3 23.2 %all_to_all.5.squares_ref = f32[128,1,128]{2,1,0:T(1,128)S(1)} all-to-all(f32[128,1,128]{2,1,0:T(1,128)S(1)} %get-tuple-element.155), channel_id=1, replica_groups=mesh['dp_0'=4,'dp_1'=2,'dp_2'=4,'dp_3'=2,'mp'=2] {'dp_0','dp_1','dp_2','..., dimensions={0} | all-to-all | bytes 131072 | tf_op jit(solution)/shard_map/all_to_all | solution.py:519
  114.4 0.9 scale.1
  (21 shorter events, 0.2 us)
Async XLA Ops:
  2.6 27.3 %collective-permute-start.1 = (bf16[336,1536]{1,0:T(8,128)(2,1)S(1)}, bf16[336,1536]{1,0:T(8,128)(2,1)S(1)}, u32[]{:S(2)}, u32[]{:S(2)}) collective-permute-start(bf16[336,1536]{1,0:T(8,128)(2,1)S(1)} %half.1), channel_id=1, source_target_pairs={{0,17},{17,0},{1,16},{16,1},{2,19},{19,2},{3,18},{18,3},{4,21},{21... | collective-permute-start | bytes 3096584 | tf_op jit(solution)/shard_map/ppermute | solution.py:386
  7.2 6.1 %copy-start.1 = (bf16[256,2652]{0,1:T(8,128)(2,1)S(1)}, bf16[256,2652]{0,1:T(8,128)(2,1)}, u32[]{:S(2)}) copy-start(bf16[256,2652]{0,1:T(8,128)(2,1)} %param.7) | copy-start | bytes 4073476
  7.2 6.2 %copy-start = (bf16[768,1536]{1,0:T(8,128)(2,1)S(1)}, bf16[768,1536]{1,0:T(8,128)(2,1)}, u32[]{:S(2)}) copy-start(bf16[768,1536]{1,0:T(8,128)(2,1)} %w_middle_ref.1) | copy-start | bytes 7077892
  7.2 6.2 %copy-start.3 = (s32[2]{0:T(128)S(1)}, s32[2]{0:T(128)}, u32[]{:S(2)}) copy-start(s32[2]{0:T(128)} %counts_ref.1) | copy-start | bytes 28
  7.2 6.2 %copy-start.4 = (s32[2,768,1]{2,1,0:T(8,128)S(1)}, s32[2,768,1]{2,1,0:T(8,128)}, u32[]{:S(2)}) copy-start(s32[2,768,1]{2,1,0:T(8,128)} %constant.21.clone.orders_ref) | copy-start | bytes 18436
  12.3 18.7 %collective-permute-start = (bf16[256,1536]{1,0:T(8,128)(2,1)S(1)}, bf16[256,1536]{1,0:T(8,128)(2,1)S(1)}, u32[]{:S(2)}, u32[]{:S(2)}) collective-permute-start(bf16[256,1536]{1,0:T(8,128)(2,1)S(1)} %get-tuple-element.82.partial_ref), channel_id=1, source_target_pairs={{0,1},{1,0},{2,3},{3,2},{4,5},{5,4},{6,7},{7,6},{8,9},{9,8},{10,11... | collective-permute-start | bytes 2359304 | tf_op jit(solution)/shard_map/ppermute | solution.py:37
  12.4 35.3 %collective-permute-start.7 = (bf16[256,768]{1,0:T(8,128)(2,1)}, bf16[256,768]{1,0:T(8,128)(2,1)S(1)}, u32[]{:S(2)}, u32[]{:S(2)}) collective-permute-start(bf16[256,768]{1,0:T(8,128)(2,1)} %get-tuple-element.106.act_ref), channel_id=1, source_target_pairs={{0,2},{2,0},{1,3},{3,1},{4,6},{6,4},{5,7},{7,5},{8,10},{10,8},{9,1... | collective-permute-start | bytes 1179656 | tf_op jit(solution)/shard_map/ppermute | solution.py:37
  13.4 29.4 %collective-permute-start.4 = (bf16[2652,256]{1,0:T(8,128)(2,1)S(1)}, bf16[2652,256]{1,0:T(8,128)(2,1)S(1)}, u32[]{:S(2)}, u32[]{:S(2)}) collective-permute-start(bf16[2652,256]{1,0:T(8,128)(2,1)S(1)} %bitcast.11), channel_id=1, source_target_pairs={{0,2},{2,0},{1,3},{3,1},{4,6},{6,4},{5,7},{7,5},{8,10},{10,8},{9,1... | collective-permute-start | bytes 4073480 | tf_op jit(solution)/shard_map/ppermute | solution.py:37
  13.5 1.1 copy-start.5
  29.9 5.9 %collective-permute-start.2 = (bf16[336,1536]{1,0:T(8,128)(2,1)S(1)}, bf16[336,1536]{1,0:T(8,128)(2,1)S(1)}, u32[]{:S(2)}, u32[]{:S(2)}) collective-permute-start(bf16[336,1536]{1,0:T(8,128)(2,1)S(1)} %collective-permute-done.1.fetched_ref), channel_id=1, source_target_pairs={{0,2},{2,0},{1,3},{3,1},{4,6},{6,4},{5,7},{7,5},{8,10},{10,8},{9,1... | collective-permute-start | bytes 3096584 | tf_op jit(solution)/shard_map/ppermute | solution.py:37
  34.1 6.0 %collective-permute-start.6 = (bf16[1431,256]{1,0:T(8,128)(2,1)S(1)}, bf16[1431,256]{1,0:T(8,128)(2,1)S(1)}, u32[]{:S(2)}, u32[]{:S(2)}) collective-permute-start(bf16[1431,256]{1,0:T(8,128)(2,1)S(1)} %get-tuple-element.104.sent_ref), channel_id=1, source_target_pairs={{0,2},{2,0},{1,3},{3,1},{4,6},{6,4},{5,7},{7,5},{8,10},{10,8},{9,1... | collective-permute-start | bytes 2198024 | tf_op jit(solution)/shard_map/ppermute | solution.py:37
  40.0 2.8 %collective-permute-start.3 = (bf16[1152,256]{1,0:T(8,128)(2,1)S(1)}, bf16[1152,256]{1,0:T(8,128)(2,1)S(1)}, u32[]{:S(2)}, u32[]{:S(2)}) collective-permute-start(bf16[1152,256]{1,0:T(8,128)(2,1)S(1)} %get-tuple-element.98), channel_id=1, source_target_pairs={{0,2},{2,0},{1,3},{3,1},{4,6},{6,4},{5,7},{7,5},{8,10},{10,8},{9,1... | collective-permute-start | bytes 1769480 | tf_op jit(solution)/shard_map/ppermute | solution.py:37
  41.5 6.3 %copy-start.2 = (bf16[256,768]{1,0:T(8,128)(2,1)S(1)}, bf16[256,768]{1,0:T(8,128)(2,1)}, u32[]{:S(2)}) copy-start(bf16[256,768]{1,0:T(8,128)(2,1)} %get-tuple-element.106.act_ref) | copy-start | bytes 1179652
  41.5 14.5 %collective-permute-start.9 = (bf16[2,4,4,24,384]{4,3,2,1,0:T(8,128)(2,1)S(1)}, bf16[2,4,4,24,384]{4,3,2,1,0:T(8,128)(2,1)S(1)}, u32[]{:S(2)}, u32[]{:S(2)}) collective-permute-start(bf16[2,4,4,24,384]{4,3,2,1,0:T(8,128)(2,1)S(1)} %get-tuple-element.105), channel_id=1, source_target_pairs={{0,4},{4,0},{8,12},{12,8},{1,5},{5,1},{9,13},{13,9},{2,6},{6,2},{1... | collective-permute-start | bytes 1769480 | tf_op jit(solution)/shard_map/ppermute | solution.py:42
  44.9 13.7 %collective-permute-start.11 = (bf16[2,4,3,24,384]{4,3,2,1,0:T(8,128)(2,1)S(1)}, bf16[2,4,3,24,384]{4,3,2,1,0:T(8,128)(2,1)S(1)}, u32[]{:S(2)}, u32[]{:S(2)}) collective-permute-start(bf16[2,4,3,24,384]{4,3,2,1,0:T(8,128)(2,1)S(1)} %get-tuple-element.108), channel_id=1, source_target_pairs={{0,96},{32,64},{64,32},{96,0},{1,97},{33,65},{65,33},{97,1},{2,98}... | collective-permute-start | bytes 1327112 | tf_op jit(solution)/shard_map/ppermute | solution.py:42
  49.1 15.1 %collective-permute-start.10 = (bf16[2,4,4,24,384]{4,3,2,1,0:T(8,128)(2,1)S(1)}, bf16[2,4,4,24,384]{4,3,2,1,0:T(8,128)(2,1)S(1)}, u32[]{:S(2)}, u32[]{:S(2)}) collective-permute-start(bf16[2,4,4,24,384]{4,3,2,1,0:T(8,128)(2,1)S(1)} %get-tuple-element.107), channel_id=1, source_target_pairs={{0,12},{4,8},{8,4},{12,0},{1,13},{5,9},{9,5},{13,1},{2,14},{6,10},... | collective-permute-start | bytes 1769480 | tf_op jit(solution)/shard_map/ppermute | solution.py:42
  51.0 13.5 %collective-permute-start.5 = (bf16[2,4,4,24,384]{4,3,2,1,0:T(8,128)(2,1)S(1)}, bf16[2,4,4,24,384]{4,3,2,1,0:T(8,128)(2,1)S(1)}, u32[]{:S(2)}, u32[]{:S(2)}) collective-permute-start(bf16[2,4,4,24,384]{4,3,2,1,0:T(8,128)(2,1)S(1)} %get-tuple-element.102), channel_id=1, source_target_pairs={{0,32},{32,0},{64,96},{96,64},{1,33},{33,1},{65,97},{97,65},{2,34}... | collective-permute-start | bytes 1769480 | tf_op jit(solution)/shard_map/ppermute | solution.py:42
  56.1 14.3 %collective-permute-start.13 = (bf16[4,4,24,384]{3,2,1,0:T(8,128)(2,1)S(1)}, bf16[4,4,24,384]{3,2,1,0:T(8,128)(2,1)S(1)}, u32[]{:S(2)}, u32[]{:S(2)}) collective-permute-start(bf16[4,4,24,384]{3,2,1,0:T(8,128)(2,1)S(1)} %get-tuple-element.114), channel_id=1, source_target_pairs={{0,12},{4,8},{8,4},{12,0},{1,13},{5,9},{9,5},{13,1},{2,14},{6,10},... | collective-permute-start | bytes 884744 | tf_op jit(solution)/shard_map/ppermute | solution.py:42
  58.8 12.4 %collective-permute-start.15 = (bf16[4,3,24,384]{3,2,1,0:T(8,128)(2,1)S(1)}, bf16[4,3,24,384]{3,2,1,0:T(8,128)(2,1)S(1)}, u32[]{:S(2)}, u32[]{:S(2)}) collective-permute-start(bf16[4,3,24,384]{3,2,1,0:T(8,128)(2,1)S(1)} %get-tuple-element.120), channel_id=1, source_target_pairs={{0,32},{32,0},{64,96},{96,64},{1,33},{33,1},{65,97},{97,65},{2,34}... | collective-permute-start | bytes 663560 | tf_op jit(solution)/shard_map/ppermute | solution.py:42
  64.6 9.1 %collective-permute-start.14 = (bf16[4,4,24,384]{3,2,1,0:T(8,128)(2,1)S(1)}, bf16[4,4,24,384]{3,2,1,0:T(8,128)(2,1)S(1)}, u32[]{:S(2)}, u32[]{:S(2)}) collective-permute-start(bf16[4,4,24,384]{3,2,1,0:T(8,128)(2,1)S(1)} %get-tuple-element.117), channel_id=1, source_target_pairs={{0,4},{4,0},{8,12},{12,8},{1,5},{5,1},{9,13},{13,9},{2,6},{6,2},{1... | collective-permute-start | bytes 884744 | tf_op jit(solution)/shard_map/ppermute | solution.py:42
  65.1 8.6 %collective-permute-start.8 = (bf16[4,4,24,384]{3,2,1,0:T(8,128)(2,1)S(1)}, bf16[4,4,24,384]{3,2,1,0:T(8,128)(2,1)S(1)}, u32[]{:S(2)}, u32[]{:S(2)}) collective-permute-start(bf16[4,4,24,384]{3,2,1,0:T(8,128)(2,1)S(1)} %get-tuple-element.111), channel_id=1, source_target_pairs={{0,96},{32,64},{64,32},{96,0},{1,97},{33,65},{65,33},{97,1},{2,98}... | collective-permute-start | bytes 884744 | tf_op jit(solution)/shard_map/ppermute | solution.py:42
  71.1 4.7 %collective-permute-start.17 = (bf16[2,4,24,384]{3,2,1,0:T(8,128)(2,1)S(1)}, bf16[2,4,24,384]{3,2,1,0:T(8,128)(2,1)S(1)}, u32[]{:S(2)}, u32[]{:S(2)}) collective-permute-start(bf16[2,4,24,384]{3,2,1,0:T(8,128)(2,1)S(1)} %get-tuple-element.126), channel_id=1, source_target_pairs={{0,32},{32,0},{64,96},{96,64},{1,33},{33,1},{65,97},{97,65},{2,34}... | collective-permute-start | bytes 442376 | tf_op jit(solution)/shard_map/ppermute | solution.py:42
  71.8 5.2 %collective-permute-start.19 = (bf16[2,3,24,384]{3,2,1,0:T(8,128)(2,1)S(1)}, bf16[2,3,24,384]{3,2,1,0:T(8,128)(2,1)S(1)}, u32[]{:S(2)}, u32[]{:S(2)}) collective-permute-start(bf16[2,3,24,384]{3,2,1,0:T(8,128)(2,1)S(1)} %get-tuple-element.132), channel_id=1, source_target_pairs={{0,12},{4,8},{8,4},{12,0},{1,13},{5,9},{9,5},{13,1},{2,14},{6,10},... | collective-permute-start | bytes 331784 | tf_op jit(solution)/shard_map/ppermute | solution.py:42
  74.3 5.3 %collective-permute-start.18 = (bf16[2,4,24,384]{3,2,1,0:T(8,128)(2,1)S(1)}, bf16[2,4,24,384]{3,2,1,0:T(8,128)(2,1)S(1)}, u32[]{:S(2)}, u32[]{:S(2)}) collective-permute-start(bf16[2,4,24,384]{3,2,1,0:T(8,128)(2,1)S(1)} %get-tuple-element.129), channel_id=1, source_target_pairs={{0,96},{32,64},{64,32},{96,0},{1,97},{33,65},{65,33},{97,1},{2,98}... | collective-permute-start | bytes 442376 | tf_op jit(solution)/shard_map/ppermute | solution.py:42
  75.6 4.6 %collective-permute-start.12 = (bf16[2,4,24,384]{3,2,1,0:T(8,128)(2,1)S(1)}, bf16[2,4,24,384]{3,2,1,0:T(8,128)(2,1)S(1)}, u32[]{:S(2)}, u32[]{:S(2)}) collective-permute-start(bf16[2,4,24,384]{3,2,1,0:T(8,128)(2,1)S(1)} %get-tuple-element.123), channel_id=1, source_target_pairs={{0,4},{4,0},{8,12},{12,8},{1,5},{5,1},{9,13},{13,9},{2,6},{6,2},{1... | collective-permute-start | bytes 442376 | tf_op jit(solution)/shard_map/ppermute | solution.py:42
  77.0 4.4 %collective-permute-start.21 = (bf16[4,24,384]{2,1,0:T(8,128)(2,1)S(1)}, bf16[4,24,384]{2,1,0:T(8,128)(2,1)S(1)}, u32[]{:S(2)}, u32[]{:S(2)}) collective-permute-start(bf16[4,24,384]{2,1,0:T(8,128)(2,1)S(1)} %get-tuple-element.138), channel_id=1, source_target_pairs={{0,96},{32,64},{64,32},{96,0},{1,97},{33,65},{65,33},{97,1},{2,98}... | collective-permute-start | bytes 221192 | tf_op jit(solution)/shard_map/ppermute | solution.py:42
  79.7 4.5 %collective-permute-start.22 = (bf16[4,24,384]{2,1,0:T(8,128)(2,1)S(1)}, bf16[4,24,384]{2,1,0:T(8,128)(2,1)S(1)}, u32[]{:S(2)}, u32[]{:S(2)}) collective-permute-start(bf16[4,24,384]{2,1,0:T(8,128)(2,1)S(1)} %get-tuple-element.141), channel_id=1, source_target_pairs={{0,32},{32,0},{64,96},{96,64},{1,33},{33,1},{65,97},{97,65},{2,34}... | collective-permute-start | bytes 221192 | tf_op jit(solution)/shard_map/ppermute | solution.py:42
  80.3 4.5 %collective-permute-start.16 = (bf16[4,24,384]{2,1,0:T(8,128)(2,1)S(1)}, bf16[4,24,384]{2,1,0:T(8,128)(2,1)S(1)}, u32[]{:S(2)}, u32[]{:S(2)}) collective-permute-start(bf16[4,24,384]{2,1,0:T(8,128)(2,1)S(1)} %get-tuple-element.135), channel_id=1, source_target_pairs={{0,12},{4,8},{8,4},{12,0},{1,13},{5,9},{9,5},{13,1},{2,14},{6,10},... | collective-permute-start | bytes 221192 | tf_op jit(solution)/shard_map/ppermute | solution.py:42
  81.0 3.1 %collective-permute-start.20 = (bf16[3,24,384]{2,1,0:T(8,128)(2,1)S(1)}, bf16[3,24,384]{2,1,0:T(8,128)(2,1)S(1)}, u32[]{:S(2)}, u32[]{:S(2)}) collective-permute-start(bf16[3,24,384]{2,1,0:T(8,128)(2,1)S(1)} %get-tuple-element.144), channel_id=1, source_target_pairs={{0,4},{4,0},{8,12},{12,8},{1,5},{5,1},{9,13},{13,9},{2,6},{6,2},{1... | collective-permute-start | bytes 165896 | tf_op jit(solution)/shard_map/ppermute | solution.py:42
  85.5 5.6 %collective-permute-start.23 = (bf16[8,24,384]{2,1,0:T(8,128)(2,1)S(1)}, bf16[8,24,384]{2,1,0:T(8,128)(2,1)S(1)}, u32[]{:S(2)}, u32[]{:S(2)}) collective-permute-start(bf16[8,24,384]{2,1,0:T(8,128)(2,1)S(1)} %get-tuple-element.153), channel_id=1, source_target_pairs={{0,16},{16,0},{1,17},{17,1},{2,18},{18,2},{3,19},{19,3},{4,20},{20... | collective-permute-start | bytes 442376 | tf_op jit(solution)/shard_map/ppermute | solution.py:37

commit v16 on v15

--- a/solution.py
+++ b/solution.py
@@ -285,7 +285,7 @@
 def first_kernel(place_ref, own_ref, arrived_ref, belief_ref, sibling_belief_ref, *out_refs):
     start_row = own_ref.shape[0] // 3 * 2
     cuts = column_cuts(belief_ref.shape[0])
-    for order, part in enumerate((cuts[0:4], cuts[4:7])):
+    for order, part in enumerate((cuts[0:3], cuts[3:7])):
         kept, sent = kept_and_sent(place_ref[1], order)
         own, arrived = (
             jnp.concatenate(
@@ -330,7 +330,7 @@
     )
     last_sum[...] = last
     middle_sum[...] = middle
-    rows = [low[granule] for granule in range(4)] + [high[granule] for granule in range(3)]
+    rows = [low[granule] for granule in range(3)] + [high[granule] for granule in range(4)]
     for side, out_ref in ((1 - z_hi, sent_ref), (z_hi, own_ref)):
         kind = out_ref.dtype
         out_ref[0:2] = last_sum[pl.ds(2 * side, 2)].astype(kind)
@@ -491,7 +491,7 @@
         first_kernel,
         "first",
         [SMEM] + [VMEM] * 4,
-        pairs((2, 4, 4), (2, 4, 3)),
+        pairs((2, 4, 3), (2, 4, 4)),
     )(place, slopes_own, slopes_arrived, belief_t, sibling_belief)
     middle_parts = call(
         middle_kernel, "middle", [SMEM] + [VMEM] * 4, pairs((2, 4, 4))

time: 116 us -> 115 us (level)
  blocking collectives: 23.2 us -> 21.3 us
  waiting for transfers between devices: 36 us -> 37.4 us
    all_to_all x1, blocking collectives: 23.2 us -> 21.3 us  [per_device(): squares = lax.all_to_all(squares, ALL, 0, 0, tiled=True)]
    ppermute x16, waiting for transfers between devices: 21.1 us -> 22.4 us  [to_pair(): return lax.ppermute(shard, axis, pairs)]
  transfers between devices with their start and end apart: 24 -> 24, of which waited for: 11 -> 8; matrix products, arithmetic and copies ran while one was open for 0% -> 0% of each run, Pallas kernels for 22% -> 22%
where the time goes in v16:
time: 115 us
  waiting for transfers between devices  37.4 us (33%)
  Pallas kernels  28.8 us (25%)
  starting transfers between devices  25.4 us (22%)
  blocking collectives  21.3 us (19%)
  local copies, waits for them, and re-layouts  1.24 us (1%)
    pallas_call x23, Pallas kernels, run(): kernel(*(operand if spec is SMEM else pltpu.with_memory_space_constraint(...  28.8 us
    ppermute x16, waiting for transfers between devices, to_pair(): return lax.ppermute(shard, axis, pairs)  22.4 us
    all_to_all x1, blocking collectives, per_device(): squares = lax.all_to_all(squares, ALL, 0, 0, tiled=True)  21.3 us
    ppermute x16, starting transfers between devices, to_pair(): return lax.ppermute(shard, axis, pairs)  15.7 us
    ppermute x1, waiting for transfers between devices, per_device(): fetched = lax.ppermute(half, (ZH, 'mp'), [(0, 3), (3, 0), (1, 2), (2, 1)])  10.3 us
    ppermute x7, starting transfers between devices, swap(): return lax.ppermute(shard, axis, [(0, 1), (1, 0)])  5.01 us
    ppermute x1, starting transfers between devices, per_device(): fetched = lax.ppermute(half, (ZH, 'mp'), [(0, 3), (3, 0), (1, 2), (2, 1)])  4.67 us
    ppermute x7, waiting for transfers between devices, swap(): return lax.ppermute(shard, axis, [(0, 1), (1, 0)])  4.58 us
  transfers between devices with their start and end apart: 24, of which 8 were waited for; matrix products, arithmetic and copies ran while one was open for 0% of the time, Pallas kernels for 22%

profile of v16, /device:TPU:1, one launch (start us, length us, event | category | flops | bytes accessed | tf_op | source)
XLA Modules:
  0.0 114.9 jit_solution(7074295293767538569)
XLA Ops:
  0.6 0.1 stack.23.place_ref
  0.7 1.8 %half.1 = bf16[336,1536]{1,0:T(8,128)(2,1)S(1)} custom-call(s32[5]{0:T(128)S(1)} %stack.23.place_ref, bf16[663,1536]{1,0:T(8,128)(2,1)} %bitcast.13), custom_call_target="tpu_custom_call" | custom-call | flops 17179869184 | bytes 67108864 | tf_op jit(solution)/shard_map/half/pallas_call | solution.py:73
  2.6 4.7 %collective-permute-start.1 = (bf16[336,1536]{1,0:T(8,128)(2,1)S(1)}, bf16[336,1536]{1,0:T(8,128)(2,1)S(1)}, u32[]{:S(2)}, u32[]{:S(2)}) collective-permute-start(bf16[336,1536]{1,0:T(8,128)(2,1)S(1)} %half.1), channel_id=1, source_target_pairs={{0,17},{17,0},{1,16},{16,1},{2,19},{19,2},{3,18},{18,3},{4,21},{21... | collective-permute-start | bytes 3096584 | tf_op jit(solution)/shard_map/ppermute | solution.py:386
  7.3 5.1 %forward.1 = (f32[256,768]{1,0:T(8,128)}, bf16[256,768]{1,0:T(8,128)(2,1)}, bf16[256,1536]{1,0:T(8,128)(2,1)S(1)}) custom-call(bf16[2652,256]{1,0:T(8,128)(2,1)} %bitcast.10, bf16[2652,768]{1,0:T(8,128)(2,1)} %w_first_hbm.1, bf16[768,1536]{1,0:T(8,128)(2,1)} %w_middle_ref.1), custom_call_target="tpu_custom_call" | custom-call | flops 17179869184 | bytes 67108864 | tf_op jit(solution)/shard_map/forward/pallas_call | solution.py:73
  12.3 0.1 collective-permute-start
  12.4 1.0 collective-permute-start.7
  13.4 0.1 collective-permute-start.4
  13.5 1.1 copy-done.5
  14.6 4.9 %stage.1 = (bf16[663,1536]{1,0:T(8,128)(2,1)S(1)}, bf16[663,256]{1,0:T(8,128)(2,1)S(1)}, bf16[2,336,256]{2,1,0:T(8,128)(2,1)S(1)}, f32[768,256]{1,0:T(8,128)S(1)...) custom-call(s32[5]{0:T(128)S(1)} %stack.23.place_ref, s32[2]{0:T(128)S(1)} %copy-done.3, f32[256,768]{1,0:T(8,128)S(1)} %copy-done.5, ...), custom_call_target="tpu_custom_call" | custom-call | flops 17179869184 | bytes 67108864 | tf_op jit(solution)/shard_map/stage/pallas_call | solution.py:73
  19.5 10.3 %collective-permute-done.1.fetched_ref = bf16[336,1536]{1,0:T(8,128)(2,1)S(1)} collective-permute-done((bf16[336,1536]{1,0:T(8,128)(2,1)S(1)}, bf16[336,1536]{1,0:T(8,128)(2,1)S(1)}, u32[]{:S(2)}, u32[]{:S(2)}) %collective-permute-start.1) | collective-permute-done | bytes 1032224 | tf_op jit(solution)/shard_map/ppermute | solution.py:386
  29.9 1.1 collective-permute-start.2
  31.0 0.0 collective-permute-done.arrived_ref
  31.0 3.1 %hidden.1 = (bf16[256,1536]{1,0:T(8,128)(2,1)S(1)}, f32[256,1536]{1,0:T(8,128)S(1)}, f32[256,1536]{1,0:T(8,128)S(1)}, bf16[1431,256]{1,0:T(8,128)(2,1)S(1)}, bf16[768,256]{1,0:T(8,128)(2,1)S(1)}) custom-call(s32[5]{0:T(128)S(1)} %stack.23.place_ref, bf16[256,1536]{1,0:T(8,128)(2,1)S(1)} %get-tuple-element.82.partial_ref, ...), custom_call_target="tpu_custom_call" | custom-call | flops 17179869184 | bytes 67108864 | tf_op jit(solution)/shard_map/hidden/pallas_call | solution.py:73
  34.1 1.6 %collective-permute-start.6 = (bf16[1431,256]{1,0:T(8,128)(2,1)S(1)}, bf16[1431,256]{1,0:T(8,128)(2,1)S(1)}, u32[]{:S(2)}, u32[]{:S(2)}) collective-permute-start(bf16[1431,256]{1,0:T(8,128)(2,1)S(1)} %get-tuple-element.104.sent_ref), channel_id=1, source_target_pairs={{0,2},{2,0},{1,3},{3,1},{4,6},{6,4},{5,7},{7,5},{8,10},{10,8},{9,1... | collective-permute-start | bytes 2198024 | tf_op jit(solution)/shard_map/ppermute | solution.py:37
  35.7 0.0 collective-permute-done.2.relayed_ref
  35.7 4.3 %slopes.1 = (bf16[1152,256]{1,0:T(8,128)(2,1)S(1)}, bf16[1152,256]{1,0:T(8,128)(2,1)S(1)}) custom-call(s32[5]{0:T(128)S(1)} %stack.23.place_ref, bf16[256,1536]{1,0:T(8,128)(2,1)S(1)} %get-tuple-element.89.act_ref, f32[256,1536]{1,0:T(8,128)S(1)} %get-tuple-element.90.act_slope_ref, f32[256,1536]{1,0:T(8,128)S(1)} %get-tuple-element.91.back_ref, ...), custom_call_target="tpu_custom_call" | custom-call | flops 17179869184 | bytes 67108864 | tf_op jit(solution)/shard_map/slopes/pallas_call | solution.py:73
  40.0 0.1 collective-permute-start.3
  40.1 0.0 collective-permute-done.6.arrived_ref
  40.1 1.4 %last.1 = (f32[2,4,4,24,384]{4,3,2,1,0:T(8,128)S(1)}, bf16[2,4,4,24,384]{4,3,2,1,0:T(8,128)(2,1)S(1)}) custom-call(s32[5]{0:T(128)S(1)} %stack.23.place_ref, bf16[768,256]{1,0:T(8,128)(2,1)S(1)} %get-tuple-element.103.own_ref, bf16[1431,256]{1,0:T(8,128)(2,1)S(1)} %get-tuple-element.104.sent_ref, bf16[1431,256]{1,0:T(8,128)(2,1)S(1)} %collective-permute-done.6.arrived_ref), custom_call_target="tpu_custom_call" | custom-call | flops 17179869184 | bytes 67108864 | tf_op jit(solution)/shard_map/last/pallas_call | solution.py:73
  41.5 1.3 %collective-permute-start.9 = (bf16[2,4,4,24,384]{4,3,2,1,0:T(8,128)(2,1)S(1)}, bf16[2,4,4,24,384]{4,3,2,1,0:T(8,128)(2,1)S(1)}, u32[]{:S(2)}, u32[]{:S(2)}) collective-permute-start(bf16[2,4,4,24,384]{4,3,2,1,0:T(8,128)(2,1)S(1)} %get-tuple-element.105), channel_id=1, source_target_pairs={{0,4},{4,0},{8,12},{12,8},{1,5},{5,1},{9,13},{13,9},{2,6},{6,2},{1... | collective-permute-start | bytes 1769480 | tf_op jit(solution)/shard_map/ppermute | solution.py:42
  42.8 0.0 collective-permute-done.4.sibling_belief_ref
  42.8 2.1 %first.1 = (f32[2,4,3,24,384]{4,3,2,1,0:T(8,128)S(1)}, bf16[2,4,3,24,384]{4,3,2,1,0:T(8,128)(2,1)S(1)}, f32[2,4,4,24,384]{4,3,2,1,0:T(8,128)S(1)}, bf16[2,4,4,24,384]{4,3,2,1,0:T(8,128)(2,1)S(1)}) custom-call(s32[5]{0:T(128)S(1)} %stack.23.place_ref, bf16[1152,256]{1,0:T(8,128)(2,1)S(1)} %get-tuple-element.97.own_ref, ...), custom_call_target="tpu_custom_call" | custom-call | flops 17179869184 | bytes 67108864 | tf_op jit(solution)/shard_map/first/pallas_call | solution.py:73
  44.9 2.8 %collective-permute-start.11 = (bf16[2,4,4,24,384]{4,3,2,1,0:T(8,128)(2,1)S(1)}, bf16[2,4,4,24,384]{4,3,2,1,0:T(8,128)(2,1)S(1)}, u32[]{:S(2)}, u32[]{:S(2)}) collective-permute-start(bf16[2,4,4,24,384]{4,3,2,1,0:T(8,128)(2,1)S(1)} %get-tuple-element.108), channel_id=1, source_target_pairs={{0,96},{32,64},{64,32},{96,0},{1,97},{33,65},{65,33},{97,1},{2,98}... | collective-permute-start | bytes 1769480 | tf_op jit(solution)/shard_map/ppermute | solution.py:42
  47.8 1.3 %middle.1 = (f32[2,4,4,24,384]{4,3,2,1,0:T(8,128)S(1)}, bf16[2,4,4,24,384]{4,3,2,1,0:T(8,128)(2,1)S(1)}) custom-call(s32[5]{0:T(128)S(1)} %stack.23.place_ref, bf16[1152,256]{1,0:T(8,128)(2,1)S(1)} %get-tuple-element.97.own_ref, bf16[1152,256]{1,0:T(8,128)(2,1)S(1)} %collective-permute-done.3.arrived_ref, bf16[256,768]{1,0:T(8,128)(2,1)S(1)} %copy-done.2, ...), custom_call_target="tpu_custom_call" | custom-call | flops 17179869184 | bytes 67108864 | tf_op jit(solution)/shard_map/middle/pallas_call | solution.py:73
  49.1 1.9 %collective-permute-start.10 = (bf16[2,4,4,24,384]{4,3,2,1,0:T(8,128)(2,1)S(1)}, bf16[2,4,4,24,384]{4,3,2,1,0:T(8,128)(2,1)S(1)}, u32[]{:S(2)}, u32[]{:S(2)}) collective-permute-start(bf16[2,4,4,24,384]{4,3,2,1,0:T(8,128)(2,1)S(1)} %get-tuple-element.107), channel_id=1, source_target_pairs={{0,12},{4,8},{8,4},{12,0},{1,13},{5,9},{9,5},{13,1},{2,14},{6,10},... | collective-permute-start | bytes 1769480 | tf_op jit(solution)/shard_map/ppermute | solution.py:42
  51.0 0.0 collective-permute-start.5
  51.0 5.0 %collective-permute-done.9.arrived_ref = bf16[2,4,4,24,384]{4,3,2,1,0:T(8,128)(2,1)S(1)} collective-permute-done((bf16[2,4,4,24,384]{4,3,2,1,0:T(8,128)(2,1)S(1)}, bf16[2,4,4,24,384]{4,3,2,1,0:T(8,128)(2,1)S(1)}, u32[]{:S(2)}, u32[]{:S(2)}) %collective-permute-start.9) | collective-permute-done | bytes 589856 | tf_op jit(solution)/shard_map/ppermute | solution.py:42
  56.0 0.1 halve.9
  56.1 2.5 %collective-permute-start.13 = (bf16[4,4,24,384]{3,2,1,0:T(8,128)(2,1)S(1)}, bf16[4,4,24,384]{3,2,1,0:T(8,128)(2,1)S(1)}, u32[]{:S(2)}, u32[]{:S(2)}) collective-permute-start(bf16[4,4,24,384]{3,2,1,0:T(8,128)(2,1)S(1)} %get-tuple-element.114), channel_id=1, source_target_pairs={{0,12},{4,8},{8,4},{12,0},{1,13},{5,9},{9,5},{13,1},{2,14},{6,10},... | collective-permute-start | bytes 884744 | tf_op jit(solution)/shard_map/ppermute | solution.py:42
  58.7 2.7 %collective-permute-done.5.arrived_ref = bf16[2,4,3,24,384]{4,3,2,1,0:T(8,128)(2,1)S(1)} collective-permute-done((bf16[2,4,3,24,384]{4,3,2,1,0:T(8,128)(2,1)S(1)}, bf16[2,4,3,24,384]{4,3,2,1,0:T(8,128)(2,1)S(1)}, u32[]{:S(2)}, u32[]{:S(2)}) %collective-permute-start.5) | collective-permute-done | bytes 442400 | tf_op jit(solution)/shard_map/ppermute | solution.py:42
  61.3 0.1 halve.8
  61.4 0.2 collective-permute-start.8
  61.6 0.0 collective-permute-done.11.arrived_ref
  61.6 0.1 halve.11
  61.8 0.1 collective-permute-start.15
  61.9 2.2 %collective-permute-done.10.arrived_ref = bf16[2,4,4,24,384]{4,3,2,1,0:T(8,128)(2,1)S(1)} collective-permute-done((bf16[2,4,4,24,384]{4,3,2,1,0:T(8,128)(2,1)S(1)}, bf16[2,4,4,24,384]{4,3,2,1,0:T(8,128)(2,1)S(1)}, u32[]{:S(2)}, u32[]{:S(2)}) %collective-permute-start.10) | collective-permute-done | bytes 589856 | tf_op jit(solution)/shard_map/ppermute | solution.py:42
  64.1 0.1 halve.10
  64.2 0.1 collective-permute-start.14
  64.3 6.1 %collective-permute-done.13.arrived_ref = bf16[4,4,24,384]{3,2,1,0:T(8,128)(2,1)S(1)} collective-permute-done((bf16[4,4,24,384]{3,2,1,0:T(8,128)(2,1)S(1)}, bf16[4,4,24,384]{3,2,1,0:T(8,128)(2,1)S(1)}, u32[]{:S(2)}, u32[]{:S(2)}) %collective-permute-start.13) | collective-permute-done | bytes 294944 | tf_op jit(solution)/shard_map/ppermute | solution.py:42
  70.5 0.6 turn.5
  71.1 0.1 collective-permute-start.17
  71.2 0.0 collective-permute-done.8.arrived_ref
  71.2 0.6 turn.4
  71.8 0.1 collective-permute-start.12
  71.9 0.0 collective-permute-done.15.arrived_ref
  71.9 0.6 turn.7
  72.5 1.9 %collective-permute-start.19 = (bf16[2,4,24,384]{3,2,1,0:T(8,128)(2,1)S(1)}, bf16[2,4,24,384]{3,2,1,0:T(8,128)(2,1)S(1)}, u32[]{:S(2)}, u32[]{:S(2)}) collective-permute-start(bf16[2,4,24,384]{3,2,1,0:T(8,128)(2,1)S(1)} %get-tuple-element.132), channel_id=1, source_target_pairs={{0,12},{4,8},{8,4},{12,0},{1,13},{5,9},{9,5},{13,1},{2,14},{6,10},... | collective-permute-start | bytes 442376 | tf_op jit(solution)/shard_map/ppermute | solution.py:42
  74.4 0.0 collective-permute-done.14.arrived_ref
  74.4 0.6 turn.6
  75.0 0.7 collective-permute-start.18
  75.7 0.0 collective-permute-done.17.arrived_ref
  75.8 2.1 %collective-permute-start.21 = (bf16[4,24,384]{2,1,0:T(8,128)(2,1)S(1)}, bf16[4,24,384]{2,1,0:T(8,128)(2,1)S(1)}, u32[]{:S(2)}, u32[]{:S(2)}) collective-permute-start(bf16[4,24,384]{2,1,0:T(8,128)(2,1)S(1)} %get-tuple-element.138), channel_id=1, source_target_pairs={{0,96},{32,64},{64,32},{96,0},{1,97},{33,65},{65,33},{97,1},{2,98}... | collective-permute-start | bytes 221192 | tf_op jit(solution)/shard_map/ppermute | solution.py:42
  77.9 2.7 %collective-permute-done.18.arrived_ref = bf16[2,4,24,384]{3,2,1,0:T(8,128)(2,1)S(1)} collective-permute-done((bf16[2,4,24,384]{3,2,1,0:T(8,128)(2,1)S(1)}, bf16[2,4,24,384]{3,2,1,0:T(8,128)(2,1)S(1)}, u32[]{:S(2)}, u32[]{:S(2)}) %collective-permute-start.18) | collective-permute-done | bytes 147488 | tf_op jit(solution)/shard_map/ppermute | solution.py:42
  80.7 0.3 collective-permute-start.22
  81.0 0.9 collective-permute-start.20
  82.0 0.6 collective-permute-start.16
  82.6 0.0 collective-permute-done.21.refs_5_
  82.6 3.7 %collective-permute-done.16.refs_1_ = bf16[3,24,384]{2,1,0:T(8,128)(2,1)S(1)} collective-permute-done((bf16[3,24,384]{2,1,0:T(8,128)(2,1)S(1)}, bf16[3,24,384]{2,1,0:T(8,128)(2,1)S(1)}, u32[]{:S(2)}, u32[]{:S(2)}) %collective-permute-start.16) | collective-permute-done | bytes 55328 | tf_op jit(solution)/shard_map/ppermute | solution.py:42
  86.3 0.6 z_cut.1
  86.9 1.0 collective-permute-start.23
  87.9 4.6 %collective-permute-done.23.arrived_ref = bf16[8,24,384]{2,1,0:T(8,128)(2,1)S(1)} collective-permute-done((bf16[8,24,384]{2,1,0:T(8,128)(2,1)S(1)}, bf16[8,24,384]{2,1,0:T(8,128)(2,1)S(1)}, u32[]{:S(2)}, u32[]{:S(2)}) %collective-permute-start.23) | collective-permute-done | bytes 147488 | tf_op jit(solution)/shard_map/ppermute | solution.py:37
  92.5 0.3 square.1
  92.8 21.3 %all_to_all.5.squares_ref = f32[128,1,128]{2,1,0:T(1,128)S(1)} all-to-all(f32[128,1,128]{2,1,0:T(1,128)S(1)} %get-tuple-element.155), channel_id=1, replica_groups=mesh['dp_0'=4,'dp_1'=2,'dp_2'=4,'dp_3'=2,'mp'=2] {'dp_0','dp_1','dp_2','..., dimensions={0} | all-to-all | bytes 131072 | tf_op jit(solution)/shard_map/all_to_all | solution.py:519
  114.0 0.9 scale.1
  (21 shorter events, 0.2 us)
Async XLA Ops:
  2.6 27.3 %collective-permute-start.1 = (bf16[336,1536]{1,0:T(8,128)(2,1)S(1)}, bf16[336,1536]{1,0:T(8,128)(2,1)S(1)}, u32[]{:S(2)}, u32[]{:S(2)}) collective-permute-start(bf16[336,1536]{1,0:T(8,128)(2,1)S(1)} %half.1), channel_id=1, source_target_pairs={{0,17},{17,0},{1,16},{16,1},{2,19},{19,2},{3,18},{18,3},{4,21},{21... | collective-permute-start | bytes 3096584 | tf_op jit(solution)/shard_map/ppermute | solution.py:386
  7.2 6.1 %copy-start.1 = (bf16[256,2652]{0,1:T(8,128)(2,1)S(1)}, bf16[256,2652]{0,1:T(8,128)(2,1)}, u32[]{:S(2)}) copy-start(bf16[256,2652]{0,1:T(8,128)(2,1)} %param.7) | copy-start | bytes 4073476
  7.2 6.2 %copy-start = (bf16[768,1536]{1,0:T(8,128)(2,1)S(1)}, bf16[768,1536]{1,0:T(8,128)(2,1)}, u32[]{:S(2)}) copy-start(bf16[768,1536]{1,0:T(8,128)(2,1)} %w_middle_ref.1) | copy-start | bytes 7077892
  7.2 6.2 %copy-start.3 = (s32[2]{0:T(128)S(1)}, s32[2]{0:T(128)}, u32[]{:S(2)}) copy-start(s32[2]{0:T(128)} %counts_ref.1) | copy-start | bytes 28
  7.2 6.2 %copy-start.4 = (s32[2,768,1]{2,1,0:T(8,128)S(1)}, s32[2,768,1]{2,1,0:T(8,128)}, u32[]{:S(2)}) copy-start(s32[2,768,1]{2,1,0:T(8,128)} %constant.21.clone.orders_ref) | copy-start | bytes 18436
  12.3 18.7 %collective-permute-start = (bf16[256,1536]{1,0:T(8,128)(2,1)S(1)}, bf16[256,1536]{1,0:T(8,128)(2,1)S(1)}, u32[]{:S(2)}, u32[]{:S(2)}) collective-permute-start(bf16[256,1536]{1,0:T(8,128)(2,1)S(1)} %get-tuple-element.82.partial_ref), channel_id=1, source_target_pairs={{0,1},{1,0},{2,3},{3,2},{4,5},{5,4},{6,7},{7,6},{8,9},{9,8},{10,11... | collective-permute-start | bytes 2359304 | tf_op jit(solution)/shard_map/ppermute | solution.py:37
  12.4 35.3 %collective-permute-start.7 = (bf16[256,768]{1,0:T(8,128)(2,1)}, bf16[256,768]{1,0:T(8,128)(2,1)S(1)}, u32[]{:S(2)}, u32[]{:S(2)}) collective-permute-start(bf16[256,768]{1,0:T(8,128)(2,1)} %get-tuple-element.106.act_ref), channel_id=1, source_target_pairs={{0,2},{2,0},{1,3},{3,1},{4,6},{6,4},{5,7},{7,5},{8,10},{10,8},{9,1... | collective-permute-start | bytes 1179656 | tf_op jit(solution)/shard_map/ppermute | solution.py:37
  13.4 29.4 %collective-permute-start.4 = (bf16[2652,256]{1,0:T(8,128)(2,1)S(1)}, bf16[2652,256]{1,0:T(8,128)(2,1)S(1)}, u32[]{:S(2)}, u32[]{:S(2)}) collective-permute-start(bf16[2652,256]{1,0:T(8,128)(2,1)S(1)} %bitcast.11), channel_id=1, source_target_pairs={{0,2},{2,0},{1,3},{3,1},{4,6},{6,4},{5,7},{7,5},{8,10},{10,8},{9,1... | collective-permute-start | bytes 4073480 | tf_op jit(solution)/shard_map/ppermute | solution.py:37
  13.5 1.1 copy-start.5
  29.9 5.9 %collective-permute-start.2 = (bf16[336,1536]{1,0:T(8,128)(2,1)S(1)}, bf16[336,1536]{1,0:T(8,128)(2,1)S(1)}, u32[]{:S(2)}, u32[]{:S(2)}) collective-permute-start(bf16[336,1536]{1,0:T(8,128)(2,1)S(1)} %collective-permute-done.1.fetched_ref), channel_id=1, source_target_pairs={{0,2},{2,0},{1,3},{3,1},{4,6},{6,4},{5,7},{7,5},{8,10},{10,8},{9,1... | collective-permute-start | bytes 3096584 | tf_op jit(solution)/shard_map/ppermute | solution.py:37
  34.1 6.0 %collective-permute-start.6 = (bf16[1431,256]{1,0:T(8,128)(2,1)S(1)}, bf16[1431,256]{1,0:T(8,128)(2,1)S(1)}, u32[]{:S(2)}, u32[]{:S(2)}) collective-permute-start(bf16[1431,256]{1,0:T(8,128)(2,1)S(1)} %get-tuple-element.104.sent_ref), channel_id=1, source_target_pairs={{0,2},{2,0},{1,3},{3,1},{4,6},{6,4},{5,7},{7,5},{8,10},{10,8},{9,1... | collective-permute-start | bytes 2198024 | tf_op jit(solution)/shard_map/ppermute | solution.py:37
  40.0 2.8 %collective-permute-start.3 = (bf16[1152,256]{1,0:T(8,128)(2,1)S(1)}, bf16[1152,256]{1,0:T(8,128)(2,1)S(1)}, u32[]{:S(2)}, u32[]{:S(2)}) collective-permute-start(bf16[1152,256]{1,0:T(8,128)(2,1)S(1)} %get-tuple-element.98), channel_id=1, source_target_pairs={{0,2},{2,0},{1,3},{3,1},{4,6},{6,4},{5,7},{7,5},{8,10},{10,8},{9,1... | collective-permute-start | bytes 1769480 | tf_op jit(solution)/shard_map/ppermute | solution.py:37
  41.5 6.3 %copy-start.2 = (bf16[256,768]{1,0:T(8,128)(2,1)S(1)}, bf16[256,768]{1,0:T(8,128)(2,1)}, u32[]{:S(2)}) copy-start(bf16[256,768]{1,0:T(8,128)(2,1)} %get-tuple-element.106.act_ref) | copy-start | bytes 1179652
  41.5 14.5 %collective-permute-start.9 = (bf16[2,4,4,24,384]{4,3,2,1,0:T(8,128)(2,1)S(1)}, bf16[2,4,4,24,384]{4,3,2,1,0:T(8,128)(2,1)S(1)}, u32[]{:S(2)}, u32[]{:S(2)}) collective-permute-start(bf16[2,4,4,24,384]{4,3,2,1,0:T(8,128)(2,1)S(1)} %get-tuple-element.105), channel_id=1, source_target_pairs={{0,4},{4,0},{8,12},{12,8},{1,5},{5,1},{9,13},{13,9},{2,6},{6,2},{1... | collective-permute-start | bytes 1769480 | tf_op jit(solution)/shard_map/ppermute | solution.py:42
  44.9 16.7 %collective-permute-start.11 = (bf16[2,4,4,24,384]{4,3,2,1,0:T(8,128)(2,1)S(1)}, bf16[2,4,4,24,384]{4,3,2,1,0:T(8,128)(2,1)S(1)}, u32[]{:S(2)}, u32[]{:S(2)}) collective-permute-start(bf16[2,4,4,24,384]{4,3,2,1,0:T(8,128)(2,1)S(1)} %get-tuple-element.108), channel_id=1, source_target_pairs={{0,96},{32,64},{64,32},{96,0},{1,97},{33,65},{65,33},{97,1},{2,98}... | collective-permute-start | bytes 1769480 | tf_op jit(solution)/shard_map/ppermute | solution.py:42
  49.1 15.1 %collective-permute-start.10 = (bf16[2,4,4,24,384]{4,3,2,1,0:T(8,128)(2,1)S(1)}, bf16[2,4,4,24,384]{4,3,2,1,0:T(8,128)(2,1)S(1)}, u32[]{:S(2)}, u32[]{:S(2)}) collective-permute-start(bf16[2,4,4,24,384]{4,3,2,1,0:T(8,128)(2,1)S(1)} %get-tuple-element.107), channel_id=1, source_target_pairs={{0,12},{4,8},{8,4},{12,0},{1,13},{5,9},{9,5},{13,1},{2,14},{6,10},... | collective-permute-start | bytes 1769480 | tf_op jit(solution)/shard_map/ppermute | solution.py:42
  51.0 10.3 %collective-permute-start.5 = (bf16[2,4,3,24,384]{4,3,2,1,0:T(8,128)(2,1)S(1)}, bf16[2,4,3,24,384]{4,3,2,1,0:T(8,128)(2,1)S(1)}, u32[]{:S(2)}, u32[]{:S(2)}) collective-permute-start(bf16[2,4,3,24,384]{4,3,2,1,0:T(8,128)(2,1)S(1)} %get-tuple-element.102), channel_id=1, source_target_pairs={{0,32},{32,0},{64,96},{96,64},{1,33},{33,1},{65,97},{97,65},{2,34}... | collective-permute-start | bytes 1327112 | tf_op jit(solution)/shard_map/ppermute | solution.py:42
  56.1 14.3 %collective-permute-start.13 = (bf16[4,4,24,384]{3,2,1,0:T(8,128)(2,1)S(1)}, bf16[4,4,24,384]{3,2,1,0:T(8,128)(2,1)S(1)}, u32[]{:S(2)}, u32[]{:S(2)}) collective-permute-start(bf16[4,4,24,384]{3,2,1,0:T(8,128)(2,1)S(1)} %get-tuple-element.114), channel_id=1, source_target_pairs={{0,12},{4,8},{8,4},{12,0},{1,13},{5,9},{9,5},{13,1},{2,14},{6,10},... | collective-permute-start | bytes 884744 | tf_op jit(solution)/shard_map/ppermute | solution.py:42
  61.4 9.7 %collective-permute-start.8 = (bf16[4,3,24,384]{3,2,1,0:T(8,128)(2,1)S(1)}, bf16[4,3,24,384]{3,2,1,0:T(8,128)(2,1)S(1)}, u32[]{:S(2)}, u32[]{:S(2)}) collective-permute-start(bf16[4,3,24,384]{3,2,1,0:T(8,128)(2,1)S(1)} %get-tuple-element.111), channel_id=1, source_target_pairs={{0,96},{32,64},{64,32},{96,0},{1,97},{33,65},{65,33},{97,1},{2,98}... | collective-permute-start | bytes 663560 | tf_op jit(solution)/shard_map/ppermute | solution.py:42
  61.8 10.1 %collective-permute-start.15 = (bf16[4,4,24,384]{3,2,1,0:T(8,128)(2,1)S(1)}, bf16[4,4,24,384]{3,2,1,0:T(8,128)(2,1)S(1)}, u32[]{:S(2)}, u32[]{:S(2)}) collective-permute-start(bf16[4,4,24,384]{3,2,1,0:T(8,128)(2,1)S(1)} %get-tuple-element.120), channel_id=1, source_target_pairs={{0,32},{32,0},{64,96},{96,64},{1,33},{33,1},{65,97},{97,65},{2,34}... | collective-permute-start | bytes 884744 | tf_op jit(solution)/shard_map/ppermute | solution.py:42
  64.2 10.2 %collective-permute-start.14 = (bf16[4,4,24,384]{3,2,1,0:T(8,128)(2,1)S(1)}, bf16[4,4,24,384]{3,2,1,0:T(8,128)(2,1)S(1)}, u32[]{:S(2)}, u32[]{:S(2)}) collective-permute-start(bf16[4,4,24,384]{3,2,1,0:T(8,128)(2,1)S(1)} %get-tuple-element.117), channel_id=1, source_target_pairs={{0,4},{4,0},{8,12},{12,8},{1,5},{5,1},{9,13},{13,9},{2,6},{6,2},{1... | collective-permute-start | bytes 884744 | tf_op jit(solution)/shard_map/ppermute | solution.py:42
  71.1 4.7 %collective-permute-start.17 = (bf16[2,4,24,384]{3,2,1,0:T(8,128)(2,1)S(1)}, bf16[2,4,24,384]{3,2,1,0:T(8,128)(2,1)S(1)}, u32[]{:S(2)}, u32[]{:S(2)}) collective-permute-start(bf16[2,4,24,384]{3,2,1,0:T(8,128)(2,1)S(1)} %get-tuple-element.126), channel_id=1, source_target_pairs={{0,32},{32,0},{64,96},{96,64},{1,33},{33,1},{65,97},{97,65},{2,34}... | collective-permute-start | bytes 442376 | tf_op jit(solution)/shard_map/ppermute | solution.py:42
  71.8 4.0 %collective-permute-start.12 = (bf16[2,3,24,384]{3,2,1,0:T(8,128)(2,1)S(1)}, bf16[2,3,24,384]{3,2,1,0:T(8,128)(2,1)S(1)}, u32[]{:S(2)}, u32[]{:S(2)}) collective-permute-start(bf16[2,3,24,384]{3,2,1,0:T(8,128)(2,1)S(1)} %get-tuple-element.123), channel_id=1, source_target_pairs={{0,4},{4,0},{8,12},{12,8},{1,5},{5,1},{9,13},{13,9},{2,6},{6,2},{1... | collective-permute-start | bytes 331784 | tf_op jit(solution)/shard_map/ppermute | solution.py:42
  72.5 5.4 %collective-permute-start.19 = (bf16[2,4,24,384]{3,2,1,0:T(8,128)(2,1)S(1)}, bf16[2,4,24,384]{3,2,1,0:T(8,128)(2,1)S(1)}, u32[]{:S(2)}, u32[]{:S(2)}) collective-permute-start(bf16[2,4,24,384]{3,2,1,0:T(8,128)(2,1)S(1)} %get-tuple-element.132), channel_id=1, source_target_pairs={{0,12},{4,8},{8,4},{12,0},{1,13},{5,9},{9,5},{13,1},{2,14},{6,10},... | collective-permute-start | bytes 442376 | tf_op jit(solution)/shard_map/ppermute | solution.py:42
  75.0 5.6 %collective-permute-start.18 = (bf16[2,4,24,384]{3,2,1,0:T(8,128)(2,1)S(1)}, bf16[2,4,24,384]{3,2,1,0:T(8,128)(2,1)S(1)}, u32[]{:S(2)}, u32[]{:S(2)}) collective-permute-start(bf16[2,4,24,384]{3,2,1,0:T(8,128)(2,1)S(1)} %get-tuple-element.129), channel_id=1, source_target_pairs={{0,96},{32,64},{64,32},{96,0},{1,97},{33,65},{65,33},{97,1},{2,98}... | collective-permute-start | bytes 442376 | tf_op jit(solution)/shard_map/ppermute | solution.py:42
  75.8 6.8 %collective-permute-start.21 = (bf16[4,24,384]{2,1,0:T(8,128)(2,1)S(1)}, bf16[4,24,384]{2,1,0:T(8,128)(2,1)S(1)}, u32[]{:S(2)}, u32[]{:S(2)}) collective-permute-start(bf16[4,24,384]{2,1,0:T(8,128)(2,1)S(1)} %get-tuple-element.138), channel_id=1, source_target_pairs={{0,96},{32,64},{64,32},{96,0},{1,97},{33,65},{65,33},{97,1},{2,98}... | collective-permute-start | bytes 221192 | tf_op jit(solution)/shard_map/ppermute | solution.py:42
  80.7 5.6 %collective-permute-start.22 = (bf16[4,24,384]{2,1,0:T(8,128)(2,1)S(1)}, bf16[4,24,384]{2,1,0:T(8,128)(2,1)S(1)}, u32[]{:S(2)}, u32[]{:S(2)}) collective-permute-start(bf16[4,24,384]{2,1,0:T(8,128)(2,1)S(1)} %get-tuple-element.141), channel_id=1, source_target_pairs={{0,32},{32,0},{64,96},{96,64},{1,33},{33,1},{65,97},{97,65},{2,34}... | collective-permute-start | bytes 221192 | tf_op jit(solution)/shard_map/ppermute | solution.py:42
  81.0 5.3 %collective-permute-start.20 = (bf16[4,24,384]{2,1,0:T(8,128)(2,1)S(1)}, bf16[4,24,384]{2,1,0:T(8,128)(2,1)S(1)}, u32[]{:S(2)}, u32[]{:S(2)}) collective-permute-start(bf16[4,24,384]{2,1,0:T(8,128)(2,1)S(1)} %get-tuple-element.144), channel_id=1, source_target_pairs={{0,4},{4,0},{8,12},{12,8},{1,5},{5,1},{9,13},{13,9},{2,6},{6,2},{1... | collective-permute-start | bytes 221192 | tf_op jit(solution)/shard_map/ppermute | solution.py:42
  82.0 4.3 %collective-permute-start.16 = (bf16[3,24,384]{2,1,0:T(8,128)(2,1)S(1)}, bf16[3,24,384]{2,1,0:T(8,128)(2,1)S(1)}, u32[]{:S(2)}, u32[]{:S(2)}) collective-permute-start(bf16[3,24,384]{2,1,0:T(8,128)(2,1)S(1)} %get-tuple-element.135), channel_id=1, source_target_pairs={{0,12},{4,8},{8,4},{12,0},{1,13},{5,9},{9,5},{13,1},{2,14},{6,10},... | collective-permute-start | bytes 165896 | tf_op jit(solution)/shard_map/ppermute | solution.py:42
  86.9 5.6 %collective-permute-start.23 = (bf16[8,24,384]{2,1,0:T(8,128)(2,1)S(1)}, bf16[8,24,384]{2,1,0:T(8,128)(2,1)S(1)}, u32[]{:S(2)}, u32[]{:S(2)}) collective-permute-start(bf16[8,24,384]{2,1,0:T(8,128)(2,1)S(1)} %get-tuple-element.153), channel_id=1, source_target_pairs={{0,16},{16,0},{1,17},{17,1},{2,18},{18,2},{3,19},{19,3},{4,20},{20... | collective-permute-start | bytes 442376 | tf_op jit(solution)/shard_map/ppermute | solution.py:37
